TPU v7x, 32 devices: a whole 2x2x4 slice. The times are simulated.
32 devices in a mesh: dp: 16 (over z, x, core), hd: 2 (over y).
Axes of the slice: x: 2, y: 2, z: 4, core: 2. Of those that a mesh axis runs over, the one named last changes fastest.
Arguments:
- tokens: bfloat16 [64, 64, 768], P(('dp', 'hd')), may hold values from -6 to 6
- encoder: bfloat16 [64, 576, 768], P(('dp', 'hd')), may hold values from -6 to 6
- patch_count: int32 [64], P(('dp', 'hd')), may hold values from 196 to 576, as said below
- out_grad: bfloat16 [64, 64, 768], P(('dp', 'hd')), may hold values from -6 to 6
- uni_attn_gain: bfloat16 [768], P(('dp', 'hd')), may hold values from 0.099609375 to 1.8984375
- uni_attn_shift: bfloat16 [768], P(('dp', 'hd')), may hold values from -2 to 2
- uni_qkv: bfloat16 [768, 2304], P(('dp', 'hd')), may hold values from -0.21875 to 0.21875
- uni_out: bfloat16 [768, 768], P(('dp', 'hd')), may hold values from -0.875 to 0.875
- uni_mlp_gain: bfloat16 [768], P(('dp', 'hd')), may hold values from 0.099609375 to 1.8984375
- uni_mlp_shift: bfloat16 [768], P(('dp', 'hd')), may hold values from -2 to 2
- uni_up: bfloat16 [768, 3072], P(('dp', 'hd')), may hold values from -0.21875 to 0.21875
- uni_down: bfloat16 [3072, 768], P(('dp', 'hd')), may hold values from -0.109375 to 0.109375
- multi_attn_gain: bfloat16 [768], P(('dp', 'hd')), may hold values from 0.099609375 to 1.8984375
- multi_attn_shift: bfloat16 [768], P(('dp', 'hd')), may hold values from -2 to 2
- multi_qkv: bfloat16 [768, 2304], P(('dp', 'hd')), may hold values from -0.21875 to 0.21875
- multi_out: bfloat16 [768, 768], P(('dp', 'hd')), may hold values from -0.875 to 0.875
- cross_gain: bfloat16 [768], P(('dp', 'hd')), may hold values from 0.099609375 to 1.8984375
- cross_shift: bfloat16 [768], P(('dp', 'hd')), may hold values from -2 to 2
- cross_query: bfloat16 [768, 768], P(('dp', 'hd')), may hold values from -0.21875 to 0.21875
- cross_pair: bfloat16 [768, 1536], P(('dp', 'hd')), may hold values from -0.21875 to 0.21875
- cross_out: bfloat16 [768, 768], P(('dp', 'hd')), may hold values from -1.75 to 1.75
- multi_mlp_gain: bfloat16 [768], P(('dp', 'hd')), may hold values from 0.099609375 to 1.8984375
- multi_mlp_shift: bfloat16 [768], P(('dp', 'hd')), may hold values from -2 to 2
- multi_up: bfloat16 [768, 3072], P(('dp', 'hd')), may hold values from -0.21875 to 0.21875
- multi_down: bfloat16 [3072, 768], P(('dp', 'hd')), may hold values from -0.109375 to 0.109375
Outputs:
- activations: bfloat16 [64, 64, 768], P(('dp', 'hd'))
- grad_tokens: bfloat16 [64, 64, 768], P(('dp', 'hd'))
- grad_encoder: bfloat16 [64, 576, 768], P(('dp', 'hd'))
- grad_uni_attn_gain: float32 [768], P(('dp', 'hd'))
- grad_uni_attn_shift: float32 [768], P(('dp', 'hd'))
- grad_uni_qkv: float32 [768, 2304], P(('dp', 'hd'))
- grad_uni_out: float32 [768, 768], P(('dp', 'hd'))
- grad_uni_mlp_gain: float32 [768], P(('dp', 'hd'))
- grad_uni_mlp_shift: float32 [768], P(('dp', 'hd'))
- grad_uni_up: float32 [768, 3072], P(('dp', 'hd'))
- grad_uni_down: float32 [3072, 768], P(('dp', 'hd'))
- grad_multi_attn_gain: float32 [768], P(('dp', 'hd'))
- grad_multi_attn_shift: float32 [768], P(('dp', 'hd'))
- grad_multi_qkv: float32 [768, 2304], P(('dp', 'hd'))
- grad_multi_out: float32 [768, 768], P(('dp', 'hd'))
- grad_cross_gain: float32 [768], P(('dp', 'hd'))
- grad_cross_shift: float32 [768], P(('dp', 'hd'))
- grad_cross_query: float32 [768, 768], P(('dp', 'hd'))
- grad_cross_pair: float32 [768, 1536], P(('dp', 'hd'))
- grad_cross_out: float32 [768, 768], P(('dp', 'hd'))
- grad_multi_mlp_gain: float32 [768], P(('dp', 'hd'))
- grad_multi_mlp_shift: float32 [768], P(('dp', 'hd'))
- grad_multi_up: float32 [768, 3072], P(('dp', 'hd'))
- grad_multi_down: float32 [3072, 768], P(('dp', 'hd'))
Inputs may be any that keep to these rules, and one draw needn't show every extreme that they name: Caption c's valid patches are slots 0 to patch_count[c] - 1; every count is 196 or 576, and both occur in every draw.
All inputs are finite; a program needn't handle non-finite values.
Results may differ from a plain program's by a relative error of at most 0.025.
Values may be sent and summed in bfloat16 or wider, within the bound.
No kernel may reach another device: no remote copies, remote signals or barrier semaphores. Data moves between devices by JAX's collectives and lax.ppermute only.
A program may use at most 256 MiB of HBM per device.

v0:
```python
import math

import jax
import jax.numpy as jnp
from jax import lax
from jax.sharding import PartitionSpec as P

DH = 64


epsilon = 1e-05
masked_value = -1e30


def shortened(x):

    def short(part):
        return part.astype(jnp.bfloat16) if part.dtype == jnp.float32 else part

    return jax.tree.map(short, x)


def layer_norm(hidden, norm_gain, norm_shift):
    centred = hidden - jnp.mean(hidden, axis=-1, keepdims=True)
    spread = jnp.mean(centred * centred, axis=-1, keepdims=True)
    return centred * lax.rsqrt(spread + epsilon) * norm_gain + norm_shift


def widen_gains(arrays):
    return tuple((member.astype(jnp.float32) if member.ndim == 1 else member for member in arrays))


def gather_block(shards):
    gathered = (
        lax.all_gather(shards[0], ("dp", "hd"), axis=0, tiled=True),
        lax.all_gather(shards[1], ("dp", "hd"), axis=0, tiled=True),
        lax.all_gather(shards[2], ("dp", "hd"), axis=0, tiled=True),
        lax.all_gather(shards[3], ("dp", "hd"), axis=0, tiled=True),
        lax.all_gather(shards[4], ("dp", "hd"), axis=0, tiled=True),
        lax.all_gather(shards[5], ("dp", "hd"), axis=0, tiled=True),
        lax.all_gather(shards[6], ("dp", "hd"), axis=0, tiled=True),
        lax.all_gather(shards[7], ("dp", "hd"), axis=0, tiled=True),
    )
    return widen_gains(gathered)


def gather_cross(shards):
    gathered = (
        lax.all_gather(shards[0], ("dp", "hd"), axis=0, tiled=True),
        lax.all_gather(shards[1], ("dp", "hd"), axis=0, tiled=True),
        lax.all_gather(shards[2], ("dp", "hd"), axis=0, tiled=True),
        lax.all_gather(shards[3], ("dp", "hd"), axis=0, tiled=True),
        lax.all_gather(shards[4], ("dp", "hd"), axis=0, tiled=True),
    )
    return widen_gains(gathered)


def scatter_block(grads_in):
    return (
        lax.psum_scatter(grads_in[0], ("dp", "hd"), scatter_dimension=0, tiled=True),
        lax.psum_scatter(grads_in[1], ("dp", "hd"), scatter_dimension=0, tiled=True),
        lax.psum_scatter(grads_in[2], ("dp", "hd"), scatter_dimension=0, tiled=True),
        lax.psum_scatter(grads_in[3], ("dp", "hd"), scatter_dimension=0, tiled=True),
        lax.psum_scatter(grads_in[4], ("dp", "hd"), scatter_dimension=0, tiled=True),
        lax.psum_scatter(grads_in[5], ("dp", "hd"), scatter_dimension=0, tiled=True),
        lax.psum_scatter(grads_in[6], ("dp", "hd"), scatter_dimension=0, tiled=True),
        lax.psum_scatter(grads_in[7], ("dp", "hd"), scatter_dimension=0, tiled=True),
    )


def to_heads(arrays):
    return jax.tree.map(
        lambda part, own: part.astype(own.dtype),
        lax.all_to_all(shortened(arrays), "hd", split_axis=2, concat_axis=0, tiled=True),
        arrays,
    )


def to_batch(arrays):
    return jax.tree.map(
        lambda part, own: part.astype(own.dtype),
        lax.all_to_all(shortened(arrays), "hd", split_axis=0, concat_axis=2, tiled=True),
        arrays,
    )


def in_blocks(tensor, block_rows):
    return tensor.reshape((tensor.shape[0] // block_rows, block_rows) + tensor.shape[1:])


def head_view(tensor):
    return tensor.reshape(tensor.shape[:2] + (tensor.shape[2] // DH, DH))


def block_count(queries):
    return math.gcd(queries.shape[0], max(1, 512 // queries.shape[1]))


def masked_scores(query_block, key_block, valid_block, causal):
    scores = jnp.einsum(
        "bqhd,bkhd->bhqk",
        head_view(query_block),
        head_view(key_block),
        preferred_element_type=jnp.float32,
    ) * DH ** (-0.5)
    allowed = (valid_block > 0)[:, None, None, :]
    if causal:
        rows_at = lax.broadcasted_iota(jnp.int32, scores.shape[2:], 0)
        cols_at = lax.broadcasted_iota(jnp.int32, scores.shape[2:], 1)
        allowed = allowed & (rows_at >= cols_at)[None, None]
    return jnp.where(allowed, scores, masked_value)


def attend_forward(queries, keys_in, values_in, key_valid, causal):
    block_rows = block_count(queries)

    def one_block(pieces):
        query_block, key_block, value_block, valid_block = pieces
        scores = masked_scores(query_block, key_block, valid_block, causal)
        highest = jnp.max(scores, axis=-1, keepdims=True)
        row_total = jnp.sum(jnp.exp(scores - highest), axis=-1, keepdims=True)
        logsum = highest + jnp.log(row_total)
        attn_weights = jnp.exp(scores - logsum).astype(jnp.bfloat16)
        attended = jnp.einsum(
            "bhqk,bkhd->bqhd",
            attn_weights,
            head_view(value_block),
            preferred_element_type=jnp.float32,
        )
        return (attended.reshape(query_block.shape).astype(jnp.bfloat16), logsum)

    attended, logsums = lax.map(
        one_block,
        (
            in_blocks(queries, block_rows),
            in_blocks(keys_in, block_rows),
            in_blocks(values_in, block_rows),
            in_blocks(key_valid, block_rows),
        ),
    )
    return (attended.reshape(queries.shape), logsums)


def attend_backward(queries, keys_in, values_in, key_valid, causal, logsums, grad_attended):
    block_rows = block_count(queries)
    score_scale = DH ** (-0.5)

    def one_block(pieces):
        query_block, key_block, value_block, valid_block, logsum, grad_block = pieces
        scores = masked_scores(query_block, key_block, valid_block, causal)
        attn_weights = jnp.exp(scores - logsum)
        grad_heads = head_view(grad_block)
        grad_weights = jnp.einsum(
            "bqhd,bkhd->bhqk",
            grad_heads,
            head_view(value_block),
            preferred_element_type=jnp.float32,
        )
        row_inner = jnp.sum(attn_weights * grad_weights, axis=-1, keepdims=True)
        grad_scores = (attn_weights * (grad_weights - row_inner)).astype(jnp.bfloat16)
        grad_query = (
            jnp.einsum(
                "bhqk,bkhd->bqhd",
                grad_scores,
                head_view(key_block),
                preferred_element_type=jnp.float32,
            )
            * score_scale
        )
        grad_key = (
            jnp.einsum(
                "bhqk,bqhd->bkhd",
                grad_scores,
                head_view(query_block),
                preferred_element_type=jnp.float32,
            )
            * score_scale
        )
        grad_value = jnp.einsum(
            "bhqk,bqhd->bkhd",
            attn_weights.astype(jnp.bfloat16),
            grad_heads,
            preferred_element_type=jnp.float32,
        )
        return (
            grad_query.reshape(query_block.shape).astype(jnp.bfloat16),
            grad_key.reshape(key_block.shape).astype(jnp.bfloat16),
            grad_value.reshape(value_block.shape).astype(jnp.bfloat16),
        )

    grad_blocks = lax.map(
        one_block,
        (
            in_blocks(queries, block_rows),
            in_blocks(keys_in, block_rows),
            in_blocks(values_in, block_rows),
            in_blocks(key_valid, block_rows),
            logsums,
            in_blocks(grad_attended, block_rows),
        ),
    )
    return tuple((member.reshape((-1,) + member.shape[2:]) for member in grad_blocks))


def weight_grad(inputs, grad_rows):
    return jnp.einsum("csi,csj->ij", inputs, grad_rows, preferred_element_type=jnp.float32)


def input_grad(grad_rows, weight):
    return jnp.einsum("csj,ij->csi", grad_rows, weight, preferred_element_type=jnp.float32)


def norm_backward(hidden, norm_gain, norm_shift, grad_normed):
    unused, pull_back = jax.vjp(layer_norm, hidden, norm_gain, norm_shift)
    return pull_back(grad_normed)


def self_forward(hidden, norm_gain, norm_shift, w_qkv, w_out):
    normed = layer_norm(hidden, norm_gain, norm_shift).astype(jnp.bfloat16)
    mixed = jnp.dot(normed, w_qkv, preferred_element_type=jnp.float32).astype(jnp.bfloat16)
    model_width = w_out.shape[0]
    head_query, head_key, head_value = to_heads(
        (
            mixed[..., :model_width],
            mixed[..., model_width : 2 * model_width],
            mixed[..., 2 * model_width :],
        )
    )
    key_valid = jnp.ones(head_key.shape[:2], jnp.float32)
    attended_heads, logsums = attend_forward(head_query, head_key, head_value, key_valid, True)
    (attended,) = to_batch((attended_heads,))
    branch = jnp.dot(attended, w_out, preferred_element_type=jnp.float32)
    return (hidden + branch, (normed, head_query, head_key, head_value, logsums, attended))


def self_backward(hidden, norm_gain, norm_shift, w_qkv, w_out, kept_values, grad_next):
    normed, head_query, head_key, head_value, logsums, attended = kept_values
    grad_branch = grad_next.astype(jnp.bfloat16)
    grad_out = weight_grad(attended, grad_branch)
    grad_attended = input_grad(grad_branch, w_out).astype(jnp.bfloat16)
    (grad_heads,) = to_heads((grad_attended,))
    key_valid = jnp.ones(head_key.shape[:2], jnp.float32)
    grad_query, grad_key, grad_value = attend_backward(
        head_query, head_key, head_value, key_valid, True, logsums, grad_heads
    )
    batch_query, batch_key, batch_value = to_batch((grad_query, grad_key, grad_value))
    grad_mixed = jnp.concatenate((batch_query, batch_key, batch_value), axis=-1)
    grad_qkv = weight_grad(normed, grad_mixed)
    grad_normed = input_grad(grad_mixed, w_qkv)
    grad_hidden, grad_gain, grad_shift = norm_backward(hidden, norm_gain, norm_shift, grad_normed)
    return (grad_next + grad_hidden, (grad_gain, grad_shift, grad_qkv, grad_out))


def cross_forward(hidden, encoder, patch_flags, norm_gain, norm_shift, w_query, w_pair, w_out):
    normed = layer_norm(hidden, norm_gain, norm_shift).astype(jnp.bfloat16)
    queries = jnp.dot(normed, w_query, preferred_element_type=jnp.float32).astype(jnp.bfloat16)
    pair_rows = jnp.dot(encoder, w_pair, preferred_element_type=jnp.float32).astype(jnp.bfloat16)
    model_width = w_out.shape[0]
    head_query, head_key, head_value, head_flags = to_heads(
        (queries, pair_rows[..., :model_width], pair_rows[..., model_width:], patch_flags)
    )
    key_valid = head_flags[..., 0].astype(jnp.float32)
    attended_heads, logsums = attend_forward(head_query, head_key, head_value, key_valid, False)
    (attended,) = to_batch((attended_heads,))
    branch = jnp.dot(attended, w_out, preferred_element_type=jnp.float32)
    return (
        hidden + branch,
        (normed, head_query, head_key, head_value, key_valid, logsums, attended),
    )


def cross_backward(
    hidden, encoder, norm_gain, norm_shift, w_query, w_pair, w_out, kept_values, grad_next
):
    normed, head_query, head_key, head_value, key_valid, logsums, attended = kept_values
    grad_branch = grad_next.astype(jnp.bfloat16)
    grad_out = weight_grad(attended, grad_branch)
    grad_attended = input_grad(grad_branch, w_out).astype(jnp.bfloat16)
    (grad_heads,) = to_heads((grad_attended,))
    grad_query_heads, grad_key_heads, grad_value_heads = attend_backward(
        head_query, head_key, head_value, key_valid, False, logsums, grad_heads
    )
    batch_query, batch_key, batch_value = to_batch(
        (grad_query_heads, grad_key_heads, grad_value_heads)
    )
    grad_pair_rows = jnp.concatenate((batch_key, batch_value), axis=-1)
    grad_pair = weight_grad(encoder, grad_pair_rows)
    grad_encoder = input_grad(grad_pair_rows, w_pair)
    grad_query = weight_grad(normed, batch_query)
    grad_normed = input_grad(batch_query, w_query)
    grad_hidden, grad_gain, grad_shift = norm_backward(hidden, norm_gain, norm_shift, grad_normed)
    return (
        grad_next + grad_hidden,
        grad_encoder,
        (grad_gain, grad_shift, grad_query, grad_pair, grad_out),
    )


def feed_forward(hidden, norm_gain, norm_shift, w_up, w_down):
    normed = layer_norm(hidden, norm_gain, norm_shift).astype(jnp.bfloat16)
    upward = jnp.dot(normed, w_up, preferred_element_type=jnp.float32)
    active = jax.nn.gelu(upward).astype(jnp.bfloat16)
    return (
        hidden + jnp.dot(active, w_down, preferred_element_type=jnp.float32),
        (normed, upward, active),
    )


def feed_backward(hidden, norm_gain, norm_shift, w_up, w_down, kept_values, grad_next):
    normed, upward, active = kept_values
    grad_branch = grad_next.astype(jnp.bfloat16)
    grad_down = weight_grad(active, grad_branch)
    grad_active = input_grad(grad_branch, w_down)
    unused, gelu_back = jax.vjp(jax.nn.gelu, upward)
    (grad_upward,) = gelu_back(grad_active)
    grad_upward = grad_upward.astype(jnp.bfloat16)
    grad_up = weight_grad(normed, grad_upward)
    grad_normed = input_grad(grad_upward, w_up)
    grad_hidden, grad_gain, grad_shift = norm_backward(hidden, norm_gain, norm_shift, grad_normed)
    return (grad_next + grad_hidden, (grad_gain, grad_shift, grad_up, grad_down))


def uni_forward(hidden, weights):
    middle, self_kept = self_forward(hidden, weights[0], weights[1], weights[2], weights[3])
    result, feed_kept = feed_forward(middle, weights[4], weights[5], weights[6], weights[7])
    return (result, (middle, self_kept, feed_kept))


def uni_backward(hidden, weights, grad_next):
    unused, (middle, self_kept, feed_kept) = uni_forward(hidden, weights)
    grad_middle, feed_grads = feed_backward(
        middle, weights[4], weights[5], weights[6], weights[7], feed_kept, grad_next
    )
    grad_hidden, self_grads = self_backward(
        hidden, weights[0], weights[1], weights[2], weights[3], self_kept, grad_middle
    )
    return (grad_hidden, self_grads + feed_grads)


def multi_forward(hidden, encoder, patch_flags, weights, cross_weights):
    after_self, self_kept = self_forward(hidden, weights[0], weights[1], weights[2], weights[3])
    after_cross, cross_kept = cross_forward(
        after_self,
        encoder,
        patch_flags,
        cross_weights[0],
        cross_weights[1],
        cross_weights[2],
        cross_weights[3],
        cross_weights[4],
    )
    result, feed_kept = feed_forward(after_cross, weights[4], weights[5], weights[6], weights[7])
    return (result, (after_self, after_cross, self_kept, cross_kept, feed_kept))


def multi_backward(hidden, encoder, patch_flags, weights, cross_weights, grad_next):
    unused, (after_self, after_cross, self_kept, cross_kept, feed_kept) = multi_forward(
        hidden, encoder, patch_flags, weights, cross_weights
    )
    grad_cross_in, feed_grads = feed_backward(
        after_cross, weights[4], weights[5], weights[6], weights[7], feed_kept, grad_next
    )
    grad_self_in, grad_encoder, cross_grads_local = cross_backward(
        after_self,
        encoder,
        cross_weights[0],
        cross_weights[1],
        cross_weights[2],
        cross_weights[3],
        cross_weights[4],
        cross_kept,
        grad_cross_in,
    )
    grad_hidden, self_grads = self_backward(
        hidden, weights[0], weights[1], weights[2], weights[3], self_kept, grad_self_in
    )
    return (grad_hidden, grad_encoder, self_grads + feed_grads, cross_grads_local)


def local(
    tokens,
    encoder,
    patch_count,
    out_grad,
    uni_attn_gain,
    uni_attn_shift,
    uni_qkv,
    uni_out,
    uni_mlp_gain,
    uni_mlp_shift,
    uni_up,
    uni_down,
    multi_attn_gain,
    multi_attn_shift,
    multi_qkv,
    multi_out,
    cross_gain,
    cross_shift,
    cross_query,
    cross_pair,
    cross_out,
    multi_mlp_gain,
    multi_mlp_shift,
    multi_up,
    multi_down,
):
    uni_shards = (
        uni_attn_gain,
        uni_attn_shift,
        uni_qkv,
        uni_out,
        uni_mlp_gain,
        uni_mlp_shift,
        uni_up,
        uni_down,
    )
    multi_shards = (
        multi_attn_gain,
        multi_attn_shift,
        multi_qkv,
        multi_out,
        multi_mlp_gain,
        multi_mlp_shift,
        multi_up,
        multi_down,
    )
    cross_shards = (cross_gain, cross_shift, cross_query, cross_pair, cross_out)
    patch_slots = lax.broadcasted_iota(jnp.int32, (encoder.shape[0], encoder.shape[1]), 1)
    key_flag = (patch_slots < patch_count[:, None]).astype(jnp.bfloat16)
    patch_flags = jnp.broadcast_to(key_flag[:, :, None], key_flag.shape + (lax.axis_size("hd"),))
    start_hidden = tokens.astype(jnp.float32)
    uni_full = gather_block(uni_shards)
    middle, unused_uni = uni_forward(start_hidden, uni_full)
    multi_full = gather_block(multi_shards)
    cross_full = gather_cross(cross_shards)
    result, unused_multi = multi_forward(middle, encoder, patch_flags, multi_full, cross_full)
    grad_result = out_grad.astype(jnp.float32)
    multi_back = gather_block(multi_shards)
    cross_back = gather_cross(cross_shards)
    grad_middle, grad_encoder, multi_grads, cross_local = multi_backward(
        middle, encoder, patch_flags, multi_back, cross_back, grad_result
    )
    cross_rows = (
        lax.psum_scatter(cross_local[0], ("dp", "hd"), scatter_dimension=0, tiled=True),
        lax.psum_scatter(cross_local[1], ("dp", "hd"), scatter_dimension=0, tiled=True),
        lax.psum_scatter(cross_local[2], ("dp", "hd"), scatter_dimension=0, tiled=True),
        lax.psum_scatter(cross_local[3], ("dp", "hd"), scatter_dimension=0, tiled=True),
        lax.psum_scatter(cross_local[4], ("dp", "hd"), scatter_dimension=0, tiled=True),
    )
    multi_rows = scatter_block(multi_grads)
    uni_back = gather_block(uni_shards)
    grad_start, uni_grads = uni_backward(start_hidden, uni_back, grad_middle)
    uni_rows = scatter_block(uni_grads)
    return (
        result.astype(jnp.bfloat16),
        grad_start.astype(jnp.bfloat16),
        grad_encoder.astype(jnp.bfloat16),
        uni_rows[0],
        uni_rows[1],
        uni_rows[2],
        uni_rows[3],
        uni_rows[4],
        uni_rows[5],
        uni_rows[6],
        uni_rows[7],
        multi_rows[0],
        multi_rows[1],
        multi_rows[2],
        multi_rows[3],
        cross_rows[0],
        cross_rows[1],
        cross_rows[2],
        cross_rows[3],
        cross_rows[4],
        multi_rows[4],
        multi_rows[5],
        multi_rows[6],
        multi_rows[7],
    )


def solution(mesh):
    in_specs = (
        P(("dp", "hd"), None, None),
        P(("dp", "hd"), None, None),
        P(("dp", "hd")),
        P(("dp", "hd"), None, None),
        P(("dp", "hd")),
        P(("dp", "hd")),
        P(("dp", "hd"), None),
        P(("dp", "hd"), None),
        P(("dp", "hd")),
        P(("dp", "hd")),
        P(("dp", "hd"), None),
        P(("dp", "hd"), None),
        P(("dp", "hd")),
        P(("dp", "hd")),
        P(("dp", "hd"), None),
        P(("dp", "hd"), None),
        P(("dp", "hd")),
        P(("dp", "hd")),
        P(("dp", "hd"), None),
        P(("dp", "hd"), None),
        P(("dp", "hd"), None),
        P(("dp", "hd")),
        P(("dp", "hd")),
        P(("dp", "hd"), None),
        P(("dp", "hd"), None),
    )
    out_specs = (
        P(("dp", "hd"), None, None),
        P(("dp", "hd"), None, None),
        P(("dp", "hd"), None, None),
        P(("dp", "hd")),
        P(("dp", "hd")),
        P(("dp", "hd"), None),
        P(("dp", "hd"), None),
        P(("dp", "hd")),
        P(("dp", "hd")),
        P(("dp", "hd"), None),
        P(("dp", "hd"), None),
        P(("dp", "hd")),
        P(("dp", "hd")),
        P(("dp", "hd"), None),
        P(("dp", "hd"), None),
        P(("dp", "hd")),
        P(("dp", "hd")),
        P(("dp", "hd"), None),
        P(("dp", "hd"), None),
        P(("dp", "hd"), None),
        P(("dp", "hd")),
        P(("dp", "hd")),
        P(("dp", "hd"), None),
        P(("dp", "hd"), None),
    )
    return jax.shard_map(local, mesh=mesh, in_specs=in_specs, out_specs=out_specs, check_vma=False)
```

profile of v0, /device:TPU:0, one launch (start us, length us, event | category | flops | bytes accessed | tf_op | source)
XLA Modules:
  0.0 2044.2 jit_solution(11913736298380838912)
XLA Ops:
  22.4 42.7 %all-reduce.21 = (bf16[768]{0:T(1024)(128)(2,1)S(1)}, bf16[768]{0:T(1024)(128)(2,1)S(1)}, bf16[768]{0:T(1024)(128)(2,1)S(1)}, bf16[768]{0:T(1024)(128)(2,1)}, bf...) all-reduce(bf16[768]{0:T(1024)(128)(2,1)S(1)} %dynamic-update-slice, ...), channel_id=1, replica_groups=mesh['dp'=16,'hd'=2] {'dp','hd'}, use_global_device_ids=true, to_apply=%add.1 | all-reduce | flops 7680 | bytes 30720
  116.8 13.6 all-gather.14.cloned.1.call-done
  132.4 63.6 %all-gather.16.cloned.1.call-done = bf16[768,3072]{1,0:T(8,128)(2,1)} async-done(((bf16[24,3072]{1,0:T(8,128)(2,1)}), bf16[768,3072]{1,0:T(8,128)(2,1)}) %all-gather.16.cloned.1.call-update) | async-done | bytes 4718608 | tf_op jit(solution)/shard_map/all_gather | solution.py:41
  200.3 60.9 %all-gather.18.cloned.1.call-done = bf16[3072,768]{1,0:T(8,128)(2,1)} async-done(((bf16[96,768]{1,0:T(8,128)(2,1)}), bf16[3072,768]{1,0:T(8,128)(2,1)}) %all-gather.18.cloned.1.call-update) | async-done | bytes 4718608 | tf_op jit(solution)/shard_map/all_gather | solution.py:42
  265.4 57.6 %all-gather.20.cloned.1.call-done = bf16[768,2304]{1,0:T(8,128)(2,1)} async-done(((bf16[24,2304]{1,0:T(8,128)(2,1)}), bf16[768,2304]{1,0:T(8,128)(2,1)}) %all-gather.20.cloned.1.call-update) | async-done | bytes 3538960 | tf_op jit(solution)/shard_map/all_gather | solution.py:37
  350.6 31.4 %all-gather.24.cloned.1.call-done = bf16[768,1536]{1,0:T(8,128)(2,1)} async-done(((bf16[24,1536]{1,0:T(8,128)(2,1)}), bf16[768,1536]{1,0:T(8,128)(2,1)}) %all-gather.24.cloned.1.call-update) | async-done | bytes 2359312 | tf_op jit(solution)/shard_map/all_gather | solution.py:52
  433.2 14.8 all-to-all-done.8
  456.8 38.7 %all-gather.26.cloned.1.call-done = bf16[768,768]{1,0:T(8,128)(2,1)} async-done(((bf16[24,768]{1,0:T(8,128)(2,1)}), bf16[768,768]{1,0:T(8,128)(2,1)}) %all-gather.26.cloned.1.call-update) | async-done | bytes 1179664 | tf_op jit(solution)/shard_map/all_gather | solution.py:51
  539.2 12.4 all-gather.28.cloned.1.call-done
  555.5 61.5 %all-gather.30.cloned.1.call-done = bf16[768,3072]{1,0:T(8,128)(2,1)} async-done(((bf16[24,3072]{1,0:T(8,128)(2,1)}), bf16[768,3072]{1,0:T(8,128)(2,1)}) %all-gather.30.cloned.1.call-update) | async-done | bytes 4718608 | tf_op jit(solution)/shard_map/all_gather | solution.py:41
  621.5 60.9 %all-gather.32.cloned.1.call-done = bf16[3072,768]{1,0:T(8,128)(2,1)} async-done(((bf16[96,768]{1,0:T(8,128)(2,1)}), bf16[3072,768]{1,0:T(8,128)(2,1)}) %all-gather.32.cloned.1.call-update) | async-done | bytes 4718608 | tf_op jit(solution)/shard_map/all_gather | solution.py:42
  700.0 9.3 all_to_all.470
  831.1 9.2 all-to-all-done.23
  854.8 11.1 all-to-all-done.24
  903.1 9.2 all_to_all.472
  992.4 40.3 %all-reduce.20 = (f32[768]{0:T(1024)S(1)}, f32[768]{0:T(1024)S(1)}, f32[768]{0:T(1024)S(1)}, f32[768]{0:T(1024)S(1)}, f32[768]{0:T(1024)S(1)}, /*index=5*/f32[76...) all-reduce(f32[768]{0:T(1024)S(1)} %get-tuple-element.293, ...), channel_id=2, replica_groups=mesh['dp'=16,'hd'=2] {'dp','hd'}, use_global_device_ids=true, to_apply=%region_30.31.clone | all-reduce | flops 7680 | bytes 61440
  1046.4 62.3 %reduce-scatter.16.cloned.1.call-done = f32[24,768]{1,0:T(8,128)} async-done(((f32[768,768]{1,0:T(8,128)}), f32[24,768]{1,0:T(8,128)}) %reduce-scatter.16.cloned.1.call-update) | async-done | bytes 73744 | tf_op jit(solution)/shard_map/reduce_scatter | solution.py:63
  1108.7 112.0 %reduce-scatter.34.cloned.1.call-done = f32[24,1536]{1,0:T(8,128)} async-done(((f32[768,1536]{1,0:T(8,128)}), f32[24,1536]{1,0:T(8,128)}) %reduce-scatter.34.cloned.1.call-update) | async-done | bytes 147472
  1220.6 125.2 %reduce-scatter.22.cloned.1.call-done = f32[24,2304]{1,0:T(8,128)} async-done(((f32[768,2304]{1,0:T(8,128)}), f32[24,2304]{1,0:T(8,128)}) %reduce-scatter.22.cloned.1.call-update) | async-done | bytes 221200 | tf_op jit(solution)/shard_map/reduce_scatter | solution.py:62
  1345.8 124.7 %reduce-scatter.14.cloned.1.call-done = f32[24,2304]{1,0:T(8,128)} async-done(((f32[768,2304]{1,0:T(8,128)}), f32[24,2304]{1,0:T(8,128)}) %reduce-scatter.14.cloned.1.call-update) | async-done | bytes 221200 | tf_op jit(solution)/shard_map/reduce_scatter | solution.py:62
  1470.5 142.3 %reduce-scatter.30.cloned.1.call-done = f32[24,3072]{1,0:T(8,128)} async-done(((f32[768,3072]{1,0:T(8,128)}), f32[24,3072]{1,0:T(8,128)}) %reduce-scatter.30.cloned.1.call-update) | async-done | bytes 294928 | tf_op jit(solution)/shard_map/reduce_scatter | solution.py:66
  1612.8 141.1 %reduce-scatter.32.cloned.1.call-done = f32[96,768]{1,0:T(8,128)} async-done(((f32[3072,768]{1,0:T(8,128)}), f32[96,768]{1,0:T(8,128)}) %reduce-scatter.32.cloned.1.call-update) | async-done | bytes 294928 | tf_op jit(solution)/shard_map/reduce_scatter | solution.py:67
  1753.8 142.1 %reduce-scatter.18.cloned.1.call-done = f32[24,3072]{1,0:T(8,128)} async-done(((f32[768,3072]{1,0:T(8,128)}), f32[24,3072]{1,0:T(8,128)}) %reduce-scatter.18.cloned.1.call-update) | async-done | bytes 294928 | tf_op jit(solution)/shard_map/reduce_scatter | solution.py:66
  1895.9 141.0 %reduce-scatter.20.cloned.1.call-done = f32[96,768]{1,0:T(8,128)} async-done(((f32[3072,768]{1,0:T(8,128)}), f32[96,768]{1,0:T(8,128)}) %reduce-scatter.20.cloned.1.call-update) | async-done | bytes 294928 | tf_op jit(solution)/shard_map/reduce_scatter | solution.py:67
  (559 shorter events, 499.9 us)
Async XLA Ops:
  7.2 67.3 %all-gather.12.cloned.1.call-start = ((), (), s32[]{:S(2)}) async-start(), calls=%async_computation.36 | async-start | bytes 3649536 | tf_op jit(solution)/shard_map/all_gather | solution.py:37
  7.9 122.5 %all-gather.14.cloned.1.call-start = ((), (), s32[]{:S(2)}) async-start(), calls=%async_computation.37 | async-start | bytes 1216512 | tf_op jit(solution)/shard_map/all_gather | solution.py:38
  8.7 187.3 %all-gather.16.cloned.1.call-start = ((), (), s32[]{:S(2)}) async-start(), calls=%async_computation.38 | async-start | bytes 4866048 | tf_op jit(solution)/shard_map/all_gather | solution.py:41
  9.4 251.8 %all-gather.18.cloned.1.call-start = ((), (), s32[]{:S(2)}) async-start(), calls=%async_computation.39 | async-start | bytes 4866048 | tf_op jit(solution)/shard_map/all_gather | solution.py:42
  10.0 313.0 %all-gather.20.cloned.1.call-start = ((), (), s32[]{:S(2)}) async-start(), calls=%async_computation.40 | async-start | bytes 3649536 | tf_op jit(solution)/shard_map/all_gather | solution.py:37
  10.6 371.4 %all-gather.24.cloned.1.call-start = ((), (), s32[]{:S(2)}) async-start(), calls=%async_computation.42 | async-start | bytes 2433024 | tf_op jit(solution)/shard_map/all_gather | solution.py:52
  11.2 441.7 %all-gather.22.cloned.1.call-start = ((), (), s32[]{:S(2)}) async-start(), calls=%async_computation.41 | async-start | bytes 1216512 | tf_op jit(solution)/shard_map/all_gather | solution.py:38
  11.9 483.6 %all-gather.26.cloned.1.call-start = ((), (), s32[]{:S(2)}) async-start(), calls=%async_computation.43 | async-start | bytes 1216512 | tf_op jit(solution)/shard_map/all_gather | solution.py:51
  12.7 538.9 %all-gather.28.cloned.1.call-start = ((), (), s32[]{:S(2)}) async-start(), calls=%async_computation.44 | async-start | bytes 1216512 | tf_op jit(solution)/shard_map/all_gather | solution.py:53
  13.4 603.5 %all-gather.30.cloned.1.call-start = ((), (), s32[]{:S(2)}) async-start(), calls=%async_computation.45 | async-start | bytes 4866048 | tf_op jit(solution)/shard_map/all_gather | solution.py:41
  111.7 570.7 %all-gather.32.cloned.1.call-start = ((), (), s32[]{:S(2)}) async-start(), calls=%async_computation.46 | async-start | bytes 4866048 | tf_op jit(solution)/shard_map/all_gather | solution.py:42
  347.2 44.0 %all-to-all-start.6 = ((bf16[2,2,24576]{2,1,0:T(2,128)(2,1)}), bf16[2,2,24576]{2,1,0:T(2,128)(2,1)S(1)}, u32[]{:S(2)}, u32[]{:S(2)}) async-start(bf16[2,2,24576]{2,1,0:T(2,128)(2,1)} %reshape.594), calls=%async_computation.6 | async-start | bytes 393216 | tf_op jit(solution)/shard_map/all_to_all | solution.py:74
  448.0 53.8 %all-to-all-start.11 = ((bf16[2,576,768]{1,0,2:T(2,128)(2,1)}), bf16[2,576,768]{1,0,2:T(2,128)(2,1)}, u32[]{:S(2)}, u32[]{:S(2)}) async-start(bf16[2,576,768]{1,0,2:T(2,128)(2,1)} %copy.171), calls=%async_computation.11 | async-start | bytes 3932160 | tf_op jit(solution)/shard_map/all_to_all | solution.py:74
  530.4 516.0 %reduce-scatter.28.cloned.1.call-start = ((), (), s32[]{:S(2)}) async-start(), calls=%async_computation.54 | async-start | bytes 2433024 | tf_op jit(solution)/shard_map/reduce_scatter | solution.py:448
  693.5 352.9 %reduce-scatter.24.cloned.1.call-start = ((), (), s32[]{:S(2)}) async-start(), calls=%async_computation.52 | async-start | bytes 2433024 | tf_op jit(solution)/shard_map/reduce_scatter | solution.py:63
  748.8 297.6 %reduce-scatter.26.cloned.1.call-start = ((), (), s32[]{:S(2)}) async-start(), calls=%async_computation.53 | async-start | bytes 2433024 | tf_op jit(solution)/shard_map/reduce_scatter | solution.py:446
  784.9 323.8 %reduce-scatter.16.cloned.1.call-start = ((), (), s32[]{:S(2)}) async-start(), calls=%async_computation.48 | async-start | bytes 2433024 | tf_op jit(solution)/shard_map/reduce_scatter | solution.py:63
  844.9 375.7 %reduce-scatter.34.cloned.1.call-start = ((), (), s32[]{:S(2)}) async-start(), calls=%async_computation.57 | async-start | bytes 4866048
  890.6 455.3 %reduce-scatter.22.cloned.1.call-start = ((), (), s32[]{:S(2)}) async-start(), calls=%async_computation.51 | async-start | bytes 7299072 | tf_op jit(solution)/shard_map/reduce_scatter | solution.py:62
  944.1 526.5 %reduce-scatter.14.cloned.1.call-start = ((), (), s32[]{:S(2)}) async-start(), calls=%async_computation.47 | async-start | bytes 7299072 | tf_op jit(solution)/shard_map/reduce_scatter | solution.py:62
  956.6 656.2 %reduce-scatter.30.cloned.1.call-start = ((), (), s32[]{:S(2)}) async-start(), calls=%async_computation.55 | async-start | bytes 9732096 | tf_op jit(solution)/shard_map/reduce_scatter | solution.py:66
  963.9 790.0 %reduce-scatter.32.cloned.1.call-start = ((), (), s32[]{:S(2)}) async-start(), calls=%async_computation.56 | async-start | bytes 9732096 | tf_op jit(solution)/shard_map/reduce_scatter | solution.py:67
  971.4 924.6 %reduce-scatter.18.cloned.1.call-start = ((), (), s32[]{:S(2)}) async-start(), calls=%async_computation.49 | async-start | bytes 9732096 | tf_op jit(solution)/shard_map/reduce_scatter | solution.py:66
  978.2 1058.6 %reduce-scatter.20.cloned.1.call-start = ((), (), s32[]{:S(2)}) async-start(), calls=%async_computation.50 | async-start | bytes 9732096 | tf_op jit(solution)/shard_map/reduce_scatter | solution.py:67
  (137 other events, 1932.3 us)
Sparse Core Ops, SparseCore 0:
  11.0 63.5 all-gather.11
  77.4 52.9 all-gather.13
  133.3 62.5 all-gather.15
  198.7 62.4 all-gather.17
  264.0 58.9 all-gather.19
  325.8 56.1 all-gather.23
  384.9 54.3 all-gather.21
  442.2 53.2 all-gather.25
  498.4 53.1 all-gather.27
  554.3 62.5 all-gather.29
  619.9 62.4 all-gather.31
  693.6 97.8 reduce-scatter.27
  798.2 102.0 reduce-scatter.23
  906.0 98.1 reduce-scatter.25
  1010.7 97.9 reduce-scatter.15
  1114.6 106.0 reduce-scatter.33
  1227.7 118.1 reduce-scatter.21
  1351.9 118.5 reduce-scatter.13
  1478.0 134.7 reduce-scatter.29
  1619.1 134.7 reduce-scatter.31
  1761.3 134.5 reduce-scatter.17
  1902.4 134.4 reduce-scatter.19
where the time goes:
time: 2060 us; the launch traced here: 2040 us
  waiting for transfers between devices  1470 us (71%)
  local copies, waits for them, and re-layouts  181 us (9%)
  matrix products  156 us (8%)
  blocking collectives  110 us (5%)
  starting transfers between devices  89.2 us (4%)
    reduce_scatter x2, waiting for transfers between devices, scatter_block(): lax.psum_scatter(grads_in[6], ('dp', 'hd'), scatter_dimension=0, tiled=True)  284 us
    reduce_scatter x2, waiting for transfers between devices, scatter_block(): lax.psum_scatter(grads_in[7], ('dp', 'hd'), scatter_dimension=0, tiled=True)  282 us
    reduce_scatter x2, waiting for transfers between devices, scatter_block(): lax.psum_scatter(grads_in[2], ('dp', 'hd'), scatter_dimension=0, tiled=True)  250 us
    all_gather x2, waiting for transfers between devices, gather_block(): lax.all_gather(shards[6], ('dp', 'hd'), axis=0, tiled=True)  125 us
    all_gather x2, waiting for transfers between devices, gather_block(): lax.all_gather(shards[7], ('dp', 'hd'), axis=0, tiled=True)  122 us
    unnamed x23, waiting for transfers between devices  119 us
    unnamed x2, blocking collectives  83 us
    unnamed x290, local copies, waits for them, and re-layouts  68.2 us
  transfers between devices with their start and end apart: 44, of which 35 were waited for; matrix products, arithmetic and copies ran while one was open for 15% of the time, Pallas kernels for 0%

commit v1 on v0

v1 whole, which is shorter than its diff:
```python
import jax
import jax.numpy as jnp
from jax import lax
from jax.sharding import PartitionSpec as P

DH = 64
AXES = ("dp", "hd")
EPS = 1e-05
MASKED = -1e30
bf16 = jnp.bfloat16
f32 = jnp.float32


BIT_PAIR, BIT_CORE, BIT_NEAR = 1, 2, 4


class Place:
    def __init__(self):
        self.count = lax.axis_size("dp") * lax.axis_size("hd")
        self.outer_size = self.count // 8
        index = lax.axis_index("dp") * lax.axis_size("hd") + lax.axis_index("hd")
        self.pair = index % 2
        self.core = (index // 2) % 2
        self.near = (index // 4) % 2
        self.outer = index // 8

    def swap(self, x, bit):
        return lax.ppermute(x, AXES, [(i, i ^ bit) for i in range(self.count)])

    def shift(self, x, k):
        n = self.count
        return lax.ppermute(x, AXES, [(i, (i + 8 * k) % n) for i in range(n)])


def pick(x, index, axis):
    return lax.dynamic_index_in_dim(x, index, axis, keepdims=False)


def join(own, got, index, axis):
    shape = own.shape[:axis] + (2,) + own.shape[axis:]
    out = jnp.zeros(shape, own.dtype)
    out = lax.dynamic_update_index_in_dim(out, own, index, axis)
    return lax.dynamic_update_index_in_dim(out, got, 1 - index, axis)


def gather_rows(place, shard, near_last):
    n = place.outer_size
    got = [place.shift(shard, k) for k in range(1, n)]
    block = jnp.zeros((n,) + shard.shape, shard.dtype)
    block = lax.dynamic_update_index_in_dim(block, shard, place.outer, 0)
    for k in range(1, n):
        block = lax.dynamic_update_index_in_dim(block, got[k - 1], (place.outer - k) % n, 0)
    if near_last:
        block = join(block, place.swap(block, BIT_PAIR), place.pair, 1)
        block = join(block, place.swap(block, BIT_NEAR), place.near, 1)
    else:
        block = join(block, place.swap(block, BIT_NEAR), place.near, 1)
        block = join(block, place.swap(block, BIT_PAIR), place.pair, 2)
    block = join(block, place.swap(block, BIT_CORE), place.core, 2)
    return block.reshape(place.count * shard.shape[0], shard.shape[1])


def scatter_rows(place, full, near_first):
    n = place.outer_size
    rows = full.shape[0] // place.count
    t = full.astype(bf16).reshape(n, 2, 2, 2, rows, full.shape[1])

    def halve(t, index, bit, axis):
        got = place.swap(pick(t, 1 - index, axis), bit)
        return (pick(t, index, axis).astype(f32) + got.astype(f32)).astype(bf16)

    t = halve(t, place.core, BIT_CORE, 2)
    if near_first:
        t = halve(t, place.near, BIT_NEAR, 1)
        t = halve(t, place.pair, BIT_PAIR, 1)
    else:
        t = halve(t, place.pair, BIT_PAIR, 2)
        t = halve(t, place.near, BIT_NEAR, 1)
    total = pick(t, place.outer, 0).astype(f32)
    for k in range(1, n):
        got = place.shift(pick(t, (place.outer + k) % n, 0), k)
        total = total + got.astype(f32)
    return total


def dot(a, b):
    return jnp.dot(a, b, preferred_element_type=f32)


def dot_rows(a, b):
    return lax.dot_general(a, b, (((0,), (0,)), ((), ())), preferred_element_type=f32)


def dot_back(a, w):
    return lax.dot_general(a, w, (((1,), (1,)), ((), ())), preferred_element_type=f32)


def norm_forward(x, gain, shift):
    centred = x - jnp.mean(x, axis=-1, keepdims=True)
    inv = lax.rsqrt(jnp.mean(centred * centred, axis=-1, keepdims=True) + EPS)
    unit = centred * inv
    return (unit * gain + shift).astype(bf16), unit, inv


def norm_backward(grad, unit, inv, gain):
    du = grad * gain
    dx = inv * (
        du
        - jnp.mean(du, axis=-1, keepdims=True)
        - unit * jnp.mean(du * unit, axis=-1, keepdims=True)
    )
    return dx, jnp.sum(grad * unit, axis=0), jnp.sum(grad, axis=0)


GELU_A = 0.7978845608028654
GELU_B = 0.044715


def gelu_forward(u):
    return 0.5 * u * (1.0 + jnp.tanh(GELU_A * (u + GELU_B * u * u * u)))


def gelu_slope(u):
    t = jnp.tanh(GELU_A * (u + GELU_B * u * u * u))
    return 0.5 * (1.0 + t) + 0.5 * u * (1.0 - t * t) * GELU_A * (1.0 + 3.0 * GELU_B * u * u)


def heads(x, captions):
    return x.reshape(captions, x.shape[0] // captions, x.shape[1] // DH, DH)


def attend_forward(q, k, v, allowed, captions):
    s = jnp.einsum(
        "bqhd,bkhd->bhqk", heads(q, captions), heads(k, captions), preferred_element_type=f32
    ) * DH ** (-0.5)
    s = jnp.where(allowed, s, MASKED)
    s = s - jnp.max(s, axis=-1, keepdims=True)
    e = jnp.exp(s)
    p = e / jnp.sum(e, axis=-1, keepdims=True)
    o = jnp.einsum("bhqk,bkhd->bqhd", p.astype(bf16), heads(v, captions), preferred_element_type=f32)
    return o.reshape(q.shape).astype(bf16), p


def attend_backward(q, k, v, p, do, captions):
    doh = heads(do, captions)
    dp = jnp.einsum("bqhd,bkhd->bhqk", doh, heads(v, captions), preferred_element_type=f32)
    ds = (p * (dp - jnp.sum(p * dp, axis=-1, keepdims=True))).astype(bf16)
    scale = DH ** (-0.5)
    dq = jnp.einsum("bhqk,bkhd->bqhd", ds, heads(k, captions), preferred_element_type=f32) * scale
    dk = jnp.einsum("bhqk,bqhd->bkhd", ds, heads(q, captions), preferred_element_type=f32) * scale
    dv = jnp.einsum("bhqk,bqhd->bkhd", p.astype(bf16), doh, preferred_element_type=f32)
    return (
        dq.reshape(q.shape).astype(bf16),
        dk.reshape(k.shape).astype(bf16),
        dv.reshape(v.shape).astype(bf16),
    )


def self_forward(x, gain, shift, w_qkv, w_out, captions):
    d = x.shape[1]
    a, unit, inv = norm_forward(x, gain, shift)
    mixed = dot(a, w_qkv).astype(bf16)
    q, k, v = mixed[:, :d], mixed[:, d : 2 * d], mixed[:, 2 * d :]
    length = x.shape[0] // captions
    causal = jnp.arange(length)[:, None] >= jnp.arange(length)[None, :]
    o, p = attend_forward(q, k, v, causal[None, None], captions)
    return x + dot(o, w_out), (a, unit, inv, q, k, v, p, o)


def self_backward(kept, gain, w_qkv, w_out, dx, captions):
    a, unit, inv, q, k, v, p, o = kept
    dy = dx.astype(bf16)
    g_out = dot_rows(o, dy)
    do = dot_back(dy, w_out).astype(bf16)
    dmixed = jnp.concatenate(attend_backward(q, k, v, p, do, captions), axis=1)
    g_qkv = dot_rows(a, dmixed)
    dn, g_gain, g_shift = norm_backward(dot_back(dmixed, w_qkv), unit, inv, gain)
    return dx + dn, g_gain, g_shift, g_qkv, g_out


def cross_forward(x, enc, allowed, gain, shift, w_q, w_pair, w_out, captions):
    d = x.shape[1]
    c, unit, inv = norm_forward(x, gain, shift)
    q = dot(c, w_q).astype(bf16)
    pair = dot(enc, w_pair).astype(bf16)
    k, v = pair[:, :d], pair[:, d:]
    o, p = attend_forward(q, k, v, allowed, captions)
    return x + dot(o, w_out), (c, unit, inv, q, k, v, p, o)


def cross_backward(kept, enc, gain, w_q, w_pair, w_out, dx, captions):
    c, unit, inv, q, k, v, p, o = kept
    dy = dx.astype(bf16)
    g_out = dot_rows(o, dy)
    do = dot_back(dy, w_out).astype(bf16)
    dq, dk, dv = attend_backward(q, k, v, p, do, captions)
    dpair = jnp.concatenate((dk, dv), axis=1)
    g_pair = dot_rows(enc, dpair)
    denc = dot_back(dpair, w_pair)
    g_q = dot_rows(c, dq)
    dn, g_gain, g_shift = norm_backward(dot_back(dq, w_q), unit, inv, gain)
    return dx + dn, denc, g_gain, g_shift, g_q, g_pair, g_out


def feed_forward(x, gain, shift, w_up, w_down):
    b, unit, inv = norm_forward(x, gain, shift)
    u = dot(b, w_up)
    g = gelu_forward(u).astype(bf16)
    return x + dot(g, w_down), (b, unit, inv, u, g)


def feed_backward(kept, gain, w_up, w_down, dx):
    b, unit, inv, u, g = kept
    dz = dx.astype(bf16)
    g_down = dot_rows(g, dz)
    du = (gelu_slope(u) * dot_back(dz, w_down)).astype(bf16)
    g_up = dot_rows(b, du)
    dn, g_gain, g_shift = norm_backward(dot_back(du, w_up), unit, inv, gain)
    return dx + dn, g_gain, g_shift, g_up, g_down


LANES = 128


def pack(matrices, vectors):
    rows = matrices[0].shape[0]
    cols = jnp.stack(vectors, axis=1).astype(matrices[0].dtype)
    cols = jnp.pad(cols, ((0, 0), (0, LANES - cols.shape[1])))
    return jnp.concatenate(tuple(matrices) + (cols,), axis=1)


def unpack(packed, widths, count):
    out, at = [], 0
    for w in widths:
        out.append(packed[:, at : at + w])
        at += w
    vectors = packed[:, at : at + LANES].astype(f32)
    return out, [vectors[:, i] for i in range(count)]


def local(
    tokens, encoder, patch_count, out_grad,
    u_ag, u_as, u_qkv, u_out, u_mg, u_ms, u_up, u_down,
    m_ag, m_as, m_qkv, m_out, c_g, c_s, c_q, c_pair, c_out, m_mg, m_ms, m_up, m_down,
):
    place = Place()
    captions, length, d = tokens.shape
    patches = encoder.shape[1]
    x0 = tokens.reshape(-1, d).astype(f32)
    enc = encoder.reshape(-1, d)
    slots = lax.broadcasted_iota(jnp.int32, (captions, patches), 1)
    allowed = (slots < patch_count[:, None])[:, None, None, :]

    self_w, cross_w = (3 * d, d), (d, 2 * d, d)
    pu = gather_rows(place, pack((u_qkv, u_out), (u_ag, u_as, u_mg, u_ms)), True)
    uup = gather_rows(place, u_up, True)
    udown = gather_rows(place, u_down, False)
    pm = gather_rows(place, pack((m_qkv, m_out), (m_ag, m_as, m_mg, m_ms)), False)
    pc = gather_rows(place, pack((c_q, c_pair, c_out), (c_g, c_s)), True)
    mup = gather_rows(place, m_up, True)
    mdown = gather_rows(place, m_down, False)
    (uqkv, uout), (uag, uas, umg, ums) = unpack(pu, self_w, 4)
    (mqkv, mout), (mag, mas, mmg, mms) = unpack(pm, self_w, 4)
    (cq, cpair, cout), (cg, cs) = unpack(pc, cross_w, 2)

    x0a, k_us = self_forward(x0, uag, uas, uqkv, uout, captions)
    x1, k_uf = feed_forward(x0a, umg, ums, uup, udown)
    x1a, k_ms = self_forward(x1, mag, mas, mqkv, mout, captions)
    x1b, k_mc = cross_forward(x1a, enc, allowed, cg, cs, cq, cpair, cout, captions)
    x2, k_mf = feed_forward(x1b, mmg, mms, mup, mdown)

    dx = out_grad.reshape(-1, d).astype(f32)
    dx, g_mmg, g_mms, g_mup, g_mdown = feed_backward(k_mf, mmg, mup, mdown, dx)
    r_mup = scatter_rows(place, g_mup, True)
    r_mdown = scatter_rows(place, g_mdown, False)
    dx, denc, g_cg, g_cs, g_cq, g_cpair, g_cout = cross_backward(
        k_mc, enc, cg, cq, cpair, cout, dx, captions
    )
    r_c = scatter_rows(place, pack((g_cq, g_cpair, g_cout), (g_cg, g_cs)), True)
    dx, g_mag, g_mas, g_mqkv, g_mout = self_backward(k_ms, mag, mqkv, mout, dx, captions)
    r_m = scatter_rows(place, pack((g_mqkv, g_mout), (g_mag, g_mas, g_mmg, g_mms)), False)
    dx, g_umg, g_ums, g_uup, g_udown = feed_backward(k_uf, umg, uup, udown, dx)
    r_uup = scatter_rows(place, g_uup, True)
    r_udown = scatter_rows(place, g_udown, False)
    dx, g_uag, g_uas, g_uqkv, g_uout = self_backward(k_us, uag, uqkv, uout, dx, captions)
    r_u = scatter_rows(place, pack((g_uqkv, g_uout), (g_uag, g_uas, g_umg, g_ums)), True)

    (r_uqkv, r_uout), (r_uag, r_uas, r_umg, r_ums) = unpack(r_u, self_w, 4)
    (r_mqkv, r_mout), (r_mag, r_mas, r_mmg, r_mms) = unpack(r_m, self_w, 4)
    (r_cq, r_cpair, r_cout), (r_cg, r_cs) = unpack(r_c, cross_w, 2)
    return (
        x2.astype(bf16).reshape(tokens.shape),
        dx.astype(bf16).reshape(tokens.shape),
        denc.astype(bf16).reshape(encoder.shape),
        r_uag, r_uas, r_uqkv, r_uout, r_umg, r_ums, r_uup, r_udown,
        r_mag, r_mas, r_mqkv, r_mout, r_cg, r_cs, r_cq, r_cpair, r_cout,
        r_mmg, r_mms, r_mup, r_mdown,
    )


def solution(mesh):
    rows1 = P(AXES)
    rows2 = P(AXES, None)
    rows3 = P(AXES, None, None)
    block = (rows1, rows1, rows2, rows2)
    weights = block * 2 + block + (rows1, rows1, rows2, rows2, rows2) + block
    return jax.shard_map(
        local,
        mesh=mesh,
        in_specs=(rows3, rows3, rows1, rows3) + weights,
        out_specs=(rows3, rows3, rows3) + weights,
        check_vma=False,
    )
```

time: 2060 us -> 784 us (0.38)
  waiting for transfers between devices: 1470 us -> 284 us
  blocking collectives: 110 us -> 0 us
  matrix products: 156 us -> 125 us
  other arithmetic: 18.2 us -> 47.4 us
  local copies, waits for them, and re-layouts: 181 us -> 207 us
  starting transfers between devices: 89.2 us -> 110 us
    reduce_scatter x10 -> x0, waiting for transfers between devices: 879 us -> none  [the longest x2 284 us: scatter_block(): lax.psum_scatter(grads_in[6], ('dp', 'hd'), scatter_dimension=0, tiled=True)]
    all_gather x11 -> x0, waiting for transfers between devices: 408 us -> none  [the longest x2 125 us: gather_block(): lax.all_gather(shards[6], ('dp', 'hd'), axis=0, tiled=True)]
    ppermute x0 -> x84, waiting for transfers between devices: none -> 284 us  [the longest x42 201 us: swap(): return lax.ppermute(x, AXES, [(i, i ^ bit) for i in range(self.count)])]
    unnamed x23 -> x0, waiting for transfers between devices: 119 us -> none
    ppermute x0 -> x84, starting transfers between devices: none -> 110 us  [the longest x42 74.1 us: shift(): return lax.ppermute(x, AXES, [(i, (i + 8 * k) % n) for i in range(n)])]
    all_to_all x22 -> x0, starting transfers between devices: 87.3 us -> none  [the longest x11 44.2 us: to_batch(): lax.all_to_all(shortened(arrays), 'hd', split_axis=0, concat_axis=2, tile...]
    unnamed x2 -> x0, blocking collectives: 83 us -> none
    all_to_all x22 -> x0, waiting for transfers between devices: 67.2 us -> none  [the longest x11 34 us: to_heads(): lax.all_to_all(shortened(arrays), 'hd', split_axis=2, concat_axis=0, tile...]
  transfers between devices with their start and end apart: 44 -> 84, of which waited for: 35 -> 28; matrix products, arithmetic and copies ran while one was open for 15% -> 22% of each run, Pallas kernels for 0% -> 0%
where the time goes in v1:
time: 784 us; the launch traced here: 777 us
  waiting for transfers between devices  284 us (36%)
  local copies, waits for them, and re-layouts  207 us (26%)
  matrix products  125 us (16%)
  starting transfers between devices  110 us (14%)
  other arithmetic  47.4 us (6%)
    ppermute x42, waiting for transfers between devices, swap(): return lax.ppermute(x, AXES, [(i, i ^ bit) for i in range(self.count)])  201 us
    ppermute x42, waiting for transfers between devices, shift(): return lax.ppermute(x, AXES, [(i, (i + 8 * k) % n) for i in range(n)])  82.8 us
    ppermute x42, starting transfers between devices, shift(): return lax.ppermute(x, AXES, [(i, (i + 8 * k) % n) for i in range(n)])  74.1 us
    ppermute x42, starting transfers between devices, swap(): return lax.ppermute(x, AXES, [(i, i ^ bit) for i in range(self.count)])  36.2 us
    dot_general x11, matrix products, dot_back(): lax.dot_general(a, w, (((1,), (1,)), ((), ())), preferred_element_type=f32)  34.9 us
    reshape x20, local copies, waits for them, and re-layouts, heads(): return x.reshape(captions, x.shape[0] // captions, x.shape[1] // DH, DH)  33.1 us
    dot_general x11, matrix products, dot_rows(): lax.dot_general(a, b, (((0,), (0,)), ((), ())), preferred_element_type=f32)  30.4 us
    dot_general x11, matrix products, dot(): return jnp.dot(a, b, preferred_element_type=f32)  28.6 us
  transfers between devices with their start and end apart: 84, of which 28 were waited for; matrix products, arithmetic and copies ran while one was open for 22% of the time, Pallas kernels for 0%

profile of v1, /device:TPU:0, one launch (start us, length us, event | category | flops | bytes accessed | tf_op | source)
XLA Modules:
  0.0 777.1 jit_solution(2824945402075191934)
XLA Ops:
  40.4 5.6 collective-permute-done.31
  59.2 9.3 %collective-permute-done.37 = bf16[96,768]{1,0:T(8,128)(2,1)S(1)} collective-permute-done((bf16[96,768]{1,0:T(8,128)(2,1)S(1)}, bf16[96,768]{1,0:T(8,128)(2,1)S(1)}, u32[]{:S(2)}, u32[]{:S(2)}) %collective-permute-start.37) | collective-permute-done | bytes 147488 | tf_op jit(solution)/shard_map/ppermute | solution.py:32
  72.7 5.3 collective-permute-done.19
  84.1 8.7 %collective-permute-done.24 = bf16[24,3200]{1,0:T(8,128)(2,1)S(1)} collective-permute-done((bf16[24,3200]{1,0:T(8,128)(2,1)S(1)}, bf16[24,3200]{1,0:T(8,128)(2,1)S(1)}, u32[]{:S(2)}, u32[]{:S(2)}) %collective-permute-start.24) | collective-permute-done | bytes 153632 | tf_op jit(solution)/shard_map/ppermute | solution.py:32
  109.6 20.6 %collective-permute-done.15 = bf16[4,96,768]{2,1,0:T(8,128)(2,1)S(1)} collective-permute-done((bf16[4,96,768]{2,1,0:T(8,128)(2,1)S(1)}, bf16[4,96,768]{2,1,0:T(8,128)(2,1)S(1)}, u32[]{:S(2)}, u32[]{:S(2)}) %collective-permute-start.15) | collective-permute-done | bytes 589856 | tf_op jit(solution)/shard_map/ppermute | solution.py:28
  140.9 7.5 collective-permute-done.21
  155.2 43.7 %collective-permute-done.10 = bf16[4,2,24,3072]{3,2,1,0:T(8,128)(2,1)S(1)} collective-permute-done((bf16[4,2,24,3072]{3,2,1,0:T(8,128)(2,1)S(1)}, bf16[4,2,24,3072]{3,2,1,0:T(8,128)(2,1)S(1)}, u32[]{:S(2)}, u32[]{:S(2)}) %collective-permute-start.10) | collective-permute-done | bytes 1179680 | tf_op jit(solution)/shard_map/ppermute | solution.py:28
  217.6 9.7 %collective-permute-done.22 = bf16[4,2,24,3200]{3,2,1,0:T(8,128)(2,1)S(1)} collective-permute-done((bf16[4,2,24,3200]{3,2,1,0:T(8,128)(2,1)S(1)}, bf16[4,2,24,3200]{3,2,1,0:T(8,128)(2,1)S(1)}, u32[]{:S(2)}, u32[]{:S(2)}) %collective-permute-start.22) | collective-permute-done | bytes 1228832 | tf_op jit(solution)/shard_map/ppermute | solution.py:28
  228.2 20.1 %collective-permute-done.4 = bf16[4,2,24,3200]{3,2,1,0:T(8,128)(2,1)S(1)} collective-permute-done((bf16[4,2,24,3200]{3,2,1,0:T(8,128)(2,1)S(1)}, bf16[4,2,24,3200]{3,2,1,0:T(8,128)(2,1)S(1)}, u32[]{:S(2)}, u32[]{:S(2)}) %collective-permute-start.4) | collective-permute-done | bytes 1228832 | tf_op jit(solution)/shard_map/ppermute | solution.py:28
  327.4 5.4 reshape.428
  332.9 5.4 reshape.426
  499.0 6.7 constant_dynamic-slice_fusion.5
  535.2 6.0 convolution_convert_fusion.10
  566.3 18.9 %collective-permute-done.49 = bf16[4,2,24,3072]{3,2,0,1:T(8,128)(2,1)} collective-permute-done((bf16[4,2,24,3072]{3,2,0,1:T(8,128)(2,1)S(1)}, bf16[4,2,24,3072]{3,2,0,1:T(8,128)(2,1)}, u32[]{:S(2)}, u32[]{:S(2)}) %collective-permute-start.49) | collective-permute-done | bytes 1179680 | tf_op jit(solution)/shard_map/ppermute | solution.py:28
  590.7 15.5 %collective-permute-done.79 = bf16[4,2,96,768]{3,2,0,1:T(8,128)(2,1)} collective-permute-done((bf16[4,2,96,768]{3,2,0,1:T(8,128)(2,1)S(1)}, bf16[4,2,96,768]{3,2,0,1:T(8,128)(2,1)}, u32[]{:S(2)}, u32[]{:S(2)}) %collective-permute-start.79) | collective-permute-done | bytes 1179680 | tf_op jit(solution)/shard_map/ppermute | solution.py:28
  613.9 18.1 %collective-permute-done.61 = bf16[4,2,24,3200]{3,2,0,1:T(8,128)(2,1)S(1)} collective-permute-done((bf16[4,2,24,3200]{3,2,0,1:T(8,128)(2,1)S(1)}, bf16[4,2,24,3200]{3,2,0,1:T(8,128)(2,1)S(1)}, u32[]{:S(2)}, u32[]{:S(2)}) %collective-permute-start.61) | collective-permute-done | bytes 1228832 | tf_op jit(solution)/shard_map/ppermute | solution.py:28
  638.3 24.7 %collective-permute-done.43 = bf16[4,2,24,3200]{3,2,1,0:T(8,128)(2,1)S(1)} collective-permute-done((bf16[4,2,24,3200]{3,2,1,0:T(8,128)(2,1)S(1)}, bf16[4,2,24,3200]{3,2,1,0:T(8,128)(2,1)S(1)}, u32[]{:S(2)}, u32[]{:S(2)}) %collective-permute-start.43) | collective-permute-done | bytes 1228832 | tf_op jit(solution)/shard_map/ppermute | solution.py:28
  668.5 7.2 collective-permute-done.56
  677.7 10.6 %collective-permute-done.80 = bf16[4,96,768]{2,1,0:T(8,128)(2,1)S(1)} collective-permute-done((bf16[4,96,768]{2,1,0:T(8,128)(2,1)S(1)}, bf16[4,96,768]{2,1,0:T(8,128)(2,1)S(1)}, u32[]{:S(2)}, u32[]{:S(2)}) %collective-permute-start.80) | collective-permute-done | bytes 589856 | tf_op jit(solution)/shard_map/ppermute | solution.py:28
  695.5 7.9 %collective-permute-done.52 = bf16[24,3072]{1,0:T(8,128)(2,1)S(1)} collective-permute-done((bf16[24,3072]{1,0:T(8,128)(2,1)S(1)}, bf16[24,3072]{1,0:T(8,128)(2,1)S(1)}, u32[]{:S(2)}, u32[]{:S(2)}) %collective-permute-start.52) | collective-permute-done | bytes 147488 | tf_op jit(solution)/shard_map/ppermute | solution.py:32
  708.5 8.6 %collective-permute-done.58 = bf16[96,768]{1,0:T(8,128)(2,1)S(1)} collective-permute-done((bf16[96,768]{1,0:T(8,128)(2,1)S(1)}, bf16[96,768]{1,0:T(8,128)(2,1)S(1)}, u32[]{:S(2)}, u32[]{:S(2)}) %collective-permute-start.58) | collective-permute-done | bytes 147488 | tf_op jit(solution)/shard_map/ppermute | solution.py:32
  721.8 6.4 collective-permute-done.82
  744.6 6.8 collective-permute-done.69
  758.6 7.6 collective-permute-done.70
  (758 shorter events, 486.7 us)
Async XLA Ops:
  6.8 43.3 %collective-permute-start.12 = (bf16[96,768]{1,0:T(8,128)(2,1)}, bf16[96,768]{1,0:T(8,128)(2,1)}, u32[]{:S(2)}, u32[]{:S(2)}) collective-permute-start(bf16[96,768]{1,0:T(8,128)(2,1)} %param.36), channel_id=1, source_target_pairs={{0,8},{1,9},{2,10},{3,11},{4,12},{5,13},{6,14},{7,15},{8,16},{9,17... | collective-permute-start | bytes 442376 | tf_op jit(solution)/shard_map/ppermute | solution.py:32
  8.4 45.8 %collective-permute-start.14 = (bf16[96,768]{1,0:T(8,128)(2,1)}, bf16[96,768]{1,0:T(8,128)(2,1)}, u32[]{:S(2)}, u32[]{:S(2)}) collective-permute-start(bf16[96,768]{1,0:T(8,128)(2,1)} %param.36), channel_id=1, source_target_pairs={{0,24},{1,25},{2,26},{3,27},{4,28},{5,29},{6,30},{7,31},{8,0},{9,1... | collective-permute-start | bytes 442376 | tf_op jit(solution)/shard_map/ppermute | solution.py:32
  68.5 38.7 %collective-permute-start.1 = (bf16[24,3200]{1,0:T(8,128)(2,1)S(1)}, bf16[24,3200]{1,0:T(8,128)(2,1)S(1)}, u32[]{:S(2)}, u32[]{:S(2)}) collective-permute-start(bf16[24,3200]{1,0:T(8,128)(2,1)S(1)} %fusion.137), channel_id=1, source_target_pairs={{0,16},{1,17},{2,18},{3,19},{4,20},{5,21},{6,22},{7,23},{8,24},{9,... | collective-permute-start | bytes 460808 | tf_op jit(solution)/shard_map/ppermute | solution.py:32
  68.8 39.7 %collective-permute-start.2 = (bf16[24,3200]{1,0:T(8,128)(2,1)S(1)}, bf16[24,3200]{1,0:T(8,128)(2,1)S(1)}, u32[]{:S(2)}, u32[]{:S(2)}) collective-permute-start(bf16[24,3200]{1,0:T(8,128)(2,1)S(1)} %fusion.137), channel_id=1, source_target_pairs={{0,24},{1,25},{2,26},{3,27},{4,28},{5,29},{6,30},{7,31},{8,0},{9,1... | collective-permute-start | bytes 460808 | tf_op jit(solution)/shard_map/ppermute | solution.py:32
  108.5 41.4 %collective-permute-start.27 = (bf16[4,24,3200]{2,1,0:T(8,128)(2,1)}, bf16[4,24,3200]{2,1,0:T(8,128)(2,1)S(1)}, u32[]{:S(2)}, u32[]{:S(2)}) collective-permute-start(bf16[4,24,3200]{2,1,0:T(8,128)(2,1)} %bitcast_dynamic-update-slice_fusion.42), channel_id=1, source_target_pairs={{0,1},{1,0},{2,3},{3,2},{4,5},{5,4},{6,7},{7,6},{8,9},{9,8},{10,11... | collective-permute-start | bytes 1843208 | tf_op jit(solution)/shard_map/ppermute | solution.py:28
  133.1 68.4 %collective-permute-start.34 = (bf16[4,2,24,3072]{3,2,1,0:T(8,128)(2,1)S(1)}, bf16[4,2,24,3072]{3,2,1,0:T(8,128)(2,1)S(1)}, u32[]{:S(2)}, u32[]{:S(2)}) collective-permute-start(bf16[4,2,24,3072]{3,2,1,0:T(8,128)(2,1)S(1)} %bitcast_dynamic-update-slice_fusion.36), channel_id=1, source_target_pairs={{0,4},{1,5},{2,6},{3,7},{4,0},{5,1},{6,2},{7,3},{8,12},{9,13},{10,... | collective-permute-start | bytes 3538952 | tf_op jit(solution)/shard_map/ppermute | solution.py:28
  137.0 66.2 %collective-permute-start.40 = (bf16[4,2,96,768]{3,2,1,0:T(8,128)(2,1)S(1)}, bf16[4,2,96,768]{3,2,1,0:T(8,128)(2,1)S(1)}, u32[]{:S(2)}, u32[]{:S(2)}) collective-permute-start(bf16[4,2,96,768]{3,2,1,0:T(8,128)(2,1)S(1)} %bitcast_dynamic-update-slice_fusion.34), channel_id=1, source_target_pairs={{0,1},{1,0},{2,3},{3,2},{4,5},{5,4},{6,7},{7,6},{8,9},{9,8},{10,11... | collective-permute-start | bytes 3538952 | tf_op jit(solution)/shard_map/ppermute | solution.py:28
  148.4 61.8 %collective-permute-start.16 = (bf16[4,2,96,768]{3,2,1,0:T(8,128)(2,1)S(1)}, bf16[4,2,96,768]{3,2,1,0:T(8,128)(2,1)S(1)}, u32[]{:S(2)}, u32[]{:S(2)}) collective-permute-start(bf16[4,2,96,768]{3,2,1,0:T(8,128)(2,1)S(1)} %bitcast_dynamic-update-slice_fusion.40), channel_id=1, source_target_pairs={{0,1},{1,0},{2,3},{3,2},{4,5},{5,4},{6,7},{7,6},{8,9},{9,8},{10,11... | collective-permute-start | bytes 3538952 | tf_op jit(solution)/shard_map/ppermute | solution.py:28
  149.9 49.0 %collective-permute-start.10 = (bf16[4,2,24,3072]{3,2,1,0:T(8,128)(2,1)S(1)}, bf16[4,2,24,3072]{3,2,1,0:T(8,128)(2,1)S(1)}, u32[]{:S(2)}, u32[]{:S(2)}) collective-permute-start(bf16[4,2,24,3072]{3,2,1,0:T(8,128)(2,1)S(1)} %bitcast_dynamic-update-slice_fusion.41), channel_id=1, source_target_pairs={{0,4},{1,5},{2,6},{3,7},{4,0},{5,1},{6,2},{7,3},{8,12},{9,13},{10,... | collective-permute-start | bytes 3538952 | tf_op jit(solution)/shard_map/ppermute | solution.py:28
  153.7 95.4 %collective-permute-start.28 = (bf16[4,2,24,3200]{3,2,1,0:T(8,128)(2,1)S(1)}, bf16[4,2,24,3200]{3,2,1,0:T(8,128)(2,1)S(1)}, u32[]{:S(2)}, u32[]{:S(2)}) collective-permute-start(bf16[4,2,24,3200]{3,2,1,0:T(8,128)(2,1)S(1)} %bitcast_dynamic-update-slice_fusion.28), channel_id=1, source_target_pairs={{0,4},{1,5},{2,6},{3,7},{4,0},{5,1},{6,2},{7,3},{8,12},{9,13},{10,... | collective-permute-start | bytes 3686408 | tf_op jit(solution)/shard_map/ppermute | solution.py:28
  198.9 49.3 %collective-permute-start.4 = (bf16[4,2,24,3200]{3,2,1,0:T(8,128)(2,1)S(1)}, bf16[4,2,24,3200]{3,2,1,0:T(8,128)(2,1)S(1)}, u32[]{:S(2)}, u32[]{:S(2)}) collective-permute-start(bf16[4,2,24,3200]{3,2,1,0:T(8,128)(2,1)S(1)} %bitcast_dynamic-update-slice_fusion.33), channel_id=1, source_target_pairs={{0,4},{1,5},{2,6},{3,7},{4,0},{5,1},{6,2},{7,3},{8,12},{9,13},{10,... | collective-permute-start | bytes 3686408 | tf_op jit(solution)/shard_map/ppermute | solution.py:28
  203.2 61.9 %collective-permute-start.35 = (bf16[4,2,2,24,3072]{4,3,2,1,0:T(8,128)(2,1)}, bf16[4,2,2,24,3072]{4,3,2,1,0:T(8,128)(2,1)}, u32[]{:S(2)}, u32[]{:S(2)}) collective-permute-start(bf16[4,2,2,24,3072]{4,3,2,1,0:T(8,128)(2,1)} %bitcast_dynamic-update-slice_fusion.22), channel_id=1, source_target_pairs={{0,2},{1,3},{2,0},{3,1},{4,6},{5,7},{6,4},{7,5},{8,10},{9,11},{10,... | collective-permute-start | bytes 7077896 | tf_op jit(solution)/shard_map/ppermute | solution.py:28
  210.2 50.0 %collective-permute-start.41 = (bf16[4,2,2,96,768]{4,3,2,1,0:T(8,128)(2,1)S(1)}, bf16[4,2,2,96,768]{4,3,2,1,0:T(8,128)(2,1)}, u32[]{:S(2)}, u32[]{:S(2)}) collective-permute-start(bf16[4,2,2,96,768]{4,3,2,1,0:T(8,128)(2,1)S(1)} %bitcast_dynamic-update-slice_fusion.20), channel_id=1, source_target_pairs={{0,2},{1,3},{2,0},{3,1},{4,6},{5,7},{6,4},{7,5},{8,10},{9,11},{10,... | collective-permute-start | bytes 7077896 | tf_op jit(solution)/shard_map/ppermute | solution.py:28
  253.2 58.0 %collective-permute-start.29 = (bf16[4,2,2,24,3200]{4,3,2,1,0:T(8,128)(2,1)}, bf16[4,2,2,24,3200]{4,3,2,1,0:T(8,128)(2,1)}, u32[]{:S(2)}, u32[]{:S(2)}) collective-permute-start(bf16[4,2,2,24,3200]{4,3,2,1,0:T(8,128)(2,1)} %bitcast_dynamic-update-slice_fusion.14), channel_id=1, source_target_pairs={{0,2},{1,3},{2,0},{3,1},{4,6},{5,7},{6,4},{7,5},{8,10},{9,11},{10,... | collective-permute-start | bytes 7372808 | tf_op jit(solution)/shard_map/ppermute | solution.py:28
  510.7 45.4 %collective-permute-start.60 = (bf16[4,2,2,24,3200]{4,3,0,1,2:T(8,128)(2,1)}, bf16[4,2,2,24,3200]{4,3,0,1,2:T(8,128)(2,1)}, u32[]{:S(2)}, u32[]{:S(2)}) collective-permute-start(bf16[4,2,2,24,3200]{4,3,0,1,2:T(8,128)(2,1)} %bitcast.584), channel_id=1, source_target_pairs={{0,2},{1,3},{2,0},{3,1},{4,6},{5,7},{6,4},{7,5},{8,10},{9,11},{10,... | collective-permute-start | bytes 7372808 | tf_op jit(solution)/shard_map/ppermute | solution.py:28
  554.3 51.9 %collective-permute-start.79 = (bf16[4,2,96,768]{3,2,0,1:T(8,128)(2,1)S(1)}, bf16[4,2,96,768]{3,2,0,1:T(8,128)(2,1)}, u32[]{:S(2)}, u32[]{:S(2)}) collective-permute-start(bf16[4,2,96,768]{3,2,0,1:T(8,128)(2,1)S(1)} %dynamic-slice_bitcast_fusion.4), channel_id=1, source_target_pairs={{0,1},{1,0},{2,3},{3,2},{4,5},{5,4},{6,7},{7,6},{8,9},{9,8},{10,11... | collective-permute-start | bytes 3538952 | tf_op jit(solution)/shard_map/ppermute | solution.py:28
  560.2 50.2 %collective-permute-start.73 = (bf16[4,2,24,3072]{3,2,0,1:T(8,128)(2,1)S(1)}, bf16[4,2,24,3072]{3,2,0,1:T(8,128)(2,1)}, u32[]{:S(2)}, u32[]{:S(2)}) collective-permute-start(bf16[4,2,24,3072]{3,2,0,1:T(8,128)(2,1)S(1)} %dynamic-slice_bitcast_fusion.5), channel_id=1, source_target_pairs={{0,4},{1,5},{2,6},{3,7},{4,0},{5,1},{6,2},{7,3},{8,12},{9,13},{10,... | collective-permute-start | bytes 3538952 | tf_op jit(solution)/shard_map/ppermute | solution.py:28
  562.5 69.6 %collective-permute-start.61 = (bf16[4,2,24,3200]{3,2,0,1:T(8,128)(2,1)S(1)}, bf16[4,2,24,3200]{3,2,0,1:T(8,128)(2,1)S(1)}, u32[]{:S(2)}, u32[]{:S(2)}) collective-permute-start(bf16[4,2,24,3200]{3,2,0,1:T(8,128)(2,1)S(1)} %dynamic-slice_bitcast_fusion.2), channel_id=1, source_target_pairs={{0,1},{1,0},{2,3},{3,2},{4,5},{5,4},{6,7},{7,6},{8,9},{9,8},{10,11... | collective-permute-start | bytes 3686408 | tf_op jit(solution)/shard_map/ppermute | solution.py:28
  585.2 51.5 %collective-permute-start.67 = (bf16[4,2,24,3200]{3,2,0,1:T(8,128)(2,1)S(1)}, bf16[4,2,24,3200]{3,2,0,1:T(8,128)(2,1)S(1)}, u32[]{:S(2)}, u32[]{:S(2)}) collective-permute-start(bf16[4,2,24,3200]{3,2,0,1:T(8,128)(2,1)S(1)} %dynamic-slice_bitcast_fusion.1), channel_id=1, source_target_pairs={{0,4},{1,5},{2,6},{3,7},{4,0},{5,1},{6,2},{7,3},{8,12},{9,13},{10,... | collective-permute-start | bytes 3686408 | tf_op jit(solution)/shard_map/ppermute | solution.py:28
  588.4 74.6 %collective-permute-start.43 = (bf16[4,2,24,3200]{3,2,1,0:T(8,128)(2,1)S(1)}, bf16[4,2,24,3200]{3,2,1,0:T(8,128)(2,1)S(1)}, u32[]{:S(2)}, u32[]{:S(2)}) collective-permute-start(bf16[4,2,24,3200]{3,2,1,0:T(8,128)(2,1)S(1)} %dynamic-slice_bitcast_fusion.3), channel_id=1, source_target_pairs={{0,4},{1,5},{2,6},{3,7},{4,0},{5,1},{6,2},{7,3},{8,12},{9,13},{10,... | collective-permute-start | bytes 3686408 | tf_op jit(solution)/shard_map/ppermute | solution.py:28
  606.2 69.5 %collective-permute-start.56 = (bf16[4,96,768]{2,1,0:T(8,128)(2,1)S(1)}, bf16[4,96,768]{2,1,0:T(8,128)(2,1)S(1)}, u32[]{:S(2)}, u32[]{:S(2)}) collective-permute-start(bf16[4,96,768]{2,1,0:T(8,128)(2,1)S(1)} %dynamic-slice_bitcast_fusion.13), channel_id=1, source_target_pairs={{0,4},{1,5},{2,6},{3,7},{4,0},{5,1},{6,2},{7,3},{8,12},{9,13},{10,... | collective-permute-start | bytes 1769480 | tf_op jit(solution)/shard_map/ppermute | solution.py:28
  610.5 77.8 %collective-permute-start.80 = (bf16[4,96,768]{2,1,0:T(8,128)(2,1)S(1)}, bf16[4,96,768]{2,1,0:T(8,128)(2,1)S(1)}, u32[]{:S(2)}, u32[]{:S(2)}) collective-permute-start(bf16[4,96,768]{2,1,0:T(8,128)(2,1)S(1)} %dynamic-slice_bitcast_fusion.11), channel_id=1, source_target_pairs={{0,4},{1,5},{2,6},{3,7},{4,0},{5,1},{6,2},{7,3},{8,12},{9,13},{10,... | collective-permute-start | bytes 1769480 | tf_op jit(solution)/shard_map/ppermute | solution.py:28
  663.0 72.8 %collective-permute-start.62 = (bf16[4,24,3200]{2,1,0:T(8,128)(2,1)S(1)}, bf16[4,24,3200]{2,1,0:T(8,128)(2,1)S(1)}, u32[]{:S(2)}, u32[]{:S(2)}) collective-permute-start(bf16[4,24,3200]{2,1,0:T(8,128)(2,1)S(1)} %dynamic-slice_bitcast_fusion.9), channel_id=1, source_target_pairs={{0,4},{1,5},{2,6},{3,7},{4,0},{5,1},{6,2},{7,3},{8,12},{9,13},{10,... | collective-permute-start | bytes 1843208 | tf_op jit(solution)/shard_map/ppermute | solution.py:28
  665.0 74.9 %collective-permute-start.68 = (bf16[4,24,3200]{2,1,0:T(8,128)(2,1)S(1)}, bf16[4,24,3200]{2,1,0:T(8,128)(2,1)S(1)}, u32[]{:S(2)}, u32[]{:S(2)}) collective-permute-start(bf16[4,24,3200]{2,1,0:T(8,128)(2,1)S(1)} %dynamic-slice_bitcast_fusion.8), channel_id=1, source_target_pairs={{0,1},{1,0},{2,3},{3,2},{4,5},{5,4},{6,7},{7,6},{8,9},{9,8},{10,11... | collective-permute-start | bytes 1843208 | tf_op jit(solution)/shard_map/ppermute | solution.py:28
  (188 other events, 2669.3 us)

commit v2 on v1

v2 whole, which is shorter than its diff:
```python
import functools

import jax
import jax.numpy as jnp
from jax import lax
from jax.experimental import pallas as pl
from jax.experimental.pallas import tpu as pltpu
from jax.sharding import PartitionSpec as P

DH = 64
AXES = ("dp", "hd")
EPS = 1e-05
MASKED = -1e30
LANES = 128
bf16 = jnp.bfloat16
f32 = jnp.float32
sds = jax.ShapeDtypeStruct


BIT_PAIR, BIT_CORE, BIT_NEAR = 1, 2, 4


class Place:
    def __init__(self):
        self.count = lax.axis_size("dp") * lax.axis_size("hd")
        self.outer_size = self.count // 8
        index = lax.axis_index("dp") * lax.axis_size("hd") + lax.axis_index("hd")
        self.pair = index % 2
        self.core = (index // 2) % 2
        self.near = (index // 4) % 2
        self.outer = index // 8

    def swap(self, x, bit):
        return lax.ppermute(x, AXES, [(i, i ^ bit) for i in range(self.count)])

    def shift(self, x, k):
        n = self.count
        return lax.ppermute(x, AXES, [(i, (i + 8 * k) % n) for i in range(n)])

    def order(self, d):
        n, rows = self.outer_size, d // self.count
        k = lax.broadcasted_iota(jnp.int32, (d, 1), 0)
        row = k % rows
        outer = (self.outer + (k // rows) % n) % n
        rest = k // (rows * n)
        pair = (self.pair + rest % 2) % 2
        near = (self.near + (rest // 2) % 2) % 2
        core = (self.core + rest // 4) % 2
        feature = (((outer * 2 + near) * 2 + core) * 2 + pair) * rows + row
        return (feature == lax.broadcasted_iota(jnp.int32, (d, d), 1)).astype(bf16)


def plus(a, b):
    return (a.astype(f32) + b.astype(f32)).astype(bf16)


def scatter_rows(place, kept, got):
    n = place.outer_size
    half = kept[0].shape[0]
    rows = half // (4 * n)

    def view(x):
        return x.reshape(2, 2, n * rows, x.shape[1])

    ka, ga = view(kept[0]), view(got[0])
    kb, gb = view(kept[1]), view(got[1])
    got_a = place.swap(plus(ka[1], ga[1]), BIT_NEAR)
    got_b = place.swap(plus(kb[:, 1], gb[:, 1]), BIT_PAIR)
    keep_a = plus(ka[0], ga[0])
    keep_b = plus(kb[:, 0], gb[:, 0])
    got_a2 = place.swap(plus(keep_a[1], got_a[1]), BIT_PAIR)
    got_b2 = place.swap(plus(keep_b[1], got_b[1]), BIT_NEAR)
    a = plus(plus(keep_a[0], got_a[0]), got_a2)
    b = plus(plus(keep_b[0], got_b[0]), got_b2)
    t = jnp.concatenate((a, b), axis=1).reshape(n, rows, -1)
    total = t[0].astype(f32)
    for k in range(1, n):
        total = total + place.shift(t[k], k).astype(f32)
    return total


def nn(a, b):
    return jnp.dot(a, b, preferred_element_type=f32)


def nt(a, b):
    return lax.dot_general(a, b, (((1,), (1,)), ((), ())), preferred_element_type=f32)


def tn(a, b):
    return lax.dot_general(a, b, (((0,), (0,)), ((), ())), preferred_element_type=f32)


def unit_norm(x):
    centred = x - jnp.mean(x, axis=-1, keepdims=True)
    inv = lax.rsqrt(jnp.mean(centred * centred, axis=-1, keepdims=True) + EPS)
    return centred * inv, inv


def norm_backward(grad, x, gain):
    unit, inv = unit_norm(x)
    du = grad * gain
    dx = inv * (
        du
        - jnp.mean(du, axis=-1, keepdims=True)
        - unit * jnp.mean(du * unit, axis=-1, keepdims=True)
    )
    return dx, jnp.sum(grad * unit, axis=0, keepdims=True), jnp.sum(grad, axis=0, keepdims=True)


GELU_A = 0.7978845608028654
GELU_B = 0.044715


def two_heads(x):
    first = lax.broadcasted_iota(jnp.int32, x.shape, 1) < DH
    zero = jnp.zeros_like(x)
    return jnp.concatenate((jnp.where(first, x, zero), jnp.where(first, zero, x)), axis=0)


def side_by_side(x):
    n = x.shape[0] // 2
    first = lax.broadcasted_iota(jnp.int32, (n, LANES), 1) < DH
    return jnp.where(first, x[:n], x[n:])


def probabilities(qs, k2, allowed):
    s = jnp.where(allowed, nt(qs, k2) * DH ** (-0.5), MASKED)
    e = jnp.exp(s - jnp.max(s, axis=-1, keepdims=True))
    return e / jnp.sum(e, axis=-1, keepdims=True)


def causal_mask(length):
    row = lax.broadcasted_iota(jnp.int32, (2 * length, length), 0)
    col = lax.broadcasted_iota(jnp.int32, (2 * length, length), 1)
    return jnp.where(row >= length, row - length, row) >= col


def attend_back(q2, k2, v2, do2, allowed):
    scale = DH ** (-0.5)
    qs, dos = two_heads(q2), two_heads(do2)
    p = probabilities(qs, k2, allowed)
    dp = nt(dos, v2)
    ds = (p * (dp - jnp.sum(p * dp, axis=-1, keepdims=True))).astype(bf16)
    dq = side_by_side(nn(ds, k2)) * scale
    dk = tn(ds, qs) * scale
    dv = tn(p.astype(bf16), dos)
    return dq.astype(bf16), dk.astype(bf16), dv.astype(bf16)


def self_forward_kernel(captions, row, x_ref, vec_ref, w_ref, y_ref, a_ref, qkv_ref, o_ref):
    j = pl.program_id(0)

    @pl.when(j == 0)
    def _():
        unit, _inv = unit_norm(x_ref[...])
        a_ref[...] = (unit * vec_ref[row : row + 1] + vec_ref[row + 1 : row + 2]).astype(bf16)

    @pl.when(j < 3)
    def _():
        qkv_ref[j] = nn(a_ref[...], w_ref[...]).astype(bf16)

    @pl.when(j == 3)
    def _():
        length = x_ref.shape[0] // captions
        allowed = causal_mask(length)
        for c in range(captions):
            at = slice(c * length, (c + 1) * length)
            for h in range(0, x_ref.shape[1], LANES):
                cols = slice(h, h + LANES)
                p = probabilities(two_heads(qkv_ref[0, at, cols]), qkv_ref[1, at, cols], allowed)
                o_ref[at, cols] = side_by_side(nn(p.astype(bf16), qkv_ref[2, at, cols])).astype(bf16)
        y_ref[...] = x_ref[...] + nn(o_ref[...], w_ref[...])


def self_backward_kernel(
    captions, row, x_ref, vec_ref, order_ref, a_ref, qkv_ref, o_ref, dx_ref, w_ref,
    out_ref, vg_ref, keep_ref, send_ref, dqkv_ref, at_ref, acc_ref,
):
    j = pl.program_id(0)
    half = keep_ref.shape[0]

    def emit(g):
        keep_ref[...] = g[:half].astype(bf16)
        send_ref[...] = g[half:].astype(bf16)

    @pl.when(j == 0)
    def _():
        dy = dx_ref[...].astype(bf16)
        emit(nn(nt(order_ref[...], o_ref[...]).astype(bf16), dy))
        do = nt(dy, w_ref[...]).astype(bf16)
        length = x_ref.shape[0] // captions
        allowed = causal_mask(length)
        for c in range(captions):
            at = slice(c * length, (c + 1) * length)
            for h in range(0, x_ref.shape[1], LANES):
                cols = slice(h, h + LANES)
                dq, dk, dv = attend_back(
                    qkv_ref[0, at, cols], qkv_ref[1, at, cols], qkv_ref[2, at, cols],
                    do[at, cols], allowed,
                )
                dqkv_ref[0, at, cols] = dq
                dqkv_ref[1, at, cols] = dk
                dqkv_ref[2, at, cols] = dv
        at_ref[...] = nt(order_ref[...], a_ref[...]).astype(bf16)
        acc_ref[...] = jnp.zeros_like(acc_ref)

    @pl.when(j > 0)
    def _():
        d = dqkv_ref[j - 1]
        emit(nn(at_ref[...], d))
        acc_ref[...] += nt(d, w_ref[...])

    @pl.when(j == 3)
    def _():
        dn, gg, gs = norm_backward(acc_ref[...], x_ref[...], vec_ref[row : row + 1])
        out_ref[...] = dx_ref[...] + dn
        vg_ref[0:1] = gg
        vg_ref[1:2] = gs


def cross_forward_kernel(
    captions, row, count_ref, x_ref, vec_ref, kv_ref, w_ref, y_ref, c_ref, q_ref, o_ref
):
    j = pl.program_id(0)
    d = x_ref.shape[1]

    @pl.when(j == 0)
    def _():
        unit, _inv = unit_norm(x_ref[...])
        c = (unit * vec_ref[row : row + 1] + vec_ref[row + 1 : row + 2]).astype(bf16)
        c_ref[...] = c
        q_ref[...] = nn(c, w_ref[...]).astype(bf16)

    @pl.when(j == 1)
    def _():
        length = x_ref.shape[0] // captions
        patches = kv_ref.shape[0] // captions
        slot = lax.broadcasted_iota(jnp.int32, (2 * length, patches), 1)
        for c in range(captions):
            at = slice(c * length, (c + 1) * length)
            keys = slice(c * patches, (c + 1) * patches)
            allowed = slot < count_ref[c]
            for h in range(0, d, LANES):
                cols = slice(h, h + LANES)
                vcols = slice(d + h, d + h + LANES)
                p = probabilities(two_heads(q_ref[at, cols]), kv_ref[keys, cols], allowed)
                o_ref[at, cols] = side_by_side(nn(p.astype(bf16), kv_ref[keys, vcols])).astype(bf16)
        y_ref[...] = x_ref[...] + nn(o_ref[...], w_ref[...])


def cross_backward_kernel(
    captions, row, count_ref, x_ref, vec_ref, order_ref, c_ref, q_ref, o_ref, kv_ref, dx_ref, w_ref,
    out_ref, vg_ref, keep_ref, send_ref, dkv_ref, dq_ref,
):
    j = pl.program_id(0)
    half = keep_ref.shape[0]
    d = x_ref.shape[1]

    def emit(g):
        keep_ref[...] = g[:half].astype(bf16)
        send_ref[...] = g[half:].astype(bf16)

    @pl.when(j == 0)
    def _():
        dy = dx_ref[...].astype(bf16)
        emit(nn(nt(order_ref[...], o_ref[...]).astype(bf16), dy))
        do = nt(dy, w_ref[...]).astype(bf16)
        length = x_ref.shape[0] // captions
        patches = kv_ref.shape[0] // captions
        slot = lax.broadcasted_iota(jnp.int32, (2 * length, patches), 1)
        for c in range(captions):
            at = slice(c * length, (c + 1) * length)
            keys = slice(c * patches, (c + 1) * patches)
            allowed = slot < count_ref[c]
            for h in range(0, d, LANES):
                cols = slice(h, h + LANES)
                vcols = slice(d + h, d + h + LANES)
                dq, dk, dv = attend_back(
                    q_ref[at, cols], kv_ref[keys, cols], kv_ref[keys, vcols], do[at, cols], allowed
                )
                dq_ref[at, cols] = dq
                dkv_ref[keys, cols] = dk
                dkv_ref[keys, vcols] = dv

    @pl.when(j == 1)
    def _():
        dq = dq_ref[...]
        emit(nn(nt(order_ref[...], c_ref[...]).astype(bf16), dq))
        dn, gg, gs = norm_backward(nt(dq, w_ref[...]), x_ref[...], vec_ref[row : row + 1])
        out_ref[...] = dx_ref[...] + dn
        vg_ref[0:1] = gg
        vg_ref[1:2] = gs


def feed_forward_kernel(row, x_ref, vec_ref, up_ref, down_ref, y_ref, b_ref, u_ref):
    @pl.when(pl.program_id(0) == 0)
    def _():
        unit, _inv = unit_norm(x_ref[...])
        b_ref[...] = (unit * vec_ref[row : row + 1] + vec_ref[row + 1 : row + 2]).astype(bf16)
        y_ref[...] = x_ref[...]

    u = nn(b_ref[...], up_ref[...])
    u_ref[...] = u
    g = 0.5 * u * (1.0 + jnp.tanh(GELU_A * (u + GELU_B * u * u * u)))
    y_ref[...] += nn(g.astype(bf16), down_ref[...])


def feed_backward_kernel(
    row, x_ref, vec_ref, order_ref, b_ref, u_ref, dx_ref, up_ref, down_ref,
    out_ref, vg_ref, keep_ref, send_ref, bt_ref, acc_ref,
):
    j = pl.program_id(0)
    half = keep_ref.shape[0]
    d = x_ref.shape[1]

    @pl.when(j == 0)
    def _():
        bt_ref[...] = nt(order_ref[...], b_ref[...]).astype(bf16)
        acc_ref[...] = jnp.zeros_like(acc_ref)

    u = u_ref[...]
    t = jnp.tanh(GELU_A * (u + GELU_B * u * u * u))
    g = (0.5 * u * (1.0 + t)).astype(bf16)
    slope = 0.5 * (1.0 + t) + 0.5 * u * (1.0 - t * t) * GELU_A * (1.0 + 3.0 * GELU_B * u * u)
    dz = dx_ref[...].astype(bf16)
    du = (slope * nt(dz, down_ref[...])).astype(bf16)
    acc_ref[...] += nt(du, up_ref[...])
    g_up = nn(bt_ref[...], du)
    keep_ref[:, :d] = g_up[:half].astype(bf16)
    send_ref[:, :d] = g_up[half:].astype(bf16)
    g_down = nn(nt(order_ref[...], g).astype(bf16), dz)
    keep_ref[:, d:] = g_down[:half].astype(bf16)
    send_ref[:, d:] = g_down[half:].astype(bf16)

    @pl.when(j == 3)
    def _():
        dn, gg, gs = norm_backward(acc_ref[...], x_ref[...], vec_ref[row : row + 1])
        out_ref[...] = dx_ref[...] + dn
        vg_ref[0:1] = gg
        vg_ref[1:2] = gs


def whole(x):
    return pl.BlockSpec(x.shape, lambda *_: (0,) * len(x.shape))


def call(kernel, steps, ins, in_specs, outs, out_specs, scratch=(), scalars=0, flops=0):
    size = sum(x.size * x.dtype.itemsize for x in outs)
    return pl.pallas_call(
        kernel,
        out_shape=outs,
        grid_spec=pltpu.PrefetchScalarGridSpec(
            num_scalar_prefetch=scalars,
            grid=(steps,),
            in_specs=in_specs,
            out_specs=out_specs,
            scratch_shapes=scratch,
        ),
        compiler_params=pltpu.CompilerParams(
            dimension_semantics=("arbitrary",), vmem_limit_bytes=40 << 20
        ),
        cost_estimate=pl.CostEstimate(flops=flops, bytes_accessed=2 * size, transcendentals=0),
    )(*ins)


class Layers:
    def __init__(self, captions, tokens, d, w, vec, order, count):
        self.captions, self.t, self.d = captions, tokens, d
        self.w, self.vec, self.order, self.count = w, vec, order, count
        self.xs = sds((tokens, d), f32)
        self.hs = sds((tokens, d), bf16)

    def weight(self, index):
        return pl.BlockSpec((self.d, self.d), lambda j, *_: (0, index(j)))

    def self_forward(self, x, at, row):
        outs = (self.xs, self.hs, sds((3, self.t, self.d), bf16), self.hs)
        return call(
            functools.partial(self_forward_kernel, self.captions, row), 4,
            (x, self.vec, self.w),
            [whole(x), whole(self.vec), self.weight(lambda j: at + j)],
            outs, [whole(o) for o in outs], flops=8 * self.t * self.d * self.d,
        )

    def self_backward(self, x, kept, dx, at, row):
        d, t = self.d, self.t
        a, qkv, o = kept
        outs = (self.xs, sds((8, d), f32), sds((d // 2, 4 * d), bf16), sds((d // 2, 4 * d), bf16))
        grad = pl.BlockSpec((d // 2, d), lambda j: (0, (j + 3) % 4))
        ins = (x, self.vec, self.order, a, qkv, o, dx)
        return call(
            functools.partial(self_backward_kernel, self.captions, row), 4,
            ins + (self.w,),
            [whole(i) for i in ins] + [self.weight(lambda j: at + (j + 3) % 4)],
            outs, [whole(outs[0]), whole(outs[1]), grad, grad],
            scratch=[pltpu.VMEM((3, t, d), bf16), pltpu.VMEM((d, t), bf16), pltpu.VMEM((t, d), f32)],
            flops=20 * t * d * d,
        )

    def cross_forward(self, x, kv, at, row):
        outs = (self.xs, self.hs, self.hs, self.hs)
        return call(
            functools.partial(cross_forward_kernel, self.captions, row), 2,
            (self.count, x, self.vec, kv, self.w),
            [whole(x), whole(self.vec), whole(kv), self.weight(lambda j: at + 3 * j)],
            outs, [whole(o) for o in outs], scalars=1, flops=10 * self.t * self.d * self.d,
        )

    def cross_backward(self, x, kept, kv, dx, at, row):
        d, t = self.d, self.t
        c, q, o = kept
        outs = (
            self.xs, sds((8, d), f32), sds((d // 2, 2 * d), bf16), sds((d // 2, 2 * d), bf16),
            sds(kv.shape, bf16),
        )
        grad = pl.BlockSpec((d // 2, d), lambda j, *_: (0, 1 - j))
        ins = (x, self.vec, self.order, c, q, o, kv, dx)
        return call(
            functools.partial(cross_backward_kernel, self.captions, row), 2,
            (self.count,) + ins + (self.w,),
            [whole(i) for i in ins] + [self.weight(lambda j: at + 3 - 3 * j)],
            outs, [whole(outs[0]), whole(outs[1]), grad, grad, whole(outs[4])],
            scratch=[pltpu.VMEM((t, d), bf16)], scalars=1, flops=30 * t * d * d,
        )

    def feed_forward(self, x, at, row):
        d, t = self.d, self.t
        outs = (self.xs, self.hs, sds((t, 4 * d), f32))
        return call(
            functools.partial(feed_forward_kernel, row), 4,
            (x, self.vec, self.w, self.w),
            [whole(x), whole(self.vec), self.weight(lambda j: at + j), self.weight(lambda j: at + 4 + j)],
            outs, [whole(outs[0]), whole(outs[1]), pl.BlockSpec((t, d), lambda j: (0, j))],
            flops=16 * t * d * d,
        )

    def feed_backward(self, x, kept, dx, at, row):
        d, t = self.d, self.t
        b, u = kept
        outs = (self.xs, sds((8, d), f32), sds((d // 2, 8 * d), bf16), sds((d // 2, 8 * d), bf16))
        grad = pl.BlockSpec((d // 2, 2 * d), lambda j: (0, j))
        return call(
            functools.partial(feed_backward_kernel, row), 4,
            (x, self.vec, self.order, b, u, dx, self.w, self.w),
            [
                whole(x), whole(self.vec), whole(self.order), whole(b),
                pl.BlockSpec((t, d), lambda j: (0, j)), whole(dx),
                self.weight(lambda j: at + j), self.weight(lambda j: at + 4 + j),
            ],
            outs, [whole(outs[0]), whole(outs[1]), grad, grad],
            scratch=[pltpu.VMEM((d, t), bf16), pltpu.VMEM((t, d), f32)],
            flops=44 * t * d * d,
        )


def spread_matrix():
    k = lax.broadcasted_iota(jnp.int32, (512, 512), 0)
    n = lax.broadcasted_iota(jnp.int32, (512, 512), 1)
    return (k % 4) * 128 + k // 4 == n


def spread(up):
    rows, wide = up.shape
    y = nn(up.reshape(rows * (wide // 512), 512), spread_matrix().astype(bf16)).astype(bf16)
    return y.reshape(rows, wide // 512, 4, 128).transpose(0, 2, 1, 3).reshape(rows, wide)


def unspread(up):
    rows, wide = up.shape
    y = up.reshape(rows, 4, wide // 512, 128).transpose(0, 2, 1, 3)
    y = lax.dot_general(
        y.reshape(rows * (wide // 512), 512), spread_matrix().astype(f32),
        (((1,), (1,)), ((), ())), precision=lax.Precision.HIGHEST,
    )
    return y.reshape(rows, wide)


def local(
    tokens, encoder, patch_count, out_grad,
    u_ag, u_as, u_qkv, u_out, u_mg, u_ms, u_up, u_down,
    m_ag, m_as, m_qkv, m_out, c_g, c_s, c_q, c_pair, c_out, m_mg, m_ms, m_up, m_down,
):
    place = Place()
    captions, length, d = tokens.shape
    rows = u_qkv.shape[0]
    x0 = tokens.reshape(-1, d).astype(f32)
    enc = encoder.reshape(-1, d)
    order = place.order(d)

    vectors = (u_ag, u_as, u_mg, u_ms, m_ag, m_as, c_g, c_s, m_mg, m_ms)
    cols = jnp.pad(jnp.stack(vectors, axis=1), ((0, 0), (0, LANES - len(vectors))))
    shard = jnp.concatenate(
        (
            u_qkv, u_out, spread(u_up), u_down.reshape(rows, -1),
            m_qkv, m_out, spread(m_up), m_down.reshape(rows, -1),
            c_q, c_pair, c_out, cols,
        ),
        axis=1,
    )
    w = lax.all_gather(shard, AXES, axis=0, tiled=True)
    vec = w[:, 28 * d : 28 * d + 16].astype(f32).T
    enc_t = nt(order, enc).astype(bf16)

    net = Layers(captions, captions * length, d, w, vec, order, patch_count)

    w_pair = w[:, 25 * d : 27 * d]
    kv = nn(enc, w_pair).astype(bf16)
    x0a, *k_us = net.self_forward(x0, 0, 0)
    x1, *k_uf = net.feed_forward(x0a, 4, 2)
    x1a, *k_ms = net.self_forward(x1, 12, 4)
    x1b, *k_mc = net.cross_forward(x1a, kv, 24, 6)
    x2, *k_mf = net.feed_forward(x1b, 16, 8)

    def core(x):
        return place.swap(x, BIT_CORE)

    def halves(x):
        at = x.shape[1] // 2
        return x[:, :at], x[:, at:]

    dx = out_grad.reshape(-1, d).astype(f32)
    dx, v_mf, keep, send = net.feed_backward(x1b, k_mf, dx, 16, 8)
    r_mf = scatter_rows(place, halves(keep), halves(core(send)))
    dx, v_mc, keep, send, dkv = net.cross_backward(x1a, k_mc, kv, dx, 24, 6)
    g_pair = nn(enc_t, dkv).astype(bf16)
    denc = nt(dkv, w_pair).astype(bf16)
    r_mc = scatter_rows(
        place, (keep, g_pair[: d // 2]), (core(send), core(g_pair[d // 2 :]))
    )
    dx, v_ms, keep, send = net.self_backward(x1, k_ms, dx, 12, 4)
    r_ms = scatter_rows(place, halves(keep), halves(core(send)))
    dx, v_uf, keep, send = net.feed_backward(x0a, k_uf, dx, 4, 2)
    r_uf = scatter_rows(place, halves(keep), halves(core(send)))
    dx, v_us, keep, send = net.self_backward(x0, k_us, dx, 0, 0)
    v = jnp.concatenate([g[:2] for g in (v_us, v_uf, v_ms, v_mc, v_mf)], axis=0).astype(bf16)
    v = nt(order, jnp.pad(v, ((0, LANES - v.shape[0]), (0, 0)))).astype(bf16)
    got = core(send)
    got_v = core(v[d // 2 :])
    at = 2 * d
    r_us = scatter_rows(
        place,
        (keep[:, :at], jnp.concatenate((keep[:, at:], v[: d // 2]), axis=1)),
        (got[:, :at], jnp.concatenate((got[:, at:], got_v), axis=1)),
    )

    def feed_rows(r):
        up = jnp.concatenate([r[:, (2 * j) * d : (2 * j + 1) * d] for j in range(4)], axis=1)
        down = jnp.concatenate([r[:, (2 * j + 1) * d : (2 * j + 2) * d] for j in range(4)], axis=1)
        return unspread(up), down.reshape(-1, d)

    r_uup, r_udown = feed_rows(r_uf)
    r_mup, r_mdown = feed_rows(r_mf)
    vs = r_us[:, 4 * d :]
    v = [vs[:, i] for i in range(10)]
    return (
        x2.astype(bf16).reshape(tokens.shape),
        dx.astype(bf16).reshape(tokens.shape),
        denc.reshape(encoder.shape),
        v[0], v[1], r_us[:, : 3 * d], r_us[:, 3 * d : 4 * d], v[2], v[3], r_uup, r_udown,
        v[4], v[5], r_ms[:, : 3 * d], r_ms[:, 3 * d :], v[6], v[7],
        r_mc[:, :d], r_mc[:, 2 * d :], r_mc[:, d : 2 * d],
        v[8], v[9], r_mup, r_mdown,
    )


def solution(mesh):
    rows1 = P(AXES)
    rows2 = P(AXES, None)
    rows3 = P(AXES, None, None)
    block = (rows1, rows1, rows2, rows2)
    weights = block * 2 + block + (rows1, rows1, rows2, rows2, rows2) + block
    return jax.shard_map(
        local,
        mesh=mesh,
        in_specs=(rows3, rows3, rows1, rows3) + weights,
        out_specs=(rows3, rows3, rows3) + weights,
        check_vma=False,
    )
```

time: 784 us -> 625 us (0.80)
  local copies, waits for them, and re-layouts: 207 us -> 60.9 us
  matrix products: 125 us -> 23.6 us
  Pallas kernels: 0 us -> 96.9 us
  waiting for transfers between devices: 284 us -> 359 us
  starting transfers between devices: 110 us -> 44.2 us
  other arithmetic: 47.4 us -> 20.5 us
  between operations: 3.92 us -> 15.7 us
    all_gather x0 -> x1, waiting for transfers between devices: none -> 194 us  [local(): w = lax.all_gather(shard, AXES, axis=0, tiled=True)]
    dot_general x51 -> x8, matrix products: 125 us -> 23.6 us  [the longest x4 14.4 us: nn(): return jnp.dot(a, b, preferred_element_type=f32)]
    pallas_call x0 -> x10, Pallas kernels: none -> 96.9 us  [call(): pl.pallas_call(kernel, out_shape=outs, grid_spec=pltpu.PrefetchScalarGrid...]
    ppermute x42 -> x27, waiting for transfers between devices: 201 us -> 108 us  [swap(): return lax.ppermute(x, AXES, [(i, i ^ bit) for i in range(self.count)])]
    dynamic_update_slice x67 -> x0, local copies, waits for them, and re-layouts: 53.2 us -> none  [the longest x21 25.9 us: join(): return lax.dynamic_update_index_in_dim(out, got, 1 - index, axis)]
    ppermute x42 -> x15, starting transfers between devices: 74.1 us -> 21.2 us  [shift(): return lax.ppermute(x, AXES, [(i, (i + 8 * k) % n) for i in range(n)])]
    convert_element_type x24 -> x0, local copies, waits for them, and re-layouts: 44.1 us -> none  [the longest x6 15.7 us: attend_backward(): dv.reshape(v.shape).astype(bf16)]
    reshape x20 -> x16, local copies, waits for them, and re-layouts: 33.1 us -> 5.52 us  [the longest x2 1.7 us: unspread(): return y.reshape(rows, wide)]
  transfers between devices with their start and end apart: 84 -> 43, of which waited for: 28 -> 25; matrix products, arithmetic and copies ran while one was open for 22% -> 9% of each run, Pallas kernels for 0% -> 7%
where the time goes in v2:
time: 625 us; the launch traced here: 621 us
  waiting for transfers between devices  359 us (57%)
  Pallas kernels  96.9 us (16%)
  local copies, waits for them, and re-layouts  60.9 us (10%)
  starting transfers between devices  44.2 us (7%)
  matrix products  23.6 us (4%)
  other arithmetic  20.5 us (3%)
  between operations  15.7 us (3%)
    all_gather x1, waiting for transfers between devices, local(): w = lax.all_gather(shard, AXES, axis=0, tiled=True)  194 us
    ppermute x27, waiting for transfers between devices, swap(): return lax.ppermute(x, AXES, [(i, i ^ bit) for i in range(self.count)])  108 us
    pallas_call x10, Pallas kernels, call(): pl.pallas_call(kernel, out_shape=outs, grid_spec=pltpu.PrefetchScalarGrid...  96.9 us
    ppermute x15, waiting for transfers between devices, shift(): return lax.ppermute(x, AXES, [(i, (i + 8 * k) % n) for i in range(n)])  56.9 us
    ppermute x27, starting transfers between devices, swap(): return lax.ppermute(x, AXES, [(i, i ^ bit) for i in range(self.count)])  22.9 us
    unnamed x159, local copies, waits for them, and re-layouts  22.7 us
    ppermute x15, starting transfers between devices, shift(): return lax.ppermute(x, AXES, [(i, (i + 8 * k) % n) for i in range(n)])  21.2 us
    dot_general x4, matrix products, nn(): return jnp.dot(a, b, preferred_element_type=f32)  14.4 us
  transfers between devices with their start and end apart: 43, of which 25 were waited for; matrix products, arithmetic and copies ran while one was open for 9% of the time, Pallas kernels for 7%

profile of v2, /device:TPU:0, one launch (start us, length us, event | category | flops | bytes accessed | tf_op | source)
XLA Modules:
  0.0 620.8 jit_solution(13789938665460271455)
XLA Ops:
  31.6 194.0 %all-gather.2.cloned.1.call-done.w_ref.up_ref.down_ref = bf16[768,21632]{1,0:T(8,128)(2,1)} async-done(((bf16[24,21632]{1,0:T(8,128)(2,1)}), bf16[768,21632]{1,0:T(8,128)(2,1)}) %all-gather.2.cloned.1.call-update) | async-done | bytes 33226768 | tf_op jit(solution)/shard_map/all_gather | solution.py:501
  228.4 5.4 shard_map.424
  236.0 5.9 shard_map.425
  243.0 5.1 shard_map.426
  255.2 7.5 %shard_map.427 = (f32[128,768]{1,0:T(8,128)S(1)}, bf16[128,768]{1,0:T(8,128)(2,1)S(1)}, bf16[128,768]{1,0:T(8,128)(2,1)S(1)}, bf16[128,768]{1,0:T(8,128)(2,1)S(1)}) custom-call(s32[2]{0:T(128)S(1)} %copy-done.35, f32[128,768]{1,0:T(8,128)S(1)} %get-tuple-element.65.x_ref, f32[16,768]{1,0:T(8,128)S(1)} %copy.85.vec_ref, bf16[1152,1536]{1,0:T(8,128)(2,1)S(1)} %fusion.kv_ref, ...), custom_call_target="tpu_custom_call" | custom-call | flops 754974720 | bytes 1966080 | tf_op jit(solution)/shard_map/pallas_call | solution.py:350
  262.8 5.8 shard_map.428
  269.3 13.0 %shard_map.429 = (f32[128,768]{1,0:T(8,128)S(1)}, f32[8,768]{1,0:T(8,128)S(1)}, bf16[384,6144]{1,0:T(8,128)(2,1)S(1)}, bf16[384,6144]{1,0:T(8,128)(2,1)S(1)}) custom-call(f32[128,768]{1,0:T(8,128)S(1)} %get-tuple-element.66.x_ref, f32[16,768]{1,0:T(8,128)S(1)} %copy.85.vec_ref, bf16[768,768]{1,0:T(8,128)(2,1)S(1)} %fusion.2.order_ref, ...), custom_call_target="tpu_custom_call" | custom-call | flops 3321888768 | bytes 19709952 | tf_op jit(solution)/shard_map/pallas_call | solution.py:350
  286.6 13.6 %shard_map.430 = (f32[128,768]{1,0:T(8,128)S(1)}, f32[8,768]{1,0:T(8,128)S(1)}, bf16[384,1536]{1,0:T(8,128)(2,1)S(1)}, bf16[384,1536]{1,0:T(8,128)(2,1)}, bf16[1152,1536]{1,0:T(8,128)(2,1)S(1)}) custom-call(s32[2]{0:T(128)S(1)} %copy-done.35, f32[128,768]{1,0:T(8,128)S(1)} %get-tuple-element.65.x_ref, f32[16,768]{1,0:T(8,128)S(1)} %copy.85.vec_ref, ...), custom_call_target="tpu_custom_call" | custom-call | flops 2264924160 | bytes 12632064 | tf_op jit(solution)/shard_map/pallas_call | solution.py:350
  304.0 8.3 %convolution_convert_fusion.1 = bf16[768,1536]{1,0:T(8,128)(2,1)} fusion(bf16[1152,1536]{1,0:T(8,128)(2,1)} %copy-done.38, bf16[1152,768]{1,0:T(8,128)(2,1)S(1)} %bitcast.248, s32[768]{0:T(1024)S(1)} %fusion.103), kind=kOutput, calls=%fused_computation.2 | convolution fusion | flops 4079517696 | bytes 7670784 | tf_op jit(solution)/shard_map/dot_general | solution.py:83
  319.2 13.3 %shard_map.431 = (f32[128,768]{1,0:T(8,128)S(1)}, f32[8,768]{1,0:T(8,128)S(1)}, bf16[384,3072]{1,0:T(8,128)(2,1)S(1)}, bf16[384,3072]{1,0:T(8,128)(2,1)}) custom-call(f32[128,768]{1,0:T(8,128)S(1)} %copy-done.11, f32[16,768]{1,0:T(8,128)S(1)} %copy.85.vec_ref, bf16[768,768]{1,0:T(8,128)(2,1)S(1)} %fusion.2.order_ref, bf16[128,768]{1,0:T(8,128)(2,1)S(1)} %copy-done.30, ...), custom_call_target="tpu_custom_call" | custom-call | flops 1509949440 | bytes 10272768 | tf_op jit(solution)/shard_map/pallas_call | solution.py:350
  335.3 13.1 %shard_map.432 = (f32[128,768]{1,0:T(8,128)S(1)}, f32[8,768]{1,0:T(8,128)S(1)}, bf16[384,6144]{1,0:T(8,128)(2,1)S(1)}, bf16[384,6144]{1,0:T(8,128)(2,1)S(1)}) custom-call(f32[128,768]{1,0:T(8,128)S(1)} %copy-done.9, f32[16,768]{1,0:T(8,128)S(1)} %copy.85.vec_ref, bf16[768,768]{1,0:T(8,128)(2,1)S(1)} %fusion.2.order_ref, bf16[128,768]{1,0:T(8,128)(2,1)S(1)} %copy-done.34, ...), custom_call_target="tpu_custom_call" | custom-call | flops 3321888768 | bytes 19709952 | tf_op jit(solution)/shard_map/pallas_call | solution.py:350
  348.5 14.3 %shard_map.433 = (f32[128,768]{1,0:T(8,128)S(1)}, f32[8,768]{1,0:T(8,128)S(1)}, bf16[384,3072]{1,0:T(8,128)(2,1)S(1)}, bf16[384,3072]{1,0:T(8,128)(2,1)}) custom-call(f32[128,768]{1,0:T(8,128)S(1)} %bitcast_convert_fusion.1.x_ref, f32[16,768]{1,0:T(8,128)S(1)} %copy.85.vec_ref, bf16[768,768]{1,0:T(8,128)(2,1)S(1)} %fusion.2.order_ref, ...), custom_call_target="tpu_custom_call" | custom-call | flops 1509949440 | bytes 10272768 | tf_op jit(solution)/shard_map/pallas_call | solution.py:350
  372.1 6.4 %convolution_convert_fusion.3 = bf16[1152,768]{1,0:T(8,128)(2,1)} fusion(bf16[1152,1536]{1,0:T(8,128)(2,1)S(1)} %copy-done.39, bf16[768,21632]{1,0:T(8,128)(2,1)} %all-gather.2.cloned.1.call-done.w_ref.up_ref.down_ref), kind=kOutput, calls=%fused_computation.4 | convolution fusion | flops 2718793728 | bytes 7667712 | tf_op jit(solution)/shard_map/dot_general | solution.py:87
  387.5 5.5 collective-permute-done.27
  404.0 5.1 collective-permute-done.32
  420.9 7.3 %collective-permute-done.20 = bf16[2,96,1536]{2,1,0:T(8,128)(2,1)S(1)} collective-permute-done((bf16[2,96,1536]{2,1,0:T(8,128)(2,1)S(1)}, bf16[2,96,1536]{2,1,0:T(8,128)(2,1)S(1)}, u32[]{:S(2)}, u32[]{:S(2)}) %collective-permute-start.20) | collective-permute-done | bytes 589856 | tf_op jit(solution)/shard_map/ppermute | solution.py:34
  432.8 11.4 %collective-permute-done.1 = bf16[2,96,1536]{2,1,0:T(8,128)(2,1)S(1)} collective-permute-done((bf16[2,96,1536]{2,1,0:T(8,128)(2,1)S(1)}, bf16[2,96,1536]{2,1,0:T(8,128)(2,1)S(1)}, u32[]{:S(2)}, u32[]{:S(2)}) %collective-permute-start.1) | collective-permute-done | bytes 589856 | tf_op jit(solution)/shard_map/ppermute | solution.py:34
  475.0 7.6 %collective-permute-done.7 = bf16[24,3200]{1,0:T(8,128)(2,1)S(1)} collective-permute-done((bf16[24,3200]{1,0:T(8,128)(2,1)S(1)}, bf16[24,3200]{1,0:T(8,128)(2,1)S(1)}, u32[]{:S(2)}, u32[]{:S(2)}) %collective-permute-start.7) | collective-permute-done | bytes 153632 | tf_op jit(solution)/shard_map/ppermute | solution.py:38
  495.0 21.6 %collective-permute-done.37 = bf16[2,96,3072]{2,1,0:T(8,128)(2,1)S(1)} collective-permute-done((bf16[2,96,3072]{2,1,0:T(8,128)(2,1)S(1)}, bf16[2,96,3072]{2,1,0:T(8,128)(2,1)S(1)}, u32[]{:S(2)}, u32[]{:S(2)}) %collective-permute-start.37) | collective-permute-done | bytes 1179680 | tf_op jit(solution)/shard_map/ppermute | solution.py:34
  519.8 22.0 %collective-permute-done.12 = bf16[2,96,3072]{2,1,0:T(8,128)(2,1)S(1)} collective-permute-done((bf16[2,96,3072]{2,1,0:T(8,128)(2,1)S(1)}, bf16[2,96,3072]{2,1,0:T(8,128)(2,1)S(1)}, u32[]{:S(2)}, u32[]{:S(2)}) %collective-permute-start.12) | collective-permute-done | bytes 1179680 | tf_op jit(solution)/shard_map/ppermute | solution.py:34
  545.1 11.5 %collective-permute-done.38 = bf16[96,3072]{1,0:T(8,128)(2,1)S(1)} collective-permute-done((bf16[96,3072]{1,0:T(8,128)(2,1)S(1)}, bf16[96,3072]{1,0:T(8,128)(2,1)S(1)}, u32[]{:S(2)}, u32[]{:S(2)}) %collective-permute-start.38) | collective-permute-done | bytes 589856 | tf_op jit(solution)/shard_map/ppermute | solution.py:34
  561.0 6.1 collective-permute-done.13
  575.5 21.9 %collective-permute-done.40 = bf16[24,6144]{1,0:T(8,128)(2,1)S(1)} collective-permute-done((bf16[24,6144]{1,0:T(8,128)(2,1)S(1)}, bf16[24,6144]{1,0:T(8,128)(2,1)S(1)}, u32[]{:S(2)}, u32[]{:S(2)}) %collective-permute-start.40) | collective-permute-done | bytes 294944 | tf_op jit(solution)/shard_map/ppermute | solution.py:38
  600.7 8.8 %collective-permute-done.15 = bf16[24,6144]{1,0:T(8,128)(2,1)} collective-permute-done((bf16[24,6144]{1,0:T(8,128)(2,1)S(1)}, bf16[24,6144]{1,0:T(8,128)(2,1)}, u32[]{:S(2)}, u32[]{:S(2)}) %collective-permute-start.15) | collective-permute-done | bytes 294944 | tf_op jit(solution)/shard_map/ppermute | solution.py:38
  (356 shorter events, 170.7 us)
Async XLA Ops:
  7.2 218.4 %all-gather.2.cloned.1.call-start = ((), (), s32[]{:S(2)}) async-start(), calls=%async_computation | async-start | bytes 34265088 | tf_op jit(solution)/shard_map/all_gather | solution.py:501
  303.7 62.4 %collective-permute-start.25 = (bf16[384,1536]{1,0:T(8,128)(2,1)}, bf16[384,1536]{1,0:T(8,128)(2,1)}, u32[]{:S(2)}, u32[]{:S(2)}) collective-permute-start(bf16[384,1536]{1,0:T(8,128)(2,1)} %get-tuple-element.99), channel_id=1, source_target_pairs={{0,2},{1,3},{2,0},{3,1},{4,6},{5,7},{6,4},{7,5},{8,10},{9,11},{10,... | collective-permute-start | bytes 3538952 | tf_op jit(solution)/shard_map/ppermute | solution.py:34
  315.5 54.1 %collective-permute-start.28 = (bf16[384,1536]{1,0:T(8,128)(2,1)}, bf16[384,1536]{1,0:T(8,128)(2,1)}, u32[]{:S(2)}, u32[]{:S(2)}) collective-permute-start(bf16[384,1536]{1,0:T(8,128)(2,1)} %get-tuple-element.131), channel_id=1, source_target_pairs={{0,2},{1,3},{2,0},{3,1},{4,6},{5,7},{6,4},{7,5},{8,10},{9,11},{10,... | collective-permute-start | bytes 3538952 | tf_op jit(solution)/shard_map/ppermute | solution.py:34
  334.3 76.2 %collective-permute-start.17 = (bf16[384,3072]{1,0:T(8,128)(2,1)}, bf16[384,3072]{1,0:T(8,128)(2,1)}, u32[]{:S(2)}, u32[]{:S(2)}) collective-permute-start(bf16[384,3072]{1,0:T(8,128)(2,1)} %get-tuple-element.97), channel_id=1, source_target_pairs={{0,2},{1,3},{2,0},{3,1},{4,6},{5,7},{6,4},{7,5},{8,10},{9,11},{10,... | collective-permute-start | bytes 7077896 | tf_op jit(solution)/shard_map/ppermute | solution.py:34
  365.2 50.2 %collective-permute-start = (bf16[384,3072]{1,0:T(8,128)(2,1)}, bf16[384,3072]{1,0:T(8,128)(2,1)}, u32[]{:S(2)}, u32[]{:S(2)}) collective-permute-start(bf16[384,3072]{1,0:T(8,128)(2,1)} %get-tuple-element.88), channel_id=1, source_target_pairs={{0,2},{1,3},{2,0},{3,1},{4,6},{5,7},{6,4},{7,5},{8,10},{9,11},{10,... | collective-permute-start | bytes 7077896 | tf_op jit(solution)/shard_map/ppermute | solution.py:34
  403.5 81.5 %collective-permute-start.34 = (bf16[384,6144]{1,0:T(8,128)(2,1)S(1)}, bf16[384,6144]{1,0:T(8,128)(2,1)S(1)}, u32[]{:S(2)}, u32[]{:S(2)}) collective-permute-start(bf16[384,6144]{1,0:T(8,128)(2,1)S(1)} %bitcast.254), channel_id=1, source_target_pairs={{0,2},{1,3},{2,0},{3,1},{4,6},{5,7},{6,4},{7,5},{8,10},{9,11},{10,... | collective-permute-start | bytes 14155784 | tf_op jit(solution)/shard_map/ppermute | solution.py:34
  409.1 81.8 %collective-permute-start.9 = (bf16[384,6144]{1,0:T(8,128)(2,1)S(1)}, bf16[384,6144]{1,0:T(8,128)(2,1)S(1)}, u32[]{:S(2)}, u32[]{:S(2)}) collective-permute-start(bf16[384,6144]{1,0:T(8,128)(2,1)S(1)} %bitcast.256), channel_id=1, source_target_pairs={{0,2},{1,3},{2,0},{3,1},{4,6},{5,7},{6,4},{7,5},{8,10},{9,11},{10,... | collective-permute-start | bytes 14155784 | tf_op jit(solution)/shard_map/ppermute | solution.py:34
  415.4 16.2 %collective-permute-start.18 = (bf16[2,96,1536]{2,1,0:T(8,128)(2,1)S(1)}, bf16[2,96,1536]{2,1,0:T(8,128)(2,1)S(1)}, u32[]{:S(2)}, u32[]{:S(2)}) collective-permute-start(bf16[2,96,1536]{2,1,0:T(8,128)(2,1)S(1)} %bitcast.272), channel_id=1, source_target_pairs={{0,4},{1,5},{2,6},{3,7},{4,0},{5,1},{6,2},{7,3},{8,12},{9,13},{10,... | collective-permute-start | bytes 1769480 | tf_op jit(solution)/shard_map/ppermute | solution.py:34
  419.5 24.7 %collective-permute-start.1 = (bf16[2,96,1536]{2,1,0:T(8,128)(2,1)S(1)}, bf16[2,96,1536]{2,1,0:T(8,128)(2,1)S(1)}, u32[]{:S(2)}, u32[]{:S(2)}) collective-permute-start(bf16[2,96,1536]{2,1,0:T(8,128)(2,1)S(1)} %bitcast.273), channel_id=1, source_target_pairs={{0,4},{1,5},{2,6},{3,7},{4,0},{5,1},{6,2},{7,3},{8,12},{9,13},{10,... | collective-permute-start | bytes 1769480 | tf_op jit(solution)/shard_map/ppermute | solution.py:34
  428.2 17.1 %collective-permute-start.4 = (bf16[2,96,1664]{2,1,0:T(8,128)(2,1)S(1)}, bf16[2,96,1664]{2,1,0:T(8,128)(2,1)S(1)}, u32[]{:S(2)}, u32[]{:S(2)}) collective-permute-start(bf16[2,96,1664]{2,1,0:T(8,128)(2,1)S(1)} %get-tuple-element.125), channel_id=1, source_target_pairs={{0,1},{1,0},{2,3},{3,2},{4,5},{5,4},{6,7},{7,6},{8,9},{9,8},{10,11... | collective-permute-start | bytes 1916936 | tf_op jit(solution)/shard_map/ppermute | solution.py:34
  431.6 18.6 %collective-permute-start.21 = (bf16[96,1536]{1,0:T(8,128)(2,1)S(1)}, bf16[96,1536]{1,0:T(8,128)(2,1)S(1)}, u32[]{:S(2)}, u32[]{:S(2)}) collective-permute-start(bf16[96,1536]{1,0:T(8,128)(2,1)S(1)} %fusion.60), channel_id=1, source_target_pairs={{0,4},{1,5},{2,6},{3,7},{4,0},{5,1},{6,2},{7,3},{8,12},{9,13},{10,... | collective-permute-start | bytes 884744 | tf_op jit(solution)/shard_map/ppermute | solution.py:34
  487.6 29.0 %collective-permute-start.37 = (bf16[2,96,3072]{2,1,0:T(8,128)(2,1)S(1)}, bf16[2,96,3072]{2,1,0:T(8,128)(2,1)S(1)}, u32[]{:S(2)}, u32[]{:S(2)}) collective-permute-start(bf16[2,96,3072]{2,1,0:T(8,128)(2,1)S(1)} %get-tuple-element.117), channel_id=1, source_target_pairs={{0,1},{1,0},{2,3},{3,2},{4,5},{5,4},{6,7},{7,6},{8,9},{9,8},{10,11... | collective-permute-start | bytes 3538952 | tf_op jit(solution)/shard_map/ppermute | solution.py:34
  489.7 29.0 %collective-permute-start.35 = (bf16[2,96,3072]{2,1,0:T(8,128)(2,1)S(1)}, bf16[2,96,3072]{2,1,0:T(8,128)(2,1)S(1)}, u32[]{:S(2)}, u32[]{:S(2)}) collective-permute-start(bf16[2,96,3072]{2,1,0:T(8,128)(2,1)S(1)} %bitcast.268), channel_id=1, source_target_pairs={{0,4},{1,5},{2,6},{3,7},{4,0},{5,1},{6,2},{7,3},{8,12},{9,13},{10,... | collective-permute-start | bytes 3538952 | tf_op jit(solution)/shard_map/ppermute | solution.py:34
  492.0 49.8 %collective-permute-start.12 = (bf16[2,96,3072]{2,1,0:T(8,128)(2,1)S(1)}, bf16[2,96,3072]{2,1,0:T(8,128)(2,1)S(1)}, u32[]{:S(2)}, u32[]{:S(2)}) collective-permute-start(bf16[2,96,3072]{2,1,0:T(8,128)(2,1)S(1)} %get-tuple-element.121), channel_id=1, source_target_pairs={{0,1},{1,0},{2,3},{3,2},{4,5},{5,4},{6,7},{7,6},{8,9},{9,8},{10,11... | collective-permute-start | bytes 3538952 | tf_op jit(solution)/shard_map/ppermute | solution.py:34
  494.0 49.9 %collective-permute-start.10 = (bf16[2,96,3072]{2,1,0:T(8,128)(2,1)S(1)}, bf16[2,96,3072]{2,1,0:T(8,128)(2,1)S(1)}, u32[]{:S(2)}, u32[]{:S(2)}) collective-permute-start(bf16[2,96,3072]{2,1,0:T(8,128)(2,1)S(1)} %bitcast.269), channel_id=1, source_target_pairs={{0,4},{1,5},{2,6},{3,7},{4,0},{5,1},{6,2},{7,3},{8,12},{9,13},{10,... | collective-permute-start | bytes 3538952 | tf_op jit(solution)/shard_map/ppermute | solution.py:34
  516.7 39.9 %collective-permute-start.38 = (bf16[96,3072]{1,0:T(8,128)(2,1)S(1)}, bf16[96,3072]{1,0:T(8,128)(2,1)S(1)}, u32[]{:S(2)}, u32[]{:S(2)}) collective-permute-start(bf16[96,3072]{1,0:T(8,128)(2,1)S(1)} %fusion.37), channel_id=1, source_target_pairs={{0,4},{1,5},{2,6},{3,7},{4,0},{5,1},{6,2},{7,3},{8,12},{9,13},{10,... | collective-permute-start | bytes 1769480 | tf_op jit(solution)/shard_map/ppermute | solution.py:34
  518.8 38.0 %collective-permute-start.36 = (bf16[96,3072]{1,0:T(8,128)(2,1)S(1)}, bf16[96,3072]{1,0:T(8,128)(2,1)S(1)}, u32[]{:S(2)}, u32[]{:S(2)}) collective-permute-start(bf16[96,3072]{1,0:T(8,128)(2,1)S(1)} %fusion.35), channel_id=1, source_target_pairs={{0,1},{1,0},{2,3},{3,2},{4,5},{5,4},{6,7},{7,6},{8,9},{9,8},{10,11... | collective-permute-start | bytes 1769480 | tf_op jit(solution)/shard_map/ppermute | solution.py:34
  542.0 25.1 %collective-permute-start.13 = (bf16[96,3072]{1,0:T(8,128)(2,1)S(1)}, bf16[96,3072]{1,0:T(8,128)(2,1)S(1)}, u32[]{:S(2)}, u32[]{:S(2)}) collective-permute-start(bf16[96,3072]{1,0:T(8,128)(2,1)S(1)} %fusion.33), channel_id=1, source_target_pairs={{0,4},{1,5},{2,6},{3,7},{4,0},{5,1},{6,2},{7,3},{8,12},{9,13},{10,... | collective-permute-start | bytes 1769480 | tf_op jit(solution)/shard_map/ppermute | solution.py:34
  544.1 23.2 %collective-permute-start.11 = (bf16[96,3072]{1,0:T(8,128)(2,1)S(1)}, bf16[96,3072]{1,0:T(8,128)(2,1)S(1)}, u32[]{:S(2)}, u32[]{:S(2)}) collective-permute-start(bf16[96,3072]{1,0:T(8,128)(2,1)S(1)} %fusion.31), channel_id=1, source_target_pairs={{0,1},{1,0},{2,3},{3,2},{4,5},{5,4},{6,7},{7,6},{8,9},{9,8},{10,11... | collective-permute-start | bytes 1769480 | tf_op jit(solution)/shard_map/ppermute | solution.py:34
  557.6 17.9 %collective-permute-start.41 = (bf16[24,6144]{1,0:T(8,128)(2,1)S(1)}, bf16[24,6144]{1,0:T(8,128)(2,1)S(1)}, u32[]{:S(2)}, u32[]{:S(2)}) collective-permute-start(bf16[24,6144]{1,0:T(8,128)(2,1)S(1)} %get-tuple-element.135), channel_id=1, source_target_pairs={{0,24},{1,25},{2,26},{3,27},{4,28},{5,29},{6,30},{7,31},{8,0},{9,1... | collective-permute-start | bytes 884744 | tf_op jit(solution)/shard_map/ppermute | solution.py:38
  561.0 36.4 %collective-permute-start.40 = (bf16[24,6144]{1,0:T(8,128)(2,1)S(1)}, bf16[24,6144]{1,0:T(8,128)(2,1)S(1)}, u32[]{:S(2)}, u32[]{:S(2)}) collective-permute-start(bf16[24,6144]{1,0:T(8,128)(2,1)S(1)} %get-tuple-element.136), channel_id=1, source_target_pairs={{0,16},{1,17},{2,18},{3,19},{4,20},{5,21},{6,22},{7,23},{8,24},{9,... | collective-permute-start | bytes 884744 | tf_op jit(solution)/shard_map/ppermute | solution.py:38
  567.6 33.1 %collective-permute-start.14 = (bf16[24,6144]{1,0:T(8,128)(2,1)S(1)}, bf16[24,6144]{1,0:T(8,128)(2,1)S(1)}, u32[]{:S(2)}, u32[]{:S(2)}) collective-permute-start(bf16[24,6144]{1,0:T(8,128)(2,1)S(1)} %get-tuple-element.137), channel_id=1, source_target_pairs={{0,8},{1,9},{2,10},{3,11},{4,12},{5,13},{6,14},{7,15},{8,16},{9,17... | collective-permute-start | bytes 884744 | tf_op jit(solution)/shard_map/ppermute | solution.py:38
  569.0 31.7 %collective-permute-start.16 = (bf16[24,6144]{1,0:T(8,128)(2,1)S(1)}, bf16[24,6144]{1,0:T(8,128)(2,1)S(1)}, u32[]{:S(2)}, u32[]{:S(2)}) collective-permute-start(bf16[24,6144]{1,0:T(8,128)(2,1)S(1)} %get-tuple-element.138), channel_id=1, source_target_pairs={{0,24},{1,25},{2,26},{3,27},{4,28},{5,29},{6,30},{7,31},{8,0},{9,1... | collective-permute-start | bytes 884744 | tf_op jit(solution)/shard_map/ppermute | solution.py:38
  571.9 37.7 %collective-permute-start.15 = (bf16[24,6144]{1,0:T(8,128)(2,1)S(1)}, bf16[24,6144]{1,0:T(8,128)(2,1)}, u32[]{:S(2)}, u32[]{:S(2)}) collective-permute-start(bf16[24,6144]{1,0:T(8,128)(2,1)S(1)} %get-tuple-element.139), channel_id=1, source_target_pairs={{0,16},{1,17},{2,18},{3,19},{4,20},{5,21},{6,22},{7,23},{8,24},{9,... | collective-permute-start | bytes 884744 | tf_op jit(solution)/shard_map/ppermute | solution.py:38
  (93 other events, 916.2 us)
Sparse Core Ops, SparseCore 0:
  29.6 195.9 all-gather.1

commit v3 on v2

--- a/solution.py
+++ b/solution.py
@@ -54,29 +54,57 @@
     return (a.astype(f32) + b.astype(f32)).astype(bf16)
 
 
-def scatter_rows(place, kept, got):
-    n = place.outer_size
-    half = kept[0].shape[0]
-    rows = half // (4 * n)
-
-    def view(x):
-        return x.reshape(2, 2, n * rows, x.shape[1])
-
-    ka, ga = view(kept[0]), view(got[0])
-    kb, gb = view(kept[1]), view(got[1])
-    got_a = place.swap(plus(ka[1], ga[1]), BIT_NEAR)
-    got_b = place.swap(plus(kb[:, 1], gb[:, 1]), BIT_PAIR)
-    keep_a = plus(ka[0], ga[0])
-    keep_b = plus(kb[:, 0], gb[:, 0])
-    got_a2 = place.swap(plus(keep_a[1], got_a[1]), BIT_PAIR)
-    got_b2 = place.swap(plus(keep_b[1], got_b[1]), BIT_NEAR)
-    a = plus(plus(keep_a[0], got_a[0]), got_a2)
-    b = plus(plus(keep_b[0], got_b[0]), got_b2)
-    t = jnp.concatenate((a, b), axis=1).reshape(n, rows, -1)
-    total = t[0].astype(f32)
-    for k in range(1, n):
-        total = total + place.shift(t[k], k).astype(f32)
-    return total
+class Sum:
+    def __init__(self, place, kept, send):
+        self.place, self.kept, self.send, self.stage = place, kept, send, 0
+
+    def swap(self):
+        place = self.place
+        if self.stage < 3:
+            bits = ((BIT_CORE,) * 2, (BIT_NEAR, BIT_PAIR), (BIT_PAIR, BIT_NEAR))[self.stage]
+            self.got = tuple(place.swap(x, bit) for x, bit in zip(self.send, bits))
+        else:
+            self.got = tuple(place.shift(t, k + 1) for k, t in enumerate(self.send))
+
+    def sums(self):
+        (ka, kb), (ga, gb) = self.kept, self.got
+        if self.stage == 0:
+            rows = ka.shape[0] // 4
+            ka, kb, ga, gb = (x.reshape(2, 2, rows, x.shape[1]) for x in (ka, kb, ga, gb))
+            self.send = plus(ka[1], ga[1]), plus(kb[:, 1], gb[:, 1])
+            self.kept = plus(ka[0], ga[0]), plus(kb[:, 0], gb[:, 0])
+        elif self.stage == 1:
+            self.send = plus(ka[1], ga[1]), plus(kb[1], gb[1])
+            self.kept = plus(ka[0], ga[0]), plus(kb[0], gb[0])
+        else:
+            n = self.place.outer_size
+            t = jnp.concatenate((plus(ka, ga), plus(kb, gb)), axis=1)
+            t = t.reshape(n, t.shape[0] // n, t.shape[1])
+            self.send = tuple(t[k] for k in range(1, n))
+            self.kept = (t[0],)
+        self.stage += 1
+
+    def total(self):
+        return sum([g.astype(f32) for g in self.got], self.kept[0].astype(f32))
+
+
+def tie(x, *others):
+    out = lax.optimization_barrier((x,) + others)
+    return out[0], out[1:]
+
+
+def hold(x, *groups):
+    x, kept = tie(x, *[g.kept for g in groups])
+    for g, k in zip(groups, kept):
+        g.kept = k
+    return x
+
+
+def need(x, *groups):
+    x, send = tie(x, *[g.send for g in groups])
+    for g, k in zip(groups, send):
+        g.send = k
+    return x
 
 
 def nn(a, b):
@@ -153,7 +181,7 @@
 
     @pl.when(j == 0)
     def _():
-        unit, _inv = unit_norm(x_ref[...])
+        unit, _inv = unit_norm(x_ref[...].astype(f32))
         a_ref[...] = (unit * vec_ref[row : row + 1] + vec_ref[row + 1 : row + 2]).astype(bf16)
 
     @pl.when(j < 3)
@@ -170,24 +198,25 @@
                 cols = slice(h, h + LANES)
                 p = probabilities(two_heads(qkv_ref[0, at, cols]), qkv_ref[1, at, cols], allowed)
                 o_ref[at, cols] = side_by_side(nn(p.astype(bf16), qkv_ref[2, at, cols])).astype(bf16)
-        y_ref[...] = x_ref[...] + nn(o_ref[...], w_ref[...])
+        y_ref[...] = x_ref[...].astype(f32) + nn(o_ref[...], w_ref[...])
+
+
+def emit(g, keep_ref, send_ref):
+    half = keep_ref.shape[0]
+    keep_ref[...] = g[:half].astype(bf16)
+    send_ref[...] = g[half:].astype(bf16)
 
 
 def self_backward_kernel(
     captions, row, x_ref, vec_ref, order_ref, a_ref, qkv_ref, o_ref, dx_ref, w_ref,
-    out_ref, vg_ref, keep_ref, send_ref, dqkv_ref, at_ref, acc_ref,
+    out_ref, vg_ref, keep_a_ref, keep_b_ref, send_a_ref, send_b_ref, dqkv_ref, at_ref, acc_ref,
 ):
     j = pl.program_id(0)
-    half = keep_ref.shape[0]
-
-    def emit(g):
-        keep_ref[...] = g[:half].astype(bf16)
-        send_ref[...] = g[half:].astype(bf16)
 
     @pl.when(j == 0)
     def _():
         dy = dx_ref[...].astype(bf16)
-        emit(nn(nt(order_ref[...], o_ref[...]).astype(bf16), dy))
+        emit(nn(nt(order_ref[...], o_ref[...]).astype(bf16), dy), keep_b_ref, send_b_ref)
         do = nt(dy, w_ref[...]).astype(bf16)
         length = x_ref.shape[0] // captions
         allowed = causal_mask(length)
@@ -207,13 +236,16 @@
 
     @pl.when(j > 0)
     def _():
-        d = dqkv_ref[j - 1]
-        emit(nn(at_ref[...], d))
-        acc_ref[...] += nt(d, w_ref[...])
+        acc_ref[...] += nt(dqkv_ref[j - 1], w_ref[...])
+
+    @pl.when((j == 1) | (j == 2))
+    def _():
+        emit(nn(at_ref[...], dqkv_ref[j - 1]), keep_a_ref, send_a_ref)
 
     @pl.when(j == 3)
     def _():
-        dn, gg, gs = norm_backward(acc_ref[...], x_ref[...], vec_ref[row : row + 1])
+        emit(nn(at_ref[...], dqkv_ref[2]), keep_b_ref, send_b_ref)
+        dn, gg, gs = norm_backward(acc_ref[...], x_ref[...].astype(f32), vec_ref[row : row + 1])
         out_ref[...] = dx_ref[...] + dn
         vg_ref[0:1] = gg
         vg_ref[1:2] = gs
@@ -254,17 +286,12 @@
     out_ref, vg_ref, keep_ref, send_ref, dkv_ref, dq_ref,
 ):
     j = pl.program_id(0)
-    half = keep_ref.shape[0]
     d = x_ref.shape[1]
 
-    def emit(g):
-        keep_ref[...] = g[:half].astype(bf16)
-        send_ref[...] = g[half:].astype(bf16)
-
     @pl.when(j == 0)
     def _():
         dy = dx_ref[...].astype(bf16)
-        emit(nn(nt(order_ref[...], o_ref[...]).astype(bf16), dy))
+        emit(nn(nt(order_ref[...], o_ref[...]).astype(bf16), dy), keep_ref, send_ref)
         do = nt(dy, w_ref[...]).astype(bf16)
         length = x_ref.shape[0] // captions
         patches = kv_ref.shape[0] // captions
@@ -286,7 +313,7 @@
     @pl.when(j == 1)
     def _():
         dq = dq_ref[...]
-        emit(nn(nt(order_ref[...], c_ref[...]).astype(bf16), dq))
+        emit(nn(nt(order_ref[...], c_ref[...]).astype(bf16), dq), keep_ref, send_ref)
         dn, gg, gs = norm_backward(nt(dq, w_ref[...]), x_ref[...], vec_ref[row : row + 1])
         out_ref[...] = dx_ref[...] + dn
         vg_ref[0:1] = gg
@@ -306,32 +333,32 @@
     y_ref[...] += nn(g.astype(bf16), down_ref[...])
 
 
-def feed_backward_kernel(
-    row, x_ref, vec_ref, order_ref, b_ref, u_ref, dx_ref, up_ref, down_ref,
-    out_ref, vg_ref, keep_ref, send_ref, bt_ref, acc_ref,
-):
-    j = pl.program_id(0)
-    half = keep_ref.shape[0]
-    d = x_ref.shape[1]
-
-    @pl.when(j == 0)
-    def _():
-        bt_ref[...] = nt(order_ref[...], b_ref[...]).astype(bf16)
-        acc_ref[...] = jnp.zeros_like(acc_ref)
-
-    u = u_ref[...]
+def feed_backward_step(j, order_ref, u, dz, up_ref, down_ref, refs, bt_ref, acc_ref):
+    keep_a_ref, keep_b_ref, send_a_ref, send_b_ref = refs
     t = jnp.tanh(GELU_A * (u + GELU_B * u * u * u))
     g = (0.5 * u * (1.0 + t)).astype(bf16)
     slope = 0.5 * (1.0 + t) + 0.5 * u * (1.0 - t * t) * GELU_A * (1.0 + 3.0 * GELU_B * u * u)
-    dz = dx_ref[...].astype(bf16)
     du = (slope * nt(dz, down_ref[...])).astype(bf16)
     acc_ref[...] += nt(du, up_ref[...])
-    g_up = nn(bt_ref[...], du)
-    keep_ref[:, :d] = g_up[:half].astype(bf16)
-    send_ref[:, :d] = g_up[half:].astype(bf16)
-    g_down = nn(nt(order_ref[...], g).astype(bf16), dz)
-    keep_ref[:, d:] = g_down[:half].astype(bf16)
-    send_ref[:, d:] = g_down[half:].astype(bf16)
+    emit(nn(bt_ref[...], du), keep_a_ref, send_a_ref)
+    emit(nn(nt(order_ref[...], g).astype(bf16), dz), keep_b_ref, send_b_ref)
+    return g
+
+
+def feed_backward_kernel(
+    row, x_ref, vec_ref, order_ref, b_ref, u_ref, dx_ref, up_ref, down_ref,
+    out_ref, vg_ref, keep_a_ref, keep_b_ref, send_a_ref, send_b_ref, bt_ref, acc_ref,
+):
+    j = pl.program_id(0)
+
+    @pl.when(j == 0)
+    def _():
+        bt_ref[...] = nt(order_ref[...], b_ref[...]).astype(bf16)
+        acc_ref[...] = jnp.zeros_like(acc_ref)
+
+    refs = keep_a_ref, keep_b_ref, send_a_ref, send_b_ref
+    dz = dx_ref[...].astype(bf16)
+    feed_backward_step(j, order_ref, u_ref[...], dz, up_ref, down_ref, refs, bt_ref, acc_ref)
 
     @pl.when(j == 3)
     def _():
@@ -341,12 +368,73 @@
         vg_ref[1:2] = gs
 
 
+def feed_both_kernel(
+    row, x_ref, vec_ref, order_ref, dx_ref, up_ref, down_ref,
+    y_ref, out_ref, vg_ref, keep_a_ref, keep_b_ref, send_a_ref, send_b_ref,
+    b_ref, sum_ref, bt_ref, acc_ref,
+):
+    j = pl.program_id(0)
+
+    @pl.when(j == 0)
+    def _():
+        unit, _inv = unit_norm(x_ref[...])
+        b_ref[...] = (unit * vec_ref[row : row + 1] + vec_ref[row + 1 : row + 2]).astype(bf16)
+        bt_ref[...] = nt(order_ref[...], b_ref[...]).astype(bf16)
+        acc_ref[...] = jnp.zeros_like(acc_ref)
+        sum_ref[...] = x_ref[...]
+
+    refs = keep_a_ref, keep_b_ref, send_a_ref, send_b_ref
+    u = nn(b_ref[...], up_ref[...])
+    dz = dx_ref[...]
+    g = feed_backward_step(j, order_ref, u, dz, up_ref, down_ref, refs, bt_ref, acc_ref)
+    sum_ref[...] += nn(g, down_ref[...])
+
+    @pl.when(j == 3)
+    def _():
+        y_ref[...] = sum_ref[...].astype(bf16)
+        dn, gg, gs = norm_backward(acc_ref[...], x_ref[...], vec_ref[row : row + 1])
+        out_ref[...] = dx_ref[...].astype(f32) + dn
+        vg_ref[0:1] = gg
+        vg_ref[1:2] = gs
+
+
+def pair_backward_kernel(enc_ref, dkv_ref, keep_ref, send_ref):
+    emit(nn(enc_ref[...], dkv_ref[...]), keep_ref, send_ref)
+
+
+def pack_kernel(u_qkv, u_out, u_up, u_down, m_qkv, m_out, m_up, m_down, c_q, c_pair, c_out, vec, out):
+    rows, d = u_out.shape
+    spread = spread_matrix().astype(bf16)
+    i = lax.broadcasted_iota(jnp.int32, (rows, 4 * rows), 0)
+    k = lax.broadcasted_iota(jnp.int32, (rows, 4 * rows), 1)
+
+    def layer(at, qkv, w_out, up, down):
+        out[:, at : at + 3 * d] = qkv[...]
+        out[:, at + 3 * d : at + 4 * d] = w_out[...]
+        for b in range(4 * d // 512):
+            y = nn(up[:, b * 512 : (b + 1) * 512], spread).astype(bf16)
+            for j in range(4):
+                to = at + (4 + j) * d + b * LANES
+                out[:, to : to + LANES] = y[:, j * LANES : (j + 1) * LANES]
+        for j in range(4):
+            y = nn((k == 4 * i + j).astype(bf16), down[...])
+            out[:, at + (8 + j) * d : at + (9 + j) * d] = y.astype(bf16)
+
+    layer(0, u_qkv, u_out, u_up, u_down)
+    layer(12 * d, m_qkv, m_out, m_up, m_down)
+    out[:, 24 * d : 25 * d] = c_q[...]
+    out[:, 25 * d : 27 * d] = c_pair[...]
+    out[:, 27 * d : 28 * d] = c_out[...]
+    eye = lax.broadcasted_iota(jnp.int32, (rows, rows), 0) == lax.broadcasted_iota(jnp.int32, (rows, rows), 1)
+    out[:, 28 * d :] = nt(eye.astype(bf16), vec[...]).astype(bf16)
+
+
 def whole(x):
     return pl.BlockSpec(x.shape, lambda *_: (0,) * len(x.shape))
 
 
 def call(kernel, steps, ins, in_specs, outs, out_specs, scratch=(), scalars=0, flops=0):
-    size = sum(x.size * x.dtype.itemsize for x in outs)
+    size = sum(x.size * x.dtype.itemsize for x in jax.tree.leaves(outs))
     return pl.pallas_call(
         kernel,
         out_shape=outs,
@@ -386,14 +474,15 @@
     def self_backward(self, x, kept, dx, at, row):
         d, t = self.d, self.t
         a, qkv, o = kept
-        outs = (self.xs, sds((8, d), f32), sds((d // 2, 4 * d), bf16), sds((d // 2, 4 * d), bf16))
-        grad = pl.BlockSpec((d // 2, d), lambda j: (0, (j + 3) % 4))
+        outs = (self.xs, sds((8, d), f32)) + (sds((d // 2, 2 * d), bf16),) * 4
+        grad_a = pl.BlockSpec((d // 2, d), lambda j: (0, j // 2))
+        grad_b = pl.BlockSpec((d // 2, d), lambda j: (0, 1 - jnp.minimum(j, 1)))
         ins = (x, self.vec, self.order, a, qkv, o, dx)
         return call(
             functools.partial(self_backward_kernel, self.captions, row), 4,
             ins + (self.w,),
             [whole(i) for i in ins] + [self.weight(lambda j: at + (j + 3) % 4)],
-            outs, [whole(outs[0]), whole(outs[1]), grad, grad],
+            outs, [whole(outs[0]), whole(outs[1]), grad_a, grad_b, grad_a, grad_b],
             scratch=[pltpu.VMEM((3, t, d), bf16), pltpu.VMEM((d, t), bf16), pltpu.VMEM((t, d), f32)],
             flops=20 * t * d * d,
         )
@@ -410,10 +499,8 @@
     def cross_backward(self, x, kept, kv, dx, at, row):
         d, t = self.d, self.t
         c, q, o = kept
-        outs = (
-            self.xs, sds((8, d), f32), sds((d // 2, 2 * d), bf16), sds((d // 2, 2 * d), bf16),
-            sds(kv.shape, bf16),
-        )
+        outs = (self.xs, sds((8, d), f32)) + (sds((d // 2, 2 * d), bf16),) * 2
+        outs = outs + (sds(kv.shape, bf16),)
         grad = pl.BlockSpec((d // 2, d), lambda j, *_: (0, 1 - j))
         ins = (x, self.vec, self.order, c, q, o, kv, dx)
         return call(
@@ -424,6 +511,16 @@
             scratch=[pltpu.VMEM((t, d), bf16)], scalars=1, flops=30 * t * d * d,
         )
 
+    def pair_backward(self, enc_t, dkv):
+        d = self.d
+        outs = (sds((d // 2, 2 * d), bf16),) * 2
+        grad = pl.BlockSpec((d // 2, d), lambda j: (0, j))
+        return call(
+            pair_backward_kernel, 2, (enc_t, dkv),
+            [whole(enc_t), pl.BlockSpec((dkv.shape[0], d), lambda j: (0, j))],
+            outs, [grad, grad], flops=4 * enc_t.shape[1] * d * d,
+        )
+
     def feed_forward(self, x, at, row):
         d, t = self.d, self.t
         outs = (self.xs, self.hs, sds((t, 4 * d), f32))
@@ -438,8 +535,8 @@
     def feed_backward(self, x, kept, dx, at, row):
         d, t = self.d, self.t
         b, u = kept
-        outs = (self.xs, sds((8, d), f32), sds((d // 2, 8 * d), bf16), sds((d // 2, 8 * d), bf16))
-        grad = pl.BlockSpec((d // 2, 2 * d), lambda j: (0, j))
+        outs = (self.xs, sds((8, d), f32)) + (sds((d // 2, 4 * d), bf16),) * 4
+        grad = pl.BlockSpec((d // 2, d), lambda j: (0, j))
         return call(
             functools.partial(feed_backward_kernel, row), 4,
             (x, self.vec, self.order, b, u, dx, self.w, self.w),
@@ -448,9 +545,26 @@
                 pl.BlockSpec((t, d), lambda j: (0, j)), whole(dx),
                 self.weight(lambda j: at + j), self.weight(lambda j: at + 4 + j),
             ],
-            outs, [whole(outs[0]), whole(outs[1]), grad, grad],
+            outs, [whole(outs[0]), whole(outs[1])] + [grad] * 4,
             scratch=[pltpu.VMEM((d, t), bf16), pltpu.VMEM((t, d), f32)],
             flops=44 * t * d * d,
+        )
+
+    def feed_both(self, x, dx, at, row):
+        d, t = self.d, self.t
+        outs = (self.hs, self.xs, sds((8, d), f32)) + (sds((d // 2, 4 * d), bf16),) * 4
+        grad = pl.BlockSpec((d // 2, d), lambda j: (0, j))
+        ins = (x, self.vec, self.order, dx)
+        return call(
+            functools.partial(feed_both_kernel, row), 4,
+            ins + (self.w, self.w),
+            [whole(i) for i in ins] + [self.weight(lambda j: at + j), self.weight(lambda j: at + 4 + j)],
+            outs, [whole(o) for o in outs[:3]] + [grad] * 4,
+            scratch=[
+                pltpu.VMEM((t, d), bf16), pltpu.VMEM((t, d), f32),
+                pltpu.VMEM((d, t), bf16), pltpu.VMEM((t, d), f32),
+            ],
+            flops=60 * t * d * d,
         )
 
 
@@ -458,12 +572,6 @@
     k = lax.broadcasted_iota(jnp.int32, (512, 512), 0)
     n = lax.broadcasted_iota(jnp.int32, (512, 512), 1)
     return (k % 4) * 128 + k // 4 == n
-
-
-def spread(up):
-    rows, wide = up.shape
-    y = nn(up.reshape(rows * (wide // 512), 512), spread_matrix().astype(bf16)).astype(bf16)
-    return y.reshape(rows, wide // 512, 4, 128).transpose(0, 2, 1, 3).reshape(rows, wide)
 
 
 def unspread(up):
@@ -484,22 +592,17 @@
     place = Place()
     captions, length, d = tokens.shape
     rows = u_qkv.shape[0]
-    x0 = tokens.reshape(-1, d).astype(f32)
+    x0 = tokens.reshape(-1, d)
     enc = encoder.reshape(-1, d)
     order = place.order(d)
 
     vectors = (u_ag, u_as, u_mg, u_ms, m_ag, m_as, c_g, c_s, m_mg, m_ms)
-    cols = jnp.pad(jnp.stack(vectors, axis=1), ((0, 0), (0, LANES - len(vectors))))
-    shard = jnp.concatenate(
-        (
-            u_qkv, u_out, spread(u_up), u_down.reshape(rows, -1),
-            m_qkv, m_out, spread(m_up), m_down.reshape(rows, -1),
-            c_q, c_pair, c_out, cols,
-        ),
-        axis=1,
-    )
+    vectors = jnp.pad(jnp.stack(vectors, axis=0), ((0, LANES - len(vectors)), (0, 0)))
+    parts = (u_qkv, u_out, u_up, u_down, m_qkv, m_out, m_up, m_down, c_q, c_pair, c_out, vectors)
+    packed = sds((rows, 28 * d + LANES), bf16)
+    shard = call(pack_kernel, 1, parts, [whole(p) for p in parts], packed, whole(packed))
     w = lax.all_gather(shard, AXES, axis=0, tiled=True)
-    vec = w[:, 28 * d : 28 * d + 16].astype(f32).T
+    vec = nt(jnp.eye(16, LANES, dtype=bf16), w[:, 28 * d :])
     enc_t = nt(order, enc).astype(bf16)
 
     net = Layers(captions, captions * length, d, w, vec, order, patch_count)
@@ -510,51 +613,66 @@
     x1, *k_uf = net.feed_forward(x0a, 4, 2)
     x1a, *k_ms = net.self_forward(x1, 12, 4)
     x1b, *k_mc = net.cross_forward(x1a, kv, 24, 6)
-    x2, *k_mf = net.feed_forward(x1b, 16, 8)
-
-    def core(x):
-        return place.swap(x, BIT_CORE)
-
-    def halves(x):
-        at = x.shape[1] // 2
-        return x[:, :at], x[:, at:]
-
-    dx = out_grad.reshape(-1, d).astype(f32)
-    dx, v_mf, keep, send = net.feed_backward(x1b, k_mf, dx, 16, 8)
-    r_mf = scatter_rows(place, halves(keep), halves(core(send)))
+
+    x2, dx, v_mf, *g = net.feed_both(x1b, out_grad.reshape(-1, d), 16, 8)
+    s_mf = Sum(place, g[:2], g[2:])
+    s_mf.swap()
     dx, v_mc, keep, send, dkv = net.cross_backward(x1a, k_mc, kv, dx, 24, 6)
-    g_pair = nn(enc_t, dkv).astype(bf16)
-    denc = nt(dkv, w_pair).astype(bf16)
-    r_mc = scatter_rows(
-        place, (keep, g_pair[: d // 2]), (core(send), core(g_pair[d // 2 :]))
-    )
-    dx, v_ms, keep, send = net.self_backward(x1, k_ms, dx, 12, 4)
-    r_ms = scatter_rows(place, halves(keep), halves(core(send)))
-    dx, v_uf, keep, send = net.feed_backward(x0a, k_uf, dx, 4, 2)
-    r_uf = scatter_rows(place, halves(keep), halves(core(send)))
-    dx, v_us, keep, send = net.self_backward(x0, k_us, dx, 0, 0)
+    keep_p, send_p = net.pair_backward(enc_t, dkv)
+    s_mc = Sum(place, (keep, keep_p), (send, send_p))
+    dx = hold(dx, s_mf)
+    s_mf.sums()
+    dx = need(dx, s_mf, s_mc)
+    s_mf.swap()
+    s_mc.swap()
+    dx, v_ms, *g = net.self_backward(x1, k_ms, dx, 12, 4)
+    s_ms = Sum(place, g[:2], g[2:])
+    dx = hold(dx, s_mc)
+    s_mc.sums()
+    dx = need(dx, s_mc, s_ms)
+    s_mc.swap()
+    s_ms.swap()
+    dx, v_uf, *g = net.feed_backward(x0a, k_uf, dx, 4, 2)
+    s_uf = Sum(place, g[:2], g[2:])
+    dx = hold(dx, s_mf, s_ms)
+    s_mf.sums()
+    s_ms.sums()
+    dx = need(dx, s_mf, s_ms, s_uf)
+    s_mf.swap()
+    s_ms.swap()
+    s_uf.swap()
+    dx, v_us, *g = net.self_backward(x0, k_us, dx, 0, 0)
     v = jnp.concatenate([g[:2] for g in (v_us, v_uf, v_ms, v_mc, v_mf)], axis=0).astype(bf16)
     v = nt(order, jnp.pad(v, ((0, LANES - v.shape[0]), (0, 0)))).astype(bf16)
-    got = core(send)
-    got_v = core(v[d // 2 :])
-    at = 2 * d
-    r_us = scatter_rows(
-        place,
-        (keep[:, :at], jnp.concatenate((keep[:, at:], v[: d // 2]), axis=1)),
-        (got[:, :at], jnp.concatenate((got[:, at:], got_v), axis=1)),
-    )
+    s_us = Sum(place, g[:2], g[2:])
+    s_us.kept = s_us.kept[0], jnp.concatenate((s_us.kept[1], v[: d // 2]), axis=1)
+    dx = hold(dx, s_uf, s_mc)
+    s_uf.sums()
+    s_mc.sums()
+    dx = need(dx, s_uf, s_mc, s_us)
+    s_us.send = s_us.send[0], jnp.concatenate((s_us.send[1], v[d // 2 :]), axis=1)
+    s_us.swap()
+    s_uf.swap()
+    s_mc.swap()
+    dx, (dkv,) = tie(dx, dkv)
+    denc = nt(dkv, w_pair).astype(bf16)
+    dx, (denc,) = tie(dx, denc)
+    for group in (s_us, s_mf, s_ms, s_uf, s_mc, s_us, s_ms, s_uf, s_us):
+        dx = hold(dx, group)
+        group.sums()
+        dx = need(dx, group)
+        group.swap()
+    r_mf, r_mc, r_ms, r_uf, r_us = (x.total() for x in (s_mf, s_mc, s_ms, s_uf, s_us))
 
     def feed_rows(r):
-        up = jnp.concatenate([r[:, (2 * j) * d : (2 * j + 1) * d] for j in range(4)], axis=1)
-        down = jnp.concatenate([r[:, (2 * j + 1) * d : (2 * j + 2) * d] for j in range(4)], axis=1)
-        return unspread(up), down.reshape(-1, d)
+        return unspread(r[:, : 4 * d]), r[:, 4 * d :].reshape(-1, d)
 
     r_uup, r_udown = feed_rows(r_uf)
     r_mup, r_mdown = feed_rows(r_mf)
     vs = r_us[:, 4 * d :]
     v = [vs[:, i] for i in range(10)]
     return (
-        x2.astype(bf16).reshape(tokens.shape),
+        x2.reshape(tokens.shape),
         dx.astype(bf16).reshape(tokens.shape),
         denc.reshape(encoder.shape),
         v[0], v[1], r_us[:, : 3 * d], r_us[:, 3 * d : 4 * d], v[2], v[3], r_uup, r_udown,

time: 625 us -> 554 us (0.89)
  waiting for transfers between devices: 359 us -> 294 us
  local copies, waits for them, and re-layouts: 60.9 us -> 30 us
  other arithmetic: 20.5 us -> 44.8 us
  matrix products: 23.6 us -> 16.5 us
    ppermute x27 -> x30, waiting for transfers between devices: 108 us -> 41.5 us  [swap(): return lax.ppermute(x, AXES, [(i, i ^ bit) for i in range(self.count)])]
    convert_element_type x30, other arithmetic: 13.3 us -> 42.2 us  [plus(): return (a.astype(f32) + b.astype(f32)).astype(bf16)]
    slice x12 -> x3, local copies, waits for them, and re-layouts: 12.7 us -> 0.1 us  [the longest x2 0.08 us: feed_rows(): return (unspread(r[:, :4 * d]), r[:, 4 * d:].reshape(-1, d))]
    another operation x11 -> x1, local copies, waits for them, and re-layouts: 13.8 us -> 1.61 us  [local(): jnp.stack(vectors, axis=0)]
    dot_general x4 -> x1, matrix products: 14.4 us -> 5.11 us  [nn(): return jnp.dot(a, b, preferred_element_type=f32)]
    unnamed x159 -> x146, local copies, waits for them, and re-layouts: 22.7 us -> 18.8 us
    ppermute x27 -> x30, starting transfers between devices: 22.9 us -> 21.7 us  [swap(): return lax.ppermute(x, AXES, [(i, i ^ bit) for i in range(self.count)])]
    pallas_call x10 -> x11, Pallas kernels: 96.9 us -> 96.8 us  [call(): pl.pallas_call(kernel, out_shape=outs, grid_spec=pltpu.PrefetchScalarGrid...]
  transfers between devices with their start and end apart: 43 -> 46, of which waited for: 25 -> 18; matrix products, arithmetic and copies ran while one was open for 9% -> 10% of each run, Pallas kernels for 7% -> 10%
where the time goes in v3:
time: 554 us; the launch traced here: 544 us
  waiting for transfers between devices  294 us (53%)
  Pallas kernels  96.8 us (17%)
  starting transfers between devices  46.1 us (8%)
  other arithmetic  44.8 us (8%)
  local copies, waits for them, and re-layouts  30 us (5%)
  matrix products  16.5 us (3%)
  between operations  15.6 us (3%)
    all_gather x1, waiting for transfers between devices, local(): w = lax.all_gather(shard, AXES, axis=0, tiled=True)  196 us
    pallas_call x11, Pallas kernels, call(): pl.pallas_call(kernel, out_shape=outs, grid_spec=pltpu.PrefetchScalarGrid...  96.8 us
    ppermute x15, waiting for transfers between devices, shift(): return lax.ppermute(x, AXES, [(i, (i + 8 * k) % n) for i in range(n)])  57.1 us
    convert_element_type x30, other arithmetic, plus(): return (a.astype(f32) + b.astype(f32)).astype(bf16)  42.2 us
    ppermute x30, waiting for transfers between devices, swap(): return lax.ppermute(x, AXES, [(i, i ^ bit) for i in range(self.count)])  41.5 us
    ppermute x15, starting transfers between devices, shift(): return lax.ppermute(x, AXES, [(i, (i + 8 * k) % n) for i in range(n)])  24.4 us
    ppermute x30, starting transfers between devices, swap(): return lax.ppermute(x, AXES, [(i, i ^ bit) for i in range(self.count)])  21.7 us
    unnamed x146, local copies, waits for them, and re-layouts  18.8 us
  transfers between devices with their start and end apart: 46, of which 18 were waited for; matrix products, arithmetic and copies ran while one was open for 10% of the time, Pallas kernels for 10%

profile of v3, /device:TPU:0, one launch (start us, length us, event | category | flops | bytes accessed | tf_op | source)
XLA Modules:
  0.0 544.2 jit_solution(14427362004173043491)
XLA Ops:
  21.0 195.8 %all-gather.2.cloned.1.call-done.w_ref.up_ref.down_ref = bf16[768,21632]{1,0:T(8,128)(2,1)} async-done(((bf16[24,21632]{1,0:T(8,128)(2,1)}), bf16[768,21632]{1,0:T(8,128)(2,1)}) %all-gather.2.cloned.1.call-update) | async-done | bytes 33226768 | tf_op jit(solution)/shard_map/all_gather | solution.py:604
  217.9 4.9 shard_map.425
  224.3 5.8 %shard_map.426 = (f32[128,768]{1,0:T(8,128)S(1)}, bf16[128,768]{1,0:T(8,128)(2,1)S(1)}, f32[128,3072]{1,0:T(8,128)S(1)}) custom-call(f32[128,768]{1,0:T(8,128)S(1)} %get-tuple-element.174.x_ref, f32[16,768]{1,0:T(8,128)S(1)} %fusion.50.vec_ref, bf16[768,21632]{1,0:T(8,128)(2,1)} %all-gather.2.cloned.1.call-done.w_ref.up_ref.down_ref, ...), custom_call_target="tpu_custom_call" | custom-call | flops 1207959552 | bytes 4325376 | tf_op jit(solution)/shard_map/pallas_call | solution.py:438
  230.1 5.5 %shard_map.427 = (f32[128,768]{1,0:T(8,128)S(1)}, bf16[128,768]{1,0:T(8,128)(2,1)S(1)}, bf16[3,128,768]{2,1,0:T(8,128)(2,1)S(1)}, bf16[128,768]{1,0:T(8,128)(2,1)S(1)}) custom-call(f32[128,768]{1,0:T(8,128)S(1)} %get-tuple-element.175.x_ref, f32[16,768]{1,0:T(8,128)S(1)} %fusion.50.vec_ref, bf16[768,21632]{1,0:T(8,128)(2,1)} %all-gather.2.cloned.1.call-done.w_ref.up_ref.down_ref), custom_call_target="tpu_custom_call" | custom-call | flops 603979776 | bytes 2752512 | tf_op jit(solution)/shard_map/pallas_call | solution.py:438
  235.7 5.1 fusion.kv_ref
  240.9 7.5 %shard_map.428 = (f32[128,768]{1,0:T(8,128)S(1)}, bf16[128,768]{1,0:T(8,128)(2,1)S(1)}, bf16[128,768]{1,0:T(8,128)(2,1)S(1)}, bf16[128,768]{1,0:T(8,128)(2,1)S(1)}) custom-call(s32[2]{0:T(128)S(1)} %copy-done.43, f32[128,768]{1,0:T(8,128)S(1)} %get-tuple-element.176.x_ref, f32[16,768]{1,0:T(8,128)S(1)} %fusion.50.vec_ref, ...), custom_call_target="tpu_custom_call" | custom-call | flops 754974720 | bytes 1966080 | tf_op jit(solution)/shard_map/pallas_call | solution.py:438
  248.4 14.6 %shard_map.429 = (bf16[128,768]{1,0:T(8,128)(2,1)}, f32[128,768]{1,0:T(8,128)S(1)}, f32[8,768]{1,0:T(8,128)S(1)}, bf16[384,3072]{1,0:T(8,128)(2,1)S(1)}, bf16[38...) custom-call(f32[128,768]{1,0:T(8,128)S(1)} %get-tuple-element.177.x_ref, ...), custom_call_target="tpu_custom_call" | custom-call | flops 4529848320 | bytes 20103168 | tf_op jit(solution)/shard_map/pallas_call | solution.py:438
  265.5 13.5 %shard_map.430 = (f32[128,768]{1,0:T(8,128)S(1)}, f32[8,768]{1,0:T(8,128)S(1)}, bf16[384,1536]{1,0:T(8,128)(2,1)S(1)}, bf16[384,1536]{1,0:T(8,128)(2,1)}, bf16[1152,1536]{1,0:T(8,128)(2,1)S(1)}) custom-call(s32[2]{0:T(128)S(1)} %copy-done.43, f32[128,768]{1,0:T(8,128)S(1)} %get-tuple-element.176.x_ref, f32[16,768]{1,0:T(8,128)S(1)} %fusion.50.vec_ref, ...), custom_call_target="tpu_custom_call" | custom-call | flops 2264924160 | bytes 12632064 | tf_op jit(solution)/shard_map/pallas_call | solution.py:438
  279.9 4.0 shard_map.431
  291.0 12.4 %shard_map.432 = (f32[128,768]{1,0:T(8,128)S(1)}, f32[8,768]{1,0:T(8,128)S(1)}, bf16[384,1536]{1,0:T(8,128)(2,1)S(1)}, bf16[384,1536]{1,0:T(8,128)(2,1)S(1)}, bf...) custom-call(f32[128,768]{1,0:T(8,128)S(1)} %get-tuple-element.175.x_ref, f32[16,768]{1,0:T(8,128)S(1)} %fusion.50.vec_ref, ...), custom_call_target="tpu_custom_call" | custom-call | flops 1509949440 | bytes 10272768 | tf_op jit(solution)/shard_map/pallas_call | solution.py:438
  306.6 13.8 %shard_map.433 = (f32[128,768]{1,0:T(8,128)S(1)}, f32[8,768]{1,0:T(8,128)S(1)}, bf16[384,3072]{1,0:T(8,128)(2,1)S(1)}, bf16[384,3072]{1,0:T(8,128)(2,1)S(1)}, bf...) custom-call(f32[128,768]{1,0:T(8,128)S(1)} %get-tuple-element.174.x_ref, f32[16,768]{1,0:T(8,128)S(1)} %fusion.50.vec_ref, ...), custom_call_target="tpu_custom_call" | custom-call | flops 3321888768 | bytes 19709952 | tf_op jit(solution)/shard_map/pallas_call | solution.py:438
  337.7 12.6 %shard_map.434 = (f32[128,768]{1,0:T(8,128)S(1)}, f32[8,768]{1,0:T(8,128)S(1)}, bf16[384,1536]{1,0:T(8,128)(2,1)S(1)}, bf16[384,1536]{1,0:T(8,128)(2,1)S(1)}, bf...) custom-call(bf16[128,768]{1,0:T(8,128)(2,1)S(1)} %bitcast.200, f32[16,768]{1,0:T(8,128)S(1)} %fusion.50.vec_ref, ...), custom_call_target="tpu_custom_call" | custom-call | flops 1509949440 | bytes 10272768 | tf_op jit(solution)/shard_map/pallas_call | solution.py:438
  366.6 5.8 %convolution_convert_fusion.1 = bf16[1152,768]{1,0:T(8,128)(2,1)} fusion(bf16[1152,1536]{1,0:T(8,128)(2,1)S(1)} %copy-done.46, bf16[768,21632]{1,0:T(8,128)(2,1)} %all-gather.2.cloned.1.call-done.w_ref.up_ref.down_ref), kind=kOutput, calls=%fused_computation.2 | convolution fusion | flops 2718793728 | bytes 7667712 | tf_op jit(solution)/shard_map/dot_general | solution.py:115
  384.5 4.0 collective-permute-done.17
  389.5 24.7 %collective-permute-done.18 = bf16[2,96,3072]{2,1,0:T(8,128)(2,1)S(1)} collective-permute-done((bf16[2,96,3072]{2,1,0:T(8,128)(2,1)S(1)}, bf16[2,96,3072]{2,1,0:T(8,128)(2,1)S(1)}, u32[]{:S(2)}, u32[]{:S(2)}) %collective-permute-start.18) | collective-permute-done | bytes 1179680 | tf_op jit(solution)/shard_map/ppermute | solution.py:34
  415.5 4.2 collective-permute-done.19
  429.9 3.8 collective-permute-start.42
  436.2 6.2 %collective-permute-start.44 = (bf16[24,6144]{1,0:T(8,128)(2,1)S(1)}, bf16[24,6144]{1,0:T(8,128)(2,1)S(1)}, u32[]{:S(2)}, u32[]{:S(2)}) collective-permute-start(bf16[24,6144]{1,0:T(8,128)(2,1)S(1)} %get-tuple-element.323), channel_id=1, source_target_pairs={{0,24},{1,25},{2,26},{3,27},{4,28},{5,29},{6,30},{7,31},{8,0},{9,1... | collective-permute-start | bytes 884744 | tf_op jit(solution)/shard_map/ppermute | solution.py:38
  444.3 12.8 %collective-permute-done.43 = bf16[24,6144]{1,0:T(8,128)(2,1)S(1)} collective-permute-done((bf16[24,6144]{1,0:T(8,128)(2,1)S(1)}, bf16[24,6144]{1,0:T(8,128)(2,1)S(1)}, u32[]{:S(2)}, u32[]{:S(2)}) %collective-permute-start.43) | collective-permute-done | bytes 294944 | tf_op jit(solution)/shard_map/ppermute | solution.py:38
  457.7 4.7 collective-permute-done.44
  489.0 4.2 collective-permute-done.38
  498.2 12.0 %collective-permute-done.34 = bf16[24,6144]{1,0:T(8,128)(2,1)S(1)} collective-permute-done((bf16[24,6144]{1,0:T(8,128)(2,1)S(1)}, bf16[24,6144]{1,0:T(8,128)(2,1)S(1)}, u32[]{:S(2)}, u32[]{:S(2)}) %collective-permute-start.34) | collective-permute-done | bytes 294944 | tf_op jit(solution)/shard_map/ppermute | solution.py:38
  510.2 6.0 %collective-permute-done.35 = bf16[24,6144]{1,0:T(8,128)(2,1)S(1)} collective-permute-done((bf16[24,6144]{1,0:T(8,128)(2,1)S(1)}, bf16[24,6144]{1,0:T(8,128)(2,1)S(1)}, u32[]{:S(2)}, u32[]{:S(2)}) %collective-permute-start.35) | collective-permute-done | bytes 294944 | tf_op jit(solution)/shard_map/ppermute | solution.py:38
  529.0 5.7 %collective-permute-done.31 = bf16[24,3200]{1,0:T(8,128)(2,1)S(1)} collective-permute-done((bf16[24,3200]{1,0:T(8,128)(2,1)S(1)}, bf16[24,3200]{1,0:T(8,128)(2,1)S(1)}, u32[]{:S(2)}, u32[]{:S(2)}) %collective-permute-start.31) | collective-permute-done | bytes 153632 | tf_op jit(solution)/shard_map/ppermute | solution.py:38
  (307 shorter events, 139.0 us)
Async XLA Ops:
  7.2 209.6 %all-gather.2.cloned.1.call-start = ((), (), s32[]{:S(2)}) async-start(), calls=%async_computation | async-start | bytes 34265088 | tf_op jit(solution)/shard_map/all_gather | solution.py:604
  263.4 21.5 %collective-permute-start = (bf16[384,3072]{1,0:T(8,128)(2,1)}, bf16[384,3072]{1,0:T(8,128)(2,1)}, u32[]{:S(2)}, u32[]{:S(2)}) collective-permute-start(bf16[384,3072]{1,0:T(8,128)(2,1)} %get-tuple-element.196), channel_id=1, source_target_pairs={{0,2},{1,3},{2,0},{3,1},{4,6},{5,7},{6,4},{7,5},{8,10},{9,11},{10,... | collective-permute-start | bytes 7077896 | tf_op jit(solution)/shard_map/ppermute | solution.py:34
  289.0 32.9 %collective-permute-start.4 = (bf16[2,96,3072]{2,1,0:T(8,128)(2,1)}, bf16[2,96,3072]{2,1,0:T(8,128)(2,1)}, u32[]{:S(2)}, u32[]{:S(2)}) collective-permute-start(bf16[2,96,3072]{2,1,0:T(8,128)(2,1)} %bitcast.15), channel_id=1, source_target_pairs={{0,4},{1,5},{2,6},{3,7},{4,0},{5,1},{6,2},{7,3},{8,12},{9,13},{10,... | collective-permute-start | bytes 3538952 | tf_op jit(solution)/shard_map/ppermute | solution.py:34
  290.4 35.0 %collective-permute-start.5 = (bf16[2,96,3072]{2,1,0:T(8,128)(2,1)S(1)}, bf16[2,96,3072]{2,1,0:T(8,128)(2,1)}, u32[]{:S(2)}, u32[]{:S(2)}) collective-permute-start(bf16[2,96,3072]{2,1,0:T(8,128)(2,1)S(1)} %get-tuple-element.221), channel_id=1, source_target_pairs={{0,1},{1,0},{2,3},{3,2},{4,5},{5,4},{6,7},{7,6},{8,9},{9,8},{10,11... | collective-permute-start | bytes 3538952 | tf_op jit(solution)/shard_map/ppermute | solution.py:34
  306.1 24.6 %collective-permute-start.6 = (bf16[384,1536]{1,0:T(8,128)(2,1)S(1)}, bf16[384,1536]{1,0:T(8,128)(2,1)}, u32[]{:S(2)}, u32[]{:S(2)}) collective-permute-start(bf16[384,1536]{1,0:T(8,128)(2,1)S(1)} %get-tuple-element.223), channel_id=1, source_target_pairs={{0,2},{1,3},{2,0},{3,1},{4,6},{5,7},{6,4},{7,5},{8,10},{9,11},{10,... | collective-permute-start | bytes 3538952 | tf_op jit(solution)/shard_map/ppermute | solution.py:34
  306.1 22.0 %collective-permute-start.7 = (bf16[384,1536]{1,0:T(8,128)(2,1)S(1)}, bf16[384,1536]{1,0:T(8,128)(2,1)}, u32[]{:S(2)}, u32[]{:S(2)}) collective-permute-start(bf16[384,1536]{1,0:T(8,128)(2,1)S(1)} %get-tuple-element.225), channel_id=1, source_target_pairs={{0,2},{1,3},{2,0},{3,1},{4,6},{5,7},{6,4},{7,5},{8,10},{9,11},{10,... | collective-permute-start | bytes 3538952 | tf_op jit(solution)/shard_map/ppermute | solution.py:34
  333.3 25.4 %collective-permute-start.9 = (bf16[384,3072]{1,0:T(8,128)(2,1)}, bf16[384,3072]{1,0:T(8,128)(2,1)}, u32[]{:S(2)}, u32[]{:S(2)}) collective-permute-start(bf16[384,3072]{1,0:T(8,128)(2,1)} %get-tuple-element.236), channel_id=1, source_target_pairs={{0,2},{1,3},{2,0},{3,1},{4,6},{5,7},{6,4},{7,5},{8,10},{9,11},{10,... | collective-permute-start | bytes 7077896 | tf_op jit(solution)/shard_map/ppermute | solution.py:34
  336.2 41.3 %collective-permute-start.14 = (bf16[96,3072]{1,0:T(8,128)(2,1)}, bf16[96,3072]{1,0:T(8,128)(2,1)}, u32[]{:S(2)}, u32[]{:S(2)}) collective-permute-start(bf16[96,3072]{1,0:T(8,128)(2,1)} %get-tuple-element.262), channel_id=1, source_target_pairs={{0,1},{1,0},{2,3},{3,2},{4,5},{5,4},{6,7},{7,6},{8,9},{9,8},{10,11... | collective-permute-start | bytes 1769480 | tf_op jit(solution)/shard_map/ppermute | solution.py:34
  337.6 23.8 %collective-permute-start.8 = (bf16[384,3072]{1,0:T(8,128)(2,1)}, bf16[384,3072]{1,0:T(8,128)(2,1)}, u32[]{:S(2)}, u32[]{:S(2)}) collective-permute-start(bf16[384,3072]{1,0:T(8,128)(2,1)} %get-tuple-element.234), channel_id=1, source_target_pairs={{0,2},{1,3},{2,0},{3,1},{4,6},{5,7},{6,4},{7,5},{8,10},{9,11},{10,... | collective-permute-start | bytes 7077896 | tf_op jit(solution)/shard_map/ppermute | solution.py:34
  354.0 22.6 %collective-permute-start.15 = (bf16[96,3072]{1,0:T(8,128)(2,1)}, bf16[96,3072]{1,0:T(8,128)(2,1)S(1)}, u32[]{:S(2)}, u32[]{:S(2)}) collective-permute-start(bf16[96,3072]{1,0:T(8,128)(2,1)} %get-tuple-element.264), channel_id=1, source_target_pairs={{0,4},{1,5},{2,6},{3,7},{4,0},{5,1},{6,2},{7,3},{8,12},{9,13},{10,... | collective-permute-start | bytes 1769480 | tf_op jit(solution)/shard_map/ppermute | solution.py:34
  356.0 27.0 %collective-permute-start.16 = (bf16[2,96,1536]{2,1,0:T(8,128)(2,1)S(1)}, bf16[2,96,1536]{2,1,0:T(8,128)(2,1)S(1)}, u32[]{:S(2)}, u32[]{:S(2)}) collective-permute-start(bf16[2,96,1536]{2,1,0:T(8,128)(2,1)S(1)} %bitcast.214), channel_id=1, source_target_pairs={{0,4},{1,5},{2,6},{3,7},{4,0},{5,1},{6,2},{7,3},{8,12},{9,13},{10,... | collective-permute-start | bytes 1769480 | tf_op jit(solution)/shard_map/ppermute | solution.py:34
  374.1 47.0 %collective-permute-start.20 = (bf16[96,1536]{1,0:T(8,128)(2,1)S(1)}, bf16[96,1536]{1,0:T(8,128)(2,1)S(1)}, u32[]{:S(2)}, u32[]{:S(2)}) collective-permute-start(bf16[96,1536]{1,0:T(8,128)(2,1)S(1)} %get-tuple-element.280), channel_id=1, source_target_pairs={{0,1},{1,0},{2,3},{3,2},{4,5},{5,4},{6,7},{7,6},{8,9},{9,8},{10,11... | collective-permute-start | bytes 884744 | tf_op jit(solution)/shard_map/ppermute | solution.py:34
  376.6 44.3 %collective-permute-start.21 = (bf16[96,1536]{1,0:T(8,128)(2,1)S(1)}, bf16[96,1536]{1,0:T(8,128)(2,1)S(1)}, u32[]{:S(2)}, u32[]{:S(2)}) collective-permute-start(bf16[96,1536]{1,0:T(8,128)(2,1)S(1)} %get-tuple-element.282), channel_id=1, source_target_pairs={{0,4},{1,5},{2,6},{3,7},{4,0},{5,1},{6,2},{7,3},{8,12},{9,13},{10,... | collective-permute-start | bytes 884744 | tf_op jit(solution)/shard_map/ppermute | solution.py:34
  377.4 36.8 %collective-permute-start.18 = (bf16[2,96,3072]{2,1,0:T(8,128)(2,1)S(1)}, bf16[2,96,3072]{2,1,0:T(8,128)(2,1)S(1)}, u32[]{:S(2)}, u32[]{:S(2)}) collective-permute-start(bf16[2,96,3072]{2,1,0:T(8,128)(2,1)S(1)} %bitcast.212), channel_id=1, source_target_pairs={{0,4},{1,5},{2,6},{3,7},{4,0},{5,1},{6,2},{7,3},{8,12},{9,13},{10,... | collective-permute-start | bytes 3538952 | tf_op jit(solution)/shard_map/ppermute | solution.py:34
  383.0 36.7 %collective-permute-start.19 = (bf16[2,96,3072]{2,1,0:T(8,128)(2,1)S(1)}, bf16[2,96,3072]{2,1,0:T(8,128)(2,1)S(1)}, u32[]{:S(2)}, u32[]{:S(2)}) collective-permute-start(bf16[2,96,3072]{2,1,0:T(8,128)(2,1)S(1)} %get-tuple-element.276), channel_id=1, source_target_pairs={{0,1},{1,0},{2,3},{3,2},{4,5},{5,4},{6,7},{7,6},{8,9},{9,8},{10,11... | collective-permute-start | bytes 3538952 | tf_op jit(solution)/shard_map/ppermute | solution.py:34
  425.7 40.4 %collective-permute-start.22 = (bf16[2,96,1536]{2,1,0:T(8,128)(2,1)}, bf16[2,96,1536]{2,1,0:T(8,128)(2,1)}, u32[]{:S(2)}, u32[]{:S(2)}) collective-permute-start(bf16[2,96,1536]{2,1,0:T(8,128)(2,1)} %bitcast.39), channel_id=1, source_target_pairs={{0,4},{1,5},{2,6},{3,7},{4,0},{5,1},{6,2},{7,3},{8,12},{9,13},{10,... | collective-permute-start | bytes 1769480 | tf_op jit(solution)/shard_map/ppermute | solution.py:34
  426.4 43.2 %collective-permute-start.23 = (bf16[2,96,1664]{2,1,0:T(8,128)(2,1)}, bf16[2,96,1664]{2,1,0:T(8,128)(2,1)}, u32[]{:S(2)}, u32[]{:S(2)}) collective-permute-start(bf16[2,96,1664]{2,1,0:T(8,128)(2,1)} %get-tuple-element.288), channel_id=1, source_target_pairs={{0,1},{1,0},{2,3},{3,2},{4,5},{5,4},{6,7},{7,6},{8,9},{9,8},{10,11... | collective-permute-start | bytes 1916936 | tf_op jit(solution)/shard_map/ppermute | solution.py:34
  436.2 20.9 %collective-permute-start.43 = (bf16[24,6144]{1,0:T(8,128)(2,1)S(1)}, bf16[24,6144]{1,0:T(8,128)(2,1)S(1)}, u32[]{:S(2)}, u32[]{:S(2)}) collective-permute-start(bf16[24,6144]{1,0:T(8,128)(2,1)S(1)} %get-tuple-element.322), channel_id=1, source_target_pairs={{0,16},{1,17},{2,18},{3,19},{4,20},{5,21},{6,22},{7,23},{8,24},{9,... | collective-permute-start | bytes 884744 | tf_op jit(solution)/shard_map/ppermute | solution.py:38
  436.2 26.1 %collective-permute-start.44 = (bf16[24,6144]{1,0:T(8,128)(2,1)S(1)}, bf16[24,6144]{1,0:T(8,128)(2,1)S(1)}, u32[]{:S(2)}, u32[]{:S(2)}) collective-permute-start(bf16[24,6144]{1,0:T(8,128)(2,1)S(1)} %get-tuple-element.323), channel_id=1, source_target_pairs={{0,24},{1,25},{2,26},{3,27},{4,28},{5,29},{6,30},{7,31},{8,0},{9,1... | collective-permute-start | bytes 884744 | tf_op jit(solution)/shard_map/ppermute | solution.py:38
  443.9 30.9 %collective-permute-start.24 = (bf16[96,1536]{1,0:T(8,128)(2,1)}, bf16[96,1536]{1,0:T(8,128)(2,1)S(1)}, u32[]{:S(2)}, u32[]{:S(2)}) collective-permute-start(bf16[96,1536]{1,0:T(8,128)(2,1)} %get-tuple-element.292), channel_id=1, source_target_pairs={{0,1},{1,0},{2,3},{3,2},{4,5},{5,4},{6,7},{7,6},{8,9},{9,8},{10,11... | collective-permute-start | bytes 884744 | tf_op jit(solution)/shard_map/ppermute | solution.py:34
  471.7 45.8 %collective-permute-start.28 = (bf16[96,1536]{1,0:T(8,128)(2,1)}, bf16[96,1536]{1,0:T(8,128)(2,1)S(1)}, u32[]{:S(2)}, u32[]{:S(2)}) collective-permute-start(bf16[96,1536]{1,0:T(8,128)(2,1)} %get-tuple-element.304), channel_id=1, source_target_pairs={{0,1},{1,0},{2,3},{3,2},{4,5},{5,4},{6,7},{7,6},{8,9},{9,8},{10,11... | collective-permute-start | bytes 884744 | tf_op jit(solution)/shard_map/ppermute | solution.py:34
  472.3 45.3 %collective-permute-start.29 = (bf16[96,1664]{1,0:T(8,128)(2,1)}, bf16[96,1664]{1,0:T(8,128)(2,1)}, u32[]{:S(2)}, u32[]{:S(2)}) collective-permute-start(bf16[96,1664]{1,0:T(8,128)(2,1)} %get-tuple-element.306), channel_id=1, source_target_pairs={{0,4},{1,5},{2,6},{3,7},{4,0},{5,1},{6,2},{7,3},{8,12},{9,13},{10,... | collective-permute-start | bytes 958472 | tf_op jit(solution)/shard_map/ppermute | solution.py:34
  489.0 21.3 %collective-permute-start.34 = (bf16[24,6144]{1,0:T(8,128)(2,1)S(1)}, bf16[24,6144]{1,0:T(8,128)(2,1)S(1)}, u32[]{:S(2)}, u32[]{:S(2)}) collective-permute-start(bf16[24,6144]{1,0:T(8,128)(2,1)S(1)} %get-tuple-element.313), channel_id=1, source_target_pairs={{0,16},{1,17},{2,18},{3,19},{4,20},{5,21},{6,22},{7,23},{8,24},{9,... | collective-permute-start | bytes 884744 | tf_op jit(solution)/shard_map/ppermute | solution.py:38
  493.2 23.0 %collective-permute-start.35 = (bf16[24,6144]{1,0:T(8,128)(2,1)S(1)}, bf16[24,6144]{1,0:T(8,128)(2,1)S(1)}, u32[]{:S(2)}, u32[]{:S(2)}) collective-permute-start(bf16[24,6144]{1,0:T(8,128)(2,1)S(1)} %get-tuple-element.314), channel_id=1, source_target_pairs={{0,24},{1,25},{2,26},{3,27},{4,28},{5,29},{6,30},{7,31},{8,0},{9,1... | collective-permute-start | bytes 884744 | tf_op jit(solution)/shard_map/ppermute | solution.py:38
  (95 other events, 1372.5 us)
Sparse Core Ops, SparseCore 0:
  20.7 195.9 all-gather.1

commit v4 on v3

v4 whole, which is shorter than its diff:
```python
import functools

import jax
import jax.numpy as jnp
from jax import lax
from jax.experimental import pallas as pl
from jax.experimental.pallas import tpu as pltpu
from jax.sharding import PartitionSpec as P

DH = 64
AXES = ("dp", "hd")
EPS = 1e-05
MASKED = -1e30
LANES = 128
bf16 = jnp.bfloat16
f32 = jnp.float32
sds = jax.ShapeDtypeStruct


BIT_PAIR, BIT_CORE, BIT_NEAR = 1, 2, 4


class Place:
    def __init__(self):
        self.count = lax.axis_size("dp") * lax.axis_size("hd")
        self.outer_size = self.count // 8
        index = lax.axis_index("dp") * lax.axis_size("hd") + lax.axis_index("hd")
        self.pair = index % 2
        self.core = (index // 2) % 2
        self.near = (index // 4) % 2
        self.outer = index // 8
        self.outer_bits = self.outer_size.bit_length() - 1

    def swap(self, x, bit):
        return lax.ppermute(x, AXES, [(i, i ^ bit) for i in range(self.count)])

    def order(self, d, near_first):
        n, rows = self.outer_size, d // self.count
        k = lax.broadcasted_iota(jnp.int32, (d, 1), 0)
        row, place = k % rows, (k // rows) % n
        outer = jnp.zeros_like(k)
        for b in range(self.outer_bits):
            outer = outer + ((place >> (self.outer_bits - 1 - b)) & 1) * (1 << b)
        outer = outer ^ self.outer
        rest = k // (rows * n)
        low, high = rest % 2, (rest // 2) % 2
        near, pair = (high, low) if near_first else (low, high)
        feature = outer * 2 + (near ^ self.near)
        feature = (feature * 2 + ((rest // 4) ^ self.core)) * 2 + (pair ^ self.pair)
        feature = feature * rows + row
        return (feature == lax.broadcasted_iota(jnp.int32, (d, d), 1)).astype(bf16)


def plus(a, b):
    return (a.astype(f32) + b.astype(f32)).astype(bf16)


class Sum:
    def __init__(self, place, grads):
        self.place, self.stage = place, 0
        send_a, keep_a, send_b, keep_b = grads
        self.send, self.kept = (send_a, send_b), (keep_a, keep_b)

    def swap(self):
        if self.stage < 2:
            bits = ((BIT_NEAR, BIT_PAIR), (BIT_PAIR, BIT_NEAR))[self.stage]
        else:
            bits = (8 << (self.stage - 2),)
        self.got = tuple(self.place.swap(x, bit) for x, bit in zip(self.send, bits))

    def sums(self):
        def part(at):
            return tuple(plus(k[at], g[at]) for k, g in zip(self.kept, self.got))

        if self.stage == 1:
            t = jnp.concatenate(part(slice(None)), axis=1)
            half = t.shape[0] // 2
            self.kept, self.send = (t[:half],), (t[half:],)
        else:
            half = self.kept[0].shape[0] // 2
            self.kept, self.send = part(slice(half)), part(slice(half, None))
        self.stage += 1

    def total(self):
        return self.kept[0].astype(f32) + self.got[0].astype(f32)


def tie(x, *others):
    out = lax.optimization_barrier((x,) + others)
    return out[0], out[1:]


def hold(x, *groups):
    x, kept = tie(x, *[g.kept for g in groups])
    for g, k in zip(groups, kept):
        g.kept = k
    return x


def need(x, *groups):
    x, send = tie(x, *[g.send for g in groups])
    for g, k in zip(groups, send):
        g.send = k
    return x


def nn(a, b):
    return jnp.dot(a, b, preferred_element_type=f32)


def nt(a, b):
    return lax.dot_general(a, b, (((1,), (1,)), ((), ())), preferred_element_type=f32)


def tn(a, b):
    return lax.dot_general(a, b, (((0,), (0,)), ((), ())), preferred_element_type=f32)


def unit_norm(x):
    centred = x - jnp.mean(x, axis=-1, keepdims=True)
    inv = lax.rsqrt(jnp.mean(centred * centred, axis=-1, keepdims=True) + EPS)
    return centred * inv, inv


def norm_backward(grad, x, gain):
    unit, inv = unit_norm(x)
    du = grad * gain
    dx = inv * (
        du
        - jnp.mean(du, axis=-1, keepdims=True)
        - unit * jnp.mean(du * unit, axis=-1, keepdims=True)
    )
    return dx, jnp.sum(grad * unit, axis=0, keepdims=True), jnp.sum(grad, axis=0, keepdims=True)


GELU_A = 0.7978845608028654
GELU_B = 0.044715


def two_heads(x):
    first = lax.broadcasted_iota(jnp.int32, x.shape, 1) < DH
    zero = jnp.zeros_like(x)
    return jnp.concatenate((jnp.where(first, x, zero), jnp.where(first, zero, x)), axis=0)


def side_by_side(x):
    n = x.shape[0] // 2
    first = lax.broadcasted_iota(jnp.int32, (n, LANES), 1) < DH
    return jnp.where(first, x[:n], x[n:])


def probabilities(qs, k2, allowed):
    s = jnp.where(allowed, nt(qs, k2) * DH ** (-0.5), MASKED)
    e = jnp.exp(s - jnp.max(s, axis=-1, keepdims=True))
    return e / jnp.sum(e, axis=-1, keepdims=True)


def causal_mask(length):
    row = lax.broadcasted_iota(jnp.int32, (2 * length, length), 0)
    col = lax.broadcasted_iota(jnp.int32, (2 * length, length), 1)
    return jnp.where(row >= length, row - length, row) >= col


def attend_back(q2, k2, v2, do2, allowed):
    scale = DH ** (-0.5)
    qs, dos = two_heads(q2), two_heads(do2)
    p = probabilities(qs, k2, allowed)
    dp = nt(dos, v2)
    ds = (p * (dp - jnp.sum(p * dp, axis=-1, keepdims=True))).astype(bf16)
    dq = side_by_side(nn(ds, k2)) * scale
    dk = tn(ds, qs) * scale
    dv = tn(p.astype(bf16), dos)
    return dq.astype(bf16), dk.astype(bf16), dv.astype(bf16)


def self_forward_kernel(captions, row, x_ref, vec_ref, w_ref, y_ref, a_ref, qkv_ref, o_ref):
    j = pl.program_id(0)

    @pl.when(j == 0)
    def _():
        unit, _inv = unit_norm(x_ref[...].astype(f32))
        a_ref[...] = (unit * vec_ref[row : row + 1] + vec_ref[row + 1 : row + 2]).astype(bf16)

    @pl.when(j < 3)
    def _():
        qkv_ref[j] = nn(a_ref[...], w_ref[...]).astype(bf16)

    @pl.when(j == 3)
    def _():
        length = x_ref.shape[0] // captions
        allowed = causal_mask(length)
        for c in range(captions):
            at = slice(c * length, (c + 1) * length)
            for h in range(0, x_ref.shape[1], LANES):
                cols = slice(h, h + LANES)
                p = probabilities(two_heads(qkv_ref[0, at, cols]), qkv_ref[1, at, cols], allowed)
                o_ref[at, cols] = side_by_side(nn(p.astype(bf16), qkv_ref[2, at, cols])).astype(bf16)
        y_ref[...] = x_ref[...].astype(f32) + nn(o_ref[...], w_ref[...])


def self_backward_kernel(
    captions, row, x_ref, vec_ref, a_ref, qkv_ref, o_ref, dx_ref, w_ref, *refs
):
    out_ref, vg_ref, p_ref, acc_ref = refs[-4:]
    j = pl.program_id(0)

    @pl.when(j == 0)
    def _():
        dy = dx_ref[...].astype(bf16)
        p_ref[0] = a_ref[...]
        p_ref[1] = o_ref[...]
        p_ref[5] = dy
        do = nt(dy, w_ref[...]).astype(bf16)
        length = x_ref.shape[0] // captions
        allowed = causal_mask(length)
        for c in range(captions):
            at = slice(c * length, (c + 1) * length)
            for h in range(0, x_ref.shape[1], LANES):
                cols = slice(h, h + LANES)
                dq, dk, dv = attend_back(
                    qkv_ref[0, at, cols], qkv_ref[1, at, cols], qkv_ref[2, at, cols],
                    do[at, cols], allowed,
                )
                p_ref[2, at, cols] = dq
                p_ref[3, at, cols] = dk
                p_ref[4, at, cols] = dv
        acc_ref[...] = jnp.zeros_like(acc_ref)

    @pl.when(j > 0)
    def _():
        acc_ref[...] += nt(p_ref[1 + j], w_ref[...])

    @pl.when(j == 3)
    def _():
        dn, gg, gs = norm_backward(acc_ref[...], x_ref[...].astype(f32), vec_ref[row : row + 1])
        out_ref[...] = dx_ref[...] + dn
        vg_ref[0:1] = gg
        vg_ref[1:2] = gs
        if len(refs) > 4:
            at = lax.broadcasted_iota(jnp.int32, refs[0].shape, 0)
            rows = jnp.where(at == 0, gg, jnp.where(at == 1, gs, refs[0][...]))
            p_ref[6] = jnp.zeros_like(p_ref[6])
            p_ref[6, 0 : refs[0].shape[0]] = rows.astype(bf16)


def cross_forward_kernel(
    captions, row, count_ref, x_ref, vec_ref, kv_ref, w_ref, y_ref, c_ref, q_ref, o_ref
):
    j = pl.program_id(0)
    d = x_ref.shape[1]

    @pl.when(j == 0)
    def _():
        unit, _inv = unit_norm(x_ref[...])
        c = (unit * vec_ref[row : row + 1] + vec_ref[row + 1 : row + 2]).astype(bf16)
        c_ref[...] = c
        q_ref[...] = nn(c, w_ref[...]).astype(bf16)

    @pl.when(j == 1)
    def _():
        length = x_ref.shape[0] // captions
        patches = kv_ref.shape[0] // captions
        slot = lax.broadcasted_iota(jnp.int32, (2 * length, patches), 1)
        for c in range(captions):
            at = slice(c * length, (c + 1) * length)
            keys = slice(c * patches, (c + 1) * patches)
            allowed = slot < count_ref[c]
            for h in range(0, d, LANES):
                cols = slice(h, h + LANES)
                vcols = slice(d + h, d + h + LANES)
                p = probabilities(two_heads(q_ref[at, cols]), kv_ref[keys, cols], allowed)
                o_ref[at, cols] = side_by_side(nn(p.astype(bf16), kv_ref[keys, vcols])).astype(bf16)
        y_ref[...] = x_ref[...] + nn(o_ref[...], w_ref[...])


def cross_backward_kernel(
    captions, row, count_ref, x_ref, vec_ref, c_ref, q_ref, o_ref, kv_ref, dx_ref, w_ref,
    out_ref, vg_ref, p_ref, dkv_ref,
):
    j = pl.program_id(0)
    d = x_ref.shape[1]

    @pl.when(j == 0)
    def _():
        dy = dx_ref[...].astype(bf16)
        p_ref[0] = c_ref[...]
        p_ref[1] = o_ref[...]
        p_ref[3] = dy
        do = nt(dy, w_ref[...]).astype(bf16)
        length = x_ref.shape[0] // captions
        patches = kv_ref.shape[0] // captions
        slot = lax.broadcasted_iota(jnp.int32, (2 * length, patches), 1)
        for c in range(captions):
            at = slice(c * length, (c + 1) * length)
            keys = slice(c * patches, (c + 1) * patches)
            allowed = slot < count_ref[c]
            for h in range(0, d, LANES):
                cols = slice(h, h + LANES)
                vcols = slice(d + h, d + h + LANES)
                dq, dk, dv = attend_back(
                    q_ref[at, cols], kv_ref[keys, cols], kv_ref[keys, vcols], do[at, cols], allowed
                )
                p_ref[2, at, cols] = dq
                dkv_ref[keys, cols] = dk
                dkv_ref[keys, vcols] = dv

    @pl.when(j == 1)
    def _():
        dn, gg, gs = norm_backward(nt(p_ref[2], w_ref[...]), x_ref[...], vec_ref[row : row + 1])
        out_ref[...] = dx_ref[...] + dn
        vg_ref[0:1] = gg
        vg_ref[1:2] = gs


def feed_forward_kernel(row, x_ref, vec_ref, up_ref, down_ref, y_ref, b_ref, u_ref):
    @pl.when(pl.program_id(0) == 0)
    def _():
        unit, _inv = unit_norm(x_ref[...])
        b_ref[...] = (unit * vec_ref[row : row + 1] + vec_ref[row + 1 : row + 2]).astype(bf16)
        y_ref[...] = x_ref[...]

    u = nn(b_ref[...], up_ref[...])
    u_ref[...] = u
    g = 0.5 * u * (1.0 + jnp.tanh(GELU_A * (u + GELU_B * u * u * u)))
    y_ref[...] += nn(g.astype(bf16), down_ref[...])


def feed_backward_kernel(
    row, x_ref, vec_ref, dx_ref, up_ref, down_ref, *refs
):
    out_ref, vg_ref, p_ref, acc_ref = refs[-4:]
    j = pl.program_id(0)

    @pl.when(j == 0)
    def _():
        if len(refs) > 4:
            p_ref[0] = refs[0][...]
        else:
            unit, _inv = unit_norm(x_ref[...])
            p_ref[0] = (unit * vec_ref[row : row + 1] + vec_ref[row + 1 : row + 2]).astype(bf16)
        p_ref[1] = dx_ref[...].astype(bf16)
        acc_ref[...] = jnp.zeros_like(acc_ref)

    u = refs[1][...] if len(refs) > 4 else nn(p_ref[0], up_ref[...])
    t = jnp.tanh(GELU_A * (u + GELU_B * u * u * u))
    p_ref[2 + j] = (0.5 * u * (1.0 + t)).astype(bf16)
    slope = 0.5 * (1.0 + t) + 0.5 * u * (1.0 - t * t) * GELU_A * (1.0 + 3.0 * GELU_B * u * u)
    du = (slope * nt(p_ref[1], down_ref[...])).astype(bf16)
    p_ref[6 + j] = du
    acc_ref[...] += nt(du, up_ref[...])

    @pl.when(j == 3)
    def _():
        dn, gg, gs = norm_backward(acc_ref[...], x_ref[...], vec_ref[row : row + 1])
        out_ref[...] = dx_ref[...].astype(f32) + dn
        vg_ref[0:1] = gg
        vg_ref[1:2] = gs


def feed_out_kernel(x_ref, g_ref, down_ref, y_ref, acc_ref):
    j = pl.program_id(0)

    @pl.when(j == 0)
    def _():
        acc_ref[...] = x_ref[...]

    acc_ref[...] += nn(g_ref[0], down_ref[...])

    @pl.when(j == 3)
    def _():
        y_ref[...] = acc_ref[...].astype(bf16)


def both(own_ref, got_ref):
    return jnp.concatenate((own_ref[0], got_ref[0]), axis=0)


def emit(g, send_ref, keep_ref):
    half = keep_ref.shape[0]
    keep_ref[...] = g[:half].astype(bf16)
    send_ref[...] = g[half:].astype(bf16)


def feed_grads_kernel(
    order_ref, b_ref, b2_ref, z_ref, z2_ref, g_ref, g2_ref, u_ref, u2_ref,
    send_a_ref, keep_a_ref, send_b_ref, keep_b_ref, bt_ref,
):
    @pl.when(pl.program_id(0) == 0)
    def _():
        bt_ref[...] = nt(order_ref[0], both(b_ref, b2_ref)).astype(bf16)

    emit(nn(bt_ref[...], both(u_ref, u2_ref)), send_a_ref, keep_a_ref)
    gt = nt(order_ref[1], both(g_ref, g2_ref)).astype(bf16)
    emit(nn(gt, both(z_ref, z2_ref)), send_b_ref, keep_b_ref)


def attend_grads_kernel(
    order_ref, s_ref, s2_ref, sd_ref, sd2_ref, *refs
):
    send_a_ref, keep_a_ref, send_b_ref, keep_b_ref = refs[-4:]
    j = pl.program_id(0)

    def product(a_ref, a2_ref, d_ref, d2_ref):
        at = nt(order_ref[0], both(a_ref, a2_ref)).astype(bf16)
        return nn(at, both(d_ref, d2_ref))

    @pl.when(j < 2)
    def _():
        emit(product(s_ref, s2_ref, sd_ref, sd2_ref), send_a_ref, keep_a_ref)

    @pl.when((j == 2) | (j == 3))
    def _():
        emit(product(s_ref, s2_ref, sd_ref, sd2_ref), send_b_ref, keep_b_ref)

    if len(refs) > 4:
        c_ref, c2_ref, cd_ref, cd2_ref, pair_ref, pair2_ref = refs[:6]

        @pl.when((j == 4) | (j == 5))
        def _():
            emit(product(c_ref, c2_ref, cd_ref, cd2_ref), send_a_ref, keep_a_ref)

        @pl.when(j > 5)
        def _():
            emit(pair_ref[...].astype(f32) + pair2_ref[...].astype(f32), send_b_ref, keep_b_ref)


def pair_grads_kernel(enc_ref, dkv_ref, keep_ref, send_ref):
    emit(nn(enc_ref[...], dkv_ref[...]), send_ref, keep_ref)


def pack_kernel(u_qkv, u_out, u_up, u_down, m_qkv, m_out, m_up, m_down, c_q, c_pair, c_out, vec, out):
    rows, d = u_out.shape
    spread = spread_matrix().astype(bf16)
    i = lax.broadcasted_iota(jnp.int32, (rows, 4 * rows), 0)
    k = lax.broadcasted_iota(jnp.int32, (rows, 4 * rows), 1)

    def layer(at, qkv, w_out, up, down):
        out[:, at : at + 3 * d] = qkv[...]
        out[:, at + 3 * d : at + 4 * d] = w_out[...]
        for b in range(4 * d // 512):
            y = nn(up[:, b * 512 : (b + 1) * 512], spread).astype(bf16)
            for j in range(4):
                to = at + (4 + j) * d + b * LANES
                out[:, to : to + LANES] = y[:, j * LANES : (j + 1) * LANES]
        for j in range(4):
            y = nn((k == 4 * i + j).astype(bf16), down[...])
            out[:, at + (8 + j) * d : at + (9 + j) * d] = y.astype(bf16)

    layer(0, u_qkv, u_out, u_up, u_down)
    layer(12 * d, m_qkv, m_out, m_up, m_down)
    out[:, 24 * d : 25 * d] = c_q[...]
    out[:, 25 * d : 27 * d] = c_pair[...]
    out[:, 27 * d : 28 * d] = c_out[...]
    eye = lax.broadcasted_iota(jnp.int32, (rows, rows), 0) == lax.broadcasted_iota(jnp.int32, (rows, rows), 1)
    out[:, 28 * d :] = nt(eye.astype(bf16), vec[...]).astype(bf16)


def whole(x):
    return pl.BlockSpec(x.shape, lambda *_: (0,) * len(x.shape))


def call(kernel, steps, ins, in_specs, outs, out_specs, scratch=(), scalars=0):
    return pl.pallas_call(
        kernel,
        out_shape=outs,
        grid_spec=pltpu.PrefetchScalarGridSpec(
            num_scalar_prefetch=scalars,
            grid=(steps,),
            in_specs=in_specs,
            out_specs=out_specs,
            scratch_shapes=scratch,
        ),
        compiler_params=pltpu.CompilerParams(
            dimension_semantics=("arbitrary",), vmem_limit_bytes=40 << 20
        ),
        cost_estimate=pl.CostEstimate(flops=1000, bytes_accessed=1000, transcendentals=0),
    )(*ins)


class Layers:
    def __init__(self, captions, tokens, d, w, vec, order, count):
        self.captions, self.t, self.d = captions, tokens, d
        self.w, self.vec, self.order, self.count = w, vec, order, count
        self.xs = sds((tokens, d), f32)
        self.hs = sds((tokens, d), bf16)

    def weight(self, index):
        return pl.BlockSpec((self.d, self.d), lambda j, *_: (0, index(j)))

    def self_forward(self, x, at, row):
        outs = (self.xs, self.hs, sds((3, self.t, self.d), bf16), self.hs)
        return call(
            functools.partial(self_forward_kernel, self.captions, row), 4,
            (x, self.vec, self.w),
            [whole(x), whole(self.vec), self.weight(lambda j: at + j)],
            outs, [whole(o) for o in outs],
        )

    def self_backward(self, x, kept, dx, at, row, vectors=()):
        d, t = self.d, self.t
        a, qkv, o = kept
        outs = (self.xs, sds((8, d), f32), sds((6 + len(vectors), t, d), bf16))
        ins = (x, self.vec, a, qkv, o, dx)
        return call(
            functools.partial(self_backward_kernel, self.captions, row), 4,
            ins + (self.w,) + vectors,
            [whole(i) for i in ins] + [self.weight(lambda j: at + (j + 3) % 4)]
            + [whole(v) for v in vectors],
            outs, [whole(i) for i in outs],
            scratch=[pltpu.VMEM((t, d), f32)],
        )

    def cross_forward(self, x, kv, at, row):
        outs = (self.xs, self.hs, self.hs, self.hs)
        return call(
            functools.partial(cross_forward_kernel, self.captions, row), 2,
            (self.count, x, self.vec, kv, self.w),
            [whole(x), whole(self.vec), whole(kv), self.weight(lambda j: at + 3 * j)],
            outs, [whole(o) for o in outs], scalars=1,
        )

    def cross_backward(self, x, kept, kv, dx, at, row):
        d, t = self.d, self.t
        c, q, o = kept
        outs = (self.xs, sds((8, d), f32), sds((4, t, d), bf16), sds(kv.shape, bf16))
        ins = (x, self.vec, c, q, o, kv, dx)
        return call(
            functools.partial(cross_backward_kernel, self.captions, row), 2,
            (self.count,) + ins + (self.w,),
            [whole(i) for i in ins] + [self.weight(lambda j: at + 3 - 3 * j)],
            outs, [whole(i) for i in outs], scalars=1,
        )

    def pair_grads(self, enc_t, dkv):
        d = self.d
        outs = (sds((d // 2, 2 * d), bf16),) * 2
        grad = pl.BlockSpec((d // 2, d), lambda j: (0, j))
        return call(
            pair_grads_kernel, 2, (enc_t, dkv),
            [whole(enc_t), pl.BlockSpec((dkv.shape[0], d), lambda j: (0, j))],
            outs, [grad, grad],
        )

    def block(self, index):
        return pl.BlockSpec((1, self.t, self.d), lambda j: (index(j), 0, 0))

    def feed_grads(self, own, got):
        d, t = self.d, self.t
        outs = (sds((d // 4, 4 * d), bf16),) * 4
        at = [self.block(i) for i in (lambda j: 0, lambda j: 1, lambda j: 2 + j, lambda j: 6 + j)]
        return call(
            feed_grads_kernel, 4, (self.order,) + (own, got) * 4,
            [whole(self.order)] + [at[i // 2] for i in range(8)],
            outs, [pl.BlockSpec((d // 4, d), lambda j: (0, j))] * 4,
            scratch=[pltpu.VMEM((d // 2, 2 * t), bf16)],
        )

    def attend_grads(self, own, got, cross=()):
        d, t = self.d, self.t
        steps = 8 if cross else 4
        outs = (sds((d // 4, steps // 2 * d), bf16),) * 4

        def first(j):
            return jnp.where(j < 4, jnp.minimum(j, 1), jnp.minimum(j - 2, 3))

        def second(j):
            return jnp.where(j < 6, jnp.clip(j - 2, 0, 1), j - 4)

        grad_a = pl.BlockSpec((d // 4, d), lambda j: (0, first(j)))
        grad_b = pl.BlockSpec((d // 4, d), lambda j: (0, second(j)))
        order = pl.BlockSpec(
            (1, d // 2, d), lambda j: (jnp.where((j == 2) | (j == 3), 1, 0), 0, 0)
        )
        lhs = self.block(lambda j: jnp.minimum(j // 3, 1))
        rhs = self.block(lambda j: 2 + jnp.minimum(j, 3))
        ins, specs = (self.order, own, got, own, got), [order, lhs, lhs, rhs, rhs]
        if cross:
            own_c, got_c, pair, pair2 = cross
            lhs = self.block(lambda j: jnp.clip(j - 4, 0, 1))
            rhs = self.block(lambda j: 2 + jnp.clip(j - 4, 0, 1))
            half = pl.BlockSpec((d // 2, d), lambda j: (0, jnp.clip(j - 6, 0, 1)))
            ins = ins + (own_c, got_c, own_c, got_c, pair, pair2)
            specs = specs + [lhs, lhs, rhs, rhs, half, half]
        return call(
            attend_grads_kernel, steps, ins, specs, outs, [grad_a, grad_a, grad_b, grad_b]
        )

    def feed_forward(self, x, at, row):
        d, t = self.d, self.t
        outs = (self.xs, self.hs, sds((t, 4 * d), f32))
        return call(
            functools.partial(feed_forward_kernel, row), 4,
            (x, self.vec, self.w, self.w),
            [whole(x), whole(self.vec), self.weight(lambda j: at + j), self.weight(lambda j: at + 4 + j)],
            outs, [whole(outs[0]), whole(outs[1]), pl.BlockSpec((t, d), lambda j: (0, j))],
        )

    def feed_backward(self, x, kept, dx, at, row):
        d, t = self.d, self.t
        outs = (self.xs, sds((8, d), f32), sds((10, t, d), bf16))
        specs = [whole(kept[0]), pl.BlockSpec((t, d), lambda j: (0, j))] if kept else []
        return call(
            functools.partial(feed_backward_kernel, row), 4,
            (x, self.vec, dx, self.w, self.w) + tuple(kept),
            [
                whole(x), whole(self.vec), whole(dx),
                self.weight(lambda j: at + j), self.weight(lambda j: at + 4 + j),
            ] + specs,
            outs, [whole(i) for i in outs],
            scratch=[pltpu.VMEM((t, d), f32)],
        )

    def feed_out(self, x, p, at):
        return call(
            feed_out_kernel, 4, (x, p, self.w),
            [whole(x), self.block(lambda j: 2 + j), self.weight(lambda j: at + 4 + j)],
            self.hs, whole(self.hs), scratch=[pltpu.VMEM((self.t, self.d), f32)],
        )


def spread_matrix():
    k = lax.broadcasted_iota(jnp.int32, (512, 512), 0)
    n = lax.broadcasted_iota(jnp.int32, (512, 512), 1)
    return (k % 4) * 128 + k // 4 == n


def unspread(up):
    rows, wide = up.shape
    y = up.reshape(rows, 4, wide // 512, 128).transpose(0, 2, 1, 3)
    y = lax.dot_general(
        y.reshape(rows * (wide // 512), 512), spread_matrix().astype(f32),
        (((1,), (1,)), ((), ())), precision=lax.Precision.HIGHEST,
    )
    return y.reshape(rows, wide)


def local(
    tokens, encoder, patch_count, out_grad,
    u_ag, u_as, u_qkv, u_out, u_mg, u_ms, u_up, u_down,
    m_ag, m_as, m_qkv, m_out, c_g, c_s, c_q, c_pair, c_out, m_mg, m_ms, m_up, m_down,
):
    place = Place()
    captions, length, d = tokens.shape
    rows = u_qkv.shape[0]
    x0 = tokens.reshape(-1, d)
    enc = encoder.reshape(-1, d)
    order = jnp.stack((place.order(d, True), place.order(d, False)))
    order_pair = order[1]
    order = order[:, : d // 2]

    vectors = (u_ag, u_as, u_mg, u_ms, m_ag, m_as, c_g, c_s, m_mg, m_ms)
    vectors = jnp.pad(jnp.stack(vectors, axis=0), ((0, LANES - len(vectors)), (0, 0)))
    parts = (u_qkv, u_out, u_up, u_down, m_qkv, m_out, m_up, m_down, c_q, c_pair, c_out, vectors)
    packed = sds((rows, 28 * d + LANES), bf16)
    shard = call(pack_kernel, 1, parts, [whole(p) for p in parts], packed, whole(packed))
    enc_t = nt(order_pair, enc).astype(bf16)
    w = lax.all_gather(shard, AXES, axis=0, tiled=True)
    w, (order, enc_t) = tie(w, order, enc_t)
    vec = nt(jnp.eye(16, LANES, dtype=bf16), w[:, 28 * d :])

    net = Layers(captions, captions * length, d, w, vec, order, patch_count)

    w_pair = w[:, 25 * d : 27 * d]
    kv = nn(enc, w_pair).astype(bf16)
    x0a, *k_us = net.self_forward(x0, 0, 0)
    x1, *k_uf = net.feed_forward(x0a, 4, 2)
    x1a, *k_ms = net.self_forward(x1, 12, 4)
    x1b, *k_mc = net.cross_forward(x1a, kv, 24, 6)

    def core(x):
        return place.swap(x, BIT_CORE)

    def go_on(x, sums=(), start=()):
        x = hold(x, *sums)
        for g in sums:
            g.sums()
        x = need(x, *(tuple(sums) + tuple(g for g in start if g not in sums)))
        for g in start:
            g.swap()
        return x

    def rest(x, *groups):
        for _ in range(place.outer_bits - 1):
            for g in groups:
                x = go_on(x, [g], [g])
        return x

    dx, v_mf, p = net.feed_backward(x1b, (), out_grad.reshape(-1, d), 16, 8)
    q = core(p)
    x2 = net.feed_out(x1b, p, 16)
    p, (x2,) = tie(p, x2)
    s_mf = Sum(place, net.feed_grads(p, q))
    dx = go_on(dx, start=[s_mf])
    dx, v_mc, p_c, dkv = net.cross_backward(x1a, k_mc, kv, dx, 24, 6)
    q_c = core(p_c)
    keep, send = net.pair_grads(enc_t, dkv)
    dx, (send,) = tie(dx, send)
    got = core(send)
    dx, v_ms, p = net.self_backward(x1, k_ms, dx, 12, 4)
    q = core(p)
    dx = go_on(dx, [s_mf], [s_mf])
    dx, (p, p_c, keep) = tie(dx, p, p_c, keep)
    s_ma = Sum(place, net.attend_grads(p, q, (p_c, q_c, keep, got)))
    dx = go_on(dx, start=[s_ma])
    dx, v_uf, p = net.feed_backward(x0a, k_uf, dx, 4, 2)
    s_uf = Sum(place, net.feed_grads(p, core(p)))
    dx = need(dx, s_uf)
    dx = go_on(dx, [s_mf], [s_uf])
    v = [g[:2] for g in (v_uf, v_ms, v_mc, v_mf)]
    v = jnp.pad(jnp.concatenate(v, axis=0), ((2, 6), (0, 0)))
    dx, _v, p = net.self_backward(x0, k_us, dx, 0, 0, (v,))
    q = core(p)
    dx, (dkv,) = tie(dx, dkv)
    denc = nt(dkv, w_pair).astype(bf16)
    p, (denc,) = tie(p, denc)
    send_a, keep_a, send_b, keep_b = net.attend_grads(p, q)
    v = nt(order[1], plus(p[6], q[6])[:LANES]).astype(bf16)
    send_b = jnp.concatenate((send_b, v[d // 4 :]), axis=1)
    keep_b = jnp.concatenate((keep_b, v[: d // 4]), axis=1)
    s_us = Sum(place, (send_a, keep_a, send_b, keep_b))
    dx = need(dx, s_us)
    dx = go_on(dx, start=[s_mf])
    dx = go_on(dx, [s_ma], [s_ma])
    dx = rest(dx, s_mf)
    dx = go_on(dx, [s_uf], [s_us])
    dx, (r_mf,) = tie(dx, s_mf.total())
    dx = go_on(dx, [s_ma], [s_ma, s_uf])
    dx = go_on(dx, [s_us], [s_us])
    dx = rest(dx, s_ma)
    dx = go_on(dx, [s_uf], [s_uf])
    dx, (r_ma,) = tie(dx, s_ma.total())
    dx = go_on(dx, [s_us], [s_us])
    dx = rest(dx, s_uf, s_us)
    r_uf, r_us = s_uf.total(), s_us.total()

    def feed_rows(r):
        return unspread(r[:, : 4 * d]), r[:, 4 * d :].reshape(-1, d)

    def columns(r, *blocks):
        parts = [r[:, b * d : (b + 1) * d] for b in blocks]
        return jnp.concatenate(parts, axis=1) if len(parts) > 1 else parts[0]

    r_uup, r_udown = feed_rows(r_uf)
    r_mup, r_mdown = feed_rows(r_mf)
    vs = r_us[:, 4 * d :]
    v = [vs[:, i] for i in range(10)]
    return (
        x2.reshape(tokens.shape),
        dx.astype(bf16).reshape(tokens.shape),
        denc.reshape(encoder.shape),
        v[0], v[1], r_us[:, : 3 * d], r_us[:, 3 * d : 4 * d], v[2], v[3], r_uup, r_udown,
        v[4], v[5], columns(r_ma, 0, 1, 4), columns(r_ma, 5), v[6], v[7],
        columns(r_ma, 2), columns(r_ma, 6, 7), columns(r_ma, 3),
        v[8], v[9], r_mup, r_mdown,
    )


def solution(mesh):
    rows1 = P(AXES)
    rows2 = P(AXES, None)
    rows3 = P(AXES, None, None)
    block = (rows1, rows1, rows2, rows2)
    weights = block * 2 + block + (rows1, rows1, rows2, rows2, rows2) + block
    return jax.shard_map(
        local,
        mesh=mesh,
        in_specs=(rows3, rows3, rows1, rows3) + weights,
        out_specs=(rows3, rows3, rows3) + weights,
        check_vma=False,
    )
```

time: 554 us -> 497 us (0.90)
  other arithmetic: 44.8 us -> 17.2 us
  starting transfers between devices: 46.1 us -> 24 us
  local copies, waits for them, and re-layouts: 30 us -> 23.7 us
    ppermute x30, waiting for transfers between devices: 41.5 us -> 102 us  [swap(): return lax.ppermute(x, AXES, [(i, i ^ bit) for i in range(self.count)])]
    ppermute x15 -> x0, waiting for transfers between devices: 57.1 us -> none  [shift(): return lax.ppermute(x, AXES, [(i, (i + 8 * k) % n) for i in range(n)])]
    convert_element_type x30 -> x20, other arithmetic: 42.2 us -> 11.1 us  [plus(): return (a.astype(f32) + b.astype(f32)).astype(bf16)]
    ppermute x15 -> x0, starting transfers between devices: 24.4 us -> none  [shift(): return lax.ppermute(x, AXES, [(i, (i + 8 * k) % n) for i in range(n)])]
    unnamed x146 -> x64, local copies, waits for them, and re-layouts: 18.8 us -> 11.9 us
    pallas_call x11 -> x16, Pallas kernels: 96.8 us -> 101 us  [call(): pl.pallas_call(kernel, out_shape=outs, grid_spec=pltpu.PrefetchScalarGrid...]
  transfers between devices with their start and end apart: 46 -> 31, of which waited for: 18 -> 19; matrix products, arithmetic and copies ran while one was open for 10% -> 7% of each run, Pallas kernels for 10% -> 7%
where the time goes in v4:
time: 497 us; the launch traced here: 492 us
  waiting for transfers between devices  294 us (59%)
  Pallas kernels  101 us (20%)
  starting transfers between devices  24 us (5%)
  local copies, waits for them, and re-layouts  23.7 us (5%)
  matrix products  18.1 us (4%)
  other arithmetic  17.2 us (3%)
  between operations  15 us (3%)
    all_gather x1, waiting for transfers between devices, local(): w = lax.all_gather(shard, AXES, axis=0, tiled=True)  192 us
    ppermute x30, waiting for transfers between devices, swap(): return lax.ppermute(x, AXES, [(i, i ^ bit) for i in range(self.count)])  102 us
    pallas_call x16, Pallas kernels, call(): pl.pallas_call(kernel, out_shape=outs, grid_spec=pltpu.PrefetchScalarGrid...  101 us
    ppermute x30, starting transfers between devices, swap(): return lax.ppermute(x, AXES, [(i, i ^ bit) for i in range(self.count)])  23.9 us
    unnamed x64, local copies, waits for them, and re-layouts  11.9 us
    convert_element_type x20, other arithmetic, plus(): return (a.astype(f32) + b.astype(f32)).astype(bf16)  11.1 us
    dot_general x4, matrix products, nt(): lax.dot_general(a, b, (((1,), (1,)), ((), ())), preferred_element_type=f32)  10.1 us
  transfers between devices with their start and end apart: 31, of which 19 were waited for; matrix products, arithmetic and copies ran while one was open for 7% of the time, Pallas kernels for 7%

profile of v4, /device:TPU:0, one launch (start us, length us, event | category | flops | bytes accessed | tf_op | source)
XLA Modules:
  0.0 492.3 jit_solution(11071709807839165785)
XLA Ops:
  24.7 192.1 %all-gather.2.cloned.1.call-done.w_ref.up_ref.down_ref = bf16[768,21632]{1,0:T(8,128)(2,1)} async-done(((bf16[24,21632]{1,0:T(8,128)(2,1)}), bf16[768,21632]{1,0:T(8,128)(2,1)}) %all-gather.2.cloned.1.call-update) | async-done | bytes 33226768 | tf_op jit(solution)/shard_map/all_gather | solution.py:657
  217.9 5.0 %fusion.kv_ref = bf16[1152,1536]{1,0:T(8,128)(2,1)S(1)} fusion(bf16[1152,768]{1,0:T(8,128)(2,1)S(1)} %bitcast.40, bf16[768,21632]{1,0:T(8,128)(2,1)} %all-gather.2.cloned.1.call-done.w_ref.up_ref.down_ref), kind=kOutput, calls=%fused_computation.1 | convolution fusion | flops 2719678464 | bytes 7667712 | tf_op jit(solution)/shard_map/dot_general | solution.py:108
  222.8 4.9 shard_map.425
  228.6 5.7 %shard_map.426 = (f32[128,768]{1,0:T(8,128)S(1)}, bf16[128,768]{1,0:T(8,128)(2,1)S(1)}, f32[128,3072]{1,0:T(8,128)S(1)}) custom-call(f32[128,768]{1,0:T(8,128)S(1)} %get-tuple-element.172.x_ref, f32[16,768]{1,0:T(8,128)S(1)} %fusion.21.vec_ref, bf16[768,21632]{1,0:T(8,128)(2,1)} %all-gather.2.cloned.1.call-done.w_ref.up_ref.down_ref, ...), custom_call_target="tpu_custom_call" | custom-call | flops 1000 | bytes 1000 | tf_op jit(solution)/shard_map/pallas_call | solution.py:463
  234.3 4.9 shard_map.427
  239.2 7.5 %shard_map.428 = (f32[128,768]{1,0:T(8,128)S(1)}, bf16[128,768]{1,0:T(8,128)(2,1)S(1)}, bf16[128,768]{1,0:T(8,128)(2,1)S(1)}, bf16[128,768]{1,0:T(8,128)(2,1)S(1)}) custom-call(s32[2]{0:T(128)S(1)} %copy-done.28, f32[128,768]{1,0:T(8,128)S(1)} %get-tuple-element.174.x_ref, f32[16,768]{1,0:T(8,128)S(1)} %fusion.21.vec_ref, ...), custom_call_target="tpu_custom_call" | custom-call | flops 1000 | bytes 1000 | tf_op jit(solution)/shard_map/pallas_call | solution.py:463
  247.4 7.9 %shard_map.429 = (f32[128,768]{1,0:T(8,128)S(1)}, f32[8,768]{1,0:T(8,128)S(1)}, bf16[10,128,768]{2,1,0:T(8,128)(2,1)S(1)}) custom-call(f32[128,768]{1,0:T(8,128)S(1)} %get-tuple-element.175.x_ref, f32[16,768]{1,0:T(8,128)S(1)} %fusion.21.vec_ref, bf16[128,768]{1,0:T(8,128)(2,1)S(1)} %bitcast.43, ...), custom_call_target="tpu_custom_call" | custom-call | flops 1000 | bytes 1000 | tf_op jit(solution)/shard_map/pallas_call | solution.py:463
  255.7 4.4 shard_map.430
  260.1 5.1 %shard_map.431 = (bf16[192,3072]{1,0:T(8,128)(2,1)}, bf16[192,3072]{1,0:T(8,128)(2,1)S(1)}, bf16[192,3072]{1,0:T(8,128)(2,1)}, bf16[192,3072]{1,0:T(8,128)(2,1)S(1)}) custom-call(bf16[2,384,768]{2,1,0:T(8,128)(2,1)S(1)} %fusion.1.order_ref, bf16[10,128,768]{2,1,0:T(8,128)(2,1)S(1)} %get-tuple-element.189.g_ref.b_ref.z_ref.u_ref, ...), custom_call_target="tpu_custom_call" | custom-call | flops 1000 | bytes 1000 | tf_op jit(solution)/shard_map/pallas_call | solution.py:463
  267.2 10.6 %shard_map.432 = (f32[128,768]{1,0:T(8,128)S(1)}, f32[8,768]{1,0:T(8,128)S(1)}, bf16[4,128,768]{2,1,0:T(8,128)(2,1)S(1)}, bf16[1152,1536]{1,0:T(8,128)(2,1)S(1)}) custom-call(s32[2]{0:T(128)S(1)} %copy-done.28, f32[128,768]{1,0:T(8,128)S(1)} %get-tuple-element.174.x_ref, f32[16,768]{1,0:T(8,128)S(1)} %fusion.21.vec_ref, bf16[128,768]{1,0:T(8,128)(2,1)S(1)} %copy-done.12, ...), custom_call_target="tpu_custom_call" | custom-call | flops 1000 | bytes 1000 | tf_op jit(solution)/shard_map/pallas_call | solution.py:463
  281.7 9.8 %shard_map.434 = (f32[128,768]{1,0:T(8,128)S(1)}, f32[8,768]{1,0:T(8,128)S(1)}, bf16[6,128,768]{2,1,0:T(8,128)(2,1)S(1)}) custom-call(f32[128,768]{1,0:T(8,128)S(1)} %get-tuple-element.173.x_ref, f32[16,768]{1,0:T(8,128)S(1)} %fusion.21.vec_ref, bf16[128,768]{1,0:T(8,128)(2,1)S(1)} %get-tuple-element.181.a_ref, bf16[3,128,768]{2,1,0:T(8,128)(2,1)S(1)} %copy-done.9, ...), custom_call_target="tpu_custom_call" | custom-call | flops 1000 | bytes 1000 | tf_op jit(solution)/shard_map/pallas_call | solution.py:463
  297.3 7.7 %shard_map.435 = (bf16[192,3072]{1,0:T(8,128)(2,1)}, bf16[192,3072]{1,0:T(8,128)(2,1)S(1)}, bf16[192,3072]{1,0:T(8,128)(2,1)}, bf16[192,3072]{1,0:T(8,128)(2,1)S(1)}) custom-call(bf16[2,384,768]{2,1,0:T(8,128)(2,1)S(1)} %fusion.1.order_ref, bf16[6,128,768]{2,1,0:T(8,128)(2,1)S(1)} %get-tuple-element.211.s_ref.sd_ref, ...), custom_call_target="tpu_custom_call" | custom-call | flops 1000 | bytes 1000 | tf_op jit(solution)/shard_map/pallas_call | solution.py:463
  305.0 7.2 %shard_map.436 = (f32[128,768]{1,0:T(8,128)S(1)}, f32[8,768]{1,0:T(8,128)S(1)}, bf16[10,128,768]{2,1,0:T(8,128)(2,1)S(1)}) custom-call(f32[128,768]{1,0:T(8,128)S(1)} %get-tuple-element.172.x_ref, f32[16,768]{1,0:T(8,128)S(1)} %fusion.21.vec_ref, f32[128,768]{1,0:T(8,128)S(1)} %get-tuple-element.217.dx_ref, ...), custom_call_target="tpu_custom_call" | custom-call | flops 1000 | bytes 1000 | tf_op jit(solution)/shard_map/pallas_call | solution.py:463
  316.3 4.5 shard_map.437
  320.8 7.3 %collective-permute-done.7 = bf16[96,3072]{1,0:T(8,128)(2,1)S(1)} collective-permute-done((bf16[96,3072]{1,0:T(8,128)(2,1)S(1)}, bf16[96,3072]{1,0:T(8,128)(2,1)S(1)}, u32[]{:S(2)}, u32[]{:S(2)}) %collective-permute-start.7) | collective-permute-done | bytes 589856 | tf_op jit(solution)/shard_map/ppermute | solution.py:35
  330.5 10.4 %shard_map.438 = (f32[128,768]{1,0:T(8,128)S(1)}, f32[8,768]{1,0:T(8,128)}, bf16[7,128,768]{2,1,0:T(8,128)(2,1)S(1)}) custom-call(bf16[128,768]{1,0:T(8,128)(2,1)S(1)} %bitcast.42, f32[16,768]{1,0:T(8,128)S(1)} %fusion.21.vec_ref, bf16[128,768]{1,0:T(8,128)(2,1)S(1)} %get-tuple-element.178.a_ref, bf16[3,128,768]{2,1,0:T(8,128)(2,1)S(1)} %copy-done.7, ...), custom_call_target="tpu_custom_call" | custom-call | flops 1000 | bytes 1000 | tf_op jit(solution)/shard_map/pallas_call | solution.py:463
  343.1 5.7 %convolution_convert_fusion.1 = bf16[1152,768]{1,0:T(8,128)(2,1)} fusion(bf16[1152,1536]{1,0:T(8,128)(2,1)S(1)} %get-tuple-element.240.dkv_ref, bf16[768,21632]{1,0:T(8,128)(2,1)} %all-gather.2.cloned.1.call-done.w_ref.up_ref.down_ref), kind=kOutput, calls=%fused_computation.2 | convolution fusion | flops 2718793728 | bytes 7667712 | tf_op jit(solution)/shard_map/dot_general | solution.py:112
  355.8 14.1 %collective-permute-done.11 = bf16[192,3072]{1,0:T(8,128)(2,1)S(1)} collective-permute-done((bf16[192,3072]{1,0:T(8,128)(2,1)}, bf16[192,3072]{1,0:T(8,128)(2,1)S(1)}, u32[]{:S(2)}, u32[]{:S(2)}) %collective-permute-start.11) | collective-permute-done | bytes 1179680 | tf_op jit(solution)/shard_map/ppermute | solution.py:35
  374.8 20.4 %collective-permute-done.14 = bf16[192,3072]{1,0:T(8,128)(2,1)S(1)} collective-permute-done((bf16[192,3072]{1,0:T(8,128)(2,1)S(1)}, bf16[192,3072]{1,0:T(8,128)(2,1)S(1)}, u32[]{:S(2)}, u32[]{:S(2)}) %collective-permute-start.14) | collective-permute-done | bytes 1179680 | tf_op jit(solution)/shard_map/ppermute | solution.py:35
  400.1 7.8 %collective-permute-done.16 = bf16[96,3072]{1,0:T(8,128)(2,1)S(1)} collective-permute-done((bf16[96,3072]{1,0:T(8,128)(2,1)S(1)}, bf16[96,3072]{1,0:T(8,128)(2,1)S(1)}, u32[]{:S(2)}, u32[]{:S(2)}) %collective-permute-start.16) | collective-permute-done | bytes 589856 | tf_op jit(solution)/shard_map/ppermute | solution.py:35
  428.5 5.8 %collective-permute-done.21 = bf16[96,3072]{1,0:T(8,128)(2,1)} collective-permute-done((bf16[96,3072]{1,0:T(8,128)(2,1)}, bf16[96,3072]{1,0:T(8,128)(2,1)}, u32[]{:S(2)}, u32[]{:S(2)}) %collective-permute-start.21) | collective-permute-done | bytes 589856 | tf_op jit(solution)/shard_map/ppermute | solution.py:35
  443.2 9.9 %collective-permute-done.26 = bf16[48,6144]{1,0:T(8,128)(2,1)S(1)} collective-permute-done((bf16[48,6144]{1,0:T(8,128)(2,1)S(1)}, bf16[48,6144]{1,0:T(8,128)(2,1)S(1)}, u32[]{:S(2)}, u32[]{:S(2)}) %collective-permute-start.26) | collective-permute-done | bytes 589856 | tf_op jit(solution)/shard_map/ppermute | solution.py:35
  453.2 6.4 %collective-permute-done.27 = bf16[48,3200]{1,0:T(8,128)(2,1)S(1)} collective-permute-done((bf16[48,3200]{1,0:T(8,128)(2,1)S(1)}, bf16[48,3200]{1,0:T(8,128)(2,1)S(1)}, u32[]{:S(2)}, u32[]{:S(2)}) %collective-permute-start.27) | collective-permute-done | bytes 307232 | tf_op jit(solution)/shard_map/ppermute | solution.py:35
  464.0 11.9 %collective-permute-done.28 = bf16[24,3200]{1,0:T(8,128)(2,1)S(1)} collective-permute-done((bf16[24,3200]{1,0:T(8,128)(2,1)S(1)}, bf16[24,3200]{1,0:T(8,128)(2,1)S(1)}, u32[]{:S(2)}, u32[]{:S(2)}) %collective-permute-start.28) | collective-permute-done | bytes 153632 | tf_op jit(solution)/shard_map/ppermute | solution.py:35
  (188 shorter events, 100.2 us)
Async XLA Ops:
  7.2 209.6 %all-gather.2.cloned.1.call-start = ((), (), s32[]{:S(2)}) async-start(), calls=%async_computation | async-start | bytes 34265088 | tf_op jit(solution)/shard_map/all_gather | solution.py:657
  265.2 28.3 %collective-permute-start.2 = (bf16[192,3072]{1,0:T(8,128)(2,1)}, bf16[192,3072]{1,0:T(8,128)(2,1)S(1)}, u32[]{:S(2)}, u32[]{:S(2)}) collective-permute-start(bf16[192,3072]{1,0:T(8,128)(2,1)} %get-tuple-element.205), channel_id=1, source_target_pairs={{0,1},{1,0},{2,3},{3,2},{4,5},{5,4},{6,7},{7,6},{8,9},{9,8},{10,11... | collective-permute-start | bytes 3538952 | tf_op jit(solution)/shard_map/ppermute | solution.py:35
  266.7 28.1 %collective-permute-start.1 = (bf16[192,3072]{1,0:T(8,128)(2,1)}, bf16[192,3072]{1,0:T(8,128)(2,1)S(1)}, u32[]{:S(2)}, u32[]{:S(2)}) collective-permute-start(bf16[192,3072]{1,0:T(8,128)(2,1)} %get-tuple-element.203), channel_id=1, source_target_pairs={{0,4},{1,5},{2,6},{3,7},{4,0},{5,1},{6,2},{7,3},{8,12},{9,13},{10,... | collective-permute-start | bytes 3538952 | tf_op jit(solution)/shard_map/ppermute | solution.py:35
  312.4 15.6 %collective-permute-start.7 = (bf16[96,3072]{1,0:T(8,128)(2,1)S(1)}, bf16[96,3072]{1,0:T(8,128)(2,1)S(1)}, u32[]{:S(2)}, u32[]{:S(2)}) collective-permute-start(bf16[96,3072]{1,0:T(8,128)(2,1)S(1)} %get-tuple-element.227), channel_id=1, source_target_pairs={{0,1},{1,0},{2,3},{3,2},{4,5},{5,4},{6,7},{7,6},{8,9},{9,8},{10,11... | collective-permute-start | bytes 1769480 | tf_op jit(solution)/shard_map/ppermute | solution.py:35
  313.9 15.4 %collective-permute-start.8 = (bf16[96,3072]{1,0:T(8,128)(2,1)S(1)}, bf16[96,3072]{1,0:T(8,128)(2,1)S(1)}, u32[]{:S(2)}, u32[]{:S(2)}) collective-permute-start(bf16[96,3072]{1,0:T(8,128)(2,1)S(1)} %get-tuple-element.229), channel_id=1, source_target_pairs={{0,4},{1,5},{2,6},{3,7},{4,0},{5,1},{6,2},{7,3},{8,12},{9,13},{10,... | collective-permute-start | bytes 1769480 | tf_op jit(solution)/shard_map/ppermute | solution.py:35
  340.9 29.0 %collective-permute-start.11 = (bf16[192,3072]{1,0:T(8,128)(2,1)}, bf16[192,3072]{1,0:T(8,128)(2,1)S(1)}, u32[]{:S(2)}, u32[]{:S(2)}) collective-permute-start(bf16[192,3072]{1,0:T(8,128)(2,1)} %get-tuple-element.253), channel_id=1, source_target_pairs={{0,1},{1,0},{2,3},{3,2},{4,5},{5,4},{6,7},{7,6},{8,9},{9,8},{10,11... | collective-permute-start | bytes 3538952 | tf_op jit(solution)/shard_map/ppermute | solution.py:35
  341.6 29.0 %collective-permute-start.10 = (bf16[192,3072]{1,0:T(8,128)(2,1)}, bf16[192,3072]{1,0:T(8,128)(2,1)S(1)}, u32[]{:S(2)}, u32[]{:S(2)}) collective-permute-start(bf16[192,3072]{1,0:T(8,128)(2,1)} %get-tuple-element.251), channel_id=1, source_target_pairs={{0,4},{1,5},{2,6},{3,7},{4,0},{5,1},{6,2},{7,3},{8,12},{9,13},{10,... | collective-permute-start | bytes 3538952 | tf_op jit(solution)/shard_map/ppermute | solution.py:35
  348.8 46.5 %collective-permute-start.14 = (bf16[192,3072]{1,0:T(8,128)(2,1)S(1)}, bf16[192,3072]{1,0:T(8,128)(2,1)S(1)}, u32[]{:S(2)}, u32[]{:S(2)}) collective-permute-start(bf16[192,3072]{1,0:T(8,128)(2,1)S(1)} %get-tuple-element.265), channel_id=1, source_target_pairs={{0,1},{1,0},{2,3},{3,2},{4,5},{5,4},{6,7},{7,6},{8,9},{9,8},{10,11... | collective-permute-start | bytes 3538952 | tf_op jit(solution)/shard_map/ppermute | solution.py:35
  349.3 47.1 %collective-permute-start.13 = (bf16[192,3072]{1,0:T(8,128)(2,1)S(1)}, bf16[192,3072]{1,0:T(8,128)(2,1)S(1)}, u32[]{:S(2)}, u32[]{:S(2)}) collective-permute-start(bf16[192,3072]{1,0:T(8,128)(2,1)S(1)} %get-tuple-element.263), channel_id=1, source_target_pairs={{0,4},{1,5},{2,6},{3,7},{4,0},{5,1},{6,2},{7,3},{8,12},{9,13},{10,... | collective-permute-start | bytes 3538952 | tf_op jit(solution)/shard_map/ppermute | solution.py:35
  355.8 17.3 %collective-permute-start.12 = (bf16[48,6144]{1,0:T(8,128)(2,1)S(1)}, bf16[48,6144]{1,0:T(8,128)(2,1)S(1)}, u32[]{:S(2)}, u32[]{:S(2)}) collective-permute-start(bf16[48,6144]{1,0:T(8,128)(2,1)S(1)} %get-tuple-element.257), channel_id=1, source_target_pairs={{0,8},{1,9},{2,10},{3,11},{4,12},{5,13},{6,14},{7,15},{8,0},{9,1},... | collective-permute-start | bytes 1769480 | tf_op jit(solution)/shard_map/ppermute | solution.py:35
  371.0 36.9 %collective-permute-start.16 = (bf16[96,3072]{1,0:T(8,128)(2,1)S(1)}, bf16[96,3072]{1,0:T(8,128)(2,1)S(1)}, u32[]{:S(2)}, u32[]{:S(2)}) collective-permute-start(bf16[96,3072]{1,0:T(8,128)(2,1)S(1)} %get-tuple-element.273), channel_id=1, source_target_pairs={{0,1},{1,0},{2,3},{3,2},{4,5},{5,4},{6,7},{7,6},{8,9},{9,8},{10,11... | collective-permute-start | bytes 1769480 | tf_op jit(solution)/shard_map/ppermute | solution.py:35
  372.5 36.0 %collective-permute-start.17 = (bf16[96,3072]{1,0:T(8,128)(2,1)S(1)}, bf16[96,3072]{1,0:T(8,128)(2,1)S(1)}, u32[]{:S(2)}, u32[]{:S(2)}) collective-permute-start(bf16[96,3072]{1,0:T(8,128)(2,1)S(1)} %get-tuple-element.275), channel_id=1, source_target_pairs={{0,4},{1,5},{2,6},{3,7},{4,0},{5,1},{6,2},{7,3},{8,12},{9,13},{10,... | collective-permute-start | bytes 1769480 | tf_op jit(solution)/shard_map/ppermute | solution.py:35
  373.2 26.7 %collective-permute-start.15 = (bf16[24,6144]{1,0:T(8,128)(2,1)S(1)}, bf16[24,6144]{1,0:T(8,128)(2,1)S(1)}, u32[]{:S(2)}, u32[]{:S(2)}) collective-permute-start(bf16[24,6144]{1,0:T(8,128)(2,1)S(1)} %add_convert_fusion.29), channel_id=1, source_target_pairs={{0,16},{1,17},{2,18},{3,19},{4,20},{5,21},{6,22},{7,23},{8,24},{9,... | collective-permute-start | bytes 884744 | tf_op jit(solution)/shard_map/ppermute | solution.py:35
  397.9 24.6 %collective-permute-start.19 = (bf16[192,1664]{1,0:T(8,128)(2,1)}, bf16[192,1664]{1,0:T(8,128)(2,1)}, u32[]{:S(2)}, u32[]{:S(2)}) collective-permute-start(bf16[192,1664]{1,0:T(8,128)(2,1)} %pad_maximum_fusion), channel_id=1, source_target_pairs={{0,1},{1,0},{2,3},{3,2},{4,5},{5,4},{6,7},{7,6},{8,9},{9,8},{10,11... | collective-permute-start | bytes 1916936 | tf_op jit(solution)/shard_map/ppermute | solution.py:35
  398.7 22.5 %collective-permute-start.18 = (bf16[192,1536]{1,0:T(8,128)(2,1)S(1)}, bf16[192,1536]{1,0:T(8,128)(2,1)}, u32[]{:S(2)}, u32[]{:S(2)}) collective-permute-start(bf16[192,1536]{1,0:T(8,128)(2,1)S(1)} %get-tuple-element.283), channel_id=1, source_target_pairs={{0,4},{1,5},{2,6},{3,7},{4,0},{5,1},{6,2},{7,3},{8,12},{9,13},{10,... | collective-permute-start | bytes 1769480 | tf_op jit(solution)/shard_map/ppermute | solution.py:35
  409.8 16.1 %collective-permute-start.20 = (bf16[48,6144]{1,0:T(8,128)(2,1)}, bf16[48,6144]{1,0:T(8,128)(2,1)}, u32[]{:S(2)}, u32[]{:S(2)}) collective-permute-start(bf16[48,6144]{1,0:T(8,128)(2,1)} %get-tuple-element.289), channel_id=1, source_target_pairs={{0,8},{1,9},{2,10},{3,11},{4,12},{5,13},{6,14},{7,15},{8,0},{9,1},... | collective-permute-start | bytes 1769480 | tf_op jit(solution)/shard_map/ppermute | solution.py:35
  409.8 24.5 %collective-permute-start.21 = (bf16[96,3072]{1,0:T(8,128)(2,1)}, bf16[96,3072]{1,0:T(8,128)(2,1)}, u32[]{:S(2)}, u32[]{:S(2)}) collective-permute-start(bf16[96,3072]{1,0:T(8,128)(2,1)} %get-tuple-element.293), channel_id=1, source_target_pairs={{0,1},{1,0},{2,3},{3,2},{4,5},{5,4},{6,7},{7,6},{8,9},{9,8},{10,11... | collective-permute-start | bytes 1769480 | tf_op jit(solution)/shard_map/ppermute | solution.py:35
  411.2 24.3 %collective-permute-start.22 = (bf16[96,3072]{1,0:T(8,128)(2,1)}, bf16[96,3072]{1,0:T(8,128)(2,1)}, u32[]{:S(2)}, u32[]{:S(2)}) collective-permute-start(bf16[96,3072]{1,0:T(8,128)(2,1)} %get-tuple-element.295), channel_id=1, source_target_pairs={{0,4},{1,5},{2,6},{3,7},{4,0},{5,1},{6,2},{7,3},{8,12},{9,13},{10,... | collective-permute-start | bytes 1769480 | tf_op jit(solution)/shard_map/ppermute | solution.py:35
  423.8 17.7 %collective-permute-start.24 = (bf16[96,1536]{1,0:T(8,128)(2,1)S(1)}, bf16[96,1536]{1,0:T(8,128)(2,1)S(1)}, u32[]{:S(2)}, u32[]{:S(2)}) collective-permute-start(bf16[96,1536]{1,0:T(8,128)(2,1)S(1)} %get-tuple-element.301), channel_id=1, source_target_pairs={{0,1},{1,0},{2,3},{3,2},{4,5},{5,4},{6,7},{7,6},{8,9},{9,8},{10,11... | collective-permute-start | bytes 884744 | tf_op jit(solution)/shard_map/ppermute | solution.py:35
  425.3 16.3 %collective-permute-start.25 = (bf16[96,1664]{1,0:T(8,128)(2,1)S(1)}, bf16[96,1664]{1,0:T(8,128)(2,1)S(1)}, u32[]{:S(2)}, u32[]{:S(2)}) collective-permute-start(bf16[96,1664]{1,0:T(8,128)(2,1)S(1)} %get-tuple-element.303), channel_id=1, source_target_pairs={{0,4},{1,5},{2,6},{3,7},{4,0},{5,1},{6,2},{7,3},{8,12},{9,13},{10,... | collective-permute-start | bytes 958472 | tf_op jit(solution)/shard_map/ppermute | solution.py:35
  436.9 16.3 %collective-permute-start.26 = (bf16[48,6144]{1,0:T(8,128)(2,1)S(1)}, bf16[48,6144]{1,0:T(8,128)(2,1)S(1)}, u32[]{:S(2)}, u32[]{:S(2)}) collective-permute-start(bf16[48,6144]{1,0:T(8,128)(2,1)S(1)} %get-tuple-element.307), channel_id=1, source_target_pairs={{0,8},{1,9},{2,10},{3,11},{4,12},{5,13},{6,14},{7,15},{8,0},{9,1},... | collective-permute-start | bytes 1769480 | tf_op jit(solution)/shard_map/ppermute | solution.py:35
  441.8 17.8 %collective-permute-start.27 = (bf16[48,3200]{1,0:T(8,128)(2,1)S(1)}, bf16[48,3200]{1,0:T(8,128)(2,1)S(1)}, u32[]{:S(2)}, u32[]{:S(2)}) collective-permute-start(bf16[48,3200]{1,0:T(8,128)(2,1)S(1)} %get-tuple-element.311), channel_id=1, source_target_pairs={{0,8},{1,9},{2,10},{3,11},{4,12},{5,13},{6,14},{7,15},{8,0},{9,1},... | collective-permute-start | bytes 921608 | tf_op jit(solution)/shard_map/ppermute | solution.py:35
  459.6 16.2 %collective-permute-start.28 = (bf16[24,3200]{1,0:T(8,128)(2,1)S(1)}, bf16[24,3200]{1,0:T(8,128)(2,1)S(1)}, u32[]{:S(2)}, u32[]{:S(2)}) collective-permute-start(bf16[24,3200]{1,0:T(8,128)(2,1)S(1)} %add_convert_fusion.32), channel_id=1, source_target_pairs={{0,16},{1,17},{2,18},{3,19},{4,20},{5,21},{6,22},{7,23},{8,24},{9,... | collective-permute-start | bytes 460808 | tf_op jit(solution)/shard_map/ppermute | solution.py:35
  460.8 21.3 %collective-permute-start.29 = (bf16[24,6144]{1,0:T(8,128)(2,1)S(1)}, bf16[24,6144]{1,0:T(8,128)(2,1)S(1)}, u32[]{:S(2)}, u32[]{:S(2)}) collective-permute-start(bf16[24,6144]{1,0:T(8,128)(2,1)S(1)} %add_convert_fusion.22), channel_id=1, source_target_pairs={{0,16},{1,17},{2,18},{3,19},{4,20},{5,21},{6,22},{7,23},{8,24},{9,... | collective-permute-start | bytes 884744 | tf_op jit(solution)/shard_map/ppermute | solution.py:35
  (39 other events, 189.6 us)
Sparse Core Ops, SparseCore 0:
  20.7 195.9 all-gather.1

commit v5 on v4

--- a/solution.py
+++ b/solution.py
@@ -91,9 +91,9 @@
 
 
 def hold(x, *groups):
-    x, kept = tie(x, *[g.kept for g in groups])
-    for g, k in zip(groups, kept):
-        g.kept = k
+    x, terms = tie(x, *[(g.kept, g.got) for g in groups])
+    for g, t in zip(groups, terms):
+        g.kept, g.got = t
     return x
 
 
@@ -173,17 +173,17 @@
     return dq.astype(bf16), dk.astype(bf16), dv.astype(bf16)
 
 
-def self_forward_kernel(captions, row, x_ref, vec_ref, w_ref, y_ref, a_ref, qkv_ref, o_ref):
+def self_forward_kernel(captions, row, x_ref, vec_ref, w_ref, y_ref, f_ref, qkv_ref):
     j = pl.program_id(0)
 
     @pl.when(j == 0)
     def _():
         unit, _inv = unit_norm(x_ref[...].astype(f32))
-        a_ref[...] = (unit * vec_ref[row : row + 1] + vec_ref[row + 1 : row + 2]).astype(bf16)
+        f_ref[0] = (unit * vec_ref[row : row + 1] + vec_ref[row + 1 : row + 2]).astype(bf16)
 
     @pl.when(j < 3)
     def _():
-        qkv_ref[j] = nn(a_ref[...], w_ref[...]).astype(bf16)
+        qkv_ref[j] = nn(f_ref[0], w_ref[...]).astype(bf16)
 
     @pl.when(j == 3)
     def _():
@@ -194,12 +194,13 @@
             for h in range(0, x_ref.shape[1], LANES):
                 cols = slice(h, h + LANES)
                 p = probabilities(two_heads(qkv_ref[0, at, cols]), qkv_ref[1, at, cols], allowed)
-                o_ref[at, cols] = side_by_side(nn(p.astype(bf16), qkv_ref[2, at, cols])).astype(bf16)
-        y_ref[...] = x_ref[...].astype(f32) + nn(o_ref[...], w_ref[...])
+                o = side_by_side(nn(p.astype(bf16), qkv_ref[2, at, cols]))
+                f_ref[1, at, cols] = o.astype(bf16)
+        y_ref[...] = x_ref[...].astype(f32) + nn(f_ref[1], w_ref[...])
 
 
 def self_backward_kernel(
-    captions, row, x_ref, vec_ref, a_ref, qkv_ref, o_ref, dx_ref, w_ref, *refs
+    captions, row, x_ref, vec_ref, qkv_ref, dx_ref, w_ref, *refs
 ):
     out_ref, vg_ref, p_ref, acc_ref = refs[-4:]
     j = pl.program_id(0)
@@ -207,9 +208,7 @@
     @pl.when(j == 0)
     def _():
         dy = dx_ref[...].astype(bf16)
-        p_ref[0] = a_ref[...]
-        p_ref[1] = o_ref[...]
-        p_ref[5] = dy
+        p_ref[3] = dy
         do = nt(dy, w_ref[...]).astype(bf16)
         length = x_ref.shape[0] // captions
         allowed = causal_mask(length)
@@ -221,14 +220,14 @@
                     qkv_ref[0, at, cols], qkv_ref[1, at, cols], qkv_ref[2, at, cols],
                     do[at, cols], allowed,
                 )
-                p_ref[2, at, cols] = dq
-                p_ref[3, at, cols] = dk
-                p_ref[4, at, cols] = dv
+                p_ref[0, at, cols] = dq
+                p_ref[1, at, cols] = dk
+                p_ref[2, at, cols] = dv
         acc_ref[...] = jnp.zeros_like(acc_ref)
 
     @pl.when(j > 0)
     def _():
-        acc_ref[...] += nt(p_ref[1 + j], w_ref[...])
+        acc_ref[...] += nt(p_ref[j - 1], w_ref[...])
 
     @pl.when(j == 3)
     def _():
@@ -239,12 +238,12 @@
         if len(refs) > 4:
             at = lax.broadcasted_iota(jnp.int32, refs[0].shape, 0)
             rows = jnp.where(at == 0, gg, jnp.where(at == 1, gs, refs[0][...]))
-            p_ref[6] = jnp.zeros_like(p_ref[6])
-            p_ref[6, 0 : refs[0].shape[0]] = rows.astype(bf16)
+            p_ref[4] = jnp.zeros_like(p_ref[4])
+            p_ref[4, 0 : refs[0].shape[0]] = rows.astype(bf16)
 
 
 def cross_forward_kernel(
-    captions, row, count_ref, x_ref, vec_ref, kv_ref, w_ref, y_ref, c_ref, q_ref, o_ref
+    captions, row, count_ref, x_ref, vec_ref, kv_ref, w_ref, y_ref, f_ref, q_ref
 ):
     j = pl.program_id(0)
     d = x_ref.shape[1]
@@ -253,7 +252,7 @@
     def _():
         unit, _inv = unit_norm(x_ref[...])
         c = (unit * vec_ref[row : row + 1] + vec_ref[row + 1 : row + 2]).astype(bf16)
-        c_ref[...] = c
+        f_ref[0] = c
         q_ref[...] = nn(c, w_ref[...]).astype(bf16)
 
     @pl.when(j == 1)
@@ -269,12 +268,13 @@
                 cols = slice(h, h + LANES)
                 vcols = slice(d + h, d + h + LANES)
                 p = probabilities(two_heads(q_ref[at, cols]), kv_ref[keys, cols], allowed)
-                o_ref[at, cols] = side_by_side(nn(p.astype(bf16), kv_ref[keys, vcols])).astype(bf16)
-        y_ref[...] = x_ref[...] + nn(o_ref[...], w_ref[...])
+                o = side_by_side(nn(p.astype(bf16), kv_ref[keys, vcols]))
+                f_ref[1, at, cols] = o.astype(bf16)
+        y_ref[...] = x_ref[...] + nn(f_ref[1], w_ref[...])
 
 
 def cross_backward_kernel(
-    captions, row, count_ref, x_ref, vec_ref, c_ref, q_ref, o_ref, kv_ref, dx_ref, w_ref,
+    captions, row, count_ref, x_ref, vec_ref, q_ref, kv_ref, dx_ref, w_ref,
     out_ref, vg_ref, p_ref, dkv_ref,
 ):
     j = pl.program_id(0)
@@ -283,9 +283,7 @@
     @pl.when(j == 0)
     def _():
         dy = dx_ref[...].astype(bf16)
-        p_ref[0] = c_ref[...]
-        p_ref[1] = o_ref[...]
-        p_ref[3] = dy
+        p_ref[1] = dy
         do = nt(dy, w_ref[...]).astype(bf16)
         length = x_ref.shape[0] // captions
         patches = kv_ref.shape[0] // captions
@@ -300,53 +298,54 @@
                 dq, dk, dv = attend_back(
                     q_ref[at, cols], kv_ref[keys, cols], kv_ref[keys, vcols], do[at, cols], allowed
                 )
-                p_ref[2, at, cols] = dq
+                p_ref[0, at, cols] = dq
                 dkv_ref[keys, cols] = dk
                 dkv_ref[keys, vcols] = dv
 
     @pl.when(j == 1)
     def _():
-        dn, gg, gs = norm_backward(nt(p_ref[2], w_ref[...]), x_ref[...], vec_ref[row : row + 1])
+        dn, gg, gs = norm_backward(nt(p_ref[0], w_ref[...]), x_ref[...], vec_ref[row : row + 1])
         out_ref[...] = dx_ref[...] + dn
         vg_ref[0:1] = gg
         vg_ref[1:2] = gs
 
 
-def feed_forward_kernel(row, x_ref, vec_ref, up_ref, down_ref, y_ref, b_ref, u_ref):
-    @pl.when(pl.program_id(0) == 0)
+def feed_forward_kernel(row, x_ref, vec_ref, up_ref, down_ref, y_ref, f_ref, u_ref):
+    j = pl.program_id(0)
+
+    @pl.when(j == 0)
     def _():
         unit, _inv = unit_norm(x_ref[...])
-        b_ref[...] = (unit * vec_ref[row : row + 1] + vec_ref[row + 1 : row + 2]).astype(bf16)
+        f_ref[0] = (unit * vec_ref[row : row + 1] + vec_ref[row + 1 : row + 2]).astype(bf16)
         y_ref[...] = x_ref[...]
 
-    u = nn(b_ref[...], up_ref[...])
+    u = nn(f_ref[0], up_ref[...])
     u_ref[...] = u
-    g = 0.5 * u * (1.0 + jnp.tanh(GELU_A * (u + GELU_B * u * u * u)))
-    y_ref[...] += nn(g.astype(bf16), down_ref[...])
-
-
-def feed_backward_kernel(
-    row, x_ref, vec_ref, dx_ref, up_ref, down_ref, *refs
-):
-    out_ref, vg_ref, p_ref, acc_ref = refs[-4:]
+    g = (0.5 * u * (1.0 + jnp.tanh(GELU_A * (u + GELU_B * u * u * u)))).astype(bf16)
+    f_ref[1 + j] = g
+    y_ref[...] += nn(g, down_ref[...])
+
+
+def feed_backward_kernel(row, kept, x_ref, vec_ref, dx_ref, up_ref, down_ref, *refs):
+    out_ref, vg_ref, p_ref = refs[1:4] if kept else refs[:3]
+    acc_ref = refs[-1]
     j = pl.program_id(0)
 
     @pl.when(j == 0)
     def _():
-        if len(refs) > 4:
-            p_ref[0] = refs[0][...]
-        else:
+        if not kept:
             unit, _inv = unit_norm(x_ref[...])
-            p_ref[0] = (unit * vec_ref[row : row + 1] + vec_ref[row + 1 : row + 2]).astype(bf16)
-        p_ref[1] = dx_ref[...].astype(bf16)
+            refs[3][0] = (unit * vec_ref[row : row + 1] + vec_ref[row + 1 : row + 2]).astype(bf16)
+        p_ref[0] = dx_ref[...].astype(bf16)
         acc_ref[...] = jnp.zeros_like(acc_ref)
 
-    u = refs[1][...] if len(refs) > 4 else nn(p_ref[0], up_ref[...])
+    u = refs[0][...] if kept else nn(refs[3][0], up_ref[...])
     t = jnp.tanh(GELU_A * (u + GELU_B * u * u * u))
-    p_ref[2 + j] = (0.5 * u * (1.0 + t)).astype(bf16)
+    if not kept:
+        refs[3][1 + j] = (0.5 * u * (1.0 + t)).astype(bf16)
     slope = 0.5 * (1.0 + t) + 0.5 * u * (1.0 - t * t) * GELU_A * (1.0 + 3.0 * GELU_B * u * u)
-    du = (slope * nt(p_ref[1], down_ref[...])).astype(bf16)
-    p_ref[6 + j] = du
+    du = (slope * nt(p_ref[0], down_ref[...])).astype(bf16)
+    p_ref[1 + j] = du
     acc_ref[...] += nt(du, up_ref[...])
 
     @pl.when(j == 3)
@@ -459,7 +458,7 @@
     return pl.BlockSpec(x.shape, lambda *_: (0,) * len(x.shape))
 
 
-def call(kernel, steps, ins, in_specs, outs, out_specs, scratch=(), scalars=0):
+def call(kernel, steps, ins, in_specs, outs, out_specs, scratch=(), scalars=0, vmem=40):
     return pl.pallas_call(
         kernel,
         out_shape=outs,
@@ -471,7 +470,7 @@
             scratch_shapes=scratch,
         ),
         compiler_params=pltpu.CompilerParams(
-            dimension_semantics=("arbitrary",), vmem_limit_bytes=40 << 20
+            dimension_semantics=("arbitrary",), vmem_limit_bytes=vmem << 20
         ),
         cost_estimate=pl.CostEstimate(flops=1000, bytes_accessed=1000, transcendentals=0),
     )(*ins)
@@ -488,7 +487,7 @@
         return pl.BlockSpec((self.d, self.d), lambda j, *_: (0, index(j)))
 
     def self_forward(self, x, at, row):
-        outs = (self.xs, self.hs, sds((3, self.t, self.d), bf16), self.hs)
+        outs = (self.xs, sds((2, self.t, self.d), bf16), sds((3, self.t, self.d), bf16))
         return call(
             functools.partial(self_forward_kernel, self.captions, row), 4,
             (x, self.vec, self.w),
@@ -498,9 +497,8 @@
 
     def self_backward(self, x, kept, dx, at, row, vectors=()):
         d, t = self.d, self.t
-        a, qkv, o = kept
-        outs = (self.xs, sds((8, d), f32), sds((6 + len(vectors), t, d), bf16))
-        ins = (x, self.vec, a, qkv, o, dx)
+        outs = (self.xs, sds((8, d), f32), sds((4 + len(vectors), t, d), bf16))
+        ins = (x, self.vec, kept, dx)
         return call(
             functools.partial(self_backward_kernel, self.captions, row), 4,
             ins + (self.w,) + vectors,
@@ -511,7 +509,7 @@
         )
 
     def cross_forward(self, x, kv, at, row):
-        outs = (self.xs, self.hs, self.hs, self.hs)
+        outs = (self.xs, sds((2, self.t, self.d), bf16), self.hs)
         return call(
             functools.partial(cross_forward_kernel, self.captions, row), 2,
             (self.count, x, self.vec, kv, self.w),
@@ -521,9 +519,8 @@
 
     def cross_backward(self, x, kept, kv, dx, at, row):
         d, t = self.d, self.t
-        c, q, o = kept
-        outs = (self.xs, sds((8, d), f32), sds((4, t, d), bf16), sds(kv.shape, bf16))
-        ins = (x, self.vec, c, q, o, kv, dx)
+        outs = (self.xs, sds((8, d), f32), sds((2, t, d), bf16), sds(kv.shape, bf16))
+        ins = (x, self.vec, kept, kv, dx)
         return call(
             functools.partial(cross_backward_kernel, self.captions, row), 2,
             (self.count,) + ins + (self.w,),
@@ -544,18 +541,18 @@
     def block(self, index):
         return pl.BlockSpec((1, self.t, self.d), lambda j: (index(j), 0, 0))
 
-    def feed_grads(self, own, got):
+    def feed_grads(self, f, p):
         d, t = self.d, self.t
         outs = (sds((d // 4, 4 * d), bf16),) * 4
-        at = [self.block(i) for i in (lambda j: 0, lambda j: 1, lambda j: 2 + j, lambda j: 6 + j)]
-        return call(
-            feed_grads_kernel, 4, (self.order,) + (own, got) * 4,
-            [whole(self.order)] + [at[i // 2] for i in range(8)],
+        first, later = self.block(lambda j: 0), self.block(lambda j: 1 + j)
+        return call(
+            feed_grads_kernel, 4, (self.order,) + f + p + f + p,
+            [whole(self.order)] + [first] * 4 + [later] * 4,
             outs, [pl.BlockSpec((d // 4, d), lambda j: (0, j))] * 4,
             scratch=[pltpu.VMEM((d // 2, 2 * t), bf16)],
         )
 
-    def attend_grads(self, own, got, cross=()):
+    def attend_grads(self, f, p, cross=()):
         d, t = self.d, self.t
         steps = 8 if cross else 4
         outs = (sds((d // 4, steps // 2 * d), bf16),) * 4
@@ -572,14 +569,14 @@
             (1, d // 2, d), lambda j: (jnp.where((j == 2) | (j == 3), 1, 0), 0, 0)
         )
         lhs = self.block(lambda j: jnp.minimum(j // 3, 1))
-        rhs = self.block(lambda j: 2 + jnp.minimum(j, 3))
-        ins, specs = (self.order, own, got, own, got), [order, lhs, lhs, rhs, rhs]
+        rhs = self.block(lambda j: jnp.minimum(j, 3))
+        ins, specs = (self.order,) + f + p, [order, lhs, lhs, rhs, rhs]
         if cross:
-            own_c, got_c, pair, pair2 = cross
+            f, p, pair = cross
             lhs = self.block(lambda j: jnp.clip(j - 4, 0, 1))
-            rhs = self.block(lambda j: 2 + jnp.clip(j - 4, 0, 1))
+            rhs = lhs
             half = pl.BlockSpec((d // 2, d), lambda j: (0, jnp.clip(j - 6, 0, 1)))
-            ins = ins + (own_c, got_c, own_c, got_c, pair, pair2)
+            ins = ins + f + p + pair
             specs = specs + [lhs, lhs, rhs, rhs, half, half]
         return call(
             attend_grads_kernel, steps, ins, specs, outs, [grad_a, grad_a, grad_b, grad_b]
@@ -587,7 +584,7 @@
 
     def feed_forward(self, x, at, row):
         d, t = self.d, self.t
-        outs = (self.xs, self.hs, sds((t, 4 * d), f32))
+        outs = (self.xs, sds((5, t, d), bf16), sds((t, 4 * d), f32))
         return call(
             functools.partial(feed_forward_kernel, row), 4,
             (x, self.vec, self.w, self.w),
@@ -597,15 +594,16 @@
 
     def feed_backward(self, x, kept, dx, at, row):
         d, t = self.d, self.t
-        outs = (self.xs, sds((8, d), f32), sds((10, t, d), bf16))
-        specs = [whole(kept[0]), pl.BlockSpec((t, d), lambda j: (0, j))] if kept else []
-        return call(
-            functools.partial(feed_backward_kernel, row), 4,
-            (x, self.vec, dx, self.w, self.w) + tuple(kept),
+        outs = (self.xs, sds((8, d), f32), sds((5, t, d), bf16))
+        if not kept:
+            outs = outs + (sds((5, t, d), bf16),)
+        return call(
+            functools.partial(feed_backward_kernel, row, bool(kept)), 4,
+            (x, self.vec, dx, self.w, self.w) + kept,
             [
                 whole(x), whole(self.vec), whole(dx),
                 self.weight(lambda j: at + j), self.weight(lambda j: at + 4 + j),
-            ] + specs,
+            ] + [pl.BlockSpec((t, d), lambda j: (0, j)) for _ in kept],
             outs, [whole(i) for i in outs],
             scratch=[pltpu.VMEM((t, d), f32)],
         )
@@ -613,7 +611,7 @@
     def feed_out(self, x, p, at):
         return call(
             feed_out_kernel, 4, (x, p, self.w),
-            [whole(x), self.block(lambda j: 2 + j), self.weight(lambda j: at + 4 + j)],
+            [whole(x), self.block(lambda j: 1 + j), self.weight(lambda j: at + 4 + j)],
             self.hs, whole(self.hs), scratch=[pltpu.VMEM((self.t, self.d), f32)],
         )
 
@@ -652,7 +650,7 @@
     vectors = jnp.pad(jnp.stack(vectors, axis=0), ((0, LANES - len(vectors)), (0, 0)))
     parts = (u_qkv, u_out, u_up, u_down, m_qkv, m_out, m_up, m_down, c_q, c_pair, c_out, vectors)
     packed = sds((rows, 28 * d + LANES), bf16)
-    shard = call(pack_kernel, 1, parts, [whole(p) for p in parts], packed, whole(packed))
+    shard = call(pack_kernel, 1, parts, [whole(p) for p in parts], packed, whole(packed), vmem=60)
     enc_t = nt(order_pair, enc).astype(bf16)
     w = lax.all_gather(shard, AXES, axis=0, tiled=True)
     w, (order, enc_t) = tie(w, order, enc_t)
@@ -662,10 +660,10 @@
 
     w_pair = w[:, 25 * d : 27 * d]
     kv = nn(enc, w_pair).astype(bf16)
-    x0a, *k_us = net.self_forward(x0, 0, 0)
-    x1, *k_uf = net.feed_forward(x0a, 4, 2)
-    x1a, *k_ms = net.self_forward(x1, 12, 4)
-    x1b, *k_mc = net.cross_forward(x1a, kv, 24, 6)
+    x0a, f_us, k_us = net.self_forward(x0, 0, 0)
+    x1, f_uf, k_uf = net.feed_forward(x0a, 4, 2)
+    x1a, f_ms, k_ms = net.self_forward(x1, 12, 4)
+    x1b, f_mc, k_mc = net.cross_forward(x1a, kv, 24, 6)
 
     def core(x):
         return place.swap(x, BIT_CORE)
@@ -685,50 +683,60 @@
                 x = go_on(x, [g], [g])
         return x
 
-    dx, v_mf, p = net.feed_backward(x1b, (), out_grad.reshape(-1, d), 16, 8)
-    q = core(p)
-    x2 = net.feed_out(x1b, p, 16)
+    def pairs(x):
+        return x, core(x)
+
+    f_us, f_uf, f_ms = pairs(f_us), pairs(f_uf), pairs(f_ms)
+    x1b, (f_us, f_uf, f_ms) = tie(x1b, f_us, f_uf, f_ms)
+    f_mc = pairs(f_mc)
+    dx, v_mf, p, f = net.feed_backward(x1b, (), out_grad.reshape(-1, d), 16, 8)
+    p, f = pairs(p), pairs(f)
+    x2 = net.feed_out(x1b, f[0], 16)
     p, (x2,) = tie(p, x2)
-    s_mf = Sum(place, net.feed_grads(p, q))
+    s_mf = Sum(place, net.feed_grads(f, p))
+    dx, (f_mc,) = tie(dx, f_mc)
     dx = go_on(dx, start=[s_mf])
     dx, v_mc, p_c, dkv = net.cross_backward(x1a, k_mc, kv, dx, 24, 6)
-    q_c = core(p_c)
-    keep, send = net.pair_grads(enc_t, dkv)
+    p_c = pairs(p_c)
+    pair, send = net.pair_grads(enc_t, dkv)
     dx, (send,) = tie(dx, send)
-    got = core(send)
+    pair = pair, core(send)
     dx, v_ms, p = net.self_backward(x1, k_ms, dx, 12, 4)
-    q = core(p)
+    p = pairs(p)
     dx = go_on(dx, [s_mf], [s_mf])
-    dx, (p, p_c, keep) = tie(dx, p, p_c, keep)
-    s_ma = Sum(place, net.attend_grads(p, q, (p_c, q_c, keep, got)))
+    dx, (p, p_c, pair) = tie(dx, p, p_c, pair)
+    s_ma = Sum(place, net.attend_grads(f_ms, p, (f_mc, p_c, pair)))
     dx = go_on(dx, start=[s_ma])
-    dx, v_uf, p = net.feed_backward(x0a, k_uf, dx, 4, 2)
-    s_uf = Sum(place, net.feed_grads(p, core(p)))
-    dx = need(dx, s_uf)
-    dx = go_on(dx, [s_mf], [s_uf])
+    dx, v_uf, p = net.feed_backward(x0a, (k_uf,), dx, 4, 2)
+    p = pairs(p)
+    dx = go_on(dx, [s_ma, s_mf])
+    dx, (p,) = tie(dx, p)
+    s_uf = Sum(place, net.feed_grads(f_uf, p))
+    dx = go_on(dx, start=[s_uf, s_ma])
     v = [g[:2] for g in (v_uf, v_ms, v_mc, v_mf)]
     v = jnp.pad(jnp.concatenate(v, axis=0), ((2, 6), (0, 0)))
     dx, _v, p = net.self_backward(x0, k_us, dx, 0, 0, (v,))
-    q = core(p)
+    p = pairs(p)
+    dx = go_on(dx, [s_ma, s_uf])
     dx, (dkv,) = tie(dx, dkv)
     denc = nt(dkv, w_pair).astype(bf16)
-    p, (denc,) = tie(p, denc)
-    send_a, keep_a, send_b, keep_b = net.attend_grads(p, q)
-    v = nt(order[1], plus(p[6], q[6])[:LANES]).astype(bf16)
+    dx, (denc,) = tie(dx, denc)
+    dx, (p,) = tie(dx, p)
+    dx = go_on(dx, start=[s_mf, s_uf])
+    dx, (p,) = tie(dx, p)
+    send_a, keep_a, send_b, keep_b = net.attend_grads(f_us, p)
+    v = nt(order[1], plus(p[0][4], p[1][4])[:LANES]).astype(bf16)
     send_b = jnp.concatenate((send_b, v[d // 4 :]), axis=1)
     keep_b = jnp.concatenate((keep_b, v[: d // 4]), axis=1)
     s_us = Sum(place, (send_a, keep_a, send_b, keep_b))
-    dx = need(dx, s_us)
-    dx = go_on(dx, start=[s_mf])
-    dx = go_on(dx, [s_ma], [s_ma])
+    dx = go_on(dx, start=[s_us])
     dx = rest(dx, s_mf)
-    dx = go_on(dx, [s_uf], [s_us])
     dx, (r_mf,) = tie(dx, s_mf.total())
-    dx = go_on(dx, [s_ma], [s_ma, s_uf])
+    dx = go_on(dx, start=[s_ma])
+    dx = rest(dx, s_ma)
     dx = go_on(dx, [s_us], [s_us])
-    dx = rest(dx, s_ma)
+    dx, (r_ma,) = tie(dx, s_ma.total())
     dx = go_on(dx, [s_uf], [s_uf])
-    dx, (r_ma,) = tie(dx, s_ma.total())
     dx = go_on(dx, [s_us], [s_us])
     dx = rest(dx, s_uf, s_us)
     r_uf, r_us = s_uf.total(), s_us.total()

time: 497 us -> 513 us (1.032)
  waiting for transfers between devices: 294 us -> 318 us
  local copies, waits for them, and re-layouts: 23.7 us -> 13.7 us
    ppermute x30 -> x35, waiting for transfers between devices: 102 us -> 126 us  [swap(): return lax.ppermute(x, AXES, [(i, i ^ bit) for i in range(self.count)])]
    unnamed x64 -> x50, local copies, waits for them, and re-layouts: 11.9 us -> 2.35 us
    ppermute x30 -> x35, starting transfers between devices: 23.9 us -> 25.9 us  [swap(): return lax.ppermute(x, AXES, [(i, i ^ bit) for i in range(self.count)])]
  transfers between devices with their start and end apart: 31 -> 36, of which waited for: 19 -> 13; matrix products, arithmetic and copies ran while one was open for 7% -> 8% of each run, Pallas kernels for 7% -> 12%
where the time goes in v5:
time: 513 us; the launch traced here: 508 us
  waiting for transfers between devices  318 us (62%)
  Pallas kernels  101 us (20%)
  starting transfers between devices  25.9 us (5%)
  other arithmetic  18 us (4%)
  matrix products  17.1 us (3%)
  between operations  15.1 us (3%)
  local copies, waits for them, and re-layouts  13.7 us (3%)
    all_gather x1, waiting for transfers between devices, local(): w = lax.all_gather(shard, AXES, axis=0, tiled=True)  192 us
    ppermute x35, waiting for transfers between devices, swap(): return lax.ppermute(x, AXES, [(i, i ^ bit) for i in range(self.count)])  126 us
    pallas_call x16, Pallas kernels, call(): pl.pallas_call(kernel, out_shape=outs, grid_spec=pltpu.PrefetchScalarGrid...  101 us
    ppermute x35, starting transfers between devices, swap(): return lax.ppermute(x, AXES, [(i, i ^ bit) for i in range(self.count)])  25.9 us
    convert_element_type x20, other arithmetic, plus(): return (a.astype(f32) + b.astype(f32)).astype(bf16)  12 us
  transfers between devices with their start and end apart: 36, of which 13 were waited for; matrix products, arithmetic and copies ran while one was open for 8% of the time, Pallas kernels for 12%

profile of v5, /device:TPU:0, one launch (start us, length us, event | category | flops | bytes accessed | tf_op | source)
XLA Modules:
  0.0 508.1 jit_solution(16594995929773534464)
XLA Ops:
  17.2 192.0 %all-gather.2.cloned.1.call-done.w_ref.up_ref.down_ref = bf16[768,21632]{1,0:T(8,128)(2,1)} async-done(((bf16[24,21632]{1,0:T(8,128)(2,1)}), bf16[768,21632]{1,0:T(8,128)(2,1)}) %all-gather.2.cloned.1.call-update) | async-done | bytes 33226768 | tf_op jit(solution)/shard_map/all_gather | solution.py:655
  210.4 5.1 shard_map.425
  215.4 6.1 %shard_map.426 = (f32[128,768]{1,0:T(8,128)S(1)}, bf16[5,128,768]{2,1,0:T(8,128)(2,1)S(1)}, f32[128,3072]{1,0:T(8,128)S(1)}) custom-call(f32[128,768]{1,0:T(8,128)S(1)} %get-tuple-element.209.x_ref, f32[16,768]{1,0:T(8,128)S(1)} %fusion.21.vec_ref, bf16[768,21632]{1,0:T(8,128)(2,1)} %all-gather.2.cloned.1.call-done.w_ref.up_ref.down_ref, ...), custom_call_target="tpu_custom_call" | custom-call | flops 1000 | bytes 1000 | tf_op jit(solution)/shard_map/pallas_call | solution.py:462
  222.1 4.9 shard_map.427
  227.4 4.8 fusion.kv_ref
  232.2 7.6 %shard_map.428 = (f32[128,768]{1,0:T(8,128)S(1)}, bf16[2,128,768]{2,1,0:T(8,128)(2,1)S(1)}, bf16[128,768]{1,0:T(8,128)(2,1)S(1)}) custom-call(s32[2]{0:T(128)S(1)} %copy-done.21, f32[128,768]{1,0:T(8,128)S(1)} %get-tuple-element.211.x_ref, f32[16,768]{1,0:T(8,128)S(1)} %fusion.21.vec_ref, bf16[1152,1536]{1,0:T(8,128)(2,1)S(1)} %fusion.kv_ref, ...), custom_call_target="tpu_custom_call" | custom-call | flops 1000 | bytes 1000 | tf_op jit(solution)/shard_map/pallas_call | solution.py:462
  239.8 7.6 %shard_map.429 = (f32[128,768]{1,0:T(8,128)S(1)}, f32[8,768]{1,0:T(8,128)S(1)}, bf16[5,128,768]{2,1,0:T(8,128)(2,1)S(1)}, bf16[5,128,768]{2,1,0:T(8,128)(2,1)S(1)}) custom-call(f32[128,768]{1,0:T(8,128)S(1)} %get-tuple-element.216.x_ref, f32[16,768]{1,0:T(8,128)S(1)} %fusion.21.vec_ref, bf16[128,768]{1,0:T(8,128)(2,1)S(1)} %bitcast.43, ...), custom_call_target="tpu_custom_call" | custom-call | flops 1000 | bytes 1000 | tf_op jit(solution)/shard_map/pallas_call | solution.py:462
  253.4 5.1 %shard_map.431 = (bf16[192,3072]{1,0:T(8,128)(2,1)}, bf16[192,3072]{1,0:T(8,128)(2,1)S(1)}, bf16[192,3072]{1,0:T(8,128)(2,1)}, bf16[192,3072]{1,0:T(8,128)(2,1)S(1)}) custom-call(bf16[2,384,768]{2,1,0:T(8,128)(2,1)S(1)} %fusion.1.order_ref, bf16[5,128,768]{2,1,0:T(8,128)(2,1)S(1)} %get-tuple-element.218.g_ref.b_ref, ...), custom_call_target="tpu_custom_call" | custom-call | flops 1000 | bytes 1000 | tf_op jit(solution)/shard_map/pallas_call | solution.py:462
  260.5 10.6 %shard_map.432 = (f32[128,768]{1,0:T(8,128)S(1)}, f32[8,768]{1,0:T(8,128)S(1)}, bf16[2,128,768]{2,1,0:T(8,128)(2,1)S(1)}, bf16[1152,1536]{1,0:T(8,128)(2,1)S(1)}) custom-call(s32[2]{0:T(128)S(1)} %copy-done.21, f32[128,768]{1,0:T(8,128)S(1)} %get-tuple-element.211.x_ref, f32[16,768]{1,0:T(8,128)S(1)} %fusion.21.vec_ref, ...), custom_call_target="tpu_custom_call" | custom-call | flops 1000 | bytes 1000 | tf_op jit(solution)/shard_map/pallas_call | solution.py:462
  275.1 9.9 %shard_map.434 = (f32[128,768]{1,0:T(8,128)S(1)}, f32[8,768]{1,0:T(8,128)S(1)}, bf16[4,128,768]{2,1,0:T(8,128)(2,1)S(1)}) custom-call(f32[128,768]{1,0:T(8,128)S(1)} %get-tuple-element.210.x_ref, f32[16,768]{1,0:T(8,128)S(1)} %fusion.21.vec_ref, bf16[3,128,768]{2,1,0:T(8,128)(2,1)S(1)} %copy-done.9, f32[128,768]{1,0:T(8,128)S(1)} %get-tuple-element.236.dx_ref, ...), custom_call_target="tpu_custom_call" | custom-call | flops 1000 | bytes 1000 | tf_op jit(solution)/shard_map/pallas_call | solution.py:462
  290.4 6.7 %shard_map.435 = (bf16[192,3072]{1,0:T(8,128)(2,1)S(1)}, bf16[192,3072]{1,0:T(8,128)(2,1)S(1)}, bf16[192,3072]{1,0:T(8,128)(2,1)S(1)}, bf16[192,3072]{1,0:T(8,128)(2,1)S(1)}) custom-call(bf16[2,384,768]{2,1,0:T(8,128)(2,1)S(1)} %fusion.1.order_ref, bf16[2,128,768]{2,1,0:T(8,128)(2,1)S(1)} %get-tuple-element.253.s_ref, bf16[2,128,768]{2,1,0:T(8,128)(2,1)S(1)} %copy-done.11, ...), custom_call_target="tpu_custom_call" | custom-call | flops 1000 | bytes 1000 | tf_op jit(solution)/shard_map/pallas_call | solution.py:462
  301.3 6.8 %shard_map.436 = (f32[128,768]{1,0:T(8,128)S(1)}, f32[8,768]{1,0:T(8,128)S(1)}, bf16[5,128,768]{2,1,0:T(8,128)(2,1)S(1)}) custom-call(f32[128,768]{1,0:T(8,128)S(1)} %get-tuple-element.209.x_ref, f32[16,768]{1,0:T(8,128)S(1)} %fusion.21.vec_ref, f32[128,768]{1,0:T(8,128)S(1)} %get-tuple-element.265.dx_ref, ...), custom_call_target="tpu_custom_call" | custom-call | flops 1000 | bytes 1000 | tf_op jit(solution)/shard_map/pallas_call | solution.py:462
  308.1 29.9 %collective-permute-done.13 = bf16[96,3072]{1,0:T(8,128)(2,1)S(1)} collective-permute-done((bf16[96,3072]{1,0:T(8,128)(2,1)S(1)}, bf16[96,3072]{1,0:T(8,128)(2,1)S(1)}, u32[]{:S(2)}, u32[]{:S(2)}) %collective-permute-start.13) | collective-permute-done | bytes 589856 | tf_op jit(solution)/shard_map/ppermute | solution.py:35
  339.3 4.5 shard_map.437
  348.0 10.4 %shard_map.438 = (f32[128,768]{1,0:T(8,128)S(1)}, f32[8,768]{1,0:T(8,128)}, bf16[5,128,768]{2,1,0:T(8,128)(2,1)S(1)}) custom-call(bf16[128,768]{1,0:T(8,128)(2,1)S(1)} %bitcast.42, f32[16,768]{1,0:T(8,128)S(1)} %fusion.21.vec_ref, bf16[3,128,768]{2,1,0:T(8,128)(2,1)S(1)} %copy-done.7, f32[128,768]{1,0:T(8,128)S(1)} %get-tuple-element.294.dx_ref, ...), custom_call_target="tpu_custom_call" | custom-call | flops 1000 | bytes 1000 | tf_op jit(solution)/shard_map/pallas_call | solution.py:462
  358.4 25.1 %collective-permute-done.16 = bf16[96,3072]{1,0:T(8,128)(2,1)S(1)} collective-permute-done((bf16[96,3072]{1,0:T(8,128)(2,1)S(1)}, bf16[96,3072]{1,0:T(8,128)(2,1)S(1)}, u32[]{:S(2)}, u32[]{:S(2)}) %collective-permute-start.16) | collective-permute-done | bytes 589856 | tf_op jit(solution)/shard_map/ppermute | solution.py:35
  387.6 5.7 %convolution_convert_fusion.1 = bf16[1152,768]{1,0:T(8,128)(2,1)} fusion(bf16[1152,1536]{1,0:T(8,128)(2,1)S(1)} %get-tuple-element.317.dkv_ref, bf16[768,21632]{1,0:T(8,128)(2,1)} %all-gather.2.cloned.1.call-done.w_ref.up_ref.down_ref), kind=kOutput, calls=%fused_computation.2 | convolution fusion | flops 2718793728 | bytes 7667712 | tf_op jit(solution)/shard_map/dot_general | solution.py:112
  399.1 7.1 %collective-permute-done.21 = bf16[48,6144]{1,0:T(8,128)(2,1)S(1)} collective-permute-done((bf16[48,6144]{1,0:T(8,128)(2,1)S(1)}, bf16[48,6144]{1,0:T(8,128)(2,1)S(1)}, u32[]{:S(2)}, u32[]{:S(2)}) %collective-permute-start.21) | collective-permute-done | bytes 589856 | tf_op jit(solution)/shard_map/ppermute | solution.py:35
  412.6 6.7 %collective-permute-done.22 = bf16[24,6144]{1,0:T(8,128)(2,1)S(1)} collective-permute-done((bf16[24,6144]{1,0:T(8,128)(2,1)S(1)}, bf16[24,6144]{1,0:T(8,128)(2,1)S(1)}, u32[]{:S(2)}, u32[]{:S(2)}) %collective-permute-start.22) | collective-permute-done | bytes 294944 | tf_op jit(solution)/shard_map/ppermute | solution.py:35
  424.1 10.1 %collective-permute-done.23 = bf16[48,6144]{1,0:T(8,128)(2,1)} collective-permute-done((bf16[48,6144]{1,0:T(8,128)(2,1)}, bf16[48,6144]{1,0:T(8,128)(2,1)}, u32[]{:S(2)}, u32[]{:S(2)}) %collective-permute-start.23) | collective-permute-done | bytes 589856 | tf_op jit(solution)/shard_map/ppermute | solution.py:35
  439.6 10.2 %collective-permute-done.26 = bf16[24,6144]{1,0:T(8,128)(2,1)S(1)} collective-permute-done((bf16[24,6144]{1,0:T(8,128)(2,1)S(1)}, bf16[24,6144]{1,0:T(8,128)(2,1)S(1)}, u32[]{:S(2)}, u32[]{:S(2)}) %collective-permute-start.26) | collective-permute-done | bytes 294944 | tf_op jit(solution)/shard_map/ppermute | solution.py:35
  457.2 13.2 %collective-permute-done.31 = bf16[48,6144]{1,0:T(8,128)(2,1)S(1)} collective-permute-done((bf16[48,6144]{1,0:T(8,128)(2,1)S(1)}, bf16[48,6144]{1,0:T(8,128)(2,1)S(1)}, u32[]{:S(2)}, u32[]{:S(2)}) %collective-permute-start.31) | collective-permute-done | bytes 589856 | tf_op jit(solution)/shard_map/ppermute | solution.py:35
  470.4 5.6 %collective-permute-done.32 = bf16[48,3200]{1,0:T(8,128)(2,1)S(1)} collective-permute-done((bf16[48,3200]{1,0:T(8,128)(2,1)S(1)}, bf16[48,3200]{1,0:T(8,128)(2,1)S(1)}, u32[]{:S(2)}, u32[]{:S(2)}) %collective-permute-start.32) | collective-permute-done | bytes 307232 | tf_op jit(solution)/shard_map/ppermute | solution.py:35
  480.4 11.4 %collective-permute-done.33 = bf16[24,3200]{1,0:T(8,128)(2,1)S(1)} collective-permute-done((bf16[24,3200]{1,0:T(8,128)(2,1)S(1)}, bf16[24,3200]{1,0:T(8,128)(2,1)S(1)}, u32[]{:S(2)}, u32[]{:S(2)}) %collective-permute-start.33) | collective-permute-done | bytes 153632 | tf_op jit(solution)/shard_map/ppermute | solution.py:35
  (184 shorter events, 86.2 us)
Async XLA Ops:
  7.2 202.0 %all-gather.2.cloned.1.call-start = ((), (), s32[]{:S(2)}) async-start(), calls=%async_computation | async-start | bytes 34265088 | tf_op jit(solution)/shard_map/all_gather | solution.py:655
  221.5 18.2 %collective-permute-start.1 = (bf16[5,128,768]{2,1,0:T(8,128)(2,1)S(1)}, bf16[5,128,768]{2,1,0:T(8,128)(2,1)S(1)}, u32[]{:S(2)}, u32[]{:S(2)}) collective-permute-start(bf16[5,128,768]{2,1,0:T(8,128)(2,1)S(1)} %get-tuple-element.286.b_ref.g_ref), channel_id=1, source_target_pairs={{0,2},{1,3},{2,0},{3,1},{4,6},{5,7},{6,4},{7,5},{8,10},{9,11},{10,... | collective-permute-start | bytes 2949128 | tf_op jit(solution)/shard_map/ppermute | solution.py:35
  221.9 17.9 %collective-permute-start = (bf16[2,128,768]{2,1,0:T(8,128)(2,1)S(1)}, bf16[2,128,768]{2,1,0:T(8,128)(2,1)S(1)}, u32[]{:S(2)}, u32[]{:S(2)}) collective-permute-start(bf16[2,128,768]{2,1,0:T(8,128)(2,1)S(1)} %get-tuple-element.328.s_ref), channel_id=1, source_target_pairs={{0,2},{1,3},{2,0},{3,1},{4,6},{5,7},{6,4},{7,5},{8,10},{9,11},{10,... | collective-permute-start | bytes 1179656 | tf_op jit(solution)/shard_map/ppermute | solution.py:35
  258.5 28.4 %collective-permute-start.6 = (bf16[192,3072]{1,0:T(8,128)(2,1)}, bf16[192,3072]{1,0:T(8,128)(2,1)S(1)}, u32[]{:S(2)}, u32[]{:S(2)}) collective-permute-start(bf16[192,3072]{1,0:T(8,128)(2,1)} %get-tuple-element.240), channel_id=1, source_target_pairs={{0,4},{1,5},{2,6},{3,7},{4,0},{5,1},{6,2},{7,3},{8,12},{9,13},{10,... | collective-permute-start | bytes 3538952 | tf_op jit(solution)/shard_map/ppermute | solution.py:35
  259.9 28.1 %collective-permute-start.7 = (bf16[192,3072]{1,0:T(8,128)(2,1)}, bf16[192,3072]{1,0:T(8,128)(2,1)S(1)}, u32[]{:S(2)}, u32[]{:S(2)}) collective-permute-start(bf16[192,3072]{1,0:T(8,128)(2,1)} %get-tuple-element.241), channel_id=1, source_target_pairs={{0,1},{1,0},{2,3},{3,2},{4,5},{5,4},{6,7},{7,6},{8,9},{9,8},{10,11... | collective-permute-start | bytes 3538952 | tf_op jit(solution)/shard_map/ppermute | solution.py:35
  271.1 18.5 %collective-permute-start.9 = (bf16[2,128,768]{2,1,0:T(8,128)(2,1)S(1)}, bf16[2,128,768]{2,1,0:T(8,128)(2,1)S(1)}, u32[]{:S(2)}, u32[]{:S(2)}) collective-permute-start(bf16[2,128,768]{2,1,0:T(8,128)(2,1)S(1)} %get-tuple-element.259.refs_2_), channel_id=1, source_target_pairs={{0,2},{1,3},{2,0},{3,1},{4,6},{5,7},{6,4},{7,5},{8,10},{9,11},{10,... | collective-permute-start | bytes 1179656 | tf_op jit(solution)/shard_map/ppermute | solution.py:35
  297.1 40.9 %collective-permute-start.11 = (bf16[192,3072]{1,0:T(8,128)(2,1)S(1)}, bf16[192,3072]{1,0:T(8,128)(2,1)S(1)}, u32[]{:S(2)}, u32[]{:S(2)}) collective-permute-start(bf16[192,3072]{1,0:T(8,128)(2,1)S(1)} %get-tuple-element.270), channel_id=1, source_target_pairs={{0,4},{1,5},{2,6},{3,7},{4,0},{5,1},{6,2},{7,3},{8,12},{9,13},{10,... | collective-permute-start | bytes 3538952 | tf_op jit(solution)/shard_map/ppermute | solution.py:35
  297.8 40.2 %collective-permute-start.12 = (bf16[192,3072]{1,0:T(8,128)(2,1)S(1)}, bf16[192,3072]{1,0:T(8,128)(2,1)S(1)}, u32[]{:S(2)}, u32[]{:S(2)}) collective-permute-start(bf16[192,3072]{1,0:T(8,128)(2,1)S(1)} %get-tuple-element.271), channel_id=1, source_target_pairs={{0,1},{1,0},{2,3},{3,2},{4,5},{5,4},{6,7},{7,6},{8,9},{9,8},{10,11... | collective-permute-start | bytes 3538952 | tf_op jit(solution)/shard_map/ppermute | solution.py:35
  299.3 38.8 %collective-permute-start.13 = (bf16[96,3072]{1,0:T(8,128)(2,1)S(1)}, bf16[96,3072]{1,0:T(8,128)(2,1)S(1)}, u32[]{:S(2)}, u32[]{:S(2)}) collective-permute-start(bf16[96,3072]{1,0:T(8,128)(2,1)S(1)} %copy-done.24), channel_id=1, source_target_pairs={{0,1},{1,0},{2,3},{3,2},{4,5},{5,4},{6,7},{7,6},{8,9},{9,8},{10,11... | collective-permute-start | bytes 1769480 | tf_op jit(solution)/shard_map/ppermute | solution.py:35
  299.8 38.2 %collective-permute-start.14 = (bf16[96,3072]{1,0:T(8,128)(2,1)S(1)}, bf16[96,3072]{1,0:T(8,128)(2,1)S(1)}, u32[]{:S(2)}, u32[]{:S(2)}) collective-permute-start(bf16[96,3072]{1,0:T(8,128)(2,1)S(1)} %get-tuple-element.273), channel_id=1, source_target_pairs={{0,4},{1,5},{2,6},{3,7},{4,0},{5,1},{6,2},{7,3},{8,12},{9,13},{10,... | collective-permute-start | bytes 1769480 | tf_op jit(solution)/shard_map/ppermute | solution.py:35
  308.0 31.3 %collective-permute-start.15 = (bf16[5,128,768]{2,1,0:T(8,128)(2,1)S(1)}, bf16[5,128,768]{2,1,0:T(8,128)(2,1)S(1)}, u32[]{:S(2)}, u32[]{:S(2)}) collective-permute-start(bf16[5,128,768]{2,1,0:T(8,128)(2,1)S(1)} %get-tuple-element.288.z_ref.u_ref), channel_id=1, source_target_pairs={{0,2},{1,3},{2,0},{3,1},{4,6},{5,7},{6,4},{7,5},{8,10},{9,11},{10,... | collective-permute-start | bytes 2949128 | tf_op jit(solution)/shard_map/ppermute | solution.py:35
  343.8 39.7 %collective-permute-start.18 = (bf16[192,3072]{1,0:T(8,128)(2,1)S(1)}, bf16[192,3072]{1,0:T(8,128)(2,1)S(1)}, u32[]{:S(2)}, u32[]{:S(2)}) collective-permute-start(bf16[192,3072]{1,0:T(8,128)(2,1)S(1)} %get-tuple-element.304), channel_id=1, source_target_pairs={{0,4},{1,5},{2,6},{3,7},{4,0},{5,1},{6,2},{7,3},{8,12},{9,13},{10,... | collective-permute-start | bytes 3538952 | tf_op jit(solution)/shard_map/ppermute | solution.py:35
  344.4 39.1 %collective-permute-start.19 = (bf16[192,3072]{1,0:T(8,128)(2,1)S(1)}, bf16[192,3072]{1,0:T(8,128)(2,1)S(1)}, u32[]{:S(2)}, u32[]{:S(2)}) collective-permute-start(bf16[192,3072]{1,0:T(8,128)(2,1)S(1)} %get-tuple-element.305), channel_id=1, source_target_pairs={{0,1},{1,0},{2,3},{3,2},{4,5},{5,4},{6,7},{7,6},{8,9},{9,8},{10,11... | collective-permute-start | bytes 3538952 | tf_op jit(solution)/shard_map/ppermute | solution.py:35
  345.8 37.7 %collective-permute-start.16 = (bf16[96,3072]{1,0:T(8,128)(2,1)S(1)}, bf16[96,3072]{1,0:T(8,128)(2,1)S(1)}, u32[]{:S(2)}, u32[]{:S(2)}) collective-permute-start(bf16[96,3072]{1,0:T(8,128)(2,1)S(1)} %get-tuple-element.300), channel_id=1, source_target_pairs={{0,1},{1,0},{2,3},{3,2},{4,5},{5,4},{6,7},{7,6},{8,9},{9,8},{10,11... | collective-permute-start | bytes 1769480 | tf_op jit(solution)/shard_map/ppermute | solution.py:35
  346.5 37.0 %collective-permute-start.17 = (bf16[96,3072]{1,0:T(8,128)(2,1)S(1)}, bf16[96,3072]{1,0:T(8,128)(2,1)S(1)}, u32[]{:S(2)}, u32[]{:S(2)}) collective-permute-start(bf16[96,3072]{1,0:T(8,128)(2,1)S(1)} %get-tuple-element.301), channel_id=1, source_target_pairs={{0,4},{1,5},{2,6},{3,7},{4,0},{5,1},{6,2},{7,3},{8,12},{9,13},{10,... | collective-permute-start | bytes 1769480 | tf_op jit(solution)/shard_map/ppermute | solution.py:35
  358.4 34.9 %collective-permute-start.20 = (bf16[5,128,768]{2,1,0:T(8,128)(2,1)S(1)}, bf16[5,128,768]{2,1,0:T(8,128)(2,1)S(1)}, u32[]{:S(2)}, u32[]{:S(2)}) collective-permute-start(bf16[5,128,768]{2,1,0:T(8,128)(2,1)S(1)} %get-tuple-element.330.sd_ref), channel_id=1, source_target_pairs={{0,2},{1,3},{2,0},{3,1},{4,6},{5,7},{6,4},{7,5},{8,10},{9,11},{10,... | collective-permute-start | bytes 2949128 | tf_op jit(solution)/shard_map/ppermute | solution.py:35
  408.5 26.9 %collective-permute-start.24 = (bf16[192,1536]{1,0:T(8,128)(2,1)S(1)}, bf16[192,1536]{1,0:T(8,128)(2,1)}, u32[]{:S(2)}, u32[]{:S(2)}) collective-permute-start(bf16[192,1536]{1,0:T(8,128)(2,1)S(1)} %get-tuple-element.351), channel_id=1, source_target_pairs={{0,4},{1,5},{2,6},{3,7},{4,0},{5,1},{6,2},{7,3},{8,12},{9,13},{10,... | collective-permute-start | bytes 1769480 | tf_op jit(solution)/shard_map/ppermute | solution.py:35
  409.9 41.0 %collective-permute-start.27 = (bf16[96,3072]{1,0:T(8,128)(2,1)}, bf16[96,3072]{1,0:T(8,128)(2,1)}, u32[]{:S(2)}, u32[]{:S(2)}) collective-permute-start(bf16[96,3072]{1,0:T(8,128)(2,1)} %get-tuple-element.361), channel_id=1, source_target_pairs={{0,1},{1,0},{2,3},{3,2},{4,5},{5,4},{6,7},{7,6},{8,9},{9,8},{10,11... | collective-permute-start | bytes 1769480 | tf_op jit(solution)/shard_map/ppermute | solution.py:35
  410.3 40.5 %collective-permute-start.28 = (bf16[96,3072]{1,0:T(8,128)(2,1)}, bf16[96,3072]{1,0:T(8,128)(2,1)}, u32[]{:S(2)}, u32[]{:S(2)}) collective-permute-start(bf16[96,3072]{1,0:T(8,128)(2,1)} %get-tuple-element.362), channel_id=1, source_target_pairs={{0,4},{1,5},{2,6},{3,7},{4,0},{5,1},{6,2},{7,3},{8,12},{9,13},{10,... | collective-permute-start | bytes 1769480 | tf_op jit(solution)/shard_map/ppermute | solution.py:35
  411.8 23.6 %collective-permute-start.25 = (bf16[192,1664]{1,0:T(8,128)(2,1)}, bf16[192,1664]{1,0:T(8,128)(2,1)}, u32[]{:S(2)}, u32[]{:S(2)}) collective-permute-start(bf16[192,1664]{1,0:T(8,128)(2,1)} %pad_maximum_fusion), channel_id=1, source_target_pairs={{0,1},{1,0},{2,3},{3,2},{4,5},{5,4},{6,7},{7,6},{8,9},{9,8},{10,11... | collective-permute-start | bytes 1916936 | tf_op jit(solution)/shard_map/ppermute | solution.py:35
  437.9 17.0 %collective-permute-start.29 = (bf16[96,1536]{1,0:T(8,128)(2,1)S(1)}, bf16[96,1536]{1,0:T(8,128)(2,1)S(1)}, u32[]{:S(2)}, u32[]{:S(2)}) collective-permute-start(bf16[96,1536]{1,0:T(8,128)(2,1)S(1)} %get-tuple-element.369), channel_id=1, source_target_pairs={{0,1},{1,0},{2,3},{3,2},{4,5},{5,4},{6,7},{7,6},{8,9},{9,8},{10,11... | collective-permute-start | bytes 884744 | tf_op jit(solution)/shard_map/ppermute | solution.py:35
  454.2 16.2 %collective-permute-start.31 = (bf16[48,6144]{1,0:T(8,128)(2,1)S(1)}, bf16[48,6144]{1,0:T(8,128)(2,1)S(1)}, u32[]{:S(2)}, u32[]{:S(2)}) collective-permute-start(bf16[48,6144]{1,0:T(8,128)(2,1)S(1)} %get-tuple-element.377), channel_id=1, source_target_pairs={{0,8},{1,9},{2,10},{3,11},{4,12},{5,13},{6,14},{7,15},{8,0},{9,1},... | collective-permute-start | bytes 1769480 | tf_op jit(solution)/shard_map/ppermute | solution.py:35
  455.1 20.9 %collective-permute-start.32 = (bf16[48,3200]{1,0:T(8,128)(2,1)S(1)}, bf16[48,3200]{1,0:T(8,128)(2,1)S(1)}, u32[]{:S(2)}, u32[]{:S(2)}) collective-permute-start(bf16[48,3200]{1,0:T(8,128)(2,1)S(1)} %get-tuple-element.382), channel_id=1, source_target_pairs={{0,8},{1,9},{2,10},{3,11},{4,12},{5,13},{6,14},{7,15},{8,0},{9,1},... | collective-permute-start | bytes 921608 | tf_op jit(solution)/shard_map/ppermute | solution.py:35
  477.5 20.5 %collective-permute-start.34 = (bf16[24,6144]{1,0:T(8,128)(2,1)S(1)}, bf16[24,6144]{1,0:T(8,128)(2,1)S(1)}, u32[]{:S(2)}, u32[]{:S(2)}) collective-permute-start(bf16[24,6144]{1,0:T(8,128)(2,1)S(1)} %add_convert_fusion.22), channel_id=1, source_target_pairs={{0,16},{1,17},{2,18},{3,19},{4,20},{5,21},{6,22},{7,23},{8,24},{9,... | collective-permute-start | bytes 884744 | tf_op jit(solution)/shard_map/ppermute | solution.py:35
  (37 other events, 462.0 us)
Sparse Core Ops, SparseCore 0:
  13.2 195.9 all-gather.1

commit v6 on v5

--- a/solution.py
+++ b/solution.py
@@ -709,21 +709,19 @@
     dx = go_on(dx, start=[s_ma])
     dx, v_uf, p = net.feed_backward(x0a, (k_uf,), dx, 4, 2)
     p = pairs(p)
-    dx = go_on(dx, [s_ma, s_mf])
+    dx = go_on(dx, [s_ma], [s_ma])
     dx, (p,) = tie(dx, p)
     s_uf = Sum(place, net.feed_grads(f_uf, p))
-    dx = go_on(dx, start=[s_uf, s_ma])
+    dx = need(dx, s_uf)
+    dx = go_on(dx, [s_mf], [s_uf])
     v = [g[:2] for g in (v_uf, v_ms, v_mc, v_mf)]
     v = jnp.pad(jnp.concatenate(v, axis=0), ((2, 6), (0, 0)))
     dx, _v, p = net.self_backward(x0, k_us, dx, 0, 0, (v,))
     p = pairs(p)
-    dx = go_on(dx, [s_ma, s_uf])
+    dx = go_on(dx, [s_ma], [s_mf])
     dx, (dkv,) = tie(dx, dkv)
     denc = nt(dkv, w_pair).astype(bf16)
-    dx, (denc,) = tie(dx, denc)
-    dx, (p,) = tie(dx, p)
-    dx = go_on(dx, start=[s_mf, s_uf])
-    dx, (p,) = tie(dx, p)
+    dx, (p, denc) = tie(dx, p, denc)
     send_a, keep_a, send_b, keep_b = net.attend_grads(f_us, p)
     v = nt(order[1], plus(p[0][4], p[1][4])[:LANES]).astype(bf16)
     send_b = jnp.concatenate((send_b, v[d // 4 :]), axis=1)
@@ -731,12 +729,13 @@
     s_us = Sum(place, (send_a, keep_a, send_b, keep_b))
     dx = go_on(dx, start=[s_us])
     dx = rest(dx, s_mf)
+    dx = go_on(dx, [s_uf], [s_uf])
     dx, (r_mf,) = tie(dx, s_mf.total())
     dx = go_on(dx, start=[s_ma])
+    dx = go_on(dx, [s_us], [s_us])
     dx = rest(dx, s_ma)
-    dx = go_on(dx, [s_us], [s_us])
+    dx = go_on(dx, [s_uf], [s_uf])
     dx, (r_ma,) = tie(dx, s_ma.total())
-    dx = go_on(dx, [s_uf], [s_uf])
     dx = go_on(dx, [s_us], [s_us])
     dx = rest(dx, s_uf, s_us)
     r_uf, r_us = s_uf.total(), s_us.total()

time: 513 us -> 478 us (0.932)
  waiting for transfers between devices: 318 us -> 276 us
    ppermute x35, waiting for transfers between devices: 126 us -> 84.3 us  [swap(): return lax.ppermute(x, AXES, [(i, i ^ bit) for i in range(self.count)])]
  transfers between devices with their start and end apart: 36 -> 36, of which waited for: 13 -> 15; matrix products, arithmetic and copies ran while one was open for 8% -> 10% of each run, Pallas kernels for 12% -> 14%
where the time goes in v6:
time: 478 us; the launch traced here: 473 us
  waiting for transfers between devices  276 us (58%)
  Pallas kernels  101 us (21%)
  starting transfers between devices  24.7 us (5%)
  other arithmetic  21 us (4%)
  matrix products  17.9 us (4%)
  local copies, waits for them, and re-layouts  17.7 us (4%)
  between operations  15 us (3%)
    all_gather x1, waiting for transfers between devices, local(): w = lax.all_gather(shard, AXES, axis=0, tiled=True)  192 us
    pallas_call x16, Pallas kernels, call(): pl.pallas_call(kernel, out_shape=outs, grid_spec=pltpu.PrefetchScalarGrid...  101 us
    ppermute x35, waiting for transfers between devices, swap(): return lax.ppermute(x, AXES, [(i, i ^ bit) for i in range(self.count)])  84.3 us
    ppermute x35, starting transfers between devices, swap(): return lax.ppermute(x, AXES, [(i, i ^ bit) for i in range(self.count)])  24.7 us
    convert_element_type x20, other arithmetic, plus(): return (a.astype(f32) + b.astype(f32)).astype(bf16)  15.4 us
    dot_general x4, matrix products, nt(): lax.dot_general(a, b, (((1,), (1,)), ((), ())), preferred_element_type=f32)  10.1 us
  transfers between devices with their start and end apart: 36, of which 15 were waited for; matrix products, arithmetic and copies ran while one was open for 10% of the time, Pallas kernels for 14%

profile of v6, /device:TPU:0, one launch (start us, length us, event | category | flops | bytes accessed | tf_op | source)
XLA Modules:
  0.0 473.4 jit_solution(5119331267735778723)
XLA Ops:
  17.2 192.0 %all-gather.2.cloned.1.call-done.w_ref.up_ref.down_ref = bf16[768,21632]{1,0:T(8,128)(2,1)} async-done(((bf16[24,21632]{1,0:T(8,128)(2,1)}), bf16[768,21632]{1,0:T(8,128)(2,1)}) %all-gather.2.cloned.1.call-update) | async-done | bytes 33226768 | tf_op jit(solution)/shard_map/all_gather | solution.py:655
  210.3 5.1 %shard_map.425 = (f32[128,768]{1,0:T(8,128)S(1)}, bf16[2,128,768]{2,1,0:T(8,128)(2,1)S(1)}, bf16[3,128,768]{2,1,0:T(8,128)(2,1)S(1)}) custom-call(bf16[128,768]{1,0:T(8,128)(2,1)S(1)} %bitcast.41, f32[16,768]{1,0:T(8,128)S(1)} %fusion.21.vec_ref, bf16[768,21632]{1,0:T(8,128)(2,1)} %all-gather.2.cloned.1.call-done.w_ref.up_ref.down_ref), custom_call_target="tpu_custom_call" | custom-call | flops 1000 | bytes 1000 | tf_op jit(solution)/shard_map/pallas_call | solution.py:462
  215.4 6.1 %shard_map.426 = (f32[128,768]{1,0:T(8,128)S(1)}, bf16[5,128,768]{2,1,0:T(8,128)(2,1)S(1)}, f32[128,3072]{1,0:T(8,128)S(1)}) custom-call(f32[128,768]{1,0:T(8,128)S(1)} %get-tuple-element.206.x_ref, f32[16,768]{1,0:T(8,128)S(1)} %fusion.21.vec_ref, bf16[768,21632]{1,0:T(8,128)(2,1)} %all-gather.2.cloned.1.call-done.w_ref.up_ref.down_ref, ...), custom_call_target="tpu_custom_call" | custom-call | flops 1000 | bytes 1000 | tf_op jit(solution)/shard_map/pallas_call | solution.py:462
  222.1 4.9 %shard_map.427 = (f32[128,768]{1,0:T(8,128)S(1)}, bf16[2,128,768]{2,1,0:T(8,128)(2,1)S(1)}, bf16[3,128,768]{2,1,0:T(8,128)(2,1)S(1)}) custom-call(f32[128,768]{1,0:T(8,128)S(1)} %get-tuple-element.207.x_ref, f32[16,768]{1,0:T(8,128)S(1)} %fusion.21.vec_ref, bf16[768,21632]{1,0:T(8,128)(2,1)} %all-gather.2.cloned.1.call-done.w_ref.up_ref.down_ref), custom_call_target="tpu_custom_call" | custom-call | flops 1000 | bytes 1000 | tf_op jit(solution)/shard_map/pallas_call | solution.py:462
  227.3 4.8 %fusion.kv_ref = bf16[1152,1536]{1,0:T(8,128)(2,1)S(1)} fusion(bf16[1152,768]{1,0:T(8,128)(2,1)S(1)} %bitcast.40, bf16[768,21632]{1,0:T(8,128)(2,1)} %all-gather.2.cloned.1.call-done.w_ref.up_ref.down_ref), kind=kOutput, calls=%fused_computation.1 | convolution fusion | flops 2719678464 | bytes 7667712 | tf_op jit(solution)/shard_map/dot_general | solution.py:108
  232.2 7.5 %shard_map.428 = (f32[128,768]{1,0:T(8,128)S(1)}, bf16[2,128,768]{2,1,0:T(8,128)(2,1)S(1)}, bf16[128,768]{1,0:T(8,128)(2,1)S(1)}) custom-call(s32[2]{0:T(128)S(1)} %copy-done.21, f32[128,768]{1,0:T(8,128)S(1)} %get-tuple-element.208.x_ref, f32[16,768]{1,0:T(8,128)S(1)} %fusion.21.vec_ref, bf16[1152,1536]{1,0:T(8,128)(2,1)S(1)} %fusion.kv_ref, ...), custom_call_target="tpu_custom_call" | custom-call | flops 1000 | bytes 1000 | tf_op jit(solution)/shard_map/pallas_call | solution.py:462
  239.7 7.6 %shard_map.429 = (f32[128,768]{1,0:T(8,128)S(1)}, f32[8,768]{1,0:T(8,128)S(1)}, bf16[5,128,768]{2,1,0:T(8,128)(2,1)S(1)}, bf16[5,128,768]{2,1,0:T(8,128)(2,1)S(1)}) custom-call(f32[128,768]{1,0:T(8,128)S(1)} %get-tuple-element.213.x_ref, f32[16,768]{1,0:T(8,128)S(1)} %fusion.21.vec_ref, bf16[128,768]{1,0:T(8,128)(2,1)S(1)} %bitcast.43, ...), custom_call_target="tpu_custom_call" | custom-call | flops 1000 | bytes 1000 | tf_op jit(solution)/shard_map/pallas_call | solution.py:462
  248.2 4.4 shard_map.430
  253.4 5.1 %shard_map.431 = (bf16[192,3072]{1,0:T(8,128)(2,1)}, bf16[192,3072]{1,0:T(8,128)(2,1)S(1)}, bf16[192,3072]{1,0:T(8,128)(2,1)}, bf16[192,3072]{1,0:T(8,128)(2,1)S(1)}) custom-call(bf16[2,384,768]{2,1,0:T(8,128)(2,1)S(1)} %fusion.1.order_ref, bf16[5,128,768]{2,1,0:T(8,128)(2,1)S(1)} %get-tuple-element.215.g_ref.b_ref, ...), custom_call_target="tpu_custom_call" | custom-call | flops 1000 | bytes 1000 | tf_op jit(solution)/shard_map/pallas_call | solution.py:462
  260.5 10.6 %shard_map.432 = (f32[128,768]{1,0:T(8,128)S(1)}, f32[8,768]{1,0:T(8,128)S(1)}, bf16[2,128,768]{2,1,0:T(8,128)(2,1)S(1)}, bf16[1152,1536]{1,0:T(8,128)(2,1)S(1)}) custom-call(s32[2]{0:T(128)S(1)} %copy-done.21, f32[128,768]{1,0:T(8,128)S(1)} %get-tuple-element.208.x_ref, f32[16,768]{1,0:T(8,128)S(1)} %fusion.21.vec_ref, ...), custom_call_target="tpu_custom_call" | custom-call | flops 1000 | bytes 1000 | tf_op jit(solution)/shard_map/pallas_call | solution.py:462
  271.2 3.8 shard_map.433
  275.1 9.9 %shard_map.434 = (f32[128,768]{1,0:T(8,128)S(1)}, f32[8,768]{1,0:T(8,128)S(1)}, bf16[4,128,768]{2,1,0:T(8,128)(2,1)S(1)}) custom-call(f32[128,768]{1,0:T(8,128)S(1)} %get-tuple-element.207.x_ref, f32[16,768]{1,0:T(8,128)S(1)} %fusion.21.vec_ref, bf16[3,128,768]{2,1,0:T(8,128)(2,1)S(1)} %copy-done.9, f32[128,768]{1,0:T(8,128)S(1)} %get-tuple-element.233.dx_ref, ...), custom_call_target="tpu_custom_call" | custom-call | flops 1000 | bytes 1000 | tf_op jit(solution)/shard_map/pallas_call | solution.py:462
  293.3 6.8 %shard_map.435 = (bf16[192,3072]{1,0:T(8,128)(2,1)S(1)}, bf16[192,3072]{1,0:T(8,128)(2,1)S(1)}, bf16[192,3072]{1,0:T(8,128)(2,1)S(1)}, bf16[192,3072]{1,0:T(8,128)(2,1)S(1)}) custom-call(bf16[2,384,768]{2,1,0:T(8,128)(2,1)S(1)} %fusion.1.order_ref, bf16[2,128,768]{2,1,0:T(8,128)(2,1)S(1)} %get-tuple-element.250.s_ref, bf16[2,128,768]{2,1,0:T(8,128)(2,1)S(1)} %copy-done.11, ...), custom_call_target="tpu_custom_call" | custom-call | flops 1000 | bytes 1000 | tf_op jit(solution)/shard_map/pallas_call | solution.py:462
  304.9 6.8 %shard_map.436 = (f32[128,768]{1,0:T(8,128)S(1)}, f32[8,768]{1,0:T(8,128)S(1)}, bf16[5,128,768]{2,1,0:T(8,128)(2,1)S(1)}) custom-call(f32[128,768]{1,0:T(8,128)S(1)} %get-tuple-element.206.x_ref, f32[16,768]{1,0:T(8,128)S(1)} %fusion.21.vec_ref, f32[128,768]{1,0:T(8,128)S(1)} %get-tuple-element.262.dx_ref, ...), custom_call_target="tpu_custom_call" | custom-call | flops 1000 | bytes 1000 | tf_op jit(solution)/shard_map/pallas_call | solution.py:462
  311.7 17.3 %collective-permute-done.11 = bf16[192,3072]{1,0:T(8,128)(2,1)S(1)} collective-permute-done((bf16[192,3072]{1,0:T(8,128)(2,1)S(1)}, bf16[192,3072]{1,0:T(8,128)(2,1)S(1)}, u32[]{:S(2)}, u32[]{:S(2)}) %collective-permute-start.11) | collective-permute-done | bytes 1179680 | tf_op jit(solution)/shard_map/ppermute | solution.py:35
  332.6 4.5 shard_map.437
  337.1 5.3 %collective-permute-done.14 = bf16[96,3072]{1,0:T(8,128)(2,1)S(1)} collective-permute-done((bf16[96,3072]{1,0:T(8,128)(2,1)}, bf16[96,3072]{1,0:T(8,128)(2,1)S(1)}, u32[]{:S(2)}, u32[]{:S(2)}) %collective-permute-start.14) | collective-permute-done | bytes 589856 | tf_op jit(solution)/shard_map/ppermute | solution.py:35
  344.8 10.4 %shard_map.438 = (f32[128,768]{1,0:T(8,128)S(1)}, f32[8,768]{1,0:T(8,128)}, bf16[5,128,768]{2,1,0:T(8,128)(2,1)S(1)}) custom-call(bf16[128,768]{1,0:T(8,128)(2,1)S(1)} %bitcast.42, f32[16,768]{1,0:T(8,128)S(1)} %fusion.21.vec_ref, bf16[3,128,768]{2,1,0:T(8,128)(2,1)S(1)} %copy-done.7, f32[128,768]{1,0:T(8,128)S(1)} %get-tuple-element.293.dx_ref, ...), custom_call_target="tpu_custom_call" | custom-call | flops 1000 | bytes 1000 | tf_op jit(solution)/shard_map/pallas_call | solution.py:462
  358.6 5.7 %convolution_convert_fusion.1 = bf16[1152,768]{1,0:T(8,128)(2,1)} fusion(bf16[1152,1536]{1,0:T(8,128)(2,1)S(1)} %get-tuple-element.310.dkv_ref, bf16[768,21632]{1,0:T(8,128)(2,1)} %all-gather.2.cloned.1.call-done.w_ref.up_ref.down_ref), kind=kOutput, calls=%fused_computation.2 | convolution fusion | flops 2718793728 | bytes 7667712 | tf_op jit(solution)/shard_map/dot_general | solution.py:112
  375.4 8.5 %collective-permute-done.20 = bf16[192,3072]{1,0:T(8,128)(2,1)S(1)} collective-permute-done((bf16[192,3072]{1,0:T(8,128)(2,1)S(1)}, bf16[192,3072]{1,0:T(8,128)(2,1)S(1)}, u32[]{:S(2)}, u32[]{:S(2)}) %collective-permute-start.20) | collective-permute-done | bytes 1179680 | tf_op jit(solution)/shard_map/ppermute | solution.py:35
  403.9 10.1 %collective-permute-done.25 = bf16[48,6144]{1,0:T(8,128)(2,1)S(1)} collective-permute-done((bf16[48,6144]{1,0:T(8,128)(2,1)}, bf16[48,6144]{1,0:T(8,128)(2,1)S(1)}, u32[]{:S(2)}, u32[]{:S(2)}) %collective-permute-start.25) | collective-permute-done | bytes 589856 | tf_op jit(solution)/shard_map/ppermute | solution.py:35
  417.8 10.9 %collective-permute-done.28 = bf16[24,6144]{1,0:T(8,128)(2,1)S(1)} collective-permute-done((bf16[24,6144]{1,0:T(8,128)(2,1)S(1)}, bf16[24,6144]{1,0:T(8,128)(2,1)S(1)}, u32[]{:S(2)}, u32[]{:S(2)}) %collective-permute-start.28) | collective-permute-done | bytes 294944 | tf_op jit(solution)/shard_map/ppermute | solution.py:35
  430.5 8.9 %collective-permute-done.31 = bf16[48,6144]{1,0:T(8,128)(2,1)S(1)} collective-permute-done((bf16[48,6144]{1,0:T(8,128)(2,1)S(1)}, bf16[48,6144]{1,0:T(8,128)(2,1)S(1)}, u32[]{:S(2)}, u32[]{:S(2)}) %collective-permute-start.31) | collective-permute-done | bytes 589856 | tf_op jit(solution)/shard_map/ppermute | solution.py:35
  447.6 10.5 %collective-permute-done.33 = bf16[24,3200]{1,0:T(8,128)(2,1)S(1)} collective-permute-done((bf16[24,3200]{1,0:T(8,128)(2,1)S(1)}, bf16[24,3200]{1,0:T(8,128)(2,1)S(1)}, u32[]{:S(2)}, u32[]{:S(2)}) %collective-permute-start.33) | collective-permute-done | bytes 153632 | tf_op jit(solution)/shard_map/ppermute | solution.py:35
  (186 shorter events, 91.0 us)
Async XLA Ops:
  7.2 202.0 %all-gather.2.cloned.1.call-start = ((), (), s32[]{:S(2)}) async-start(), calls=%async_computation | async-start | bytes 34265088 | tf_op jit(solution)/shard_map/all_gather | solution.py:655
  221.5 18.2 %collective-permute-start.1 = (bf16[5,128,768]{2,1,0:T(8,128)(2,1)S(1)}, bf16[5,128,768]{2,1,0:T(8,128)(2,1)S(1)}, u32[]{:S(2)}, u32[]{:S(2)}) collective-permute-start(bf16[5,128,768]{2,1,0:T(8,128)(2,1)S(1)} %get-tuple-element.277.b_ref.g_ref), channel_id=1, source_target_pairs={{0,2},{1,3},{2,0},{3,1},{4,6},{5,7},{6,4},{7,5},{8,10},{9,11},{10,... | collective-permute-start | bytes 2949128 | tf_op jit(solution)/shard_map/ppermute | solution.py:35
  221.9 17.8 %collective-permute-start = (bf16[2,128,768]{2,1,0:T(8,128)(2,1)S(1)}, bf16[2,128,768]{2,1,0:T(8,128)(2,1)S(1)}, u32[]{:S(2)}, u32[]{:S(2)}) collective-permute-start(bf16[2,128,768]{2,1,0:T(8,128)(2,1)S(1)} %get-tuple-element.312.s_ref), channel_id=1, source_target_pairs={{0,2},{1,3},{2,0},{3,1},{4,6},{5,7},{6,4},{7,5},{8,10},{9,11},{10,... | collective-permute-start | bytes 1179656 | tf_op jit(solution)/shard_map/ppermute | solution.py:35
  258.5 28.4 %collective-permute-start.6 = (bf16[192,3072]{1,0:T(8,128)(2,1)}, bf16[192,3072]{1,0:T(8,128)(2,1)}, u32[]{:S(2)}, u32[]{:S(2)}) collective-permute-start(bf16[192,3072]{1,0:T(8,128)(2,1)} %get-tuple-element.237), channel_id=1, source_target_pairs={{0,4},{1,5},{2,6},{3,7},{4,0},{5,1},{6,2},{7,3},{8,12},{9,13},{10,... | collective-permute-start | bytes 3538952 | tf_op jit(solution)/shard_map/ppermute | solution.py:35
  259.9 28.2 %collective-permute-start.7 = (bf16[192,3072]{1,0:T(8,128)(2,1)}, bf16[192,3072]{1,0:T(8,128)(2,1)}, u32[]{:S(2)}, u32[]{:S(2)}) collective-permute-start(bf16[192,3072]{1,0:T(8,128)(2,1)} %get-tuple-element.238), channel_id=1, source_target_pairs={{0,1},{1,0},{2,3},{3,2},{4,5},{5,4},{6,7},{7,6},{8,9},{9,8},{10,11... | collective-permute-start | bytes 3538952 | tf_op jit(solution)/shard_map/ppermute | solution.py:35
  271.1 22.2 %collective-permute-start.9 = (bf16[2,128,768]{2,1,0:T(8,128)(2,1)S(1)}, bf16[2,128,768]{2,1,0:T(8,128)(2,1)S(1)}, u32[]{:S(2)}, u32[]{:S(2)}) collective-permute-start(bf16[2,128,768]{2,1,0:T(8,128)(2,1)S(1)} %get-tuple-element.256.refs_2_), channel_id=1, source_target_pairs={{0,2},{1,3},{2,0},{3,1},{4,6},{5,7},{6,4},{7,5},{8,10},{9,11},{10,... | collective-permute-start | bytes 1179656 | tf_op jit(solution)/shard_map/ppermute | solution.py:35
  300.1 29.0 %collective-permute-start.11 = (bf16[192,3072]{1,0:T(8,128)(2,1)S(1)}, bf16[192,3072]{1,0:T(8,128)(2,1)S(1)}, u32[]{:S(2)}, u32[]{:S(2)}) collective-permute-start(bf16[192,3072]{1,0:T(8,128)(2,1)S(1)} %get-tuple-element.267), channel_id=1, source_target_pairs={{0,4},{1,5},{2,6},{3,7},{4,0},{5,1},{6,2},{7,3},{8,12},{9,13},{10,... | collective-permute-start | bytes 3538952 | tf_op jit(solution)/shard_map/ppermute | solution.py:35
  300.8 28.9 %collective-permute-start.12 = (bf16[192,3072]{1,0:T(8,128)(2,1)S(1)}, bf16[192,3072]{1,0:T(8,128)(2,1)S(1)}, u32[]{:S(2)}, u32[]{:S(2)}) collective-permute-start(bf16[192,3072]{1,0:T(8,128)(2,1)S(1)} %get-tuple-element.268), channel_id=1, source_target_pairs={{0,1},{1,0},{2,3},{3,2},{4,5},{5,4},{6,7},{7,6},{8,9},{9,8},{10,11... | collective-permute-start | bytes 3538952 | tf_op jit(solution)/shard_map/ppermute | solution.py:35
  302.8 39.5 %collective-permute-start.14 = (bf16[96,3072]{1,0:T(8,128)(2,1)}, bf16[96,3072]{1,0:T(8,128)(2,1)S(1)}, u32[]{:S(2)}, u32[]{:S(2)}) collective-permute-start(bf16[96,3072]{1,0:T(8,128)(2,1)} %get-tuple-element.284), channel_id=1, source_target_pairs={{0,1},{1,0},{2,3},{3,2},{4,5},{5,4},{6,7},{7,6},{8,9},{9,8},{10,11... | collective-permute-start | bytes 1769480 | tf_op jit(solution)/shard_map/ppermute | solution.py:35
  303.4 38.9 %collective-permute-start.15 = (bf16[96,3072]{1,0:T(8,128)(2,1)}, bf16[96,3072]{1,0:T(8,128)(2,1)}, u32[]{:S(2)}, u32[]{:S(2)}) collective-permute-start(bf16[96,3072]{1,0:T(8,128)(2,1)} %get-tuple-element.285), channel_id=1, source_target_pairs={{0,4},{1,5},{2,6},{3,7},{4,0},{5,1},{6,2},{7,3},{8,12},{9,13},{10,... | collective-permute-start | bytes 1769480 | tf_op jit(solution)/shard_map/ppermute | solution.py:35
  311.6 18.9 %collective-permute-start.13 = (bf16[5,128,768]{2,1,0:T(8,128)(2,1)S(1)}, bf16[5,128,768]{2,1,0:T(8,128)(2,1)S(1)}, u32[]{:S(2)}, u32[]{:S(2)}) collective-permute-start(bf16[5,128,768]{2,1,0:T(8,128)(2,1)S(1)} %get-tuple-element.279.z_ref.u_ref), channel_id=1, source_target_pairs={{0,2},{1,3},{2,0},{3,1},{4,6},{5,7},{6,4},{7,5},{8,10},{9,11},{10,... | collective-permute-start | bytes 2949128 | tf_op jit(solution)/shard_map/ppermute | solution.py:35
  330.5 26.7 %collective-permute-start.16 = (bf16[96,3072]{1,0:T(8,128)(2,1)S(1)}, bf16[96,3072]{1,0:T(8,128)(2,1)S(1)}, u32[]{:S(2)}, u32[]{:S(2)}) collective-permute-start(bf16[96,3072]{1,0:T(8,128)(2,1)S(1)} %get-tuple-element.299), channel_id=1, source_target_pairs={{0,1},{1,0},{2,3},{3,2},{4,5},{5,4},{6,7},{7,6},{8,9},{9,8},{10,11... | collective-permute-start | bytes 1769480 | tf_op jit(solution)/shard_map/ppermute | solution.py:35
  332.0 25.2 %collective-permute-start.17 = (bf16[96,3072]{1,0:T(8,128)(2,1)S(1)}, bf16[96,3072]{1,0:T(8,128)(2,1)S(1)}, u32[]{:S(2)}, u32[]{:S(2)}) collective-permute-start(bf16[96,3072]{1,0:T(8,128)(2,1)S(1)} %get-tuple-element.300), channel_id=1, source_target_pairs={{0,4},{1,5},{2,6},{3,7},{4,0},{5,1},{6,2},{7,3},{8,12},{9,13},{10,... | collective-permute-start | bytes 1769480 | tf_op jit(solution)/shard_map/ppermute | solution.py:35
  355.2 28.8 %collective-permute-start.20 = (bf16[192,3072]{1,0:T(8,128)(2,1)S(1)}, bf16[192,3072]{1,0:T(8,128)(2,1)S(1)}, u32[]{:S(2)}, u32[]{:S(2)}) collective-permute-start(bf16[192,3072]{1,0:T(8,128)(2,1)S(1)} %get-tuple-element.326), channel_id=1, source_target_pairs={{0,4},{1,5},{2,6},{3,7},{4,0},{5,1},{6,2},{7,3},{8,12},{9,13},{10,... | collective-permute-start | bytes 3538952 | tf_op jit(solution)/shard_map/ppermute | solution.py:35
  356.6 28.8 %collective-permute-start.21 = (bf16[192,3072]{1,0:T(8,128)(2,1)S(1)}, bf16[192,3072]{1,0:T(8,128)(2,1)S(1)}, u32[]{:S(2)}, u32[]{:S(2)}) collective-permute-start(bf16[192,3072]{1,0:T(8,128)(2,1)S(1)} %get-tuple-element.327), channel_id=1, source_target_pairs={{0,1},{1,0},{2,3},{3,2},{4,5},{5,4},{6,7},{7,6},{8,9},{9,8},{10,11... | collective-permute-start | bytes 3538952 | tf_op jit(solution)/shard_map/ppermute | solution.py:35
  370.2 29.3 %collective-permute-start.23 = (bf16[192,1536]{1,0:T(8,128)(2,1)S(1)}, bf16[192,1536]{1,0:T(8,128)(2,1)}, u32[]{:S(2)}, u32[]{:S(2)}) collective-permute-start(bf16[192,1536]{1,0:T(8,128)(2,1)S(1)} %get-tuple-element.340), channel_id=1, source_target_pairs={{0,4},{1,5},{2,6},{3,7},{4,0},{5,1},{6,2},{7,3},{8,12},{9,13},{10,... | collective-permute-start | bytes 1769480 | tf_op jit(solution)/shard_map/ppermute | solution.py:35
  371.6 27.8 %collective-permute-start.24 = (bf16[192,1664]{1,0:T(8,128)(2,1)}, bf16[192,1664]{1,0:T(8,128)(2,1)}, u32[]{:S(2)}, u32[]{:S(2)}) collective-permute-start(bf16[192,1664]{1,0:T(8,128)(2,1)} %pad_maximum_fusion), channel_id=1, source_target_pairs={{0,1},{1,0},{2,3},{3,2},{4,5},{5,4},{6,7},{7,6},{8,9},{9,8},{10,11... | collective-permute-start | bytes 1916936 | tf_op jit(solution)/shard_map/ppermute | solution.py:35
  373.9 16.1 %collective-permute-start.22 = (bf16[24,6144]{1,0:T(8,128)(2,1)S(1)}, bf16[24,6144]{1,0:T(8,128)(2,1)S(1)}, u32[]{:S(2)}, u32[]{:S(2)}) collective-permute-start(bf16[24,6144]{1,0:T(8,128)(2,1)S(1)} %add_convert_fusion.29), channel_id=1, source_target_pairs={{0,16},{1,17},{2,18},{3,19},{4,20},{5,21},{6,22},{7,23},{8,24},{9,... | collective-permute-start | bytes 884744 | tf_op jit(solution)/shard_map/ppermute | solution.py:35
  387.8 26.3 %collective-permute-start.26 = (bf16[96,3072]{1,0:T(8,128)(2,1)}, bf16[96,3072]{1,0:T(8,128)(2,1)}, u32[]{:S(2)}, u32[]{:S(2)}) collective-permute-start(bf16[96,3072]{1,0:T(8,128)(2,1)} %get-tuple-element.353), channel_id=1, source_target_pairs={{0,1},{1,0},{2,3},{3,2},{4,5},{5,4},{6,7},{7,6},{8,9},{9,8},{10,11... | collective-permute-start | bytes 1769480 | tf_op jit(solution)/shard_map/ppermute | solution.py:35
  388.5 25.7 %collective-permute-start.27 = (bf16[96,3072]{1,0:T(8,128)(2,1)}, bf16[96,3072]{1,0:T(8,128)(2,1)}, u32[]{:S(2)}, u32[]{:S(2)}) collective-permute-start(bf16[96,3072]{1,0:T(8,128)(2,1)} %get-tuple-element.354), channel_id=1, source_target_pairs={{0,4},{1,5},{2,6},{3,7},{4,0},{5,1},{6,2},{7,3},{8,12},{9,13},{10,... | collective-permute-start | bytes 1769480 | tf_op jit(solution)/shard_map/ppermute | solution.py:35
  401.9 26.9 %collective-permute-start.29 = (bf16[96,1536]{1,0:T(8,128)(2,1)S(1)}, bf16[96,1536]{1,0:T(8,128)(2,1)S(1)}, u32[]{:S(2)}, u32[]{:S(2)}) collective-permute-start(bf16[96,1536]{1,0:T(8,128)(2,1)S(1)} %get-tuple-element.363), channel_id=1, source_target_pairs={{0,1},{1,0},{2,3},{3,2},{4,5},{5,4},{6,7},{7,6},{8,9},{9,8},{10,11... | collective-permute-start | bytes 884744 | tf_op jit(solution)/shard_map/ppermute | solution.py:35
  402.6 26.2 %collective-permute-start.30 = (bf16[96,1664]{1,0:T(8,128)(2,1)S(1)}, bf16[96,1664]{1,0:T(8,128)(2,1)S(1)}, u32[]{:S(2)}, u32[]{:S(2)}) collective-permute-start(bf16[96,1664]{1,0:T(8,128)(2,1)S(1)} %get-tuple-element.364), channel_id=1, source_target_pairs={{0,4},{1,5},{2,6},{3,7},{4,0},{5,1},{6,2},{7,3},{8,12},{9,13},{10,... | collective-permute-start | bytes 958472 | tf_op jit(solution)/shard_map/ppermute | solution.py:35
  417.3 22.1 %collective-permute-start.31 = (bf16[48,6144]{1,0:T(8,128)(2,1)S(1)}, bf16[48,6144]{1,0:T(8,128)(2,1)S(1)}, u32[]{:S(2)}, u32[]{:S(2)}) collective-permute-start(bf16[48,6144]{1,0:T(8,128)(2,1)S(1)} %get-tuple-element.371), channel_id=1, source_target_pairs={{0,8},{1,9},{2,10},{3,11},{4,12},{5,13},{6,14},{7,15},{8,0},{9,1},... | collective-permute-start | bytes 1769480 | tf_op jit(solution)/shard_map/ppermute | solution.py:35
  444.0 19.3 %collective-permute-start.34 = (bf16[24,6144]{1,0:T(8,128)(2,1)S(1)}, bf16[24,6144]{1,0:T(8,128)(2,1)S(1)}, u32[]{:S(2)}, u32[]{:S(2)}) collective-permute-start(bf16[24,6144]{1,0:T(8,128)(2,1)S(1)} %add_convert_fusion.22), channel_id=1, source_target_pairs={{0,16},{1,17},{2,18},{3,19},{4,20},{5,21},{6,22},{7,23},{8,24},{9,... | collective-permute-start | bytes 884744 | tf_op jit(solution)/shard_map/ppermute | solution.py:35
  (38 other events, 473.4 us)
Sparse Core Ops, SparseCore 0:
  13.2 195.9 all-gather.1

commit v7 on v6

--- a/solution.py
+++ b/solution.py
@@ -83,6 +83,31 @@
 
     def total(self):
         return self.kept[0].astype(f32) + self.got[0].astype(f32)
+
+
+class Gather:
+    def __init__(self, place, shard):
+        self.place, self.x, self.stage = place, (shard,), 0
+
+    def swap(self):
+        outer = self.place.outer_bits
+        at = self.stage - outer
+        if at < 0:
+            bits = (8 << (outer - 1 - self.stage),)
+        else:
+            bits = ((BIT_PAIR, BIT_NEAR), (BIT_NEAR, BIT_PAIR), (BIT_CORE,) * 2)[at]
+        self.got = tuple(self.place.swap(x, bit) for x, bit in zip(self.x, bits))
+
+    def join(self):
+        self.stage += 1
+        terms = list(zip(self.x, self.got))
+        if self.stage == self.place.outer_bits:
+            (x, got), half = terms[0], self.x[0].shape[1] // 2
+            terms = [(x[:, :half], got[:, :half]), (x[:, half:], got[:, half:])]
+        self.x = tuple(jnp.concatenate(t, axis=0) for t in terms)
+
+    def halves(self):
+        return self.x[0], self.got[0], self.x[1], self.got[1]
 
 
 def tie(x, *others):
@@ -310,7 +335,15 @@
         vg_ref[1:2] = gs
 
 
-def feed_forward_kernel(row, x_ref, vec_ref, up_ref, down_ref, y_ref, f_ref, u_ref):
+def by_rows(x, order, top_ref, low_ref):
+    half = top_ref.shape[0]
+    x = nt(x, order).astype(bf16)
+    return nn(x[:, :half], top_ref[...]) + nn(x[:, half:], low_ref[...])
+
+
+def feed_forward_kernel(
+    row, x_ref, vec_ref, order_ref, up_ref, up2_ref, down_ref, down2_ref, y_ref, f_ref, u_ref
+):
     j = pl.program_id(0)
 
     @pl.when(j == 0)
@@ -319,17 +352,20 @@
         f_ref[0] = (unit * vec_ref[row : row + 1] + vec_ref[row + 1 : row + 2]).astype(bf16)
         y_ref[...] = x_ref[...]
 
-    u = nn(f_ref[0], up_ref[...])
+    u = by_rows(f_ref[0], order_ref[0], up_ref, up2_ref)
     u_ref[...] = u
     g = (0.5 * u * (1.0 + jnp.tanh(GELU_A * (u + GELU_B * u * u * u)))).astype(bf16)
     f_ref[1 + j] = g
-    y_ref[...] += nn(g, down_ref[...])
-
-
-def feed_backward_kernel(row, kept, x_ref, vec_ref, dx_ref, up_ref, down_ref, *refs):
+    y_ref[...] += by_rows(g, order_ref[1], down_ref, down2_ref)
+
+
+def feed_backward_kernel(
+    row, kept, x_ref, vec_ref, order_ref, dx_ref, up_ref, up2_ref, down_ref, down2_ref, *refs
+):
     out_ref, vg_ref, p_ref = refs[1:4] if kept else refs[:3]
     acc_ref = refs[-1]
     j = pl.program_id(0)
+    half = up_ref.shape[0]
 
     @pl.when(j == 0)
     def _():
@@ -339,31 +375,38 @@
         p_ref[0] = dx_ref[...].astype(bf16)
         acc_ref[...] = jnp.zeros_like(acc_ref)
 
-    u = refs[0][...] if kept else nn(refs[3][0], up_ref[...])
+    u = refs[0][...] if kept else by_rows(refs[3][0], order_ref[0], up_ref, up2_ref)
     t = jnp.tanh(GELU_A * (u + GELU_B * u * u * u))
     if not kept:
         refs[3][1 + j] = (0.5 * u * (1.0 + t)).astype(bf16)
     slope = 0.5 * (1.0 + t) + 0.5 * u * (1.0 - t * t) * GELU_A * (1.0 + 3.0 * GELU_B * u * u)
-    du = (slope * nt(p_ref[0], down_ref[...])).astype(bf16)
+    dz = p_ref[0]
+    dg = jnp.concatenate((nt(dz, down_ref[...]), nt(dz, down2_ref[...])), axis=1)
+    du = (slope * nn(dg.astype(bf16), order_ref[1])).astype(bf16)
     p_ref[1 + j] = du
-    acc_ref[...] += nt(du, up_ref[...])
+    acc_ref[:, :half] += nt(du, up_ref[...])
+    acc_ref[:, half:] += nt(du, up2_ref[...])
 
     @pl.when(j == 3)
     def _():
-        dn, gg, gs = norm_backward(acc_ref[...], x_ref[...], vec_ref[row : row + 1])
+        db = acc_ref[...]
+        high = db.astype(bf16)
+        low = (db - high.astype(f32)).astype(bf16)
+        db = nn(high, order_ref[0]) + nn(low, order_ref[0])
+        dn, gg, gs = norm_backward(db, x_ref[...], vec_ref[row : row + 1])
         out_ref[...] = dx_ref[...].astype(f32) + dn
         vg_ref[0:1] = gg
         vg_ref[1:2] = gs
 
 
-def feed_out_kernel(x_ref, g_ref, down_ref, y_ref, acc_ref):
+def feed_out_kernel(x_ref, order_ref, g_ref, down_ref, down2_ref, y_ref, acc_ref):
     j = pl.program_id(0)
 
     @pl.when(j == 0)
     def _():
         acc_ref[...] = x_ref[...]
 
-    acc_ref[...] += nn(g_ref[0], down_ref[...])
+    acc_ref[...] += by_rows(g_ref[0], order_ref[1], down_ref, down2_ref)
 
     @pl.when(j == 3)
     def _():
@@ -427,31 +470,33 @@
     emit(nn(enc_ref[...], dkv_ref[...]), send_ref, keep_ref)
 
 
-def pack_kernel(u_qkv, u_out, u_up, u_down, m_qkv, m_out, m_up, m_down, c_q, c_pair, c_out, vec, out):
+def pack_kernel(u_qkv, u_out, u_up, u_down, m_qkv, m_out, m_up, m_down, c_q, c_pair, c_out, vec, out, u_feed, m_feed):
     rows, d = u_out.shape
     spread = spread_matrix().astype(bf16)
     i = lax.broadcasted_iota(jnp.int32, (rows, 4 * rows), 0)
     k = lax.broadcasted_iota(jnp.int32, (rows, 4 * rows), 1)
 
-    def layer(at, qkv, w_out, up, down):
-        out[:, at : at + 3 * d] = qkv[...]
-        out[:, at + 3 * d : at + 4 * d] = w_out[...]
+    def feed(out, up, down):
         for b in range(4 * d // 512):
             y = nn(up[:, b * 512 : (b + 1) * 512], spread).astype(bf16)
             for j in range(4):
-                to = at + (4 + j) * d + b * LANES
+                to = j * d + b * LANES
                 out[:, to : to + LANES] = y[:, j * LANES : (j + 1) * LANES]
         for j in range(4):
             y = nn((k == 4 * i + j).astype(bf16), down[...])
-            out[:, at + (8 + j) * d : at + (9 + j) * d] = y.astype(bf16)
-
-    layer(0, u_qkv, u_out, u_up, u_down)
-    layer(12 * d, m_qkv, m_out, m_up, m_down)
-    out[:, 24 * d : 25 * d] = c_q[...]
-    out[:, 25 * d : 27 * d] = c_pair[...]
-    out[:, 27 * d : 28 * d] = c_out[...]
+            out[:, (4 + j) * d : (5 + j) * d] = y.astype(bf16)
+
+    feed(u_feed, u_up, u_down)
+    feed(m_feed, m_up, m_down)
+    out[:, : 3 * d] = u_qkv[...]
+    out[:, 3 * d : 4 * d] = u_out[...]
+    out[:, 4 * d : 7 * d] = m_qkv[...]
+    out[:, 7 * d : 8 * d] = m_out[...]
+    out[:, 8 * d : 9 * d] = c_q[...]
+    out[:, 9 * d : 11 * d] = c_pair[...]
+    out[:, 11 * d : 12 * d] = c_out[...]
     eye = lax.broadcasted_iota(jnp.int32, (rows, rows), 0) == lax.broadcasted_iota(jnp.int32, (rows, rows), 1)
-    out[:, 28 * d :] = nt(eye.astype(bf16), vec[...]).astype(bf16)
+    out[:, 12 * d :] = nt(eye.astype(bf16), vec[...]).astype(bf16)
 
 
 def whole(x):
@@ -547,7 +592,7 @@
         first, later = self.block(lambda j: 0), self.block(lambda j: 1 + j)
         return call(
             feed_grads_kernel, 4, (self.order,) + f + p + f + p,
-            [whole(self.order)] + [first] * 4 + [later] * 4,
+            [pl.BlockSpec((2, d // 2, d), lambda j: (0, 0, 0))] + [first] * 4 + [later] * 4,
             outs, [pl.BlockSpec((d // 4, d), lambda j: (0, j))] * 4,
             scratch=[pltpu.VMEM((d // 2, 2 * t), bf16)],
         )
@@ -582,36 +627,38 @@
             attend_grads_kernel, steps, ins, specs, outs, [grad_a, grad_a, grad_b, grad_b]
         )
 
-    def feed_forward(self, x, at, row):
+    def feed_forward(self, x, w, row):
         d, t = self.d, self.t
         outs = (self.xs, sds((5, t, d), bf16), sds((t, 4 * d), f32))
+        ins = (x, self.vec, self.order)
+        half = pl.BlockSpec((d // 2, d), lambda j: (0, j))
         return call(
             functools.partial(feed_forward_kernel, row), 4,
-            (x, self.vec, self.w, self.w),
-            [whole(x), whole(self.vec), self.weight(lambda j: at + j), self.weight(lambda j: at + 4 + j)],
+            ins + w, [whole(i) for i in ins] + [half] * 4,
             outs, [whole(outs[0]), whole(outs[1]), pl.BlockSpec((t, d), lambda j: (0, j))],
         )
 
-    def feed_backward(self, x, kept, dx, at, row):
+    def feed_backward(self, x, kept, dx, w, row):
         d, t = self.d, self.t
         outs = (self.xs, sds((8, d), f32), sds((5, t, d), bf16))
         if not kept:
             outs = outs + (sds((5, t, d), bf16),)
+        ins = (x, self.vec, self.order, dx)
+        half = pl.BlockSpec((d // 2, d), lambda j: (0, j))
         return call(
             functools.partial(feed_backward_kernel, row, bool(kept)), 4,
-            (x, self.vec, dx, self.w, self.w) + kept,
-            [
-                whole(x), whole(self.vec), whole(dx),
-                self.weight(lambda j: at + j), self.weight(lambda j: at + 4 + j),
-            ] + [pl.BlockSpec((t, d), lambda j: (0, j)) for _ in kept],
+            ins + w + kept,
+            [whole(i) for i in ins] + [half] * 4
+            + [pl.BlockSpec((t, d), lambda j: (0, j)) for _ in kept],
             outs, [whole(i) for i in outs],
             scratch=[pltpu.VMEM((t, d), f32)],
         )
 
-    def feed_out(self, x, p, at):
-        return call(
-            feed_out_kernel, 4, (x, p, self.w),
-            [whole(x), self.block(lambda j: 1 + j), self.weight(lambda j: at + 4 + j)],
+    def feed_out(self, x, p, w):
+        half = pl.BlockSpec((self.d // 2, self.d), lambda j: (0, j))
+        return call(
+            feed_out_kernel, 4, (x, self.order, p) + w[2:],
+            [whole(x), whole(self.order), self.block(lambda j: 1 + j), half, half],
             self.hs, whole(self.hs), scratch=[pltpu.VMEM((self.t, self.d), f32)],
         )
 
@@ -643,27 +690,48 @@
     x0 = tokens.reshape(-1, d)
     enc = encoder.reshape(-1, d)
     order = jnp.stack((place.order(d, True), place.order(d, False)))
-    order_pair = order[1]
-    order = order[:, : d // 2]
 
     vectors = (u_ag, u_as, u_mg, u_ms, m_ag, m_as, c_g, c_s, m_mg, m_ms)
     vectors = jnp.pad(jnp.stack(vectors, axis=0), ((0, LANES - len(vectors)), (0, 0)))
     parts = (u_qkv, u_out, u_up, u_down, m_qkv, m_out, m_up, m_down, c_q, c_pair, c_out, vectors)
-    packed = sds((rows, 28 * d + LANES), bf16)
-    shard = call(pack_kernel, 1, parts, [whole(p) for p in parts], packed, whole(packed), vmem=60)
-    enc_t = nt(order_pair, enc).astype(bf16)
+    packed = sds((rows, 12 * d + LANES), bf16), sds((rows, 8 * d), bf16), sds((rows, 8 * d), bf16)
+    shard, u_feed, m_feed = call(
+        pack_kernel, 1, parts, [whole(p) for p in parts], packed, [whole(p) for p in packed], vmem=60
+    )
+    enc_t = nt(order[1], enc).astype(bf16)
     w = lax.all_gather(shard, AXES, axis=0, tiled=True)
-    w, (order, enc_t) = tie(w, order, enc_t)
-    vec = nt(jnp.eye(16, LANES, dtype=bf16), w[:, 28 * d :])
+
+    u_feed, m_feed = Gather(place, u_feed), Gather(place, m_feed)
+    feeds = (u_feed, m_feed)
+    for _ in range(place.outer_bits):
+        for g in feeds:
+            g.swap()
+            g.join()
+    u_feed.swap()
+    u_feed.join()
+    u_feed.swap()
+    m_feed.swap()
+    u_feed.join()
+    u_feed.swap()
+    m_feed.join()
+    w, (order, enc_t, m_feed.x, u_feed.x, u_feed.got) = tie(
+        w, order, enc_t, m_feed.x, u_feed.x, u_feed.got
+    )
+    m_feed.swap()
+    vec = nt(jnp.eye(16, LANES, dtype=bf16), w[:, 12 * d :])
 
     net = Layers(captions, captions * length, d, w, vec, order, patch_count)
 
-    w_pair = w[:, 25 * d : 27 * d]
+    w_pair = w[:, 9 * d : 11 * d]
     kv = nn(enc, w_pair).astype(bf16)
     x0a, f_us, k_us = net.self_forward(x0, 0, 0)
-    x1, f_uf, k_uf = net.feed_forward(x0a, 4, 2)
-    x1a, f_ms, k_ms = net.self_forward(x1, 12, 4)
-    x1b, f_mc, k_mc = net.cross_forward(x1a, kv, 24, 6)
+    x1, f_uf, k_uf = net.feed_forward(x0a, u_feed.halves(), 2)
+    x1, (m_feed.x, m_feed.got) = tie(x1, m_feed.x, m_feed.got)
+    m_feed.join()
+    x1, (m_feed.x,) = tie(x1, m_feed.x)
+    m_feed.swap()
+    x1a, f_ms, k_ms = net.self_forward(x1, 4, 4)
+    x1b, f_mc, k_mc = net.cross_forward(x1a, kv, 8, 6)
 
     def core(x):
         return place.swap(x, BIT_CORE)
@@ -689,25 +757,25 @@
     f_us, f_uf, f_ms = pairs(f_us), pairs(f_uf), pairs(f_ms)
     x1b, (f_us, f_uf, f_ms) = tie(x1b, f_us, f_uf, f_ms)
     f_mc = pairs(f_mc)
-    dx, v_mf, p, f = net.feed_backward(x1b, (), out_grad.reshape(-1, d), 16, 8)
+    dx, v_mf, p, f = net.feed_backward(x1b, (), out_grad.reshape(-1, d), m_feed.halves(), 8)
     p, f = pairs(p), pairs(f)
-    x2 = net.feed_out(x1b, f[0], 16)
+    x2 = net.feed_out(x1b, f[0], m_feed.halves())
     p, (x2,) = tie(p, x2)
     s_mf = Sum(place, net.feed_grads(f, p))
     dx, (f_mc,) = tie(dx, f_mc)
     dx = go_on(dx, start=[s_mf])
-    dx, v_mc, p_c, dkv = net.cross_backward(x1a, k_mc, kv, dx, 24, 6)
+    dx, v_mc, p_c, dkv = net.cross_backward(x1a, k_mc, kv, dx, 8, 6)
     p_c = pairs(p_c)
     pair, send = net.pair_grads(enc_t, dkv)
     dx, (send,) = tie(dx, send)
     pair = pair, core(send)
-    dx, v_ms, p = net.self_backward(x1, k_ms, dx, 12, 4)
+    dx, v_ms, p = net.self_backward(x1, k_ms, dx, 4, 4)
     p = pairs(p)
     dx = go_on(dx, [s_mf], [s_mf])
     dx, (p, p_c, pair) = tie(dx, p, p_c, pair)
     s_ma = Sum(place, net.attend_grads(f_ms, p, (f_mc, p_c, pair)))
     dx = go_on(dx, start=[s_ma])
-    dx, v_uf, p = net.feed_backward(x0a, (k_uf,), dx, 4, 2)
+    dx, v_uf, p = net.feed_backward(x0a, (k_uf,), dx, u_feed.halves(), 2)
     p = pairs(p)
     dx = go_on(dx, [s_ma], [s_ma])
     dx, (p,) = tie(dx, p)
@@ -723,7 +791,7 @@
     denc = nt(dkv, w_pair).astype(bf16)
     dx, (p, denc) = tie(dx, p, denc)
     send_a, keep_a, send_b, keep_b = net.attend_grads(f_us, p)
-    v = nt(order[1], plus(p[0][4], p[1][4])[:LANES]).astype(bf16)
+    v = nt(order[1, : d // 2], plus(p[0][4], p[1][4])[:LANES]).astype(bf16)
     send_b = jnp.concatenate((send_b, v[d // 4 :]), axis=1)
     keep_b = jnp.concatenate((keep_b, v[: d // 4]), axis=1)
     s_us = Sum(place, (send_a, keep_a, send_b, keep_b))

time: 478 us -> 478 us (level)
  waiting for transfers between devices: 276 us -> 221 us
  local copies, waits for them, and re-layouts: 17.7 us -> 35.6 us
  starting transfers between devices: 24.7 us -> 42.6 us
  Pallas kernels: 101 us -> 115 us
    all_gather x1, waiting for transfers between devices: 192 us -> 0.01 us  [local(): w = lax.all_gather(shard, AXES, axis=0, tiled=True)]
    ppermute x35 -> x51, waiting for transfers between devices: 84.3 us -> 221 us  [swap(): return lax.ppermute(x, AXES, [(i, i ^ bit) for i in range(self.count)])]
    unnamed x52 -> x148, local copies, waits for them, and re-layouts: 2.59 us -> 24.8 us
    ppermute x35 -> x51, starting transfers between devices: 24.7 us -> 42.5 us  [swap(): return lax.ppermute(x, AXES, [(i, i ^ bit) for i in range(self.count)])]
    pallas_call x16, Pallas kernels: 101 us -> 115 us  [call(): pl.pallas_call(kernel, out_shape=outs, grid_spec=pltpu.PrefetchScalarGrid...]
  transfers between devices with their start and end apart: 36 -> 52, of which waited for: 15 -> 26; matrix products, arithmetic and copies ran while one was open for 10% -> 10% of each run, Pallas kernels for 14% -> 19%
where the time goes in v7:
time: 478 us; the launch traced here: 472 us
  waiting for transfers between devices  221 us (46%)
  Pallas kernels  115 us (24%)
  starting transfers between devices  42.6 us (9%)
  local copies, waits for them, and re-layouts  35.6 us (7%)
  other arithmetic  25 us (5%)
  matrix products  17.1 us (4%)
  between operations  15.8 us (3%)
    ppermute x51, waiting for transfers between devices, swap(): return lax.ppermute(x, AXES, [(i, i ^ bit) for i in range(self.count)])  221 us
    pallas_call x16, Pallas kernels, call(): pl.pallas_call(kernel, out_shape=outs, grid_spec=pltpu.PrefetchScalarGrid...  115 us
    ppermute x51, starting transfers between devices, swap(): return lax.ppermute(x, AXES, [(i, i ^ bit) for i in range(self.count)])  42.5 us
    unnamed x148, local copies, waits for them, and re-layouts  24.8 us
    convert_element_type x20, other arithmetic, plus(): return (a.astype(f32) + b.astype(f32)).astype(bf16)  14.4 us
    dot_general x4, matrix products, nt(): lax.dot_general(a, b, (((1,), (1,)), ((), ())), preferred_element_type=f32)  10.1 us
  transfers between devices with their start and end apart: 52, of which 26 were waited for; matrix products, arithmetic and copies ran while one was open for 10% of the time, Pallas kernels for 19%

profile of v7, /device:TPU:0, one launch (start us, length us, event | category | flops | bytes accessed | tf_op | source)
XLA Modules:
  0.0 472.0 jit_solution(15736852444284294745)
XLA Ops:
  18.3 29.2 %collective-permute-done.4 = bf16[24,6144]{1,0:T(8,128)(2,1)} collective-permute-done((bf16[24,6144]{1,0:T(8,128)(2,1)}, bf16[24,6144]{1,0:T(8,128)(2,1)}, u32[]{:S(2)}, u32[]{:S(2)}) %collective-permute-start.4) | collective-permute-done | bytes 294944 | tf_op jit(solution)/shard_map/ppermute | solution.py:35
  48.6 36.1 %collective-permute-done.5 = bf16[48,6144]{1,0:T(8,128)(2,1)S(1)} collective-permute-done((bf16[48,6144]{1,0:T(8,128)(2,1)S(1)}, bf16[48,6144]{1,0:T(8,128)(2,1)S(1)}, u32[]{:S(2)}, u32[]{:S(2)}) %collective-permute-start.5) | collective-permute-done | bytes 589856 | tf_op jit(solution)/shard_map/ppermute | solution.py:35
  91.1 19.2 %collective-permute-done.8 = bf16[96,3072]{1,0:T(8,128)(2,1)S(1)} collective-permute-done((bf16[96,3072]{1,0:T(8,128)(2,1)S(1)}, bf16[96,3072]{1,0:T(8,128)(2,1)S(1)}, u32[]{:S(2)}, u32[]{:S(2)}) %collective-permute-start.8) | collective-permute-done | bytes 589856 | tf_op jit(solution)/shard_map/ppermute | solution.py:35
  114.6 37.9 %collective-permute-done.9 = bf16[192,3072]{1,0:T(8,128)(2,1)S(1)} collective-permute-done((bf16[192,3072]{1,0:T(8,128)(2,1)S(1)}, bf16[192,3072]{1,0:T(8,128)(2,1)S(1)}, u32[]{:S(2)}, u32[]{:S(2)}) %collective-permute-start.9) | collective-permute-done | bytes 1179680 | tf_op jit(solution)/shard_map/ppermute | solution.py:35
  160.4 9.7 %collective-permute-done.3 = bf16[96,3072]{1,0:T(8,128)(2,1)S(1)} collective-permute-done((bf16[96,3072]{1,0:T(8,128)(2,1)S(1)}, bf16[96,3072]{1,0:T(8,128)(2,1)S(1)}, u32[]{:S(2)}, u32[]{:S(2)}) %collective-permute-start.3) | collective-permute-done | bytes 589856 | tf_op jit(solution)/shard_map/ppermute | solution.py:35
  178.6 7.2 %shard_map.425 = (f32[128,768]{1,0:T(8,128)S(1)}, bf16[2,128,768]{2,1,0:T(8,128)(2,1)}, bf16[3,128,768]{2,1,0:T(8,128)(2,1)S(1)}) custom-call(bf16[128,768]{1,0:T(8,128)(2,1)S(1)} %bitcast.41, f32[16,768]{1,0:T(8,128)S(1)} %fusion.20.vec_ref, bf16[768,9344]{1,0:T(8,128)(2,1)} %all-gather.2.cloned.1.call-done.w_ref), custom_call_target="tpu_custom_call" | custom-call | flops 1000 | bytes 1000 | tf_op jit(solution)/shard_map/pallas_call | solution.py:507
  185.8 9.2 %shard_map.426 = (f32[128,768]{1,0:T(8,128)S(1)}, bf16[5,128,768]{2,1,0:T(8,128)(2,1)S(1)}, f32[128,3072]{1,0:T(8,128)S(1)}) custom-call(f32[128,768]{1,0:T(8,128)S(1)} %get-tuple-element.226.x_ref, f32[16,768]{1,0:T(8,128)S(1)} %fusion.20.vec_ref, bf16[2,768,768]{2,1,0:T(8,128)(2,1)S(1)} %copy-done.2, bf16[384,3072]{1,0:T(8,128)(2,1)S(1)} %copy-done.6, ...), custom_call_target="tpu_custom_call" | custom-call | flops 1000 | bytes 1000 | tf_op jit(solution)/shard_map/pallas_call | solution.py:507
  195.0 5.7 %collective-permute-done.12 = bf16[192,3072]{1,0:T(8,128)(2,1)S(1)} collective-permute-done((bf16[192,3072]{1,0:T(8,128)(2,1)}, bf16[192,3072]{1,0:T(8,128)(2,1)S(1)}, u32[]{:S(2)}, u32[]{:S(2)}) %collective-permute-start.12) | collective-permute-done | bytes 1179680 | tf_op jit(solution)/shard_map/ppermute | solution.py:35
  215.2 9.0 %shard_map.428 = (f32[128,768]{1,0:T(8,128)S(1)}, bf16[2,128,768]{2,1,0:T(8,128)(2,1)S(1)}, bf16[128,768]{1,0:T(8,128)(2,1)S(1)}) custom-call(s32[2]{0:T(128)S(1)} %copy-done.59, f32[128,768]{1,0:T(8,128)S(1)} %get-tuple-element.241.x_ref, f32[16,768]{1,0:T(8,128)S(1)} %fusion.20.vec_ref, bf16[1152,1536]{1,0:T(8,128)(2,1)S(1)} %fusion.kv_ref, ...), custom_call_target="tpu_custom_call" | custom-call | flops 1000 | bytes 1000 | tf_op jit(solution)/shard_map/pallas_call | solution.py:507
  227.9 10.2 %shard_map.429 = (f32[128,768]{1,0:T(8,128)S(1)}, f32[8,768]{1,0:T(8,128)S(1)}, bf16[5,128,768]{2,1,0:T(8,128)(2,1)S(1)}, bf16[5,128,768]{2,1,0:T(8,128)(2,1)S(1)}) custom-call(f32[128,768]{1,0:T(8,128)S(1)} %get-tuple-element.246.x_ref, f32[16,768]{1,0:T(8,128)S(1)} %fusion.20.vec_ref, bf16[2,768,768]{2,1,0:T(8,128)(2,1)S(1)} %copy-done.2, ...), custom_call_target="tpu_custom_call" | custom-call | flops 1000 | bytes 1000 | tf_op jit(solution)/shard_map/pallas_call | solution.py:507
  239.2 5.7 %shard_map.430 = bf16[128,768]{1,0:T(8,128)(2,1)} custom-call(f32[128,768]{1,0:T(8,128)S(1)} %get-tuple-element.246.x_ref, bf16[2,768,768]{2,1,0:T(8,128)(2,1)S(1)} %copy-done.2, bf16[5,128,768]{2,1,0:T(8,128)(2,1)S(1)} %get-tuple-element.250.g_ref.b_ref, bf16[384,3072]{1,0:T(8,128)(2,1)S(1)} %copy-done.8, bf16[384,3072]{1,0:T(8,128)(2,1)S(1)} %copy-done.15), custom_call_target="tpu_custom_call" | custom-call | flops 1000 | bytes 1000 | tf_op jit(solution)/shard_map/pallas_call | solution.py:507
  247.9 5.2 %shard_map.431 = (bf16[192,3072]{1,0:T(8,128)(2,1)}, bf16[192,3072]{1,0:T(8,128)(2,1)S(1)}, bf16[192,3072]{1,0:T(8,128)(2,1)}, bf16[192,3072]{1,0:T(8,128)(2,1)S(1)}) custom-call(bf16[2,768,768]{2,1,0:T(8,128)(2,1)S(1)} %copy-done.2, bf16[5,128,768]{2,1,0:T(8,128)(2,1)S(1)} %get-tuple-element.250.g_ref.b_ref, bf16[5,128,768]{2,1,0:T(8,128)(2,1)S(1)} %copy-done.17, ...), custom_call_target="tpu_custom_call" | custom-call | flops 1000 | bytes 1000 | tf_op jit(solution)/shard_map/pallas_call | solution.py:507
  257.3 10.4 %shard_map.432 = (f32[128,768]{1,0:T(8,128)S(1)}, f32[8,768]{1,0:T(8,128)S(1)}, bf16[2,128,768]{2,1,0:T(8,128)(2,1)S(1)}, bf16[1152,1536]{1,0:T(8,128)(2,1)S(1)}) custom-call(s32[2]{0:T(128)S(1)} %copy-done.59, f32[128,768]{1,0:T(8,128)S(1)} %copy-done.26, f32[16,768]{1,0:T(8,128)S(1)} %fusion.20.vec_ref, bf16[128,768]{1,0:T(8,128)(2,1)S(1)} %copy-done.57, ...), custom_call_target="tpu_custom_call" | custom-call | flops 1000 | bytes 1000 | tf_op jit(solution)/shard_map/pallas_call | solution.py:507
  271.5 10.1 %shard_map.434 = (f32[128,768]{1,0:T(8,128)S(1)}, f32[8,768]{1,0:T(8,128)S(1)}, bf16[4,128,768]{2,1,0:T(8,128)(2,1)S(1)}) custom-call(f32[128,768]{1,0:T(8,128)S(1)} %get-tuple-element.240.x_ref, f32[16,768]{1,0:T(8,128)S(1)} %fusion.20.vec_ref, bf16[3,128,768]{2,1,0:T(8,128)(2,1)S(1)} %copy-done.40, f32[128,768]{1,0:T(8,128)S(1)} %get-tuple-element.267.dx_ref, ...), custom_call_target="tpu_custom_call" | custom-call | flops 1000 | bytes 1000 | tf_op jit(solution)/shard_map/pallas_call | solution.py:507
  291.3 7.2 %shard_map.435 = (bf16[192,3072]{1,0:T(8,128)(2,1)S(1)}, bf16[192,3072]{1,0:T(8,128)(2,1)S(1)}, bf16[192,3072]{1,0:T(8,128)(2,1)}, bf16[192,3072]{1,0:T(8,128)(2,1)S(1)}) custom-call(bf16[2,768,768]{2,1,0:T(8,128)(2,1)S(1)} %copy-done.2, bf16[2,128,768]{2,1,0:T(8,128)(2,1)S(1)} %copy-done.44, bf16[2,128,768]{2,1,0:T(8,128)(2,1)S(1)} %copy-done.46, ...), custom_call_target="tpu_custom_call" | custom-call | flops 1000 | bytes 1000 | tf_op jit(solution)/shard_map/pallas_call | solution.py:507
  302.7 7.3 %shard_map.436 = (f32[128,768]{1,0:T(8,128)S(1)}, f32[8,768]{1,0:T(8,128)S(1)}, bf16[5,128,768]{2,1,0:T(8,128)(2,1)S(1)}) custom-call(f32[128,768]{1,0:T(8,128)S(1)} %copy-done.22, f32[16,768]{1,0:T(8,128)S(1)} %fusion.20.vec_ref, bf16[2,768,768]{2,1,0:T(8,128)(2,1)S(1)} %copy-done.2, f32[128,768]{1,0:T(8,128)S(1)} %get-tuple-element.296.dx_ref, ...), custom_call_target="tpu_custom_call" | custom-call | flops 1000 | bytes 1000 | tf_op jit(solution)/shard_map/pallas_call | solution.py:507
  311.3 17.2 %collective-permute-done.27 = bf16[192,3072]{1,0:T(8,128)(2,1)S(1)} collective-permute-done((bf16[192,3072]{1,0:T(8,128)(2,1)S(1)}, bf16[192,3072]{1,0:T(8,128)(2,1)S(1)}, u32[]{:S(2)}, u32[]{:S(2)}) %collective-permute-start.27) | collective-permute-done | bytes 1179680 | tf_op jit(solution)/shard_map/ppermute | solution.py:35
  331.1 5.7 %shard_map.437 = (bf16[192,3072]{1,0:T(8,128)(2,1)S(1)}, bf16[192,3072]{1,0:T(8,128)(2,1)S(1)}, bf16[192,3072]{1,0:T(8,128)(2,1)S(1)}, bf16[192,3072]{1,0:T(8,128)(2,1)S(1)}) custom-call(bf16[2,768,768]{2,1,0:T(8,128)(2,1)S(1)} %copy-done.2, bf16[5,128,768]{2,1,0:T(8,128)(2,1)S(1)} %get-tuple-element.311.b_ref.g_ref, ...), custom_call_target="tpu_custom_call" | custom-call | flops 1000 | bytes 1000 | tf_op jit(solution)/shard_map/pallas_call | solution.py:507
  344.0 10.6 %shard_map.438 = (f32[128,768]{1,0:T(8,128)S(1)}, f32[8,768]{1,0:T(8,128)}, bf16[5,128,768]{2,1,0:T(8,128)(2,1)S(1)}) custom-call(bf16[128,768]{1,0:T(8,128)(2,1)S(1)} %bitcast.42, f32[16,768]{1,0:T(8,128)S(1)} %fusion.20.vec_ref, bf16[3,128,768]{2,1,0:T(8,128)(2,1)S(1)} %copy-done.42, f32[128,768]{1,0:T(8,128)S(1)} %get-tuple-element.327.dx_ref, ...), custom_call_target="tpu_custom_call" | custom-call | flops 1000 | bytes 1000 | tf_op jit(solution)/shard_map/pallas_call | solution.py:507
  359.3 5.7 %convolution_convert_fusion.1 = bf16[1152,768]{1,0:T(8,128)(2,1)} fusion(bf16[1152,1536]{1,0:T(8,128)(2,1)S(1)} %copy-done.19, bf16[768,9344]{1,0:T(8,128)(2,1)} %all-gather.2.cloned.1.call-done.w_ref), kind=kOutput, calls=%fused_computation.3 | convolution fusion | flops 2718793728 | bytes 7667712 | tf_op jit(solution)/shard_map/dot_general | solution.py:137
  377.3 6.1 %collective-permute-done.36 = bf16[192,3072]{1,0:T(8,128)(2,1)S(1)} collective-permute-done((bf16[192,3072]{1,0:T(8,128)(2,1)S(1)}, bf16[192,3072]{1,0:T(8,128)(2,1)S(1)}, u32[]{:S(2)}, u32[]{:S(2)}) %collective-permute-start.36) | collective-permute-done | bytes 1179680 | tf_op jit(solution)/shard_map/ppermute | solution.py:35
  413.9 8.2 %collective-permute-done.44 = bf16[24,6144]{1,0:T(8,128)(2,1)S(1)} collective-permute-done((bf16[24,6144]{1,0:T(8,128)(2,1)S(1)}, bf16[24,6144]{1,0:T(8,128)(2,1)S(1)}, u32[]{:S(2)}, u32[]{:S(2)}) %collective-permute-start.44) | collective-permute-done | bytes 294944 | tf_op jit(solution)/shard_map/ppermute | solution.py:35
  425.4 9.3 %collective-permute-done.47 = bf16[48,6144]{1,0:T(8,128)(2,1)S(1)} collective-permute-done((bf16[48,6144]{1,0:T(8,128)(2,1)S(1)}, bf16[48,6144]{1,0:T(8,128)(2,1)S(1)}, u32[]{:S(2)}, u32[]{:S(2)}) %collective-permute-start.47) | collective-permute-done | bytes 589856 | tf_op jit(solution)/shard_map/ppermute | solution.py:35
  444.2 12.2 %collective-permute-done.49 = bf16[24,3200]{1,0:T(8,128)(2,1)S(1)} collective-permute-done((bf16[24,3200]{1,0:T(8,128)(2,1)S(1)}, bf16[24,3200]{1,0:T(8,128)(2,1)S(1)}, u32[]{:S(2)}, u32[]{:S(2)}) %collective-permute-start.49) | collective-permute-done | bytes 153632 | tf_op jit(solution)/shard_map/ppermute | solution.py:35
  (332 shorter events, 161.8 us)
Async XLA Ops:
  7.2 167.2 %all-gather.2.cloned.1.call-start = ((), (), s32[]{:S(2)}) async-start(), calls=%async_computation | async-start | bytes 14800896 | tf_op jit(solution)/shard_map/all_gather | solution.py:702
  13.0 34.5 %collective-permute-start.4 = (bf16[24,6144]{1,0:T(8,128)(2,1)}, bf16[24,6144]{1,0:T(8,128)(2,1)}, u32[]{:S(2)}, u32[]{:S(2)}) collective-permute-start(bf16[24,6144]{1,0:T(8,128)(2,1)} %get-tuple-element.224), channel_id=1, source_target_pairs={{0,16},{1,17},{2,18},{3,19},{4,20},{5,21},{6,22},{7,23},{8,24},{9,... | collective-permute-start | bytes 884744 | tf_op jit(solution)/shard_map/ppermute | solution.py:35
  17.1 97.3 %collective-permute-start = (bf16[24,6144]{1,0:T(8,128)(2,1)}, bf16[24,6144]{1,0:T(8,128)(2,1)S(1)}, u32[]{:S(2)}, u32[]{:S(2)}) collective-permute-start(bf16[24,6144]{1,0:T(8,128)(2,1)} %get-tuple-element.223), channel_id=1, source_target_pairs={{0,16},{1,17},{2,18},{3,19},{4,20},{5,21},{6,22},{7,23},{8,24},{9,... | collective-permute-start | bytes 884744 | tf_op jit(solution)/shard_map/ppermute | solution.py:35
  48.5 36.3 %collective-permute-start.5 = (bf16[48,6144]{1,0:T(8,128)(2,1)S(1)}, bf16[48,6144]{1,0:T(8,128)(2,1)S(1)}, u32[]{:S(2)}, u32[]{:S(2)}) collective-permute-start(bf16[48,6144]{1,0:T(8,128)(2,1)S(1)} %constant_dynamic-update-slice_fusion.2), channel_id=1, source_target_pairs={{0,8},{1,9},{2,10},{3,11},{4,12},{5,13},{6,14},{7,15},{8,0},{9,1},... | collective-permute-start | bytes 1769480 | tf_op jit(solution)/shard_map/ppermute | solution.py:35
  84.9 25.5 %collective-permute-start.8 = (bf16[96,3072]{1,0:T(8,128)(2,1)S(1)}, bf16[96,3072]{1,0:T(8,128)(2,1)S(1)}, u32[]{:S(2)}, u32[]{:S(2)}) collective-permute-start(bf16[96,3072]{1,0:T(8,128)(2,1)S(1)} %pad_maximum_fusion.16), channel_id=1, source_target_pairs={{0,4},{1,5},{2,6},{3,7},{4,0},{5,1},{6,2},{7,3},{8,12},{9,13},{10,... | collective-permute-start | bytes 1769480 | tf_op jit(solution)/shard_map/ppermute | solution.py:35
  86.5 27.8 %collective-permute-start.6 = (bf16[96,3072]{1,0:T(8,128)(2,1)S(1)}, bf16[96,3072]{1,0:T(8,128)(2,1)S(1)}, u32[]{:S(2)}, u32[]{:S(2)}) collective-permute-start(bf16[96,3072]{1,0:T(8,128)(2,1)S(1)} %pad_maximum_fusion.15), channel_id=1, source_target_pairs={{0,1},{1,0},{2,3},{3,2},{4,5},{5,4},{6,7},{7,6},{8,9},{9,8},{10,11... | collective-permute-start | bytes 1769480 | tf_op jit(solution)/shard_map/ppermute | solution.py:35
  110.4 42.1 %collective-permute-start.9 = (bf16[192,3072]{1,0:T(8,128)(2,1)S(1)}, bf16[192,3072]{1,0:T(8,128)(2,1)S(1)}, u32[]{:S(2)}, u32[]{:S(2)}) collective-permute-start(bf16[192,3072]{1,0:T(8,128)(2,1)S(1)} %pad_maximum_fusion.7), channel_id=1, source_target_pairs={{0,1},{1,0},{2,3},{3,2},{4,5},{5,4},{6,7},{7,6},{8,9},{9,8},{10,11... | collective-permute-start | bytes 3538952 | tf_op jit(solution)/shard_map/ppermute | solution.py:35
  114.4 38.4 %collective-permute-start.7 = (bf16[192,3072]{1,0:T(8,128)(2,1)S(1)}, bf16[192,3072]{1,0:T(8,128)(2,1)S(1)}, u32[]{:S(2)}, u32[]{:S(2)}) collective-permute-start(bf16[192,3072]{1,0:T(8,128)(2,1)S(1)} %pad_maximum_fusion.6), channel_id=1, source_target_pairs={{0,4},{1,5},{2,6},{3,7},{4,0},{5,1},{6,2},{7,3},{8,12},{9,13},{10,... | collective-permute-start | bytes 3538952 | tf_op jit(solution)/shard_map/ppermute | solution.py:35
  114.5 39.7 %collective-permute-start.1 = (bf16[48,6144]{1,0:T(8,128)(2,1)S(1)}, bf16[48,6144]{1,0:T(8,128)(2,1)S(1)}, u32[]{:S(2)}, u32[]{:S(2)}) collective-permute-start(bf16[48,6144]{1,0:T(8,128)(2,1)S(1)} %constant_dynamic-update-slice_fusion), channel_id=1, source_target_pairs={{0,8},{1,9},{2,10},{3,11},{4,12},{5,13},{6,14},{7,15},{8,0},{9,1},... | collective-permute-start | bytes 1769480 | tf_op jit(solution)/shard_map/ppermute | solution.py:35
  174.4 26.3 %collective-permute-start.12 = (bf16[192,3072]{1,0:T(8,128)(2,1)}, bf16[192,3072]{1,0:T(8,128)(2,1)S(1)}, u32[]{:S(2)}, u32[]{:S(2)}) collective-permute-start(bf16[192,3072]{1,0:T(8,128)(2,1)} %pad_maximum_fusion.4), channel_id=1, source_target_pairs={{0,4},{1,5},{2,6},{3,7},{4,0},{5,1},{6,2},{7,3},{8,12},{9,13},{10,... | collective-permute-start | bytes 3538952 | tf_op jit(solution)/shard_map/ppermute | solution.py:35
  176.0 25.7 %collective-permute-start.13 = (bf16[192,3072]{1,0:T(8,128)(2,1)S(1)}, bf16[192,3072]{1,0:T(8,128)(2,1)S(1)}, u32[]{:S(2)}, u32[]{:S(2)}) collective-permute-start(bf16[192,3072]{1,0:T(8,128)(2,1)S(1)} %pad_maximum_fusion.5), channel_id=1, source_target_pairs={{0,1},{1,0},{2,3},{3,2},{4,5},{5,4},{6,7},{7,6},{8,9},{9,8},{10,11... | collective-permute-start | bytes 3538952 | tf_op jit(solution)/shard_map/ppermute | solution.py:35
  203.1 23.4 %collective-permute-start.17 = (bf16[384,3072]{1,0:T(8,128)(2,1)S(1)}, bf16[384,3072]{1,0:T(8,128)(2,1)}, u32[]{:S(2)}, u32[]{:S(2)}) collective-permute-start(bf16[384,3072]{1,0:T(8,128)(2,1)S(1)} %pad_maximum_fusion.2.up_ref), channel_id=1, source_target_pairs={{0,2},{1,3},{2,0},{3,1},{4,6},{5,7},{6,4},{7,5},{8,10},{9,11},{10,... | collective-permute-start | bytes 7077896 | tf_op jit(solution)/shard_map/ppermute | solution.py:35
  255.2 28.2 %collective-permute-start.22 = (bf16[192,3072]{1,0:T(8,128)(2,1)}, bf16[192,3072]{1,0:T(8,128)(2,1)S(1)}, u32[]{:S(2)}, u32[]{:S(2)}) collective-permute-start(bf16[192,3072]{1,0:T(8,128)(2,1)} %get-tuple-element.271), channel_id=1, source_target_pairs={{0,4},{1,5},{2,6},{3,7},{4,0},{5,1},{6,2},{7,3},{8,12},{9,13},{10,... | collective-permute-start | bytes 3538952 | tf_op jit(solution)/shard_map/ppermute | solution.py:35
  255.8 28.0 %collective-permute-start.23 = (bf16[192,3072]{1,0:T(8,128)(2,1)}, bf16[192,3072]{1,0:T(8,128)(2,1)}, u32[]{:S(2)}, u32[]{:S(2)}) collective-permute-start(bf16[192,3072]{1,0:T(8,128)(2,1)} %get-tuple-element.272), channel_id=1, source_target_pairs={{0,1},{1,0},{2,3},{3,2},{4,5},{5,4},{6,7},{7,6},{8,9},{9,8},{10,11... | collective-permute-start | bytes 3538952 | tf_op jit(solution)/shard_map/ppermute | solution.py:35
  299.6 28.9 %collective-permute-start.27 = (bf16[192,3072]{1,0:T(8,128)(2,1)S(1)}, bf16[192,3072]{1,0:T(8,128)(2,1)S(1)}, u32[]{:S(2)}, u32[]{:S(2)}) collective-permute-start(bf16[192,3072]{1,0:T(8,128)(2,1)S(1)} %get-tuple-element.301), channel_id=1, source_target_pairs={{0,4},{1,5},{2,6},{3,7},{4,0},{5,1},{6,2},{7,3},{8,12},{9,13},{10,... | collective-permute-start | bytes 3538952 | tf_op jit(solution)/shard_map/ppermute | solution.py:35
  301.1 29.1 %collective-permute-start.28 = (bf16[192,3072]{1,0:T(8,128)(2,1)}, bf16[192,3072]{1,0:T(8,128)(2,1)S(1)}, u32[]{:S(2)}, u32[]{:S(2)}) collective-permute-start(bf16[192,3072]{1,0:T(8,128)(2,1)} %get-tuple-element.302), channel_id=1, source_target_pairs={{0,1},{1,0},{2,3},{3,2},{4,5},{5,4},{6,7},{7,6},{8,9},{9,8},{10,11... | collective-permute-start | bytes 3538952 | tf_op jit(solution)/shard_map/ppermute | solution.py:35
  310.1 30.5 %collective-permute-start.30 = (bf16[96,3072]{1,0:T(8,128)(2,1)S(1)}, bf16[96,3072]{1,0:T(8,128)(2,1)S(1)}, u32[]{:S(2)}, u32[]{:S(2)}) collective-permute-start(bf16[96,3072]{1,0:T(8,128)(2,1)S(1)} %copy-done.67), channel_id=1, source_target_pairs={{0,1},{1,0},{2,3},{3,2},{4,5},{5,4},{6,7},{7,6},{8,9},{9,8},{10,11... | collective-permute-start | bytes 1769480 | tf_op jit(solution)/shard_map/ppermute | solution.py:35
  310.7 29.8 %collective-permute-start.31 = (bf16[96,3072]{1,0:T(8,128)(2,1)S(1)}, bf16[96,3072]{1,0:T(8,128)(2,1)S(1)}, u32[]{:S(2)}, u32[]{:S(2)}) collective-permute-start(bf16[96,3072]{1,0:T(8,128)(2,1)S(1)} %copy-done.66), channel_id=1, source_target_pairs={{0,4},{1,5},{2,6},{3,7},{4,0},{5,1},{6,2},{7,3},{8,12},{9,13},{10,... | collective-permute-start | bytes 1769480 | tf_op jit(solution)/shard_map/ppermute | solution.py:35
  354.6 28.8 %collective-permute-start.36 = (bf16[192,3072]{1,0:T(8,128)(2,1)S(1)}, bf16[192,3072]{1,0:T(8,128)(2,1)S(1)}, u32[]{:S(2)}, u32[]{:S(2)}) collective-permute-start(bf16[192,3072]{1,0:T(8,128)(2,1)S(1)} %get-tuple-element.360), channel_id=1, source_target_pairs={{0,4},{1,5},{2,6},{3,7},{4,0},{5,1},{6,2},{7,3},{8,12},{9,13},{10,... | collective-permute-start | bytes 3538952 | tf_op jit(solution)/shard_map/ppermute | solution.py:35
  356.1 28.8 %collective-permute-start.37 = (bf16[192,3072]{1,0:T(8,128)(2,1)S(1)}, bf16[192,3072]{1,0:T(8,128)(2,1)S(1)}, u32[]{:S(2)}, u32[]{:S(2)}) collective-permute-start(bf16[192,3072]{1,0:T(8,128)(2,1)S(1)} %get-tuple-element.361), channel_id=1, source_target_pairs={{0,1},{1,0},{2,3},{3,2},{4,5},{5,4},{6,7},{7,6},{8,9},{9,8},{10,11... | collective-permute-start | bytes 3538952 | tf_op jit(solution)/shard_map/ppermute | solution.py:35
  371.4 27.3 %collective-permute-start.40 = (bf16[192,1664]{1,0:T(8,128)(2,1)}, bf16[192,1664]{1,0:T(8,128)(2,1)}, u32[]{:S(2)}, u32[]{:S(2)}) collective-permute-start(bf16[192,1664]{1,0:T(8,128)(2,1)} %pad_maximum_fusion.8), channel_id=1, source_target_pairs={{0,1},{1,0},{2,3},{3,2},{4,5},{5,4},{6,7},{7,6},{8,9},{9,8},{10,11... | collective-permute-start | bytes 1916936 | tf_op jit(solution)/shard_map/ppermute | solution.py:35
  372.7 23.4 %collective-permute-start.39 = (bf16[192,1536]{1,0:T(8,128)(2,1)S(1)}, bf16[192,1536]{1,0:T(8,128)(2,1)}, u32[]{:S(2)}, u32[]{:S(2)}) collective-permute-start(bf16[192,1536]{1,0:T(8,128)(2,1)S(1)} %get-tuple-element.374), channel_id=1, source_target_pairs={{0,4},{1,5},{2,6},{3,7},{4,0},{5,1},{6,2},{7,3},{8,12},{9,13},{10,... | collective-permute-start | bytes 1769480 | tf_op jit(solution)/shard_map/ppermute | solution.py:35
  387.5 23.8 %collective-permute-start.42 = (bf16[96,3072]{1,0:T(8,128)(2,1)}, bf16[96,3072]{1,0:T(8,128)(2,1)}, u32[]{:S(2)}, u32[]{:S(2)}) collective-permute-start(bf16[96,3072]{1,0:T(8,128)(2,1)} %get-tuple-element.387), channel_id=1, source_target_pairs={{0,1},{1,0},{2,3},{3,2},{4,5},{5,4},{6,7},{7,6},{8,9},{9,8},{10,11... | collective-permute-start | bytes 1769480 | tf_op jit(solution)/shard_map/ppermute | solution.py:35
  388.2 23.1 %collective-permute-start.43 = (bf16[96,3072]{1,0:T(8,128)(2,1)}, bf16[96,3072]{1,0:T(8,128)(2,1)}, u32[]{:S(2)}, u32[]{:S(2)}) collective-permute-start(bf16[96,3072]{1,0:T(8,128)(2,1)} %get-tuple-element.388), channel_id=1, source_target_pairs={{0,4},{1,5},{2,6},{3,7},{4,0},{5,1},{6,2},{7,3},{8,12},{9,13},{10,... | collective-permute-start | bytes 1769480 | tf_op jit(solution)/shard_map/ppermute | solution.py:35
  (101 other events, 1082.0 us)
Sparse Core Ops, SparseCore 0:
  13.1 150.1 all-gather.1

commit v8 on v6

--- a/solution.py
+++ b/solution.py
@@ -34,7 +34,11 @@
     def swap(self, x, bit):
         return lax.ppermute(x, AXES, [(i, i ^ bit) for i in range(self.count)])
 
-    def order(self, d, near_first):
+    def swap_by_core(self, x, bits):
+        pairs = [(i, i ^ bits[(i // BIT_CORE) % 2]) for i in range(self.count)]
+        return lax.ppermute(x, AXES, pairs)
+
+    def order(self, d):
         n, rows = self.outer_size, d // self.count
         k = lax.broadcasted_iota(jnp.int32, (d, 1), 0)
         row, place = k % rows, (k // rows) % n
@@ -44,7 +48,8 @@
         outer = outer ^ self.outer
         rest = k // (rows * n)
         low, high = rest % 2, (rest // 2) % 2
-        near, pair = (high, low) if near_first else (low, high)
+        near = jnp.where((rest // 4) ^ self.core == 0, high, low)
+        pair = high + low - near
         feature = outer * 2 + (near ^ self.near)
         feature = (feature * 2 + ((rest // 4) ^ self.core)) * 2 + (pair ^ self.pair)
         feature = feature * rows + row
@@ -58,31 +63,26 @@
 class Sum:
     def __init__(self, place, grads):
         self.place, self.stage = place, 0
-        send_a, keep_a, send_b, keep_b = grads
-        self.send, self.kept = (send_a, send_b), (keep_a, keep_b)
+        self.send, self.kept = grads
 
     def swap(self):
         if self.stage < 2:
             bits = ((BIT_NEAR, BIT_PAIR), (BIT_PAIR, BIT_NEAR))[self.stage]
+            self.got = self.place.swap_by_core(self.send, bits)
         else:
-            bits = (8 << (self.stage - 2),)
-        self.got = tuple(self.place.swap(x, bit) for x, bit in zip(self.send, bits))
+            self.got = self.place.swap(self.send, 8 << (self.stage - 2))
 
     def sums(self):
-        def part(at):
-            return tuple(plus(k[at], g[at]) for k, g in zip(self.kept, self.got))
-
-        if self.stage == 1:
-            t = jnp.concatenate(part(slice(None)), axis=1)
-            half = t.shape[0] // 2
-            self.kept, self.send = (t[:half],), (t[half:],)
+        if self.stage < 2:
+            self.send, self.kept = half_sums(self.kept, self.got)
         else:
-            half = self.kept[0].shape[0] // 2
-            self.kept, self.send = part(slice(half)), part(slice(half, None))
+            half = self.kept.shape[0] // 2
+            self.send = plus(self.kept[half:], self.got[half:])
+            self.kept = plus(self.kept[:half], self.got[:half])
         self.stage += 1
 
     def total(self):
-        return self.kept[0].astype(f32) + self.got[0].astype(f32)
+        return self.kept.astype(f32) + self.got.astype(f32)
 
 
 def tie(x, *others):
@@ -381,46 +381,61 @@
 
 
 def feed_grads_kernel(
-    order_ref, b_ref, b2_ref, z_ref, z2_ref, g_ref, g2_ref, u_ref, u2_ref,
-    send_a_ref, keep_a_ref, send_b_ref, keep_b_ref, bt_ref,
+    order_ref, b_ref, b2_ref, z_ref, z2_ref, g_ref, g2_ref, u_ref, u2_ref, send_ref, keep_ref, bt_ref
 ):
+    d = order_ref.shape[1]
+
     @pl.when(pl.program_id(0) == 0)
     def _():
-        bt_ref[...] = nt(order_ref[0], both(b_ref, b2_ref)).astype(bf16)
-
-    emit(nn(bt_ref[...], both(u_ref, u2_ref)), send_a_ref, keep_a_ref)
-    gt = nt(order_ref[1], both(g_ref, g2_ref)).astype(bf16)
-    emit(nn(gt, both(z_ref, z2_ref)), send_b_ref, keep_b_ref)
-
-
-def attend_grads_kernel(
-    order_ref, s_ref, s2_ref, sd_ref, sd2_ref, *refs
-):
-    send_a_ref, keep_a_ref, send_b_ref, keep_b_ref = refs[-4:]
+        bt_ref[...] = nt(order_ref[...], both(b_ref, b2_ref)).astype(bf16)
+
+    up, down = (slice(None), slice(0, d)), (slice(None), slice(d, 2 * d))
+    emit(nn(bt_ref[...], both(u_ref, u2_ref)), send_ref.at[up], keep_ref.at[up])
+    gt = nt(order_ref[...], both(g_ref, g2_ref)).astype(bf16)
+    emit(nn(gt, both(z_ref, z2_ref)), send_ref.at[down], keep_ref.at[down])
+
+
+def attend_grads_kernel(order_ref, s_ref, s2_ref, sd_ref, sd2_ref, *refs):
+    send_ref, keep_ref = refs[-2:]
     j = pl.program_id(0)
 
     def product(a_ref, a2_ref, d_ref, d2_ref):
-        at = nt(order_ref[0], both(a_ref, a2_ref)).astype(bf16)
-        return nn(at, both(d_ref, d2_ref))
-
-    @pl.when(j < 2)
-    def _():
-        emit(product(s_ref, s2_ref, sd_ref, sd2_ref), send_a_ref, keep_a_ref)
-
-    @pl.when((j == 2) | (j == 3))
-    def _():
-        emit(product(s_ref, s2_ref, sd_ref, sd2_ref), send_b_ref, keep_b_ref)
-
-    if len(refs) > 4:
+        at = nt(order_ref[...], both(a_ref, a2_ref)).astype(bf16)
+        emit(nn(at, both(d_ref, d2_ref)), send_ref, keep_ref)
+
+    @pl.when(j < 4)
+    def _():
+        product(s_ref, s2_ref, sd_ref, sd2_ref)
+
+    if len(refs) > 2:
         c_ref, c2_ref, cd_ref, cd2_ref, pair_ref, pair2_ref = refs[:6]
 
         @pl.when((j == 4) | (j == 5))
         def _():
-            emit(product(c_ref, c2_ref, cd_ref, cd2_ref), send_a_ref, keep_a_ref)
+            product(c_ref, c2_ref, cd_ref, cd2_ref)
 
         @pl.when(j > 5)
         def _():
-            emit(pair_ref[...].astype(f32) + pair2_ref[...].astype(f32), send_b_ref, keep_b_ref)
+            emit(pair_ref[...].astype(f32) + pair2_ref[...].astype(f32), send_ref, keep_ref)
+
+
+def half_sums_kernel(kept_ref, got_ref, send_ref, keep_ref):
+    emit(kept_ref[...].astype(f32) + got_ref[...].astype(f32), send_ref, keep_ref)
+
+
+def half_sums(kept, got):
+    rows, wide = kept.shape
+    steps = 2 if wide % (2 * LANES) == 0 else 1
+    full = pl.BlockSpec((rows, wide // steps), lambda j: (0, j))
+    half = pl.BlockSpec((rows // 2, wide // steps), lambda j: (0, j))
+    outs = (sds((rows // 2, wide), bf16),) * 2
+    return call(half_sums_kernel, steps, (kept, got), [full] * 2, outs, [half] * 2, vmem=24)
+
+
+def pair_input_kernel(dkv_ref, k_ref, v_ref, out_ref):
+    d = k_ref.shape[0]
+    g = nt(dkv_ref[:, :d], k_ref[...]) + nt(dkv_ref[:, d:], v_ref[...])
+    out_ref[...] = g.astype(bf16)
 
 
 def pair_grads_kernel(enc_ref, dkv_ref, keep_ref, send_ref):
@@ -538,48 +553,47 @@
             outs, [grad, grad],
         )
 
+    def pair_input(self, dkv, at):
+        d, rows = self.d, dkv.shape[0] // self.captions
+        out = sds((dkv.shape[0], d), bf16)
+        return call(
+            pair_input_kernel, self.captions, (dkv, self.w, self.w),
+            [pl.BlockSpec((rows, 2 * d), lambda j: (j, 0))]
+            + [self.weight(lambda j: at), self.weight(lambda j: at + 1)],
+            out, pl.BlockSpec((rows, d), lambda j: (j, 0)),
+        )
+
     def block(self, index):
         return pl.BlockSpec((1, self.t, self.d), lambda j: (index(j), 0, 0))
 
     def feed_grads(self, f, p):
         d, t = self.d, self.t
-        outs = (sds((d // 4, 4 * d), bf16),) * 4
+        outs = (sds((d // 4, 8 * d), bf16),) * 2
         first, later = self.block(lambda j: 0), self.block(lambda j: 1 + j)
+        half = pl.BlockSpec((d // 2, d), lambda j: (0, 0))
         return call(
             feed_grads_kernel, 4, (self.order,) + f + p + f + p,
-            [whole(self.order)] + [first] * 4 + [later] * 4,
-            outs, [pl.BlockSpec((d // 4, d), lambda j: (0, j))] * 4,
+            [half] + [first] * 4 + [later] * 4,
+            outs, [pl.BlockSpec((d // 4, 2 * d), lambda j: (0, j))] * 2,
             scratch=[pltpu.VMEM((d // 2, 2 * t), bf16)],
         )
 
     def attend_grads(self, f, p, cross=()):
         d, t = self.d, self.t
         steps = 8 if cross else 4
-        outs = (sds((d // 4, steps // 2 * d), bf16),) * 4
-
-        def first(j):
-            return jnp.where(j < 4, jnp.minimum(j, 1), jnp.minimum(j - 2, 3))
-
-        def second(j):
-            return jnp.where(j < 6, jnp.clip(j - 2, 0, 1), j - 4)
-
-        grad_a = pl.BlockSpec((d // 4, d), lambda j: (0, first(j)))
-        grad_b = pl.BlockSpec((d // 4, d), lambda j: (0, second(j)))
-        order = pl.BlockSpec(
-            (1, d // 2, d), lambda j: (jnp.where((j == 2) | (j == 3), 1, 0), 0, 0)
-        )
+        outs = (sds((d // 4, steps * d), bf16),) * 2
+        half = pl.BlockSpec((d // 2, d), lambda j: (0, 0))
         lhs = self.block(lambda j: jnp.minimum(j // 3, 1))
         rhs = self.block(lambda j: jnp.minimum(j, 3))
-        ins, specs = (self.order,) + f + p, [order, lhs, lhs, rhs, rhs]
+        ins, specs = (self.order,) + f + p, [half, lhs, lhs, rhs, rhs]
         if cross:
             f, p, pair = cross
-            lhs = self.block(lambda j: jnp.clip(j - 4, 0, 1))
-            rhs = lhs
-            half = pl.BlockSpec((d // 2, d), lambda j: (0, jnp.clip(j - 6, 0, 1)))
-            ins = ins + f + p + pair
-            specs = specs + [lhs, lhs, rhs, rhs, half, half]
-        return call(
-            attend_grads_kernel, steps, ins, specs, outs, [grad_a, grad_a, grad_b, grad_b]
+            at = self.block(lambda j: jnp.clip(j - 4, 0, 1))
+            columns = pl.BlockSpec((d // 2, d), lambda j: (0, jnp.clip(j - 6, 0, 1)))
+            ins, specs = ins + f + p + pair, specs + [at] * 4 + [columns] * 2
+        return call(
+            attend_grads_kernel, steps, ins, specs,
+            outs, [pl.BlockSpec((d // 4, d), lambda j: (0, j))] * 2,
         )
 
     def feed_forward(self, x, at, row):
@@ -642,16 +656,14 @@
     rows = u_qkv.shape[0]
     x0 = tokens.reshape(-1, d)
     enc = encoder.reshape(-1, d)
-    order = jnp.stack((place.order(d, True), place.order(d, False)))
-    order_pair = order[1]
-    order = order[:, : d // 2]
+    order = place.order(d)
 
     vectors = (u_ag, u_as, u_mg, u_ms, m_ag, m_as, c_g, c_s, m_mg, m_ms)
     vectors = jnp.pad(jnp.stack(vectors, axis=0), ((0, LANES - len(vectors)), (0, 0)))
     parts = (u_qkv, u_out, u_up, u_down, m_qkv, m_out, m_up, m_down, c_q, c_pair, c_out, vectors)
     packed = sds((rows, 28 * d + LANES), bf16)
     shard = call(pack_kernel, 1, parts, [whole(p) for p in parts], packed, whole(packed), vmem=60)
-    enc_t = nt(order_pair, enc).astype(bf16)
+    enc_t = nt(order, enc).astype(bf16)
     w = lax.all_gather(shard, AXES, axis=0, tiled=True)
     w, (order, enc_t) = tie(w, order, enc_t)
     vec = nt(jnp.eye(16, LANES, dtype=bf16), w[:, 28 * d :])
@@ -709,43 +721,46 @@
     dx = go_on(dx, start=[s_ma])
     dx, v_uf, p = net.feed_backward(x0a, (k_uf,), dx, 4, 2)
     p = pairs(p)
-    dx = go_on(dx, [s_ma], [s_ma])
+    dx = go_on(dx, [s_ma])
     dx, (p,) = tie(dx, p)
     s_uf = Sum(place, net.feed_grads(f_uf, p))
     dx = need(dx, s_uf)
-    dx = go_on(dx, [s_mf], [s_uf])
+    dx = go_on(dx, [s_mf], [s_ma, s_uf, s_mf])
     v = [g[:2] for g in (v_uf, v_ms, v_mc, v_mf)]
     v = jnp.pad(jnp.concatenate(v, axis=0), ((2, 6), (0, 0)))
     dx, _v, p = net.self_backward(x0, k_us, dx, 0, 0, (v,))
     p = pairs(p)
-    dx = go_on(dx, [s_ma], [s_mf])
+    dx = go_on(dx, [s_mf, s_ma], [s_mf, s_ma])
     dx, (dkv,) = tie(dx, dkv)
-    denc = nt(dkv, w_pair).astype(bf16)
-    dx, (p, denc) = tie(dx, p, denc)
-    send_a, keep_a, send_b, keep_b = net.attend_grads(f_us, p)
-    v = nt(order[1], plus(p[0][4], p[1][4])[:LANES]).astype(bf16)
-    send_b = jnp.concatenate((send_b, v[d // 4 :]), axis=1)
-    keep_b = jnp.concatenate((keep_b, v[: d // 4]), axis=1)
-    s_us = Sum(place, (send_a, keep_a, send_b, keep_b))
+    denc = net.pair_input(dkv, 25)
+    dx, (denc,) = tie(dx, denc)
+    dx, (p,) = tie(dx, p)
+    send, keep = net.attend_grads(f_us, p)
+    v = nt(order[: d // 2], plus(p[0][4], p[1][4])[:LANES]).astype(bf16)
+    send = jnp.concatenate((send, v[d // 4 :]), axis=1)
+    keep = jnp.concatenate((keep, v[: d // 4]), axis=1)
+    s_us = Sum(place, (send, keep))
     dx = go_on(dx, start=[s_us])
-    dx = rest(dx, s_mf)
+    for _ in range(place.outer_bits - 2):
+        dx = go_on(dx, [s_mf], [s_mf])
     dx = go_on(dx, [s_uf], [s_uf])
+    dx = go_on(dx, [s_us], [s_us])
     dx, (r_mf,) = tie(dx, s_mf.total())
-    dx = go_on(dx, start=[s_ma])
-    dx = go_on(dx, [s_us], [s_us])
     dx = rest(dx, s_ma)
     dx = go_on(dx, [s_uf], [s_uf])
     dx, (r_ma,) = tie(dx, s_ma.total())
     dx = go_on(dx, [s_us], [s_us])
-    dx = rest(dx, s_uf, s_us)
-    r_uf, r_us = s_uf.total(), s_us.total()
-
-    def feed_rows(r):
-        return unspread(r[:, : 4 * d]), r[:, 4 * d :].reshape(-1, d)
+    dx = rest(dx, s_uf)
+    dx, (r_uf,) = tie(dx, s_uf.total())
+    dx = rest(dx, s_us)
+    r_us = s_us.total()
 
     def columns(r, *blocks):
         parts = [r[:, b * d : (b + 1) * d] for b in blocks]
         return jnp.concatenate(parts, axis=1) if len(parts) > 1 else parts[0]
+
+    def feed_rows(r):
+        return unspread(columns(r, 0, 2, 4, 6)), columns(r, 1, 3, 5, 7).reshape(-1, d)
 
     r_uup, r_udown = feed_rows(r_uf)
     r_mup, r_mdown = feed_rows(r_mf)
@@ -756,8 +771,8 @@
         dx.astype(bf16).reshape(tokens.shape),
         denc.reshape(encoder.shape),
         v[0], v[1], r_us[:, : 3 * d], r_us[:, 3 * d : 4 * d], v[2], v[3], r_uup, r_udown,
-        v[4], v[5], columns(r_ma, 0, 1, 4), columns(r_ma, 5), v[6], v[7],
-        columns(r_ma, 2), columns(r_ma, 6, 7), columns(r_ma, 3),
+        v[4], v[5], r_ma[:, : 3 * d], columns(r_ma, 3), v[6], v[7],
+        columns(r_ma, 4), r_ma[:, 6 * d :], columns(r_ma, 5),
         v[8], v[9], r_mup, r_mdown,
     )
 

time: 478 us -> 477 us (level)
  waiting for transfers between devices: 276 us -> 289 us
  other arithmetic: 21 us -> 8.46 us
  Pallas kernels: 101 us -> 113 us
  matrix products: 17.9 us -> 11.3 us
  starting transfers between devices: 24.7 us -> 19.9 us
    ppermute x0 -> x8, waiting for transfers between devices: none -> 54.2 us  [swap_by_core(): return lax.ppermute(x, AXES, pairs)]
    ppermute x35 -> x19, waiting for transfers between devices: 84.3 us -> 41.8 us  [swap(): return lax.ppermute(x, AXES, [(i, i ^ bit) for i in range(self.count)])]
    ppermute x35 -> x19, starting transfers between devices: 24.7 us -> 10.3 us  [swap(): return lax.ppermute(x, AXES, [(i, i ^ bit) for i in range(self.count)])]
    convert_element_type x20 -> x4, other arithmetic: 15.4 us -> 1.88 us  [plus(): return (a.astype(f32) + b.astype(f32)).astype(bf16)]
    pallas_call x16 -> x25, Pallas kernels: 101 us -> 113 us  [call(): pl.pallas_call(kernel, out_shape=outs, grid_spec=pltpu.PrefetchScalarGrid...]
    ppermute x0 -> x8, starting transfers between devices: none -> 9.52 us  [swap_by_core(): return lax.ppermute(x, AXES, pairs)]
    dot_general x4 -> x3, matrix products: 10.1 us -> 4.42 us  [nt(): lax.dot_general(a, b, (((1,), (1,)), ((), ())), preferred_element_type=f32)]
  transfers between devices with their start and end apart: 36 -> 28, of which waited for: 15 -> 12; matrix products, arithmetic and copies ran while one was open for 10% -> 5% of each run, Pallas kernels for 14% -> 17%
where the time goes in v8:
time: 477 us; the launch traced here: 473 us
  waiting for transfers between devices  289 us (61%)
  Pallas kernels  113 us (24%)
  starting transfers between devices  19.9 us (4%)
  local copies, waits for them, and re-layouts  16.4 us (3%)
  between operations  15 us (3%)
  matrix products  11.3 us (2%)
  other arithmetic  8.46 us (2%)
    all_gather x1, waiting for transfers between devices, local(): w = lax.all_gather(shard, AXES, axis=0, tiled=True)  193 us
    pallas_call x25, Pallas kernels, call(): pl.pallas_call(kernel, out_shape=outs, grid_spec=pltpu.PrefetchScalarGrid...  113 us
    ppermute x8, waiting for transfers between devices, swap_by_core(): return lax.ppermute(x, AXES, pairs)  54.2 us
    ppermute x19, waiting for transfers between devices, swap(): return lax.ppermute(x, AXES, [(i, i ^ bit) for i in range(self.count)])  41.8 us
    ppermute x19, starting transfers between devices, swap(): return lax.ppermute(x, AXES, [(i, i ^ bit) for i in range(self.count)])  10.3 us
  transfers between devices with their start and end apart: 28, of which 12 were waited for; matrix products, arithmetic and copies ran while one was open for 5% of the time, Pallas kernels for 17%

profile of v8, /device:TPU:0, one launch (start us, length us, event | category | flops | bytes accessed | tf_op | source)
XLA Modules:
  0.0 473.3 jit_solution(14200112339429888585)
XLA Ops:
  16.5 192.8 %all-gather.2.cloned.1.call-done.w_ref.up_ref.down_ref.k_ref.v_ref = bf16[768,21632]{1,0:T(8,128)(2,1)} async-done(((bf16[24,21632]{1,0:T(8,128)(2,1)}), bf16[768,21632]{1,0:T(8,128)(2,1)}) %all-gather.2.cloned.1.call-update) | async-done | bytes 33226768 | tf_op jit(solution)/shard_map/all_gather | solution.py:667
  210.3 5.1 %shard_map.425 = (f32[128,768]{1,0:T(8,128)S(1)}, bf16[2,128,768]{2,1,0:T(8,128)(2,1)S(1)}, bf16[3,128,768]{2,1,0:T(8,128)(2,1)S(1)}) custom-call(bf16[128,768]{1,0:T(8,128)(2,1)S(1)} %bitcast.37, f32[16,768]{1,0:T(8,128)S(1)} %fusion.15.vec_ref, bf16[768,21632]{1,0:T(8,128)(2,1)} %all-gather.2.cloned.1.call-done.w_ref.up_ref.down_ref.k_ref.v_ref), custom_call_target="tpu_custom_call" | custom-call | flops 1000 | bytes 1000 | tf_op jit(solution)/shard_map/pallas_call | solution.py:477
  216.2 5.9 %shard_map.426 = (f32[128,768]{1,0:T(8,128)S(1)}, bf16[5,128,768]{2,1,0:T(8,128)(2,1)S(1)}, f32[128,3072]{1,0:T(8,128)S(1)}) custom-call(f32[128,768]{1,0:T(8,128)S(1)} %get-tuple-element.188.x_ref, f32[16,768]{1,0:T(8,128)S(1)} %fusion.15.vec_ref, bf16[768,21632]{1,0:T(8,128)(2,1)} %all-gather.2.cloned.1.call-done.w_ref.up_ref.down_ref.k_ref.v_ref, ...), custom_call_target="tpu_custom_call" | custom-call | flops 1000 | bytes 1000 | tf_op jit(solution)/shard_map/pallas_call | solution.py:477
  223.8 4.9 %shard_map.427 = (f32[128,768]{1,0:T(8,128)S(1)}, bf16[2,128,768]{2,1,0:T(8,128)(2,1)S(1)}, bf16[3,128,768]{2,1,0:T(8,128)(2,1)S(1)}) custom-call(f32[128,768]{1,0:T(8,128)S(1)} %get-tuple-element.189.x_ref, f32[16,768]{1,0:T(8,128)S(1)} %fusion.15.vec_ref, bf16[768,21632]{1,0:T(8,128)(2,1)} %all-gather.2.cloned.1.call-done.w_ref.up_ref.down_ref.k_ref.v_ref), custom_call_target="tpu_custom_call" | custom-call | flops 1000 | bytes 1000 | tf_op jit(solution)/shard_map/pallas_call | solution.py:477
  229.0 4.8 %fusion.kv_ref = bf16[1152,1536]{1,0:T(8,128)(2,1)S(1)} fusion(bf16[1152,768]{1,0:T(8,128)(2,1)S(1)} %bitcast.36, bf16[768,21632]{1,0:T(8,128)(2,1)} %all-gather.2.cloned.1.call-done.w_ref.up_ref.down_ref.k_ref.v_ref), kind=kOutput, calls=%fused_computation.1 | convolution fusion | flops 2719678464 | bytes 7667712 | tf_op jit(solution)/shard_map/dot_general | solution.py:108
  233.8 7.5 %shard_map.428 = (f32[128,768]{1,0:T(8,128)S(1)}, bf16[2,128,768]{2,1,0:T(8,128)(2,1)S(1)}, bf16[128,768]{1,0:T(8,128)(2,1)S(1)}) custom-call(s32[2]{0:T(128)S(1)} %copy-done.27, f32[128,768]{1,0:T(8,128)S(1)} %get-tuple-element.190.x_ref, f32[16,768]{1,0:T(8,128)S(1)} %fusion.15.vec_ref, bf16[1152,1536]{1,0:T(8,128)(2,1)S(1)} %fusion.kv_ref, ...), custom_call_target="tpu_custom_call" | custom-call | flops 1000 | bytes 1000 | tf_op jit(solution)/shard_map/pallas_call | solution.py:477
  242.2 7.4 %shard_map.429 = (f32[128,768]{1,0:T(8,128)S(1)}, f32[8,768]{1,0:T(8,128)S(1)}, bf16[5,128,768]{2,1,0:T(8,128)(2,1)S(1)}, bf16[5,128,768]{2,1,0:T(8,128)(2,1)S(1)}) custom-call(f32[128,768]{1,0:T(8,128)S(1)} %get-tuple-element.195.x_ref, f32[16,768]{1,0:T(8,128)S(1)} %fusion.15.vec_ref, bf16[128,768]{1,0:T(8,128)(2,1)S(1)} %bitcast.39, ...), custom_call_target="tpu_custom_call" | custom-call | flops 1000 | bytes 1000 | tf_op jit(solution)/shard_map/pallas_call | solution.py:477
  250.4 4.4 shard_map.430
  254.8 5.2 %shard_map.431 = (bf16[192,6144]{1,0:T(8,128)(2,1)}, bf16[192,6144]{1,0:T(8,128)(2,1)S(1)}) custom-call(bf16[768,768]{1,0:T(8,128)(2,1)S(1)} %fusion.2.order_ref, bf16[5,128,768]{2,1,0:T(8,128)(2,1)S(1)} %get-tuple-element.197.g_ref.b_ref, bf16[5,128,768]{2,1,0:T(8,128)(2,1)S(1)} %collective-permute-done.5.b2_ref.g2_ref, ...), custom_call_target="tpu_custom_call" | custom-call | flops 1000 | bytes 1000 | tf_op jit(solution)/shard_map/pallas_call | solution.py:477
  261.5 10.6 %shard_map.432 = (f32[128,768]{1,0:T(8,128)S(1)}, f32[8,768]{1,0:T(8,128)S(1)}, bf16[2,128,768]{2,1,0:T(8,128)(2,1)S(1)}, bf16[1152,1536]{1,0:T(8,128)(2,1)S(1)}) custom-call(s32[2]{0:T(128)S(1)} %copy-done.27, f32[128,768]{1,0:T(8,128)S(1)} %get-tuple-element.190.x_ref, f32[16,768]{1,0:T(8,128)S(1)} %fusion.15.vec_ref, ...), custom_call_target="tpu_custom_call" | custom-call | flops 1000 | bytes 1000 | tf_op jit(solution)/shard_map/pallas_call | solution.py:477
  272.1 3.8 shard_map.433
  276.0 9.8 %shard_map.434 = (f32[128,768]{1,0:T(8,128)S(1)}, f32[8,768]{1,0:T(8,128)S(1)}, bf16[4,128,768]{2,1,0:T(8,128)(2,1)S(1)}) custom-call(f32[128,768]{1,0:T(8,128)S(1)} %get-tuple-element.189.x_ref, f32[16,768]{1,0:T(8,128)S(1)} %fusion.15.vec_ref, bf16[3,128,768]{2,1,0:T(8,128)(2,1)S(1)} %get-tuple-element.200.qkv_ref, ...), custom_call_target="tpu_custom_call" | custom-call | flops 1000 | bytes 1000 | tf_op jit(solution)/shard_map/pallas_call | solution.py:477
  292.1 6.4 %shard_map.436 = (bf16[192,6144]{1,0:T(8,128)(2,1)S(1)}, bf16[192,6144]{1,0:T(8,128)(2,1)S(1)}) custom-call(bf16[768,768]{1,0:T(8,128)(2,1)S(1)} %fusion.2.order_ref, bf16[2,128,768]{2,1,0:T(8,128)(2,1)S(1)} %copy-done.13, bf16[2,128,768]{2,1,0:T(8,128)(2,1)S(1)} %copy-done.15, bf16[4,128,768]{2,1,0:T(8,128)(2,1)S(1)} %get-tuple-element.230.sd_ref, ...), custom_call_target="tpu_custom_call" | custom-call | flops 1000 | bytes 1000 | tf_op jit(solution)/shard_map/pallas_call | solution.py:477
  300.7 6.8 %shard_map.437 = (f32[128,768]{1,0:T(8,128)S(1)}, f32[8,768]{1,0:T(8,128)S(1)}, bf16[5,128,768]{2,1,0:T(8,128)(2,1)S(1)}) custom-call(f32[128,768]{1,0:T(8,128)S(1)} %get-tuple-element.188.x_ref, f32[16,768]{1,0:T(8,128)S(1)} %fusion.15.vec_ref, f32[128,768]{1,0:T(8,128)S(1)} %get-tuple-element.239.dx_ref, ...), custom_call_target="tpu_custom_call" | custom-call | flops 1000 | bytes 1000 | tf_op jit(solution)/shard_map/pallas_call | solution.py:477
  307.5 32.4 %collective-permute-done.10.got_ref = bf16[192,6144]{1,0:T(8,128)(2,1)S(1)} collective-permute-done((bf16[192,6144]{1,0:T(8,128)(2,1)S(1)}, bf16[192,6144]{1,0:T(8,128)(2,1)S(1)}, u32[]{:S(2)}, u32[]{:S(2)}) %collective-permute-start.10) | collective-permute-done | bytes 2359328 | tf_op jit(solution)/shard_map/ppermute | solution.py:39
  341.0 4.5 shard_map.439
  347.3 10.4 %shard_map.441 = (f32[128,768]{1,0:T(8,128)S(1)}, f32[8,768]{1,0:T(8,128)}, bf16[5,128,768]{2,1,0:T(8,128)(2,1)S(1)}) custom-call(bf16[128,768]{1,0:T(8,128)(2,1)S(1)} %bitcast.38, f32[16,768]{1,0:T(8,128)S(1)} %fusion.15.vec_ref, bf16[3,128,768]{2,1,0:T(8,128)(2,1)S(1)} %copy-done.11, f32[128,768]{1,0:T(8,128)S(1)} %get-tuple-element.265.dx_ref, ...), custom_call_target="tpu_custom_call" | custom-call | flops 1000 | bytes 1000 | tf_op jit(solution)/shard_map/pallas_call | solution.py:477
  363.7 5.8 %shard_map.443 = bf16[1152,768]{1,0:T(8,128)(2,1)} custom-call(bf16[1152,1536]{1,0:T(8,128)(2,1)S(1)} %get-tuple-element.283.dkv_ref, bf16[768,21632]{1,0:T(8,128)(2,1)} %all-gather.2.cloned.1.call-done.w_ref.up_ref.down_ref.k_ref.v_ref, bf16[768,21632]{1,0:T(8,128)(2,1)} %all-gather.2.cloned.1.call-done.w_ref.up_ref.down_ref.k_ref.v_ref), custom_call_target="tpu_custom_call" | custom-call | flops 1000 | bytes 1000 | tf_op jit(solution)/shard_map/pallas_call | solution.py:477
  376.2 11.5 %collective-permute-done.18 = bf16[24,6144]{1,0:T(8,128)(2,1)S(1)} collective-permute-done((bf16[24,6144]{1,0:T(8,128)(2,1)S(1)}, bf16[24,6144]{1,0:T(8,128)(2,1)S(1)}, u32[]{:S(2)}, u32[]{:S(2)}) %collective-permute-start.18) | collective-permute-done | bytes 294944 | tf_op jit(solution)/shard_map/ppermute | solution.py:35
  391.3 17.2 %collective-permute-done.17.got_ref = bf16[192,3200]{1,0:T(8,128)(2,1)S(1)} collective-permute-done((bf16[192,3200]{1,0:T(8,128)(2,1)S(1)}, bf16[192,3200]{1,0:T(8,128)(2,1)S(1)}, u32[]{:S(2)}, u32[]{:S(2)}) %collective-permute-start.17) | collective-permute-done | bytes 1228832 | tf_op jit(solution)/shard_map/ppermute | solution.py:39
  419.8 6.1 %collective-permute-done.21 = bf16[24,6144]{1,0:T(8,128)(2,1)} collective-permute-done((bf16[24,6144]{1,0:T(8,128)(2,1)}, bf16[24,6144]{1,0:T(8,128)(2,1)}, u32[]{:S(2)}, u32[]{:S(2)}) %collective-permute-start.21) | collective-permute-done | bytes 294944 | tf_op jit(solution)/shard_map/ppermute | solution.py:35
  428.0 8.5 %collective-permute-done.23 = bf16[48,6144]{1,0:T(8,128)(2,1)S(1)} collective-permute-done((bf16[48,6144]{1,0:T(8,128)(2,1)S(1)}, bf16[48,6144]{1,0:T(8,128)(2,1)S(1)}, u32[]{:S(2)}, u32[]{:S(2)}) %collective-permute-start.23) | collective-permute-done | bytes 589856 | tf_op jit(solution)/shard_map/ppermute | solution.py:35
  444.7 7.1 %collective-permute-done.24 = bf16[24,6144]{1,0:T(8,128)(2,1)} collective-permute-done((bf16[24,6144]{1,0:T(8,128)(2,1)}, bf16[24,6144]{1,0:T(8,128)(2,1)}, u32[]{:S(2)}, u32[]{:S(2)}) %collective-permute-start.24) | collective-permute-done | bytes 294944 | tf_op jit(solution)/shard_map/ppermute | solution.py:35
  459.8 4.1 collective-permute-done.26
  (184 shorter events, 75.3 us)
Async XLA Ops:
  7.2 202.0 %all-gather.2.cloned.1.call-start = ((), (), s32[]{:S(2)}) async-start(), calls=%async_computation | async-start | bytes 34265088 | tf_op jit(solution)/shard_map/all_gather | solution.py:667
  223.3 18.9 %collective-permute-start.1 = (bf16[5,128,768]{2,1,0:T(8,128)(2,1)S(1)}, bf16[5,128,768]{2,1,0:T(8,128)(2,1)S(1)}, u32[]{:S(2)}, u32[]{:S(2)}) collective-permute-start(bf16[5,128,768]{2,1,0:T(8,128)(2,1)S(1)} %get-tuple-element.251.b_ref.g_ref), channel_id=1, source_target_pairs={{0,2},{1,3},{2,0},{3,1},{4,6},{5,7},{6,4},{7,5},{8,10},{9,11},{10,... | collective-permute-start | bytes 2949128 | tf_op jit(solution)/shard_map/ppermute | solution.py:35
  223.5 17.8 %collective-permute-start = (bf16[2,128,768]{2,1,0:T(8,128)(2,1)S(1)}, bf16[2,128,768]{2,1,0:T(8,128)(2,1)S(1)}, u32[]{:S(2)}, u32[]{:S(2)}) collective-permute-start(bf16[2,128,768]{2,1,0:T(8,128)(2,1)S(1)} %get-tuple-element.287.s_ref), channel_id=1, source_target_pairs={{0,2},{1,3},{2,0},{3,1},{4,6},{5,7},{6,4},{7,5},{8,10},{9,11},{10,... | collective-permute-start | bytes 1179656 | tf_op jit(solution)/shard_map/ppermute | solution.py:35
  228.7 13.5 %collective-permute-start.2 = (bf16[2,128,768]{2,1,0:T(8,128)(2,1)S(1)}, bf16[2,128,768]{2,1,0:T(8,128)(2,1)S(1)}, u32[]{:S(2)}, u32[]{:S(2)}) collective-permute-start(bf16[2,128,768]{2,1,0:T(8,128)(2,1)S(1)} %get-tuple-element.228.s_ref), channel_id=1, source_target_pairs={{0,2},{1,3},{2,0},{3,1},{4,6},{5,7},{6,4},{7,5},{8,10},{9,11},{10,... | collective-permute-start | bytes 1179656 | tf_op jit(solution)/shard_map/ppermute | solution.py:35
  260.1 29.2 %collective-permute-start.6 = (bf16[192,6144]{1,0:T(8,128)(2,1)}, bf16[192,6144]{1,0:T(8,128)(2,1)}, u32[]{:S(2)}, u32[]{:S(2)}) collective-permute-start(bf16[192,6144]{1,0:T(8,128)(2,1)} %get-tuple-element.217), channel_id=1, source_target_pairs={{0,4},{1,5},{2,3},{3,2},{4,0},{5,1},{6,7},{7,6},{8,12},{9,13},{10,... | collective-permute-start | bytes 7077896 | tf_op jit(solution)/shard_map/ppermute | solution.py:39
  276.0 16.1 %collective-permute-start.9 = (bf16[384,1536]{1,0:T(8,128)(2,1)S(1)}, bf16[384,1536]{1,0:T(8,128)(2,1)S(1)}, u32[]{:S(2)}, u32[]{:S(2)}) collective-permute-start(bf16[384,1536]{1,0:T(8,128)(2,1)S(1)} %get-tuple-element.226), channel_id=1, source_target_pairs={{0,2},{1,3},{2,0},{3,1},{4,6},{5,7},{6,4},{7,5},{8,10},{9,11},{10,... | collective-permute-start | bytes 3538952 | tf_op jit(solution)/shard_map/ppermute | solution.py:35
  285.8 6.2 %collective-permute-start.7 = (bf16[4,128,768]{2,1,0:T(8,128)(2,1)S(1)}, bf16[4,128,768]{2,1,0:T(8,128)(2,1)S(1)}, u32[]{:S(2)}, u32[]{:S(2)}) collective-permute-start(bf16[4,128,768]{2,1,0:T(8,128)(2,1)S(1)} %get-tuple-element.230.sd_ref), channel_id=1, source_target_pairs={{0,2},{1,3},{2,0},{3,1},{4,6},{5,7},{6,4},{7,5},{8,10},{9,11},{10,... | collective-permute-start | bytes 2359304 | tf_op jit(solution)/shard_map/ppermute | solution.py:35
  298.6 41.4 %collective-permute-start.10 = (bf16[192,6144]{1,0:T(8,128)(2,1)S(1)}, bf16[192,6144]{1,0:T(8,128)(2,1)S(1)}, u32[]{:S(2)}, u32[]{:S(2)}) collective-permute-start(bf16[192,6144]{1,0:T(8,128)(2,1)S(1)} %get-tuple-element.243), channel_id=1, source_target_pairs={{0,4},{1,5},{2,3},{3,2},{4,0},{5,1},{6,7},{7,6},{8,12},{9,13},{10,... | collective-permute-start | bytes 7077896 | tf_op jit(solution)/shard_map/ppermute | solution.py:39
  300.1 45.4 %collective-permute-start.12 = (bf16[96,6144]{1,0:T(8,128)(2,1)}, bf16[96,6144]{1,0:T(8,128)(2,1)S(1)}, u32[]{:S(2)}, u32[]{:S(2)}) collective-permute-start(bf16[96,6144]{1,0:T(8,128)(2,1)} %get-tuple-element.258), channel_id=1, source_target_pairs={{0,1},{1,0},{2,6},{3,7},{4,5},{5,4},{6,2},{7,3},{8,9},{9,8},{10,14... | collective-permute-start | bytes 3538952 | tf_op jit(solution)/shard_map/ppermute | solution.py:39
  307.4 33.6 %collective-permute-start.11 = (bf16[5,128,768]{2,1,0:T(8,128)(2,1)S(1)}, bf16[5,128,768]{2,1,0:T(8,128)(2,1)S(1)}, u32[]{:S(2)}, u32[]{:S(2)}) collective-permute-start(bf16[5,128,768]{2,1,0:T(8,128)(2,1)S(1)} %get-tuple-element.253.z_ref.u_ref), channel_id=1, source_target_pairs={{0,2},{1,3},{2,0},{3,1},{4,6},{5,7},{6,4},{7,5},{8,10},{9,11},{10,... | collective-permute-start | bytes 2949128 | tf_op jit(solution)/shard_map/ppermute | solution.py:35
  346.1 17.0 %collective-permute-start.14 = (bf16[96,6144]{1,0:T(8,128)(2,1)S(1)}, bf16[96,6144]{1,0:T(8,128)(2,1)S(1)}, u32[]{:S(2)}, u32[]{:S(2)}) collective-permute-start(bf16[96,6144]{1,0:T(8,128)(2,1)S(1)} %get-tuple-element.274), channel_id=1, source_target_pairs={{0,1},{1,0},{2,6},{3,7},{4,5},{5,4},{6,2},{7,3},{8,9},{9,8},{10,14... | collective-permute-start | bytes 3538952 | tf_op jit(solution)/shard_map/ppermute | solution.py:39
  346.7 14.5 %collective-permute-start.13 = (bf16[48,6144]{1,0:T(8,128)(2,1)S(1)}, bf16[48,6144]{1,0:T(8,128)(2,1)S(1)}, u32[]{:S(2)}, u32[]{:S(2)}) collective-permute-start(bf16[48,6144]{1,0:T(8,128)(2,1)S(1)} %get-tuple-element.272), channel_id=1, source_target_pairs={{0,8},{1,9},{2,10},{3,11},{4,12},{5,13},{6,14},{7,15},{8,0},{9,1},... | collective-permute-start | bytes 1769480 | tf_op jit(solution)/shard_map/ppermute | solution.py:35
  358.5 11.1 %collective-permute-start.15 = (bf16[5,128,768]{2,1,0:T(8,128)(2,1)S(1)}, bf16[5,128,768]{2,1,0:T(8,128)(2,1)S(1)}, u32[]{:S(2)}, u32[]{:S(2)}) collective-permute-start(bf16[5,128,768]{2,1,0:T(8,128)(2,1)S(1)} %get-tuple-element.289.sd_ref), channel_id=1, source_target_pairs={{0,2},{1,3},{2,0},{3,1},{4,6},{5,7},{6,4},{7,5},{8,10},{9,11},{10,... | collective-permute-start | bytes 2949128 | tf_op jit(solution)/shard_map/ppermute | solution.py:35
  358.5 29.3 %collective-permute-start.16 = (bf16[192,6144]{1,0:T(8,128)(2,1)S(1)}, bf16[192,6144]{1,0:T(8,128)(2,1)S(1)}, u32[]{:S(2)}, u32[]{:S(2)}) collective-permute-start(bf16[192,6144]{1,0:T(8,128)(2,1)S(1)} %get-tuple-element.294), channel_id=1, source_target_pairs={{0,4},{1,5},{2,3},{3,2},{4,0},{5,1},{6,7},{7,6},{8,12},{9,13},{10,... | collective-permute-start | bytes 7077896 | tf_op jit(solution)/shard_map/ppermute | solution.py:39
  374.2 13.5 %collective-permute-start.18 = (bf16[24,6144]{1,0:T(8,128)(2,1)S(1)}, bf16[24,6144]{1,0:T(8,128)(2,1)S(1)}, u32[]{:S(2)}, u32[]{:S(2)}) collective-permute-start(bf16[24,6144]{1,0:T(8,128)(2,1)S(1)} %add_convert_fusion.5), channel_id=1, source_target_pairs={{0,16},{1,17},{2,18},{3,19},{4,20},{5,21},{6,22},{7,23},{8,24},{9,... | collective-permute-start | bytes 884744 | tf_op jit(solution)/shard_map/ppermute | solution.py:35
  375.4 33.4 %collective-permute-start.19 = (bf16[48,6144]{1,0:T(8,128)(2,1)S(1)}, bf16[48,6144]{1,0:T(8,128)(2,1)S(1)}, u32[]{:S(2)}, u32[]{:S(2)}) collective-permute-start(bf16[48,6144]{1,0:T(8,128)(2,1)S(1)} %get-tuple-element.310), channel_id=1, source_target_pairs={{0,8},{1,9},{2,10},{3,11},{4,12},{5,13},{6,14},{7,15},{8,0},{9,1},... | collective-permute-start | bytes 1769480 | tf_op jit(solution)/shard_map/ppermute | solution.py:35
  375.6 32.9 %collective-permute-start.17 = (bf16[192,3200]{1,0:T(8,128)(2,1)S(1)}, bf16[192,3200]{1,0:T(8,128)(2,1)S(1)}, u32[]{:S(2)}, u32[]{:S(2)}) collective-permute-start(bf16[192,3200]{1,0:T(8,128)(2,1)S(1)} %pad_maximum_fusion), channel_id=1, source_target_pairs={{0,4},{1,5},{2,3},{3,2},{4,0},{5,1},{6,7},{7,6},{8,12},{9,13},{10,... | collective-permute-start | bytes 3686408 | tf_op jit(solution)/shard_map/ppermute | solution.py:39
  389.7 27.8 %collective-permute-start.20 = (bf16[96,6144]{1,0:T(8,128)(2,1)}, bf16[96,6144]{1,0:T(8,128)(2,1)S(1)}, u32[]{:S(2)}, u32[]{:S(2)}) collective-permute-start(bf16[96,6144]{1,0:T(8,128)(2,1)} %get-tuple-element.316), channel_id=1, source_target_pairs={{0,1},{1,0},{2,6},{3,7},{4,5},{5,4},{6,2},{7,3},{8,9},{9,8},{10,14... | collective-permute-start | bytes 3538952 | tf_op jit(solution)/shard_map/ppermute | solution.py:39
  409.7 16.2 %collective-permute-start.21 = (bf16[24,6144]{1,0:T(8,128)(2,1)}, bf16[24,6144]{1,0:T(8,128)(2,1)}, u32[]{:S(2)}, u32[]{:S(2)}) collective-permute-start(bf16[24,6144]{1,0:T(8,128)(2,1)} %add_convert_fusion.3), channel_id=1, source_target_pairs={{0,16},{1,17},{2,18},{3,19},{4,20},{5,21},{6,22},{7,23},{8,24},{9,... | collective-permute-start | bytes 884744 | tf_op jit(solution)/shard_map/ppermute | solution.py:35
  414.7 13.1 %collective-permute-start.22 = (bf16[96,3200]{1,0:T(8,128)(2,1)}, bf16[96,3200]{1,0:T(8,128)(2,1)S(1)}, u32[]{:S(2)}, u32[]{:S(2)}) collective-permute-start(bf16[96,3200]{1,0:T(8,128)(2,1)} %copy-done.28), channel_id=1, source_target_pairs={{0,1},{1,0},{2,6},{3,7},{4,5},{5,4},{6,2},{7,3},{8,9},{9,8},{10,14... | collective-permute-start | bytes 1843208 | tf_op jit(solution)/shard_map/ppermute | solution.py:39
  418.2 18.3 %collective-permute-start.23 = (bf16[48,6144]{1,0:T(8,128)(2,1)S(1)}, bf16[48,6144]{1,0:T(8,128)(2,1)S(1)}, u32[]{:S(2)}, u32[]{:S(2)}) collective-permute-start(bf16[48,6144]{1,0:T(8,128)(2,1)S(1)} %get-tuple-element.332), channel_id=1, source_target_pairs={{0,8},{1,9},{2,10},{3,11},{4,12},{5,13},{6,14},{7,15},{8,0},{9,1},... | collective-permute-start | bytes 1769480 | tf_op jit(solution)/shard_map/ppermute | solution.py:35
  437.4 14.4 %collective-permute-start.24 = (bf16[24,6144]{1,0:T(8,128)(2,1)}, bf16[24,6144]{1,0:T(8,128)(2,1)}, u32[]{:S(2)}, u32[]{:S(2)}) collective-permute-start(bf16[24,6144]{1,0:T(8,128)(2,1)} %add_convert_fusion.1), channel_id=1, source_target_pairs={{0,16},{1,17},{2,18},{3,19},{4,20},{5,21},{6,22},{7,23},{8,24},{9,... | collective-permute-start | bytes 884744 | tf_op jit(solution)/shard_map/ppermute | solution.py:35
  441.6 14.4 %collective-permute-start.25 = (bf16[48,3200]{1,0:T(8,128)(2,1)S(1)}, bf16[48,3200]{1,0:T(8,128)(2,1)S(1)}, u32[]{:S(2)}, u32[]{:S(2)}) collective-permute-start(bf16[48,3200]{1,0:T(8,128)(2,1)S(1)} %get-tuple-element.340), channel_id=1, source_target_pairs={{0,8},{1,9},{2,10},{3,11},{4,12},{5,13},{6,14},{7,15},{8,0},{9,1},... | collective-permute-start | bytes 921608 | tf_op jit(solution)/shard_map/ppermute | solution.py:35
  456.7 7.2 %collective-permute-start.26 = (bf16[24,3200]{1,0:T(8,128)(2,1)S(1)}, bf16[24,3200]{1,0:T(8,128)(2,1)S(1)}, u32[]{:S(2)}, u32[]{:S(2)}) collective-permute-start(bf16[24,3200]{1,0:T(8,128)(2,1)S(1)} %add_convert_fusion.8), channel_id=1, source_target_pairs={{0,16},{1,17},{2,18},{3,19},{4,20},{5,21},{6,22},{7,23},{8,24},{9,... | collective-permute-start | bytes 460808 | tf_op jit(solution)/shard_map/ppermute | solution.py:35
  (42 other events, 503.2 us)
Sparse Core Ops, SparseCore 0:
  13.2 195.9 all-gather.1

commit v9 on v8

--- a/solution.py
+++ b/solution.py
@@ -83,6 +83,26 @@
 
     def total(self):
         return self.kept.astype(f32) + self.got.astype(f32)
+
+
+class Gather:
+    def __init__(self, place, shard):
+        self.place, self.x, self.stage = place, shard, 0
+
+    def swap(self):
+        outer = self.place.outer_bits
+        at = self.stage - outer
+        if at < 0:
+            self.got = self.place.swap(self.x, 8 << (outer - 1 - self.stage))
+        elif at < 2:
+            bits = ((BIT_PAIR, BIT_NEAR), (BIT_NEAR, BIT_PAIR))[at]
+            self.got = self.place.swap_by_core(self.x, bits)
+        else:
+            self.got = self.place.swap(self.x, BIT_CORE)
+
+    def join(self):
+        self.x = jnp.concatenate((self.x, self.got), axis=0)
+        self.stage += 1
 
 
 def tie(x, *others):
@@ -326,24 +346,23 @@
     y_ref[...] += nn(g, down_ref[...])
 
 
-def feed_backward_kernel(row, kept, x_ref, vec_ref, dx_ref, up_ref, down_ref, *refs):
-    out_ref, vg_ref, p_ref = refs[1:4] if kept else refs[:3]
-    acc_ref = refs[-1]
+def gelu_terms(u):
+    t = jnp.tanh(GELU_A * (u + GELU_B * u * u * u))
+    slope = 0.5 * (1.0 + t) + 0.5 * u * (1.0 - t * t) * GELU_A * (1.0 + 3.0 * GELU_B * u * u)
+    return 0.5 * u * (1.0 + t), slope
+
+
+def feed_backward_kernel(
+    row, x_ref, vec_ref, dx_ref, up_ref, down_ref, u_ref, out_ref, vg_ref, p_ref, acc_ref
+):
     j = pl.program_id(0)
 
     @pl.when(j == 0)
     def _():
-        if not kept:
-            unit, _inv = unit_norm(x_ref[...])
-            refs[3][0] = (unit * vec_ref[row : row + 1] + vec_ref[row + 1 : row + 2]).astype(bf16)
         p_ref[0] = dx_ref[...].astype(bf16)
         acc_ref[...] = jnp.zeros_like(acc_ref)
 
-    u = refs[0][...] if kept else nn(refs[3][0], up_ref[...])
-    t = jnp.tanh(GELU_A * (u + GELU_B * u * u * u))
-    if not kept:
-        refs[3][1 + j] = (0.5 * u * (1.0 + t)).astype(bf16)
-    slope = 0.5 * (1.0 + t) + 0.5 * u * (1.0 - t * t) * GELU_A * (1.0 + 3.0 * GELU_B * u * u)
+    slope = gelu_terms(u_ref[...])[1]
     du = (slope * nt(p_ref[0], down_ref[...])).astype(bf16)
     p_ref[1 + j] = du
     acc_ref[...] += nt(du, up_ref[...])
@@ -351,19 +370,60 @@
     @pl.when(j == 3)
     def _():
         dn, gg, gs = norm_backward(acc_ref[...], x_ref[...], vec_ref[row : row + 1])
+        out_ref[...] = dx_ref[...] + dn
+        vg_ref[0:1] = gg
+        vg_ref[1:2] = gs
+
+
+def by_rows(x, order_ref, top_ref, low_ref):
+    half = top_ref.shape[0]
+    x = nt(x, order_ref[...]).astype(bf16)
+    return nn(x[:, :half], top_ref[...]) + nn(x[:, half:], low_ref[...])
+
+
+def last_backward_kernel(
+    row, x_ref, vec_ref, order_ref, dx_ref, up_ref, up2_ref, down_ref, down2_ref,
+    out_ref, vg_ref, p_ref, f_ref, acc_ref,
+):
+    j = pl.program_id(0)
+    half = up_ref.shape[0]
+
+    @pl.when(j == 0)
+    def _():
+        unit, _inv = unit_norm(x_ref[...])
+        f_ref[0] = (unit * vec_ref[row : row + 1] + vec_ref[row + 1 : row + 2]).astype(bf16)
+        p_ref[0] = dx_ref[...]
+        acc_ref[...] = jnp.zeros_like(acc_ref)
+
+    g, slope = gelu_terms(by_rows(f_ref[0], order_ref, up_ref, up2_ref))
+    f_ref[1 + j] = g.astype(bf16)
+    dz = p_ref[0]
+    dg = jnp.concatenate((nt(dz, down_ref[...]), nt(dz, down2_ref[...])), axis=1)
+    du = (slope * nn(dg.astype(bf16), order_ref[...])).astype(bf16)
+    p_ref[1 + j] = du
+    acc_ref[:, :half] += nt(du, up_ref[...])
+    acc_ref[:, half:] += nt(du, up2_ref[...])
+
+    @pl.when(j == 3)
+    def _():
+        db = acc_ref[...]
+        high = db.astype(bf16)
+        low = (db - high.astype(f32)).astype(bf16)
+        db = nn(high, order_ref[...]) + nn(low, order_ref[...])
+        dn, gg, gs = norm_backward(db, x_ref[...], vec_ref[row : row + 1])
         out_ref[...] = dx_ref[...].astype(f32) + dn
         vg_ref[0:1] = gg
         vg_ref[1:2] = gs
 
 
-def feed_out_kernel(x_ref, g_ref, down_ref, y_ref, acc_ref):
+def last_output_kernel(x_ref, order_ref, g_ref, down_ref, down2_ref, y_ref, acc_ref):
     j = pl.program_id(0)
 
     @pl.when(j == 0)
     def _():
         acc_ref[...] = x_ref[...]
 
-    acc_ref[...] += nn(g_ref[0], down_ref[...])
+    acc_ref[...] += by_rows(g_ref[0], order_ref, down_ref, down2_ref)
 
     @pl.when(j == 3)
     def _():
@@ -442,31 +502,35 @@
     emit(nn(enc_ref[...], dkv_ref[...]), send_ref, keep_ref)
 
 
-def pack_kernel(u_qkv, u_out, u_up, u_down, m_qkv, m_out, m_up, m_down, c_q, c_pair, c_out, vec, out):
+def pack_kernel(u_qkv, u_out, u_up, u_down, m_qkv, m_out, m_up, m_down, c_q, c_pair, c_out, vec, out, feed_out):
     rows, d = u_out.shape
     spread = spread_matrix().astype(bf16)
     i = lax.broadcasted_iota(jnp.int32, (rows, 4 * rows), 0)
     k = lax.broadcasted_iota(jnp.int32, (rows, 4 * rows), 1)
 
-    def layer(at, qkv, w_out, up, down):
+    def attend(at, qkv, w_out):
         out[:, at : at + 3 * d] = qkv[...]
         out[:, at + 3 * d : at + 4 * d] = w_out[...]
+
+    def feed(out, at, up, down):
         for b in range(4 * d // 512):
             y = nn(up[:, b * 512 : (b + 1) * 512], spread).astype(bf16)
             for j in range(4):
-                to = at + (4 + j) * d + b * LANES
+                to = at + j * d + b * LANES
                 out[:, to : to + LANES] = y[:, j * LANES : (j + 1) * LANES]
         for j in range(4):
             y = nn((k == 4 * i + j).astype(bf16), down[...])
-            out[:, at + (8 + j) * d : at + (9 + j) * d] = y.astype(bf16)
-
-    layer(0, u_qkv, u_out, u_up, u_down)
-    layer(12 * d, m_qkv, m_out, m_up, m_down)
-    out[:, 24 * d : 25 * d] = c_q[...]
-    out[:, 25 * d : 27 * d] = c_pair[...]
-    out[:, 27 * d : 28 * d] = c_out[...]
+            out[:, at + (4 + j) * d : at + (5 + j) * d] = y.astype(bf16)
+
+    feed(feed_out, 0, m_up, m_down)
+    attend(0, u_qkv, u_out)
+    feed(out, 4 * d, u_up, u_down)
+    attend(12 * d, m_qkv, m_out)
+    out[:, 16 * d : 17 * d] = c_q[...]
+    out[:, 17 * d : 19 * d] = c_pair[...]
+    out[:, 19 * d : 20 * d] = c_out[...]
     eye = lax.broadcasted_iota(jnp.int32, (rows, rows), 0) == lax.broadcasted_iota(jnp.int32, (rows, rows), 1)
-    out[:, 28 * d :] = nt(eye.astype(bf16), vec[...]).astype(bf16)
+    out[:, 20 * d :] = nt(eye.astype(bf16), vec[...]).astype(bf16)
 
 
 def whole(x):
@@ -606,26 +670,39 @@
             outs, [whole(outs[0]), whole(outs[1]), pl.BlockSpec((t, d), lambda j: (0, j))],
         )
 
-    def feed_backward(self, x, kept, dx, at, row):
+    def feed_backward(self, x, u, dx, at, row):
         d, t = self.d, self.t
         outs = (self.xs, sds((8, d), f32), sds((5, t, d), bf16))
-        if not kept:
-            outs = outs + (sds((5, t, d), bf16),)
-        return call(
-            functools.partial(feed_backward_kernel, row, bool(kept)), 4,
-            (x, self.vec, dx, self.w, self.w) + kept,
+        return call(
+            functools.partial(feed_backward_kernel, row), 4,
+            (x, self.vec, dx, self.w, self.w, u),
             [
                 whole(x), whole(self.vec), whole(dx),
                 self.weight(lambda j: at + j), self.weight(lambda j: at + 4 + j),
-            ] + [pl.BlockSpec((t, d), lambda j: (0, j)) for _ in kept],
+                pl.BlockSpec((t, d), lambda j: (0, j)),
+            ],
             outs, [whole(i) for i in outs],
             scratch=[pltpu.VMEM((t, d), f32)],
         )
 
-    def feed_out(self, x, p, at):
-        return call(
-            feed_out_kernel, 4, (x, p, self.w),
-            [whole(x), self.block(lambda j: 1 + j), self.weight(lambda j: at + 4 + j)],
+    def last_backward(self, x, dx, w, row):
+        d, t = self.d, self.t
+        outs = (self.xs, sds((8, d), f32)) + (sds((5, t, d), bf16),) * 2
+        ins = (x, self.vec, self.order, dx)
+        up = pl.BlockSpec((d // 2, d), lambda j: (0, j))
+        down = pl.BlockSpec((d // 2, d), lambda j: (0, 4 + j))
+        return call(
+            functools.partial(last_backward_kernel, row), 4,
+            ins + w + w, [whole(i) for i in ins] + [up, up, down, down],
+            outs, [whole(i) for i in outs],
+            scratch=[pltpu.VMEM((t, d), f32)],
+        )
+
+    def last_output(self, x, f, w):
+        down = pl.BlockSpec((self.d // 2, self.d), lambda j: (0, 4 + j))
+        return call(
+            last_output_kernel, 4, (x, self.order, f) + w,
+            [whole(x), whole(self.order), self.block(lambda j: 1 + j), down, down],
             self.hs, whole(self.hs), scratch=[pltpu.VMEM((self.t, self.d), f32)],
         )
 
@@ -661,21 +738,30 @@
     vectors = (u_ag, u_as, u_mg, u_ms, m_ag, m_as, c_g, c_s, m_mg, m_ms)
     vectors = jnp.pad(jnp.stack(vectors, axis=0), ((0, LANES - len(vectors)), (0, 0)))
     parts = (u_qkv, u_out, u_up, u_down, m_qkv, m_out, m_up, m_down, c_q, c_pair, c_out, vectors)
-    packed = sds((rows, 28 * d + LANES), bf16)
-    shard = call(pack_kernel, 1, parts, [whole(p) for p in parts], packed, whole(packed), vmem=60)
+    packed = sds((rows, 20 * d + LANES), bf16), sds((rows, 8 * d), bf16)
+    shard, last = call(
+        pack_kernel, 1, parts, [whole(p) for p in parts], packed, [whole(p) for p in packed], vmem=60
+    )
     enc_t = nt(order, enc).astype(bf16)
     w = lax.all_gather(shard, AXES, axis=0, tiled=True)
-    w, (order, enc_t) = tie(w, order, enc_t)
-    vec = nt(jnp.eye(16, LANES, dtype=bf16), w[:, 28 * d :])
+
+    last = Gather(place, last)
+    for _ in range(place.outer_bits + 2):
+        last.swap()
+        last.join()
+    w, (order, enc_t, last.x) = tie(w, order, enc_t, last.x)
+    last.swap()
+    vec = nt(jnp.eye(16, LANES, dtype=bf16), w[:, 20 * d :])
 
     net = Layers(captions, captions * length, d, w, vec, order, patch_count)
 
-    w_pair = w[:, 25 * d : 27 * d]
-    kv = nn(enc, w_pair).astype(bf16)
+    kv = nn(enc, w[:, 17 * d : 19 * d]).astype(bf16)
     x0a, f_us, k_us = net.self_forward(x0, 0, 0)
     x1, f_uf, k_uf = net.feed_forward(x0a, 4, 2)
     x1a, f_ms, k_ms = net.self_forward(x1, 12, 4)
-    x1b, f_mc, k_mc = net.cross_forward(x1a, kv, 24, 6)
+    x1a, (last.x, last.got) = tie(x1a, last.x, last.got)
+    w_last = last.x, last.got
+    x1b, f_mc, k_mc = net.cross_forward(x1a, kv, 16, 6)
 
     def core(x):
         return place.swap(x, BIT_CORE)
@@ -701,14 +787,14 @@
     f_us, f_uf, f_ms = pairs(f_us), pairs(f_uf), pairs(f_ms)
     x1b, (f_us, f_uf, f_ms) = tie(x1b, f_us, f_uf, f_ms)
     f_mc = pairs(f_mc)
-    dx, v_mf, p, f = net.feed_backward(x1b, (), out_grad.reshape(-1, d), 16, 8)
+    dx, v_mf, p, f = net.last_backward(x1b, out_grad.reshape(-1, d), w_last, 8)
     p, f = pairs(p), pairs(f)
-    x2 = net.feed_out(x1b, f[0], 16)
+    x2 = net.last_output(x1b, f[0], w_last)
     p, (x2,) = tie(p, x2)
     s_mf = Sum(place, net.feed_grads(f, p))
     dx, (f_mc,) = tie(dx, f_mc)
     dx = go_on(dx, start=[s_mf])
-    dx, v_mc, p_c, dkv = net.cross_backward(x1a, k_mc, kv, dx, 24, 6)
+    dx, v_mc, p_c, dkv = net.cross_backward(x1a, k_mc, kv, dx, 16, 6)
     p_c = pairs(p_c)
     pair, send = net.pair_grads(enc_t, dkv)
     dx, (send,) = tie(dx, send)
@@ -719,38 +805,37 @@
     dx, (p, p_c, pair) = tie(dx, p, p_c, pair)
     s_ma = Sum(place, net.attend_grads(f_ms, p, (f_mc, p_c, pair)))
     dx = go_on(dx, start=[s_ma])
-    dx, v_uf, p = net.feed_backward(x0a, (k_uf,), dx, 4, 2)
+    dx, v_uf, p = net.feed_backward(x0a, k_uf, dx, 4, 2)
     p = pairs(p)
-    dx = go_on(dx, [s_ma])
     dx, (p,) = tie(dx, p)
     s_uf = Sum(place, net.feed_grads(f_uf, p))
     dx = need(dx, s_uf)
-    dx = go_on(dx, [s_mf], [s_ma, s_uf, s_mf])
     v = [g[:2] for g in (v_uf, v_ms, v_mc, v_mf)]
     v = jnp.pad(jnp.concatenate(v, axis=0), ((2, 6), (0, 0)))
     dx, _v, p = net.self_backward(x0, k_us, dx, 0, 0, (v,))
     p = pairs(p)
-    dx = go_on(dx, [s_mf, s_ma], [s_mf, s_ma])
+    dx = go_on(dx, [s_mf], [s_uf, s_mf])
+    dx = go_on(dx, [s_ma], [s_ma])
     dx, (dkv,) = tie(dx, dkv)
-    denc = net.pair_input(dkv, 25)
+    denc = net.pair_input(dkv, 17)
     dx, (denc,) = tie(dx, denc)
+    dx = rest(dx, s_mf)
     dx, (p,) = tie(dx, p)
     send, keep = net.attend_grads(f_us, p)
     v = nt(order[: d // 2], plus(p[0][4], p[1][4])[:LANES]).astype(bf16)
     send = jnp.concatenate((send, v[d // 4 :]), axis=1)
     keep = jnp.concatenate((keep, v[: d // 4]), axis=1)
     s_us = Sum(place, (send, keep))
-    dx = go_on(dx, start=[s_us])
-    for _ in range(place.outer_bits - 2):
-        dx = go_on(dx, [s_mf], [s_mf])
-    dx = go_on(dx, [s_uf], [s_uf])
-    dx = go_on(dx, [s_us], [s_us])
+    dx = need(dx, s_us)
+    dx = go_on(dx, [s_ma], [s_ma])
+    dx = go_on(dx, [s_uf], [s_uf, s_us])
     dx, (r_mf,) = tie(dx, s_mf.total())
     dx = rest(dx, s_ma)
     dx = go_on(dx, [s_uf], [s_uf])
+    dx = go_on(dx, [s_us], [s_us])
     dx, (r_ma,) = tie(dx, s_ma.total())
+    dx = rest(dx, s_uf)
     dx = go_on(dx, [s_us], [s_us])
-    dx = rest(dx, s_uf)
     dx, (r_uf,) = tie(dx, s_uf.total())
     dx = rest(dx, s_us)
     r_us = s_us.total()

time: 477 us -> 458 us (0.960)
  waiting for transfers between devices: 289 us -> 234 us
  local copies, waits for them, and re-layouts: 16.4 us -> 27.1 us
  starting transfers between devices: 19.9 us -> 30.5 us
  Pallas kernels: 113 us -> 121 us
  other arithmetic: 8.46 us -> 14.9 us
    all_gather x1, waiting for transfers between devices: 193 us -> 56.2 us  [local(): w = lax.all_gather(shard, AXES, axis=0, tiled=True)]
    ppermute x8 -> x10, waiting for transfers between devices: 54.2 us -> 112 us  [swap_by_core(): return lax.ppermute(x, AXES, pairs)]
    ppermute x19 -> x22, waiting for transfers between devices: 41.8 us -> 65.4 us  [swap(): return lax.ppermute(x, AXES, [(i, i ^ bit) for i in range(self.count)])]
    ppermute x19 -> x22, starting transfers between devices: 10.3 us -> 19.1 us  [swap(): return lax.ppermute(x, AXES, [(i, i ^ bit) for i in range(self.count)])]
    pallas_call x25, Pallas kernels: 113 us -> 121 us  [call(): pl.pallas_call(kernel, out_shape=outs, grid_spec=pltpu.PrefetchScalarGrid...]
    unnamed x76 -> x102, local copies, waits for them, and re-layouts: 4.43 us -> 10.7 us
    ppermute x8 -> x10, starting transfers between devices: 9.52 us -> 11.4 us  [swap_by_core(): return lax.ppermute(x, AXES, pairs)]
  transfers between devices with their start and end apart: 28 -> 33, of which waited for: 12 -> 16; matrix products, arithmetic and copies ran while one was open for 5% -> 9% of each run, Pallas kernels for 17% -> 21%
where the time goes in v9:
time: 458 us; the launch traced here: 453 us
  waiting for transfers between devices  234 us (51%)
  Pallas kernels  121 us (26%)
  starting transfers between devices  30.5 us (7%)
  local copies, waits for them, and re-layouts  27.1 us (6%)
  between operations  15 us (3%)
  other arithmetic  14.9 us (3%)
  matrix products  11.3 us (2%)
    pallas_call x25, Pallas kernels, call(): pl.pallas_call(kernel, out_shape=outs, grid_spec=pltpu.PrefetchScalarGrid...  121 us
    ppermute x10, waiting for transfers between devices, swap_by_core(): return lax.ppermute(x, AXES, pairs)  112 us
    ppermute x22, waiting for transfers between devices, swap(): return lax.ppermute(x, AXES, [(i, i ^ bit) for i in range(self.count)])  65.4 us
    all_gather x1, waiting for transfers between devices, local(): w = lax.all_gather(shard, AXES, axis=0, tiled=True)  56.2 us
    ppermute x22, starting transfers between devices, swap(): return lax.ppermute(x, AXES, [(i, i ^ bit) for i in range(self.count)])  19.1 us
    ppermute x10, starting transfers between devices, swap_by_core(): return lax.ppermute(x, AXES, pairs)  11.4 us
    unnamed x102, local copies, waits for them, and re-layouts  10.7 us
  transfers between devices with their start and end apart: 33, of which 16 were waited for; matrix products, arithmetic and copies ran while one was open for 9% of the time, Pallas kernels for 21%

profile of v9, /device:TPU:0, one launch (start us, length us, event | category | flops | bytes accessed | tf_op | source)
XLA Modules:
  0.0 453.2 jit_solution(17486569937555062041)
XLA Ops:
  17.1 20.1 %collective-permute-done = bf16[24,6144]{1,0:T(8,128)(2,1)S(1)} collective-permute-done((bf16[24,6144]{1,0:T(8,128)(2,1)}, bf16[24,6144]{1,0:T(8,128)(2,1)S(1)}, u32[]{:S(2)}, u32[]{:S(2)}) %collective-permute-start) | collective-permute-done | bytes 294944 | tf_op jit(solution)/shard_map/ppermute | solution.py:35
  42.3 19.9 %collective-permute-done.1 = bf16[48,6144]{1,0:T(8,128)(2,1)S(1)} collective-permute-done((bf16[48,6144]{1,0:T(8,128)(2,1)S(1)}, bf16[48,6144]{1,0:T(8,128)(2,1)S(1)}, u32[]{:S(2)}, u32[]{:S(2)}) %collective-permute-start.1) | collective-permute-done | bytes 589856 | tf_op jit(solution)/shard_map/ppermute | solution.py:35
  67.1 14.4 %collective-permute-done.2 = bf16[96,6144]{1,0:T(8,128)(2,1)} collective-permute-done((bf16[96,6144]{1,0:T(8,128)(2,1)}, bf16[96,6144]{1,0:T(8,128)(2,1)}, u32[]{:S(2)}, u32[]{:S(2)}) %collective-permute-start.2) | collective-permute-done | bytes 1179680 | tf_op jit(solution)/shard_map/ppermute | solution.py:39
  91.8 47.1 %collective-permute-done.3 = bf16[192,6144]{1,0:T(8,128)(2,1)S(1)} collective-permute-done((bf16[192,6144]{1,0:T(8,128)(2,1)S(1)}, bf16[192,6144]{1,0:T(8,128)(2,1)S(1)}, u32[]{:S(2)}, u32[]{:S(2)}) %collective-permute-start.3) | collective-permute-done | bytes 2359328 | tf_op jit(solution)/shard_map/ppermute | solution.py:39
  140.5 56.2 %all-gather.2.cloned.1.call-done.w_ref.up_ref.down_ref.k_ref.v_ref = bf16[768,15488]{1,0:T(8,128)(2,1)} async-done(((bf16[24,15488]{1,0:T(8,128)(2,1)}), bf16[768,15488]{1,0:T(8,128)(2,1)}) %all-gather.2.cloned.1.call-update) | async-done | bytes 23789584 | tf_op jit(solution)/shard_map/all_gather | solution.py:746
  198.0 5.1 %shard_map.425 = (f32[128,768]{1,0:T(8,128)S(1)}, bf16[2,128,768]{2,1,0:T(8,128)(2,1)S(1)}, bf16[3,128,768]{2,1,0:T(8,128)(2,1)S(1)}) custom-call(bf16[128,768]{1,0:T(8,128)(2,1)S(1)} %bitcast.37, f32[16,768]{1,0:T(8,128)S(1)} %fusion.15.vec_ref, bf16[768,15488]{1,0:T(8,128)(2,1)} %all-gather.2.cloned.1.call-done.w_ref.up_ref.down_ref.k_ref.v_ref), custom_call_target="tpu_custom_call" | custom-call | flops 1000 | bytes 1000 | tf_op jit(solution)/shard_map/pallas_call | solution.py:541
  203.9 5.9 %shard_map.426 = (f32[128,768]{1,0:T(8,128)S(1)}, bf16[5,128,768]{2,1,0:T(8,128)(2,1)S(1)}, f32[128,3072]{1,0:T(8,128)S(1)}) custom-call(f32[128,768]{1,0:T(8,128)S(1)} %get-tuple-element.198.x_ref, f32[16,768]{1,0:T(8,128)S(1)} %fusion.15.vec_ref, bf16[768,15488]{1,0:T(8,128)(2,1)} %all-gather.2.cloned.1.call-done.w_ref.up_ref.down_ref.k_ref.v_ref, ...), custom_call_target="tpu_custom_call" | custom-call | flops 1000 | bytes 1000 | tf_op jit(solution)/shard_map/pallas_call | solution.py:541
  211.2 4.9 %shard_map.427 = (f32[128,768]{1,0:T(8,128)S(1)}, bf16[2,128,768]{2,1,0:T(8,128)(2,1)S(1)}, bf16[3,128,768]{2,1,0:T(8,128)(2,1)S(1)}) custom-call(f32[128,768]{1,0:T(8,128)S(1)} %get-tuple-element.199.x_ref, f32[16,768]{1,0:T(8,128)S(1)} %fusion.15.vec_ref, bf16[768,15488]{1,0:T(8,128)(2,1)} %all-gather.2.cloned.1.call-done.w_ref.up_ref.down_ref.k_ref.v_ref), custom_call_target="tpu_custom_call" | custom-call | flops 1000 | bytes 1000 | tf_op jit(solution)/shard_map/pallas_call | solution.py:541
  221.6 8.3 %shard_map.428 = (f32[128,768]{1,0:T(8,128)S(1)}, bf16[2,128,768]{2,1,0:T(8,128)(2,1)S(1)}, bf16[128,768]{1,0:T(8,128)(2,1)S(1)}) custom-call(s32[2]{0:T(128)S(1)} %copy-done.39, f32[128,768]{1,0:T(8,128)S(1)} %get-tuple-element.202.x_ref, f32[16,768]{1,0:T(8,128)S(1)} %fusion.15.vec_ref, bf16[1152,1536]{1,0:T(8,128)(2,1)S(1)} %fusion.kv_ref, ...), custom_call_target="tpu_custom_call" | custom-call | flops 1000 | bytes 1000 | tf_op jit(solution)/shard_map/pallas_call | solution.py:541
  230.8 10.0 %shard_map.429 = (f32[128,768]{1,0:T(8,128)S(1)}, f32[8,768]{1,0:T(8,128)S(1)}, bf16[5,128,768]{2,1,0:T(8,128)(2,1)S(1)}, bf16[5,128,768]{2,1,0:T(8,128)(2,1)S(1)}) custom-call(f32[128,768]{1,0:T(8,128)S(1)} %get-tuple-element.207.x_ref, f32[16,768]{1,0:T(8,128)S(1)} %fusion.15.vec_ref, bf16[768,768]{1,0:T(8,128)(2,1)S(1)} %fusion.2.order_ref, ...), custom_call_target="tpu_custom_call" | custom-call | flops 1000 | bytes 1000 | tf_op jit(solution)/shard_map/pallas_call | solution.py:541
  241.6 6.3 %shard_map.430 = bf16[128,768]{1,0:T(8,128)(2,1)} custom-call(f32[128,768]{1,0:T(8,128)S(1)} %get-tuple-element.207.x_ref, bf16[768,768]{1,0:T(8,128)(2,1)S(1)} %fusion.2.order_ref, bf16[5,128,768]{2,1,0:T(8,128)(2,1)S(1)} %get-tuple-element.212.g_ref.b_ref, bf16[384,6144]{1,0:T(8,128)(2,1)} %constant_dynamic-update-slice_fusion.up_ref.down_ref, ...), custom_call_target="tpu_custom_call" | custom-call | flops 1000 | bytes 1000 | tf_op jit(solution)/shard_map/pallas_call | solution.py:541
  248.8 5.5 %shard_map.431 = (bf16[192,6144]{1,0:T(8,128)(2,1)}, bf16[192,6144]{1,0:T(8,128)(2,1)S(1)}) custom-call(bf16[768,768]{1,0:T(8,128)(2,1)S(1)} %fusion.2.order_ref, bf16[5,128,768]{2,1,0:T(8,128)(2,1)S(1)} %get-tuple-element.212.g_ref.b_ref, bf16[5,128,768]{2,1,0:T(8,128)(2,1)S(1)} %collective-permute-done.10.b2_ref.g2_ref, ...), custom_call_target="tpu_custom_call" | custom-call | flops 1000 | bytes 1000 | tf_op jit(solution)/shard_map/pallas_call | solution.py:541
  254.8 10.7 %shard_map.432 = (f32[128,768]{1,0:T(8,128)S(1)}, f32[8,768]{1,0:T(8,128)S(1)}, bf16[2,128,768]{2,1,0:T(8,128)(2,1)S(1)}, bf16[1152,1536]{1,0:T(8,128)(2,1)S(1)}) custom-call(s32[2]{0:T(128)S(1)} %copy-done.39, f32[128,768]{1,0:T(8,128)S(1)} %copy-done.10, f32[16,768]{1,0:T(8,128)S(1)} %fusion.15.vec_ref, bf16[128,768]{1,0:T(8,128)(2,1)S(1)} %get-tuple-element.216.q_ref, ...), custom_call_target="tpu_custom_call" | custom-call | flops 1000 | bytes 1000 | tf_op jit(solution)/shard_map/pallas_call | solution.py:541
  270.2 10.0 %shard_map.434 = (f32[128,768]{1,0:T(8,128)S(1)}, f32[8,768]{1,0:T(8,128)S(1)}, bf16[4,128,768]{2,1,0:T(8,128)(2,1)S(1)}) custom-call(f32[128,768]{1,0:T(8,128)S(1)} %copy-done.12, f32[16,768]{1,0:T(8,128)S(1)} %fusion.15.vec_ref, bf16[3,128,768]{2,1,0:T(8,128)(2,1)S(1)} %copy-done.19, f32[128,768]{1,0:T(8,128)S(1)} %get-tuple-element.228.dx_ref, ...), custom_call_target="tpu_custom_call" | custom-call | flops 1000 | bytes 1000 | tf_op jit(solution)/shard_map/pallas_call | solution.py:541
  286.5 7.0 %shard_map.436 = (bf16[192,6144]{1,0:T(8,128)(2,1)}, bf16[192,6144]{1,0:T(8,128)(2,1)S(1)}) custom-call(bf16[768,768]{1,0:T(8,128)(2,1)S(1)} %fusion.2.order_ref, bf16[2,128,768]{2,1,0:T(8,128)(2,1)S(1)} %copy-done.23, bf16[2,128,768]{2,1,0:T(8,128)(2,1)S(1)} %copy-done.25, bf16[4,128,768]{2,1,0:T(8,128)(2,1)S(1)} %get-tuple-element.244.sd_ref, ...), custom_call_target="tpu_custom_call" | custom-call | flops 1000 | bytes 1000 | tf_op jit(solution)/shard_map/pallas_call | solution.py:541
  295.7 6.8 %shard_map.437 = (f32[128,768]{1,0:T(8,128)S(1)}, f32[8,768]{1,0:T(8,128)S(1)}, bf16[5,128,768]{2,1,0:T(8,128)(2,1)S(1)}) custom-call(f32[128,768]{1,0:T(8,128)S(1)} %get-tuple-element.198.x_ref, f32[16,768]{1,0:T(8,128)S(1)} %fusion.15.vec_ref, f32[128,768]{1,0:T(8,128)S(1)} %get-tuple-element.253.dx_ref, ...), custom_call_target="tpu_custom_call" | custom-call | flops 1000 | bytes 1000 | tf_op jit(solution)/shard_map/pallas_call | solution.py:541
  305.1 5.2 %shard_map.438 = (bf16[192,6144]{1,0:T(8,128)(2,1)}, bf16[192,6144]{1,0:T(8,128)(2,1)S(1)}) custom-call(bf16[768,768]{1,0:T(8,128)(2,1)S(1)} %fusion.2.order_ref, bf16[5,128,768]{2,1,0:T(8,128)(2,1)S(1)} %get-tuple-element.258.b_ref.g_ref, bf16[5,128,768]{2,1,0:T(8,128)(2,1)S(1)} %collective-permute-done.6.b2_ref.g2_ref, ...), custom_call_target="tpu_custom_call" | custom-call | flops 1000 | bytes 1000 | tf_op jit(solution)/shard_map/pallas_call | solution.py:541
  310.3 10.5 %shard_map.439 = (f32[128,768]{1,0:T(8,128)S(1)}, f32[8,768]{1,0:T(8,128)}, bf16[5,128,768]{2,1,0:T(8,128)(2,1)S(1)}) custom-call(bf16[128,768]{1,0:T(8,128)(2,1)S(1)} %bitcast.38, f32[16,768]{1,0:T(8,128)S(1)} %fusion.15.vec_ref, bf16[3,128,768]{2,1,0:T(8,128)(2,1)S(1)} %copy-done.17, f32[128,768]{1,0:T(8,128)S(1)} %get-tuple-element.263.dx_ref, ...), custom_call_target="tpu_custom_call" | custom-call | flops 1000 | bytes 1000 | tf_op jit(solution)/shard_map/pallas_call | solution.py:541
  327.9 7.1 %collective-permute-done.17.got_ref = bf16[192,6144]{1,0:T(8,128)(2,1)S(1)} collective-permute-done((bf16[192,6144]{1,0:T(8,128)(2,1)}, bf16[192,6144]{1,0:T(8,128)(2,1)S(1)}, u32[]{:S(2)}, u32[]{:S(2)}) %collective-permute-start.17) | collective-permute-done | bytes 2359328 | tf_op jit(solution)/shard_map/ppermute | solution.py:39
  336.0 5.7 %shard_map.442 = bf16[1152,768]{1,0:T(8,128)(2,1)} custom-call(bf16[1152,1536]{1,0:T(8,128)(2,1)S(1)} %get-tuple-element.285.dkv_ref, bf16[768,15488]{1,0:T(8,128)(2,1)} %all-gather.2.cloned.1.call-done.w_ref.up_ref.down_ref.k_ref.v_ref, bf16[768,15488]{1,0:T(8,128)(2,1)} %all-gather.2.cloned.1.call-done.w_ref.up_ref.down_ref.k_ref.v_ref), custom_call_target="tpu_custom_call" | custom-call | flops 1000 | bytes 1000 | tf_op jit(solution)/shard_map/pallas_call | solution.py:541
  347.6 23.3 %collective-permute-done.20.got_ref = bf16[96,6144]{1,0:T(8,128)(2,1)S(1)} collective-permute-done((bf16[96,6144]{1,0:T(8,128)(2,1)S(1)}, bf16[96,6144]{1,0:T(8,128)(2,1)S(1)}, u32[]{:S(2)}, u32[]{:S(2)}) %collective-permute-start.20) | collective-permute-done | bytes 1179680 | tf_op jit(solution)/shard_map/ppermute | solution.py:39
  379.8 6.6 %collective-permute-done.23 = bf16[48,6144]{1,0:T(8,128)(2,1)} collective-permute-done((bf16[48,6144]{1,0:T(8,128)(2,1)}, bf16[48,6144]{1,0:T(8,128)(2,1)}, u32[]{:S(2)}, u32[]{:S(2)}) %collective-permute-start.23) | collective-permute-done | bytes 589856 | tf_op jit(solution)/shard_map/ppermute | solution.py:35
  390.9 15.2 %collective-permute-done.24.got_ref = bf16[96,6144]{1,0:T(8,128)(2,1)S(1)} collective-permute-done((bf16[96,6144]{1,0:T(8,128)(2,1)}, bf16[96,6144]{1,0:T(8,128)(2,1)S(1)}, u32[]{:S(2)}, u32[]{:S(2)}) %collective-permute-start.24) | collective-permute-done | bytes 1179680 | tf_op jit(solution)/shard_map/ppermute | solution.py:39
  410.6 8.1 %collective-permute-done.27 = bf16[48,6144]{1,0:T(8,128)(2,1)S(1)} collective-permute-done((bf16[48,6144]{1,0:T(8,128)(2,1)S(1)}, bf16[48,6144]{1,0:T(8,128)(2,1)S(1)}, u32[]{:S(2)}, u32[]{:S(2)}) %collective-permute-start.27) | collective-permute-done | bytes 589856 | tf_op jit(solution)/shard_map/ppermute | solution.py:35
  (224 shorter events, 118.4 us)
Async XLA Ops:
  7.2 189.4 %all-gather.2.cloned.1.call-start = ((), (), s32[]{:S(2)}) async-start(), calls=%async_computation | async-start | bytes 24532992 | tf_op jit(solution)/shard_map/all_gather | solution.py:746
  13.0 24.2 %collective-permute-start = (bf16[24,6144]{1,0:T(8,128)(2,1)}, bf16[24,6144]{1,0:T(8,128)(2,1)S(1)}, u32[]{:S(2)}, u32[]{:S(2)}) collective-permute-start(bf16[24,6144]{1,0:T(8,128)(2,1)} %get-tuple-element.196), channel_id=1, source_target_pairs={{0,16},{1,17},{2,18},{3,19},{4,20},{5,21},{6,22},{7,23},{8,24},{9,... | collective-permute-start | bytes 884744 | tf_op jit(solution)/shard_map/ppermute | solution.py:35
  38.3 23.9 %collective-permute-start.1 = (bf16[48,6144]{1,0:T(8,128)(2,1)S(1)}, bf16[48,6144]{1,0:T(8,128)(2,1)S(1)}, u32[]{:S(2)}, u32[]{:S(2)}) collective-permute-start(bf16[48,6144]{1,0:T(8,128)(2,1)S(1)} %pad_maximum_fusion.4), channel_id=1, source_target_pairs={{0,8},{1,9},{2,10},{3,11},{4,12},{5,13},{6,14},{7,15},{8,0},{9,1},... | collective-permute-start | bytes 1769480 | tf_op jit(solution)/shard_map/ppermute | solution.py:35
  64.2 17.3 %collective-permute-start.2 = (bf16[96,6144]{1,0:T(8,128)(2,1)}, bf16[96,6144]{1,0:T(8,128)(2,1)}, u32[]{:S(2)}, u32[]{:S(2)}) collective-permute-start(bf16[96,6144]{1,0:T(8,128)(2,1)} %pad_maximum_fusion.3), channel_id=1, source_target_pairs={{0,1},{1,0},{2,6},{3,7},{4,5},{5,4},{6,2},{7,3},{8,9},{9,8},{10,14... | collective-permute-start | bytes 3538952 | tf_op jit(solution)/shard_map/ppermute | solution.py:39
  83.0 55.9 %collective-permute-start.3 = (bf16[192,6144]{1,0:T(8,128)(2,1)S(1)}, bf16[192,6144]{1,0:T(8,128)(2,1)S(1)}, u32[]{:S(2)}, u32[]{:S(2)}) collective-permute-start(bf16[192,6144]{1,0:T(8,128)(2,1)S(1)} %pad_maximum_fusion), channel_id=1, source_target_pairs={{0,4},{1,5},{2,3},{3,2},{4,0},{5,1},{6,7},{7,6},{8,12},{9,13},{10,... | collective-permute-start | bytes 7077896 | tf_op jit(solution)/shard_map/ppermute | solution.py:39
  196.7 24.9 %collective-permute-start.4 = (bf16[384,6144]{1,0:T(8,128)(2,1)}, bf16[384,6144]{1,0:T(8,128)(2,1)S(1)}, u32[]{:S(2)}, u32[]{:S(2)}) collective-permute-start(bf16[384,6144]{1,0:T(8,128)(2,1)} %constant_dynamic-update-slice_fusion.up_ref.down_ref), channel_id=1, source_target_pairs={{0,2},{1,3},{2,0},{3,1},{4,6},{5,7},{6,4},{7,5},{8,10},{9,11},{10,... | collective-permute-start | bytes 14155784 | tf_op jit(solution)/shard_map/ppermute | solution.py:35
  211.0 19.8 %collective-permute-start.6 = (bf16[5,128,768]{2,1,0:T(8,128)(2,1)S(1)}, bf16[5,128,768]{2,1,0:T(8,128)(2,1)S(1)}, u32[]{:S(2)}, u32[]{:S(2)}) collective-permute-start(bf16[5,128,768]{2,1,0:T(8,128)(2,1)S(1)} %get-tuple-element.258.b_ref.g_ref), channel_id=1, source_target_pairs={{0,2},{1,3},{2,0},{3,1},{4,6},{5,7},{6,4},{7,5},{8,10},{9,11},{10,... | collective-permute-start | bytes 2949128 | tf_op jit(solution)/shard_map/ppermute | solution.py:35
  216.1 13.8 %collective-permute-start.7 = (bf16[2,128,768]{2,1,0:T(8,128)(2,1)S(1)}, bf16[2,128,768]{2,1,0:T(8,128)(2,1)S(1)}, u32[]{:S(2)}, u32[]{:S(2)}) collective-permute-start(bf16[2,128,768]{2,1,0:T(8,128)(2,1)S(1)} %get-tuple-element.242.s_ref), channel_id=1, source_target_pairs={{0,2},{1,3},{2,0},{3,1},{4,6},{5,7},{6,4},{7,5},{8,10},{9,11},{10,... | collective-permute-start | bytes 1179656 | tf_op jit(solution)/shard_map/ppermute | solution.py:35
  216.5 13.5 %collective-permute-start.5 = (bf16[2,128,768]{2,1,0:T(8,128)(2,1)S(1)}, bf16[2,128,768]{2,1,0:T(8,128)(2,1)S(1)}, u32[]{:S(2)}, u32[]{:S(2)}) collective-permute-start(bf16[2,128,768]{2,1,0:T(8,128)(2,1)S(1)} %get-tuple-element.295.s_ref), channel_id=1, source_target_pairs={{0,2},{1,3},{2,0},{3,1},{4,6},{5,7},{6,4},{7,5},{8,10},{9,11},{10,... | collective-permute-start | bytes 1179656 | tf_op jit(solution)/shard_map/ppermute | solution.py:35
  254.3 29.1 %collective-permute-start.11 = (bf16[192,6144]{1,0:T(8,128)(2,1)}, bf16[192,6144]{1,0:T(8,128)(2,1)S(1)}, u32[]{:S(2)}, u32[]{:S(2)}) collective-permute-start(bf16[192,6144]{1,0:T(8,128)(2,1)} %get-tuple-element.231), channel_id=1, source_target_pairs={{0,4},{1,5},{2,3},{3,2},{4,0},{5,1},{6,7},{7,6},{8,12},{9,13},{10,... | collective-permute-start | bytes 7077896 | tf_op jit(solution)/shard_map/ppermute | solution.py:39
  269.3 17.1 %collective-permute-start.14 = (bf16[384,1536]{1,0:T(8,128)(2,1)S(1)}, bf16[384,1536]{1,0:T(8,128)(2,1)S(1)}, u32[]{:S(2)}, u32[]{:S(2)}) collective-permute-start(bf16[384,1536]{1,0:T(8,128)(2,1)S(1)} %get-tuple-element.240), channel_id=1, source_target_pairs={{0,2},{1,3},{2,0},{3,1},{4,6},{5,7},{6,4},{7,5},{8,10},{9,11},{10,... | collective-permute-start | bytes 3538952 | tf_op jit(solution)/shard_map/ppermute | solution.py:35
  293.5 41.4 %collective-permute-start.17 = (bf16[192,6144]{1,0:T(8,128)(2,1)}, bf16[192,6144]{1,0:T(8,128)(2,1)S(1)}, u32[]{:S(2)}, u32[]{:S(2)}) collective-permute-start(bf16[192,6144]{1,0:T(8,128)(2,1)} %get-tuple-element.278), channel_id=1, source_target_pairs={{0,4},{1,5},{2,3},{3,2},{4,0},{5,1},{6,7},{7,6},{8,12},{9,13},{10,... | collective-permute-start | bytes 7077896 | tf_op jit(solution)/shard_map/ppermute | solution.py:39
  294.0 29.2 %collective-permute-start.16 = (bf16[96,6144]{1,0:T(8,128)(2,1)}, bf16[96,6144]{1,0:T(8,128)(2,1)}, u32[]{:S(2)}, u32[]{:S(2)}) collective-permute-start(bf16[96,6144]{1,0:T(8,128)(2,1)} %get-tuple-element.270), channel_id=1, source_target_pairs={{0,1},{1,0},{2,6},{3,7},{4,5},{5,4},{6,2},{7,3},{8,9},{9,8},{10,14... | collective-permute-start | bytes 3538952 | tf_op jit(solution)/shard_map/ppermute | solution.py:39
  324.7 17.0 %collective-permute-start.18 = (bf16[48,6144]{1,0:T(8,128)(2,1)S(1)}, bf16[48,6144]{1,0:T(8,128)(2,1)S(1)}, u32[]{:S(2)}, u32[]{:S(2)}) collective-permute-start(bf16[48,6144]{1,0:T(8,128)(2,1)S(1)} %get-tuple-element.288), channel_id=1, source_target_pairs={{0,8},{1,9},{2,10},{3,11},{4,12},{5,13},{6,14},{7,15},{8,0},{9,1},... | collective-permute-start | bytes 1769480 | tf_op jit(solution)/shard_map/ppermute | solution.py:35
  325.7 16.2 %collective-permute-start.19 = (bf16[5,128,768]{2,1,0:T(8,128)(2,1)S(1)}, bf16[5,128,768]{2,1,0:T(8,128)(2,1)S(1)}, u32[]{:S(2)}, u32[]{:S(2)}) collective-permute-start(bf16[5,128,768]{2,1,0:T(8,128)(2,1)S(1)} %get-tuple-element.297.sd_ref), channel_id=1, source_target_pairs={{0,2},{1,3},{2,0},{3,1},{4,6},{5,7},{6,4},{7,5},{8,10},{9,11},{10,... | collective-permute-start | bytes 2949128 | tf_op jit(solution)/shard_map/ppermute | solution.py:35
  325.8 47.9 %collective-permute-start.21 = (bf16[192,6144]{1,0:T(8,128)(2,1)}, bf16[192,6144]{1,0:T(8,128)(2,1)S(1)}, u32[]{:S(2)}, u32[]{:S(2)}) collective-permute-start(bf16[192,6144]{1,0:T(8,128)(2,1)} %get-tuple-element.309), channel_id=1, source_target_pairs={{0,4},{1,5},{2,3},{3,2},{4,0},{5,1},{6,7},{7,6},{8,12},{9,13},{10,... | collective-permute-start | bytes 7077896 | tf_op jit(solution)/shard_map/ppermute | solution.py:39
  341.9 31.7 %collective-permute-start.22 = (bf16[24,6144]{1,0:T(8,128)(2,1)S(1)}, bf16[24,6144]{1,0:T(8,128)(2,1)S(1)}, u32[]{:S(2)}, u32[]{:S(2)}) collective-permute-start(bf16[24,6144]{1,0:T(8,128)(2,1)S(1)} %add_convert_fusion.5), channel_id=1, source_target_pairs={{0,16},{1,17},{2,18},{3,19},{4,20},{5,21},{6,22},{7,23},{8,24},{9,... | collective-permute-start | bytes 884744 | tf_op jit(solution)/shard_map/ppermute | solution.py:35
  341.9 29.0 %collective-permute-start.20 = (bf16[96,6144]{1,0:T(8,128)(2,1)S(1)}, bf16[96,6144]{1,0:T(8,128)(2,1)S(1)}, u32[]{:S(2)}, u32[]{:S(2)}) collective-permute-start(bf16[96,6144]{1,0:T(8,128)(2,1)S(1)} %get-tuple-element.302), channel_id=1, source_target_pairs={{0,1},{1,0},{2,6},{3,7},{4,5},{5,4},{6,2},{7,3},{8,9},{9,8},{10,14... | collective-permute-start | bytes 3538952 | tf_op jit(solution)/shard_map/ppermute | solution.py:39
  372.1 14.3 %collective-permute-start.23 = (bf16[48,6144]{1,0:T(8,128)(2,1)}, bf16[48,6144]{1,0:T(8,128)(2,1)}, u32[]{:S(2)}, u32[]{:S(2)}) collective-permute-start(bf16[48,6144]{1,0:T(8,128)(2,1)} %get-tuple-element.319), channel_id=1, source_target_pairs={{0,8},{1,9},{2,10},{3,11},{4,12},{5,13},{6,14},{7,15},{8,0},{9,1},... | collective-permute-start | bytes 1769480 | tf_op jit(solution)/shard_map/ppermute | solution.py:35
  378.6 27.5 %collective-permute-start.24 = (bf16[96,6144]{1,0:T(8,128)(2,1)}, bf16[96,6144]{1,0:T(8,128)(2,1)S(1)}, u32[]{:S(2)}, u32[]{:S(2)}) collective-permute-start(bf16[96,6144]{1,0:T(8,128)(2,1)} %copy-done.40), channel_id=1, source_target_pairs={{0,1},{1,0},{2,6},{3,7},{4,5},{5,4},{6,2},{7,3},{8,9},{9,8},{10,14... | collective-permute-start | bytes 3538952 | tf_op jit(solution)/shard_map/ppermute | solution.py:39
  379.8 29.2 %collective-permute-start.25 = (bf16[192,3200]{1,0:T(8,128)(2,1)}, bf16[192,3200]{1,0:T(8,128)(2,1)S(1)}, u32[]{:S(2)}, u32[]{:S(2)}) collective-permute-start(bf16[192,3200]{1,0:T(8,128)(2,1)} %pad_maximum_fusion.1), channel_id=1, source_target_pairs={{0,4},{1,5},{2,3},{3,2},{4,0},{5,1},{6,7},{7,6},{8,12},{9,13},{10,... | collective-permute-start | bytes 3686408 | tf_op jit(solution)/shard_map/ppermute | solution.py:39
  387.4 19.6 %collective-permute-start.26 = (bf16[24,6144]{1,0:T(8,128)(2,1)S(1)}, bf16[24,6144]{1,0:T(8,128)(2,1)S(1)}, u32[]{:S(2)}, u32[]{:S(2)}) collective-permute-start(bf16[24,6144]{1,0:T(8,128)(2,1)S(1)} %add_convert_fusion.3), channel_id=1, source_target_pairs={{0,16},{1,17},{2,18},{3,19},{4,20},{5,21},{6,22},{7,23},{8,24},{9,... | collective-permute-start | bytes 884744 | tf_op jit(solution)/shard_map/ppermute | solution.py:35
  406.7 12.0 %collective-permute-start.27 = (bf16[48,6144]{1,0:T(8,128)(2,1)S(1)}, bf16[48,6144]{1,0:T(8,128)(2,1)S(1)}, u32[]{:S(2)}, u32[]{:S(2)}) collective-permute-start(bf16[48,6144]{1,0:T(8,128)(2,1)S(1)} %get-tuple-element.341), channel_id=1, source_target_pairs={{0,8},{1,9},{2,10},{3,11},{4,12},{5,13},{6,14},{7,15},{8,0},{9,1},... | collective-permute-start | bytes 1769480 | tf_op jit(solution)/shard_map/ppermute | solution.py:35
  409.2 19.0 %collective-permute-start.28 = (bf16[96,3200]{1,0:T(8,128)(2,1)S(1)}, bf16[96,3200]{1,0:T(8,128)(2,1)S(1)}, u32[]{:S(2)}, u32[]{:S(2)}) collective-permute-start(bf16[96,3200]{1,0:T(8,128)(2,1)S(1)} %get-tuple-element.347), channel_id=1, source_target_pairs={{0,1},{1,0},{2,6},{3,7},{4,5},{5,4},{6,2},{7,3},{8,9},{9,8},{10,14... | collective-permute-start | bytes 1843208 | tf_op jit(solution)/shard_map/ppermute | solution.py:39
  (58 other events, 639.3 us)
Sparse Core Ops, SparseCore 0:
  13.1 183.4 all-gather.1

commit v10 on v9

--- a/solution.py
+++ b/solution.py
@@ -193,17 +193,39 @@
     return dq.astype(bf16), dk.astype(bf16), dv.astype(bf16)
 
 
-def self_forward_kernel(captions, row, x_ref, vec_ref, w_ref, y_ref, f_ref, qkv_ref):
+def relative(x, order_ref):
+    return nt(x, order_ref[...]).astype(bf16)
+
+
+def times(x, top_ref, low_ref):
+    half = top_ref.shape[0]
+    return nn(x[:, :half], top_ref[...]) + nn(x[:, half:], low_ref[...])
+
+
+def times_back(g, top_ref, low_ref):
+    return jnp.concatenate((nt(g, top_ref[...]), nt(g, low_ref[...])), axis=1)
+
+
+def natural(x, order_ref):
+    high = x.astype(bf16)
+    low = (x - high.astype(f32)).astype(bf16)
+    return nn(high, order_ref[...]) + nn(low, order_ref[...])
+
+
+def self_forward_kernel(
+    captions, row, x_ref, vec_ref, order_ref, top_ref, low_ref, y_ref, f_ref, qkv_ref, rel_ref
+):
     j = pl.program_id(0)
 
     @pl.when(j == 0)
     def _():
         unit, _inv = unit_norm(x_ref[...].astype(f32))
         f_ref[0] = (unit * vec_ref[row : row + 1] + vec_ref[row + 1 : row + 2]).astype(bf16)
+        rel_ref[...] = relative(f_ref[0], order_ref)
 
     @pl.when(j < 3)
     def _():
-        qkv_ref[j] = nn(f_ref[0], w_ref[...]).astype(bf16)
+        qkv_ref[j] = times(rel_ref[...], top_ref, low_ref).astype(bf16)
 
     @pl.when(j == 3)
     def _():
@@ -216,11 +238,11 @@
                 p = probabilities(two_heads(qkv_ref[0, at, cols]), qkv_ref[1, at, cols], allowed)
                 o = side_by_side(nn(p.astype(bf16), qkv_ref[2, at, cols]))
                 f_ref[1, at, cols] = o.astype(bf16)
-        y_ref[...] = x_ref[...].astype(f32) + nn(f_ref[1], w_ref[...])
+        y_ref[...] = x_ref[...].astype(f32) + times(relative(f_ref[1], order_ref), top_ref, low_ref)
 
 
 def self_backward_kernel(
-    captions, row, x_ref, vec_ref, qkv_ref, dx_ref, w_ref, *refs
+    captions, row, x_ref, vec_ref, order_ref, qkv_ref, dx_ref, top_ref, low_ref, *refs
 ):
     out_ref, vg_ref, p_ref, acc_ref = refs[-4:]
     j = pl.program_id(0)
@@ -229,7 +251,8 @@
     def _():
         dy = dx_ref[...].astype(bf16)
         p_ref[3] = dy
-        do = nt(dy, w_ref[...]).astype(bf16)
+        do = times_back(dy, top_ref, low_ref).astype(bf16)
+        do = nn(do, order_ref[...]).astype(bf16)
         length = x_ref.shape[0] // captions
         allowed = causal_mask(length)
         for c in range(captions):
@@ -247,11 +270,12 @@
 
     @pl.when(j > 0)
     def _():
-        acc_ref[...] += nt(p_ref[j - 1], w_ref[...])
+        acc_ref[...] += times_back(p_ref[j - 1], top_ref, low_ref)
 
     @pl.when(j == 3)
     def _():
-        dn, gg, gs = norm_backward(acc_ref[...], x_ref[...].astype(f32), vec_ref[row : row + 1])
+        da = natural(acc_ref[...], order_ref)
+        dn, gg, gs = norm_backward(da, x_ref[...].astype(f32), vec_ref[row : row + 1])
         out_ref[...] = dx_ref[...] + dn
         vg_ref[0:1] = gg
         vg_ref[1:2] = gs
@@ -263,7 +287,7 @@
 
 
 def cross_forward_kernel(
-    captions, row, count_ref, x_ref, vec_ref, kv_ref, w_ref, y_ref, f_ref, q_ref
+    captions, row, count_ref, x_ref, vec_ref, order_ref, kv_ref, top_ref, low_ref, y_ref, f_ref, q_ref
 ):
     j = pl.program_id(0)
     d = x_ref.shape[1]
@@ -273,7 +297,7 @@
         unit, _inv = unit_norm(x_ref[...])
         c = (unit * vec_ref[row : row + 1] + vec_ref[row + 1 : row + 2]).astype(bf16)
         f_ref[0] = c
-        q_ref[...] = nn(c, w_ref[...]).astype(bf16)
+        q_ref[...] = times(relative(c, order_ref), top_ref, low_ref).astype(bf16)
 
     @pl.when(j == 1)
     def _():
@@ -290,11 +314,11 @@
                 p = probabilities(two_heads(q_ref[at, cols]), kv_ref[keys, cols], allowed)
                 o = side_by_side(nn(p.astype(bf16), kv_ref[keys, vcols]))
                 f_ref[1, at, cols] = o.astype(bf16)
-        y_ref[...] = x_ref[...] + nn(f_ref[1], w_ref[...])
+        y_ref[...] = x_ref[...] + times(relative(f_ref[1], order_ref), top_ref, low_ref)
 
 
 def cross_backward_kernel(
-    captions, row, count_ref, x_ref, vec_ref, q_ref, kv_ref, dx_ref, w_ref,
+    captions, row, count_ref, x_ref, vec_ref, order_ref, q_ref, kv_ref, dx_ref, top_ref, low_ref,
     out_ref, vg_ref, p_ref, dkv_ref,
 ):
     j = pl.program_id(0)
@@ -304,7 +328,8 @@
     def _():
         dy = dx_ref[...].astype(bf16)
         p_ref[1] = dy
-        do = nt(dy, w_ref[...]).astype(bf16)
+        do = times_back(dy, top_ref, low_ref).astype(bf16)
+        do = nn(do, order_ref[...]).astype(bf16)
         length = x_ref.shape[0] // captions
         patches = kv_ref.shape[0] // captions
         slot = lax.broadcasted_iota(jnp.int32, (2 * length, patches), 1)
@@ -324,26 +349,30 @@
 
     @pl.when(j == 1)
     def _():
-        dn, gg, gs = norm_backward(nt(p_ref[0], w_ref[...]), x_ref[...], vec_ref[row : row + 1])
+        dc = natural(times_back(p_ref[0], top_ref, low_ref), order_ref)
+        dn, gg, gs = norm_backward(dc, x_ref[...], vec_ref[row : row + 1])
         out_ref[...] = dx_ref[...] + dn
         vg_ref[0:1] = gg
         vg_ref[1:2] = gs
 
 
-def feed_forward_kernel(row, x_ref, vec_ref, up_ref, down_ref, y_ref, f_ref, u_ref):
+def feed_forward_kernel(
+    row, x_ref, vec_ref, order_ref, up_ref, up2_ref, down_ref, down2_ref, y_ref, f_ref, u_ref, rel_ref
+):
     j = pl.program_id(0)
 
     @pl.when(j == 0)
     def _():
         unit, _inv = unit_norm(x_ref[...])
         f_ref[0] = (unit * vec_ref[row : row + 1] + vec_ref[row + 1 : row + 2]).astype(bf16)
+        rel_ref[...] = relative(f_ref[0], order_ref)
         y_ref[...] = x_ref[...]
 
-    u = nn(f_ref[0], up_ref[...])
+    u = times(rel_ref[...], up_ref, up2_ref)
     u_ref[...] = u
     g = (0.5 * u * (1.0 + jnp.tanh(GELU_A * (u + GELU_B * u * u * u)))).astype(bf16)
     f_ref[1 + j] = g
-    y_ref[...] += nn(g, down_ref[...])
+    y_ref[...] += times(relative(g, order_ref), down_ref, down2_ref)
 
 
 def gelu_terms(u):
@@ -352,8 +381,25 @@
     return 0.5 * u * (1.0 + t), slope
 
 
+def feed_backward_step(j, order_ref, slope, refs, p_ref, acc_ref):
+    up_ref, up2_ref, down_ref, down2_ref = refs
+    dg = times_back(p_ref[0], down_ref, down2_ref).astype(bf16)
+    du = (slope * nn(dg, order_ref[...])).astype(bf16)
+    p_ref[1 + j] = du
+    acc_ref[...] += times_back(du, up_ref, up2_ref)
+
+
+def feed_backward_end(row, order_ref, x_ref, vec_ref, dx_ref, acc_ref, out_ref, vg_ref):
+    db = natural(acc_ref[...], order_ref)
+    dn, gg, gs = norm_backward(db, x_ref[...], vec_ref[row : row + 1])
+    out_ref[...] = dx_ref[...].astype(f32) + dn
+    vg_ref[0:1] = gg
+    vg_ref[1:2] = gs
+
+
 def feed_backward_kernel(
-    row, x_ref, vec_ref, dx_ref, up_ref, down_ref, u_ref, out_ref, vg_ref, p_ref, acc_ref
+    row, x_ref, vec_ref, order_ref, dx_ref, up_ref, up2_ref, down_ref, down2_ref, u_ref,
+    out_ref, vg_ref, p_ref, acc_ref,
 ):
     j = pl.program_id(0)
 
@@ -362,58 +408,36 @@
         p_ref[0] = dx_ref[...].astype(bf16)
         acc_ref[...] = jnp.zeros_like(acc_ref)
 
-    slope = gelu_terms(u_ref[...])[1]
-    du = (slope * nt(p_ref[0], down_ref[...])).astype(bf16)
-    p_ref[1 + j] = du
-    acc_ref[...] += nt(du, up_ref[...])
+    refs = up_ref, up2_ref, down_ref, down2_ref
+    feed_backward_step(j, order_ref, gelu_terms(u_ref[...])[1], refs, p_ref, acc_ref)
 
     @pl.when(j == 3)
     def _():
-        dn, gg, gs = norm_backward(acc_ref[...], x_ref[...], vec_ref[row : row + 1])
-        out_ref[...] = dx_ref[...] + dn
-        vg_ref[0:1] = gg
-        vg_ref[1:2] = gs
-
-
-def by_rows(x, order_ref, top_ref, low_ref):
-    half = top_ref.shape[0]
-    x = nt(x, order_ref[...]).astype(bf16)
-    return nn(x[:, :half], top_ref[...]) + nn(x[:, half:], low_ref[...])
+        feed_backward_end(row, order_ref, x_ref, vec_ref, dx_ref, acc_ref, out_ref, vg_ref)
 
 
 def last_backward_kernel(
     row, x_ref, vec_ref, order_ref, dx_ref, up_ref, up2_ref, down_ref, down2_ref,
-    out_ref, vg_ref, p_ref, f_ref, acc_ref,
+    out_ref, vg_ref, p_ref, f_ref, acc_ref, rel_ref,
 ):
     j = pl.program_id(0)
-    half = up_ref.shape[0]
 
     @pl.when(j == 0)
     def _():
         unit, _inv = unit_norm(x_ref[...])
         f_ref[0] = (unit * vec_ref[row : row + 1] + vec_ref[row + 1 : row + 2]).astype(bf16)
+        rel_ref[...] = relative(f_ref[0], order_ref)
         p_ref[0] = dx_ref[...]
         acc_ref[...] = jnp.zeros_like(acc_ref)
 
-    g, slope = gelu_terms(by_rows(f_ref[0], order_ref, up_ref, up2_ref))
+    g, slope = gelu_terms(times(rel_ref[...], up_ref, up2_ref))
     f_ref[1 + j] = g.astype(bf16)
-    dz = p_ref[0]
-    dg = jnp.concatenate((nt(dz, down_ref[...]), nt(dz, down2_ref[...])), axis=1)
-    du = (slope * nn(dg.astype(bf16), order_ref[...])).astype(bf16)
-    p_ref[1 + j] = du
-    acc_ref[:, :half] += nt(du, up_ref[...])
-    acc_ref[:, half:] += nt(du, up2_ref[...])
+    refs = up_ref, up2_ref, down_ref, down2_ref
+    feed_backward_step(j, order_ref, slope, refs, p_ref, acc_ref)
 
     @pl.when(j == 3)
     def _():
-        db = acc_ref[...]
-        high = db.astype(bf16)
-        low = (db - high.astype(f32)).astype(bf16)
-        db = nn(high, order_ref[...]) + nn(low, order_ref[...])
-        dn, gg, gs = norm_backward(db, x_ref[...], vec_ref[row : row + 1])
-        out_ref[...] = dx_ref[...].astype(f32) + dn
-        vg_ref[0:1] = gg
-        vg_ref[1:2] = gs
+        feed_backward_end(row, order_ref, x_ref, vec_ref, dx_ref, acc_ref, out_ref, vg_ref)
 
 
 def last_output_kernel(x_ref, order_ref, g_ref, down_ref, down2_ref, y_ref, acc_ref):
@@ -423,7 +447,7 @@
     def _():
         acc_ref[...] = x_ref[...]
 
-    acc_ref[...] += by_rows(g_ref[0], order_ref, down_ref, down2_ref)
+    acc_ref[...] += times(relative(g_ref[0], order_ref), down_ref, down2_ref)
 
     @pl.when(j == 3)
     def _():
@@ -492,45 +516,49 @@
     return call(half_sums_kernel, steps, (kept, got), [full] * 2, outs, [half] * 2, vmem=24)
 
 
-def pair_input_kernel(dkv_ref, k_ref, v_ref, out_ref):
-    d = k_ref.shape[0]
-    g = nt(dkv_ref[:, :d], k_ref[...]) + nt(dkv_ref[:, d:], v_ref[...])
-    out_ref[...] = g.astype(bf16)
+def pair_forward_kernel(enc_ref, top_ref, low_ref, kv_ref):
+    kv_ref[...] = times(enc_ref[...], top_ref, low_ref).astype(bf16)
+
+
+def pair_input_kernel(dkv_ref, order_ref, top_ref, low_ref, out_ref):
+    g = times_back(dkv_ref[...], top_ref, low_ref).astype(bf16)
+    out_ref[...] = nn(g, order_ref[...]).astype(bf16)
 
 
 def pair_grads_kernel(enc_ref, dkv_ref, keep_ref, send_ref):
     emit(nn(enc_ref[...], dkv_ref[...]), send_ref, keep_ref)
 
 
-def pack_kernel(u_qkv, u_out, u_up, u_down, m_qkv, m_out, m_up, m_down, c_q, c_pair, c_out, vec, out, feed_out):
+def pack_kernel(
+    u_qkv, u_out, u_up, u_down, m_qkv, m_out, m_up, m_down, c_q, c_pair, c_out, vec,
+    first_out, feed_out, middle_out, last_out,
+):
     rows, d = u_out.shape
     spread = spread_matrix().astype(bf16)
     i = lax.broadcasted_iota(jnp.int32, (rows, 4 * rows), 0)
     k = lax.broadcasted_iota(jnp.int32, (rows, 4 * rows), 1)
 
-    def attend(at, qkv, w_out):
-        out[:, at : at + 3 * d] = qkv[...]
-        out[:, at + 3 * d : at + 4 * d] = w_out[...]
-
-    def feed(out, at, up, down):
+    def feed(out, up, down):
         for b in range(4 * d // 512):
             y = nn(up[:, b * 512 : (b + 1) * 512], spread).astype(bf16)
             for j in range(4):
-                to = at + j * d + b * LANES
+                to = j * d + b * LANES
                 out[:, to : to + LANES] = y[:, j * LANES : (j + 1) * LANES]
         for j in range(4):
             y = nn((k == 4 * i + j).astype(bf16), down[...])
-            out[:, at + (4 + j) * d : at + (5 + j) * d] = y.astype(bf16)
-
-    feed(feed_out, 0, m_up, m_down)
-    attend(0, u_qkv, u_out)
-    feed(out, 4 * d, u_up, u_down)
-    attend(12 * d, m_qkv, m_out)
-    out[:, 16 * d : 17 * d] = c_q[...]
-    out[:, 17 * d : 19 * d] = c_pair[...]
-    out[:, 19 * d : 20 * d] = c_out[...]
+            out[:, (4 + j) * d : (5 + j) * d] = y.astype(bf16)
+
+    first_out[:, : 3 * d] = u_qkv[...]
+    first_out[:, 3 * d : 4 * d] = u_out[...]
     eye = lax.broadcasted_iota(jnp.int32, (rows, rows), 0) == lax.broadcasted_iota(jnp.int32, (rows, rows), 1)
-    out[:, 20 * d :] = nt(eye.astype(bf16), vec[...]).astype(bf16)
+    first_out[:, 4 * d :] = nt(eye.astype(bf16), vec[...]).astype(bf16)
+    feed(feed_out, u_up, u_down)
+    middle_out[:, : 2 * d] = c_pair[...]
+    middle_out[:, 2 * d : 3 * d] = c_q[...]
+    middle_out[:, 3 * d : 4 * d] = c_out[...]
+    middle_out[:, 4 * d : 7 * d] = m_qkv[...]
+    middle_out[:, 7 * d : 8 * d] = m_out[...]
+    feed(last_out, m_up, m_down)
 
 
 def whole(x):
@@ -556,55 +584,68 @@
 
 
 class Layers:
-    def __init__(self, captions, tokens, d, w, vec, order, count):
+    def __init__(self, captions, tokens, d, vec, order, count):
         self.captions, self.t, self.d = captions, tokens, d
-        self.w, self.vec, self.order, self.count = w, vec, order, count
+        self.vec, self.order, self.count = vec, order, count
         self.xs = sds((tokens, d), f32)
         self.hs = sds((tokens, d), bf16)
 
-    def weight(self, index):
-        return pl.BlockSpec((self.d, self.d), lambda j, *_: (0, index(j)))
-
-    def self_forward(self, x, at, row):
+    def weights(self, *columns):
+        d = self.d
+        specs = [pl.BlockSpec((d // 2, d), lambda j, *_, c=c: (0, c(j))) for c in columns]
+        return [s for s in specs for _ in range(2)]
+
+    def self_forward(self, x, w, at, row):
         outs = (self.xs, sds((2, self.t, self.d), bf16), sds((3, self.t, self.d), bf16))
+        ins = (x, self.vec, self.order)
         return call(
             functools.partial(self_forward_kernel, self.captions, row), 4,
-            (x, self.vec, self.w),
-            [whole(x), whole(self.vec), self.weight(lambda j: at + j)],
-            outs, [whole(o) for o in outs],
-        )
-
-    def self_backward(self, x, kept, dx, at, row, vectors=()):
+            ins + w, [whole(i) for i in ins] + self.weights(lambda j: at + j),
+            outs, [whole(o) for o in outs], scratch=[pltpu.VMEM((self.t, self.d), bf16)],
+        )
+
+    def self_backward(self, x, kept, dx, w, at, row, vectors=()):
         d, t = self.d, self.t
         outs = (self.xs, sds((8, d), f32), sds((4 + len(vectors), t, d), bf16))
-        ins = (x, self.vec, kept, dx)
+        ins = (x, self.vec, self.order, kept, dx)
         return call(
             functools.partial(self_backward_kernel, self.captions, row), 4,
-            ins + (self.w,) + vectors,
-            [whole(i) for i in ins] + [self.weight(lambda j: at + (j + 3) % 4)]
+            ins + w + vectors,
+            [whole(i) for i in ins] + self.weights(lambda j: at + (j + 3) % 4)
             + [whole(v) for v in vectors],
             outs, [whole(i) for i in outs],
             scratch=[pltpu.VMEM((t, d), f32)],
         )
 
-    def cross_forward(self, x, kv, at, row):
+    def cross_forward(self, x, kv, w, at, row):
         outs = (self.xs, sds((2, self.t, self.d), bf16), self.hs)
+        ins = (x, self.vec, self.order, kv)
         return call(
             functools.partial(cross_forward_kernel, self.captions, row), 2,
-            (self.count, x, self.vec, kv, self.w),
-            [whole(x), whole(self.vec), whole(kv), self.weight(lambda j: at + 3 * j)],
+            (self.count,) + ins + w,
+            [whole(i) for i in ins] + self.weights(lambda j: at + j),
             outs, [whole(o) for o in outs], scalars=1,
         )
 
-    def cross_backward(self, x, kept, kv, dx, at, row):
+    def cross_backward(self, x, kept, kv, dx, w, at, row):
         d, t = self.d, self.t
         outs = (self.xs, sds((8, d), f32), sds((2, t, d), bf16), sds(kv.shape, bf16))
-        ins = (x, self.vec, kept, kv, dx)
+        ins = (x, self.vec, self.order, kept, kv, dx)
         return call(
             functools.partial(cross_backward_kernel, self.captions, row), 2,
-            (self.count,) + ins + (self.w,),
-            [whole(i) for i in ins] + [self.weight(lambda j: at + 3 - 3 * j)],
+            (self.count,) + ins + w,
+            [whole(i) for i in ins] + self.weights(lambda j: at + 1 - j),
             outs, [whole(i) for i in outs], scalars=1,
+        )
+
+    def pair_forward(self, enc, w):
+        d, rows = self.d, enc.shape[0] // self.captions
+        half = pl.BlockSpec((d // 2, 2 * d), lambda j: (0, 0))
+        out = sds((enc.shape[0], 2 * d), bf16)
+        return call(
+            pair_forward_kernel, self.captions, (enc,) + w,
+            [pl.BlockSpec((rows, d), lambda j: (j, 0)), half, half],
+            out, pl.BlockSpec((rows, 2 * d), lambda j: (j, 0)),
         )
 
     def pair_grads(self, enc_t, dkv):
@@ -617,13 +658,13 @@
             outs, [grad, grad],
         )
 
-    def pair_input(self, dkv, at):
+    def pair_input(self, dkv, w):
         d, rows = self.d, dkv.shape[0] // self.captions
+        half = pl.BlockSpec((d // 2, 2 * d), lambda j: (0, 0))
         out = sds((dkv.shape[0], d), bf16)
         return call(
-            pair_input_kernel, self.captions, (dkv, self.w, self.w),
-            [pl.BlockSpec((rows, 2 * d), lambda j: (j, 0))]
-            + [self.weight(lambda j: at), self.weight(lambda j: at + 1)],
+            pair_input_kernel, self.captions, (dkv, self.order) + w,
+            [pl.BlockSpec((rows, 2 * d), lambda j: (j, 0)), whole(self.order), half, half],
             out, pl.BlockSpec((rows, d), lambda j: (j, 0)),
         )
 
@@ -660,27 +701,27 @@
             outs, [pl.BlockSpec((d // 4, d), lambda j: (0, j))] * 2,
         )
 
-    def feed_forward(self, x, at, row):
+    def feed_forward(self, x, w, row):
         d, t = self.d, self.t
         outs = (self.xs, sds((5, t, d), bf16), sds((t, 4 * d), f32))
+        ins = (x, self.vec, self.order)
         return call(
             functools.partial(feed_forward_kernel, row), 4,
-            (x, self.vec, self.w, self.w),
-            [whole(x), whole(self.vec), self.weight(lambda j: at + j), self.weight(lambda j: at + 4 + j)],
+            ins + w + w,
+            [whole(i) for i in ins] + self.weights(lambda j: j, lambda j: 4 + j),
             outs, [whole(outs[0]), whole(outs[1]), pl.BlockSpec((t, d), lambda j: (0, j))],
-        )
-
-    def feed_backward(self, x, u, dx, at, row):
+            scratch=[pltpu.VMEM((t, d), bf16)],
+        )
+
+    def feed_backward(self, x, u, dx, w, row):
         d, t = self.d, self.t
         outs = (self.xs, sds((8, d), f32), sds((5, t, d), bf16))
+        ins = (x, self.vec, self.order, dx)
         return call(
             functools.partial(feed_backward_kernel, row), 4,
-            (x, self.vec, dx, self.w, self.w, u),
-            [
-                whole(x), whole(self.vec), whole(dx),
-                self.weight(lambda j: at + j), self.weight(lambda j: at + 4 + j),
-                pl.BlockSpec((t, d), lambda j: (0, j)),
-            ],
+            ins + w + w + (u,),
+            [whole(i) for i in ins] + self.weights(lambda j: j, lambda j: 4 + j)
+            + [pl.BlockSpec((t, d), lambda j: (0, j))],
             outs, [whole(i) for i in outs],
             scratch=[pltpu.VMEM((t, d), f32)],
         )
@@ -689,20 +730,19 @@
         d, t = self.d, self.t
         outs = (self.xs, sds((8, d), f32)) + (sds((5, t, d), bf16),) * 2
         ins = (x, self.vec, self.order, dx)
-        up = pl.BlockSpec((d // 2, d), lambda j: (0, j))
-        down = pl.BlockSpec((d // 2, d), lambda j: (0, 4 + j))
         return call(
             functools.partial(last_backward_kernel, row), 4,
-            ins + w + w, [whole(i) for i in ins] + [up, up, down, down],
+            ins + w + w,
+            [whole(i) for i in ins] + self.weights(lambda j: j, lambda j: 4 + j),
             outs, [whole(i) for i in outs],
-            scratch=[pltpu.VMEM((t, d), f32)],
+            scratch=[pltpu.VMEM((t, d), f32), pltpu.VMEM((t, d), bf16)],
         )
 
     def last_output(self, x, f, w):
-        down = pl.BlockSpec((self.d // 2, self.d), lambda j: (0, 4 + j))
         return call(
             last_output_kernel, 4, (x, self.order, f) + w,
-            [whole(x), whole(self.order), self.block(lambda j: 1 + j), down, down],
+            [whole(x), whole(self.order), self.block(lambda j: 1 + j)]
+            + self.weights(lambda j: 4 + j),
             self.hs, whole(self.hs), scratch=[pltpu.VMEM((self.t, self.d), f32)],
         )
 
@@ -738,30 +778,64 @@
     vectors = (u_ag, u_as, u_mg, u_ms, m_ag, m_as, c_g, c_s, m_mg, m_ms)
     vectors = jnp.pad(jnp.stack(vectors, axis=0), ((0, LANES - len(vectors)), (0, 0)))
     parts = (u_qkv, u_out, u_up, u_down, m_qkv, m_out, m_up, m_down, c_q, c_pair, c_out, vectors)
-    packed = sds((rows, 20 * d + LANES), bf16), sds((rows, 8 * d), bf16)
-    shard, last = call(
+    packed = tuple(sds((rows, c), bf16) for c in (4 * d + LANES, 8 * d, 8 * d, 8 * d))
+    shards = call(
         pack_kernel, 1, parts, [whole(p) for p in parts], packed, [whole(p) for p in packed], vmem=60
     )
+    first, feed, middle, last = (Gather(place, x) for x in shards)
+
+    def go(token, groups=(), start=()):
+        token, got = tie(token, *[(g.x, g.got) for g in groups])
+        for g, (x, y) in zip(groups, got):
+            g.x, g.got = x, y
+            g.join()
+        every = tuple(groups) + tuple(start)
+        token, xs = tie(token, *[g.x for g in every])
+        for g, x in zip(every, xs):
+            g.x = x
+            g.swap()
+        return token
+
+    def end(token, group):
+        token, (group.x, group.got) = tie(token, group.x, group.got)
+        return token, (group.x, group.got)
+
+    steps = place.outer_bits
+    x0 = go(x0, start=[first])
+    enc_rel = nt(enc, order).astype(bf16)
     enc_t = nt(order, enc).astype(bf16)
-    w = lax.all_gather(shard, AXES, axis=0, tiled=True)
-
-    last = Gather(place, last)
-    for _ in range(place.outer_bits + 2):
-        last.swap()
-        last.join()
-    w, (order, enc_t, last.x) = tie(w, order, enc_t, last.x)
-    last.swap()
-    vec = nt(jnp.eye(16, LANES, dtype=bf16), w[:, 20 * d :])
-
-    net = Layers(captions, captions * length, d, w, vec, order, patch_count)
-
-    kv = nn(enc, w[:, 17 * d : 19 * d]).astype(bf16)
-    x0a, f_us, k_us = net.self_forward(x0, 0, 0)
-    x1, f_uf, k_uf = net.feed_forward(x0a, 4, 2)
-    x1a, f_ms, k_ms = net.self_forward(x1, 12, 4)
-    x1a, (last.x, last.got) = tie(x1a, last.x, last.got)
-    w_last = last.x, last.got
-    x1b, f_mc, k_mc = net.cross_forward(x1a, kv, 16, 6)
+    for k in range(steps - 1):
+        x0 = go(x0, [first], [feed] if k == 0 else [])
+    x0 = go(x0, [first])
+    for k in range(steps - 1):
+        x0 = go(x0, [feed])
+    x0 = go(x0, [first])
+    x0 = go(x0, [feed], [middle])
+    x0 = go(x0, [first])
+    x0 = go(x0, [feed])
+    for k in range(steps - 1):
+        x0 = go(x0, [middle])
+    x0, (order, enc_rel, enc_t) = tie(x0, order, enc_rel, enc_t)
+    x0, w_first = end(x0, first)
+    vec = tn(jnp.concatenate([x[:, 4 * d :] for x in w_first], axis=0), order)[:16]
+    net = Layers(captions, captions * length, d, vec, order, patch_count)
+    x0 = go(x0, [middle], [last])
+    x0a, f_us, k_us = net.self_forward(x0, w_first, 0, 0)
+    x0a = go(x0a, [feed])
+    for k in range(steps - 1):
+        x0a = go(x0a, [last])
+    x0a = go(x0a, [middle])
+    x0a, w_feed = end(x0a, feed)
+    x1, f_uf, k_uf = net.feed_forward(x0a, w_feed, 2)
+    x1 = go(x1, [last])
+    x1 = go(x1, [middle])
+    x1 = go(x1, [last])
+    x1, w_middle = end(x1, middle)
+    x1a, f_ms, k_ms = net.self_forward(x1, w_middle, 4, 4)
+    kv = net.pair_forward(enc_rel, w_middle)
+    x1b, f_mc, k_mc = net.cross_forward(x1a, kv, w_middle, 2, 6)
+    x1b = go(x1b, [last])
+    x1b, w_last = end(x1b, last)
 
     def core(x):
         return place.swap(x, BIT_CORE)
@@ -794,30 +868,30 @@
     s_mf = Sum(place, net.feed_grads(f, p))
     dx, (f_mc,) = tie(dx, f_mc)
     dx = go_on(dx, start=[s_mf])
-    dx, v_mc, p_c, dkv = net.cross_backward(x1a, k_mc, kv, dx, 16, 6)
+    dx, v_mc, p_c, dkv = net.cross_backward(x1a, k_mc, kv, dx, w_middle, 2, 6)
     p_c = pairs(p_c)
     pair, send = net.pair_grads(enc_t, dkv)
     dx, (send,) = tie(dx, send)
     pair = pair, core(send)
-    dx, v_ms, p = net.self_backward(x1, k_ms, dx, 12, 4)
+    dx, v_ms, p = net.self_backward(x1, k_ms, dx, w_middle, 4, 4)
     p = pairs(p)
     dx = go_on(dx, [s_mf], [s_mf])
     dx, (p, p_c, pair) = tie(dx, p, p_c, pair)
     s_ma = Sum(place, net.attend_grads(f_ms, p, (f_mc, p_c, pair)))
     dx = go_on(dx, start=[s_ma])
-    dx, v_uf, p = net.feed_backward(x0a, k_uf, dx, 4, 2)
+    dx, v_uf, p = net.feed_backward(x0a, k_uf, dx, w_feed, 2)
     p = pairs(p)
     dx, (p,) = tie(dx, p)
     s_uf = Sum(place, net.feed_grads(f_uf, p))
     dx = need(dx, s_uf)
     v = [g[:2] for g in (v_uf, v_ms, v_mc, v_mf)]
     v = jnp.pad(jnp.concatenate(v, axis=0), ((2, 6), (0, 0)))
-    dx, _v, p = net.self_backward(x0, k_us, dx, 0, 0, (v,))
+    dx, _v, p = net.self_backward(x0, k_us, dx, w_first, 0, 0, (v,))
     p = pairs(p)
     dx = go_on(dx, [s_mf], [s_uf, s_mf])
     dx = go_on(dx, [s_ma], [s_ma])
     dx, (dkv,) = tie(dx, dkv)
-    denc = net.pair_input(dkv, 17)
+    denc = net.pair_input(dkv, w_middle)
     dx, (denc,) = tie(dx, denc)
     dx = rest(dx, s_mf)
     dx, (p,) = tie(dx, p)

time: 458 us -> 462 us (level)
  waiting for transfers between devices: 234 us -> 207 us
  Pallas kernels: 121 us -> 139 us
  between operations: 15 us -> 1.78 us
  local copies, waits for them, and re-layouts: 27.1 us -> 37.9 us
  other arithmetic: 14.9 us -> 25.5 us
  starting transfers between devices: 30.5 us -> 38.3 us
    all_gather x1 -> x0, waiting for transfers between devices: 56.2 us -> none  [local(): w = lax.all_gather(shard, AXES, axis=0, tiled=True)]
    ppermute x22 -> x31, waiting for transfers between devices: 65.4 us -> 104 us  [swap(): return lax.ppermute(x, AXES, [(i, i ^ bit) for i in range(self.count)])]
    pallas_call x25 -> x26, Pallas kernels: 121 us -> 139 us  [call(): pl.pallas_call(kernel, out_shape=outs, grid_spec=pltpu.PrefetchScalarGrid...]
    unnamed x102 -> x142, local copies, waits for them, and re-layouts: 10.7 us -> 21.5 us
    ppermute x10 -> x16, waiting for transfers between devices: 112 us -> 103 us  [swap_by_core(): return lax.ppermute(x, AXES, pairs)]
    concatenate x3 -> x16, other arithmetic: 4.62 us -> 13.7 us  [join(): self.x = jnp.concatenate((self.x, self.got), axis=0)]
    ppermute x10 -> x16, starting transfers between devices: 11.4 us -> 18.5 us  [swap_by_core(): return lax.ppermute(x, AXES, pairs)]
    ppermute x22 -> x31, starting transfers between devices: 19.1 us -> 19.8 us  [swap(): return lax.ppermute(x, AXES, [(i, i ^ bit) for i in range(self.count)])]
  transfers between devices with their start and end apart: 33 -> 47, of which waited for: 16 -> 24; matrix products, arithmetic and copies ran while one was open for 9% -> 8% of each run, Pallas kernels for 21% -> 25%
where the time goes in v10:
time: 462 us; the launch traced here: 456 us
  waiting for transfers between devices  207 us (45%)
  Pallas kernels  139 us (30%)
  starting transfers between devices  38.3 us (8%)
  local copies, waits for them, and re-layouts  37.9 us (8%)
  other arithmetic  25.5 us (6%)
  matrix products  6.71 us (1%)
    pallas_call x26, Pallas kernels, call(): pl.pallas_call(kernel, out_shape=outs, grid_spec=pltpu.PrefetchScalarGrid...  139 us
    ppermute x31, waiting for transfers between devices, swap(): return lax.ppermute(x, AXES, [(i, i ^ bit) for i in range(self.count)])  104 us
    ppermute x16, waiting for transfers between devices, swap_by_core(): return lax.ppermute(x, AXES, pairs)  103 us
    unnamed x142, local copies, waits for them, and re-layouts  21.5 us
    ppermute x31, starting transfers between devices, swap(): return lax.ppermute(x, AXES, [(i, i ^ bit) for i in range(self.count)])  19.8 us
    ppermute x16, starting transfers between devices, swap_by_core(): return lax.ppermute(x, AXES, pairs)  18.5 us
    concatenate x16, other arithmetic, join(): self.x = jnp.concatenate((self.x, self.got), axis=0)  13.7 us
  transfers between devices with their start and end apart: 47, of which 24 were waited for; matrix products, arithmetic and copies ran while one was open for 8% of the time, Pallas kernels for 25%

profile of v10, /device:TPU:0, one launch (start us, length us, event | category | flops | bytes accessed | tf_op | source)
XLA Modules:
  0.0 456.3 jit_solution(9959540756516147495)
XLA Ops:
  10.3 7.5 %collective-permute-done = bf16[24,3200]{1,0:T(8,128)(2,1)S(1)} collective-permute-done((bf16[24,3200]{1,0:T(8,128)(2,1)}, bf16[24,3200]{1,0:T(8,128)(2,1)S(1)}, u32[]{:S(2)}, u32[]{:S(2)}) %collective-permute-start) | collective-permute-done | bytes 153632 | tf_op jit(solution)/shard_map/ppermute | solution.py:35
  22.9 10.5 %collective-permute-done.1 = bf16[48,3200]{1,0:T(8,128)(2,1)S(1)} collective-permute-done((bf16[48,3200]{1,0:T(8,128)(2,1)S(1)}, bf16[48,3200]{1,0:T(8,128)(2,1)S(1)}, u32[]{:S(2)}, u32[]{:S(2)}) %collective-permute-start.1) | collective-permute-done | bytes 307232 | tf_op jit(solution)/shard_map/ppermute | solution.py:35
  39.4 9.6 %collective-permute-done.3 = bf16[96,3200]{1,0:T(8,128)(2,1)S(1)} collective-permute-done((bf16[96,3200]{1,0:T(8,128)(2,1)S(1)}, bf16[96,3200]{1,0:T(8,128)(2,1)S(1)}, u32[]{:S(2)}, u32[]{:S(2)}) %collective-permute-start.3) | collective-permute-done | bytes 614432 | tf_op jit(solution)/shard_map/ppermute | solution.py:39
  53.7 24.3 %collective-permute-done.5 = bf16[192,3200]{1,0:T(8,128)(2,1)S(1)} collective-permute-done((bf16[192,3200]{1,0:T(8,128)(2,1)S(1)}, bf16[192,3200]{1,0:T(8,128)(2,1)S(1)}, u32[]{:S(2)}, u32[]{:S(2)}) %collective-permute-start.5) | collective-permute-done | bytes 1228832 | tf_op jit(solution)/shard_map/ppermute | solution.py:39
  81.6 9.8 %collective-permute-done.7 = bf16[24,6144]{1,0:T(8,128)(2,1)S(1)} collective-permute-done((bf16[24,6144]{1,0:T(8,128)(2,1)S(1)}, bf16[24,6144]{1,0:T(8,128)(2,1)S(1)}, u32[]{:S(2)}, u32[]{:S(2)}) %collective-permute-start.7) | collective-permute-done | bytes 294944 | tf_op jit(solution)/shard_map/ppermute | solution.py:35
  96.6 10.2 %collective-permute-done.9 = bf16[48,6144]{1,0:T(8,128)(2,1)S(1)} collective-permute-done((bf16[48,6144]{1,0:T(8,128)(2,1)S(1)}, bf16[48,6144]{1,0:T(8,128)(2,1)S(1)}, u32[]{:S(2)}, u32[]{:S(2)}) %collective-permute-start.9) | collective-permute-done | bytes 589856 | tf_op jit(solution)/shard_map/ppermute | solution.py:35
  116.1 15.4 %collective-permute-done.11 = bf16[24,6144]{1,0:T(8,128)(2,1)S(1)} collective-permute-done((bf16[24,6144]{1,0:T(8,128)(2,1)S(1)}, bf16[24,6144]{1,0:T(8,128)(2,1)S(1)}, u32[]{:S(2)}, u32[]{:S(2)}) %collective-permute-start.11) | collective-permute-done | bytes 294944 | tf_op jit(solution)/shard_map/ppermute | solution.py:35
  140.2 8.5 %collective-permute-done.14 = bf16[48,6144]{1,0:T(8,128)(2,1)S(1)} collective-permute-done((bf16[48,6144]{1,0:T(8,128)(2,1)S(1)}, bf16[48,6144]{1,0:T(8,128)(2,1)S(1)}, u32[]{:S(2)}, u32[]{:S(2)}) %collective-permute-start.14) | collective-permute-done | bytes 589856 | tf_op jit(solution)/shard_map/ppermute | solution.py:35
  148.9 11.9 %collective-permute-done.15 = bf16[192,6144]{1,0:T(8,128)(2,1)S(1)} collective-permute-done((bf16[192,6144]{1,0:T(8,128)(2,1)S(1)}, bf16[192,6144]{1,0:T(8,128)(2,1)S(1)}, u32[]{:S(2)}, u32[]{:S(2)}) %collective-permute-start.15) | collective-permute-done | bytes 2359328 | tf_op jit(solution)/shard_map/ppermute | solution.py:39
  165.4 14.4 %collective-permute-done.16 = bf16[96,6144]{1,0:T(8,128)(2,1)S(1)} collective-permute-done((bf16[96,6144]{1,0:T(8,128)(2,1)S(1)}, bf16[96,6144]{1,0:T(8,128)(2,1)S(1)}, u32[]{:S(2)}, u32[]{:S(2)}) %collective-permute-start.16) | collective-permute-done | bytes 1179680 | tf_op jit(solution)/shard_map/ppermute | solution.py:39
  191.6 7.0 %shard_map.427 = (f32[128,768]{1,0:T(8,128)S(1)}, bf16[2,128,768]{2,1,0:T(8,128)(2,1)S(1)}, bf16[3,128,768]{2,1,0:T(8,128)(2,1)S(1)}) custom-call(f32[128,768]{1,0:T(8,128)S(1)} %get-tuple-element.384.x_ref, f32[16,768]{1,0:T(8,128)S(1)} %fusion.11.vec_ref, bf16[768,768]{1,0:T(8,128)(2,1)S(1)} %fusion.order_ref, ...), custom_call_target="tpu_custom_call" | custom-call | flops 1000 | bytes 1000 | tf_op jit(solution)/shard_map/pallas_call | solution.py:569
  198.6 9.5 %shard_map.429 = (f32[128,768]{1,0:T(8,128)S(1)}, bf16[2,128,768]{2,1,0:T(8,128)(2,1)S(1)}, bf16[128,768]{1,0:T(8,128)(2,1)S(1)}) custom-call(s32[2]{0:T(128)S(1)} %copy-done.59, f32[128,768]{1,0:T(8,128)S(1)} %get-tuple-element.387.x_ref, f32[16,768]{1,0:T(8,128)S(1)} %fusion.11.vec_ref, bf16[768,768]{1,0:T(8,128)(2,1)S(1)} %fusion.order_ref, ...), custom_call_target="tpu_custom_call" | custom-call | flops 1000 | bytes 1000 | tf_op jit(solution)/shard_map/pallas_call | solution.py:569
  214.7 6.9 %collective-permute-done.19.up2_ref.down2_ref = bf16[384,6144]{1,0:T(8,128)(2,1)S(1)} collective-permute-done((bf16[384,6144]{1,0:T(8,128)(2,1)S(1)}, bf16[384,6144]{1,0:T(8,128)(2,1)S(1)}, u32[]{:S(2)}, u32[]{:S(2)}) %collective-permute-start.19) | collective-permute-done | bytes 4718624 | tf_op jit(solution)/shard_map/ppermute | solution.py:35
  225.0 7.7 %shard_map.430 = (f32[128,768]{1,0:T(8,128)S(1)}, f32[8,768]{1,0:T(8,128)S(1)}, bf16[5,128,768]{2,1,0:T(8,128)(2,1)S(1)}, bf16[5,128,768]{2,1,0:T(8,128)(2,1)S(1)}) custom-call(f32[128,768]{1,0:T(8,128)S(1)} %get-tuple-element.400.x_ref, f32[16,768]{1,0:T(8,128)S(1)} %fusion.11.vec_ref, bf16[768,768]{1,0:T(8,128)(2,1)S(1)} %fusion.order_ref, ...), custom_call_target="tpu_custom_call" | custom-call | flops 1000 | bytes 1000 | tf_op jit(solution)/shard_map/pallas_call | solution.py:569
  247.4 12.0 %shard_map.433 = (f32[128,768]{1,0:T(8,128)S(1)}, f32[8,768]{1,0:T(8,128)S(1)}, bf16[2,128,768]{2,1,0:T(8,128)(2,1)}, bf16[1152,1536]{1,0:T(8,128)(2,1)S(1)}) custom-call(s32[2]{0:T(128)S(1)} %copy-done.59, f32[128,768]{1,0:T(8,128)S(1)} %get-tuple-element.387.x_ref, f32[16,768]{1,0:T(8,128)S(1)} %fusion.11.vec_ref, bf16[768,768]{1,0:T(8,128)(2,1)S(1)} %fusion.order_ref, ...), custom_call_target="tpu_custom_call" | custom-call | flops 1000 | bytes 1000 | tf_op jit(solution)/shard_map/pallas_call | solution.py:569
  265.0 11.2 %shard_map.435 = (f32[128,768]{1,0:T(8,128)S(1)}, f32[8,768]{1,0:T(8,128)S(1)}, bf16[4,128,768]{2,1,0:T(8,128)(2,1)}) custom-call(f32[128,768]{1,0:T(8,128)S(1)} %get-tuple-element.384.x_ref, f32[16,768]{1,0:T(8,128)S(1)} %fusion.11.vec_ref, bf16[768,768]{1,0:T(8,128)(2,1)S(1)} %fusion.order_ref, bf16[3,128,768]{2,1,0:T(8,128)(2,1)S(1)} %copy-done.35, ...), custom_call_target="tpu_custom_call" | custom-call | flops 1000 | bytes 1000 | tf_op jit(solution)/shard_map/pallas_call | solution.py:569
  287.9 8.2 %shard_map.437 = (bf16[192,6144]{1,0:T(8,128)(2,1)}, bf16[192,6144]{1,0:T(8,128)(2,1)S(1)}) custom-call(bf16[768,768]{1,0:T(8,128)(2,1)S(1)} %fusion.order_ref, bf16[2,128,768]{2,1,0:T(8,128)(2,1)S(1)} %copy-done.44, bf16[2,128,768]{2,1,0:T(8,128)(2,1)S(1)} %copy-done.48, bf16[4,128,768]{2,1,0:T(8,128)(2,1)} %get-tuple-element.436.sd_ref, ...), custom_call_target="tpu_custom_call" | custom-call | flops 1000 | bytes 1000 | tf_op jit(solution)/shard_map/pallas_call | solution.py:569
  317.7 10.9 %shard_map.440 = (f32[128,768]{1,0:T(8,128)S(1)}, f32[8,768]{1,0:T(8,128)}, bf16[5,128,768]{2,1,0:T(8,128)(2,1)S(1)}) custom-call(bf16[128,768]{1,0:T(8,128)(2,1)S(1)} %bitcast.39, f32[16,768]{1,0:T(8,128)S(1)} %fusion.11.vec_ref, bf16[768,768]{1,0:T(8,128)(2,1)S(1)} %fusion.order_ref, bf16[3,128,768]{2,1,0:T(8,128)(2,1)S(1)} %copy-done.33, ...), custom_call_target="tpu_custom_call" | custom-call | flops 1000 | bytes 1000 | tf_op jit(solution)/shard_map/pallas_call | solution.py:569
  331.5 7.5 %collective-permute-done.32.got_ref = bf16[192,6144]{1,0:T(8,128)(2,1)} collective-permute-done((bf16[192,6144]{1,0:T(8,128)(2,1)}, bf16[192,6144]{1,0:T(8,128)(2,1)}, u32[]{:S(2)}, u32[]{:S(2)}) %collective-permute-start.32) | collective-permute-done | bytes 2359328 | tf_op jit(solution)/shard_map/ppermute | solution.py:39
  342.8 8.2 %shard_map.443 = bf16[1152,768]{1,0:T(8,128)(2,1)} custom-call(bf16[1152,1536]{1,0:T(8,128)(2,1)S(1)} %get-tuple-element.477.dkv_ref, bf16[768,768]{1,0:T(8,128)(2,1)S(1)} %fusion.order_ref, bf16[384,6144]{1,0:T(8,128)(2,1)} %pad_maximum_fusion.1.top_ref, bf16[384,6144]{1,0:T(8,128)(2,1)} %collective-permute-done.17.low_ref), custom_call_target="tpu_custom_call" | custom-call | flops 1000 | bytes 1000 | tf_op jit(solution)/shard_map/pallas_call | solution.py:569
  361.1 15.5 %collective-permute-done.35.got_ref = bf16[96,6144]{1,0:T(8,128)(2,1)S(1)} collective-permute-done((bf16[96,6144]{1,0:T(8,128)(2,1)}, bf16[96,6144]{1,0:T(8,128)(2,1)S(1)}, u32[]{:S(2)}, u32[]{:S(2)}) %collective-permute-start.35) | collective-permute-done | bytes 1179680 | tf_op jit(solution)/shard_map/ppermute | solution.py:39
  387.0 6.5 %collective-permute-done.38 = bf16[48,6144]{1,0:T(8,128)(2,1)} collective-permute-done((bf16[48,6144]{1,0:T(8,128)(2,1)}, bf16[48,6144]{1,0:T(8,128)(2,1)}, u32[]{:S(2)}, u32[]{:S(2)}) %collective-permute-start.38) | collective-permute-done | bytes 589856 | tf_op jit(solution)/shard_map/ppermute | solution.py:35
  396.7 17.3 %collective-permute-done.39.got_ref = bf16[96,6144]{1,0:T(8,128)(2,1)S(1)} collective-permute-done((bf16[96,6144]{1,0:T(8,128)(2,1)}, bf16[96,6144]{1,0:T(8,128)(2,1)S(1)}, u32[]{:S(2)}, u32[]{:S(2)}) %collective-permute-start.39) | collective-permute-done | bytes 1179680 | tf_op jit(solution)/shard_map/ppermute | solution.py:39
  419.9 8.0 %collective-permute-done.42 = bf16[48,6144]{1,0:T(8,128)(2,1)S(1)} collective-permute-done((bf16[48,6144]{1,0:T(8,128)(2,1)S(1)}, bf16[48,6144]{1,0:T(8,128)(2,1)S(1)}, u32[]{:S(2)}, u32[]{:S(2)}) %collective-permute-start.42) | collective-permute-done | bytes 589856 | tf_op jit(solution)/shard_map/ppermute | solution.py:35
  (307 shorter events, 196.1 us)
Async XLA Ops:
  19.6 16.8 %collective-permute-start.2 = (bf16[24,6144]{1,0:T(8,128)(2,1)}, bf16[24,6144]{1,0:T(8,128)(2,1)S(1)}, u32[]{:S(2)}, u32[]{:S(2)}) collective-permute-start(bf16[24,6144]{1,0:T(8,128)(2,1)} %get-tuple-element.306), channel_id=1, source_target_pairs={{0,16},{1,17},{2,18},{3,19},{4,20},{5,21},{6,22},{7,23},{8,24},{9,... | collective-permute-start | bytes 884744 | tf_op jit(solution)/shard_map/ppermute | solution.py:35
  49.1 29.0 %collective-permute-start.5 = (bf16[192,3200]{1,0:T(8,128)(2,1)S(1)}, bf16[192,3200]{1,0:T(8,128)(2,1)S(1)}, u32[]{:S(2)}, u32[]{:S(2)}) collective-permute-start(bf16[192,3200]{1,0:T(8,128)(2,1)S(1)} %pad_maximum_fusion.7), channel_id=1, source_target_pairs={{0,4},{1,5},{2,3},{3,2},{4,0},{5,1},{6,7},{7,6},{8,12},{9,13},{10,... | collective-permute-start | bytes 3686408 | tf_op jit(solution)/shard_map/ppermute | solution.py:39
  52.1 27.6 %collective-permute-start.6 = (bf16[96,6144]{1,0:T(8,128)(2,1)S(1)}, bf16[96,6144]{1,0:T(8,128)(2,1)}, u32[]{:S(2)}, u32[]{:S(2)}) collective-permute-start(bf16[96,6144]{1,0:T(8,128)(2,1)S(1)} %pad_maximum_fusion.10), channel_id=1, source_target_pairs={{0,1},{1,0},{2,6},{3,7},{4,5},{5,4},{6,2},{7,3},{8,9},{9,8},{10,14... | collective-permute-start | bytes 3538952 | tf_op jit(solution)/shard_map/ppermute | solution.py:39
  81.2 32.3 %collective-permute-start.10 = (bf16[192,6144]{1,0:T(8,128)(2,1)S(1)}, bf16[192,6144]{1,0:T(8,128)(2,1)S(1)}, u32[]{:S(2)}, u32[]{:S(2)}) collective-permute-start(bf16[192,6144]{1,0:T(8,128)(2,1)S(1)} %pad_maximum_fusion.4), channel_id=1, source_target_pairs={{0,4},{1,5},{2,3},{3,2},{4,0},{5,1},{6,7},{7,6},{8,12},{9,13},{10,... | collective-permute-start | bytes 7077896 | tf_op jit(solution)/shard_map/ppermute | solution.py:39
  114.5 19.3 %collective-permute-start.13 = (bf16[384,6144]{1,0:T(8,128)(2,1)S(1)}, bf16[384,6144]{1,0:T(8,128)(2,1)S(1)}, u32[]{:S(2)}, u32[]{:S(2)}) collective-permute-start(bf16[384,6144]{1,0:T(8,128)(2,1)S(1)} %pad_maximum_fusion.up_ref.down_ref), channel_id=1, source_target_pairs={{0,2},{1,3},{2,0},{3,1},{4,6},{5,7},{6,4},{7,5},{8,10},{9,11},{10,... | collective-permute-start | bytes 14155784 | tf_op jit(solution)/shard_map/ppermute | solution.py:35
  114.5 17.1 %collective-permute-start.12 = (bf16[96,6144]{1,0:T(8,128)(2,1)S(1)}, bf16[96,6144]{1,0:T(8,128)(2,1)S(1)}, u32[]{:S(2)}, u32[]{:S(2)}) collective-permute-start(bf16[96,6144]{1,0:T(8,128)(2,1)S(1)} %pad_maximum_fusion.11), channel_id=1, source_target_pairs={{0,1},{1,0},{2,6},{3,7},{4,5},{5,4},{6,2},{7,3},{8,9},{9,8},{10,14... | collective-permute-start | bytes 3538952 | tf_op jit(solution)/shard_map/ppermute | solution.py:39
  114.8 16.7 %collective-permute-start.11 = (bf16[24,6144]{1,0:T(8,128)(2,1)S(1)}, bf16[24,6144]{1,0:T(8,128)(2,1)S(1)}, u32[]{:S(2)}, u32[]{:S(2)}) collective-permute-start(bf16[24,6144]{1,0:T(8,128)(2,1)S(1)} %copy-done.65), channel_id=1, source_target_pairs={{0,16},{1,17},{2,18},{3,19},{4,20},{5,21},{6,22},{7,23},{8,24},{9,... | collective-permute-start | bytes 884744 | tf_op jit(solution)/shard_map/ppermute | solution.py:35
  131.8 28.9 %collective-permute-start.15 = (bf16[192,6144]{1,0:T(8,128)(2,1)S(1)}, bf16[192,6144]{1,0:T(8,128)(2,1)S(1)}, u32[]{:S(2)}, u32[]{:S(2)}) collective-permute-start(bf16[192,6144]{1,0:T(8,128)(2,1)S(1)} %pad_maximum_fusion.5), channel_id=1, source_target_pairs={{0,4},{1,5},{2,3},{3,2},{4,0},{5,1},{6,7},{7,6},{8,12},{9,13},{10,... | collective-permute-start | bytes 7077896 | tf_op jit(solution)/shard_map/ppermute | solution.py:39
  163.5 22.4 %collective-permute-start.17 = (bf16[384,6144]{1,0:T(8,128)(2,1)}, bf16[384,6144]{1,0:T(8,128)(2,1)}, u32[]{:S(2)}, u32[]{:S(2)}) collective-permute-start(bf16[384,6144]{1,0:T(8,128)(2,1)} %pad_maximum_fusion.1.top_ref), channel_id=1, source_target_pairs={{0,2},{1,3},{2,0},{3,1},{4,6},{5,7},{6,4},{7,5},{8,10},{9,11},{10,... | collective-permute-start | bytes 14155784 | tf_op jit(solution)/shard_map/ppermute | solution.py:35
  163.5 16.3 %collective-permute-start.16 = (bf16[96,6144]{1,0:T(8,128)(2,1)S(1)}, bf16[96,6144]{1,0:T(8,128)(2,1)S(1)}, u32[]{:S(2)}, u32[]{:S(2)}) collective-permute-start(bf16[96,6144]{1,0:T(8,128)(2,1)S(1)} %pad_maximum_fusion.12), channel_id=1, source_target_pairs={{0,1},{1,0},{2,6},{3,7},{4,5},{5,4},{6,2},{7,3},{8,9},{9,8},{10,14... | collective-permute-start | bytes 3538952 | tf_op jit(solution)/shard_map/ppermute | solution.py:39
  181.4 29.2 %collective-permute-start.18 = (bf16[192,6144]{1,0:T(8,128)(2,1)}, bf16[192,6144]{1,0:T(8,128)(2,1)}, u32[]{:S(2)}, u32[]{:S(2)}) collective-permute-start(bf16[192,6144]{1,0:T(8,128)(2,1)} %pad_maximum_fusion.6), channel_id=1, source_target_pairs={{0,4},{1,5},{2,3},{3,2},{4,0},{5,1},{6,7},{7,6},{8,12},{9,13},{10,... | collective-permute-start | bytes 7077896 | tf_op jit(solution)/shard_map/ppermute | solution.py:39
  245.6 31.1 %collective-permute-start.26 = (bf16[192,6144]{1,0:T(8,128)(2,1)}, bf16[192,6144]{1,0:T(8,128)(2,1)}, u32[]{:S(2)}, u32[]{:S(2)}) collective-permute-start(bf16[192,6144]{1,0:T(8,128)(2,1)} %get-tuple-element.423), channel_id=1, source_target_pairs={{0,4},{1,5},{2,3},{3,2},{4,0},{5,1},{6,7},{7,6},{8,12},{9,13},{10,... | collective-permute-start | bytes 7077896 | tf_op jit(solution)/shard_map/ppermute | solution.py:39
  264.9 17.9 %collective-permute-start.29 = (bf16[384,1536]{1,0:T(8,128)(2,1)}, bf16[384,1536]{1,0:T(8,128)(2,1)S(1)}, u32[]{:S(2)}, u32[]{:S(2)}) collective-permute-start(bf16[384,1536]{1,0:T(8,128)(2,1)} %get-tuple-element.432), channel_id=1, source_target_pairs={{0,2},{1,3},{2,0},{3,1},{4,6},{5,7},{6,4},{7,5},{8,10},{9,11},{10,... | collective-permute-start | bytes 3538952 | tf_op jit(solution)/shard_map/ppermute | solution.py:35
  297.6 41.5 %collective-permute-start.32 = (bf16[192,6144]{1,0:T(8,128)(2,1)}, bf16[192,6144]{1,0:T(8,128)(2,1)}, u32[]{:S(2)}, u32[]{:S(2)}) collective-permute-start(bf16[192,6144]{1,0:T(8,128)(2,1)} %get-tuple-element.470), channel_id=1, source_target_pairs={{0,4},{1,5},{2,3},{3,2},{4,0},{5,1},{6,7},{7,6},{8,12},{9,13},{10,... | collective-permute-start | bytes 7077896 | tf_op jit(solution)/shard_map/ppermute | solution.py:39
  298.1 30.5 %collective-permute-start.31 = (bf16[96,6144]{1,0:T(8,128)(2,1)}, bf16[96,6144]{1,0:T(8,128)(2,1)}, u32[]{:S(2)}, u32[]{:S(2)}) collective-permute-start(bf16[96,6144]{1,0:T(8,128)(2,1)} %copy-done.60), channel_id=1, source_target_pairs={{0,1},{1,0},{2,6},{3,7},{4,5},{5,4},{6,2},{7,3},{8,9},{9,8},{10,14... | collective-permute-start | bytes 3538952 | tf_op jit(solution)/shard_map/ppermute | solution.py:39
  330.3 20.7 %collective-permute-start.33 = (bf16[48,6144]{1,0:T(8,128)(2,1)S(1)}, bf16[48,6144]{1,0:T(8,128)(2,1)}, u32[]{:S(2)}, u32[]{:S(2)}) collective-permute-start(bf16[48,6144]{1,0:T(8,128)(2,1)S(1)} %get-tuple-element.480), channel_id=1, source_target_pairs={{0,8},{1,9},{2,10},{3,11},{4,12},{5,13},{6,14},{7,15},{8,0},{9,1},... | collective-permute-start | bytes 1769480 | tf_op jit(solution)/shard_map/ppermute | solution.py:35
  331.0 22.1 %collective-permute-start.34 = (bf16[5,128,768]{2,1,0:T(8,128)(2,1)S(1)}, bf16[5,128,768]{2,1,0:T(8,128)(2,1)}, u32[]{:S(2)}, u32[]{:S(2)}) collective-permute-start(bf16[5,128,768]{2,1,0:T(8,128)(2,1)S(1)} %get-tuple-element.489.sd_ref), channel_id=1, source_target_pairs={{0,2},{1,3},{2,0},{3,1},{4,6},{5,7},{6,4},{7,5},{8,10},{9,11},{10,... | collective-permute-start | bytes 2949128 | tf_op jit(solution)/shard_map/ppermute | solution.py:35
  331.1 48.0 %collective-permute-start.36 = (bf16[192,6144]{1,0:T(8,128)(2,1)}, bf16[192,6144]{1,0:T(8,128)(2,1)S(1)}, u32[]{:S(2)}, u32[]{:S(2)}) collective-permute-start(bf16[192,6144]{1,0:T(8,128)(2,1)} %get-tuple-element.501), channel_id=1, source_target_pairs={{0,4},{1,5},{2,3},{3,2},{4,0},{5,1},{6,7},{7,6},{8,12},{9,13},{10,... | collective-permute-start | bytes 7077896 | tf_op jit(solution)/shard_map/ppermute | solution.py:39
  352.1 25.8 %collective-permute-start.37 = (bf16[24,6144]{1,0:T(8,128)(2,1)S(1)}, bf16[24,6144]{1,0:T(8,128)(2,1)S(1)}, u32[]{:S(2)}, u32[]{:S(2)}) collective-permute-start(bf16[24,6144]{1,0:T(8,128)(2,1)S(1)} %add_convert_fusion.5), channel_id=1, source_target_pairs={{0,16},{1,17},{2,18},{3,19},{4,20},{5,21},{6,22},{7,23},{8,24},{9,... | collective-permute-start | bytes 884744 | tf_op jit(solution)/shard_map/ppermute | solution.py:35
  353.1 23.6 %collective-permute-start.35 = (bf16[96,6144]{1,0:T(8,128)(2,1)}, bf16[96,6144]{1,0:T(8,128)(2,1)S(1)}, u32[]{:S(2)}, u32[]{:S(2)}) collective-permute-start(bf16[96,6144]{1,0:T(8,128)(2,1)} %get-tuple-element.494), channel_id=1, source_target_pairs={{0,1},{1,0},{2,6},{3,7},{4,5},{5,4},{6,2},{7,3},{8,9},{9,8},{10,14... | collective-permute-start | bytes 3538952 | tf_op jit(solution)/shard_map/ppermute | solution.py:39
  385.0 29.0 %collective-permute-start.39 = (bf16[96,6144]{1,0:T(8,128)(2,1)}, bf16[96,6144]{1,0:T(8,128)(2,1)S(1)}, u32[]{:S(2)}, u32[]{:S(2)}) collective-permute-start(bf16[96,6144]{1,0:T(8,128)(2,1)} %copy-done.61), channel_id=1, source_target_pairs={{0,1},{1,0},{2,6},{3,7},{4,5},{5,4},{6,2},{7,3},{8,9},{9,8},{10,14... | collective-permute-start | bytes 3538952 | tf_op jit(solution)/shard_map/ppermute | solution.py:39
  385.5 32.8 %collective-permute-start.40 = (bf16[192,3200]{1,0:T(8,128)(2,1)}, bf16[192,3200]{1,0:T(8,128)(2,1)S(1)}, u32[]{:S(2)}, u32[]{:S(2)}) collective-permute-start(bf16[192,3200]{1,0:T(8,128)(2,1)} %pad_maximum_fusion.8), channel_id=1, source_target_pairs={{0,4},{1,5},{2,3},{3,2},{4,0},{5,1},{6,7},{7,6},{8,12},{9,13},{10,... | collective-permute-start | bytes 3686408 | tf_op jit(solution)/shard_map/ppermute | solution.py:39
  394.5 21.9 %collective-permute-start.41 = (bf16[24,6144]{1,0:T(8,128)(2,1)S(1)}, bf16[24,6144]{1,0:T(8,128)(2,1)S(1)}, u32[]{:S(2)}, u32[]{:S(2)}) collective-permute-start(bf16[24,6144]{1,0:T(8,128)(2,1)S(1)} %add_convert_fusion.3), channel_id=1, source_target_pairs={{0,16},{1,17},{2,18},{3,19},{4,20},{5,21},{6,22},{7,23},{8,24},{9,... | collective-permute-start | bytes 884744 | tf_op jit(solution)/shard_map/ppermute | solution.py:35
  419.4 16.3 %collective-permute-start.43 = (bf16[96,3200]{1,0:T(8,128)(2,1)}, bf16[96,3200]{1,0:T(8,128)(2,1)S(1)}, u32[]{:S(2)}, u32[]{:S(2)}) collective-permute-start(bf16[96,3200]{1,0:T(8,128)(2,1)} %get-tuple-element.539), channel_id=1, source_target_pairs={{0,1},{1,0},{2,6},{3,7},{4,5},{5,4},{6,2},{7,3},{8,9},{9,8},{10,14... | collective-permute-start | bytes 1843208 | tf_op jit(solution)/shard_map/ppermute | solution.py:39
  (94 other events, 978.0 us)

commit v11 on v10

--- a/solution.py
+++ b/solution.py
@@ -565,7 +565,7 @@
     return pl.BlockSpec(x.shape, lambda *_: (0,) * len(x.shape))
 
 
-def call(kernel, steps, ins, in_specs, outs, out_specs, scratch=(), scalars=0, vmem=40):
+def call(kernel, steps, ins, in_specs, outs, out_specs, scratch=(), scalars=0, vmem=24):
     return pl.pallas_call(
         kernel,
         out_shape=outs,
@@ -812,24 +812,24 @@
     x0 = go(x0, [first])
     x0 = go(x0, [feed], [middle])
     x0 = go(x0, [first])
-    x0 = go(x0, [feed])
     for k in range(steps - 1):
         x0 = go(x0, [middle])
+    x0 = go(x0, [feed])
     x0, (order, enc_rel, enc_t) = tie(x0, order, enc_rel, enc_t)
     x0, w_first = end(x0, first)
     vec = tn(jnp.concatenate([x[:, 4 * d :] for x in w_first], axis=0), order)[:16]
     net = Layers(captions, captions * length, d, vec, order, patch_count)
     x0 = go(x0, [middle], [last])
     x0a, f_us, k_us = net.self_forward(x0, w_first, 0, 0)
-    x0a = go(x0a, [feed])
     for k in range(steps - 1):
         x0a = go(x0a, [last])
     x0a = go(x0a, [middle])
+    x0a = go(x0a, [last])
+    x0a = go(x0a, [feed])
     x0a, w_feed = end(x0a, feed)
     x1, f_uf, k_uf = net.feed_forward(x0a, w_feed, 2)
     x1 = go(x1, [last])
     x1 = go(x1, [middle])
-    x1 = go(x1, [last])
     x1, w_middle = end(x1, middle)
     x1a, f_ms, k_ms = net.self_forward(x1, w_middle, 4, 4)
     kv = net.pair_forward(enc_rel, w_middle)

time: 462 us -> 450 us (0.974)
  local copies, waits for them, and re-layouts: 37.9 us -> 22.5 us
  waiting for transfers between devices: 207 us -> 221 us
  Pallas kernels: 139 us -> 129 us
    ppermute x16, waiting for transfers between devices: 103 us -> 124 us  [swap_by_core(): return lax.ppermute(x, AXES, pairs)]
    unnamed x142 -> x88, local copies, waits for them, and re-layouts: 21.5 us -> 3.34 us
    pallas_call x26, Pallas kernels: 139 us -> 129 us  [call(): pl.pallas_call(kernel, out_shape=outs, grid_spec=pltpu.PrefetchScalarGrid...]
    ppermute x31, waiting for transfers between devices: 104 us -> 97.4 us  [swap(): return lax.ppermute(x, AXES, [(i, i ^ bit) for i in range(self.count)])]
  transfers between devices with their start and end apart: 47 -> 47, of which waited for: 24 -> 31; matrix products, arithmetic and copies ran while one was open for 8% -> 8% of each run, Pallas kernels for 25% -> 24%
where the time goes in v11:
time: 450 us; the launch traced here: 445 us
  waiting for transfers between devices  221 us (49%)
  Pallas kernels  129 us (29%)
  starting transfers between devices  42.6 us (9%)
  local copies, waits for them, and re-layouts  22.5 us (5%)
  other arithmetic  22.2 us (5%)
  matrix products  5.78 us (1%)
    pallas_call x26, Pallas kernels, call(): pl.pallas_call(kernel, out_shape=outs, grid_spec=pltpu.PrefetchScalarGrid...  129 us
    ppermute x16, waiting for transfers between devices, swap_by_core(): return lax.ppermute(x, AXES, pairs)  124 us
    ppermute x31, waiting for transfers between devices, swap(): return lax.ppermute(x, AXES, [(i, i ^ bit) for i in range(self.count)])  97.4 us
    ppermute x31, starting transfers between devices, swap(): return lax.ppermute(x, AXES, [(i, i ^ bit) for i in range(self.count)])  22.1 us
    ppermute x16, starting transfers between devices, swap_by_core(): return lax.ppermute(x, AXES, pairs)  20.6 us
    concatenate x16, other arithmetic, join(): self.x = jnp.concatenate((self.x, self.got), axis=0)  11.9 us
  transfers between devices with their start and end apart: 47, of which 31 were waited for; matrix products, arithmetic and copies ran while one was open for 8% of the time, Pallas kernels for 24%

profile of v11, /device:TPU:0, one launch (start us, length us, event | category | flops | bytes accessed | tf_op | source)
XLA Modules:
  0.0 445.0 jit_solution(18209833631807493651)
XLA Ops:
  10.3 7.5 %collective-permute-done = bf16[24,3200]{1,0:T(8,128)(2,1)S(1)} collective-permute-done((bf16[24,3200]{1,0:T(8,128)(2,1)}, bf16[24,3200]{1,0:T(8,128)(2,1)S(1)}, u32[]{:S(2)}, u32[]{:S(2)}) %collective-permute-start) | collective-permute-done | bytes 153632 | tf_op jit(solution)/shard_map/ppermute | solution.py:35
  22.9 10.5 %collective-permute-done.1 = bf16[48,3200]{1,0:T(8,128)(2,1)S(1)} collective-permute-done((bf16[48,3200]{1,0:T(8,128)(2,1)S(1)}, bf16[48,3200]{1,0:T(8,128)(2,1)S(1)}, u32[]{:S(2)}, u32[]{:S(2)}) %collective-permute-start.1) | collective-permute-done | bytes 307232 | tf_op jit(solution)/shard_map/ppermute | solution.py:35
  39.4 9.6 %collective-permute-done.3 = bf16[96,3200]{1,0:T(8,128)(2,1)S(1)} collective-permute-done((bf16[96,3200]{1,0:T(8,128)(2,1)S(1)}, bf16[96,3200]{1,0:T(8,128)(2,1)S(1)}, u32[]{:S(2)}, u32[]{:S(2)}) %collective-permute-start.3) | collective-permute-done | bytes 614432 | tf_op jit(solution)/shard_map/ppermute | solution.py:39
  52.1 13.8 %collective-permute-done.5 = bf16[192,3200]{1,0:T(8,128)(2,1)S(1)} collective-permute-done((bf16[192,3200]{1,0:T(8,128)(2,1)S(1)}, bf16[192,3200]{1,0:T(8,128)(2,1)S(1)}, u32[]{:S(2)}, u32[]{:S(2)}) %collective-permute-start.5) | collective-permute-done | bytes 1228832 | tf_op jit(solution)/shard_map/ppermute | solution.py:39
  72.5 9.2 %collective-permute-done.6 = bf16[24,6144]{1,0:T(8,128)(2,1)S(1)} collective-permute-done((bf16[24,6144]{1,0:T(8,128)(2,1)S(1)}, bf16[24,6144]{1,0:T(8,128)(2,1)S(1)}, u32[]{:S(2)}, u32[]{:S(2)}) %collective-permute-start.6) | collective-permute-done | bytes 294944 | tf_op jit(solution)/shard_map/ppermute | solution.py:35
  84.6 14.1 %collective-permute-done.9 = bf16[48,6144]{1,0:T(8,128)(2,1)S(1)} collective-permute-done((bf16[48,6144]{1,0:T(8,128)(2,1)S(1)}, bf16[48,6144]{1,0:T(8,128)(2,1)S(1)}, u32[]{:S(2)}, u32[]{:S(2)}) %collective-permute-start.9) | collective-permute-done | bytes 589856 | tf_op jit(solution)/shard_map/ppermute | solution.py:35
  106.6 6.4 %shard_map.425 = (f32[128,768]{1,0:T(8,128)S(1)}, bf16[2,128,768]{2,1,0:T(8,128)(2,1)S(1)}, bf16[3,128,768]{2,1,0:T(8,128)(2,1)S(1)}) custom-call(bf16[128,768]{1,0:T(8,128)(2,1)S(1)} %bitcast.40, f32[16,768]{1,0:T(8,128)S(1)} %fusion.11.vec_ref, bf16[768,768]{1,0:T(8,128)(2,1)S(1)} %fusion.order_ref, bf16[384,3200]{1,0:T(8,128)(2,1)} %pad_maximum_fusion.3.top_ref, ...), custom_call_target="tpu_custom_call" | custom-call | flops 1000 | bytes 1000 | tf_op jit(solution)/shard_map/pallas_call | solution.py:569
  114.8 12.0 %collective-permute-done.11 = bf16[96,6144]{1,0:T(8,128)(2,1)S(1)} collective-permute-done((bf16[96,6144]{1,0:T(8,128)(2,1)S(1)}, bf16[96,6144]{1,0:T(8,128)(2,1)S(1)}, u32[]{:S(2)}, u32[]{:S(2)}) %collective-permute-start.11) | collective-permute-done | bytes 1179680 | tf_op jit(solution)/shard_map/ppermute | solution.py:39
  130.1 8.1 %collective-permute-done.13 = bf16[192,6144]{1,0:T(8,128)(2,1)S(1)} collective-permute-done((bf16[192,6144]{1,0:T(8,128)(2,1)S(1)}, bf16[192,6144]{1,0:T(8,128)(2,1)S(1)}, u32[]{:S(2)}, u32[]{:S(2)}) %collective-permute-start.13) | collective-permute-done | bytes 2359328 | tf_op jit(solution)/shard_map/ppermute | solution.py:39
  154.6 16.4 %collective-permute-done.15 = bf16[96,6144]{1,0:T(8,128)(2,1)S(1)} collective-permute-done((bf16[96,6144]{1,0:T(8,128)(2,1)S(1)}, bf16[96,6144]{1,0:T(8,128)(2,1)S(1)}, u32[]{:S(2)}, u32[]{:S(2)}) %collective-permute-start.15) | collective-permute-done | bytes 1179680 | tf_op jit(solution)/shard_map/ppermute | solution.py:39
  172.7 9.4 %collective-permute-done.16 = bf16[192,6144]{1,0:T(8,128)(2,1)S(1)} collective-permute-done((bf16[192,6144]{1,0:T(8,128)(2,1)S(1)}, bf16[192,6144]{1,0:T(8,128)(2,1)S(1)}, u32[]{:S(2)}, u32[]{:S(2)}) %collective-permute-start.16) | collective-permute-done | bytes 2359328 | tf_op jit(solution)/shard_map/ppermute | solution.py:39
  204.6 9.6 %shard_map.429 = (f32[128,768]{1,0:T(8,128)S(1)}, bf16[2,128,768]{2,1,0:T(8,128)(2,1)S(1)}, bf16[128,768]{1,0:T(8,128)(2,1)S(1)}) custom-call(s32[2]{0:T(128)S(1)} %copy-done.29, f32[128,768]{1,0:T(8,128)S(1)} %get-tuple-element.387.x_ref, f32[16,768]{1,0:T(8,128)S(1)} %copy-done.6, bf16[768,768]{1,0:T(8,128)(2,1)S(1)} %fusion.order_ref, ...), custom_call_target="tpu_custom_call" | custom-call | flops 1000 | bytes 1000 | tf_op jit(solution)/shard_map/pallas_call | solution.py:569
  218.3 6.9 %collective-permute-done.19.up2_ref.down2_ref = bf16[384,6144]{1,0:T(8,128)(2,1)S(1)} collective-permute-done((bf16[384,6144]{1,0:T(8,128)(2,1)S(1)}, bf16[384,6144]{1,0:T(8,128)(2,1)S(1)}, u32[]{:S(2)}, u32[]{:S(2)}) %collective-permute-start.19) | collective-permute-done | bytes 4718624 | tf_op jit(solution)/shard_map/ppermute | solution.py:35
  227.7 7.6 %shard_map.430 = (f32[128,768]{1,0:T(8,128)S(1)}, f32[8,768]{1,0:T(8,128)S(1)}, bf16[5,128,768]{2,1,0:T(8,128)(2,1)S(1)}, bf16[5,128,768]{2,1,0:T(8,128)(2,1)S(1)}) custom-call(f32[128,768]{1,0:T(8,128)S(1)} %get-tuple-element.400.x_ref, f32[16,768]{1,0:T(8,128)S(1)} %copy-done.6, bf16[768,768]{1,0:T(8,128)(2,1)S(1)} %fusion.order_ref, ...), custom_call_target="tpu_custom_call" | custom-call | flops 1000 | bytes 1000 | tf_op jit(solution)/shard_map/pallas_call | solution.py:569
  248.4 11.3 %shard_map.433 = (f32[128,768]{1,0:T(8,128)S(1)}, f32[8,768]{1,0:T(8,128)S(1)}, bf16[2,128,768]{2,1,0:T(8,128)(2,1)S(1)}, bf16[1152,1536]{1,0:T(8,128)(2,1)S(1)}) custom-call(s32[2]{0:T(128)S(1)} %copy-done.29, f32[128,768]{1,0:T(8,128)S(1)} %get-tuple-element.387.x_ref, f32[16,768]{1,0:T(8,128)S(1)} %copy-done.6, bf16[768,768]{1,0:T(8,128)(2,1)S(1)} %fusion.order_ref, ...), custom_call_target="tpu_custom_call" | custom-call | flops 1000 | bytes 1000 | tf_op jit(solution)/shard_map/pallas_call | solution.py:569
  263.6 10.3 %shard_map.435 = (f32[128,768]{1,0:T(8,128)S(1)}, f32[8,768]{1,0:T(8,128)S(1)}, bf16[4,128,768]{2,1,0:T(8,128)(2,1)S(1)}) custom-call(f32[128,768]{1,0:T(8,128)S(1)} %copy-done.10, f32[16,768]{1,0:T(8,128)S(1)} %copy-done.6, bf16[768,768]{1,0:T(8,128)(2,1)S(1)} %fusion.order_ref, bf16[3,128,768]{2,1,0:T(8,128)(2,1)S(1)} %get-tuple-element.407.qkv_ref, ...), custom_call_target="tpu_custom_call" | custom-call | flops 1000 | bytes 1000 | tf_op jit(solution)/shard_map/pallas_call | solution.py:569
  277.2 7.0 %shard_map.437 = (bf16[192,6144]{1,0:T(8,128)(2,1)}, bf16[192,6144]{1,0:T(8,128)(2,1)S(1)}) custom-call(bf16[768,768]{1,0:T(8,128)(2,1)S(1)} %fusion.order_ref, bf16[2,128,768]{2,1,0:T(8,128)(2,1)S(1)} %get-tuple-element.434.s_ref, bf16[2,128,768]{2,1,0:T(8,128)(2,1)S(1)} %collective-permute-done.22.s2_ref, ...), custom_call_target="tpu_custom_call" | custom-call | flops 1000 | bytes 1000 | tf_op jit(solution)/shard_map/pallas_call | solution.py:569
  286.7 6.5 %shard_map.438 = (f32[128,768]{1,0:T(8,128)S(1)}, f32[8,768]{1,0:T(8,128)S(1)}, bf16[5,128,768]{2,1,0:T(8,128)(2,1)S(1)}) custom-call(f32[128,768]{1,0:T(8,128)S(1)} %copy-done.14, f32[16,768]{1,0:T(8,128)S(1)} %copy-done.6, bf16[768,768]{1,0:T(8,128)(2,1)S(1)} %fusion.order_ref, f32[128,768]{1,0:T(8,128)S(1)} %get-tuple-element.445.dx_ref, ...), custom_call_target="tpu_custom_call" | custom-call | flops 1000 | bytes 1000 | tf_op jit(solution)/shard_map/pallas_call | solution.py:569
  300.2 10.8 %shard_map.440 = (f32[128,768]{1,0:T(8,128)S(1)}, f32[8,768]{1,0:T(8,128)}, bf16[5,128,768]{2,1,0:T(8,128)(2,1)S(1)}) custom-call(bf16[128,768]{1,0:T(8,128)(2,1)S(1)} %bitcast.41, f32[16,768]{1,0:T(8,128)S(1)} %copy-done.6, bf16[768,768]{1,0:T(8,128)(2,1)S(1)} %fusion.order_ref, bf16[3,128,768]{2,1,0:T(8,128)(2,1)S(1)} %copy-done.20, ...), custom_call_target="tpu_custom_call" | custom-call | flops 1000 | bytes 1000 | tf_op jit(solution)/shard_map/pallas_call | solution.py:569
  316.7 8.7 %collective-permute-done.32.got_ref = bf16[192,6144]{1,0:T(8,128)(2,1)S(1)} collective-permute-done((bf16[192,6144]{1,0:T(8,128)(2,1)}, bf16[192,6144]{1,0:T(8,128)(2,1)S(1)}, u32[]{:S(2)}, u32[]{:S(2)}) %collective-permute-start.32) | collective-permute-done | bytes 2359328 | tf_op jit(solution)/shard_map/ppermute | solution.py:39
  326.5 8.2 %shard_map.443 = bf16[1152,768]{1,0:T(8,128)(2,1)} custom-call(bf16[1152,1536]{1,0:T(8,128)(2,1)S(1)} %get-tuple-element.477.dkv_ref, bf16[768,768]{1,0:T(8,128)(2,1)S(1)} %fusion.order_ref, bf16[384,6144]{1,0:T(8,128)(2,1)} %pad_maximum_fusion.1.top_ref, bf16[384,6144]{1,0:T(8,128)(2,1)} %collective-permute-done.17.low_ref), custom_call_target="tpu_custom_call" | custom-call | flops 1000 | bytes 1000 | tf_op jit(solution)/shard_map/pallas_call | solution.py:569
  342.5 20.6 %collective-permute-done.35.got_ref = bf16[96,6144]{1,0:T(8,128)(2,1)S(1)} collective-permute-done((bf16[96,6144]{1,0:T(8,128)(2,1)S(1)}, bf16[96,6144]{1,0:T(8,128)(2,1)S(1)}, u32[]{:S(2)}, u32[]{:S(2)}) %collective-permute-start.35) | collective-permute-done | bytes 1179680 | tf_op jit(solution)/shard_map/ppermute | solution.py:39
  383.7 17.9 %collective-permute-done.39.got_ref = bf16[96,6144]{1,0:T(8,128)(2,1)S(1)} collective-permute-done((bf16[96,6144]{1,0:T(8,128)(2,1)}, bf16[96,6144]{1,0:T(8,128)(2,1)S(1)}, u32[]{:S(2)}, u32[]{:S(2)}) %collective-permute-start.39) | collective-permute-done | bytes 1179680 | tf_op jit(solution)/shard_map/ppermute | solution.py:39
  407.4 8.2 %collective-permute-done.42 = bf16[48,6144]{1,0:T(8,128)(2,1)S(1)} collective-permute-done((bf16[48,6144]{1,0:T(8,128)(2,1)S(1)}, bf16[48,6144]{1,0:T(8,128)(2,1)S(1)}, u32[]{:S(2)}, u32[]{:S(2)}) %collective-permute-start.42) | collective-permute-done | bytes 589856 | tf_op jit(solution)/shard_map/ppermute | solution.py:35
  (254 shorter events, 192.5 us)
Async XLA Ops:
  19.6 16.8 %collective-permute-start.2 = (bf16[24,6144]{1,0:T(8,128)(2,1)}, bf16[24,6144]{1,0:T(8,128)(2,1)S(1)}, u32[]{:S(2)}, u32[]{:S(2)}) collective-permute-start(bf16[24,6144]{1,0:T(8,128)(2,1)} %get-tuple-element.306), channel_id=1, source_target_pairs={{0,16},{1,17},{2,18},{3,19},{4,20},{5,21},{6,22},{7,23},{8,24},{9,... | collective-permute-start | bytes 884744 | tf_op jit(solution)/shard_map/ppermute | solution.py:35
  49.1 16.8 %collective-permute-start.5 = (bf16[192,3200]{1,0:T(8,128)(2,1)S(1)}, bf16[192,3200]{1,0:T(8,128)(2,1)S(1)}, u32[]{:S(2)}, u32[]{:S(2)}) collective-permute-start(bf16[192,3200]{1,0:T(8,128)(2,1)S(1)} %pad_maximum_fusion.7), channel_id=1, source_target_pairs={{0,4},{1,5},{2,3},{3,2},{4,0},{5,1},{6,7},{7,6},{8,12},{9,13},{10,... | collective-permute-start | bytes 3686408 | tf_op jit(solution)/shard_map/ppermute | solution.py:39
  67.5 17.1 %collective-permute-start.8 = (bf16[384,3200]{1,0:T(8,128)(2,1)}, bf16[384,3200]{1,0:T(8,128)(2,1)}, u32[]{:S(2)}, u32[]{:S(2)}) collective-permute-start(bf16[384,3200]{1,0:T(8,128)(2,1)} %pad_maximum_fusion.3.top_ref), channel_id=1, source_target_pairs={{0,2},{1,3},{2,0},{3,1},{4,6},{5,7},{6,4},{7,5},{8,10},{9,11},{10,... | collective-permute-start | bytes 7372808 | tf_op jit(solution)/shard_map/ppermute | solution.py:35
  67.6 16.3 %collective-permute-start.7 = (bf16[96,6144]{1,0:T(8,128)(2,1)S(1)}, bf16[96,6144]{1,0:T(8,128)(2,1)S(1)}, u32[]{:S(2)}, u32[]{:S(2)}) collective-permute-start(bf16[96,6144]{1,0:T(8,128)(2,1)S(1)} %pad_maximum_fusion.10), channel_id=1, source_target_pairs={{0,1},{1,0},{2,6},{3,7},{4,5},{5,4},{6,2},{7,3},{8,9},{9,8},{10,14... | collective-permute-start | bytes 3538952 | tf_op jit(solution)/shard_map/ppermute | solution.py:39
  83.9 14.9 %collective-permute-start.9 = (bf16[48,6144]{1,0:T(8,128)(2,1)S(1)}, bf16[48,6144]{1,0:T(8,128)(2,1)S(1)}, u32[]{:S(2)}, u32[]{:S(2)}) collective-permute-start(bf16[48,6144]{1,0:T(8,128)(2,1)S(1)} %pad_maximum_fusion.15), channel_id=1, source_target_pairs={{0,8},{1,9},{2,10},{3,11},{4,12},{5,13},{6,14},{7,15},{8,0},{9,1},... | collective-permute-start | bytes 1769480 | tf_op jit(solution)/shard_map/ppermute | solution.py:35
  98.9 27.9 %collective-permute-start.11 = (bf16[96,6144]{1,0:T(8,128)(2,1)S(1)}, bf16[96,6144]{1,0:T(8,128)(2,1)S(1)}, u32[]{:S(2)}, u32[]{:S(2)}) collective-permute-start(bf16[96,6144]{1,0:T(8,128)(2,1)S(1)} %pad_maximum_fusion.11), channel_id=1, source_target_pairs={{0,1},{1,0},{2,6},{3,7},{4,5},{5,4},{6,2},{7,3},{8,9},{9,8},{10,14... | collective-permute-start | bytes 3538952 | tf_op jit(solution)/shard_map/ppermute | solution.py:39
  103.0 35.2 %collective-permute-start.13 = (bf16[192,6144]{1,0:T(8,128)(2,1)S(1)}, bf16[192,6144]{1,0:T(8,128)(2,1)S(1)}, u32[]{:S(2)}, u32[]{:S(2)}) collective-permute-start(bf16[192,6144]{1,0:T(8,128)(2,1)S(1)} %pad_maximum_fusion.4), channel_id=1, source_target_pairs={{0,4},{1,5},{2,3},{3,2},{4,0},{5,1},{6,7},{7,6},{8,12},{9,13},{10,... | collective-permute-start | bytes 7077896 | tf_op jit(solution)/shard_map/ppermute | solution.py:39
  114.7 15.3 %collective-permute-start.12 = (bf16[48,6144]{1,0:T(8,128)(2,1)S(1)}, bf16[48,6144]{1,0:T(8,128)(2,1)S(1)}, u32[]{:S(2)}, u32[]{:S(2)}) collective-permute-start(bf16[48,6144]{1,0:T(8,128)(2,1)S(1)} %pad_maximum_fusion.16), channel_id=1, source_target_pairs={{0,8},{1,9},{2,10},{3,11},{4,12},{5,13},{6,14},{7,15},{8,0},{9,1},... | collective-permute-start | bytes 1769480 | tf_op jit(solution)/shard_map/ppermute | solution.py:35
  140.6 41.5 %collective-permute-start.16 = (bf16[192,6144]{1,0:T(8,128)(2,1)S(1)}, bf16[192,6144]{1,0:T(8,128)(2,1)S(1)}, u32[]{:S(2)}, u32[]{:S(2)}) collective-permute-start(bf16[192,6144]{1,0:T(8,128)(2,1)S(1)} %pad_maximum_fusion.5), channel_id=1, source_target_pairs={{0,4},{1,5},{2,3},{3,2},{4,0},{5,1},{6,7},{7,6},{8,12},{9,13},{10,... | collective-permute-start | bytes 7077896 | tf_op jit(solution)/shard_map/ppermute | solution.py:39
  142.1 28.9 %collective-permute-start.15 = (bf16[96,6144]{1,0:T(8,128)(2,1)S(1)}, bf16[96,6144]{1,0:T(8,128)(2,1)S(1)}, u32[]{:S(2)}, u32[]{:S(2)}) collective-permute-start(bf16[96,6144]{1,0:T(8,128)(2,1)S(1)} %pad_maximum_fusion.12), channel_id=1, source_target_pairs={{0,1},{1,0},{2,6},{3,7},{4,5},{5,4},{6,2},{7,3},{8,9},{9,8},{10,14... | collective-permute-start | bytes 3538952 | tf_op jit(solution)/shard_map/ppermute | solution.py:39
  184.6 29.6 %collective-permute-start.18 = (bf16[192,6144]{1,0:T(8,128)(2,1)}, bf16[192,6144]{1,0:T(8,128)(2,1)}, u32[]{:S(2)}, u32[]{:S(2)}) collective-permute-start(bf16[192,6144]{1,0:T(8,128)(2,1)} %pad_maximum_fusion.6), channel_id=1, source_target_pairs={{0,4},{1,5},{2,3},{3,2},{4,0},{5,1},{6,7},{7,6},{8,12},{9,13},{10,... | collective-permute-start | bytes 7077896 | tf_op jit(solution)/shard_map/ppermute | solution.py:39
  246.9 29.1 %collective-permute-start.26 = (bf16[192,6144]{1,0:T(8,128)(2,1)}, bf16[192,6144]{1,0:T(8,128)(2,1)S(1)}, u32[]{:S(2)}, u32[]{:S(2)}) collective-permute-start(bf16[192,6144]{1,0:T(8,128)(2,1)} %get-tuple-element.423), channel_id=1, source_target_pairs={{0,4},{1,5},{2,3},{3,2},{4,0},{5,1},{6,7},{7,6},{8,12},{9,13},{10,... | collective-permute-start | bytes 7077896 | tf_op jit(solution)/shard_map/ppermute | solution.py:39
  284.3 41.2 %collective-permute-start.32 = (bf16[192,6144]{1,0:T(8,128)(2,1)}, bf16[192,6144]{1,0:T(8,128)(2,1)S(1)}, u32[]{:S(2)}, u32[]{:S(2)}) collective-permute-start(bf16[192,6144]{1,0:T(8,128)(2,1)} %get-tuple-element.470), channel_id=1, source_target_pairs={{0,4},{1,5},{2,3},{3,2},{4,0},{5,1},{6,7},{7,6},{8,12},{9,13},{10,... | collective-permute-start | bytes 7077896 | tf_op jit(solution)/shard_map/ppermute | solution.py:39
  285.8 28.9 %collective-permute-start.31 = (bf16[96,6144]{1,0:T(8,128)(2,1)S(1)}, bf16[96,6144]{1,0:T(8,128)(2,1)S(1)}, u32[]{:S(2)}, u32[]{:S(2)}) collective-permute-start(bf16[96,6144]{1,0:T(8,128)(2,1)S(1)} %get-tuple-element.462), channel_id=1, source_target_pairs={{0,1},{1,0},{2,6},{3,7},{4,5},{5,4},{6,2},{7,3},{8,9},{9,8},{10,14... | collective-permute-start | bytes 3538952 | tf_op jit(solution)/shard_map/ppermute | solution.py:39
  315.2 19.5 %collective-permute-start.33 = (bf16[48,6144]{1,0:T(8,128)(2,1)S(1)}, bf16[48,6144]{1,0:T(8,128)(2,1)S(1)}, u32[]{:S(2)}, u32[]{:S(2)}) collective-permute-start(bf16[48,6144]{1,0:T(8,128)(2,1)S(1)} %get-tuple-element.480), channel_id=1, source_target_pairs={{0,8},{1,9},{2,10},{3,11},{4,12},{5,13},{6,14},{7,15},{8,0},{9,1},... | collective-permute-start | bytes 1769480 | tf_op jit(solution)/shard_map/ppermute | solution.py:35
  316.1 19.8 %collective-permute-start.34 = (bf16[5,128,768]{2,1,0:T(8,128)(2,1)S(1)}, bf16[5,128,768]{2,1,0:T(8,128)(2,1)S(1)}, u32[]{:S(2)}, u32[]{:S(2)}) collective-permute-start(bf16[5,128,768]{2,1,0:T(8,128)(2,1)S(1)} %get-tuple-element.489.sd_ref), channel_id=1, source_target_pairs={{0,2},{1,3},{2,0},{3,1},{4,6},{5,7},{6,4},{7,5},{8,10},{9,11},{10,... | collective-permute-start | bytes 2949128 | tf_op jit(solution)/shard_map/ppermute | solution.py:35
  316.1 48.4 %collective-permute-start.36 = (bf16[192,6144]{1,0:T(8,128)(2,1)S(1)}, bf16[192,6144]{1,0:T(8,128)(2,1)S(1)}, u32[]{:S(2)}, u32[]{:S(2)}) collective-permute-start(bf16[192,6144]{1,0:T(8,128)(2,1)S(1)} %get-tuple-element.501), channel_id=1, source_target_pairs={{0,4},{1,5},{2,3},{3,2},{4,0},{5,1},{6,7},{7,6},{8,12},{9,13},{10,... | collective-permute-start | bytes 7077896 | tf_op jit(solution)/shard_map/ppermute | solution.py:39
  334.8 29.7 %collective-permute-start.37 = (bf16[24,6144]{1,0:T(8,128)(2,1)S(1)}, bf16[24,6144]{1,0:T(8,128)(2,1)S(1)}, u32[]{:S(2)}, u32[]{:S(2)}) collective-permute-start(bf16[24,6144]{1,0:T(8,128)(2,1)S(1)} %add_convert_fusion.5), channel_id=1, source_target_pairs={{0,16},{1,17},{2,18},{3,19},{4,20},{5,21},{6,22},{7,23},{8,24},{9,... | collective-permute-start | bytes 884744 | tf_op jit(solution)/shard_map/ppermute | solution.py:35
  335.9 27.1 %collective-permute-start.35 = (bf16[96,6144]{1,0:T(8,128)(2,1)S(1)}, bf16[96,6144]{1,0:T(8,128)(2,1)S(1)}, u32[]{:S(2)}, u32[]{:S(2)}) collective-permute-start(bf16[96,6144]{1,0:T(8,128)(2,1)S(1)} %get-tuple-element.494), channel_id=1, source_target_pairs={{0,1},{1,0},{2,6},{3,7},{4,5},{5,4},{6,2},{7,3},{8,9},{9,8},{10,14... | collective-permute-start | bytes 3538952 | tf_op jit(solution)/shard_map/ppermute | solution.py:39
  364.2 16.0 %collective-permute-start.38 = (bf16[48,6144]{1,0:T(8,128)(2,1)}, bf16[48,6144]{1,0:T(8,128)(2,1)}, u32[]{:S(2)}, u32[]{:S(2)}) collective-permute-start(bf16[48,6144]{1,0:T(8,128)(2,1)} %get-tuple-element.511), channel_id=1, source_target_pairs={{0,8},{1,9},{2,10},{3,11},{4,12},{5,13},{6,14},{7,15},{8,0},{9,1},... | collective-permute-start | bytes 1769480 | tf_op jit(solution)/shard_map/ppermute | solution.py:35
  372.5 29.1 %collective-permute-start.39 = (bf16[96,6144]{1,0:T(8,128)(2,1)}, bf16[96,6144]{1,0:T(8,128)(2,1)S(1)}, u32[]{:S(2)}, u32[]{:S(2)}) collective-permute-start(bf16[96,6144]{1,0:T(8,128)(2,1)} %copy-done.30), channel_id=1, source_target_pairs={{0,1},{1,0},{2,6},{3,7},{4,5},{5,4},{6,2},{7,3},{8,9},{9,8},{10,14... | collective-permute-start | bytes 3538952 | tf_op jit(solution)/shard_map/ppermute | solution.py:39
  373.4 32.1 %collective-permute-start.40 = (bf16[192,3200]{1,0:T(8,128)(2,1)}, bf16[192,3200]{1,0:T(8,128)(2,1)S(1)}, u32[]{:S(2)}, u32[]{:S(2)}) collective-permute-start(bf16[192,3200]{1,0:T(8,128)(2,1)} %pad_maximum_fusion.8), channel_id=1, source_target_pairs={{0,4},{1,5},{2,3},{3,2},{4,0},{5,1},{6,7},{7,6},{8,12},{9,13},{10,... | collective-permute-start | bytes 3686408 | tf_op jit(solution)/shard_map/ppermute | solution.py:39
  381.2 22.5 %collective-permute-start.41 = (bf16[24,6144]{1,0:T(8,128)(2,1)S(1)}, bf16[24,6144]{1,0:T(8,128)(2,1)S(1)}, u32[]{:S(2)}, u32[]{:S(2)}) collective-permute-start(bf16[24,6144]{1,0:T(8,128)(2,1)S(1)} %add_convert_fusion.3), channel_id=1, source_target_pairs={{0,16},{1,17},{2,18},{3,19},{4,20},{5,21},{6,22},{7,23},{8,24},{9,... | collective-permute-start | bytes 884744 | tf_op jit(solution)/shard_map/ppermute | solution.py:35
  406.6 16.3 %collective-permute-start.43 = (bf16[96,3200]{1,0:T(8,128)(2,1)}, bf16[96,3200]{1,0:T(8,128)(2,1)S(1)}, u32[]{:S(2)}, u32[]{:S(2)}) collective-permute-start(bf16[96,3200]{1,0:T(8,128)(2,1)} %get-tuple-element.539), channel_id=1, source_target_pairs={{0,1},{1,0},{2,6},{3,7},{4,5},{5,4},{6,2},{7,3},{8,9},{9,8},{10,14... | collective-permute-start | bytes 1843208 | tf_op jit(solution)/shard_map/ppermute | solution.py:39
  (67 other events, 857.1 us)

commit v12 on v11

--- a/solution.py
+++ b/solution.py
@@ -820,12 +820,12 @@
     vec = tn(jnp.concatenate([x[:, 4 * d :] for x in w_first], axis=0), order)[:16]
     net = Layers(captions, captions * length, d, vec, order, patch_count)
     x0 = go(x0, [middle], [last])
+    for k in range(steps - 1):
+        x0 = go(x0, [last])
+    x0 = go(x0, [feed])
     x0a, f_us, k_us = net.self_forward(x0, w_first, 0, 0)
-    for k in range(steps - 1):
-        x0a = go(x0a, [last])
     x0a = go(x0a, [middle])
     x0a = go(x0a, [last])
-    x0a = go(x0a, [feed])
     x0a, w_feed = end(x0a, feed)
     x1, f_uf, k_uf = net.feed_forward(x0a, w_feed, 2)
     x1 = go(x1, [last])
@@ -890,19 +890,20 @@
     p = pairs(p)
     dx = go_on(dx, [s_mf], [s_uf, s_mf])
     dx = go_on(dx, [s_ma], [s_ma])
+    dx, (p,) = tie(dx, p)
+    send, keep = net.attend_grads(f_us, p)
+    dx, (send, keep) = tie(dx, send, keep)
+    v = nt(order[: d // 2], plus(p[0][4], p[1][4])[:LANES]).astype(bf16)
     dx, (dkv,) = tie(dx, dkv)
     denc = net.pair_input(dkv, w_middle)
     dx, (denc,) = tie(dx, denc)
-    dx = rest(dx, s_mf)
-    dx, (p,) = tie(dx, p)
-    send, keep = net.attend_grads(f_us, p)
-    v = nt(order[: d // 2], plus(p[0][4], p[1][4])[:LANES]).astype(bf16)
+    dx = go_on(dx, [s_ma], [s_ma])
     send = jnp.concatenate((send, v[d // 4 :]), axis=1)
     keep = jnp.concatenate((keep, v[: d // 4]), axis=1)
     s_us = Sum(place, (send, keep))
-    dx = need(dx, s_us)
-    dx = go_on(dx, [s_ma], [s_ma])
-    dx = go_on(dx, [s_uf], [s_uf, s_us])
+    dx = go_on(dx, start=[s_us])
+    dx = rest(dx, s_mf)
+    dx = go_on(dx, [s_uf], [s_uf])
     dx, (r_mf,) = tie(dx, s_mf.total())
     dx = rest(dx, s_ma)
     dx = go_on(dx, [s_uf], [s_uf])

time: 450 us -> 452 us (level)
  waiting for transfers between devices: 221 us -> 212 us
  starting transfers between devices: 42.6 us -> 48.2 us
    ppermute x16, waiting for transfers between devices: 124 us -> 117 us  [swap_by_core(): return lax.ppermute(x, AXES, pairs)]
    ppermute x16, starting transfers between devices: 20.6 us -> 27.4 us  [swap_by_core(): return lax.ppermute(x, AXES, pairs)]
  transfers between devices with their start and end apart: 47 -> 47, of which waited for: 31 -> 29; matrix products, arithmetic and copies ran while one was open for 8% -> 8% of each run, Pallas kernels for 24% -> 24%
where the time goes in v12:
time: 452 us; the launch traced here: 446 us
  waiting for transfers between devices  212 us (47%)
  Pallas kernels  131 us (29%)
  starting transfers between devices  48.2 us (11%)
  other arithmetic  23.9 us (5%)
  local copies, waits for them, and re-layouts  23.6 us (5%)
  matrix products  5.78 us (1%)
    pallas_call x26, Pallas kernels, call(): pl.pallas_call(kernel, out_shape=outs, grid_spec=pltpu.PrefetchScalarGrid...  131 us
    ppermute x16, waiting for transfers between devices, swap_by_core(): return lax.ppermute(x, AXES, pairs)  117 us
    ppermute x31, waiting for transfers between devices, swap(): return lax.ppermute(x, AXES, [(i, i ^ bit) for i in range(self.count)])  95.4 us
    ppermute x16, starting transfers between devices, swap_by_core(): return lax.ppermute(x, AXES, pairs)  27.4 us
    ppermute x31, starting transfers between devices, swap(): return lax.ppermute(x, AXES, [(i, i ^ bit) for i in range(self.count)])  20.8 us
    concatenate x16, other arithmetic, join(): self.x = jnp.concatenate((self.x, self.got), axis=0)  13.6 us
  transfers between devices with their start and end apart: 47, of which 29 were waited for; matrix products, arithmetic and copies ran while one was open for 8% of the time, Pallas kernels for 24%

profile of v12, /device:TPU:0, one launch (start us, length us, event | category | flops | bytes accessed | tf_op | source)
XLA Modules:
  0.0 446.1 jit_solution(14971206883205327988)
XLA Ops:
  10.3 7.5 %collective-permute-done = bf16[24,3200]{1,0:T(8,128)(2,1)S(1)} collective-permute-done((bf16[24,3200]{1,0:T(8,128)(2,1)}, bf16[24,3200]{1,0:T(8,128)(2,1)S(1)}, u32[]{:S(2)}, u32[]{:S(2)}) %collective-permute-start) | collective-permute-done | bytes 153632 | tf_op jit(solution)/shard_map/ppermute | solution.py:35
  22.9 10.5 %collective-permute-done.1 = bf16[48,3200]{1,0:T(8,128)(2,1)S(1)} collective-permute-done((bf16[48,3200]{1,0:T(8,128)(2,1)S(1)}, bf16[48,3200]{1,0:T(8,128)(2,1)S(1)}, u32[]{:S(2)}, u32[]{:S(2)}) %collective-permute-start.1) | collective-permute-done | bytes 307232 | tf_op jit(solution)/shard_map/ppermute | solution.py:35
  39.4 9.6 %collective-permute-done.3 = bf16[96,3200]{1,0:T(8,128)(2,1)S(1)} collective-permute-done((bf16[96,3200]{1,0:T(8,128)(2,1)S(1)}, bf16[96,3200]{1,0:T(8,128)(2,1)S(1)}, u32[]{:S(2)}, u32[]{:S(2)}) %collective-permute-start.3) | collective-permute-done | bytes 614432 | tf_op jit(solution)/shard_map/ppermute | solution.py:39
  53.7 24.3 %collective-permute-done.5 = bf16[192,3200]{1,0:T(8,128)(2,1)S(1)} collective-permute-done((bf16[192,3200]{1,0:T(8,128)(2,1)S(1)}, bf16[192,3200]{1,0:T(8,128)(2,1)S(1)}, u32[]{:S(2)}, u32[]{:S(2)}) %collective-permute-start.5) | collective-permute-done | bytes 1228832 | tf_op jit(solution)/shard_map/ppermute | solution.py:39
  79.7 11.6 %collective-permute-done.6 = bf16[24,6144]{1,0:T(8,128)(2,1)S(1)} collective-permute-done((bf16[24,6144]{1,0:T(8,128)(2,1)S(1)}, bf16[24,6144]{1,0:T(8,128)(2,1)S(1)}, u32[]{:S(2)}, u32[]{:S(2)}) %collective-permute-start.6) | collective-permute-done | bytes 294944 | tf_op jit(solution)/shard_map/ppermute | solution.py:35
  98.8 9.5 %collective-permute-done.9 = bf16[48,6144]{1,0:T(8,128)(2,1)S(1)} collective-permute-done((bf16[48,6144]{1,0:T(8,128)(2,1)S(1)}, bf16[48,6144]{1,0:T(8,128)(2,1)S(1)}, u32[]{:S(2)}, u32[]{:S(2)}) %collective-permute-start.9) | collective-permute-done | bytes 589856 | tf_op jit(solution)/shard_map/ppermute | solution.py:35
  110.0 11.3 %collective-permute-done.10 = bf16[24,6144]{1,0:T(8,128)(2,1)S(1)} collective-permute-done((bf16[24,6144]{1,0:T(8,128)(2,1)S(1)}, bf16[24,6144]{1,0:T(8,128)(2,1)S(1)}, u32[]{:S(2)}, u32[]{:S(2)}) %collective-permute-start.10) | collective-permute-done | bytes 294944 | tf_op jit(solution)/shard_map/ppermute | solution.py:35
  127.1 6.6 %shard_map.425 = (f32[128,768]{1,0:T(8,128)S(1)}, bf16[2,128,768]{2,1,0:T(8,128)(2,1)S(1)}, bf16[3,128,768]{2,1,0:T(8,128)(2,1)S(1)}) custom-call(bf16[128,768]{1,0:T(8,128)(2,1)S(1)} %bitcast.40, f32[16,768]{1,0:T(8,128)S(1)} %fusion.11.vec_ref, bf16[768,768]{1,0:T(8,128)(2,1)S(1)} %fusion.order_ref, bf16[384,3200]{1,0:T(8,128)(2,1)} %pad_maximum_fusion.3.top_ref, ...), custom_call_target="tpu_custom_call" | custom-call | flops 1000 | bytes 1000 | tf_op jit(solution)/shard_map/pallas_call | solution.py:569
  147.5 6.4 %shard_map.426 = (f32[128,768]{1,0:T(8,128)S(1)}, bf16[5,128,768]{2,1,0:T(8,128)(2,1)S(1)}, f32[128,3072]{1,0:T(8,128)S(1)}) custom-call(f32[128,768]{1,0:T(8,128)S(1)} %get-tuple-element.371.x_ref, f32[16,768]{1,0:T(8,128)S(1)} %fusion.11.vec_ref, bf16[768,768]{1,0:T(8,128)(2,1)S(1)} %fusion.order_ref, ...), custom_call_target="tpu_custom_call" | custom-call | flops 1000 | bytes 1000 | tf_op jit(solution)/shard_map/pallas_call | solution.py:569
  154.8 19.5 %collective-permute-done.15 = bf16[96,6144]{1,0:T(8,128)(2,1)S(1)} collective-permute-done((bf16[96,6144]{1,0:T(8,128)(2,1)S(1)}, bf16[96,6144]{1,0:T(8,128)(2,1)S(1)}, u32[]{:S(2)}, u32[]{:S(2)}) %collective-permute-start.15) | collective-permute-done | bytes 1179680 | tf_op jit(solution)/shard_map/ppermute | solution.py:39
  176.0 8.7 %collective-permute-done.16 = bf16[192,6144]{1,0:T(8,128)(2,1)S(1)} collective-permute-done((bf16[192,6144]{1,0:T(8,128)(2,1)S(1)}, bf16[192,6144]{1,0:T(8,128)(2,1)S(1)}, u32[]{:S(2)}, u32[]{:S(2)}) %collective-permute-start.16) | collective-permute-done | bytes 2359328 | tf_op jit(solution)/shard_map/ppermute | solution.py:39
  207.5 9.2 %shard_map.429 = (f32[128,768]{1,0:T(8,128)S(1)}, bf16[2,128,768]{2,1,0:T(8,128)(2,1)S(1)}, bf16[128,768]{1,0:T(8,128)(2,1)S(1)}) custom-call(s32[2]{0:T(128)S(1)} %copy-done.40, f32[128,768]{1,0:T(8,128)S(1)} %get-tuple-element.389.x_ref, f32[16,768]{1,0:T(8,128)S(1)} %fusion.11.vec_ref, bf16[768,768]{1,0:T(8,128)(2,1)S(1)} %fusion.order_ref, ...), custom_call_target="tpu_custom_call" | custom-call | flops 1000 | bytes 1000 | tf_op jit(solution)/shard_map/pallas_call | solution.py:569
  221.0 6.9 %collective-permute-done.19.up2_ref.down2_ref = bf16[384,6144]{1,0:T(8,128)(2,1)S(1)} collective-permute-done((bf16[384,6144]{1,0:T(8,128)(2,1)S(1)}, bf16[384,6144]{1,0:T(8,128)(2,1)S(1)}, u32[]{:S(2)}, u32[]{:S(2)}) %collective-permute-start.19) | collective-permute-done | bytes 4718624 | tf_op jit(solution)/shard_map/ppermute | solution.py:35
  230.6 7.7 %shard_map.430 = (f32[128,768]{1,0:T(8,128)S(1)}, f32[8,768]{1,0:T(8,128)S(1)}, bf16[5,128,768]{2,1,0:T(8,128)(2,1)S(1)}, bf16[5,128,768]{2,1,0:T(8,128)(2,1)S(1)}) custom-call(f32[128,768]{1,0:T(8,128)S(1)} %get-tuple-element.402.x_ref, f32[16,768]{1,0:T(8,128)S(1)} %fusion.11.vec_ref, bf16[768,768]{1,0:T(8,128)(2,1)S(1)} %fusion.order_ref, ...), custom_call_target="tpu_custom_call" | custom-call | flops 1000 | bytes 1000 | tf_op jit(solution)/shard_map/pallas_call | solution.py:569
  252.5 11.1 %shard_map.433 = (f32[128,768]{1,0:T(8,128)S(1)}, f32[8,768]{1,0:T(8,128)S(1)}, bf16[2,128,768]{2,1,0:T(8,128)(2,1)S(1)}, bf16[1152,1536]{1,0:T(8,128)(2,1)S(1)}) custom-call(s32[2]{0:T(128)S(1)} %copy-done.40, f32[128,768]{1,0:T(8,128)S(1)} %copy-done.12, f32[16,768]{1,0:T(8,128)S(1)} %fusion.11.vec_ref, bf16[768,768]{1,0:T(8,128)(2,1)S(1)} %fusion.order_ref, ...), custom_call_target="tpu_custom_call" | custom-call | flops 1000 | bytes 1000 | tf_op jit(solution)/shard_map/pallas_call | solution.py:569
  267.8 10.3 %shard_map.435 = (f32[128,768]{1,0:T(8,128)S(1)}, f32[8,768]{1,0:T(8,128)S(1)}, bf16[4,128,768]{2,1,0:T(8,128)(2,1)S(1)}) custom-call(f32[128,768]{1,0:T(8,128)S(1)} %get-tuple-element.386.x_ref, f32[16,768]{1,0:T(8,128)S(1)} %fusion.11.vec_ref, bf16[768,768]{1,0:T(8,128)(2,1)S(1)} %fusion.order_ref, bf16[3,128,768]{2,1,0:T(8,128)(2,1)S(1)} %copy-done.20, ...), custom_call_target="tpu_custom_call" | custom-call | flops 1000 | bytes 1000 | tf_op jit(solution)/shard_map/pallas_call | solution.py:569
  289.1 6.5 %shard_map.438 = (f32[128,768]{1,0:T(8,128)S(1)}, f32[8,768]{1,0:T(8,128)S(1)}, bf16[5,128,768]{2,1,0:T(8,128)(2,1)S(1)}) custom-call(f32[128,768]{1,0:T(8,128)S(1)} %copy-done.10, f32[16,768]{1,0:T(8,128)S(1)} %fusion.11.vec_ref, bf16[768,768]{1,0:T(8,128)(2,1)S(1)} %fusion.order_ref, f32[128,768]{1,0:T(8,128)S(1)} %get-tuple-element.447.dx_ref, ...), custom_call_target="tpu_custom_call" | custom-call | flops 1000 | bytes 1000 | tf_op jit(solution)/shard_map/pallas_call | solution.py:569
  302.7 11.0 %shard_map.440 = (f32[128,768]{1,0:T(8,128)S(1)}, f32[8,768]{1,0:T(8,128)}, bf16[5,128,768]{2,1,0:T(8,128)(2,1)S(1)}) custom-call(bf16[128,768]{1,0:T(8,128)(2,1)S(1)} %bitcast.41, f32[16,768]{1,0:T(8,128)S(1)} %fusion.11.vec_ref, bf16[768,768]{1,0:T(8,128)(2,1)S(1)} %fusion.order_ref, bf16[3,128,768]{2,1,0:T(8,128)(2,1)S(1)} %copy-done.18, ...), custom_call_target="tpu_custom_call" | custom-call | flops 1000 | bytes 1000 | tf_op jit(solution)/shard_map/pallas_call | solution.py:569
  313.8 10.8 %collective-permute-done.31.got_ref = bf16[96,6144]{1,0:T(8,128)(2,1)S(1)} collective-permute-done((bf16[96,6144]{1,0:T(8,128)(2,1)S(1)}, bf16[96,6144]{1,0:T(8,128)(2,1)S(1)}, u32[]{:S(2)}, u32[]{:S(2)}) %collective-permute-start.31) | collective-permute-done | bytes 1179680 | tf_op jit(solution)/shard_map/ppermute | solution.py:39
  337.3 8.2 %shard_map.444 = bf16[1152,768]{1,0:T(8,128)(2,1)} custom-call(bf16[1152,1536]{1,0:T(8,128)(2,1)S(1)} %get-tuple-element.488.dkv_ref, bf16[768,768]{1,0:T(8,128)(2,1)S(1)} %fusion.order_ref, bf16[384,6144]{1,0:T(8,128)(2,1)} %pad_maximum_fusion.1.top_ref, bf16[384,6144]{1,0:T(8,128)(2,1)} %collective-permute-done.17.low_ref), custom_call_target="tpu_custom_call" | custom-call | flops 1000 | bytes 1000 | tf_op jit(solution)/shard_map/pallas_call | solution.py:569
  346.6 12.1 %collective-permute-done.34.got_ref = bf16[96,6144]{1,0:T(8,128)(2,1)S(1)} collective-permute-done((bf16[96,6144]{1,0:T(8,128)(2,1)S(1)}, bf16[96,6144]{1,0:T(8,128)(2,1)S(1)}, u32[]{:S(2)}, u32[]{:S(2)}) %collective-permute-start.34) | collective-permute-done | bytes 1179680 | tf_op jit(solution)/shard_map/ppermute | solution.py:39
  381.9 15.2 %collective-permute-done.39.got_ref = bf16[96,6144]{1,0:T(8,128)(2,1)} collective-permute-done((bf16[96,6144]{1,0:T(8,128)(2,1)}, bf16[96,6144]{1,0:T(8,128)(2,1)}, u32[]{:S(2)}, u32[]{:S(2)}) %collective-permute-start.39) | collective-permute-done | bytes 1179680 | tf_op jit(solution)/shard_map/ppermute | solution.py:39
  404.6 8.5 %collective-permute-done.42 = bf16[48,6144]{1,0:T(8,128)(2,1)S(1)} collective-permute-done((bf16[48,6144]{1,0:T(8,128)(2,1)S(1)}, bf16[48,6144]{1,0:T(8,128)(2,1)S(1)}, u32[]{:S(2)}, u32[]{:S(2)}) %collective-permute-start.42) | collective-permute-done | bytes 589856 | tf_op jit(solution)/shard_map/ppermute | solution.py:35
  437.3 6.1 %collective-permute-done.46 = bf16[24,3200]{1,0:T(8,128)(2,1)S(1)} collective-permute-done((bf16[24,3200]{1,0:T(8,128)(2,1)S(1)}, bf16[24,3200]{1,0:T(8,128)(2,1)S(1)}, u32[]{:S(2)}, u32[]{:S(2)}) %collective-permute-start.46) | collective-permute-done | bytes 153632 | tf_op jit(solution)/shard_map/ppermute | solution.py:35
  (274 shorter events, 194.9 us)
Async XLA Ops:
  18.8 14.7 %collective-permute-start.1 = (bf16[48,3200]{1,0:T(8,128)(2,1)S(1)}, bf16[48,3200]{1,0:T(8,128)(2,1)S(1)}, u32[]{:S(2)}, u32[]{:S(2)}) collective-permute-start(bf16[48,3200]{1,0:T(8,128)(2,1)S(1)} %pad_maximum_fusion.17), channel_id=1, source_target_pairs={{0,8},{1,9},{2,10},{3,11},{4,12},{5,13},{6,14},{7,15},{8,0},{9,1},... | collective-permute-start | bytes 921608 | tf_op jit(solution)/shard_map/ppermute | solution.py:35
  19.6 16.8 %collective-permute-start.2 = (bf16[24,6144]{1,0:T(8,128)(2,1)}, bf16[24,6144]{1,0:T(8,128)(2,1)S(1)}, u32[]{:S(2)}, u32[]{:S(2)}) collective-permute-start(bf16[24,6144]{1,0:T(8,128)(2,1)} %get-tuple-element.308), channel_id=1, source_target_pairs={{0,16},{1,17},{2,18},{3,19},{4,20},{5,21},{6,22},{7,23},{8,24},{9,... | collective-permute-start | bytes 884744 | tf_op jit(solution)/shard_map/ppermute | solution.py:35
  49.1 28.9 %collective-permute-start.5 = (bf16[192,3200]{1,0:T(8,128)(2,1)S(1)}, bf16[192,3200]{1,0:T(8,128)(2,1)S(1)}, u32[]{:S(2)}, u32[]{:S(2)}) collective-permute-start(bf16[192,3200]{1,0:T(8,128)(2,1)S(1)} %pad_maximum_fusion.7), channel_id=1, source_target_pairs={{0,4},{1,5},{2,3},{3,2},{4,0},{5,1},{6,7},{7,6},{8,12},{9,13},{10,... | collective-permute-start | bytes 3686408 | tf_op jit(solution)/shard_map/ppermute | solution.py:39
  52.1 39.2 %collective-permute-start.7 = (bf16[96,6144]{1,0:T(8,128)(2,1)S(1)}, bf16[96,6144]{1,0:T(8,128)(2,1)}, u32[]{:S(2)}, u32[]{:S(2)}) collective-permute-start(bf16[96,6144]{1,0:T(8,128)(2,1)S(1)} %pad_maximum_fusion.10), channel_id=1, source_target_pairs={{0,1},{1,0},{2,6},{3,7},{4,5},{5,4},{6,2},{7,3},{8,9},{9,8},{10,14... | collective-permute-start | bytes 3538952 | tf_op jit(solution)/shard_map/ppermute | solution.py:39
  79.6 19.1 %collective-permute-start.8 = (bf16[384,3200]{1,0:T(8,128)(2,1)}, bf16[384,3200]{1,0:T(8,128)(2,1)}, u32[]{:S(2)}, u32[]{:S(2)}) collective-permute-start(bf16[384,3200]{1,0:T(8,128)(2,1)} %pad_maximum_fusion.3.top_ref), channel_id=1, source_target_pairs={{0,2},{1,3},{2,0},{3,1},{4,6},{5,7},{6,4},{7,5},{8,10},{9,11},{10,... | collective-permute-start | bytes 7372808 | tf_op jit(solution)/shard_map/ppermute | solution.py:35
  92.8 29.4 %collective-permute-start.11 = (bf16[192,6144]{1,0:T(8,128)(2,1)S(1)}, bf16[192,6144]{1,0:T(8,128)(2,1)S(1)}, u32[]{:S(2)}, u32[]{:S(2)}) collective-permute-start(bf16[192,6144]{1,0:T(8,128)(2,1)S(1)} %pad_maximum_fusion.4), channel_id=1, source_target_pairs={{0,4},{1,5},{2,3},{3,2},{4,0},{5,1},{6,7},{7,6},{8,12},{9,13},{10,... | collective-permute-start | bytes 7077896 | tf_op jit(solution)/shard_map/ppermute | solution.py:39
  122.7 24.7 %collective-permute-start.14 = (bf16[384,6144]{1,0:T(8,128)(2,1)S(1)}, bf16[384,6144]{1,0:T(8,128)(2,1)S(1)}, u32[]{:S(2)}, u32[]{:S(2)}) collective-permute-start(bf16[384,6144]{1,0:T(8,128)(2,1)S(1)} %pad_maximum_fusion.up_ref.down_ref), channel_id=1, source_target_pairs={{0,2},{1,3},{2,0},{3,1},{4,6},{5,7},{6,4},{7,5},{8,10},{9,11},{10,... | collective-permute-start | bytes 14155784 | tf_op jit(solution)/shard_map/ppermute | solution.py:35
  122.8 16.4 %collective-permute-start.12 = (bf16[96,6144]{1,0:T(8,128)(2,1)S(1)}, bf16[96,6144]{1,0:T(8,128)(2,1)S(1)}, u32[]{:S(2)}, u32[]{:S(2)}) collective-permute-start(bf16[96,6144]{1,0:T(8,128)(2,1)S(1)} %pad_maximum_fusion.11), channel_id=1, source_target_pairs={{0,1},{1,0},{2,6},{3,7},{4,5},{5,4},{6,2},{7,3},{8,9},{9,8},{10,14... | collective-permute-start | bytes 3538952 | tf_op jit(solution)/shard_map/ppermute | solution.py:39
  127.1 14.6 %collective-permute-start.13 = (bf16[48,6144]{1,0:T(8,128)(2,1)S(1)}, bf16[48,6144]{1,0:T(8,128)(2,1)S(1)}, u32[]{:S(2)}, u32[]{:S(2)}) collective-permute-start(bf16[48,6144]{1,0:T(8,128)(2,1)S(1)} %pad_maximum_fusion.16), channel_id=1, source_target_pairs={{0,8},{1,9},{2,10},{3,11},{4,12},{5,13},{6,14},{7,15},{8,0},{9,1},... | collective-permute-start | bytes 1769480 | tf_op jit(solution)/shard_map/ppermute | solution.py:35
  141.8 43.0 %collective-permute-start.16 = (bf16[192,6144]{1,0:T(8,128)(2,1)S(1)}, bf16[192,6144]{1,0:T(8,128)(2,1)S(1)}, u32[]{:S(2)}, u32[]{:S(2)}) collective-permute-start(bf16[192,6144]{1,0:T(8,128)(2,1)S(1)} %pad_maximum_fusion.5), channel_id=1, source_target_pairs={{0,4},{1,5},{2,3},{3,2},{4,0},{5,1},{6,7},{7,6},{8,12},{9,13},{10,... | collective-permute-start | bytes 7077896 | tf_op jit(solution)/shard_map/ppermute | solution.py:39
  145.4 29.0 %collective-permute-start.15 = (bf16[96,6144]{1,0:T(8,128)(2,1)S(1)}, bf16[96,6144]{1,0:T(8,128)(2,1)S(1)}, u32[]{:S(2)}, u32[]{:S(2)}) collective-permute-start(bf16[96,6144]{1,0:T(8,128)(2,1)S(1)} %pad_maximum_fusion.12), channel_id=1, source_target_pairs={{0,1},{1,0},{2,6},{3,7},{4,5},{5,4},{6,2},{7,3},{8,9},{9,8},{10,14... | collective-permute-start | bytes 3538952 | tf_op jit(solution)/shard_map/ppermute | solution.py:39
  187.5 29.3 %collective-permute-start.18 = (bf16[192,6144]{1,0:T(8,128)(2,1)}, bf16[192,6144]{1,0:T(8,128)(2,1)}, u32[]{:S(2)}, u32[]{:S(2)}) collective-permute-start(bf16[192,6144]{1,0:T(8,128)(2,1)} %pad_maximum_fusion.6), channel_id=1, source_target_pairs={{0,4},{1,5},{2,3},{3,2},{4,0},{5,1},{6,7},{7,6},{8,12},{9,13},{10,... | collective-permute-start | bytes 7077896 | tf_op jit(solution)/shard_map/ppermute | solution.py:39
  250.5 29.1 %collective-permute-start.26 = (bf16[192,6144]{1,0:T(8,128)(2,1)}, bf16[192,6144]{1,0:T(8,128)(2,1)S(1)}, u32[]{:S(2)}, u32[]{:S(2)}) collective-permute-start(bf16[192,6144]{1,0:T(8,128)(2,1)} %get-tuple-element.425), channel_id=1, source_target_pairs={{0,4},{1,5},{2,3},{3,2},{4,0},{5,1},{6,7},{7,6},{8,12},{9,13},{10,... | collective-permute-start | bytes 7077896 | tf_op jit(solution)/shard_map/ppermute | solution.py:39
  287.2 41.5 %collective-permute-start.32 = (bf16[192,6144]{1,0:T(8,128)(2,1)S(1)}, bf16[192,6144]{1,0:T(8,128)(2,1)S(1)}, u32[]{:S(2)}, u32[]{:S(2)}) collective-permute-start(bf16[192,6144]{1,0:T(8,128)(2,1)S(1)} %get-tuple-element.472), channel_id=1, source_target_pairs={{0,4},{1,5},{2,3},{3,2},{4,0},{5,1},{6,7},{7,6},{8,12},{9,13},{10,... | collective-permute-start | bytes 7077896 | tf_op jit(solution)/shard_map/ppermute | solution.py:39
  295.7 29.0 %collective-permute-start.31 = (bf16[96,6144]{1,0:T(8,128)(2,1)S(1)}, bf16[96,6144]{1,0:T(8,128)(2,1)S(1)}, u32[]{:S(2)}, u32[]{:S(2)}) collective-permute-start(bf16[96,6144]{1,0:T(8,128)(2,1)S(1)} %get-tuple-element.464), channel_id=1, source_target_pairs={{0,1},{1,0},{2,6},{3,7},{4,5},{5,4},{6,2},{7,3},{8,9},{9,8},{10,14... | collective-permute-start | bytes 3538952 | tf_op jit(solution)/shard_map/ppermute | solution.py:39
  313.7 19.7 %collective-permute-start.33 = (bf16[5,128,768]{2,1,0:T(8,128)(2,1)S(1)}, bf16[5,128,768]{2,1,0:T(8,128)(2,1)S(1)}, u32[]{:S(2)}, u32[]{:S(2)}) collective-permute-start(bf16[5,128,768]{2,1,0:T(8,128)(2,1)S(1)} %get-tuple-element.482.sd_ref), channel_id=1, source_target_pairs={{0,2},{1,3},{2,0},{3,1},{4,6},{5,7},{6,4},{7,5},{8,10},{9,11},{10,... | collective-permute-start | bytes 2949128 | tf_op jit(solution)/shard_map/ppermute | solution.py:35
  329.8 28.9 %collective-permute-start.34 = (bf16[96,6144]{1,0:T(8,128)(2,1)S(1)}, bf16[96,6144]{1,0:T(8,128)(2,1)S(1)}, u32[]{:S(2)}, u32[]{:S(2)}) collective-permute-start(bf16[96,6144]{1,0:T(8,128)(2,1)S(1)} %get-tuple-element.491), channel_id=1, source_target_pairs={{0,1},{1,0},{2,6},{3,7},{4,5},{5,4},{6,2},{7,3},{8,9},{9,8},{10,14... | collective-permute-start | bytes 3538952 | tf_op jit(solution)/shard_map/ppermute | solution.py:39
  331.1 28.8 %collective-permute-start.35 = (bf16[48,6144]{1,0:T(8,128)(2,1)S(1)}, bf16[48,6144]{1,0:T(8,128)(2,1)S(1)}, u32[]{:S(2)}, u32[]{:S(2)}) collective-permute-start(bf16[48,6144]{1,0:T(8,128)(2,1)S(1)} %get-tuple-element.500), channel_id=1, source_target_pairs={{0,8},{1,9},{2,10},{3,11},{4,12},{5,13},{6,14},{7,15},{8,0},{9,1},... | collective-permute-start | bytes 1769480 | tf_op jit(solution)/shard_map/ppermute | solution.py:35
  331.7 38.3 %collective-permute-start.36 = (bf16[192,6144]{1,0:T(8,128)(2,1)S(1)}, bf16[192,6144]{1,0:T(8,128)(2,1)S(1)}, u32[]{:S(2)}, u32[]{:S(2)}) collective-permute-start(bf16[192,6144]{1,0:T(8,128)(2,1)S(1)} %get-tuple-element.506), channel_id=1, source_target_pairs={{0,4},{1,5},{2,3},{3,2},{4,0},{5,1},{6,7},{7,6},{8,12},{9,13},{10,... | collective-permute-start | bytes 7077896 | tf_op jit(solution)/shard_map/ppermute | solution.py:39
  360.2 17.7 %collective-permute-start.38 = (bf16[48,6144]{1,0:T(8,128)(2,1)}, bf16[48,6144]{1,0:T(8,128)(2,1)}, u32[]{:S(2)}, u32[]{:S(2)}) collective-permute-start(bf16[48,6144]{1,0:T(8,128)(2,1)} %get-tuple-element.515), channel_id=1, source_target_pairs={{0,8},{1,9},{2,10},{3,11},{4,12},{5,13},{6,14},{7,15},{8,0},{9,1},... | collective-permute-start | bytes 1769480 | tf_op jit(solution)/shard_map/ppermute | solution.py:35
  362.7 38.7 %collective-permute-start.40 = (bf16[192,3200]{1,0:T(8,128)(2,1)}, bf16[192,3200]{1,0:T(8,128)(2,1)}, u32[]{:S(2)}, u32[]{:S(2)}) collective-permute-start(bf16[192,3200]{1,0:T(8,128)(2,1)} %pad_maximum_fusion.8), channel_id=1, source_target_pairs={{0,4},{1,5},{2,3},{3,2},{4,0},{5,1},{6,7},{7,6},{8,12},{9,13},{10,... | collective-permute-start | bytes 3686408 | tf_op jit(solution)/shard_map/ppermute | solution.py:39
  372.7 24.3 %collective-permute-start.39 = (bf16[96,6144]{1,0:T(8,128)(2,1)}, bf16[96,6144]{1,0:T(8,128)(2,1)}, u32[]{:S(2)}, u32[]{:S(2)}) collective-permute-start(bf16[96,6144]{1,0:T(8,128)(2,1)} %get-tuple-element.521), channel_id=1, source_target_pairs={{0,1},{1,0},{2,6},{3,7},{4,5},{5,4},{6,2},{7,3},{8,9},{9,8},{10,14... | collective-permute-start | bytes 3538952 | tf_op jit(solution)/shard_map/ppermute | solution.py:39
  379.0 20.5 %collective-permute-start.41 = (bf16[24,6144]{1,0:T(8,128)(2,1)S(1)}, bf16[24,6144]{1,0:T(8,128)(2,1)S(1)}, u32[]{:S(2)}, u32[]{:S(2)}) collective-permute-start(bf16[24,6144]{1,0:T(8,128)(2,1)S(1)} %add_convert_fusion.3), channel_id=1, source_target_pairs={{0,16},{1,17},{2,18},{3,19},{4,20},{5,21},{6,22},{7,23},{8,24},{9,... | collective-permute-start | bytes 884744 | tf_op jit(solution)/shard_map/ppermute | solution.py:35
  403.6 16.8 %collective-permute-start.43 = (bf16[96,3200]{1,0:T(8,128)(2,1)}, bf16[96,3200]{1,0:T(8,128)(2,1)S(1)}, u32[]{:S(2)}, u32[]{:S(2)}) collective-permute-start(bf16[96,3200]{1,0:T(8,128)(2,1)} %get-tuple-element.543), channel_id=1, source_target_pairs={{0,1},{1,0},{2,6},{3,7},{4,5},{5,4},{6,2},{7,3},{8,9},{9,8},{10,14... | collective-permute-start | bytes 1843208 | tf_op jit(solution)/shard_map/ppermute | solution.py:39
  (77 other events, 825.4 us)

commit v13 on v12

--- a/solution.py
+++ b/solution.py
@@ -516,6 +516,37 @@
     return call(half_sums_kernel, steps, (kept, got), [full] * 2, outs, [half] * 2, vmem=24)
 
 
+def feed_rows_kernel(kept_ref, got_ref, up_ref, down_ref):
+    rows, wide = up_ref.shape
+    d = wide // 4
+    spread = spread_matrix().astype(bf16)
+    i = lax.broadcasted_iota(jnp.int32, (4 * rows, rows), 0)
+    k = lax.broadcasted_iota(jnp.int32, (4 * rows, rows), 1)
+
+    def part(at, size):
+        x = kept_ref[:, at : at + size].astype(f32) + got_ref[:, at : at + size].astype(f32)
+        high = x.astype(bf16)
+        return high, (x - high.astype(f32)).astype(bf16)
+
+    for b in range(wide // 512):
+        parts = [part(2 * j * d + b * LANES, LANES) for j in range(4)]
+        high, low = (jnp.concatenate(p, axis=1) for p in zip(*parts))
+        up_ref[:, b * 512 : (b + 1) * 512] = nt(high, spread) + nt(low, spread)
+    down = jnp.zeros(down_ref.shape, f32)
+    for j in range(4):
+        place = (i == 4 * k + j).astype(bf16)
+        high, low = part((2 * j + 1) * d, d)
+        down = down + nn(place, high) + nn(place, low)
+    down_ref[...] = down
+
+
+def feed_rows(kept, got):
+    rows, wide = kept.shape
+    outs = sds((rows, wide // 2), f32), sds((4 * rows, wide // 8), f32)
+    ins = kept, got
+    return call(feed_rows_kernel, 1, ins, [whole(x) for x in ins], outs, [whole(x) for x in outs])
+
+
 def pair_forward_kernel(enc_ref, top_ref, low_ref, kv_ref):
     kv_ref[...] = times(enc_ref[...], top_ref, low_ref).astype(bf16)
 
@@ -753,16 +784,6 @@
     return (k % 4) * 128 + k // 4 == n
 
 
-def unspread(up):
-    rows, wide = up.shape
-    y = up.reshape(rows, 4, wide // 512, 128).transpose(0, 2, 1, 3)
-    y = lax.dot_general(
-        y.reshape(rows * (wide // 512), 512), spread_matrix().astype(f32),
-        (((1,), (1,)), ((), ())), precision=lax.Precision.HIGHEST,
-    )
-    return y.reshape(rows, wide)
-
-
 def local(
     tokens, encoder, patch_count, out_grad,
     u_ag, u_as, u_qkv, u_out, u_mg, u_ms, u_up, u_down,
@@ -811,10 +832,10 @@
         x0 = go(x0, [feed])
     x0 = go(x0, [first])
     x0 = go(x0, [feed], [middle])
-    x0 = go(x0, [first])
-    for k in range(steps - 1):
+    x0 = go(x0, [first, middle])
+    x0 = go(x0, [feed])
+    for k in range(steps - 2):
         x0 = go(x0, [middle])
-    x0 = go(x0, [feed])
     x0, (order, enc_rel, enc_t) = tie(x0, order, enc_rel, enc_t)
     x0, w_first = end(x0, first)
     vec = tn(jnp.concatenate([x[:, 4 * d :] for x in w_first], axis=0), order)[:16]
@@ -904,14 +925,13 @@
     dx = go_on(dx, start=[s_us])
     dx = rest(dx, s_mf)
     dx = go_on(dx, [s_uf], [s_uf])
-    dx, (r_mf,) = tie(dx, s_mf.total())
+    dx, (r_mf,) = tie(dx, feed_rows(s_mf.kept, s_mf.got))
     dx = rest(dx, s_ma)
-    dx = go_on(dx, [s_uf], [s_uf])
-    dx = go_on(dx, [s_us], [s_us])
+    dx = go_on(dx, [s_uf, s_us], [s_uf, s_us])
     dx, (r_ma,) = tie(dx, s_ma.total())
     dx = rest(dx, s_uf)
     dx = go_on(dx, [s_us], [s_us])
-    dx, (r_uf,) = tie(dx, s_uf.total())
+    dx, (r_uf,) = tie(dx, feed_rows(s_uf.kept, s_uf.got))
     dx = rest(dx, s_us)
     r_us = s_us.total()
 
@@ -919,11 +939,8 @@
         parts = [r[:, b * d : (b + 1) * d] for b in blocks]
         return jnp.concatenate(parts, axis=1) if len(parts) > 1 else parts[0]
 
-    def feed_rows(r):
-        return unspread(columns(r, 0, 2, 4, 6)), columns(r, 1, 3, 5, 7).reshape(-1, d)
-
-    r_uup, r_udown = feed_rows(r_uf)
-    r_mup, r_mdown = feed_rows(r_mf)
+    r_uup, r_udown = r_uf
+    r_mup, r_mdown = r_mf
     vs = r_us[:, 4 * d :]
     v = [vs[:, i] for i in range(10)]
     return (

time: 452 us -> 430 us (0.951)
  local copies, waits for them, and re-layouts: 23.6 us -> 13.8 us
  other arithmetic: 23.9 us -> 15.3 us
    ppermute x16, waiting for transfers between devices: 117 us -> 110 us  [swap_by_core(): return lax.ppermute(x, AXES, pairs)]
    ppermute x31, waiting for transfers between devices: 95.4 us -> 102 us  [swap(): return lax.ppermute(x, AXES, [(i, i ^ bit) for i in range(self.count)])]
    reshape x6 -> x0, local copies, waits for them, and re-layouts: 6.27 us -> none  [the longest x2 2.56 us: feed_rows(): columns(r, 1, 3, 5, 7).reshape(-1, d)]
    pallas_call x26 -> x28, Pallas kernels: 131 us -> 132 us  [call(): pl.pallas_call(kernel, out_shape=outs, grid_spec=pltpu.PrefetchScalarGrid...]
  transfers between devices with their start and end apart: 47 -> 47, of which waited for: 29 -> 27; matrix products, arithmetic and copies ran while one was open for 8% -> 4% of each run, Pallas kernels for 24% -> 26%
where the time goes in v13:
time: 430 us; the launch traced here: 425 us
  waiting for transfers between devices  212 us (49%)
  Pallas kernels  132 us (31%)
  starting transfers between devices  46.4 us (11%)
  other arithmetic  15.3 us (4%)
  local copies, waits for them, and re-layouts  13.8 us (3%)
    pallas_call x28, Pallas kernels, call(): pl.pallas_call(kernel, out_shape=outs, grid_spec=pltpu.PrefetchScalarGrid...  132 us
    ppermute x16, waiting for transfers between devices, swap_by_core(): return lax.ppermute(x, AXES, pairs)  110 us
    ppermute x31, waiting for transfers between devices, swap(): return lax.ppermute(x, AXES, [(i, i ^ bit) for i in range(self.count)])  102 us
    ppermute x16, starting transfers between devices, swap_by_core(): return lax.ppermute(x, AXES, pairs)  24.5 us
    ppermute x31, starting transfers between devices, swap(): return lax.ppermute(x, AXES, [(i, i ^ bit) for i in range(self.count)])  21.9 us
    concatenate x16, other arithmetic, join(): self.x = jnp.concatenate((self.x, self.got), axis=0)  13.6 us
  transfers between devices with their start and end apart: 47, of which 27 were waited for; matrix products, arithmetic and copies ran while one was open for 4% of the time, Pallas kernels for 26%

profile of v13, /device:TPU:0, one launch (start us, length us, event | category | flops | bytes accessed | tf_op | source)
XLA Modules:
  0.0 425.2 jit_solution(14182074153733911049)
XLA Ops:
  10.3 7.5 %collective-permute-done = bf16[24,3200]{1,0:T(8,128)(2,1)S(1)} collective-permute-done((bf16[24,3200]{1,0:T(8,128)(2,1)}, bf16[24,3200]{1,0:T(8,128)(2,1)S(1)}, u32[]{:S(2)}, u32[]{:S(2)}) %collective-permute-start) | collective-permute-done | bytes 153632 | tf_op jit(solution)/shard_map/ppermute | solution.py:35
  22.9 10.5 %collective-permute-done.1 = bf16[48,3200]{1,0:T(8,128)(2,1)S(1)} collective-permute-done((bf16[48,3200]{1,0:T(8,128)(2,1)S(1)}, bf16[48,3200]{1,0:T(8,128)(2,1)S(1)}, u32[]{:S(2)}, u32[]{:S(2)}) %collective-permute-start.1) | collective-permute-done | bytes 307232 | tf_op jit(solution)/shard_map/ppermute | solution.py:35
  39.4 9.6 %collective-permute-done.3 = bf16[96,3200]{1,0:T(8,128)(2,1)S(1)} collective-permute-done((bf16[96,3200]{1,0:T(8,128)(2,1)S(1)}, bf16[96,3200]{1,0:T(8,128)(2,1)S(1)}, u32[]{:S(2)}, u32[]{:S(2)}) %collective-permute-start.3) | collective-permute-done | bytes 614432 | tf_op jit(solution)/shard_map/ppermute | solution.py:39
  56.0 10.2 %collective-permute-done.6 = bf16[24,6144]{1,0:T(8,128)(2,1)S(1)} collective-permute-done((bf16[24,6144]{1,0:T(8,128)(2,1)S(1)}, bf16[24,6144]{1,0:T(8,128)(2,1)S(1)}, u32[]{:S(2)}, u32[]{:S(2)}) %collective-permute-start.6) | collective-permute-done | bytes 294944 | tf_op jit(solution)/shard_map/ppermute | solution.py:35
  66.2 10.7 %collective-permute-done.5 = bf16[192,3200]{1,0:T(8,128)(2,1)S(1)} collective-permute-done((bf16[192,3200]{1,0:T(8,128)(2,1)S(1)}, bf16[192,3200]{1,0:T(8,128)(2,1)S(1)}, u32[]{:S(2)}, u32[]{:S(2)}) %collective-permute-start.5) | collective-permute-done | bytes 1228832 | tf_op jit(solution)/shard_map/ppermute | solution.py:39
  86.0 10.5 %collective-permute-done.9 = bf16[48,6144]{1,0:T(8,128)(2,1)S(1)} collective-permute-done((bf16[48,6144]{1,0:T(8,128)(2,1)S(1)}, bf16[48,6144]{1,0:T(8,128)(2,1)S(1)}, u32[]{:S(2)}, u32[]{:S(2)}) %collective-permute-start.9) | collective-permute-done | bytes 589856 | tf_op jit(solution)/shard_map/ppermute | solution.py:35
  96.7 13.8 %collective-permute-done.10 = bf16[24,6144]{1,0:T(8,128)(2,1)S(1)} collective-permute-done((bf16[24,6144]{1,0:T(8,128)(2,1)S(1)}, bf16[24,6144]{1,0:T(8,128)(2,1)S(1)}, u32[]{:S(2)}, u32[]{:S(2)}) %collective-permute-start.10) | collective-permute-done | bytes 294944 | tf_op jit(solution)/shard_map/ppermute | solution.py:35
  115.3 6.6 %shard_map.425 = (f32[128,768]{1,0:T(8,128)S(1)}, bf16[2,128,768]{2,1,0:T(8,128)(2,1)S(1)}, bf16[3,128,768]{2,1,0:T(8,128)(2,1)S(1)}) custom-call(bf16[128,768]{1,0:T(8,128)(2,1)S(1)} %bitcast.28, f32[16,768]{1,0:T(8,128)S(1)} %fusion.5.vec_ref, bf16[768,768]{1,0:T(8,128)(2,1)S(1)} %fusion.order_ref, bf16[384,3200]{1,0:T(8,128)(2,1)} %pad_maximum_fusion.3.top_ref, ...), custom_call_target="tpu_custom_call" | custom-call | flops 1000 | bytes 1000 | tf_op jit(solution)/shard_map/pallas_call | solution.py:600
  141.1 21.2 %collective-permute-done.15 = bf16[96,6144]{1,0:T(8,128)(2,1)S(1)} collective-permute-done((bf16[96,6144]{1,0:T(8,128)(2,1)S(1)}, bf16[96,6144]{1,0:T(8,128)(2,1)S(1)}, u32[]{:S(2)}, u32[]{:S(2)}) %collective-permute-start.15) | collective-permute-done | bytes 1179680 | tf_op jit(solution)/shard_map/ppermute | solution.py:39
  163.9 8.2 %collective-permute-done.16 = bf16[192,6144]{1,0:T(8,128)(2,1)S(1)} collective-permute-done((bf16[192,6144]{1,0:T(8,128)(2,1)S(1)}, bf16[192,6144]{1,0:T(8,128)(2,1)S(1)}, u32[]{:S(2)}, u32[]{:S(2)}) %collective-permute-start.16) | collective-permute-done | bytes 2359328 | tf_op jit(solution)/shard_map/ppermute | solution.py:39
  194.8 9.2 %shard_map.429 = (f32[128,768]{1,0:T(8,128)S(1)}, bf16[2,128,768]{2,1,0:T(8,128)(2,1)S(1)}, bf16[128,768]{1,0:T(8,128)(2,1)S(1)}) custom-call(s32[2]{0:T(128)S(1)} %copy-done.33, f32[128,768]{1,0:T(8,128)S(1)} %get-tuple-element.389.x_ref, f32[16,768]{1,0:T(8,128)S(1)} %fusion.5.vec_ref, bf16[768,768]{1,0:T(8,128)(2,1)S(1)} %fusion.order_ref, ...), custom_call_target="tpu_custom_call" | custom-call | flops 1000 | bytes 1000 | tf_op jit(solution)/shard_map/pallas_call | solution.py:600
  208.3 6.9 %collective-permute-done.19.up2_ref.down2_ref = bf16[384,6144]{1,0:T(8,128)(2,1)S(1)} collective-permute-done((bf16[384,6144]{1,0:T(8,128)(2,1)S(1)}, bf16[384,6144]{1,0:T(8,128)(2,1)S(1)}, u32[]{:S(2)}, u32[]{:S(2)}) %collective-permute-start.19) | collective-permute-done | bytes 4718624 | tf_op jit(solution)/shard_map/ppermute | solution.py:35
  217.9 7.6 %shard_map.430 = (f32[128,768]{1,0:T(8,128)S(1)}, f32[8,768]{1,0:T(8,128)S(1)}, bf16[5,128,768]{2,1,0:T(8,128)(2,1)S(1)}, bf16[5,128,768]{2,1,0:T(8,128)(2,1)S(1)}) custom-call(f32[128,768]{1,0:T(8,128)S(1)} %get-tuple-element.402.x_ref, f32[16,768]{1,0:T(8,128)S(1)} %fusion.5.vec_ref, bf16[768,768]{1,0:T(8,128)(2,1)S(1)} %fusion.order_ref, ...), custom_call_target="tpu_custom_call" | custom-call | flops 1000 | bytes 1000 | tf_op jit(solution)/shard_map/pallas_call | solution.py:600
  238.9 11.1 %shard_map.433 = (f32[128,768]{1,0:T(8,128)S(1)}, f32[8,768]{1,0:T(8,128)S(1)}, bf16[2,128,768]{2,1,0:T(8,128)(2,1)S(1)}, bf16[1152,1536]{1,0:T(8,128)(2,1)S(1)}) custom-call(s32[2]{0:T(128)S(1)} %copy-done.33, f32[128,768]{1,0:T(8,128)S(1)} %copy-done.12, f32[16,768]{1,0:T(8,128)S(1)} %fusion.5.vec_ref, bf16[768,768]{1,0:T(8,128)(2,1)S(1)} %fusion.order_ref, ...), custom_call_target="tpu_custom_call" | custom-call | flops 1000 | bytes 1000 | tf_op jit(solution)/shard_map/pallas_call | solution.py:600
  254.2 10.3 %shard_map.435 = (f32[128,768]{1,0:T(8,128)S(1)}, f32[8,768]{1,0:T(8,128)S(1)}, bf16[4,128,768]{2,1,0:T(8,128)(2,1)S(1)}) custom-call(f32[128,768]{1,0:T(8,128)S(1)} %get-tuple-element.386.x_ref, f32[16,768]{1,0:T(8,128)S(1)} %fusion.5.vec_ref, bf16[768,768]{1,0:T(8,128)(2,1)S(1)} %fusion.order_ref, bf16[3,128,768]{2,1,0:T(8,128)(2,1)S(1)} %copy-done.18, ...), custom_call_target="tpu_custom_call" | custom-call | flops 1000 | bytes 1000 | tf_op jit(solution)/shard_map/pallas_call | solution.py:600
  275.5 6.5 %shard_map.438 = (f32[128,768]{1,0:T(8,128)S(1)}, f32[8,768]{1,0:T(8,128)S(1)}, bf16[5,128,768]{2,1,0:T(8,128)(2,1)S(1)}) custom-call(f32[128,768]{1,0:T(8,128)S(1)} %copy-done.10, f32[16,768]{1,0:T(8,128)S(1)} %fusion.5.vec_ref, bf16[768,768]{1,0:T(8,128)(2,1)S(1)} %fusion.order_ref, f32[128,768]{1,0:T(8,128)S(1)} %get-tuple-element.447.dx_ref, ...), custom_call_target="tpu_custom_call" | custom-call | flops 1000 | bytes 1000 | tf_op jit(solution)/shard_map/pallas_call | solution.py:600
  289.0 11.0 %shard_map.440 = (f32[128,768]{1,0:T(8,128)S(1)}, f32[8,768]{1,0:T(8,128)}, bf16[5,128,768]{2,1,0:T(8,128)(2,1)S(1)}) custom-call(bf16[128,768]{1,0:T(8,128)(2,1)S(1)} %bitcast.29, f32[16,768]{1,0:T(8,128)S(1)} %fusion.5.vec_ref, bf16[768,768]{1,0:T(8,128)(2,1)S(1)} %fusion.order_ref, bf16[3,128,768]{2,1,0:T(8,128)(2,1)S(1)} %copy-done.16, ...), custom_call_target="tpu_custom_call" | custom-call | flops 1000 | bytes 1000 | tf_op jit(solution)/shard_map/pallas_call | solution.py:600
  300.2 10.9 %collective-permute-done.31.got_ref = bf16[96,6144]{1,0:T(8,128)(2,1)S(1)} collective-permute-done((bf16[96,6144]{1,0:T(8,128)(2,1)S(1)}, bf16[96,6144]{1,0:T(8,128)(2,1)S(1)}, u32[]{:S(2)}, u32[]{:S(2)}) %collective-permute-start.31) | collective-permute-done | bytes 1179680 | tf_op jit(solution)/shard_map/ppermute | solution.py:39
  324.1 8.2 %shard_map.444 = bf16[1152,768]{1,0:T(8,128)(2,1)} custom-call(bf16[1152,1536]{1,0:T(8,128)(2,1)S(1)} %get-tuple-element.488.dkv_ref, bf16[768,768]{1,0:T(8,128)(2,1)S(1)} %fusion.order_ref, bf16[384,6144]{1,0:T(8,128)(2,1)} %pad_maximum_fusion.1.top_ref, bf16[384,6144]{1,0:T(8,128)(2,1)} %collective-permute-done.17.low_ref), custom_call_target="tpu_custom_call" | custom-call | flops 1000 | bytes 1000 | tf_op jit(solution)/shard_map/pallas_call | solution.py:600
  332.4 13.4 %collective-permute-done.34.got_ref = bf16[96,6144]{1,0:T(8,128)(2,1)S(1)} collective-permute-done((bf16[96,6144]{1,0:T(8,128)(2,1)S(1)}, bf16[96,6144]{1,0:T(8,128)(2,1)S(1)}, u32[]{:S(2)}, u32[]{:S(2)}) %collective-permute-start.34) | collective-permute-done | bytes 1179680 | tf_op jit(solution)/shard_map/ppermute | solution.py:39
  348.7 7.6 %collective-permute-done.36.got_ref = bf16[192,6144]{1,0:T(8,128)(2,1)S(1)} collective-permute-done((bf16[192,6144]{1,0:T(8,128)(2,1)S(1)}, bf16[192,6144]{1,0:T(8,128)(2,1)S(1)}, u32[]{:S(2)}, u32[]{:S(2)}) %collective-permute-start.36) | collective-permute-done | bytes 2359328 | tf_op jit(solution)/shard_map/ppermute | solution.py:39
  366.7 16.8 %collective-permute-done.39.got_ref = bf16[96,6144]{1,0:T(8,128)(2,1)S(1)} collective-permute-done((bf16[96,6144]{1,0:T(8,128)(2,1)S(1)}, bf16[96,6144]{1,0:T(8,128)(2,1)S(1)}, u32[]{:S(2)}, u32[]{:S(2)}) %collective-permute-start.39) | collective-permute-done | bytes 1179680 | tf_op jit(solution)/shard_map/ppermute | solution.py:39
  387.2 11.5 %collective-permute-done.42 = bf16[48,6144]{1,0:T(8,128)(2,1)S(1)} collective-permute-done((bf16[48,6144]{1,0:T(8,128)(2,1)S(1)}, bf16[48,6144]{1,0:T(8,128)(2,1)S(1)}, u32[]{:S(2)}, u32[]{:S(2)}) %collective-permute-start.42) | collective-permute-done | bytes 589856 | tf_op jit(solution)/shard_map/ppermute | solution.py:35
  401.6 11.7 %collective-permute-done.44.got_ref = bf16[24,6144]{1,0:T(8,128)(2,1)S(1)} collective-permute-done((bf16[24,6144]{1,0:T(8,128)(2,1)S(1)}, bf16[24,6144]{1,0:T(8,128)(2,1)S(1)}, u32[]{:S(2)}, u32[]{:S(2)}) %collective-permute-start.44) | collective-permute-done | bytes 294944 | tf_op jit(solution)/shard_map/ppermute | solution.py:35
  (227 shorter events, 171.6 us)
Async XLA Ops:
  18.8 14.7 %collective-permute-start.1 = (bf16[48,3200]{1,0:T(8,128)(2,1)S(1)}, bf16[48,3200]{1,0:T(8,128)(2,1)S(1)}, u32[]{:S(2)}, u32[]{:S(2)}) collective-permute-start(bf16[48,3200]{1,0:T(8,128)(2,1)S(1)} %pad_maximum_fusion.17), channel_id=1, source_target_pairs={{0,8},{1,9},{2,10},{3,11},{4,12},{5,13},{6,14},{7,15},{8,0},{9,1},... | collective-permute-start | bytes 921608 | tf_op jit(solution)/shard_map/ppermute | solution.py:35
  19.6 16.8 %collective-permute-start.2 = (bf16[24,6144]{1,0:T(8,128)(2,1)}, bf16[24,6144]{1,0:T(8,128)(2,1)S(1)}, u32[]{:S(2)}, u32[]{:S(2)}) collective-permute-start(bf16[24,6144]{1,0:T(8,128)(2,1)} %get-tuple-element.310), channel_id=1, source_target_pairs={{0,16},{1,17},{2,18},{3,19},{4,20},{5,21},{6,22},{7,23},{8,24},{9,... | collective-permute-start | bytes 884744 | tf_op jit(solution)/shard_map/ppermute | solution.py:35
  49.1 27.8 %collective-permute-start.5 = (bf16[192,3200]{1,0:T(8,128)(2,1)S(1)}, bf16[192,3200]{1,0:T(8,128)(2,1)S(1)}, u32[]{:S(2)}, u32[]{:S(2)}) collective-permute-start(bf16[192,3200]{1,0:T(8,128)(2,1)S(1)} %pad_maximum_fusion.7), channel_id=1, source_target_pairs={{0,4},{1,5},{2,3},{3,2},{4,0},{5,1},{6,7},{7,6},{8,12},{9,13},{10,... | collective-permute-start | bytes 3686408 | tf_op jit(solution)/shard_map/ppermute | solution.py:39
  52.1 14.1 %collective-permute-start.6 = (bf16[24,6144]{1,0:T(8,128)(2,1)S(1)}, bf16[24,6144]{1,0:T(8,128)(2,1)S(1)}, u32[]{:S(2)}, u32[]{:S(2)}) collective-permute-start(bf16[24,6144]{1,0:T(8,128)(2,1)S(1)} %copy-done.35), channel_id=1, source_target_pairs={{0,16},{1,17},{2,18},{3,19},{4,20},{5,21},{6,22},{7,23},{8,24},{9,... | collective-permute-start | bytes 884744 | tf_op jit(solution)/shard_map/ppermute | solution.py:35
  54.5 24.1 %collective-permute-start.7 = (bf16[96,6144]{1,0:T(8,128)(2,1)S(1)}, bf16[96,6144]{1,0:T(8,128)(2,1)}, u32[]{:S(2)}, u32[]{:S(2)}) collective-permute-start(bf16[96,6144]{1,0:T(8,128)(2,1)S(1)} %pad_maximum_fusion.10), channel_id=1, source_target_pairs={{0,1},{1,0},{2,6},{3,7},{4,5},{5,4},{6,2},{7,3},{8,9},{9,8},{10,14... | collective-permute-start | bytes 3538952 | tf_op jit(solution)/shard_map/ppermute | solution.py:39
  80.1 30.5 %collective-permute-start.11 = (bf16[192,6144]{1,0:T(8,128)(2,1)S(1)}, bf16[192,6144]{1,0:T(8,128)(2,1)S(1)}, u32[]{:S(2)}, u32[]{:S(2)}) collective-permute-start(bf16[192,6144]{1,0:T(8,128)(2,1)S(1)} %pad_maximum_fusion.4), channel_id=1, source_target_pairs={{0,4},{1,5},{2,3},{3,2},{4,0},{5,1},{6,7},{7,6},{8,12},{9,13},{10,... | collective-permute-start | bytes 7077896 | tf_op jit(solution)/shard_map/ppermute | solution.py:39
  111.2 22.6 %collective-permute-start.14 = (bf16[384,6144]{1,0:T(8,128)(2,1)S(1)}, bf16[384,6144]{1,0:T(8,128)(2,1)S(1)}, u32[]{:S(2)}, u32[]{:S(2)}) collective-permute-start(bf16[384,6144]{1,0:T(8,128)(2,1)S(1)} %pad_maximum_fusion.up_ref.down_ref), channel_id=1, source_target_pairs={{0,2},{1,3},{2,0},{3,1},{4,6},{5,7},{6,4},{7,5},{8,10},{9,11},{10,... | collective-permute-start | bytes 14155784 | tf_op jit(solution)/shard_map/ppermute | solution.py:35
  111.2 16.3 %collective-permute-start.12 = (bf16[96,6144]{1,0:T(8,128)(2,1)S(1)}, bf16[96,6144]{1,0:T(8,128)(2,1)S(1)}, u32[]{:S(2)}, u32[]{:S(2)}) collective-permute-start(bf16[96,6144]{1,0:T(8,128)(2,1)S(1)} %pad_maximum_fusion.11), channel_id=1, source_target_pairs={{0,1},{1,0},{2,6},{3,7},{4,5},{5,4},{6,2},{7,3},{8,9},{9,8},{10,14... | collective-permute-start | bytes 3538952 | tf_op jit(solution)/shard_map/ppermute | solution.py:39
  115.3 15.0 %collective-permute-start.13 = (bf16[48,6144]{1,0:T(8,128)(2,1)S(1)}, bf16[48,6144]{1,0:T(8,128)(2,1)S(1)}, u32[]{:S(2)}, u32[]{:S(2)}) collective-permute-start(bf16[48,6144]{1,0:T(8,128)(2,1)S(1)} %pad_maximum_fusion.16), channel_id=1, source_target_pairs={{0,8},{1,9},{2,10},{3,11},{4,12},{5,13},{6,14},{7,15},{8,0},{9,1},... | collective-permute-start | bytes 1769480 | tf_op jit(solution)/shard_map/ppermute | solution.py:35
  130.3 41.8 %collective-permute-start.16 = (bf16[192,6144]{1,0:T(8,128)(2,1)S(1)}, bf16[192,6144]{1,0:T(8,128)(2,1)S(1)}, u32[]{:S(2)}, u32[]{:S(2)}) collective-permute-start(bf16[192,6144]{1,0:T(8,128)(2,1)S(1)} %pad_maximum_fusion.5), channel_id=1, source_target_pairs={{0,4},{1,5},{2,3},{3,2},{4,0},{5,1},{6,7},{7,6},{8,12},{9,13},{10,... | collective-permute-start | bytes 7077896 | tf_op jit(solution)/shard_map/ppermute | solution.py:39
  133.3 29.0 %collective-permute-start.15 = (bf16[96,6144]{1,0:T(8,128)(2,1)S(1)}, bf16[96,6144]{1,0:T(8,128)(2,1)S(1)}, u32[]{:S(2)}, u32[]{:S(2)}) collective-permute-start(bf16[96,6144]{1,0:T(8,128)(2,1)S(1)} %pad_maximum_fusion.12), channel_id=1, source_target_pairs={{0,1},{1,0},{2,6},{3,7},{4,5},{5,4},{6,2},{7,3},{8,9},{9,8},{10,14... | collective-permute-start | bytes 3538952 | tf_op jit(solution)/shard_map/ppermute | solution.py:39
  174.8 29.3 %collective-permute-start.18 = (bf16[192,6144]{1,0:T(8,128)(2,1)}, bf16[192,6144]{1,0:T(8,128)(2,1)}, u32[]{:S(2)}, u32[]{:S(2)}) collective-permute-start(bf16[192,6144]{1,0:T(8,128)(2,1)} %pad_maximum_fusion.6), channel_id=1, source_target_pairs={{0,4},{1,5},{2,3},{3,2},{4,0},{5,1},{6,7},{7,6},{8,12},{9,13},{10,... | collective-permute-start | bytes 7077896 | tf_op jit(solution)/shard_map/ppermute | solution.py:39
  237.9 29.1 %collective-permute-start.26 = (bf16[192,6144]{1,0:T(8,128)(2,1)}, bf16[192,6144]{1,0:T(8,128)(2,1)S(1)}, u32[]{:S(2)}, u32[]{:S(2)}) collective-permute-start(bf16[192,6144]{1,0:T(8,128)(2,1)} %get-tuple-element.425), channel_id=1, source_target_pairs={{0,4},{1,5},{2,3},{3,2},{4,0},{5,1},{6,7},{7,6},{8,12},{9,13},{10,... | collective-permute-start | bytes 7077896 | tf_op jit(solution)/shard_map/ppermute | solution.py:39
  274.3 41.5 %collective-permute-start.32 = (bf16[192,6144]{1,0:T(8,128)(2,1)S(1)}, bf16[192,6144]{1,0:T(8,128)(2,1)S(1)}, u32[]{:S(2)}, u32[]{:S(2)}) collective-permute-start(bf16[192,6144]{1,0:T(8,128)(2,1)S(1)} %get-tuple-element.472), channel_id=1, source_target_pairs={{0,4},{1,5},{2,3},{3,2},{4,0},{5,1},{6,7},{7,6},{8,12},{9,13},{10,... | collective-permute-start | bytes 7077896 | tf_op jit(solution)/shard_map/ppermute | solution.py:39
  282.2 28.9 %collective-permute-start.31 = (bf16[96,6144]{1,0:T(8,128)(2,1)S(1)}, bf16[96,6144]{1,0:T(8,128)(2,1)S(1)}, u32[]{:S(2)}, u32[]{:S(2)}) collective-permute-start(bf16[96,6144]{1,0:T(8,128)(2,1)S(1)} %get-tuple-element.464), channel_id=1, source_target_pairs={{0,1},{1,0},{2,6},{3,7},{4,5},{5,4},{6,2},{7,3},{8,9},{9,8},{10,14... | collective-permute-start | bytes 3538952 | tf_op jit(solution)/shard_map/ppermute | solution.py:39
  300.1 20.1 %collective-permute-start.33 = (bf16[5,128,768]{2,1,0:T(8,128)(2,1)S(1)}, bf16[5,128,768]{2,1,0:T(8,128)(2,1)S(1)}, u32[]{:S(2)}, u32[]{:S(2)}) collective-permute-start(bf16[5,128,768]{2,1,0:T(8,128)(2,1)S(1)} %get-tuple-element.482.sd_ref), channel_id=1, source_target_pairs={{0,2},{1,3},{2,0},{3,1},{4,6},{5,7},{6,4},{7,5},{8,10},{9,11},{10,... | collective-permute-start | bytes 2949128 | tf_op jit(solution)/shard_map/ppermute | solution.py:35
  316.9 28.9 %collective-permute-start.34 = (bf16[96,6144]{1,0:T(8,128)(2,1)S(1)}, bf16[96,6144]{1,0:T(8,128)(2,1)S(1)}, u32[]{:S(2)}, u32[]{:S(2)}) collective-permute-start(bf16[96,6144]{1,0:T(8,128)(2,1)S(1)} %get-tuple-element.491), channel_id=1, source_target_pairs={{0,1},{1,0},{2,6},{3,7},{4,5},{5,4},{6,2},{7,3},{8,9},{9,8},{10,14... | collective-permute-start | bytes 3538952 | tf_op jit(solution)/shard_map/ppermute | solution.py:39
  318.0 28.3 %collective-permute-start.35 = (bf16[48,6144]{1,0:T(8,128)(2,1)S(1)}, bf16[48,6144]{1,0:T(8,128)(2,1)S(1)}, u32[]{:S(2)}, u32[]{:S(2)}) collective-permute-start(bf16[48,6144]{1,0:T(8,128)(2,1)S(1)} %get-tuple-element.500), channel_id=1, source_target_pairs={{0,8},{1,9},{2,10},{3,11},{4,12},{5,13},{6,14},{7,15},{8,0},{9,1},... | collective-permute-start | bytes 1769480 | tf_op jit(solution)/shard_map/ppermute | solution.py:35
  318.5 37.8 %collective-permute-start.36 = (bf16[192,6144]{1,0:T(8,128)(2,1)S(1)}, bf16[192,6144]{1,0:T(8,128)(2,1)S(1)}, u32[]{:S(2)}, u32[]{:S(2)}) collective-permute-start(bf16[192,6144]{1,0:T(8,128)(2,1)S(1)} %get-tuple-element.506), channel_id=1, source_target_pairs={{0,4},{1,5},{2,3},{3,2},{4,0},{5,1},{6,7},{7,6},{8,12},{9,13},{10,... | collective-permute-start | bytes 7077896 | tf_op jit(solution)/shard_map/ppermute | solution.py:39
  346.3 16.7 %collective-permute-start.38 = (bf16[48,6144]{1,0:T(8,128)(2,1)S(1)}, bf16[48,6144]{1,0:T(8,128)(2,1)S(1)}, u32[]{:S(2)}, u32[]{:S(2)}) collective-permute-start(bf16[48,6144]{1,0:T(8,128)(2,1)S(1)} %get-tuple-element.517), channel_id=1, source_target_pairs={{0,8},{1,9},{2,10},{3,11},{4,12},{5,13},{6,14},{7,15},{8,0},{9,1},... | collective-permute-start | bytes 1769480 | tf_op jit(solution)/shard_map/ppermute | solution.py:35
  347.8 35.7 %collective-permute-start.40 = (bf16[192,3200]{1,0:T(8,128)(2,1)S(1)}, bf16[192,3200]{1,0:T(8,128)(2,1)S(1)}, u32[]{:S(2)}, u32[]{:S(2)}) collective-permute-start(bf16[192,3200]{1,0:T(8,128)(2,1)S(1)} %pad_maximum_fusion.8), channel_id=1, source_target_pairs={{0,4},{1,5},{2,3},{3,2},{4,0},{5,1},{6,7},{7,6},{8,12},{9,13},{10,... | collective-permute-start | bytes 3686408 | tf_op jit(solution)/shard_map/ppermute | solution.py:39
  357.4 26.1 %collective-permute-start.39 = (bf16[96,6144]{1,0:T(8,128)(2,1)S(1)}, bf16[96,6144]{1,0:T(8,128)(2,1)S(1)}, u32[]{:S(2)}, u32[]{:S(2)}) collective-permute-start(bf16[96,6144]{1,0:T(8,128)(2,1)S(1)} %get-tuple-element.523), channel_id=1, source_target_pairs={{0,1},{1,0},{2,6},{3,7},{4,5},{5,4},{6,2},{7,3},{8,9},{9,8},{10,14... | collective-permute-start | bytes 3538952 | tf_op jit(solution)/shard_map/ppermute | solution.py:39
  363.2 22.3 %collective-permute-start.41 = (bf16[24,6144]{1,0:T(8,128)(2,1)S(1)}, bf16[24,6144]{1,0:T(8,128)(2,1)S(1)}, u32[]{:S(2)}, u32[]{:S(2)}) collective-permute-start(bf16[24,6144]{1,0:T(8,128)(2,1)S(1)} %add_convert_fusion.3), channel_id=1, source_target_pairs={{0,16},{1,17},{2,18},{3,19},{4,20},{5,21},{6,22},{7,23},{8,24},{9,... | collective-permute-start | bytes 884744 | tf_op jit(solution)/shard_map/ppermute | solution.py:35
  399.0 17.2 %collective-permute-start.45 = (bf16[48,3200]{1,0:T(8,128)(2,1)S(1)}, bf16[48,3200]{1,0:T(8,128)(2,1)S(1)}, u32[]{:S(2)}, u32[]{:S(2)}) collective-permute-start(bf16[48,3200]{1,0:T(8,128)(2,1)S(1)} %get-tuple-element.554), channel_id=1, source_target_pairs={{0,8},{1,9},{2,10},{3,11},{4,12},{5,13},{6,14},{7,15},{8,0},{9,1},... | collective-permute-start | bytes 921608 | tf_op jit(solution)/shard_map/ppermute | solution.py:35
  (63 other events, 642.5 us)

commit v14 on v13

--- a/solution.py
+++ b/solution.py
@@ -560,11 +560,18 @@
     emit(nn(enc_ref[...], dkv_ref[...]), send_ref, keep_ref)
 
 
+def first_pack_kernel(u_qkv, u_out, vec, out):
+    rows, d = u_out.shape
+    out[:, : 3 * d] = u_qkv[...]
+    out[:, 3 * d : 4 * d] = u_out[...]
+    eye = lax.broadcasted_iota(jnp.int32, (rows, rows), 0) == lax.broadcasted_iota(jnp.int32, (rows, rows), 1)
+    out[:, 4 * d :] = nt(eye.astype(bf16), vec[...]).astype(bf16)
+
+
 def pack_kernel(
-    u_qkv, u_out, u_up, u_down, m_qkv, m_out, m_up, m_down, c_q, c_pair, c_out, vec,
-    first_out, feed_out, middle_out, last_out,
+    u_up, u_down, m_qkv, m_out, m_up, m_down, c_q, c_pair, c_out, feed_out, middle_out, last_out
 ):
-    rows, d = u_out.shape
+    rows, d = m_out.shape
     spread = spread_matrix().astype(bf16)
     i = lax.broadcasted_iota(jnp.int32, (rows, 4 * rows), 0)
     k = lax.broadcasted_iota(jnp.int32, (rows, 4 * rows), 1)
@@ -579,10 +586,6 @@
             y = nn((k == 4 * i + j).astype(bf16), down[...])
             out[:, (4 + j) * d : (5 + j) * d] = y.astype(bf16)
 
-    first_out[:, : 3 * d] = u_qkv[...]
-    first_out[:, 3 * d : 4 * d] = u_out[...]
-    eye = lax.broadcasted_iota(jnp.int32, (rows, rows), 0) == lax.broadcasted_iota(jnp.int32, (rows, rows), 1)
-    first_out[:, 4 * d :] = nt(eye.astype(bf16), vec[...]).astype(bf16)
     feed(feed_out, u_up, u_down)
     middle_out[:, : 2 * d] = c_pair[...]
     middle_out[:, 2 * d : 3 * d] = c_q[...]
@@ -798,12 +801,14 @@
 
     vectors = (u_ag, u_as, u_mg, u_ms, m_ag, m_as, c_g, c_s, m_mg, m_ms)
     vectors = jnp.pad(jnp.stack(vectors, axis=0), ((0, LANES - len(vectors)), (0, 0)))
-    parts = (u_qkv, u_out, u_up, u_down, m_qkv, m_out, m_up, m_down, c_q, c_pair, c_out, vectors)
-    packed = tuple(sds((rows, c), bf16) for c in (4 * d + LANES, 8 * d, 8 * d, 8 * d))
-    shards = call(
-        pack_kernel, 1, parts, [whole(p) for p in parts], packed, [whole(p) for p in packed], vmem=60
-    )
-    first, feed, middle, last = (Gather(place, x) for x in shards)
+    def packed(kernel, parts, *widths):
+        outs = tuple(sds((rows, c), bf16) for c in widths)
+        shards = call(kernel, 1, parts, [whole(p) for p in parts], outs, [whole(o) for o in outs], vmem=60)
+        return [Gather(place, x) for x in shards]
+
+    (first,) = packed(first_pack_kernel, (u_qkv, u_out, vectors), 4 * d + LANES)
+    parts = (u_up, u_down, m_qkv, m_out, m_up, m_down, c_q, c_pair, c_out)
+    feed, middle, last = packed(pack_kernel, parts, 8 * d, 8 * d, 8 * d)
 
     def go(token, groups=(), start=()):
         token, got = tie(token, *[(g.x, g.got) for g in groups])
@@ -846,14 +851,14 @@
     x0 = go(x0, [feed])
     x0a, f_us, k_us = net.self_forward(x0, w_first, 0, 0)
     x0a = go(x0a, [middle])
-    x0a = go(x0a, [last])
     x0a, w_feed = end(x0a, feed)
     x1, f_uf, k_uf = net.feed_forward(x0a, w_feed, 2)
+    x1 = go(x1, [middle, last])
+    x1, w_middle = end(x1, middle)
+    kv = net.pair_forward(enc_rel, w_middle)
+    x1, (kv,) = tie(x1, kv)
     x1 = go(x1, [last])
-    x1 = go(x1, [middle])
-    x1, w_middle = end(x1, middle)
     x1a, f_ms, k_ms = net.self_forward(x1, w_middle, 4, 4)
-    kv = net.pair_forward(enc_rel, w_middle)
     x1b, f_mc, k_mc = net.cross_forward(x1a, kv, w_middle, 2, 6)
     x1b = go(x1b, [last])
     x1b, w_last = end(x1b, last)
@@ -925,14 +930,15 @@
     dx = go_on(dx, start=[s_us])
     dx = rest(dx, s_mf)
     dx = go_on(dx, [s_uf], [s_uf])
+    dx = hold(dx, s_mf)
     dx, (r_mf,) = tie(dx, feed_rows(s_mf.kept, s_mf.got))
     dx = rest(dx, s_ma)
     dx = go_on(dx, [s_uf, s_us], [s_uf, s_us])
     dx, (r_ma,) = tie(dx, s_ma.total())
-    dx = rest(dx, s_uf)
     dx = go_on(dx, [s_us], [s_us])
+    dx = rest(dx, s_uf, s_us)
+    dx = hold(dx, s_uf)
     dx, (r_uf,) = tie(dx, feed_rows(s_uf.kept, s_uf.got))
-    dx = rest(dx, s_us)
     r_us = s_us.total()
 
     def columns(r, *blocks):

time: 430 us -> 440 us (1.023)
  waiting for transfers between devices: 212 us -> 222 us
    ppermute x16, waiting for transfers between devices: 110 us -> 119 us  [swap_by_core(): return lax.ppermute(x, AXES, pairs)]
    pallas_call x28 -> x29, Pallas kernels: 132 us -> 134 us  [call(): pl.pallas_call(kernel, out_shape=outs, grid_spec=pltpu.PrefetchScalarGrid...]
  transfers between devices with their start and end apart: 47 -> 47, of which waited for: 27 -> 31; matrix products, arithmetic and copies ran while one was open for 4% -> 4% of each run, Pallas kernels for 26% -> 26%
where the time goes in v14:
time: 440 us; the launch traced here: 435 us
  waiting for transfers between devices  222 us (50%)
  Pallas kernels  134 us (30%)
  starting transfers between devices  43.9 us (10%)
  other arithmetic  15.8 us (4%)
  local copies, waits for them, and re-layouts  13.6 us (3%)
    pallas_call x29, Pallas kernels, call(): pl.pallas_call(kernel, out_shape=outs, grid_spec=pltpu.PrefetchScalarGrid...  134 us
    ppermute x16, waiting for transfers between devices, swap_by_core(): return lax.ppermute(x, AXES, pairs)  119 us
    ppermute x31, waiting for transfers between devices, swap(): return lax.ppermute(x, AXES, [(i, i ^ bit) for i in range(self.count)])  103 us
    ppermute x16, starting transfers between devices, swap_by_core(): return lax.ppermute(x, AXES, pairs)  24.6 us
    ppermute x31, starting transfers between devices, swap(): return lax.ppermute(x, AXES, [(i, i ^ bit) for i in range(self.count)])  19.3 us
    concatenate x16, other arithmetic, join(): self.x = jnp.concatenate((self.x, self.got), axis=0)  14.1 us
  transfers between devices with their start and end apart: 47, of which 31 were waited for; matrix products, arithmetic and copies ran while one was open for 4% of the time, Pallas kernels for 26%

profile of v14, /device:TPU:0, one launch (start us, length us, event | category | flops | bytes accessed | tf_op | source)
XLA Modules:
  0.0 435.1 jit_solution(6865093395274813193)
XLA Ops:
  21.3 10.5 %collective-permute-done.1 = bf16[48,3200]{1,0:T(8,128)(2,1)S(1)} collective-permute-done((bf16[48,3200]{1,0:T(8,128)(2,1)S(1)}, bf16[48,3200]{1,0:T(8,128)(2,1)S(1)}, u32[]{:S(2)}, u32[]{:S(2)}) %collective-permute-start.1) | collective-permute-done | bytes 307232 | tf_op jit(solution)/shard_map/ppermute | solution.py:35
  37.8 9.6 %collective-permute-done.3 = bf16[96,3200]{1,0:T(8,128)(2,1)S(1)} collective-permute-done((bf16[96,3200]{1,0:T(8,128)(2,1)S(1)}, bf16[96,3200]{1,0:T(8,128)(2,1)S(1)}, u32[]{:S(2)}, u32[]{:S(2)}) %collective-permute-start.3) | collective-permute-done | bytes 614432 | tf_op jit(solution)/shard_map/ppermute | solution.py:39
  54.4 10.2 %collective-permute-done.6 = bf16[24,6144]{1,0:T(8,128)(2,1)S(1)} collective-permute-done((bf16[24,6144]{1,0:T(8,128)(2,1)S(1)}, bf16[24,6144]{1,0:T(8,128)(2,1)S(1)}, u32[]{:S(2)}, u32[]{:S(2)}) %collective-permute-start.6) | collective-permute-done | bytes 294944 | tf_op jit(solution)/shard_map/ppermute | solution.py:35
  64.6 10.7 %collective-permute-done.5 = bf16[192,3200]{1,0:T(8,128)(2,1)S(1)} collective-permute-done((bf16[192,3200]{1,0:T(8,128)(2,1)S(1)}, bf16[192,3200]{1,0:T(8,128)(2,1)S(1)}, u32[]{:S(2)}, u32[]{:S(2)}) %collective-permute-start.5) | collective-permute-done | bytes 1228832 | tf_op jit(solution)/shard_map/ppermute | solution.py:39
  84.4 10.5 %collective-permute-done.9 = bf16[48,6144]{1,0:T(8,128)(2,1)S(1)} collective-permute-done((bf16[48,6144]{1,0:T(8,128)(2,1)S(1)}, bf16[48,6144]{1,0:T(8,128)(2,1)S(1)}, u32[]{:S(2)}, u32[]{:S(2)}) %collective-permute-start.9) | collective-permute-done | bytes 589856 | tf_op jit(solution)/shard_map/ppermute | solution.py:35
  95.1 13.8 %collective-permute-done.10 = bf16[24,6144]{1,0:T(8,128)(2,1)S(1)} collective-permute-done((bf16[24,6144]{1,0:T(8,128)(2,1)S(1)}, bf16[24,6144]{1,0:T(8,128)(2,1)S(1)}, u32[]{:S(2)}, u32[]{:S(2)}) %collective-permute-start.10) | collective-permute-done | bytes 294944 | tf_op jit(solution)/shard_map/ppermute | solution.py:35
  113.7 6.6 %shard_map.426 = (f32[128,768]{1,0:T(8,128)S(1)}, bf16[2,128,768]{2,1,0:T(8,128)(2,1)S(1)}, bf16[3,128,768]{2,1,0:T(8,128)(2,1)S(1)}) custom-call(bf16[128,768]{1,0:T(8,128)(2,1)S(1)} %bitcast.28, f32[16,768]{1,0:T(8,128)S(1)} %fusion.5.vec_ref, bf16[768,768]{1,0:T(8,128)(2,1)S(1)} %fusion.order_ref, bf16[384,3200]{1,0:T(8,128)(2,1)} %pad_maximum_fusion.3.top_ref, ...), custom_call_target="tpu_custom_call" | custom-call | flops 1000 | bytes 1000 | tf_op jit(solution)/shard_map/pallas_call | solution.py:603
  130.2 6.4 %shard_map.427 = (f32[128,768]{1,0:T(8,128)S(1)}, bf16[5,128,768]{2,1,0:T(8,128)(2,1)S(1)}, f32[128,3072]{1,0:T(8,128)S(1)}) custom-call(f32[128,768]{1,0:T(8,128)S(1)} %get-tuple-element.370.x_ref, f32[16,768]{1,0:T(8,128)S(1)} %fusion.5.vec_ref, bf16[768,768]{1,0:T(8,128)(2,1)S(1)} %fusion.order_ref, ...), custom_call_target="tpu_custom_call" | custom-call | flops 1000 | bytes 1000 | tf_op jit(solution)/shard_map/pallas_call | solution.py:603
  143.1 13.8 %collective-permute-done.14 = bf16[192,6144]{1,0:T(8,128)(2,1)S(1)} collective-permute-done((bf16[192,6144]{1,0:T(8,128)(2,1)S(1)}, bf16[192,6144]{1,0:T(8,128)(2,1)S(1)}, u32[]{:S(2)}, u32[]{:S(2)}) %collective-permute-start.14) | collective-permute-done | bytes 2359328 | tf_op jit(solution)/shard_map/ppermute | solution.py:39
  187.4 9.2 %shard_map.430 = (f32[128,768]{1,0:T(8,128)S(1)}, bf16[2,128,768]{2,1,0:T(8,128)(2,1)S(1)}, bf16[128,768]{1,0:T(8,128)(2,1)S(1)}) custom-call(s32[2]{0:T(128)S(1)} %copy-done.33, f32[128,768]{1,0:T(8,128)S(1)} %get-tuple-element.393.x_ref, f32[16,768]{1,0:T(8,128)S(1)} %fusion.5.vec_ref, bf16[768,768]{1,0:T(8,128)(2,1)S(1)} %fusion.order_ref, ...), custom_call_target="tpu_custom_call" | custom-call | flops 1000 | bytes 1000 | tf_op jit(solution)/shard_map/pallas_call | solution.py:603
  196.7 11.6 %collective-permute-done.18 = bf16[192,6144]{1,0:T(8,128)(2,1)} collective-permute-done((bf16[192,6144]{1,0:T(8,128)(2,1)S(1)}, bf16[192,6144]{1,0:T(8,128)(2,1)}, u32[]{:S(2)}, u32[]{:S(2)}) %collective-permute-start.18) | collective-permute-done | bytes 2359328 | tf_op jit(solution)/shard_map/ppermute | solution.py:39
  211.6 6.9 %collective-permute-done.19.up2_ref.down2_ref = bf16[384,6144]{1,0:T(8,128)(2,1)S(1)} collective-permute-done((bf16[384,6144]{1,0:T(8,128)(2,1)S(1)}, bf16[384,6144]{1,0:T(8,128)(2,1)S(1)}, u32[]{:S(2)}, u32[]{:S(2)}) %collective-permute-start.19) | collective-permute-done | bytes 4718624 | tf_op jit(solution)/shard_map/ppermute | solution.py:35
  221.2 7.7 %shard_map.431 = (f32[128,768]{1,0:T(8,128)S(1)}, f32[8,768]{1,0:T(8,128)S(1)}, bf16[5,128,768]{2,1,0:T(8,128)(2,1)S(1)}, bf16[5,128,768]{2,1,0:T(8,128)(2,1)S(1)}) custom-call(f32[128,768]{1,0:T(8,128)S(1)} %get-tuple-element.406.x_ref, f32[16,768]{1,0:T(8,128)S(1)} %fusion.5.vec_ref, bf16[768,768]{1,0:T(8,128)(2,1)S(1)} %fusion.order_ref, ...), custom_call_target="tpu_custom_call" | custom-call | flops 1000 | bytes 1000 | tf_op jit(solution)/shard_map/pallas_call | solution.py:603
  243.2 11.1 %shard_map.434 = (f32[128,768]{1,0:T(8,128)S(1)}, f32[8,768]{1,0:T(8,128)S(1)}, bf16[2,128,768]{2,1,0:T(8,128)(2,1)S(1)}, bf16[1152,1536]{1,0:T(8,128)(2,1)S(1)}) custom-call(s32[2]{0:T(128)S(1)} %copy-done.33, f32[128,768]{1,0:T(8,128)S(1)} %copy-done.12, f32[16,768]{1,0:T(8,128)S(1)} %fusion.5.vec_ref, bf16[768,768]{1,0:T(8,128)(2,1)S(1)} %fusion.order_ref, ...), custom_call_target="tpu_custom_call" | custom-call | flops 1000 | bytes 1000 | tf_op jit(solution)/shard_map/pallas_call | solution.py:603
  258.5 10.3 %shard_map.436 = (f32[128,768]{1,0:T(8,128)S(1)}, f32[8,768]{1,0:T(8,128)S(1)}, bf16[4,128,768]{2,1,0:T(8,128)(2,1)S(1)}) custom-call(f32[128,768]{1,0:T(8,128)S(1)} %get-tuple-element.392.x_ref, f32[16,768]{1,0:T(8,128)S(1)} %fusion.5.vec_ref, bf16[768,768]{1,0:T(8,128)(2,1)S(1)} %fusion.order_ref, bf16[3,128,768]{2,1,0:T(8,128)(2,1)S(1)} %copy-done.18, ...), custom_call_target="tpu_custom_call" | custom-call | flops 1000 | bytes 1000 | tf_op jit(solution)/shard_map/pallas_call | solution.py:603
  279.7 6.5 %shard_map.439 = (f32[128,768]{1,0:T(8,128)S(1)}, f32[8,768]{1,0:T(8,128)S(1)}, bf16[5,128,768]{2,1,0:T(8,128)(2,1)S(1)}) custom-call(f32[128,768]{1,0:T(8,128)S(1)} %copy-done.10, f32[16,768]{1,0:T(8,128)S(1)} %fusion.5.vec_ref, bf16[768,768]{1,0:T(8,128)(2,1)S(1)} %fusion.order_ref, f32[128,768]{1,0:T(8,128)S(1)} %get-tuple-element.451.dx_ref, ...), custom_call_target="tpu_custom_call" | custom-call | flops 1000 | bytes 1000 | tf_op jit(solution)/shard_map/pallas_call | solution.py:603
  293.3 11.0 %shard_map.441 = (f32[128,768]{1,0:T(8,128)S(1)}, f32[8,768]{1,0:T(8,128)}, bf16[5,128,768]{2,1,0:T(8,128)(2,1)S(1)}) custom-call(bf16[128,768]{1,0:T(8,128)(2,1)S(1)} %bitcast.29, f32[16,768]{1,0:T(8,128)S(1)} %fusion.5.vec_ref, bf16[768,768]{1,0:T(8,128)(2,1)S(1)} %fusion.order_ref, bf16[3,128,768]{2,1,0:T(8,128)(2,1)S(1)} %copy-done.16, ...), custom_call_target="tpu_custom_call" | custom-call | flops 1000 | bytes 1000 | tf_op jit(solution)/shard_map/pallas_call | solution.py:603
  304.5 10.8 %collective-permute-done.31.got_ref = bf16[96,6144]{1,0:T(8,128)(2,1)S(1)} collective-permute-done((bf16[96,6144]{1,0:T(8,128)(2,1)S(1)}, bf16[96,6144]{1,0:T(8,128)(2,1)S(1)}, u32[]{:S(2)}, u32[]{:S(2)}) %collective-permute-start.31) | collective-permute-done | bytes 1179680 | tf_op jit(solution)/shard_map/ppermute | solution.py:39
  326.5 8.2 %shard_map.445 = bf16[1152,768]{1,0:T(8,128)(2,1)} custom-call(bf16[1152,1536]{1,0:T(8,128)(2,1)S(1)} %get-tuple-element.492.dkv_ref, bf16[768,768]{1,0:T(8,128)(2,1)S(1)} %fusion.order_ref, bf16[384,6144]{1,0:T(8,128)(2,1)} %pad_maximum_fusion.1.top_ref, bf16[384,6144]{1,0:T(8,128)(2,1)} %collective-permute-done.16.low_ref), custom_call_target="tpu_custom_call" | custom-call | flops 1000 | bytes 1000 | tf_op jit(solution)/shard_map/pallas_call | solution.py:603
  334.8 14.6 %collective-permute-done.34.got_ref = bf16[96,6144]{1,0:T(8,128)(2,1)S(1)} collective-permute-done((bf16[96,6144]{1,0:T(8,128)(2,1)S(1)}, bf16[96,6144]{1,0:T(8,128)(2,1)S(1)}, u32[]{:S(2)}, u32[]{:S(2)}) %collective-permute-start.34) | collective-permute-done | bytes 1179680 | tf_op jit(solution)/shard_map/ppermute | solution.py:39
  351.0 9.6 %collective-permute-done.36.got_ref = bf16[192,6144]{1,0:T(8,128)(2,1)S(1)} collective-permute-done((bf16[192,6144]{1,0:T(8,128)(2,1)S(1)}, bf16[192,6144]{1,0:T(8,128)(2,1)S(1)}, u32[]{:S(2)}, u32[]{:S(2)}) %collective-permute-start.36) | collective-permute-done | bytes 2359328 | tf_op jit(solution)/shard_map/ppermute | solution.py:39
  372.9 17.1 %collective-permute-done.39.got_ref = bf16[96,6144]{1,0:T(8,128)(2,1)S(1)} collective-permute-done((bf16[96,6144]{1,0:T(8,128)(2,1)S(1)}, bf16[96,6144]{1,0:T(8,128)(2,1)S(1)}, u32[]{:S(2)}, u32[]{:S(2)}) %collective-permute-start.39) | collective-permute-done | bytes 1179680 | tf_op jit(solution)/shard_map/ppermute | solution.py:39
  394.4 7.8 %collective-permute-done.42.got_ref = bf16[96,3200]{1,0:T(8,128)(2,1)S(1)} collective-permute-done((bf16[96,3200]{1,0:T(8,128)(2,1)S(1)}, bf16[96,3200]{1,0:T(8,128)(2,1)S(1)}, u32[]{:S(2)}, u32[]{:S(2)}) %collective-permute-start.42) | collective-permute-done | bytes 614432 | tf_op jit(solution)/shard_map/ppermute | solution.py:39
  409.3 12.4 %collective-permute-done.44 = bf16[48,3200]{1,0:T(8,128)(2,1)S(1)} collective-permute-done((bf16[48,3200]{1,0:T(8,128)(2,1)S(1)}, bf16[48,3200]{1,0:T(8,128)(2,1)S(1)}, u32[]{:S(2)}, u32[]{:S(2)}) %collective-permute-start.44) | collective-permute-done | bytes 307232 | tf_op jit(solution)/shard_map/ppermute | solution.py:35
  (228 shorter events, 186.2 us)
Async XLA Ops:
  17.1 14.7 %collective-permute-start.1 = (bf16[48,3200]{1,0:T(8,128)(2,1)S(1)}, bf16[48,3200]{1,0:T(8,128)(2,1)S(1)}, u32[]{:S(2)}, u32[]{:S(2)}) collective-permute-start(bf16[48,3200]{1,0:T(8,128)(2,1)S(1)} %pad_maximum_fusion.17), channel_id=1, source_target_pairs={{0,8},{1,9},{2,10},{3,11},{4,12},{5,13},{6,14},{7,15},{8,0},{9,1},... | collective-permute-start | bytes 921608 | tf_op jit(solution)/shard_map/ppermute | solution.py:35
  18.0 16.8 %collective-permute-start.2 = (bf16[24,6144]{1,0:T(8,128)(2,1)}, bf16[24,6144]{1,0:T(8,128)(2,1)S(1)}, u32[]{:S(2)}, u32[]{:S(2)}) collective-permute-start(bf16[24,6144]{1,0:T(8,128)(2,1)} %get-tuple-element.314), channel_id=1, source_target_pairs={{0,16},{1,17},{2,18},{3,19},{4,20},{5,21},{6,22},{7,23},{8,24},{9,... | collective-permute-start | bytes 884744 | tf_op jit(solution)/shard_map/ppermute | solution.py:35
  47.4 27.8 %collective-permute-start.5 = (bf16[192,3200]{1,0:T(8,128)(2,1)S(1)}, bf16[192,3200]{1,0:T(8,128)(2,1)S(1)}, u32[]{:S(2)}, u32[]{:S(2)}) collective-permute-start(bf16[192,3200]{1,0:T(8,128)(2,1)S(1)} %pad_maximum_fusion.7), channel_id=1, source_target_pairs={{0,4},{1,5},{2,3},{3,2},{4,0},{5,1},{6,7},{7,6},{8,12},{9,13},{10,... | collective-permute-start | bytes 3686408 | tf_op jit(solution)/shard_map/ppermute | solution.py:39
  52.9 24.1 %collective-permute-start.7 = (bf16[96,6144]{1,0:T(8,128)(2,1)S(1)}, bf16[96,6144]{1,0:T(8,128)(2,1)}, u32[]{:S(2)}, u32[]{:S(2)}) collective-permute-start(bf16[96,6144]{1,0:T(8,128)(2,1)S(1)} %pad_maximum_fusion.10), channel_id=1, source_target_pairs={{0,1},{1,0},{2,6},{3,7},{4,5},{5,4},{6,2},{7,3},{8,9},{9,8},{10,14... | collective-permute-start | bytes 3538952 | tf_op jit(solution)/shard_map/ppermute | solution.py:39
  78.4 30.6 %collective-permute-start.11 = (bf16[192,6144]{1,0:T(8,128)(2,1)S(1)}, bf16[192,6144]{1,0:T(8,128)(2,1)S(1)}, u32[]{:S(2)}, u32[]{:S(2)}) collective-permute-start(bf16[192,6144]{1,0:T(8,128)(2,1)S(1)} %pad_maximum_fusion.4), channel_id=1, source_target_pairs={{0,4},{1,5},{2,3},{3,2},{4,0},{5,1},{6,7},{7,6},{8,12},{9,13},{10,... | collective-permute-start | bytes 7077896 | tf_op jit(solution)/shard_map/ppermute | solution.py:39
  109.5 20.6 %collective-permute-start.13 = (bf16[384,6144]{1,0:T(8,128)(2,1)S(1)}, bf16[384,6144]{1,0:T(8,128)(2,1)S(1)}, u32[]{:S(2)}, u32[]{:S(2)}) collective-permute-start(bf16[384,6144]{1,0:T(8,128)(2,1)S(1)} %pad_maximum_fusion.up_ref.down_ref), channel_id=1, source_target_pairs={{0,2},{1,3},{2,0},{3,1},{4,6},{5,7},{6,4},{7,5},{8,10},{9,11},{10,... | collective-permute-start | bytes 14155784 | tf_op jit(solution)/shard_map/ppermute | solution.py:35
  109.6 16.3 %collective-permute-start.12 = (bf16[96,6144]{1,0:T(8,128)(2,1)S(1)}, bf16[96,6144]{1,0:T(8,128)(2,1)S(1)}, u32[]{:S(2)}, u32[]{:S(2)}) collective-permute-start(bf16[96,6144]{1,0:T(8,128)(2,1)S(1)} %pad_maximum_fusion.11), channel_id=1, source_target_pairs={{0,1},{1,0},{2,6},{3,7},{4,5},{5,4},{6,2},{7,3},{8,9},{9,8},{10,14... | collective-permute-start | bytes 3538952 | tf_op jit(solution)/shard_map/ppermute | solution.py:39
  126.0 30.9 %collective-permute-start.14 = (bf16[192,6144]{1,0:T(8,128)(2,1)S(1)}, bf16[192,6144]{1,0:T(8,128)(2,1)S(1)}, u32[]{:S(2)}, u32[]{:S(2)}) collective-permute-start(bf16[192,6144]{1,0:T(8,128)(2,1)S(1)} %pad_maximum_fusion.5), channel_id=1, source_target_pairs={{0,4},{1,5},{2,3},{3,2},{4,0},{5,1},{6,7},{7,6},{8,12},{9,13},{10,... | collective-permute-start | bytes 7077896 | tf_op jit(solution)/shard_map/ppermute | solution.py:39
  160.9 16.5 %collective-permute-start.17 = (bf16[96,6144]{1,0:T(8,128)(2,1)}, bf16[96,6144]{1,0:T(8,128)(2,1)}, u32[]{:S(2)}, u32[]{:S(2)}) collective-permute-start(bf16[96,6144]{1,0:T(8,128)(2,1)} %pad_maximum_fusion.12), channel_id=1, source_target_pairs={{0,1},{1,0},{2,6},{3,7},{4,5},{5,4},{6,2},{7,3},{8,9},{9,8},{10,14... | collective-permute-start | bytes 3538952 | tf_op jit(solution)/shard_map/ppermute | solution.py:39
  179.3 29.0 %collective-permute-start.18 = (bf16[192,6144]{1,0:T(8,128)(2,1)S(1)}, bf16[192,6144]{1,0:T(8,128)(2,1)}, u32[]{:S(2)}, u32[]{:S(2)}) collective-permute-start(bf16[192,6144]{1,0:T(8,128)(2,1)S(1)} %pad_maximum_fusion.6), channel_id=1, source_target_pairs={{0,4},{1,5},{2,3},{3,2},{4,0},{5,1},{6,7},{7,6},{8,12},{9,13},{10,... | collective-permute-start | bytes 7077896 | tf_op jit(solution)/shard_map/ppermute | solution.py:39
  241.2 29.1 %collective-permute-start.26 = (bf16[192,6144]{1,0:T(8,128)(2,1)}, bf16[192,6144]{1,0:T(8,128)(2,1)S(1)}, u32[]{:S(2)}, u32[]{:S(2)}) collective-permute-start(bf16[192,6144]{1,0:T(8,128)(2,1)} %get-tuple-element.429), channel_id=1, source_target_pairs={{0,4},{1,5},{2,3},{3,2},{4,0},{5,1},{6,7},{7,6},{8,12},{9,13},{10,... | collective-permute-start | bytes 7077896 | tf_op jit(solution)/shard_map/ppermute | solution.py:39
  277.9 41.5 %collective-permute-start.32 = (bf16[192,6144]{1,0:T(8,128)(2,1)S(1)}, bf16[192,6144]{1,0:T(8,128)(2,1)S(1)}, u32[]{:S(2)}, u32[]{:S(2)}) collective-permute-start(bf16[192,6144]{1,0:T(8,128)(2,1)S(1)} %get-tuple-element.476), channel_id=1, source_target_pairs={{0,4},{1,5},{2,3},{3,2},{4,0},{5,1},{6,7},{7,6},{8,12},{9,13},{10,... | collective-permute-start | bytes 7077896 | tf_op jit(solution)/shard_map/ppermute | solution.py:39
  286.3 29.0 %collective-permute-start.31 = (bf16[96,6144]{1,0:T(8,128)(2,1)S(1)}, bf16[96,6144]{1,0:T(8,128)(2,1)S(1)}, u32[]{:S(2)}, u32[]{:S(2)}) collective-permute-start(bf16[96,6144]{1,0:T(8,128)(2,1)S(1)} %get-tuple-element.468), channel_id=1, source_target_pairs={{0,1},{1,0},{2,6},{3,7},{4,5},{5,4},{6,2},{7,3},{8,9},{9,8},{10,14... | collective-permute-start | bytes 3538952 | tf_op jit(solution)/shard_map/ppermute | solution.py:39
  304.3 18.2 %collective-permute-start.33 = (bf16[5,128,768]{2,1,0:T(8,128)(2,1)S(1)}, bf16[5,128,768]{2,1,0:T(8,128)(2,1)S(1)}, u32[]{:S(2)}, u32[]{:S(2)}) collective-permute-start(bf16[5,128,768]{2,1,0:T(8,128)(2,1)S(1)} %get-tuple-element.486.sd_ref), channel_id=1, source_target_pairs={{0,2},{1,3},{2,0},{3,1},{4,6},{5,7},{6,4},{7,5},{8,10},{9,11},{10,... | collective-permute-start | bytes 2949128 | tf_op jit(solution)/shard_map/ppermute | solution.py:35
  320.5 28.9 %collective-permute-start.34 = (bf16[96,6144]{1,0:T(8,128)(2,1)S(1)}, bf16[96,6144]{1,0:T(8,128)(2,1)S(1)}, u32[]{:S(2)}, u32[]{:S(2)}) collective-permute-start(bf16[96,6144]{1,0:T(8,128)(2,1)S(1)} %get-tuple-element.495), channel_id=1, source_target_pairs={{0,1},{1,0},{2,6},{3,7},{4,5},{5,4},{6,2},{7,3},{8,9},{9,8},{10,14... | collective-permute-start | bytes 3538952 | tf_op jit(solution)/shard_map/ppermute | solution.py:39
  320.9 29.1 %collective-permute-start.35 = (bf16[48,6144]{1,0:T(8,128)(2,1)S(1)}, bf16[48,6144]{1,0:T(8,128)(2,1)S(1)}, u32[]{:S(2)}, u32[]{:S(2)}) collective-permute-start(bf16[48,6144]{1,0:T(8,128)(2,1)S(1)} %get-tuple-element.504), channel_id=1, source_target_pairs={{0,8},{1,9},{2,10},{3,11},{4,12},{5,13},{6,14},{7,15},{8,0},{9,1},... | collective-permute-start | bytes 1769480 | tf_op jit(solution)/shard_map/ppermute | solution.py:35
  320.9 39.7 %collective-permute-start.36 = (bf16[192,6144]{1,0:T(8,128)(2,1)S(1)}, bf16[192,6144]{1,0:T(8,128)(2,1)S(1)}, u32[]{:S(2)}, u32[]{:S(2)}) collective-permute-start(bf16[192,6144]{1,0:T(8,128)(2,1)S(1)} %get-tuple-element.510), channel_id=1, source_target_pairs={{0,4},{1,5},{2,3},{3,2},{4,0},{5,1},{6,7},{7,6},{8,12},{9,13},{10,... | collective-permute-start | bytes 7077896 | tf_op jit(solution)/shard_map/ppermute | solution.py:39
  350.0 19.3 %collective-permute-start.38 = (bf16[48,6144]{1,0:T(8,128)(2,1)S(1)}, bf16[48,6144]{1,0:T(8,128)(2,1)S(1)}, u32[]{:S(2)}, u32[]{:S(2)}) collective-permute-start(bf16[48,6144]{1,0:T(8,128)(2,1)S(1)} %get-tuple-element.524), channel_id=1, source_target_pairs={{0,8},{1,9},{2,10},{3,11},{4,12},{5,13},{6,14},{7,15},{8,0},{9,1},... | collective-permute-start | bytes 1769480 | tf_op jit(solution)/shard_map/ppermute | solution.py:35
  350.2 16.1 %collective-permute-start.37 = (bf16[24,6144]{1,0:T(8,128)(2,1)S(1)}, bf16[24,6144]{1,0:T(8,128)(2,1)S(1)}, u32[]{:S(2)}, u32[]{:S(2)}) collective-permute-start(bf16[24,6144]{1,0:T(8,128)(2,1)S(1)} %get-tuple-element.516), channel_id=1, source_target_pairs={{0,16},{1,17},{2,18},{3,19},{4,20},{5,21},{6,22},{7,23},{8,24},{9,... | collective-permute-start | bytes 884744 | tf_op jit(solution)/shard_map/ppermute | solution.py:35
  361.7 28.3 %collective-permute-start.39 = (bf16[96,6144]{1,0:T(8,128)(2,1)S(1)}, bf16[96,6144]{1,0:T(8,128)(2,1)S(1)}, u32[]{:S(2)}, u32[]{:S(2)}) collective-permute-start(bf16[96,6144]{1,0:T(8,128)(2,1)S(1)} %get-tuple-element.530), channel_id=1, source_target_pairs={{0,1},{1,0},{2,6},{3,7},{4,5},{5,4},{6,2},{7,3},{8,9},{9,8},{10,14... | collective-permute-start | bytes 3538952 | tf_op jit(solution)/shard_map/ppermute | solution.py:39
  362.0 28.8 %collective-permute-start.40 = (bf16[192,3200]{1,0:T(8,128)(2,1)S(1)}, bf16[192,3200]{1,0:T(8,128)(2,1)S(1)}, u32[]{:S(2)}, u32[]{:S(2)}) collective-permute-start(bf16[192,3200]{1,0:T(8,128)(2,1)S(1)} %pad_maximum_fusion.8), channel_id=1, source_target_pairs={{0,4},{1,5},{2,3},{3,2},{4,0},{5,1},{6,7},{7,6},{8,12},{9,13},{10,... | collective-permute-start | bytes 3686408 | tf_op jit(solution)/shard_map/ppermute | solution.py:39
  369.3 23.6 %collective-permute-start.41 = (bf16[24,6144]{1,0:T(8,128)(2,1)S(1)}, bf16[24,6144]{1,0:T(8,128)(2,1)S(1)}, u32[]{:S(2)}, u32[]{:S(2)}) collective-permute-start(bf16[24,6144]{1,0:T(8,128)(2,1)S(1)} %add_convert_fusion.3), channel_id=1, source_target_pairs={{0,16},{1,17},{2,18},{3,19},{4,20},{5,21},{6,22},{7,23},{8,24},{9,... | collective-permute-start | bytes 884744 | tf_op jit(solution)/shard_map/ppermute | solution.py:35
  392.9 15.3 %collective-permute-start.43 = (bf16[48,6144]{1,0:T(8,128)(2,1)S(1)}, bf16[48,6144]{1,0:T(8,128)(2,1)S(1)}, u32[]{:S(2)}, u32[]{:S(2)}) collective-permute-start(bf16[48,6144]{1,0:T(8,128)(2,1)S(1)} %get-tuple-element.551), channel_id=1, source_target_pairs={{0,8},{1,9},{2,10},{3,11},{4,12},{5,13},{6,14},{7,15},{8,0},{9,1},... | collective-permute-start | bytes 1769480 | tf_op jit(solution)/shard_map/ppermute | solution.py:35
  408.7 20.0 %collective-permute-start.45 = (bf16[24,6144]{1,0:T(8,128)(2,1)S(1)}, bf16[24,6144]{1,0:T(8,128)(2,1)S(1)}, u32[]{:S(2)}, u32[]{:S(2)}) collective-permute-start(bf16[24,6144]{1,0:T(8,128)(2,1)S(1)} %get-tuple-element.562), channel_id=1, source_target_pairs={{0,16},{1,17},{2,18},{3,19},{4,20},{5,21},{6,22},{7,23},{8,24},{9,... | collective-permute-start | bytes 884744 | tf_op jit(solution)/shard_map/ppermute | solution.py:35
  (63 other events, 661.5 us)

commit v15 on v14

--- a/solution.py
+++ b/solution.py
@@ -801,6 +801,12 @@
 
     vectors = (u_ag, u_as, u_mg, u_ms, m_ag, m_as, c_g, c_s, m_mg, m_ms)
     vectors = jnp.pad(jnp.stack(vectors, axis=0), ((0, LANES - len(vectors)), (0, 0)))
+    def core(x):
+        return place.swap(x, BIT_CORE)
+
+    def pairs(x):
+        return x, core(x)
+
     def packed(kernel, parts, *widths):
         outs = tuple(sds((rows, c), bf16) for c in widths)
         shards = call(kernel, 1, parts, [whole(p) for p in parts], outs, [whole(o) for o in outs], vmem=60)
@@ -851,20 +857,19 @@
     x0 = go(x0, [feed])
     x0a, f_us, k_us = net.self_forward(x0, w_first, 0, 0)
     x0a = go(x0a, [middle])
+    x0a = go(x0a, [last])
     x0a, w_feed = end(x0a, feed)
     x1, f_uf, k_uf = net.feed_forward(x0a, w_feed, 2)
-    x1 = go(x1, [middle, last])
+    x1 = go(x1, [last])
+    x1 = go(x1, [middle])
     x1, w_middle = end(x1, middle)
+    x1a, f_ms, k_ms = net.self_forward(x1, w_middle, 4, 4)
     kv = net.pair_forward(enc_rel, w_middle)
-    x1, (kv,) = tie(x1, kv)
-    x1 = go(x1, [last])
-    x1a, f_ms, k_ms = net.self_forward(x1, w_middle, 4, 4)
+    f_us, f_uf, f_ms = pairs(f_us), pairs(f_uf), pairs(f_ms)
+    x1a, (f_us, f_uf, f_ms, kv) = tie(x1a, f_us, f_uf, f_ms, kv)
+    x1a = go(x1a, [last])
     x1b, f_mc, k_mc = net.cross_forward(x1a, kv, w_middle, 2, 6)
-    x1b = go(x1b, [last])
     x1b, w_last = end(x1b, last)
-
-    def core(x):
-        return place.swap(x, BIT_CORE)
 
     def go_on(x, sums=(), start=()):
         x = hold(x, *sums)
@@ -881,11 +886,6 @@
                 x = go_on(x, [g], [g])
         return x
 
-    def pairs(x):
-        return x, core(x)
-
-    f_us, f_uf, f_ms = pairs(f_us), pairs(f_uf), pairs(f_ms)
-    x1b, (f_us, f_uf, f_ms) = tie(x1b, f_us, f_uf, f_ms)
     f_mc = pairs(f_mc)
     dx, v_mf, p, f = net.last_backward(x1b, out_grad.reshape(-1, d), w_last, 8)
     p, f = pairs(p), pairs(f)
@@ -935,8 +935,9 @@
     dx = rest(dx, s_ma)
     dx = go_on(dx, [s_uf, s_us], [s_uf, s_us])
     dx, (r_ma,) = tie(dx, s_ma.total())
+    dx = rest(dx, s_uf)
     dx = go_on(dx, [s_us], [s_us])
-    dx = rest(dx, s_uf, s_us)
+    dx = rest(dx, s_us)
     dx = hold(dx, s_uf)
     dx, (r_uf,) = tie(dx, feed_rows(s_uf.kept, s_uf.got))
     r_us = s_us.total()

time: 440 us -> 449 us (1.020)
  local copies, waits for them, and re-layouts: 13.6 us -> 35.1 us
  waiting for transfers between devices: 222 us -> 210 us
    unnamed x80 -> x110, local copies, waits for them, and re-layouts: 2.69 us -> 22.9 us
    ppermute x31, waiting for transfers between devices: 103 us -> 93.4 us  [swap(): return lax.ppermute(x, AXES, [(i, i ^ bit) for i in range(self.count)])]
    ppermute x16, starting transfers between devices: 24.6 us -> 29 us  [swap_by_core(): return lax.ppermute(x, AXES, pairs)]
  transfers between devices with their start and end apart: 47 -> 47, of which waited for: 31 -> 24; matrix products, arithmetic and copies ran while one was open for 4% -> 4% of each run, Pallas kernels for 26% -> 25%
where the time goes in v15:
time: 449 us; the launch traced here: 443 us
  waiting for transfers between devices  210 us (47%)
  Pallas kernels  132 us (29%)
  starting transfers between devices  47 us (10%)
  local copies, waits for them, and re-layouts  35.1 us (8%)
  other arithmetic  13 us (3%)
    pallas_call x29, Pallas kernels, call(): pl.pallas_call(kernel, out_shape=outs, grid_spec=pltpu.PrefetchScalarGrid...  132 us
    ppermute x16, waiting for transfers between devices, swap_by_core(): return lax.ppermute(x, AXES, pairs)  117 us
    ppermute x31, waiting for transfers between devices, swap(): return lax.ppermute(x, AXES, [(i, i ^ bit) for i in range(self.count)])  93.4 us
    ppermute x16, starting transfers between devices, swap_by_core(): return lax.ppermute(x, AXES, pairs)  29 us
    unnamed x110, local copies, waits for them, and re-layouts  22.9 us
    ppermute x31, starting transfers between devices, swap(): return lax.ppermute(x, AXES, [(i, i ^ bit) for i in range(self.count)])  18 us
    concatenate x16, other arithmetic, join(): self.x = jnp.concatenate((self.x, self.got), axis=0)  11.3 us
  transfers between devices with their start and end apart: 47, of which 24 were waited for; matrix products, arithmetic and copies ran while one was open for 4% of the time, Pallas kernels for 25%

profile of v15, /device:TPU:0, one launch (start us, length us, event | category | flops | bytes accessed | tf_op | source)
XLA Modules:
  0.0 443.3 jit_solution(10865254272623548039)
XLA Ops:
  21.3 10.5 %collective-permute-done.1 = bf16[48,3200]{1,0:T(8,128)(2,1)S(1)} collective-permute-done((bf16[48,3200]{1,0:T(8,128)(2,1)S(1)}, bf16[48,3200]{1,0:T(8,128)(2,1)S(1)}, u32[]{:S(2)}, u32[]{:S(2)}) %collective-permute-start.1) | collective-permute-done | bytes 307232 | tf_op jit(solution)/shard_map/ppermute | solution.py:35
  37.8 9.6 %collective-permute-done.3 = bf16[96,3200]{1,0:T(8,128)(2,1)S(1)} collective-permute-done((bf16[96,3200]{1,0:T(8,128)(2,1)S(1)}, bf16[96,3200]{1,0:T(8,128)(2,1)S(1)}, u32[]{:S(2)}, u32[]{:S(2)}) %collective-permute-start.3) | collective-permute-done | bytes 614432 | tf_op jit(solution)/shard_map/ppermute | solution.py:39
  54.4 10.2 %collective-permute-done.6 = bf16[24,6144]{1,0:T(8,128)(2,1)S(1)} collective-permute-done((bf16[24,6144]{1,0:T(8,128)(2,1)S(1)}, bf16[24,6144]{1,0:T(8,128)(2,1)S(1)}, u32[]{:S(2)}, u32[]{:S(2)}) %collective-permute-start.6) | collective-permute-done | bytes 294944 | tf_op jit(solution)/shard_map/ppermute | solution.py:35
  64.6 10.7 %collective-permute-done.5 = bf16[192,3200]{1,0:T(8,128)(2,1)S(1)} collective-permute-done((bf16[192,3200]{1,0:T(8,128)(2,1)S(1)}, bf16[192,3200]{1,0:T(8,128)(2,1)S(1)}, u32[]{:S(2)}, u32[]{:S(2)}) %collective-permute-start.5) | collective-permute-done | bytes 1228832 | tf_op jit(solution)/shard_map/ppermute | solution.py:39
  84.4 10.5 %collective-permute-done.9 = bf16[48,6144]{1,0:T(8,128)(2,1)S(1)} collective-permute-done((bf16[48,6144]{1,0:T(8,128)(2,1)S(1)}, bf16[48,6144]{1,0:T(8,128)(2,1)S(1)}, u32[]{:S(2)}, u32[]{:S(2)}) %collective-permute-start.9) | collective-permute-done | bytes 589856 | tf_op jit(solution)/shard_map/ppermute | solution.py:35
  95.1 13.8 %collective-permute-done.10 = bf16[24,6144]{1,0:T(8,128)(2,1)S(1)} collective-permute-done((bf16[24,6144]{1,0:T(8,128)(2,1)S(1)}, bf16[24,6144]{1,0:T(8,128)(2,1)S(1)}, u32[]{:S(2)}, u32[]{:S(2)}) %collective-permute-start.10) | collective-permute-done | bytes 294944 | tf_op jit(solution)/shard_map/ppermute | solution.py:35
  113.8 7.1 %shard_map.426 = (f32[128,768]{1,0:T(8,128)S(1)}, bf16[2,128,768]{2,1,0:T(8,128)(2,1)}, bf16[3,128,768]{2,1,0:T(8,128)(2,1)S(1)}) custom-call(bf16[128,768]{1,0:T(8,128)(2,1)S(1)} %bitcast.30, f32[16,768]{1,0:T(8,128)S(1)} %fusion.5.vec_ref, bf16[768,768]{1,0:T(8,128)(2,1)S(1)} %fusion.order_ref, bf16[384,3200]{1,0:T(8,128)(2,1)} %pad_maximum_fusion.3.top_ref, ...), custom_call_target="tpu_custom_call" | custom-call | flops 1000 | bytes 1000 | tf_op jit(solution)/shard_map/pallas_call | solution.py:603
  138.6 22.1 %collective-permute-done.15 = bf16[96,6144]{1,0:T(8,128)(2,1)S(1)} collective-permute-done((bf16[96,6144]{1,0:T(8,128)(2,1)S(1)}, bf16[96,6144]{1,0:T(8,128)(2,1)S(1)}, u32[]{:S(2)}, u32[]{:S(2)}) %collective-permute-start.15) | collective-permute-done | bytes 1179680 | tf_op jit(solution)/shard_map/ppermute | solution.py:39
  162.3 8.1 %collective-permute-done.16 = bf16[192,6144]{1,0:T(8,128)(2,1)S(1)} collective-permute-done((bf16[192,6144]{1,0:T(8,128)(2,1)S(1)}, bf16[192,6144]{1,0:T(8,128)(2,1)S(1)}, u32[]{:S(2)}, u32[]{:S(2)}) %collective-permute-start.16) | collective-permute-done | bytes 2359328 | tf_op jit(solution)/shard_map/ppermute | solution.py:39
  207.6 8.5 %shard_map.430 = (f32[128,768]{1,0:T(8,128)S(1)}, bf16[2,128,768]{2,1,0:T(8,128)(2,1)S(1)}, bf16[128,768]{1,0:T(8,128)(2,1)S(1)}) custom-call(s32[2]{0:T(128)S(1)} %copy-done.44, f32[128,768]{1,0:T(8,128)S(1)} %copy-done.23, f32[16,768]{1,0:T(8,128)S(1)} %fusion.5.vec_ref, bf16[768,768]{1,0:T(8,128)(2,1)S(1)} %fusion.order_ref, ...), custom_call_target="tpu_custom_call" | custom-call | flops 1000 | bytes 1000 | tf_op jit(solution)/shard_map/pallas_call | solution.py:603
  216.1 7.6 %shard_map.431 = (f32[128,768]{1,0:T(8,128)S(1)}, f32[8,768]{1,0:T(8,128)S(1)}, bf16[5,128,768]{2,1,0:T(8,128)(2,1)S(1)}, bf16[5,128,768]{2,1,0:T(8,128)(2,1)S(1)}) custom-call(f32[128,768]{1,0:T(8,128)S(1)} %get-tuple-element.408.x_ref, f32[16,768]{1,0:T(8,128)S(1)} %fusion.5.vec_ref, bf16[768,768]{1,0:T(8,128)(2,1)S(1)} %fusion.order_ref, ...), custom_call_target="tpu_custom_call" | custom-call | flops 1000 | bytes 1000 | tf_op jit(solution)/shard_map/pallas_call | solution.py:603
  238.0 10.2 %shard_map.434 = (f32[128,768]{1,0:T(8,128)S(1)}, f32[8,768]{1,0:T(8,128)S(1)}, bf16[2,128,768]{2,1,0:T(8,128)(2,1)S(1)}, bf16[1152,1536]{1,0:T(8,128)(2,1)S(1)}) custom-call(s32[2]{0:T(128)S(1)} %copy-done.44, f32[128,768]{1,0:T(8,128)S(1)} %copy-done.23, f32[16,768]{1,0:T(8,128)S(1)} %fusion.5.vec_ref, bf16[768,768]{1,0:T(8,128)(2,1)S(1)} %fusion.order_ref, ...), custom_call_target="tpu_custom_call" | custom-call | flops 1000 | bytes 1000 | tf_op jit(solution)/shard_map/pallas_call | solution.py:603
  252.2 8.4 %shard_map.436 = (f32[128,768]{1,0:T(8,128)S(1)}, f32[8,768]{1,0:T(8,128)S(1)}, bf16[4,128,768]{2,1,0:T(8,128)(2,1)S(1)}) custom-call(f32[128,768]{1,0:T(8,128)S(1)} %get-tuple-element.391.x_ref, f32[16,768]{1,0:T(8,128)S(1)} %fusion.5.vec_ref, bf16[768,768]{1,0:T(8,128)(2,1)S(1)} %fusion.order_ref, bf16[3,128,768]{2,1,0:T(8,128)(2,1)S(1)} %copy-done.32, ...), custom_call_target="tpu_custom_call" | custom-call | flops 1000 | bytes 1000 | tf_op jit(solution)/shard_map/pallas_call | solution.py:603
  275.1 8.3 %shard_map.438 = (bf16[192,6144]{1,0:T(8,128)(2,1)}, bf16[192,6144]{1,0:T(8,128)(2,1)S(1)}) custom-call(bf16[768,768]{1,0:T(8,128)(2,1)S(1)} %fusion.order_ref, bf16[2,128,768]{2,1,0:T(8,128)(2,1)} %get-tuple-element.442.s_ref, bf16[2,128,768]{2,1,0:T(8,128)(2,1)} %collective-permute-done.20.s2_ref, bf16[4,128,768]{2,1,0:T(8,128)(2,1)S(1)} %get-tuple-element.444.sd_ref, ...), custom_call_target="tpu_custom_call" | custom-call | flops 1000 | bytes 1000 | tf_op jit(solution)/shard_map/pallas_call | solution.py:603
  286.0 6.5 %shard_map.439 = (f32[128,768]{1,0:T(8,128)S(1)}, f32[8,768]{1,0:T(8,128)S(1)}, bf16[5,128,768]{2,1,0:T(8,128)(2,1)S(1)}) custom-call(f32[128,768]{1,0:T(8,128)S(1)} %copy-done.21, f32[16,768]{1,0:T(8,128)S(1)} %fusion.5.vec_ref, bf16[768,768]{1,0:T(8,128)(2,1)S(1)} %fusion.order_ref, f32[128,768]{1,0:T(8,128)S(1)} %copy-done.42, ...), custom_call_target="tpu_custom_call" | custom-call | flops 1000 | bytes 1000 | tf_op jit(solution)/shard_map/pallas_call | solution.py:603
  302.1 10.9 %shard_map.441 = (f32[128,768]{1,0:T(8,128)S(1)}, f32[8,768]{1,0:T(8,128)}, bf16[5,128,768]{2,1,0:T(8,128)(2,1)S(1)}) custom-call(bf16[128,768]{1,0:T(8,128)(2,1)S(1)} %bitcast.31, f32[16,768]{1,0:T(8,128)S(1)} %fusion.5.vec_ref, bf16[768,768]{1,0:T(8,128)(2,1)S(1)} %fusion.order_ref, bf16[3,128,768]{2,1,0:T(8,128)(2,1)S(1)} %copy-done.30, ...), custom_call_target="tpu_custom_call" | custom-call | flops 1000 | bytes 1000 | tf_op jit(solution)/shard_map/pallas_call | solution.py:603
  312.9 10.3 %collective-permute-done.31.got_ref = bf16[96,6144]{1,0:T(8,128)(2,1)S(1)} collective-permute-done((bf16[96,6144]{1,0:T(8,128)(2,1)S(1)}, bf16[96,6144]{1,0:T(8,128)(2,1)S(1)}, u32[]{:S(2)}, u32[]{:S(2)}) %collective-permute-start.31) | collective-permute-done | bytes 1179680 | tf_op jit(solution)/shard_map/ppermute | solution.py:39
  339.1 7.0 %shard_map.445 = bf16[1152,768]{1,0:T(8,128)(2,1)} custom-call(bf16[1152,1536]{1,0:T(8,128)(2,1)S(1)} %get-tuple-element.494.dkv_ref, bf16[768,768]{1,0:T(8,128)(2,1)S(1)} %fusion.order_ref, bf16[384,6144]{1,0:T(8,128)(2,1)S(1)} %bitcast.24, bf16[384,6144]{1,0:T(8,128)(2,1)S(1)} %copy-done.6), custom_call_target="tpu_custom_call" | custom-call | flops 1000 | bytes 1000 | tf_op jit(solution)/shard_map/pallas_call | solution.py:603
  346.2 12.2 %collective-permute-done.34.got_ref = bf16[96,6144]{1,0:T(8,128)(2,1)S(1)} collective-permute-done((bf16[96,6144]{1,0:T(8,128)(2,1)S(1)}, bf16[96,6144]{1,0:T(8,128)(2,1)S(1)}, u32[]{:S(2)}, u32[]{:S(2)}) %collective-permute-start.34) | collective-permute-done | bytes 1179680 | tf_op jit(solution)/shard_map/ppermute | solution.py:39
  359.8 9.0 %collective-permute-done.36.got_ref = bf16[192,6144]{1,0:T(8,128)(2,1)S(1)} collective-permute-done((bf16[192,6144]{1,0:T(8,128)(2,1)S(1)}, bf16[192,6144]{1,0:T(8,128)(2,1)S(1)}, u32[]{:S(2)}, u32[]{:S(2)}) %collective-permute-start.36) | collective-permute-done | bytes 2359328 | tf_op jit(solution)/shard_map/ppermute | solution.py:39
  378.0 19.6 %collective-permute-done.39.got_ref = bf16[96,6144]{1,0:T(8,128)(2,1)S(1)} collective-permute-done((bf16[96,6144]{1,0:T(8,128)(2,1)S(1)}, bf16[96,6144]{1,0:T(8,128)(2,1)S(1)}, u32[]{:S(2)}, u32[]{:S(2)}) %collective-permute-start.39) | collective-permute-done | bytes 1179680 | tf_op jit(solution)/shard_map/ppermute | solution.py:39
  402.4 13.2 %collective-permute-done.42 = bf16[48,6144]{1,0:T(8,128)(2,1)S(1)} collective-permute-done((bf16[48,6144]{1,0:T(8,128)(2,1)S(1)}, bf16[48,6144]{1,0:T(8,128)(2,1)S(1)}, u32[]{:S(2)}, u32[]{:S(2)}) %collective-permute-start.42) | collective-permute-done | bytes 589856 | tf_op jit(solution)/shard_map/ppermute | solution.py:35
  418.0 9.9 %collective-permute-done.44 = bf16[48,3200]{1,0:T(8,128)(2,1)S(1)} collective-permute-done((bf16[48,3200]{1,0:T(8,128)(2,1)S(1)}, bf16[48,3200]{1,0:T(8,128)(2,1)S(1)}, u32[]{:S(2)}, u32[]{:S(2)}) %collective-permute-start.44) | collective-permute-done | bytes 307232 | tf_op jit(solution)/shard_map/ppermute | solution.py:35
  428.7 8.1 %collective-permute-done.45.got_ref = bf16[24,6144]{1,0:T(8,128)(2,1)S(1)} collective-permute-done((bf16[24,6144]{1,0:T(8,128)(2,1)S(1)}, bf16[24,6144]{1,0:T(8,128)(2,1)S(1)}, u32[]{:S(2)}, u32[]{:S(2)}) %collective-permute-start.45) | collective-permute-done | bytes 294944 | tf_op jit(solution)/shard_map/ppermute | solution.py:35
  (259 shorter events, 189.2 us)
Async XLA Ops:
  18.0 16.8 %collective-permute-start.2 = (bf16[24,6144]{1,0:T(8,128)(2,1)}, bf16[24,6144]{1,0:T(8,128)(2,1)S(1)}, u32[]{:S(2)}, u32[]{:S(2)}) collective-permute-start(bf16[24,6144]{1,0:T(8,128)(2,1)} %get-tuple-element.315), channel_id=1, source_target_pairs={{0,16},{1,17},{2,18},{3,19},{4,20},{5,21},{6,22},{7,23},{8,24},{9,... | collective-permute-start | bytes 884744 | tf_op jit(solution)/shard_map/ppermute | solution.py:35
  47.4 27.8 %collective-permute-start.5 = (bf16[192,3200]{1,0:T(8,128)(2,1)S(1)}, bf16[192,3200]{1,0:T(8,128)(2,1)S(1)}, u32[]{:S(2)}, u32[]{:S(2)}) collective-permute-start(bf16[192,3200]{1,0:T(8,128)(2,1)S(1)} %pad_maximum_fusion.7), channel_id=1, source_target_pairs={{0,4},{1,5},{2,3},{3,2},{4,0},{5,1},{6,7},{7,6},{8,12},{9,13},{10,... | collective-permute-start | bytes 3686408 | tf_op jit(solution)/shard_map/ppermute | solution.py:39
  52.9 24.1 %collective-permute-start.7 = (bf16[96,6144]{1,0:T(8,128)(2,1)S(1)}, bf16[96,6144]{1,0:T(8,128)(2,1)}, u32[]{:S(2)}, u32[]{:S(2)}) collective-permute-start(bf16[96,6144]{1,0:T(8,128)(2,1)S(1)} %pad_maximum_fusion.10), channel_id=1, source_target_pairs={{0,1},{1,0},{2,6},{3,7},{4,5},{5,4},{6,2},{7,3},{8,9},{9,8},{10,14... | collective-permute-start | bytes 3538952 | tf_op jit(solution)/shard_map/ppermute | solution.py:39
  78.5 30.4 %collective-permute-start.11 = (bf16[192,6144]{1,0:T(8,128)(2,1)S(1)}, bf16[192,6144]{1,0:T(8,128)(2,1)S(1)}, u32[]{:S(2)}, u32[]{:S(2)}) collective-permute-start(bf16[192,6144]{1,0:T(8,128)(2,1)S(1)} %pad_maximum_fusion.4), channel_id=1, source_target_pairs={{0,4},{1,5},{2,3},{3,2},{4,0},{5,1},{6,7},{7,6},{8,12},{9,13},{10,... | collective-permute-start | bytes 7077896 | tf_op jit(solution)/shard_map/ppermute | solution.py:39
  109.5 22.7 %collective-permute-start.14 = (bf16[384,6144]{1,0:T(8,128)(2,1)S(1)}, bf16[384,6144]{1,0:T(8,128)(2,1)S(1)}, u32[]{:S(2)}, u32[]{:S(2)}) collective-permute-start(bf16[384,6144]{1,0:T(8,128)(2,1)S(1)} %pad_maximum_fusion.up_ref.down_ref), channel_id=1, source_target_pairs={{0,2},{1,3},{2,0},{3,1},{4,6},{5,7},{6,4},{7,5},{8,10},{9,11},{10,... | collective-permute-start | bytes 14155784 | tf_op jit(solution)/shard_map/ppermute | solution.py:35
  109.5 16.3 %collective-permute-start.12 = (bf16[96,6144]{1,0:T(8,128)(2,1)S(1)}, bf16[96,6144]{1,0:T(8,128)(2,1)S(1)}, u32[]{:S(2)}, u32[]{:S(2)}) collective-permute-start(bf16[96,6144]{1,0:T(8,128)(2,1)S(1)} %pad_maximum_fusion.11), channel_id=1, source_target_pairs={{0,1},{1,0},{2,6},{3,7},{4,5},{5,4},{6,2},{7,3},{8,9},{9,8},{10,14... | collective-permute-start | bytes 3538952 | tf_op jit(solution)/shard_map/ppermute | solution.py:39
  128.7 41.8 %collective-permute-start.16 = (bf16[192,6144]{1,0:T(8,128)(2,1)S(1)}, bf16[192,6144]{1,0:T(8,128)(2,1)S(1)}, u32[]{:S(2)}, u32[]{:S(2)}) collective-permute-start(bf16[192,6144]{1,0:T(8,128)(2,1)S(1)} %pad_maximum_fusion.5), channel_id=1, source_target_pairs={{0,4},{1,5},{2,3},{3,2},{4,0},{5,1},{6,7},{7,6},{8,12},{9,13},{10,... | collective-permute-start | bytes 7077896 | tf_op jit(solution)/shard_map/ppermute | solution.py:39
  131.8 29.0 %collective-permute-start.15 = (bf16[96,6144]{1,0:T(8,128)(2,1)S(1)}, bf16[96,6144]{1,0:T(8,128)(2,1)S(1)}, u32[]{:S(2)}, u32[]{:S(2)}) collective-permute-start(bf16[96,6144]{1,0:T(8,128)(2,1)S(1)} %pad_maximum_fusion.12), channel_id=1, source_target_pairs={{0,1},{1,0},{2,6},{3,7},{4,5},{5,4},{6,2},{7,3},{8,9},{9,8},{10,14... | collective-permute-start | bytes 3538952 | tf_op jit(solution)/shard_map/ppermute | solution.py:39
  171.1 30.7 %collective-permute-start.21 = (bf16[192,6144]{1,0:T(8,128)(2,1)}, bf16[192,6144]{1,0:T(8,128)(2,1)}, u32[]{:S(2)}, u32[]{:S(2)}) collective-permute-start(bf16[192,6144]{1,0:T(8,128)(2,1)} %pad_maximum_fusion.6), channel_id=1, source_target_pairs={{0,4},{1,5},{2,3},{3,2},{4,0},{5,1},{6,7},{7,6},{8,12},{9,13},{10,... | collective-permute-start | bytes 7077896 | tf_op jit(solution)/shard_map/ppermute | solution.py:39
  172.2 29.5 %collective-permute-start.19 = (bf16[5,128,768]{2,1,0:T(8,128)(2,1)S(1)}, bf16[5,128,768]{2,1,0:T(8,128)(2,1)}, u32[]{:S(2)}, u32[]{:S(2)}) collective-permute-start(bf16[5,128,768]{2,1,0:T(8,128)(2,1)S(1)} %get-tuple-element.458.b_ref.g_ref), channel_id=1, source_target_pairs={{0,2},{1,3},{2,0},{3,1},{4,6},{5,7},{6,4},{7,5},{8,10},{9,11},{10,... | collective-permute-start | bytes 2949128 | tf_op jit(solution)/shard_map/ppermute | solution.py:35
  172.3 29.4 %collective-permute-start.18 = (bf16[2,128,768]{2,1,0:T(8,128)(2,1)}, bf16[2,128,768]{2,1,0:T(8,128)(2,1)}, u32[]{:S(2)}, u32[]{:S(2)}) collective-permute-start(bf16[2,128,768]{2,1,0:T(8,128)(2,1)} %get-tuple-element.486.s_ref), channel_id=1, source_target_pairs={{0,2},{1,3},{2,0},{3,1},{4,6},{5,7},{6,4},{7,5},{8,10},{9,11},{10,... | collective-permute-start | bytes 1179656 | tf_op jit(solution)/shard_map/ppermute | solution.py:35
  236.9 29.1 %collective-permute-start.26 = (bf16[192,6144]{1,0:T(8,128)(2,1)}, bf16[192,6144]{1,0:T(8,128)(2,1)S(1)}, u32[]{:S(2)}, u32[]{:S(2)}) collective-permute-start(bf16[192,6144]{1,0:T(8,128)(2,1)} %get-tuple-element.431), channel_id=1, source_target_pairs={{0,4},{1,5},{2,3},{3,2},{4,0},{5,1},{6,7},{7,6},{8,12},{9,13},{10,... | collective-permute-start | bytes 7077896 | tf_op jit(solution)/shard_map/ppermute | solution.py:39
  252.1 18.9 %collective-permute-start.29 = (bf16[384,1536]{1,0:T(8,128)(2,1)S(1)}, bf16[384,1536]{1,0:T(8,128)(2,1)S(1)}, u32[]{:S(2)}, u32[]{:S(2)}) collective-permute-start(bf16[384,1536]{1,0:T(8,128)(2,1)S(1)} %get-tuple-element.440), channel_id=1, source_target_pairs={{0,2},{1,3},{2,0},{3,1},{4,6},{5,7},{6,4},{7,5},{8,10},{9,11},{10,... | collective-permute-start | bytes 3538952 | tf_op jit(solution)/shard_map/ppermute | solution.py:35
  284.8 41.8 %collective-permute-start.32 = (bf16[192,6144]{1,0:T(8,128)(2,1)}, bf16[192,6144]{1,0:T(8,128)(2,1)}, u32[]{:S(2)}, u32[]{:S(2)}) collective-permute-start(bf16[192,6144]{1,0:T(8,128)(2,1)} %get-tuple-element.478), channel_id=1, source_target_pairs={{0,4},{1,5},{2,3},{3,2},{4,0},{5,1},{6,7},{7,6},{8,12},{9,13},{10,... | collective-permute-start | bytes 7077896 | tf_op jit(solution)/shard_map/ppermute | solution.py:39
  292.6 30.7 %collective-permute-start.31 = (bf16[96,6144]{1,0:T(8,128)(2,1)S(1)}, bf16[96,6144]{1,0:T(8,128)(2,1)S(1)}, u32[]{:S(2)}, u32[]{:S(2)}) collective-permute-start(bf16[96,6144]{1,0:T(8,128)(2,1)S(1)} %copy-done.46), channel_id=1, source_target_pairs={{0,1},{1,0},{2,6},{3,7},{4,5},{5,4},{6,2},{7,3},{8,9},{9,8},{10,14... | collective-permute-start | bytes 3538952 | tf_op jit(solution)/shard_map/ppermute | solution.py:39
  312.9 21.1 %collective-permute-start.33 = (bf16[5,128,768]{2,1,0:T(8,128)(2,1)S(1)}, bf16[5,128,768]{2,1,0:T(8,128)(2,1)S(1)}, u32[]{:S(2)}, u32[]{:S(2)}) collective-permute-start(bf16[5,128,768]{2,1,0:T(8,128)(2,1)S(1)} %get-tuple-element.488.sd_ref), channel_id=1, source_target_pairs={{0,2},{1,3},{2,0},{3,1},{4,6},{5,7},{6,4},{7,5},{8,10},{9,11},{10,... | collective-permute-start | bytes 2949128 | tf_op jit(solution)/shard_map/ppermute | solution.py:35
  328.7 29.7 %collective-permute-start.34 = (bf16[96,6144]{1,0:T(8,128)(2,1)S(1)}, bf16[96,6144]{1,0:T(8,128)(2,1)S(1)}, u32[]{:S(2)}, u32[]{:S(2)}) collective-permute-start(bf16[96,6144]{1,0:T(8,128)(2,1)S(1)} %get-tuple-element.497), channel_id=1, source_target_pairs={{0,1},{1,0},{2,6},{3,7},{4,5},{5,4},{6,2},{7,3},{8,9},{9,8},{10,14... | collective-permute-start | bytes 3538952 | tf_op jit(solution)/shard_map/ppermute | solution.py:39
  331.6 27.4 %collective-permute-start.35 = (bf16[48,6144]{1,0:T(8,128)(2,1)S(1)}, bf16[48,6144]{1,0:T(8,128)(2,1)S(1)}, u32[]{:S(2)}, u32[]{:S(2)}) collective-permute-start(bf16[48,6144]{1,0:T(8,128)(2,1)S(1)} %get-tuple-element.506), channel_id=1, source_target_pairs={{0,8},{1,9},{2,10},{3,11},{4,12},{5,13},{6,14},{7,15},{8,0},{9,1},... | collective-permute-start | bytes 1769480 | tf_op jit(solution)/shard_map/ppermute | solution.py:35
  332.0 36.7 %collective-permute-start.36 = (bf16[192,6144]{1,0:T(8,128)(2,1)S(1)}, bf16[192,6144]{1,0:T(8,128)(2,1)S(1)}, u32[]{:S(2)}, u32[]{:S(2)}) collective-permute-start(bf16[192,6144]{1,0:T(8,128)(2,1)S(1)} %get-tuple-element.512), channel_id=1, source_target_pairs={{0,4},{1,5},{2,3},{3,2},{4,0},{5,1},{6,7},{7,6},{8,12},{9,13},{10,... | collective-permute-start | bytes 7077896 | tf_op jit(solution)/shard_map/ppermute | solution.py:39
  359.0 17.7 %collective-permute-start.38 = (bf16[48,6144]{1,0:T(8,128)(2,1)S(1)}, bf16[48,6144]{1,0:T(8,128)(2,1)S(1)}, u32[]{:S(2)}, u32[]{:S(2)}) collective-permute-start(bf16[48,6144]{1,0:T(8,128)(2,1)S(1)} %get-tuple-element.526), channel_id=1, source_target_pairs={{0,8},{1,9},{2,10},{3,11},{4,12},{5,13},{6,14},{7,15},{8,0},{9,1},... | collective-permute-start | bytes 1769480 | tf_op jit(solution)/shard_map/ppermute | solution.py:35
  369.8 27.8 %collective-permute-start.39 = (bf16[96,6144]{1,0:T(8,128)(2,1)S(1)}, bf16[96,6144]{1,0:T(8,128)(2,1)S(1)}, u32[]{:S(2)}, u32[]{:S(2)}) collective-permute-start(bf16[96,6144]{1,0:T(8,128)(2,1)S(1)} %get-tuple-element.532), channel_id=1, source_target_pairs={{0,1},{1,0},{2,6},{3,7},{4,5},{5,4},{6,2},{7,3},{8,9},{9,8},{10,14... | collective-permute-start | bytes 3538952 | tf_op jit(solution)/shard_map/ppermute | solution.py:39
  371.9 28.4 %collective-permute-start.40 = (bf16[192,3200]{1,0:T(8,128)(2,1)S(1)}, bf16[192,3200]{1,0:T(8,128)(2,1)S(1)}, u32[]{:S(2)}, u32[]{:S(2)}) collective-permute-start(bf16[192,3200]{1,0:T(8,128)(2,1)S(1)} %pad_maximum_fusion.8), channel_id=1, source_target_pairs={{0,4},{1,5},{2,3},{3,2},{4,0},{5,1},{6,7},{7,6},{8,12},{9,13},{10,... | collective-permute-start | bytes 3686408 | tf_op jit(solution)/shard_map/ppermute | solution.py:39
  376.7 25.1 %collective-permute-start.41 = (bf16[24,6144]{1,0:T(8,128)(2,1)S(1)}, bf16[24,6144]{1,0:T(8,128)(2,1)S(1)}, u32[]{:S(2)}, u32[]{:S(2)}) collective-permute-start(bf16[24,6144]{1,0:T(8,128)(2,1)S(1)} %add_convert_fusion.3), channel_id=1, source_target_pairs={{0,16},{1,17},{2,18},{3,19},{4,20},{5,21},{6,22},{7,23},{8,24},{9,... | collective-permute-start | bytes 884744 | tf_op jit(solution)/shard_map/ppermute | solution.py:35
  417.9 19.0 %collective-permute-start.45 = (bf16[24,6144]{1,0:T(8,128)(2,1)S(1)}, bf16[24,6144]{1,0:T(8,128)(2,1)S(1)}, u32[]{:S(2)}, u32[]{:S(2)}) collective-permute-start(bf16[24,6144]{1,0:T(8,128)(2,1)S(1)} %get-tuple-element.564), channel_id=1, source_target_pairs={{0,16},{1,17},{2,18},{3,19},{4,20},{5,21},{6,22},{7,23},{8,24},{9,... | collective-permute-start | bytes 884744 | tf_op jit(solution)/shard_map/ppermute | solution.py:35
  (78 other events, 813.5 us)

commit v16 on v14

--- a/solution.py
+++ b/solution.py
@@ -851,14 +851,14 @@
     x0 = go(x0, [feed])
     x0a, f_us, k_us = net.self_forward(x0, w_first, 0, 0)
     x0a = go(x0a, [middle])
+    x0a = go(x0a, [last])
     x0a, w_feed = end(x0a, feed)
     x1, f_uf, k_uf = net.feed_forward(x0a, w_feed, 2)
-    x1 = go(x1, [middle, last])
+    x1 = go(x1, [last])
+    x1 = go(x1, [middle])
     x1, w_middle = end(x1, middle)
+    x1a, f_ms, k_ms = net.self_forward(x1, w_middle, 4, 4)
     kv = net.pair_forward(enc_rel, w_middle)
-    x1, (kv,) = tie(x1, kv)
-    x1 = go(x1, [last])
-    x1a, f_ms, k_ms = net.self_forward(x1, w_middle, 4, 4)
     x1b, f_mc, k_mc = net.cross_forward(x1a, kv, w_middle, 2, 6)
     x1b = go(x1b, [last])
     x1b, w_last = end(x1b, last)
@@ -930,13 +930,13 @@
     dx = go_on(dx, start=[s_us])
     dx = rest(dx, s_mf)
     dx = go_on(dx, [s_uf], [s_uf])
-    dx = hold(dx, s_mf)
     dx, (r_mf,) = tie(dx, feed_rows(s_mf.kept, s_mf.got))
     dx = rest(dx, s_ma)
     dx = go_on(dx, [s_uf, s_us], [s_uf, s_us])
     dx, (r_ma,) = tie(dx, s_ma.total())
+    dx = rest(dx, s_uf)
     dx = go_on(dx, [s_us], [s_us])
-    dx = rest(dx, s_uf, s_us)
+    dx = rest(dx, s_us)
     dx = hold(dx, s_uf)
     dx, (r_uf,) = tie(dx, feed_rows(s_uf.kept, s_uf.got))
     r_us = s_us.total()

time: 440 us -> 430 us (0.977)
  waiting for transfers between devices: 222 us -> 210 us
    ppermute x16, waiting for transfers between devices: 119 us -> 110 us  [swap_by_core(): return lax.ppermute(x, AXES, pairs)]
  transfers between devices with their start and end apart: 47 -> 47, of which waited for: 31 -> 27; matrix products, arithmetic and copies ran while one was open for 4% -> 4% of each run, Pallas kernels for 26% -> 27%
where the time goes in v16:
time: 430 us; the launch traced here: 424 us
  waiting for transfers between devices  210 us (49%)
  Pallas kernels  134 us (31%)
  starting transfers between devices  46 us (11%)
  other arithmetic  15.3 us (4%)
  local copies, waits for them, and re-layouts  13.8 us (3%)
    pallas_call x29, Pallas kernels, call(): pl.pallas_call(kernel, out_shape=outs, grid_spec=pltpu.PrefetchScalarGrid...  134 us
    ppermute x16, waiting for transfers between devices, swap_by_core(): return lax.ppermute(x, AXES, pairs)  110 us
    ppermute x31, waiting for transfers between devices, swap(): return lax.ppermute(x, AXES, [(i, i ^ bit) for i in range(self.count)])  99.8 us
    ppermute x16, starting transfers between devices, swap_by_core(): return lax.ppermute(x, AXES, pairs)  24.6 us
    ppermute x31, starting transfers between devices, swap(): return lax.ppermute(x, AXES, [(i, i ^ bit) for i in range(self.count)])  21.4 us
    concatenate x16, other arithmetic, join(): self.x = jnp.concatenate((self.x, self.got), axis=0)  13.6 us
  transfers between devices with their start and end apart: 47, of which 27 were waited for; matrix products, arithmetic and copies ran while one was open for 4% of the time, Pallas kernels for 27%

profile of v16, /device:TPU:0, one launch (start us, length us, event | category | flops | bytes accessed | tf_op | source)
XLA Modules:
  0.0 424.4 jit_solution(13884550762730055396)
XLA Ops:
  21.3 10.5 %collective-permute-done.1 = bf16[48,3200]{1,0:T(8,128)(2,1)S(1)} collective-permute-done((bf16[48,3200]{1,0:T(8,128)(2,1)S(1)}, bf16[48,3200]{1,0:T(8,128)(2,1)S(1)}, u32[]{:S(2)}, u32[]{:S(2)}) %collective-permute-start.1) | collective-permute-done | bytes 307232 | tf_op jit(solution)/shard_map/ppermute | solution.py:35
  37.8 9.6 %collective-permute-done.3 = bf16[96,3200]{1,0:T(8,128)(2,1)S(1)} collective-permute-done((bf16[96,3200]{1,0:T(8,128)(2,1)S(1)}, bf16[96,3200]{1,0:T(8,128)(2,1)S(1)}, u32[]{:S(2)}, u32[]{:S(2)}) %collective-permute-start.3) | collective-permute-done | bytes 614432 | tf_op jit(solution)/shard_map/ppermute | solution.py:39
  54.4 10.2 %collective-permute-done.6 = bf16[24,6144]{1,0:T(8,128)(2,1)S(1)} collective-permute-done((bf16[24,6144]{1,0:T(8,128)(2,1)S(1)}, bf16[24,6144]{1,0:T(8,128)(2,1)S(1)}, u32[]{:S(2)}, u32[]{:S(2)}) %collective-permute-start.6) | collective-permute-done | bytes 294944 | tf_op jit(solution)/shard_map/ppermute | solution.py:35
  64.6 10.7 %collective-permute-done.5 = bf16[192,3200]{1,0:T(8,128)(2,1)S(1)} collective-permute-done((bf16[192,3200]{1,0:T(8,128)(2,1)S(1)}, bf16[192,3200]{1,0:T(8,128)(2,1)S(1)}, u32[]{:S(2)}, u32[]{:S(2)}) %collective-permute-start.5) | collective-permute-done | bytes 1228832 | tf_op jit(solution)/shard_map/ppermute | solution.py:39
  84.4 10.5 %collective-permute-done.9 = bf16[48,6144]{1,0:T(8,128)(2,1)S(1)} collective-permute-done((bf16[48,6144]{1,0:T(8,128)(2,1)S(1)}, bf16[48,6144]{1,0:T(8,128)(2,1)S(1)}, u32[]{:S(2)}, u32[]{:S(2)}) %collective-permute-start.9) | collective-permute-done | bytes 589856 | tf_op jit(solution)/shard_map/ppermute | solution.py:35
  95.1 13.8 %collective-permute-done.10 = bf16[24,6144]{1,0:T(8,128)(2,1)S(1)} collective-permute-done((bf16[24,6144]{1,0:T(8,128)(2,1)S(1)}, bf16[24,6144]{1,0:T(8,128)(2,1)S(1)}, u32[]{:S(2)}, u32[]{:S(2)}) %collective-permute-start.10) | collective-permute-done | bytes 294944 | tf_op jit(solution)/shard_map/ppermute | solution.py:35
  113.7 6.6 %shard_map.426 = (f32[128,768]{1,0:T(8,128)S(1)}, bf16[2,128,768]{2,1,0:T(8,128)(2,1)S(1)}, bf16[3,128,768]{2,1,0:T(8,128)(2,1)S(1)}) custom-call(bf16[128,768]{1,0:T(8,128)(2,1)S(1)} %bitcast.28, f32[16,768]{1,0:T(8,128)S(1)} %fusion.5.vec_ref, bf16[768,768]{1,0:T(8,128)(2,1)S(1)} %fusion.order_ref, bf16[384,3200]{1,0:T(8,128)(2,1)} %pad_maximum_fusion.3.top_ref, ...), custom_call_target="tpu_custom_call" | custom-call | flops 1000 | bytes 1000 | tf_op jit(solution)/shard_map/pallas_call | solution.py:603
  139.5 21.2 %collective-permute-done.15 = bf16[96,6144]{1,0:T(8,128)(2,1)S(1)} collective-permute-done((bf16[96,6144]{1,0:T(8,128)(2,1)S(1)}, bf16[96,6144]{1,0:T(8,128)(2,1)S(1)}, u32[]{:S(2)}, u32[]{:S(2)}) %collective-permute-start.15) | collective-permute-done | bytes 1179680 | tf_op jit(solution)/shard_map/ppermute | solution.py:39
  162.3 8.1 %collective-permute-done.16 = bf16[192,6144]{1,0:T(8,128)(2,1)S(1)} collective-permute-done((bf16[192,6144]{1,0:T(8,128)(2,1)S(1)}, bf16[192,6144]{1,0:T(8,128)(2,1)S(1)}, u32[]{:S(2)}, u32[]{:S(2)}) %collective-permute-start.16) | collective-permute-done | bytes 2359328 | tf_op jit(solution)/shard_map/ppermute | solution.py:39
  193.2 9.2 %shard_map.430 = (f32[128,768]{1,0:T(8,128)S(1)}, bf16[2,128,768]{2,1,0:T(8,128)(2,1)S(1)}, bf16[128,768]{1,0:T(8,128)(2,1)S(1)}) custom-call(s32[2]{0:T(128)S(1)} %copy-done.33, f32[128,768]{1,0:T(8,128)S(1)} %get-tuple-element.390.x_ref, f32[16,768]{1,0:T(8,128)S(1)} %fusion.5.vec_ref, bf16[768,768]{1,0:T(8,128)(2,1)S(1)} %fusion.order_ref, ...), custom_call_target="tpu_custom_call" | custom-call | flops 1000 | bytes 1000 | tf_op jit(solution)/shard_map/pallas_call | solution.py:603
  206.6 6.9 %collective-permute-done.19.up2_ref.down2_ref = bf16[384,6144]{1,0:T(8,128)(2,1)S(1)} collective-permute-done((bf16[384,6144]{1,0:T(8,128)(2,1)S(1)}, bf16[384,6144]{1,0:T(8,128)(2,1)S(1)}, u32[]{:S(2)}, u32[]{:S(2)}) %collective-permute-start.19) | collective-permute-done | bytes 4718624 | tf_op jit(solution)/shard_map/ppermute | solution.py:35
  216.3 7.6 %shard_map.431 = (f32[128,768]{1,0:T(8,128)S(1)}, f32[8,768]{1,0:T(8,128)S(1)}, bf16[5,128,768]{2,1,0:T(8,128)(2,1)S(1)}, bf16[5,128,768]{2,1,0:T(8,128)(2,1)S(1)}) custom-call(f32[128,768]{1,0:T(8,128)S(1)} %get-tuple-element.403.x_ref, f32[16,768]{1,0:T(8,128)S(1)} %fusion.5.vec_ref, bf16[768,768]{1,0:T(8,128)(2,1)S(1)} %fusion.order_ref, ...), custom_call_target="tpu_custom_call" | custom-call | flops 1000 | bytes 1000 | tf_op jit(solution)/shard_map/pallas_call | solution.py:603
  237.3 11.1 %shard_map.434 = (f32[128,768]{1,0:T(8,128)S(1)}, f32[8,768]{1,0:T(8,128)S(1)}, bf16[2,128,768]{2,1,0:T(8,128)(2,1)S(1)}, bf16[1152,1536]{1,0:T(8,128)(2,1)S(1)}) custom-call(s32[2]{0:T(128)S(1)} %copy-done.33, f32[128,768]{1,0:T(8,128)S(1)} %copy-done.12, f32[16,768]{1,0:T(8,128)S(1)} %fusion.5.vec_ref, bf16[768,768]{1,0:T(8,128)(2,1)S(1)} %fusion.order_ref, ...), custom_call_target="tpu_custom_call" | custom-call | flops 1000 | bytes 1000 | tf_op jit(solution)/shard_map/pallas_call | solution.py:603
  252.6 10.3 %shard_map.436 = (f32[128,768]{1,0:T(8,128)S(1)}, f32[8,768]{1,0:T(8,128)S(1)}, bf16[4,128,768]{2,1,0:T(8,128)(2,1)S(1)}) custom-call(f32[128,768]{1,0:T(8,128)S(1)} %get-tuple-element.387.x_ref, f32[16,768]{1,0:T(8,128)S(1)} %fusion.5.vec_ref, bf16[768,768]{1,0:T(8,128)(2,1)S(1)} %fusion.order_ref, bf16[3,128,768]{2,1,0:T(8,128)(2,1)S(1)} %copy-done.18, ...), custom_call_target="tpu_custom_call" | custom-call | flops 1000 | bytes 1000 | tf_op jit(solution)/shard_map/pallas_call | solution.py:603
  273.8 6.5 %shard_map.439 = (f32[128,768]{1,0:T(8,128)S(1)}, f32[8,768]{1,0:T(8,128)S(1)}, bf16[5,128,768]{2,1,0:T(8,128)(2,1)S(1)}) custom-call(f32[128,768]{1,0:T(8,128)S(1)} %copy-done.10, f32[16,768]{1,0:T(8,128)S(1)} %fusion.5.vec_ref, bf16[768,768]{1,0:T(8,128)(2,1)S(1)} %fusion.order_ref, f32[128,768]{1,0:T(8,128)S(1)} %get-tuple-element.448.dx_ref, ...), custom_call_target="tpu_custom_call" | custom-call | flops 1000 | bytes 1000 | tf_op jit(solution)/shard_map/pallas_call | solution.py:603
  287.4 11.0 %shard_map.441 = (f32[128,768]{1,0:T(8,128)S(1)}, f32[8,768]{1,0:T(8,128)}, bf16[5,128,768]{2,1,0:T(8,128)(2,1)S(1)}) custom-call(bf16[128,768]{1,0:T(8,128)(2,1)S(1)} %bitcast.29, f32[16,768]{1,0:T(8,128)S(1)} %fusion.5.vec_ref, bf16[768,768]{1,0:T(8,128)(2,1)S(1)} %fusion.order_ref, bf16[3,128,768]{2,1,0:T(8,128)(2,1)S(1)} %copy-done.16, ...), custom_call_target="tpu_custom_call" | custom-call | flops 1000 | bytes 1000 | tf_op jit(solution)/shard_map/pallas_call | solution.py:603
  298.6 10.8 %collective-permute-done.31.got_ref = bf16[96,6144]{1,0:T(8,128)(2,1)S(1)} collective-permute-done((bf16[96,6144]{1,0:T(8,128)(2,1)S(1)}, bf16[96,6144]{1,0:T(8,128)(2,1)S(1)}, u32[]{:S(2)}, u32[]{:S(2)}) %collective-permute-start.31) | collective-permute-done | bytes 1179680 | tf_op jit(solution)/shard_map/ppermute | solution.py:39
  322.5 8.2 %shard_map.445 = bf16[1152,768]{1,0:T(8,128)(2,1)} custom-call(bf16[1152,1536]{1,0:T(8,128)(2,1)S(1)} %get-tuple-element.489.dkv_ref, bf16[768,768]{1,0:T(8,128)(2,1)S(1)} %fusion.order_ref, bf16[384,6144]{1,0:T(8,128)(2,1)} %pad_maximum_fusion.1.top_ref, bf16[384,6144]{1,0:T(8,128)(2,1)} %collective-permute-done.17.low_ref), custom_call_target="tpu_custom_call" | custom-call | flops 1000 | bytes 1000 | tf_op jit(solution)/shard_map/pallas_call | solution.py:603
  330.8 13.4 %collective-permute-done.34.got_ref = bf16[96,6144]{1,0:T(8,128)(2,1)S(1)} collective-permute-done((bf16[96,6144]{1,0:T(8,128)(2,1)S(1)}, bf16[96,6144]{1,0:T(8,128)(2,1)S(1)}, u32[]{:S(2)}, u32[]{:S(2)}) %collective-permute-start.34) | collective-permute-done | bytes 1179680 | tf_op jit(solution)/shard_map/ppermute | solution.py:39
  347.1 7.6 %collective-permute-done.36.got_ref = bf16[192,6144]{1,0:T(8,128)(2,1)S(1)} collective-permute-done((bf16[192,6144]{1,0:T(8,128)(2,1)S(1)}, bf16[192,6144]{1,0:T(8,128)(2,1)S(1)}, u32[]{:S(2)}, u32[]{:S(2)}) %collective-permute-start.36) | collective-permute-done | bytes 2359328 | tf_op jit(solution)/shard_map/ppermute | solution.py:39
  365.1 16.8 %collective-permute-done.39.got_ref = bf16[96,6144]{1,0:T(8,128)(2,1)S(1)} collective-permute-done((bf16[96,6144]{1,0:T(8,128)(2,1)S(1)}, bf16[96,6144]{1,0:T(8,128)(2,1)S(1)}, u32[]{:S(2)}, u32[]{:S(2)}) %collective-permute-start.39) | collective-permute-done | bytes 1179680 | tf_op jit(solution)/shard_map/ppermute | solution.py:39
  385.6 11.5 %collective-permute-done.42 = bf16[48,6144]{1,0:T(8,128)(2,1)S(1)} collective-permute-done((bf16[48,6144]{1,0:T(8,128)(2,1)S(1)}, bf16[48,6144]{1,0:T(8,128)(2,1)S(1)}, u32[]{:S(2)}, u32[]{:S(2)}) %collective-permute-start.42) | collective-permute-done | bytes 589856 | tf_op jit(solution)/shard_map/ppermute | solution.py:35
  399.9 7.9 %collective-permute-done.44 = bf16[48,3200]{1,0:T(8,128)(2,1)S(1)} collective-permute-done((bf16[48,3200]{1,0:T(8,128)(2,1)S(1)}, bf16[48,3200]{1,0:T(8,128)(2,1)S(1)}, u32[]{:S(2)}, u32[]{:S(2)}) %collective-permute-start.44) | collective-permute-done | bytes 307232 | tf_op jit(solution)/shard_map/ppermute | solution.py:35
  408.6 9.4 %collective-permute-done.45.got_ref = bf16[24,6144]{1,0:T(8,128)(2,1)S(1)} collective-permute-done((bf16[24,6144]{1,0:T(8,128)(2,1)S(1)}, bf16[24,6144]{1,0:T(8,128)(2,1)S(1)}, u32[]{:S(2)}, u32[]{:S(2)}) %collective-permute-start.45) | collective-permute-done | bytes 294944 | tf_op jit(solution)/shard_map/ppermute | solution.py:35
  (228 shorter events, 172.8 us)
Async XLA Ops:
  17.1 14.7 %collective-permute-start.1 = (bf16[48,3200]{1,0:T(8,128)(2,1)S(1)}, bf16[48,3200]{1,0:T(8,128)(2,1)S(1)}, u32[]{:S(2)}, u32[]{:S(2)}) collective-permute-start(bf16[48,3200]{1,0:T(8,128)(2,1)S(1)} %pad_maximum_fusion.17), channel_id=1, source_target_pairs={{0,8},{1,9},{2,10},{3,11},{4,12},{5,13},{6,14},{7,15},{8,0},{9,1},... | collective-permute-start | bytes 921608 | tf_op jit(solution)/shard_map/ppermute | solution.py:35
  18.0 16.8 %collective-permute-start.2 = (bf16[24,6144]{1,0:T(8,128)(2,1)}, bf16[24,6144]{1,0:T(8,128)(2,1)S(1)}, u32[]{:S(2)}, u32[]{:S(2)}) collective-permute-start(bf16[24,6144]{1,0:T(8,128)(2,1)} %get-tuple-element.311), channel_id=1, source_target_pairs={{0,16},{1,17},{2,18},{3,19},{4,20},{5,21},{6,22},{7,23},{8,24},{9,... | collective-permute-start | bytes 884744 | tf_op jit(solution)/shard_map/ppermute | solution.py:35
  47.4 27.8 %collective-permute-start.5 = (bf16[192,3200]{1,0:T(8,128)(2,1)S(1)}, bf16[192,3200]{1,0:T(8,128)(2,1)S(1)}, u32[]{:S(2)}, u32[]{:S(2)}) collective-permute-start(bf16[192,3200]{1,0:T(8,128)(2,1)S(1)} %pad_maximum_fusion.7), channel_id=1, source_target_pairs={{0,4},{1,5},{2,3},{3,2},{4,0},{5,1},{6,7},{7,6},{8,12},{9,13},{10,... | collective-permute-start | bytes 3686408 | tf_op jit(solution)/shard_map/ppermute | solution.py:39
  50.5 14.1 %collective-permute-start.6 = (bf16[24,6144]{1,0:T(8,128)(2,1)S(1)}, bf16[24,6144]{1,0:T(8,128)(2,1)S(1)}, u32[]{:S(2)}, u32[]{:S(2)}) collective-permute-start(bf16[24,6144]{1,0:T(8,128)(2,1)S(1)} %copy-done.35), channel_id=1, source_target_pairs={{0,16},{1,17},{2,18},{3,19},{4,20},{5,21},{6,22},{7,23},{8,24},{9,... | collective-permute-start | bytes 884744 | tf_op jit(solution)/shard_map/ppermute | solution.py:35
  52.9 24.1 %collective-permute-start.7 = (bf16[96,6144]{1,0:T(8,128)(2,1)S(1)}, bf16[96,6144]{1,0:T(8,128)(2,1)}, u32[]{:S(2)}, u32[]{:S(2)}) collective-permute-start(bf16[96,6144]{1,0:T(8,128)(2,1)S(1)} %pad_maximum_fusion.10), channel_id=1, source_target_pairs={{0,1},{1,0},{2,6},{3,7},{4,5},{5,4},{6,2},{7,3},{8,9},{9,8},{10,14... | collective-permute-start | bytes 3538952 | tf_op jit(solution)/shard_map/ppermute | solution.py:39
  78.4 30.6 %collective-permute-start.11 = (bf16[192,6144]{1,0:T(8,128)(2,1)S(1)}, bf16[192,6144]{1,0:T(8,128)(2,1)S(1)}, u32[]{:S(2)}, u32[]{:S(2)}) collective-permute-start(bf16[192,6144]{1,0:T(8,128)(2,1)S(1)} %pad_maximum_fusion.4), channel_id=1, source_target_pairs={{0,4},{1,5},{2,3},{3,2},{4,0},{5,1},{6,7},{7,6},{8,12},{9,13},{10,... | collective-permute-start | bytes 7077896 | tf_op jit(solution)/shard_map/ppermute | solution.py:39
  109.5 22.6 %collective-permute-start.14 = (bf16[384,6144]{1,0:T(8,128)(2,1)S(1)}, bf16[384,6144]{1,0:T(8,128)(2,1)S(1)}, u32[]{:S(2)}, u32[]{:S(2)}) collective-permute-start(bf16[384,6144]{1,0:T(8,128)(2,1)S(1)} %pad_maximum_fusion.up_ref.down_ref), channel_id=1, source_target_pairs={{0,2},{1,3},{2,0},{3,1},{4,6},{5,7},{6,4},{7,5},{8,10},{9,11},{10,... | collective-permute-start | bytes 14155784 | tf_op jit(solution)/shard_map/ppermute | solution.py:35
  109.6 16.3 %collective-permute-start.12 = (bf16[96,6144]{1,0:T(8,128)(2,1)S(1)}, bf16[96,6144]{1,0:T(8,128)(2,1)S(1)}, u32[]{:S(2)}, u32[]{:S(2)}) collective-permute-start(bf16[96,6144]{1,0:T(8,128)(2,1)S(1)} %pad_maximum_fusion.11), channel_id=1, source_target_pairs={{0,1},{1,0},{2,6},{3,7},{4,5},{5,4},{6,2},{7,3},{8,9},{9,8},{10,14... | collective-permute-start | bytes 3538952 | tf_op jit(solution)/shard_map/ppermute | solution.py:39
  113.7 14.9 %collective-permute-start.13 = (bf16[48,6144]{1,0:T(8,128)(2,1)S(1)}, bf16[48,6144]{1,0:T(8,128)(2,1)S(1)}, u32[]{:S(2)}, u32[]{:S(2)}) collective-permute-start(bf16[48,6144]{1,0:T(8,128)(2,1)S(1)} %pad_maximum_fusion.16), channel_id=1, source_target_pairs={{0,8},{1,9},{2,10},{3,11},{4,12},{5,13},{6,14},{7,15},{8,0},{9,1},... | collective-permute-start | bytes 1769480 | tf_op jit(solution)/shard_map/ppermute | solution.py:35
  128.6 41.8 %collective-permute-start.16 = (bf16[192,6144]{1,0:T(8,128)(2,1)S(1)}, bf16[192,6144]{1,0:T(8,128)(2,1)S(1)}, u32[]{:S(2)}, u32[]{:S(2)}) collective-permute-start(bf16[192,6144]{1,0:T(8,128)(2,1)S(1)} %pad_maximum_fusion.5), channel_id=1, source_target_pairs={{0,4},{1,5},{2,3},{3,2},{4,0},{5,1},{6,7},{7,6},{8,12},{9,13},{10,... | collective-permute-start | bytes 7077896 | tf_op jit(solution)/shard_map/ppermute | solution.py:39
  131.7 29.0 %collective-permute-start.15 = (bf16[96,6144]{1,0:T(8,128)(2,1)S(1)}, bf16[96,6144]{1,0:T(8,128)(2,1)S(1)}, u32[]{:S(2)}, u32[]{:S(2)}) collective-permute-start(bf16[96,6144]{1,0:T(8,128)(2,1)S(1)} %pad_maximum_fusion.12), channel_id=1, source_target_pairs={{0,1},{1,0},{2,6},{3,7},{4,5},{5,4},{6,2},{7,3},{8,9},{9,8},{10,14... | collective-permute-start | bytes 3538952 | tf_op jit(solution)/shard_map/ppermute | solution.py:39
  173.2 29.3 %collective-permute-start.18 = (bf16[192,6144]{1,0:T(8,128)(2,1)}, bf16[192,6144]{1,0:T(8,128)(2,1)}, u32[]{:S(2)}, u32[]{:S(2)}) collective-permute-start(bf16[192,6144]{1,0:T(8,128)(2,1)} %pad_maximum_fusion.6), channel_id=1, source_target_pairs={{0,4},{1,5},{2,3},{3,2},{4,0},{5,1},{6,7},{7,6},{8,12},{9,13},{10,... | collective-permute-start | bytes 7077896 | tf_op jit(solution)/shard_map/ppermute | solution.py:39
  236.2 29.1 %collective-permute-start.26 = (bf16[192,6144]{1,0:T(8,128)(2,1)}, bf16[192,6144]{1,0:T(8,128)(2,1)S(1)}, u32[]{:S(2)}, u32[]{:S(2)}) collective-permute-start(bf16[192,6144]{1,0:T(8,128)(2,1)} %get-tuple-element.426), channel_id=1, source_target_pairs={{0,4},{1,5},{2,3},{3,2},{4,0},{5,1},{6,7},{7,6},{8,12},{9,13},{10,... | collective-permute-start | bytes 7077896 | tf_op jit(solution)/shard_map/ppermute | solution.py:39
  272.6 41.5 %collective-permute-start.32 = (bf16[192,6144]{1,0:T(8,128)(2,1)S(1)}, bf16[192,6144]{1,0:T(8,128)(2,1)S(1)}, u32[]{:S(2)}, u32[]{:S(2)}) collective-permute-start(bf16[192,6144]{1,0:T(8,128)(2,1)S(1)} %get-tuple-element.473), channel_id=1, source_target_pairs={{0,4},{1,5},{2,3},{3,2},{4,0},{5,1},{6,7},{7,6},{8,12},{9,13},{10,... | collective-permute-start | bytes 7077896 | tf_op jit(solution)/shard_map/ppermute | solution.py:39
  280.5 28.9 %collective-permute-start.31 = (bf16[96,6144]{1,0:T(8,128)(2,1)S(1)}, bf16[96,6144]{1,0:T(8,128)(2,1)S(1)}, u32[]{:S(2)}, u32[]{:S(2)}) collective-permute-start(bf16[96,6144]{1,0:T(8,128)(2,1)S(1)} %get-tuple-element.465), channel_id=1, source_target_pairs={{0,1},{1,0},{2,6},{3,7},{4,5},{5,4},{6,2},{7,3},{8,9},{9,8},{10,14... | collective-permute-start | bytes 3538952 | tf_op jit(solution)/shard_map/ppermute | solution.py:39
  298.5 20.1 %collective-permute-start.33 = (bf16[5,128,768]{2,1,0:T(8,128)(2,1)S(1)}, bf16[5,128,768]{2,1,0:T(8,128)(2,1)S(1)}, u32[]{:S(2)}, u32[]{:S(2)}) collective-permute-start(bf16[5,128,768]{2,1,0:T(8,128)(2,1)S(1)} %get-tuple-element.483.sd_ref), channel_id=1, source_target_pairs={{0,2},{1,3},{2,0},{3,1},{4,6},{5,7},{6,4},{7,5},{8,10},{9,11},{10,... | collective-permute-start | bytes 2949128 | tf_op jit(solution)/shard_map/ppermute | solution.py:35
  315.3 28.9 %collective-permute-start.34 = (bf16[96,6144]{1,0:T(8,128)(2,1)S(1)}, bf16[96,6144]{1,0:T(8,128)(2,1)S(1)}, u32[]{:S(2)}, u32[]{:S(2)}) collective-permute-start(bf16[96,6144]{1,0:T(8,128)(2,1)S(1)} %get-tuple-element.492), channel_id=1, source_target_pairs={{0,1},{1,0},{2,6},{3,7},{4,5},{5,4},{6,2},{7,3},{8,9},{9,8},{10,14... | collective-permute-start | bytes 3538952 | tf_op jit(solution)/shard_map/ppermute | solution.py:39
  316.4 28.3 %collective-permute-start.35 = (bf16[48,6144]{1,0:T(8,128)(2,1)S(1)}, bf16[48,6144]{1,0:T(8,128)(2,1)S(1)}, u32[]{:S(2)}, u32[]{:S(2)}) collective-permute-start(bf16[48,6144]{1,0:T(8,128)(2,1)S(1)} %get-tuple-element.501), channel_id=1, source_target_pairs={{0,8},{1,9},{2,10},{3,11},{4,12},{5,13},{6,14},{7,15},{8,0},{9,1},... | collective-permute-start | bytes 1769480 | tf_op jit(solution)/shard_map/ppermute | solution.py:35
  316.9 37.8 %collective-permute-start.36 = (bf16[192,6144]{1,0:T(8,128)(2,1)S(1)}, bf16[192,6144]{1,0:T(8,128)(2,1)S(1)}, u32[]{:S(2)}, u32[]{:S(2)}) collective-permute-start(bf16[192,6144]{1,0:T(8,128)(2,1)S(1)} %get-tuple-element.507), channel_id=1, source_target_pairs={{0,4},{1,5},{2,3},{3,2},{4,0},{5,1},{6,7},{7,6},{8,12},{9,13},{10,... | collective-permute-start | bytes 7077896 | tf_op jit(solution)/shard_map/ppermute | solution.py:39
  344.7 16.7 %collective-permute-start.38 = (bf16[48,6144]{1,0:T(8,128)(2,1)S(1)}, bf16[48,6144]{1,0:T(8,128)(2,1)S(1)}, u32[]{:S(2)}, u32[]{:S(2)}) collective-permute-start(bf16[48,6144]{1,0:T(8,128)(2,1)S(1)} %get-tuple-element.518), channel_id=1, source_target_pairs={{0,8},{1,9},{2,10},{3,11},{4,12},{5,13},{6,14},{7,15},{8,0},{9,1},... | collective-permute-start | bytes 1769480 | tf_op jit(solution)/shard_map/ppermute | solution.py:35
  346.2 35.7 %collective-permute-start.40 = (bf16[192,3200]{1,0:T(8,128)(2,1)S(1)}, bf16[192,3200]{1,0:T(8,128)(2,1)S(1)}, u32[]{:S(2)}, u32[]{:S(2)}) collective-permute-start(bf16[192,3200]{1,0:T(8,128)(2,1)S(1)} %pad_maximum_fusion.8), channel_id=1, source_target_pairs={{0,4},{1,5},{2,3},{3,2},{4,0},{5,1},{6,7},{7,6},{8,12},{9,13},{10,... | collective-permute-start | bytes 3686408 | tf_op jit(solution)/shard_map/ppermute | solution.py:39
  355.8 26.1 %collective-permute-start.39 = (bf16[96,6144]{1,0:T(8,128)(2,1)S(1)}, bf16[96,6144]{1,0:T(8,128)(2,1)S(1)}, u32[]{:S(2)}, u32[]{:S(2)}) collective-permute-start(bf16[96,6144]{1,0:T(8,128)(2,1)S(1)} %get-tuple-element.524), channel_id=1, source_target_pairs={{0,1},{1,0},{2,6},{3,7},{4,5},{5,4},{6,2},{7,3},{8,9},{9,8},{10,14... | collective-permute-start | bytes 3538952 | tf_op jit(solution)/shard_map/ppermute | solution.py:39
  361.5 22.3 %collective-permute-start.41 = (bf16[24,6144]{1,0:T(8,128)(2,1)S(1)}, bf16[24,6144]{1,0:T(8,128)(2,1)S(1)}, u32[]{:S(2)}, u32[]{:S(2)}) collective-permute-start(bf16[24,6144]{1,0:T(8,128)(2,1)S(1)} %add_convert_fusion.3), channel_id=1, source_target_pairs={{0,16},{1,17},{2,18},{3,19},{4,20},{5,21},{6,22},{7,23},{8,24},{9,... | collective-permute-start | bytes 884744 | tf_op jit(solution)/shard_map/ppermute | solution.py:35
  399.4 18.5 %collective-permute-start.45 = (bf16[24,6144]{1,0:T(8,128)(2,1)S(1)}, bf16[24,6144]{1,0:T(8,128)(2,1)S(1)}, u32[]{:S(2)}, u32[]{:S(2)}) collective-permute-start(bf16[24,6144]{1,0:T(8,128)(2,1)S(1)} %get-tuple-element.556), channel_id=1, source_target_pairs={{0,16},{1,17},{2,18},{3,19},{4,20},{5,21},{6,22},{7,23},{8,24},{9,... | collective-permute-start | bytes 884744 | tf_op jit(solution)/shard_map/ppermute | solution.py:35
  (63 other events, 646.3 us)

commit v17 on v16

--- a/solution.py
+++ b/solution.py
@@ -857,10 +857,11 @@
     x1 = go(x1, [last])
     x1 = go(x1, [middle])
     x1, w_middle = end(x1, middle)
+    kv = net.pair_forward(enc_rel, w_middle)
+    x1, (kv,) = tie(x1, kv)
     x1a, f_ms, k_ms = net.self_forward(x1, w_middle, 4, 4)
-    kv = net.pair_forward(enc_rel, w_middle)
+    x1a = go(x1a, [last])
     x1b, f_mc, k_mc = net.cross_forward(x1a, kv, w_middle, 2, 6)
-    x1b = go(x1b, [last])
     x1b, w_last = end(x1b, last)
 
     def core(x):

time: 430 us -> 432 us (level)
    ppermute x31, waiting for transfers between devices: 99.8 us -> 90.9 us  [swap(): return lax.ppermute(x, AXES, [(i, i ^ bit) for i in range(self.count)])]
    ppermute x16, waiting for transfers between devices: 110 us -> 118 us  [swap_by_core(): return lax.ppermute(x, AXES, pairs)]
  transfers between devices with their start and end apart: 47 -> 47, of which waited for: 27 -> 26; matrix products, arithmetic and copies ran while one was open for 4% -> 4% of each run, Pallas kernels for 27% -> 27%
where the time goes in v17:
time: 432 us; the launch traced here: 427 us
  waiting for transfers between devices  209 us (48%)
  Pallas kernels  137 us (32%)
  starting transfers between devices  45.7 us (11%)
  other arithmetic  15.3 us (4%)
  local copies, waits for them, and re-layouts  14.3 us (3%)
    pallas_call x29, Pallas kernels, call(): pl.pallas_call(kernel, out_shape=outs, grid_spec=pltpu.PrefetchScalarGrid...  137 us
    ppermute x16, waiting for transfers between devices, swap_by_core(): return lax.ppermute(x, AXES, pairs)  118 us
    ppermute x31, waiting for transfers between devices, swap(): return lax.ppermute(x, AXES, [(i, i ^ bit) for i in range(self.count)])  90.9 us
    ppermute x16, starting transfers between devices, swap_by_core(): return lax.ppermute(x, AXES, pairs)  24.5 us
    ppermute x31, starting transfers between devices, swap(): return lax.ppermute(x, AXES, [(i, i ^ bit) for i in range(self.count)])  21.3 us
    concatenate x16, other arithmetic, join(): self.x = jnp.concatenate((self.x, self.got), axis=0)  13.5 us
  transfers between devices with their start and end apart: 47, of which 26 were waited for; matrix products, arithmetic and copies ran while one was open for 4% of the time, Pallas kernels for 27%

profile of v17, /device:TPU:0, one launch (start us, length us, event | category | flops | bytes accessed | tf_op | source)
XLA Modules:
  0.0 426.8 jit_solution(3418888658731583042)
XLA Ops:
  21.3 10.5 %collective-permute-done.1 = bf16[48,3200]{1,0:T(8,128)(2,1)S(1)} collective-permute-done((bf16[48,3200]{1,0:T(8,128)(2,1)S(1)}, bf16[48,3200]{1,0:T(8,128)(2,1)S(1)}, u32[]{:S(2)}, u32[]{:S(2)}) %collective-permute-start.1) | collective-permute-done | bytes 307232 | tf_op jit(solution)/shard_map/ppermute | solution.py:35
  37.8 9.6 %collective-permute-done.3 = bf16[96,3200]{1,0:T(8,128)(2,1)S(1)} collective-permute-done((bf16[96,3200]{1,0:T(8,128)(2,1)S(1)}, bf16[96,3200]{1,0:T(8,128)(2,1)S(1)}, u32[]{:S(2)}, u32[]{:S(2)}) %collective-permute-start.3) | collective-permute-done | bytes 614432 | tf_op jit(solution)/shard_map/ppermute | solution.py:39
  54.4 10.2 %collective-permute-done.6 = bf16[24,6144]{1,0:T(8,128)(2,1)S(1)} collective-permute-done((bf16[24,6144]{1,0:T(8,128)(2,1)S(1)}, bf16[24,6144]{1,0:T(8,128)(2,1)S(1)}, u32[]{:S(2)}, u32[]{:S(2)}) %collective-permute-start.6) | collective-permute-done | bytes 294944 | tf_op jit(solution)/shard_map/ppermute | solution.py:35
  64.6 10.7 %collective-permute-done.5 = bf16[192,3200]{1,0:T(8,128)(2,1)S(1)} collective-permute-done((bf16[192,3200]{1,0:T(8,128)(2,1)S(1)}, bf16[192,3200]{1,0:T(8,128)(2,1)S(1)}, u32[]{:S(2)}, u32[]{:S(2)}) %collective-permute-start.5) | collective-permute-done | bytes 1228832 | tf_op jit(solution)/shard_map/ppermute | solution.py:39
  84.4 10.6 %collective-permute-done.9 = bf16[48,6144]{1,0:T(8,128)(2,1)S(1)} collective-permute-done((bf16[48,6144]{1,0:T(8,128)(2,1)S(1)}, bf16[48,6144]{1,0:T(8,128)(2,1)S(1)}, u32[]{:S(2)}, u32[]{:S(2)}) %collective-permute-start.9) | collective-permute-done | bytes 589856 | tf_op jit(solution)/shard_map/ppermute | solution.py:35
  95.1 13.8 %collective-permute-done.10 = bf16[24,6144]{1,0:T(8,128)(2,1)S(1)} collective-permute-done((bf16[24,6144]{1,0:T(8,128)(2,1)S(1)}, bf16[24,6144]{1,0:T(8,128)(2,1)S(1)}, u32[]{:S(2)}, u32[]{:S(2)}) %collective-permute-start.10) | collective-permute-done | bytes 294944 | tf_op jit(solution)/shard_map/ppermute | solution.py:35
  139.5 21.2 %collective-permute-done.15 = bf16[96,6144]{1,0:T(8,128)(2,1)S(1)} collective-permute-done((bf16[96,6144]{1,0:T(8,128)(2,1)S(1)}, bf16[96,6144]{1,0:T(8,128)(2,1)S(1)}, u32[]{:S(2)}, u32[]{:S(2)}) %collective-permute-start.15) | collective-permute-done | bytes 1179680 | tf_op jit(solution)/shard_map/ppermute | solution.py:39
  162.3 8.2 %collective-permute-done.16 = bf16[192,6144]{1,0:T(8,128)(2,1)S(1)} collective-permute-done((bf16[192,6144]{1,0:T(8,128)(2,1)S(1)}, bf16[192,6144]{1,0:T(8,128)(2,1)S(1)}, u32[]{:S(2)}, u32[]{:S(2)}) %collective-permute-start.16) | collective-permute-done | bytes 2359328 | tf_op jit(solution)/shard_map/ppermute | solution.py:39
  187.1 6.8 %shard_map.429 = (f32[128,768]{1,0:T(8,128)S(1)}, bf16[2,128,768]{2,1,0:T(8,128)(2,1)}, bf16[3,128,768]{2,1,0:T(8,128)(2,1)S(1)}) custom-call(f32[128,768]{1,0:T(8,128)S(1)} %get-tuple-element.393.x_ref, f32[16,768]{1,0:T(8,128)S(1)} %fusion.5.vec_ref, bf16[768,768]{1,0:T(8,128)(2,1)S(1)} %fusion.order_ref, bf16[384,6144]{1,0:T(8,128)(2,1)} %pad_maximum_fusion.1.top_ref, ...), custom_call_target="tpu_custom_call" | custom-call | flops 1000 | bytes 1000 | tf_op jit(solution)/shard_map/pallas_call | solution.py:603
  193.9 8.5 %collective-permute-done.18 = bf16[192,6144]{1,0:T(8,128)(2,1)} collective-permute-done((bf16[192,6144]{1,0:T(8,128)(2,1)}, bf16[192,6144]{1,0:T(8,128)(2,1)}, u32[]{:S(2)}, u32[]{:S(2)}) %collective-permute-start.18) | collective-permute-done | bytes 2359328 | tf_op jit(solution)/shard_map/ppermute | solution.py:39
  206.5 9.5 %shard_map.430 = (f32[128,768]{1,0:T(8,128)S(1)}, bf16[2,128,768]{2,1,0:T(8,128)(2,1)S(1)}, bf16[128,768]{1,0:T(8,128)(2,1)S(1)}) custom-call(s32[2]{0:T(128)S(1)} %copy-done.27, f32[128,768]{1,0:T(8,128)S(1)} %get-tuple-element.399.x_ref, f32[16,768]{1,0:T(8,128)S(1)} %fusion.5.vec_ref, bf16[768,768]{1,0:T(8,128)(2,1)S(1)} %fusion.order_ref, ...), custom_call_target="tpu_custom_call" | custom-call | flops 1000 | bytes 1000 | tf_op jit(solution)/shard_map/pallas_call | solution.py:603
  217.6 7.6 %shard_map.431 = (f32[128,768]{1,0:T(8,128)S(1)}, f32[8,768]{1,0:T(8,128)S(1)}, bf16[5,128,768]{2,1,0:T(8,128)(2,1)S(1)}, bf16[5,128,768]{2,1,0:T(8,128)(2,1)S(1)}) custom-call(f32[128,768]{1,0:T(8,128)S(1)} %get-tuple-element.407.x_ref, f32[16,768]{1,0:T(8,128)S(1)} %fusion.5.vec_ref, bf16[768,768]{1,0:T(8,128)(2,1)S(1)} %fusion.order_ref, ...), custom_call_target="tpu_custom_call" | custom-call | flops 1000 | bytes 1000 | tf_op jit(solution)/shard_map/pallas_call | solution.py:603
  238.5 11.3 %shard_map.434 = (f32[128,768]{1,0:T(8,128)S(1)}, f32[8,768]{1,0:T(8,128)S(1)}, bf16[2,128,768]{2,1,0:T(8,128)(2,1)S(1)}, bf16[1152,1536]{1,0:T(8,128)(2,1)S(1)}) custom-call(s32[2]{0:T(128)S(1)} %copy-done.27, f32[128,768]{1,0:T(8,128)S(1)} %get-tuple-element.399.x_ref, f32[16,768]{1,0:T(8,128)S(1)} %fusion.5.vec_ref, bf16[768,768]{1,0:T(8,128)(2,1)S(1)} %fusion.order_ref, ...), custom_call_target="tpu_custom_call" | custom-call | flops 1000 | bytes 1000 | tf_op jit(solution)/shard_map/pallas_call | solution.py:603
  254.4 10.3 %shard_map.436 = (f32[128,768]{1,0:T(8,128)S(1)}, f32[8,768]{1,0:T(8,128)S(1)}, bf16[4,128,768]{2,1,0:T(8,128)(2,1)S(1)}) custom-call(f32[128,768]{1,0:T(8,128)S(1)} %get-tuple-element.393.x_ref, f32[16,768]{1,0:T(8,128)S(1)} %fusion.5.vec_ref, bf16[768,768]{1,0:T(8,128)(2,1)S(1)} %fusion.order_ref, bf16[3,128,768]{2,1,0:T(8,128)(2,1)S(1)} %copy-done.16, ...), custom_call_target="tpu_custom_call" | custom-call | flops 1000 | bytes 1000 | tf_op jit(solution)/shard_map/pallas_call | solution.py:603
  268.5 7.2 %shard_map.438 = (bf16[192,6144]{1,0:T(8,128)(2,1)S(1)}, bf16[192,6144]{1,0:T(8,128)(2,1)S(1)}) custom-call(bf16[768,768]{1,0:T(8,128)(2,1)S(1)} %fusion.order_ref, bf16[2,128,768]{2,1,0:T(8,128)(2,1)} %get-tuple-element.441.s_ref, bf16[2,128,768]{2,1,0:T(8,128)(2,1)S(1)} %copy-done.18, bf16[4,128,768]{2,1,0:T(8,128)(2,1)S(1)} %get-tuple-element.443.sd_ref, ...), custom_call_target="tpu_custom_call" | custom-call | flops 1000 | bytes 1000 | tf_op jit(solution)/shard_map/pallas_call | solution.py:603
  290.4 10.8 %shard_map.441 = (f32[128,768]{1,0:T(8,128)S(1)}, f32[8,768]{1,0:T(8,128)}, bf16[5,128,768]{2,1,0:T(8,128)(2,1)S(1)}) custom-call(bf16[128,768]{1,0:T(8,128)(2,1)S(1)} %bitcast.29, f32[16,768]{1,0:T(8,128)S(1)} %fusion.5.vec_ref, bf16[768,768]{1,0:T(8,128)(2,1)S(1)} %fusion.order_ref, bf16[3,128,768]{2,1,0:T(8,128)(2,1)S(1)} %copy-done.14, ...), custom_call_target="tpu_custom_call" | custom-call | flops 1000 | bytes 1000 | tf_op jit(solution)/shard_map/pallas_call | solution.py:603
  301.3 11.3 %collective-permute-done.31.got_ref = bf16[96,6144]{1,0:T(8,128)(2,1)S(1)} collective-permute-done((bf16[96,6144]{1,0:T(8,128)(2,1)}, bf16[96,6144]{1,0:T(8,128)(2,1)S(1)}, u32[]{:S(2)}, u32[]{:S(2)}) %collective-permute-start.31) | collective-permute-done | bytes 1179680 | tf_op jit(solution)/shard_map/ppermute | solution.py:39
  325.5 8.5 %shard_map.445 = bf16[1152,768]{1,0:T(8,128)(2,1)} custom-call(bf16[1152,1536]{1,0:T(8,128)(2,1)S(1)} %get-tuple-element.493.dkv_ref, bf16[768,768]{1,0:T(8,128)(2,1)S(1)} %fusion.order_ref, bf16[384,6144]{1,0:T(8,128)(2,1)} %pad_maximum_fusion.1.top_ref, bf16[384,6144]{1,0:T(8,128)(2,1)} %collective-permute-done.17.low_ref), custom_call_target="tpu_custom_call" | custom-call | flops 1000 | bytes 1000 | tf_op jit(solution)/shard_map/pallas_call | solution.py:603
  334.0 13.1 %collective-permute-done.34.got_ref = bf16[96,6144]{1,0:T(8,128)(2,1)S(1)} collective-permute-done((bf16[96,6144]{1,0:T(8,128)(2,1)S(1)}, bf16[96,6144]{1,0:T(8,128)(2,1)S(1)}, u32[]{:S(2)}, u32[]{:S(2)}) %collective-permute-start.34) | collective-permute-done | bytes 1179680 | tf_op jit(solution)/shard_map/ppermute | solution.py:39
  350.1 7.6 %collective-permute-done.36.got_ref = bf16[192,6144]{1,0:T(8,128)(2,1)S(1)} collective-permute-done((bf16[192,6144]{1,0:T(8,128)(2,1)S(1)}, bf16[192,6144]{1,0:T(8,128)(2,1)S(1)}, u32[]{:S(2)}, u32[]{:S(2)}) %collective-permute-start.36) | collective-permute-done | bytes 2359328 | tf_op jit(solution)/shard_map/ppermute | solution.py:39
  368.0 16.9 %collective-permute-done.39.got_ref = bf16[96,6144]{1,0:T(8,128)(2,1)S(1)} collective-permute-done((bf16[96,6144]{1,0:T(8,128)(2,1)S(1)}, bf16[96,6144]{1,0:T(8,128)(2,1)S(1)}, u32[]{:S(2)}, u32[]{:S(2)}) %collective-permute-start.39) | collective-permute-done | bytes 1179680 | tf_op jit(solution)/shard_map/ppermute | solution.py:39
  388.3 11.5 %collective-permute-done.42 = bf16[48,6144]{1,0:T(8,128)(2,1)S(1)} collective-permute-done((bf16[48,6144]{1,0:T(8,128)(2,1)S(1)}, bf16[48,6144]{1,0:T(8,128)(2,1)S(1)}, u32[]{:S(2)}, u32[]{:S(2)}) %collective-permute-start.42) | collective-permute-done | bytes 589856 | tf_op jit(solution)/shard_map/ppermute | solution.py:35
  402.7 7.9 %collective-permute-done.44 = bf16[48,3200]{1,0:T(8,128)(2,1)S(1)} collective-permute-done((bf16[48,3200]{1,0:T(8,128)(2,1)S(1)}, bf16[48,3200]{1,0:T(8,128)(2,1)S(1)}, u32[]{:S(2)}, u32[]{:S(2)}) %collective-permute-start.44) | collective-permute-done | bytes 307232 | tf_op jit(solution)/shard_map/ppermute | solution.py:35
  411.4 9.2 %collective-permute-done.45.got_ref = bf16[24,6144]{1,0:T(8,128)(2,1)S(1)} collective-permute-done((bf16[24,6144]{1,0:T(8,128)(2,1)S(1)}, bf16[24,6144]{1,0:T(8,128)(2,1)S(1)}, u32[]{:S(2)}, u32[]{:S(2)}) %collective-permute-start.45) | collective-permute-done | bytes 294944 | tf_op jit(solution)/shard_map/ppermute | solution.py:35
  (216 shorter events, 172.5 us)
Async XLA Ops:
  17.1 14.7 %collective-permute-start.1 = (bf16[48,3200]{1,0:T(8,128)(2,1)S(1)}, bf16[48,3200]{1,0:T(8,128)(2,1)S(1)}, u32[]{:S(2)}, u32[]{:S(2)}) collective-permute-start(bf16[48,3200]{1,0:T(8,128)(2,1)S(1)} %pad_maximum_fusion.17), channel_id=1, source_target_pairs={{0,8},{1,9},{2,10},{3,11},{4,12},{5,13},{6,14},{7,15},{8,0},{9,1},... | collective-permute-start | bytes 921608 | tf_op jit(solution)/shard_map/ppermute | solution.py:35
  18.0 16.8 %collective-permute-start.2 = (bf16[24,6144]{1,0:T(8,128)(2,1)}, bf16[24,6144]{1,0:T(8,128)(2,1)S(1)}, u32[]{:S(2)}, u32[]{:S(2)}) collective-permute-start(bf16[24,6144]{1,0:T(8,128)(2,1)} %get-tuple-element.313), channel_id=1, source_target_pairs={{0,16},{1,17},{2,18},{3,19},{4,20},{5,21},{6,22},{7,23},{8,24},{9,... | collective-permute-start | bytes 884744 | tf_op jit(solution)/shard_map/ppermute | solution.py:35
  47.4 27.8 %collective-permute-start.5 = (bf16[192,3200]{1,0:T(8,128)(2,1)S(1)}, bf16[192,3200]{1,0:T(8,128)(2,1)S(1)}, u32[]{:S(2)}, u32[]{:S(2)}) collective-permute-start(bf16[192,3200]{1,0:T(8,128)(2,1)S(1)} %pad_maximum_fusion.7), channel_id=1, source_target_pairs={{0,4},{1,5},{2,3},{3,2},{4,0},{5,1},{6,7},{7,6},{8,12},{9,13},{10,... | collective-permute-start | bytes 3686408 | tf_op jit(solution)/shard_map/ppermute | solution.py:39
  50.5 14.1 %collective-permute-start.6 = (bf16[24,6144]{1,0:T(8,128)(2,1)S(1)}, bf16[24,6144]{1,0:T(8,128)(2,1)S(1)}, u32[]{:S(2)}, u32[]{:S(2)}) collective-permute-start(bf16[24,6144]{1,0:T(8,128)(2,1)S(1)} %copy-done.29), channel_id=1, source_target_pairs={{0,16},{1,17},{2,18},{3,19},{4,20},{5,21},{6,22},{7,23},{8,24},{9,... | collective-permute-start | bytes 884744 | tf_op jit(solution)/shard_map/ppermute | solution.py:35
  52.9 24.1 %collective-permute-start.7 = (bf16[96,6144]{1,0:T(8,128)(2,1)S(1)}, bf16[96,6144]{1,0:T(8,128)(2,1)}, u32[]{:S(2)}, u32[]{:S(2)}) collective-permute-start(bf16[96,6144]{1,0:T(8,128)(2,1)S(1)} %pad_maximum_fusion.10), channel_id=1, source_target_pairs={{0,1},{1,0},{2,6},{3,7},{4,5},{5,4},{6,2},{7,3},{8,9},{9,8},{10,14... | collective-permute-start | bytes 3538952 | tf_op jit(solution)/shard_map/ppermute | solution.py:39
  78.4 30.6 %collective-permute-start.11 = (bf16[192,6144]{1,0:T(8,128)(2,1)S(1)}, bf16[192,6144]{1,0:T(8,128)(2,1)S(1)}, u32[]{:S(2)}, u32[]{:S(2)}) collective-permute-start(bf16[192,6144]{1,0:T(8,128)(2,1)S(1)} %pad_maximum_fusion.4), channel_id=1, source_target_pairs={{0,4},{1,5},{2,3},{3,2},{4,0},{5,1},{6,7},{7,6},{8,12},{9,13},{10,... | collective-permute-start | bytes 7077896 | tf_op jit(solution)/shard_map/ppermute | solution.py:39
  109.5 22.6 %collective-permute-start.14 = (bf16[384,6144]{1,0:T(8,128)(2,1)S(1)}, bf16[384,6144]{1,0:T(8,128)(2,1)S(1)}, u32[]{:S(2)}, u32[]{:S(2)}) collective-permute-start(bf16[384,6144]{1,0:T(8,128)(2,1)S(1)} %pad_maximum_fusion.up_ref.down_ref), channel_id=1, source_target_pairs={{0,2},{1,3},{2,0},{3,1},{4,6},{5,7},{6,4},{7,5},{8,10},{9,11},{10,... | collective-permute-start | bytes 14155784 | tf_op jit(solution)/shard_map/ppermute | solution.py:35
  109.6 16.3 %collective-permute-start.12 = (bf16[96,6144]{1,0:T(8,128)(2,1)S(1)}, bf16[96,6144]{1,0:T(8,128)(2,1)S(1)}, u32[]{:S(2)}, u32[]{:S(2)}) collective-permute-start(bf16[96,6144]{1,0:T(8,128)(2,1)S(1)} %pad_maximum_fusion.11), channel_id=1, source_target_pairs={{0,1},{1,0},{2,6},{3,7},{4,5},{5,4},{6,2},{7,3},{8,9},{9,8},{10,14... | collective-permute-start | bytes 3538952 | tf_op jit(solution)/shard_map/ppermute | solution.py:39
  113.7 14.9 %collective-permute-start.13 = (bf16[48,6144]{1,0:T(8,128)(2,1)S(1)}, bf16[48,6144]{1,0:T(8,128)(2,1)S(1)}, u32[]{:S(2)}, u32[]{:S(2)}) collective-permute-start(bf16[48,6144]{1,0:T(8,128)(2,1)S(1)} %pad_maximum_fusion.16), channel_id=1, source_target_pairs={{0,8},{1,9},{2,10},{3,11},{4,12},{5,13},{6,14},{7,15},{8,0},{9,1},... | collective-permute-start | bytes 1769480 | tf_op jit(solution)/shard_map/ppermute | solution.py:35
  128.6 41.9 %collective-permute-start.16 = (bf16[192,6144]{1,0:T(8,128)(2,1)S(1)}, bf16[192,6144]{1,0:T(8,128)(2,1)S(1)}, u32[]{:S(2)}, u32[]{:S(2)}) collective-permute-start(bf16[192,6144]{1,0:T(8,128)(2,1)S(1)} %pad_maximum_fusion.5), channel_id=1, source_target_pairs={{0,4},{1,5},{2,3},{3,2},{4,0},{5,1},{6,7},{7,6},{8,12},{9,13},{10,... | collective-permute-start | bytes 7077896 | tf_op jit(solution)/shard_map/ppermute | solution.py:39
  131.7 29.0 %collective-permute-start.15 = (bf16[96,6144]{1,0:T(8,128)(2,1)S(1)}, bf16[96,6144]{1,0:T(8,128)(2,1)S(1)}, u32[]{:S(2)}, u32[]{:S(2)}) collective-permute-start(bf16[96,6144]{1,0:T(8,128)(2,1)S(1)} %pad_maximum_fusion.12), channel_id=1, source_target_pairs={{0,1},{1,0},{2,6},{3,7},{4,5},{5,4},{6,2},{7,3},{8,9},{9,8},{10,14... | collective-permute-start | bytes 3538952 | tf_op jit(solution)/shard_map/ppermute | solution.py:39
  173.2 29.2 %collective-permute-start.18 = (bf16[192,6144]{1,0:T(8,128)(2,1)}, bf16[192,6144]{1,0:T(8,128)(2,1)}, u32[]{:S(2)}, u32[]{:S(2)}) collective-permute-start(bf16[192,6144]{1,0:T(8,128)(2,1)} %pad_maximum_fusion.6), channel_id=1, source_target_pairs={{0,4},{1,5},{2,3},{3,2},{4,0},{5,1},{6,7},{7,6},{8,12},{9,13},{10,... | collective-permute-start | bytes 7077896 | tf_op jit(solution)/shard_map/ppermute | solution.py:39
  237.5 29.1 %collective-permute-start.26 = (bf16[192,6144]{1,0:T(8,128)(2,1)}, bf16[192,6144]{1,0:T(8,128)(2,1)S(1)}, u32[]{:S(2)}, u32[]{:S(2)}) collective-permute-start(bf16[192,6144]{1,0:T(8,128)(2,1)} %get-tuple-element.430), channel_id=1, source_target_pairs={{0,4},{1,5},{2,3},{3,2},{4,0},{5,1},{6,7},{7,6},{8,12},{9,13},{10,... | collective-permute-start | bytes 7077896 | tf_op jit(solution)/shard_map/ppermute | solution.py:39
  275.7 41.5 %collective-permute-start.32 = (bf16[192,6144]{1,0:T(8,128)(2,1)S(1)}, bf16[192,6144]{1,0:T(8,128)(2,1)S(1)}, u32[]{:S(2)}, u32[]{:S(2)}) collective-permute-start(bf16[192,6144]{1,0:T(8,128)(2,1)S(1)} %get-tuple-element.477), channel_id=1, source_target_pairs={{0,4},{1,5},{2,3},{3,2},{4,0},{5,1},{6,7},{7,6},{8,12},{9,13},{10,... | collective-permute-start | bytes 7077896 | tf_op jit(solution)/shard_map/ppermute | solution.py:39
  283.5 29.1 %collective-permute-start.31 = (bf16[96,6144]{1,0:T(8,128)(2,1)}, bf16[96,6144]{1,0:T(8,128)(2,1)S(1)}, u32[]{:S(2)}, u32[]{:S(2)}) collective-permute-start(bf16[96,6144]{1,0:T(8,128)(2,1)} %get-tuple-element.469), channel_id=1, source_target_pairs={{0,1},{1,0},{2,6},{3,7},{4,5},{5,4},{6,2},{7,3},{8,9},{9,8},{10,14... | collective-permute-start | bytes 3538952 | tf_op jit(solution)/shard_map/ppermute | solution.py:39
  301.2 20.4 %collective-permute-start.33 = (bf16[5,128,768]{2,1,0:T(8,128)(2,1)S(1)}, bf16[5,128,768]{2,1,0:T(8,128)(2,1)S(1)}, u32[]{:S(2)}, u32[]{:S(2)}) collective-permute-start(bf16[5,128,768]{2,1,0:T(8,128)(2,1)S(1)} %get-tuple-element.487.sd_ref), channel_id=1, source_target_pairs={{0,2},{1,3},{2,0},{3,1},{4,6},{5,7},{6,4},{7,5},{8,10},{9,11},{10,... | collective-permute-start | bytes 2949128 | tf_op jit(solution)/shard_map/ppermute | solution.py:35
  318.3 28.9 %collective-permute-start.34 = (bf16[96,6144]{1,0:T(8,128)(2,1)S(1)}, bf16[96,6144]{1,0:T(8,128)(2,1)S(1)}, u32[]{:S(2)}, u32[]{:S(2)}) collective-permute-start(bf16[96,6144]{1,0:T(8,128)(2,1)S(1)} %get-tuple-element.496), channel_id=1, source_target_pairs={{0,1},{1,0},{2,6},{3,7},{4,5},{5,4},{6,2},{7,3},{8,9},{9,8},{10,14... | collective-permute-start | bytes 3538952 | tf_op jit(solution)/shard_map/ppermute | solution.py:39
  319.4 28.3 %collective-permute-start.35 = (bf16[48,6144]{1,0:T(8,128)(2,1)S(1)}, bf16[48,6144]{1,0:T(8,128)(2,1)S(1)}, u32[]{:S(2)}, u32[]{:S(2)}) collective-permute-start(bf16[48,6144]{1,0:T(8,128)(2,1)S(1)} %get-tuple-element.505), channel_id=1, source_target_pairs={{0,8},{1,9},{2,10},{3,11},{4,12},{5,13},{6,14},{7,15},{8,0},{9,1},... | collective-permute-start | bytes 1769480 | tf_op jit(solution)/shard_map/ppermute | solution.py:35
  319.9 37.8 %collective-permute-start.36 = (bf16[192,6144]{1,0:T(8,128)(2,1)S(1)}, bf16[192,6144]{1,0:T(8,128)(2,1)S(1)}, u32[]{:S(2)}, u32[]{:S(2)}) collective-permute-start(bf16[192,6144]{1,0:T(8,128)(2,1)S(1)} %get-tuple-element.511), channel_id=1, source_target_pairs={{0,4},{1,5},{2,3},{3,2},{4,0},{5,1},{6,7},{7,6},{8,12},{9,13},{10,... | collective-permute-start | bytes 7077896 | tf_op jit(solution)/shard_map/ppermute | solution.py:39
  347.7 16.7 %collective-permute-start.38 = (bf16[48,6144]{1,0:T(8,128)(2,1)S(1)}, bf16[48,6144]{1,0:T(8,128)(2,1)S(1)}, u32[]{:S(2)}, u32[]{:S(2)}) collective-permute-start(bf16[48,6144]{1,0:T(8,128)(2,1)S(1)} %get-tuple-element.522), channel_id=1, source_target_pairs={{0,8},{1,9},{2,10},{3,11},{4,12},{5,13},{6,14},{7,15},{8,0},{9,1},... | collective-permute-start | bytes 1769480 | tf_op jit(solution)/shard_map/ppermute | solution.py:35
  349.3 35.6 %collective-permute-start.40 = (bf16[192,3200]{1,0:T(8,128)(2,1)S(1)}, bf16[192,3200]{1,0:T(8,128)(2,1)S(1)}, u32[]{:S(2)}, u32[]{:S(2)}) collective-permute-start(bf16[192,3200]{1,0:T(8,128)(2,1)S(1)} %pad_maximum_fusion.8), channel_id=1, source_target_pairs={{0,4},{1,5},{2,3},{3,2},{4,0},{5,1},{6,7},{7,6},{8,12},{9,13},{10,... | collective-permute-start | bytes 3686408 | tf_op jit(solution)/shard_map/ppermute | solution.py:39
  358.7 26.2 %collective-permute-start.39 = (bf16[96,6144]{1,0:T(8,128)(2,1)S(1)}, bf16[96,6144]{1,0:T(8,128)(2,1)S(1)}, u32[]{:S(2)}, u32[]{:S(2)}) collective-permute-start(bf16[96,6144]{1,0:T(8,128)(2,1)S(1)} %get-tuple-element.528), channel_id=1, source_target_pairs={{0,1},{1,0},{2,6},{3,7},{4,5},{5,4},{6,2},{7,3},{8,9},{9,8},{10,14... | collective-permute-start | bytes 3538952 | tf_op jit(solution)/shard_map/ppermute | solution.py:39
  364.5 22.1 %collective-permute-start.41 = (bf16[24,6144]{1,0:T(8,128)(2,1)S(1)}, bf16[24,6144]{1,0:T(8,128)(2,1)S(1)}, u32[]{:S(2)}, u32[]{:S(2)}) collective-permute-start(bf16[24,6144]{1,0:T(8,128)(2,1)S(1)} %add_convert_fusion.3), channel_id=1, source_target_pairs={{0,16},{1,17},{2,18},{3,19},{4,20},{5,21},{6,22},{7,23},{8,24},{9,... | collective-permute-start | bytes 884744 | tf_op jit(solution)/shard_map/ppermute | solution.py:35
  402.1 18.5 %collective-permute-start.45 = (bf16[24,6144]{1,0:T(8,128)(2,1)S(1)}, bf16[24,6144]{1,0:T(8,128)(2,1)S(1)}, u32[]{:S(2)}, u32[]{:S(2)}) collective-permute-start(bf16[24,6144]{1,0:T(8,128)(2,1)S(1)} %get-tuple-element.560), channel_id=1, source_target_pairs={{0,16},{1,17},{2,18},{3,19},{4,20},{5,21},{6,22},{7,23},{8,24},{9,... | collective-permute-start | bytes 884744 | tf_op jit(solution)/shard_map/ppermute | solution.py:35
  (57 other events, 600.9 us)

commit v18 on v16

--- a/solution.py
+++ b/solution.py
@@ -599,7 +599,7 @@
     return pl.BlockSpec(x.shape, lambda *_: (0,) * len(x.shape))
 
 
-def call(kernel, steps, ins, in_specs, outs, out_specs, scratch=(), scalars=0, vmem=24):
+def call(kernel, steps, ins, in_specs, outs, out_specs, scratch=(), scalars=0, vmem=16):
     return pl.pallas_call(
         kernel,
         out_shape=outs,
@@ -658,7 +658,7 @@
             functools.partial(cross_forward_kernel, self.captions, row), 2,
             (self.count,) + ins + w,
             [whole(i) for i in ins] + self.weights(lambda j: at + j),
-            outs, [whole(o) for o in outs], scalars=1,
+            outs, [whole(o) for o in outs], scalars=1, vmem=24,
         )
 
     def cross_backward(self, x, kept, kv, dx, w, at, row):
@@ -669,7 +669,7 @@
             functools.partial(cross_backward_kernel, self.captions, row), 2,
             (self.count,) + ins + w,
             [whole(i) for i in ins] + self.weights(lambda j: at + 1 - j),
-            outs, [whole(i) for i in outs], scalars=1,
+            outs, [whole(i) for i in outs], scalars=1, vmem=24,
         )
 
     def pair_forward(self, enc, w):

time: 430 us -> 429 us (level)
  no operation moved by 1% of the time
where the time goes in v18:
time: 429 us; the launch traced here: 424 us
  waiting for transfers between devices  210 us (49%)
  Pallas kernels  133 us (31%)
  starting transfers between devices  46.1 us (11%)
  other arithmetic  15.3 us (4%)
  local copies, waits for them, and re-layouts  13.7 us (3%)
    pallas_call x29, Pallas kernels, call(): pl.pallas_call(kernel, out_shape=outs, grid_spec=pltpu.PrefetchScalarGrid...  133 us
    ppermute x16, waiting for transfers between devices, swap_by_core(): return lax.ppermute(x, AXES, pairs)  110 us
    ppermute x31, waiting for transfers between devices, swap(): return lax.ppermute(x, AXES, [(i, i ^ bit) for i in range(self.count)])  100 us
    ppermute x16, starting transfers between devices, swap_by_core(): return lax.ppermute(x, AXES, pairs)  24.6 us
    ppermute x31, starting transfers between devices, swap(): return lax.ppermute(x, AXES, [(i, i ^ bit) for i in range(self.count)])  21.4 us
    concatenate x16, other arithmetic, join(): self.x = jnp.concatenate((self.x, self.got), axis=0)  13.6 us
  transfers between devices with their start and end apart: 47, of which 27 were waited for; matrix products, arithmetic and copies ran while one was open for 4% of the time, Pallas kernels for 27%

profile of v18, /device:TPU:0, one launch (start us, length us, event | category | flops | bytes accessed | tf_op | source)
XLA Modules:
  0.0 423.6 jit_solution(10711896397064887886)
XLA Ops:
  21.3 10.5 %collective-permute-done.1 = bf16[48,3200]{1,0:T(8,128)(2,1)S(1)} collective-permute-done((bf16[48,3200]{1,0:T(8,128)(2,1)S(1)}, bf16[48,3200]{1,0:T(8,128)(2,1)S(1)}, u32[]{:S(2)}, u32[]{:S(2)}) %collective-permute-start.1) | collective-permute-done | bytes 307232 | tf_op jit(solution)/shard_map/ppermute | solution.py:35
  37.8 9.6 %collective-permute-done.3 = bf16[96,3200]{1,0:T(8,128)(2,1)S(1)} collective-permute-done((bf16[96,3200]{1,0:T(8,128)(2,1)S(1)}, bf16[96,3200]{1,0:T(8,128)(2,1)S(1)}, u32[]{:S(2)}, u32[]{:S(2)}) %collective-permute-start.3) | collective-permute-done | bytes 614432 | tf_op jit(solution)/shard_map/ppermute | solution.py:39
  54.4 10.2 %collective-permute-done.6 = bf16[24,6144]{1,0:T(8,128)(2,1)S(1)} collective-permute-done((bf16[24,6144]{1,0:T(8,128)(2,1)S(1)}, bf16[24,6144]{1,0:T(8,128)(2,1)S(1)}, u32[]{:S(2)}, u32[]{:S(2)}) %collective-permute-start.6) | collective-permute-done | bytes 294944 | tf_op jit(solution)/shard_map/ppermute | solution.py:35
  64.6 10.7 %collective-permute-done.5 = bf16[192,3200]{1,0:T(8,128)(2,1)S(1)} collective-permute-done((bf16[192,3200]{1,0:T(8,128)(2,1)S(1)}, bf16[192,3200]{1,0:T(8,128)(2,1)S(1)}, u32[]{:S(2)}, u32[]{:S(2)}) %collective-permute-start.5) | collective-permute-done | bytes 1228832 | tf_op jit(solution)/shard_map/ppermute | solution.py:39
  84.3 10.6 %collective-permute-done.9 = bf16[48,6144]{1,0:T(8,128)(2,1)S(1)} collective-permute-done((bf16[48,6144]{1,0:T(8,128)(2,1)S(1)}, bf16[48,6144]{1,0:T(8,128)(2,1)S(1)}, u32[]{:S(2)}, u32[]{:S(2)}) %collective-permute-start.9) | collective-permute-done | bytes 589856 | tf_op jit(solution)/shard_map/ppermute | solution.py:35
  95.1 13.8 %collective-permute-done.10 = bf16[24,6144]{1,0:T(8,128)(2,1)S(1)} collective-permute-done((bf16[24,6144]{1,0:T(8,128)(2,1)S(1)}, bf16[24,6144]{1,0:T(8,128)(2,1)S(1)}, u32[]{:S(2)}, u32[]{:S(2)}) %collective-permute-start.10) | collective-permute-done | bytes 294944 | tf_op jit(solution)/shard_map/ppermute | solution.py:35
  113.7 6.6 %shard_map.426 = (f32[128,768]{1,0:T(8,128)S(1)}, bf16[2,128,768]{2,1,0:T(8,128)(2,1)S(1)}, bf16[3,128,768]{2,1,0:T(8,128)(2,1)S(1)}) custom-call(bf16[128,768]{1,0:T(8,128)(2,1)S(1)} %bitcast.28, f32[16,768]{1,0:T(8,128)S(1)} %fusion.5.vec_ref, bf16[768,768]{1,0:T(8,128)(2,1)S(1)} %fusion.order_ref, bf16[384,3200]{1,0:T(8,128)(2,1)} %pad_maximum_fusion.3.top_ref, ...), custom_call_target="tpu_custom_call" | custom-call | flops 1000 | bytes 1000 | tf_op jit(solution)/shard_map/pallas_call | solution.py:603
  139.5 21.2 %collective-permute-done.15 = bf16[96,6144]{1,0:T(8,128)(2,1)S(1)} collective-permute-done((bf16[96,6144]{1,0:T(8,128)(2,1)S(1)}, bf16[96,6144]{1,0:T(8,128)(2,1)S(1)}, u32[]{:S(2)}, u32[]{:S(2)}) %collective-permute-start.15) | collective-permute-done | bytes 1179680 | tf_op jit(solution)/shard_map/ppermute | solution.py:39
  162.3 8.2 %collective-permute-done.16 = bf16[192,6144]{1,0:T(8,128)(2,1)S(1)} collective-permute-done((bf16[192,6144]{1,0:T(8,128)(2,1)S(1)}, bf16[192,6144]{1,0:T(8,128)(2,1)S(1)}, u32[]{:S(2)}, u32[]{:S(2)}) %collective-permute-start.16) | collective-permute-done | bytes 2359328 | tf_op jit(solution)/shard_map/ppermute | solution.py:39
  193.2 9.2 %shard_map.430 = (f32[128,768]{1,0:T(8,128)S(1)}, bf16[2,128,768]{2,1,0:T(8,128)(2,1)S(1)}, bf16[128,768]{1,0:T(8,128)(2,1)S(1)}) custom-call(s32[2]{0:T(128)S(1)} %copy-done.31, f32[128,768]{1,0:T(8,128)S(1)} %get-tuple-element.390.x_ref, f32[16,768]{1,0:T(8,128)S(1)} %fusion.5.vec_ref, bf16[768,768]{1,0:T(8,128)(2,1)S(1)} %fusion.order_ref, ...), custom_call_target="tpu_custom_call" | custom-call | flops 1000 | bytes 1000 | tf_op jit(solution)/shard_map/pallas_call | solution.py:603
  206.6 6.9 %collective-permute-done.19.up2_ref.down2_ref = bf16[384,6144]{1,0:T(8,128)(2,1)S(1)} collective-permute-done((bf16[384,6144]{1,0:T(8,128)(2,1)S(1)}, bf16[384,6144]{1,0:T(8,128)(2,1)S(1)}, u32[]{:S(2)}, u32[]{:S(2)}) %collective-permute-start.19) | collective-permute-done | bytes 4718624 | tf_op jit(solution)/shard_map/ppermute | solution.py:35
  216.3 7.7 %shard_map.431 = (f32[128,768]{1,0:T(8,128)S(1)}, f32[8,768]{1,0:T(8,128)S(1)}, bf16[5,128,768]{2,1,0:T(8,128)(2,1)S(1)}, bf16[5,128,768]{2,1,0:T(8,128)(2,1)S(1)}) custom-call(f32[128,768]{1,0:T(8,128)S(1)} %get-tuple-element.403.x_ref, f32[16,768]{1,0:T(8,128)S(1)} %fusion.5.vec_ref, bf16[768,768]{1,0:T(8,128)(2,1)S(1)} %fusion.order_ref, ...), custom_call_target="tpu_custom_call" | custom-call | flops 1000 | bytes 1000 | tf_op jit(solution)/shard_map/pallas_call | solution.py:603
  236.5 11.1 %shard_map.434 = (f32[128,768]{1,0:T(8,128)S(1)}, f32[8,768]{1,0:T(8,128)S(1)}, bf16[2,128,768]{2,1,0:T(8,128)(2,1)S(1)}, bf16[1152,1536]{1,0:T(8,128)(2,1)S(1)}) custom-call(s32[2]{0:T(128)S(1)} %copy-done.31, f32[128,768]{1,0:T(8,128)S(1)} %copy-done.12, f32[16,768]{1,0:T(8,128)S(1)} %fusion.5.vec_ref, bf16[768,768]{1,0:T(8,128)(2,1)S(1)} %fusion.order_ref, ...), custom_call_target="tpu_custom_call" | custom-call | flops 1000 | bytes 1000 | tf_op jit(solution)/shard_map/pallas_call | solution.py:603
  251.8 10.3 %shard_map.436 = (f32[128,768]{1,0:T(8,128)S(1)}, f32[8,768]{1,0:T(8,128)S(1)}, bf16[4,128,768]{2,1,0:T(8,128)(2,1)S(1)}) custom-call(f32[128,768]{1,0:T(8,128)S(1)} %get-tuple-element.387.x_ref, f32[16,768]{1,0:T(8,128)S(1)} %fusion.5.vec_ref, bf16[768,768]{1,0:T(8,128)(2,1)S(1)} %fusion.order_ref, bf16[3,128,768]{2,1,0:T(8,128)(2,1)S(1)} %copy-done.18, ...), custom_call_target="tpu_custom_call" | custom-call | flops 1000 | bytes 1000 | tf_op jit(solution)/shard_map/pallas_call | solution.py:603
  273.0 6.5 %shard_map.439 = (f32[128,768]{1,0:T(8,128)S(1)}, f32[8,768]{1,0:T(8,128)S(1)}, bf16[5,128,768]{2,1,0:T(8,128)(2,1)S(1)}) custom-call(f32[128,768]{1,0:T(8,128)S(1)} %copy-done.10, f32[16,768]{1,0:T(8,128)S(1)} %fusion.5.vec_ref, bf16[768,768]{1,0:T(8,128)(2,1)S(1)} %fusion.order_ref, f32[128,768]{1,0:T(8,128)S(1)} %get-tuple-element.448.dx_ref, ...), custom_call_target="tpu_custom_call" | custom-call | flops 1000 | bytes 1000 | tf_op jit(solution)/shard_map/pallas_call | solution.py:603
  286.6 11.0 %shard_map.441 = (f32[128,768]{1,0:T(8,128)S(1)}, f32[8,768]{1,0:T(8,128)}, bf16[5,128,768]{2,1,0:T(8,128)(2,1)S(1)}) custom-call(bf16[128,768]{1,0:T(8,128)(2,1)S(1)} %bitcast.29, f32[16,768]{1,0:T(8,128)S(1)} %fusion.5.vec_ref, bf16[768,768]{1,0:T(8,128)(2,1)S(1)} %fusion.order_ref, bf16[3,128,768]{2,1,0:T(8,128)(2,1)S(1)} %copy-done.16, ...), custom_call_target="tpu_custom_call" | custom-call | flops 1000 | bytes 1000 | tf_op jit(solution)/shard_map/pallas_call | solution.py:603
  297.7 10.9 %collective-permute-done.31.got_ref = bf16[96,6144]{1,0:T(8,128)(2,1)S(1)} collective-permute-done((bf16[96,6144]{1,0:T(8,128)(2,1)S(1)}, bf16[96,6144]{1,0:T(8,128)(2,1)S(1)}, u32[]{:S(2)}, u32[]{:S(2)}) %collective-permute-start.31) | collective-permute-done | bytes 1179680 | tf_op jit(solution)/shard_map/ppermute | solution.py:39
  321.4 8.2 %shard_map.445 = bf16[1152,768]{1,0:T(8,128)(2,1)} custom-call(bf16[1152,1536]{1,0:T(8,128)(2,1)S(1)} %get-tuple-element.489.dkv_ref, bf16[768,768]{1,0:T(8,128)(2,1)S(1)} %fusion.order_ref, bf16[384,6144]{1,0:T(8,128)(2,1)} %pad_maximum_fusion.1.top_ref, bf16[384,6144]{1,0:T(8,128)(2,1)} %collective-permute-done.17.low_ref), custom_call_target="tpu_custom_call" | custom-call | flops 1000 | bytes 1000 | tf_op jit(solution)/shard_map/pallas_call | solution.py:603
  329.7 13.3 %collective-permute-done.34.got_ref = bf16[96,6144]{1,0:T(8,128)(2,1)S(1)} collective-permute-done((bf16[96,6144]{1,0:T(8,128)(2,1)S(1)}, bf16[96,6144]{1,0:T(8,128)(2,1)S(1)}, u32[]{:S(2)}, u32[]{:S(2)}) %collective-permute-start.34) | collective-permute-done | bytes 1179680 | tf_op jit(solution)/shard_map/ppermute | solution.py:39
  346.0 7.9 %collective-permute-done.36.got_ref = bf16[192,6144]{1,0:T(8,128)(2,1)S(1)} collective-permute-done((bf16[192,6144]{1,0:T(8,128)(2,1)S(1)}, bf16[192,6144]{1,0:T(8,128)(2,1)S(1)}, u32[]{:S(2)}, u32[]{:S(2)}) %collective-permute-start.36) | collective-permute-done | bytes 2359328 | tf_op jit(solution)/shard_map/ppermute | solution.py:39
  364.3 16.8 %collective-permute-done.39.got_ref = bf16[96,6144]{1,0:T(8,128)(2,1)S(1)} collective-permute-done((bf16[96,6144]{1,0:T(8,128)(2,1)S(1)}, bf16[96,6144]{1,0:T(8,128)(2,1)S(1)}, u32[]{:S(2)}, u32[]{:S(2)}) %collective-permute-start.39) | collective-permute-done | bytes 1179680 | tf_op jit(solution)/shard_map/ppermute | solution.py:39
  384.8 11.5 %collective-permute-done.42 = bf16[48,6144]{1,0:T(8,128)(2,1)S(1)} collective-permute-done((bf16[48,6144]{1,0:T(8,128)(2,1)S(1)}, bf16[48,6144]{1,0:T(8,128)(2,1)S(1)}, u32[]{:S(2)}, u32[]{:S(2)}) %collective-permute-start.42) | collective-permute-done | bytes 589856 | tf_op jit(solution)/shard_map/ppermute | solution.py:35
  399.1 7.7 %collective-permute-done.44 = bf16[48,3200]{1,0:T(8,128)(2,1)S(1)} collective-permute-done((bf16[48,3200]{1,0:T(8,128)(2,1)S(1)}, bf16[48,3200]{1,0:T(8,128)(2,1)S(1)}, u32[]{:S(2)}, u32[]{:S(2)}) %collective-permute-start.44) | collective-permute-done | bytes 307232 | tf_op jit(solution)/shard_map/ppermute | solution.py:35
  407.7 9.5 %collective-permute-done.45.got_ref = bf16[24,6144]{1,0:T(8,128)(2,1)S(1)} collective-permute-done((bf16[24,6144]{1,0:T(8,128)(2,1)S(1)}, bf16[24,6144]{1,0:T(8,128)(2,1)S(1)}, u32[]{:S(2)}, u32[]{:S(2)}) %collective-permute-start.45) | collective-permute-done | bytes 294944 | tf_op jit(solution)/shard_map/ppermute | solution.py:35
  (224 shorter events, 171.8 us)
Async XLA Ops:
  17.1 14.7 %collective-permute-start.1 = (bf16[48,3200]{1,0:T(8,128)(2,1)S(1)}, bf16[48,3200]{1,0:T(8,128)(2,1)S(1)}, u32[]{:S(2)}, u32[]{:S(2)}) collective-permute-start(bf16[48,3200]{1,0:T(8,128)(2,1)S(1)} %pad_maximum_fusion.17), channel_id=1, source_target_pairs={{0,8},{1,9},{2,10},{3,11},{4,12},{5,13},{6,14},{7,15},{8,0},{9,1},... | collective-permute-start | bytes 921608 | tf_op jit(solution)/shard_map/ppermute | solution.py:35
  18.0 16.8 %collective-permute-start.2 = (bf16[24,6144]{1,0:T(8,128)(2,1)}, bf16[24,6144]{1,0:T(8,128)(2,1)S(1)}, u32[]{:S(2)}, u32[]{:S(2)}) collective-permute-start(bf16[24,6144]{1,0:T(8,128)(2,1)} %get-tuple-element.311), channel_id=1, source_target_pairs={{0,16},{1,17},{2,18},{3,19},{4,20},{5,21},{6,22},{7,23},{8,24},{9,... | collective-permute-start | bytes 884744 | tf_op jit(solution)/shard_map/ppermute | solution.py:35
  47.4 27.8 %collective-permute-start.5 = (bf16[192,3200]{1,0:T(8,128)(2,1)S(1)}, bf16[192,3200]{1,0:T(8,128)(2,1)S(1)}, u32[]{:S(2)}, u32[]{:S(2)}) collective-permute-start(bf16[192,3200]{1,0:T(8,128)(2,1)S(1)} %pad_maximum_fusion.7), channel_id=1, source_target_pairs={{0,4},{1,5},{2,3},{3,2},{4,0},{5,1},{6,7},{7,6},{8,12},{9,13},{10,... | collective-permute-start | bytes 3686408 | tf_op jit(solution)/shard_map/ppermute | solution.py:39
  50.5 14.1 %collective-permute-start.6 = (bf16[24,6144]{1,0:T(8,128)(2,1)S(1)}, bf16[24,6144]{1,0:T(8,128)(2,1)S(1)}, u32[]{:S(2)}, u32[]{:S(2)}) collective-permute-start(bf16[24,6144]{1,0:T(8,128)(2,1)S(1)} %copy-done.33), channel_id=1, source_target_pairs={{0,16},{1,17},{2,18},{3,19},{4,20},{5,21},{6,22},{7,23},{8,24},{9,... | collective-permute-start | bytes 884744 | tf_op jit(solution)/shard_map/ppermute | solution.py:35
  52.9 24.1 %collective-permute-start.7 = (bf16[96,6144]{1,0:T(8,128)(2,1)S(1)}, bf16[96,6144]{1,0:T(8,128)(2,1)}, u32[]{:S(2)}, u32[]{:S(2)}) collective-permute-start(bf16[96,6144]{1,0:T(8,128)(2,1)S(1)} %pad_maximum_fusion.10), channel_id=1, source_target_pairs={{0,1},{1,0},{2,6},{3,7},{4,5},{5,4},{6,2},{7,3},{8,9},{9,8},{10,14... | collective-permute-start | bytes 3538952 | tf_op jit(solution)/shard_map/ppermute | solution.py:39
  78.4 30.6 %collective-permute-start.11 = (bf16[192,6144]{1,0:T(8,128)(2,1)S(1)}, bf16[192,6144]{1,0:T(8,128)(2,1)S(1)}, u32[]{:S(2)}, u32[]{:S(2)}) collective-permute-start(bf16[192,6144]{1,0:T(8,128)(2,1)S(1)} %pad_maximum_fusion.4), channel_id=1, source_target_pairs={{0,4},{1,5},{2,3},{3,2},{4,0},{5,1},{6,7},{7,6},{8,12},{9,13},{10,... | collective-permute-start | bytes 7077896 | tf_op jit(solution)/shard_map/ppermute | solution.py:39
  109.5 22.6 %collective-permute-start.14 = (bf16[384,6144]{1,0:T(8,128)(2,1)S(1)}, bf16[384,6144]{1,0:T(8,128)(2,1)S(1)}, u32[]{:S(2)}, u32[]{:S(2)}) collective-permute-start(bf16[384,6144]{1,0:T(8,128)(2,1)S(1)} %pad_maximum_fusion.up_ref.down_ref), channel_id=1, source_target_pairs={{0,2},{1,3},{2,0},{3,1},{4,6},{5,7},{6,4},{7,5},{8,10},{9,11},{10,... | collective-permute-start | bytes 14155784 | tf_op jit(solution)/shard_map/ppermute | solution.py:35
  109.6 16.3 %collective-permute-start.12 = (bf16[96,6144]{1,0:T(8,128)(2,1)S(1)}, bf16[96,6144]{1,0:T(8,128)(2,1)S(1)}, u32[]{:S(2)}, u32[]{:S(2)}) collective-permute-start(bf16[96,6144]{1,0:T(8,128)(2,1)S(1)} %pad_maximum_fusion.11), channel_id=1, source_target_pairs={{0,1},{1,0},{2,6},{3,7},{4,5},{5,4},{6,2},{7,3},{8,9},{9,8},{10,14... | collective-permute-start | bytes 3538952 | tf_op jit(solution)/shard_map/ppermute | solution.py:39
  113.7 14.9 %collective-permute-start.13 = (bf16[48,6144]{1,0:T(8,128)(2,1)S(1)}, bf16[48,6144]{1,0:T(8,128)(2,1)S(1)}, u32[]{:S(2)}, u32[]{:S(2)}) collective-permute-start(bf16[48,6144]{1,0:T(8,128)(2,1)S(1)} %pad_maximum_fusion.16), channel_id=1, source_target_pairs={{0,8},{1,9},{2,10},{3,11},{4,12},{5,13},{6,14},{7,15},{8,0},{9,1},... | collective-permute-start | bytes 1769480 | tf_op jit(solution)/shard_map/ppermute | solution.py:35
  128.6 41.9 %collective-permute-start.16 = (bf16[192,6144]{1,0:T(8,128)(2,1)S(1)}, bf16[192,6144]{1,0:T(8,128)(2,1)S(1)}, u32[]{:S(2)}, u32[]{:S(2)}) collective-permute-start(bf16[192,6144]{1,0:T(8,128)(2,1)S(1)} %pad_maximum_fusion.5), channel_id=1, source_target_pairs={{0,4},{1,5},{2,3},{3,2},{4,0},{5,1},{6,7},{7,6},{8,12},{9,13},{10,... | collective-permute-start | bytes 7077896 | tf_op jit(solution)/shard_map/ppermute | solution.py:39
  131.7 29.0 %collective-permute-start.15 = (bf16[96,6144]{1,0:T(8,128)(2,1)S(1)}, bf16[96,6144]{1,0:T(8,128)(2,1)S(1)}, u32[]{:S(2)}, u32[]{:S(2)}) collective-permute-start(bf16[96,6144]{1,0:T(8,128)(2,1)S(1)} %pad_maximum_fusion.12), channel_id=1, source_target_pairs={{0,1},{1,0},{2,6},{3,7},{4,5},{5,4},{6,2},{7,3},{8,9},{9,8},{10,14... | collective-permute-start | bytes 3538952 | tf_op jit(solution)/shard_map/ppermute | solution.py:39
  173.2 29.3 %collective-permute-start.18 = (bf16[192,6144]{1,0:T(8,128)(2,1)}, bf16[192,6144]{1,0:T(8,128)(2,1)}, u32[]{:S(2)}, u32[]{:S(2)}) collective-permute-start(bf16[192,6144]{1,0:T(8,128)(2,1)} %pad_maximum_fusion.6), channel_id=1, source_target_pairs={{0,4},{1,5},{2,3},{3,2},{4,0},{5,1},{6,7},{7,6},{8,12},{9,13},{10,... | collective-permute-start | bytes 7077896 | tf_op jit(solution)/shard_map/ppermute | solution.py:39
  235.4 28.9 %collective-permute-start.26 = (bf16[192,6144]{1,0:T(8,128)(2,1)S(1)}, bf16[192,6144]{1,0:T(8,128)(2,1)S(1)}, u32[]{:S(2)}, u32[]{:S(2)}) collective-permute-start(bf16[192,6144]{1,0:T(8,128)(2,1)S(1)} %get-tuple-element.426), channel_id=1, source_target_pairs={{0,4},{1,5},{2,3},{3,2},{4,0},{5,1},{6,7},{7,6},{8,12},{9,13},{10,... | collective-permute-start | bytes 7077896 | tf_op jit(solution)/shard_map/ppermute | solution.py:39
  271.6 41.5 %collective-permute-start.32 = (bf16[192,6144]{1,0:T(8,128)(2,1)S(1)}, bf16[192,6144]{1,0:T(8,128)(2,1)S(1)}, u32[]{:S(2)}, u32[]{:S(2)}) collective-permute-start(bf16[192,6144]{1,0:T(8,128)(2,1)S(1)} %get-tuple-element.473), channel_id=1, source_target_pairs={{0,4},{1,5},{2,3},{3,2},{4,0},{5,1},{6,7},{7,6},{8,12},{9,13},{10,... | collective-permute-start | bytes 7077896 | tf_op jit(solution)/shard_map/ppermute | solution.py:39
  279.7 28.9 %collective-permute-start.31 = (bf16[96,6144]{1,0:T(8,128)(2,1)S(1)}, bf16[96,6144]{1,0:T(8,128)(2,1)S(1)}, u32[]{:S(2)}, u32[]{:S(2)}) collective-permute-start(bf16[96,6144]{1,0:T(8,128)(2,1)S(1)} %get-tuple-element.465), channel_id=1, source_target_pairs={{0,1},{1,0},{2,6},{3,7},{4,5},{5,4},{6,2},{7,3},{8,9},{9,8},{10,14... | collective-permute-start | bytes 3538952 | tf_op jit(solution)/shard_map/ppermute | solution.py:39
  297.6 19.9 %collective-permute-start.33 = (bf16[5,128,768]{2,1,0:T(8,128)(2,1)S(1)}, bf16[5,128,768]{2,1,0:T(8,128)(2,1)S(1)}, u32[]{:S(2)}, u32[]{:S(2)}) collective-permute-start(bf16[5,128,768]{2,1,0:T(8,128)(2,1)S(1)} %get-tuple-element.483.sd_ref), channel_id=1, source_target_pairs={{0,2},{1,3},{2,0},{3,1},{4,6},{5,7},{6,4},{7,5},{8,10},{9,11},{10,... | collective-permute-start | bytes 2949128 | tf_op jit(solution)/shard_map/ppermute | solution.py:35
  314.2 28.8 %collective-permute-start.34 = (bf16[96,6144]{1,0:T(8,128)(2,1)S(1)}, bf16[96,6144]{1,0:T(8,128)(2,1)S(1)}, u32[]{:S(2)}, u32[]{:S(2)}) collective-permute-start(bf16[96,6144]{1,0:T(8,128)(2,1)S(1)} %get-tuple-element.492), channel_id=1, source_target_pairs={{0,1},{1,0},{2,6},{3,7},{4,5},{5,4},{6,2},{7,3},{8,9},{9,8},{10,14... | collective-permute-start | bytes 3538952 | tf_op jit(solution)/shard_map/ppermute | solution.py:39
  315.6 27.9 %collective-permute-start.35 = (bf16[48,6144]{1,0:T(8,128)(2,1)S(1)}, bf16[48,6144]{1,0:T(8,128)(2,1)S(1)}, u32[]{:S(2)}, u32[]{:S(2)}) collective-permute-start(bf16[48,6144]{1,0:T(8,128)(2,1)S(1)} %get-tuple-element.501), channel_id=1, source_target_pairs={{0,8},{1,9},{2,10},{3,11},{4,12},{5,13},{6,14},{7,15},{8,0},{9,1},... | collective-permute-start | bytes 1769480 | tf_op jit(solution)/shard_map/ppermute | solution.py:35
  316.1 37.8 %collective-permute-start.36 = (bf16[192,6144]{1,0:T(8,128)(2,1)S(1)}, bf16[192,6144]{1,0:T(8,128)(2,1)S(1)}, u32[]{:S(2)}, u32[]{:S(2)}) collective-permute-start(bf16[192,6144]{1,0:T(8,128)(2,1)S(1)} %get-tuple-element.507), channel_id=1, source_target_pairs={{0,4},{1,5},{2,3},{3,2},{4,0},{5,1},{6,7},{7,6},{8,12},{9,13},{10,... | collective-permute-start | bytes 7077896 | tf_op jit(solution)/shard_map/ppermute | solution.py:39
  343.6 17.1 %collective-permute-start.38 = (bf16[48,6144]{1,0:T(8,128)(2,1)S(1)}, bf16[48,6144]{1,0:T(8,128)(2,1)S(1)}, u32[]{:S(2)}, u32[]{:S(2)}) collective-permute-start(bf16[48,6144]{1,0:T(8,128)(2,1)S(1)} %get-tuple-element.518), channel_id=1, source_target_pairs={{0,8},{1,9},{2,10},{3,11},{4,12},{5,13},{6,14},{7,15},{8,0},{9,1},... | collective-permute-start | bytes 1769480 | tf_op jit(solution)/shard_map/ppermute | solution.py:35
  345.1 36.0 %collective-permute-start.40 = (bf16[192,3200]{1,0:T(8,128)(2,1)S(1)}, bf16[192,3200]{1,0:T(8,128)(2,1)S(1)}, u32[]{:S(2)}, u32[]{:S(2)}) collective-permute-start(bf16[192,3200]{1,0:T(8,128)(2,1)S(1)} %pad_maximum_fusion.8), channel_id=1, source_target_pairs={{0,4},{1,5},{2,3},{3,2},{4,0},{5,1},{6,7},{7,6},{8,12},{9,13},{10,... | collective-permute-start | bytes 3686408 | tf_op jit(solution)/shard_map/ppermute | solution.py:39
  355.0 26.1 %collective-permute-start.39 = (bf16[96,6144]{1,0:T(8,128)(2,1)S(1)}, bf16[96,6144]{1,0:T(8,128)(2,1)S(1)}, u32[]{:S(2)}, u32[]{:S(2)}) collective-permute-start(bf16[96,6144]{1,0:T(8,128)(2,1)S(1)} %get-tuple-element.524), channel_id=1, source_target_pairs={{0,1},{1,0},{2,6},{3,7},{4,5},{5,4},{6,2},{7,3},{8,9},{9,8},{10,14... | collective-permute-start | bytes 3538952 | tf_op jit(solution)/shard_map/ppermute | solution.py:39
  360.7 22.3 %collective-permute-start.41 = (bf16[24,6144]{1,0:T(8,128)(2,1)S(1)}, bf16[24,6144]{1,0:T(8,128)(2,1)S(1)}, u32[]{:S(2)}, u32[]{:S(2)}) collective-permute-start(bf16[24,6144]{1,0:T(8,128)(2,1)S(1)} %add_convert_fusion.3), channel_id=1, source_target_pairs={{0,16},{1,17},{2,18},{3,19},{4,20},{5,21},{6,22},{7,23},{8,24},{9,... | collective-permute-start | bytes 884744 | tf_op jit(solution)/shard_map/ppermute | solution.py:35
  398.7 18.6 %collective-permute-start.45 = (bf16[24,6144]{1,0:T(8,128)(2,1)S(1)}, bf16[24,6144]{1,0:T(8,128)(2,1)S(1)}, u32[]{:S(2)}, u32[]{:S(2)}) collective-permute-start(bf16[24,6144]{1,0:T(8,128)(2,1)S(1)} %get-tuple-element.556), channel_id=1, source_target_pairs={{0,16},{1,17},{2,18},{3,19},{4,20},{5,21},{6,22},{7,23},{8,24},{9,... | collective-permute-start | bytes 884744 | tf_op jit(solution)/shard_map/ppermute | solution.py:35
  (61 other events, 637.2 us)
